TPU v7x, 32 devices: a whole 2x2x4 slice. The times are simulated.
32 devices in a mesh: seq: 2 (over x), dp: 16 (over z, y, core).
Axes of the slice: x: 2, y: 2, z: 4, core: 2. Of those that a mesh axis runs over, the one named last changes fastest.
Arguments:
- tokens: bfloat16 [16384, 1536], P(('seq', 'dp')), may hold values from -6 to 6
- cotangent: bfloat16 [16384, 1536], P(('seq', 'dp')), may hold values from -6 to 6
- positions: int32 [16, 1024], P('dp'), may hold values from 0 to 1023, each once within a row
- lengths: int32 [16, 3], P('dp'), may hold values from 1 to 512, 1024 in all within a row
- routes: int32 [16384, 8], P(('seq', 'dp')), may hold values from 0 to 15, all different within a row; in each aligned block of 512 rows (0 to 511, 512 to 1023, ...) at most 320 rows name the same one
- logits: float32 [16384, 8], P(('seq', 'dp')), may hold values from -3 to 3
- w_query: bfloat16 [1536, 1536], P(('seq', 'dp')), may hold values from -0.59765625 to 0.59765625
- w_key: bfloat16 [1536, 512], P(('seq', 'dp')), may hold values from -0.59765625 to 0.59765625
- w_value: bfloat16 [1536, 512], P(('seq', 'dp')), may hold values from -0.15625 to 0.15625
- w_output: bfloat16 [1536, 1536], P(('seq', 'dp')), may hold values from -4 to 4
- gain_attn: bfloat16 [1536], P(('seq', 'dp')), may hold values from 0.5 to 1.5
- gain_ffn: bfloat16 [1536], P(('seq', 'dp')), may hold values from 0.5 to 1.5
- w_in: bfloat16 [16, 1536, 1024], P('dp', None, 'seq'), may hold values from -0.15625 to 0.15625
- w_out: bfloat16 [16, 512, 1536], P('dp', 'seq'), may hold values from -6 to 6
Outputs:
- output: bfloat16 [16384, 1536], P(('seq', 'dp'))
- grad_tokens: float32 [16384, 1536], P(('seq', 'dp'))
- grad_w_query: float32 [1536, 1536], P(('seq', 'dp'))
- grad_w_key: float32 [1536, 512], P(('seq', 'dp'))
- grad_w_value: float32 [1536, 512], P(('seq', 'dp'))
- grad_w_output: float32 [1536, 1536], P(('seq', 'dp'))
- grad_gain_attn: float32 [1536], P(('seq', 'dp'))
- grad_gain_ffn: float32 [1536], P(('seq', 'dp'))
- grad_w_in: float32 [16, 1536, 1024], P('dp', None, 'seq')
- grad_w_out: float32 [16, 512, 1536], P('dp', 'seq')
Inputs may be any that keep to these rules, and one draw needn't show every extreme that they name: `positions`: each row is a permutation of 0 to 1023. `lengths`: each row sums to 1024 and its largest entry is 512. `routes`: each row names 8 different experts. Among the rows of one device no expert is named more than 320 times, and in every draw some expert is named exactly 320 times by the rows of some device.
All inputs are finite; a program needn't handle non-finite values.
Results may differ from a plain program's by a relative error of at most 0.015.
The roundings to bfloat16 on the way count: a program that leaves them out, or rounds other values in their place, can miss the bound.
Values may be sent and summed in bfloat16 or wider, within the bound.
No kernel may reach another device: no remote copies, remote signals or barrier semaphores. Data moves between devices by JAX's collectives and lax.ppermute only.
A program may use at most 256 MiB of HBM per device.

v0:
```python
import jax
import jax.numpy as jnp
from jax import lax
from jax.sharding import PartitionSpec as P

QHEADS = 24
KVHEADS = 8
HDIM = 64
FF = 512
TOP = 8


EPSILON = 1e-06
BRANCH_SCALE = 0.22
SCORE_SCALE = 1.0 / 64.0
THETA = 10000.0


def rms_norm(value, gain):
    return value * lax.rsqrt(jnp.mean(value * value, axis=-1, keepdims=True) + EPSILON) * gain


def local_places(placing, seq_lengths):
    ends = jnp.cumsum(seq_lengths)
    segment = jnp.sum((placing[:, None] >= ends[None, :]).astype(jnp.int32), axis=1)
    starts = ends - seq_lengths
    member = segment[:, None] == jnp.arange(seq_lengths.shape[0], dtype=jnp.int32)[None, :]
    start_of = jnp.sum(jnp.where(member, starts[None, :], 0), axis=1)
    return (segment, placing - start_of)


def rotate(values, place, direction):
    half = values.shape[-1] // 2
    freqs = jnp.power(THETA, -jnp.arange(half, dtype=jnp.float32) * 2.0 / values.shape[-1])
    angles = place.astype(jnp.float32)[:, None] * freqs[None, :]
    cosine = jnp.cos(angles)[:, None, :]
    sine = direction * jnp.sin(angles)[:, None, :]
    first = values[..., :half]
    second = values[..., half:]
    return jnp.concatenate(
        [first * cosine - second * sine, second * cosine + first * sine], axis=-1
    )


def shards(
    tokens,
    cotangent,
    positions,
    lengths,
    routes,
    logits,
    w_query,
    w_key,
    w_value,
    w_output,
    gain_attn,
    gain_ffn,
    w_in,
    w_out,
):
    seq_count = lax.axis_size("seq")
    data_count = lax.axis_size("dp")
    tok_count = tokens.shape[0]
    group_len = positions.shape[1]
    local_experts = w_in.shape[0]
    experts_all = local_experts * data_count
    capacity = min(tok_count, 5 * tok_count * TOP // (4 * experts_all))
    heads_local = QHEADS // seq_count
    kv_local = KVHEADS // seq_count
    ratio = QHEADS // KVHEADS
    width = tokens.shape[1]
    query_full, key_full, value_full, output_full, gain_one, gain_two = (
        lax.all_gather(w_query, ("seq", "dp"), axis=0, tiled=True),
        lax.all_gather(w_key, ("seq", "dp"), axis=0, tiled=True),
        lax.all_gather(w_value, ("seq", "dp"), axis=0, tiled=True),
        lax.all_gather(w_output, ("seq", "dp"), axis=0, tiled=True),
        lax.all_gather(gain_attn, ("seq", "dp"), axis=0, tiled=True),
        lax.all_gather(gain_ffn, ("seq", "dp"), axis=0, tiled=True),
    )
    in_full, out_full = (
        lax.all_gather(w_in, "seq", axis=2, tiled=True),
        lax.all_gather(w_out, "seq", axis=1, tiled=True),
    )
    gain_one = gain_one.astype(jnp.float32)
    gain_two = gain_two.astype(jnp.float32)
    segment, place = local_places(positions[0], lengths[0])
    my_start = lax.axis_index("seq") * tok_count
    my_place = lax.dynamic_slice_in_dim(place, my_start, tok_count)
    inputs = tokens.astype(jnp.float32)
    normed = rms_norm(inputs, gain_one).astype(jnp.bfloat16)
    query_pre = jnp.dot(normed, query_full, preferred_element_type=jnp.float32)
    key_pre = jnp.dot(normed, key_full, preferred_element_type=jnp.float32)
    query_rot = (
        rotate(query_pre.reshape(tok_count, QHEADS, HDIM), my_place, 1.0)
        .reshape(tok_count, QHEADS * HDIM)
        .astype(jnp.bfloat16)
    )
    key_rot = (
        rotate(key_pre.reshape(tok_count, KVHEADS, HDIM), my_place, 1.0)
        .reshape(tok_count, KVHEADS * HDIM)
        .astype(jnp.bfloat16)
    )
    value_low = jnp.dot(normed, value_full, preferred_element_type=jnp.float32).astype(jnp.bfloat16)
    query_heads, key_heads, value_heads = (
        lax.all_to_all(query_rot, "seq", split_axis=1, concat_axis=0, tiled=True),
        lax.all_to_all(key_rot, "seq", split_axis=1, concat_axis=0, tiled=True),
        lax.all_to_all(value_low, "seq", split_axis=1, concat_axis=0, tiled=True),
    )
    keys_three = key_heads.reshape(group_len, kv_local, HDIM)
    values_three = value_heads.reshape(group_len, kv_local, HDIM)
    length = min(512, group_len)
    count = group_len // length

    def scores_of(query_block, seg_block, place_block):
        grouped = query_block.reshape(length, kv_local, ratio, HDIM)
        raw_scores = (
            jnp.einsum("qgrd,kgd->grqk", grouped, keys_three, preferred_element_type=jnp.float32)
            * SCORE_SCALE
        )
        allowed = (seg_block[:, None] == segment[None, :]) & (
            place[None, :] <= place_block[:, None]
        )
        return jnp.where(allowed[None, None], raw_scores, -1e30)

    def forward_block(pieces):
        query_block, seg_block, place_block = pieces
        scores = scores_of(query_block, seg_block, place_block)
        highest = jnp.max(scores, axis=-1, keepdims=True)
        expon = jnp.exp(scores - highest)
        totals = jnp.sum(expon, axis=-1, keepdims=True)
        probs = expon / totals
        mixed = jnp.einsum(
            "grqk,kgd->qgrd",
            probs.astype(jnp.bfloat16),
            values_three,
            preferred_element_type=jnp.float32,
        )
        return (
            mixed.reshape(length, heads_local * HDIM).astype(jnp.bfloat16),
            highest + jnp.log(totals),
            probs,
        )

    query_blocks = query_heads.reshape(count, length, heads_local * HDIM)
    seg_blocks = segment.reshape(count, length)
    place_blocks = place.reshape(count, length)
    block_args = (query_blocks, seg_blocks, place_blocks)

    def forward_light(pieces):
        mixed, lse_part, unused_probs = forward_block(pieces)
        return (mixed, lse_part)

    mixed_blocks, lse_blocks = lax.map(forward_light, block_args)
    mixed_heads = mixed_blocks.reshape(group_len, heads_local * HDIM)
    mixed_tokens = lax.all_to_all(mixed_heads, "seq", split_axis=0, concat_axis=1, tiled=True)
    attn = jnp.dot(mixed_tokens, output_full, preferred_element_type=jnp.float32)
    middle = inputs + BRANCH_SCALE * attn
    normed_ffn = rms_norm(middle, gain_two).astype(jnp.bfloat16)
    chosen = routes.reshape(-1)
    onehot = (chosen[:, None] == jnp.arange(experts_all, dtype=jnp.int32)[None, :]).astype(
        jnp.int32
    )
    ranking = jnp.sum(jnp.cumsum(onehot, axis=0) * onehot, axis=1) - 1
    target = chosen * capacity + ranking
    token_of = jnp.arange(tok_count * TOP, dtype=jnp.int32) // TOP
    gates = jax.nn.softmax(logits, axis=-1)
    source = jnp.full((experts_all * capacity,), tok_count, jnp.int32).at[target].set(token_of)
    slot_gate = jnp.zeros((experts_all * capacity,), jnp.float32).at[target].set(gates.reshape(-1))
    padded = jnp.concatenate([normed_ffn, jnp.zeros((1, width), jnp.bfloat16)], axis=0)
    outgoing = padded[source].reshape(data_count, local_experts * capacity, width)

    def expert_layout(arrived):
        return jnp.swapaxes(
            arrived.reshape(data_count, local_experts, capacity, width), 0, 1
        ).reshape(local_experts, data_count * capacity, width)

    def home_layout(values):
        return jnp.swapaxes(
            values.reshape(local_experts, data_count, capacity, width), 0, 1
        ).reshape(data_count, local_experts * capacity, width)

    def expert_forward(expert_rows):
        both = jnp.einsum("erd,edf->erf", expert_rows, in_full, preferred_element_type=jnp.float32)
        hidden = (jax.nn.silu(both[..., :FF]) * both[..., FF:]).astype(jnp.bfloat16)
        return (both, hidden)

    expert_rows = expert_layout(
        lax.all_to_all(outgoing, "dp", split_axis=0, concat_axis=0, tiled=True)
    )
    both, hidden = expert_forward(expert_rows)
    result = jnp.einsum(
        "erf,efd->erd", hidden, out_full, preferred_element_type=jnp.float32
    ).astype(jnp.bfloat16)
    returned = lax.all_to_all(
        home_layout(result), "dp", split_axis=0, concat_axis=0, tiled=True
    ).reshape(experts_all * capacity, width)
    picked = returned[target].reshape(tok_count, TOP, width).astype(jnp.float32)
    ffn = jnp.sum(picked * gates[:, :, None], axis=1)
    final = middle + BRANCH_SCALE * ffn
    output = final.astype(jnp.bfloat16)
    grad_final = cotangent.astype(jnp.float32)
    padded_grad = jnp.concatenate(
        [BRANCH_SCALE * grad_final, jnp.zeros((1, width), jnp.float32)], axis=0
    )
    grad_slots = (slot_gate[:, None] * padded_grad[source]).astype(jnp.bfloat16)
    grad_result = expert_layout(
        lax.all_to_all(
            grad_slots.reshape(data_count, local_experts * capacity, width),
            "dp",
            split_axis=0,
            concat_axis=0,
            tiled=True,
        )
    )
    rows_back = expert_layout(
        lax.all_to_all(outgoing, "dp", split_axis=0, concat_axis=0, tiled=True)
    )
    both_back, hidden_back = expert_forward(rows_back)
    grad_hidden = jnp.einsum(
        "erd,efd->erf", grad_result, out_full, preferred_element_type=jnp.float32
    )
    gate_part = both_back[..., :FF]
    up_part = both_back[..., FF:]
    sigma = jax.nn.sigmoid(gate_part)
    grad_gate = grad_hidden * up_part * sigma * (1.0 + gate_part * (1.0 - sigma))
    grad_up = grad_hidden * gate_part * sigma
    grad_both = jnp.concatenate([grad_gate, grad_up], axis=-1).astype(jnp.bfloat16)
    grad_out_local = jnp.einsum(
        "erf,erd->efd", hidden_back, grad_result, preferred_element_type=jnp.float32
    )
    grad_in_local = jnp.einsum(
        "erd,erf->edf", rows_back, grad_both, preferred_element_type=jnp.float32
    )
    grad_rows = jnp.einsum(
        "erf,edf->erd", grad_both, in_full, preferred_element_type=jnp.float32
    ).astype(jnp.bfloat16)
    grad_home = lax.all_to_all(
        home_layout(grad_rows), "dp", split_axis=0, concat_axis=0, tiled=True
    ).reshape(experts_all * capacity, width)
    grad_normed_ffn = jnp.sum(
        grad_home[target].reshape(tok_count, TOP, width).astype(jnp.float32), axis=1
    )
    grad_w_in, grad_w_out = (
        lax.psum_scatter(
            grad_in_local.astype(jnp.bfloat16), "seq", scatter_dimension=2, tiled=True
        ).astype(jnp.float32),
        lax.psum_scatter(
            grad_out_local.astype(jnp.bfloat16), "seq", scatter_dimension=1, tiled=True
        ).astype(jnp.float32),
    )
    unused_norm, norm_pull = jax.vjp(rms_norm, middle, gain_two)
    grad_middle_norm, grad_gain_two = norm_pull(grad_normed_ffn)
    grad_middle = grad_final + grad_middle_norm
    grad_attn = (BRANCH_SCALE * grad_middle).astype(jnp.bfloat16)
    grad_w_output = jnp.einsum(
        "te,td->ed", mixed_tokens, grad_attn, preferred_element_type=jnp.float32
    )
    grad_mixed = jnp.einsum(
        "td,ed->te", grad_attn, output_full, preferred_element_type=jnp.float32
    ).astype(jnp.bfloat16)
    grad_mixed_heads = lax.all_to_all(grad_mixed, "seq", split_axis=1, concat_axis=0, tiled=True)
    grad_blocks = grad_mixed_heads.reshape(count, length, heads_local * HDIM)
    back_args = (query_blocks, seg_blocks, place_blocks, lse_blocks, grad_blocks)

    def backward_block(carry, pieces):
        grad_keys, grad_values = carry
        query_block, seg_block, place_block, lse_block, grad_block = pieces[:5]
        probs = jnp.exp(scores_of(query_block, seg_block, place_block) - lse_block)
        grad_out = grad_block.reshape(length, kv_local, ratio, HDIM)
        grad_probs = jnp.einsum(
            "qgrd,kgd->grqk", grad_out, values_three, preferred_element_type=jnp.float32
        )
        grad_scores = (
            probs * (grad_probs - jnp.sum(probs * grad_probs, axis=-1, keepdims=True))
        ).astype(jnp.bfloat16)
        grad_query = SCORE_SCALE * jnp.einsum(
            "grqk,kgd->qgrd", grad_scores, keys_three, preferred_element_type=jnp.float32
        )
        grouped = query_block.reshape(length, kv_local, ratio, HDIM)
        grad_keys = grad_keys + SCORE_SCALE * jnp.einsum(
            "grqk,qgrd->kgd", grad_scores, grouped, preferred_element_type=jnp.float32
        )
        grad_values = grad_values + jnp.einsum(
            "grqk,qgrd->kgd",
            probs.astype(jnp.bfloat16),
            grad_out,
            preferred_element_type=jnp.float32,
        )
        return (
            (grad_keys, grad_values),
            grad_query.reshape(length, heads_local * HDIM).astype(jnp.bfloat16),
        )

    empty_keys = jnp.zeros((group_len, kv_local, HDIM), jnp.float32)
    (grad_keys, grad_values), grad_query_blocks = lax.scan(
        backward_block, (empty_keys, empty_keys), back_args
    )
    grad_query_heads = grad_query_blocks.reshape(group_len, heads_local * HDIM)
    grad_key_heads = grad_keys.reshape(group_len, kv_local * HDIM).astype(jnp.bfloat16)
    grad_value_heads = grad_values.reshape(group_len, kv_local * HDIM).astype(jnp.bfloat16)
    grad_query_tok, grad_key_tok, grad_value_tok = (
        lax.all_to_all(grad_query_heads, "seq", split_axis=0, concat_axis=1, tiled=True),
        lax.all_to_all(grad_key_heads, "seq", split_axis=0, concat_axis=1, tiled=True),
        lax.all_to_all(grad_value_heads, "seq", split_axis=0, concat_axis=1, tiled=True),
    )
    grad_query_pre = (
        rotate(grad_query_tok.astype(jnp.float32).reshape(tok_count, QHEADS, HDIM), my_place, -1.0)
        .reshape(tok_count, QHEADS * HDIM)
        .astype(jnp.bfloat16)
    )
    grad_key_pre = (
        rotate(grad_key_tok.astype(jnp.float32).reshape(tok_count, KVHEADS, HDIM), my_place, -1.0)
        .reshape(tok_count, KVHEADS * HDIM)
        .astype(jnp.bfloat16)
    )
    grad_w_query = jnp.einsum(
        "td,te->de", normed, grad_query_pre, preferred_element_type=jnp.float32
    )
    grad_w_key = jnp.einsum("td,te->de", normed, grad_key_pre, preferred_element_type=jnp.float32)
    grad_w_value = jnp.einsum(
        "td,te->de", normed, grad_value_tok, preferred_element_type=jnp.float32
    )
    grad_normed = jnp.einsum(
        "te,de->td", grad_query_pre, query_full, preferred_element_type=jnp.float32
    )
    grad_normed = grad_normed + jnp.einsum(
        "te,de->td", grad_key_pre, key_full, preferred_element_type=jnp.float32
    )
    grad_normed = grad_normed + jnp.einsum(
        "te,de->td", grad_value_tok, value_full, preferred_element_type=jnp.float32
    )
    unused_first, first_pull = jax.vjp(rms_norm, inputs, gain_one)
    grad_inputs_norm, grad_gain_one = first_pull(grad_normed)
    grad_tokens = grad_middle + grad_inputs_norm
    summed = (
        lax.psum_scatter(grad_w_query, ("seq", "dp"), scatter_dimension=0, tiled=True),
        lax.psum_scatter(grad_w_key, ("seq", "dp"), scatter_dimension=0, tiled=True),
        lax.psum_scatter(grad_w_value, ("seq", "dp"), scatter_dimension=0, tiled=True),
        lax.psum_scatter(grad_w_output, ("seq", "dp"), scatter_dimension=0, tiled=True),
        lax.psum_scatter(grad_gain_one, ("seq", "dp"), scatter_dimension=0, tiled=True),
        lax.psum_scatter(grad_gain_two, ("seq", "dp"), scatter_dimension=0, tiled=True),
    )
    return (
        output,
        grad_tokens,
        summed[0],
        summed[1],
        summed[2],
        summed[3],
        summed[4],
        summed[5],
        grad_w_in,
        grad_w_out,
    )


def solution(mesh):
    placed = (
        P(("seq", "dp"), None),
        P(("seq", "dp"), None),
        P("dp", None),
        P("dp", None),
        P(("seq", "dp"), None),
        P(("seq", "dp"), None),
        P(("seq", "dp"), None),
        P(("seq", "dp"), None),
        P(("seq", "dp"), None),
        P(("seq", "dp"), None),
        P(("seq", "dp")),
        P(("seq", "dp")),
        P("dp", None, "seq"),
        P("dp", "seq", None),
    )
    return jax.shard_map(
        shards,
        mesh=mesh,
        in_specs=placed,
        out_specs=(
            P(("seq", "dp"), None),
            P(("seq", "dp"), None),
            P(("seq", "dp"), None),
            P(("seq", "dp"), None),
            P(("seq", "dp"), None),
            P(("seq", "dp"), None),
            P(("seq", "dp")),
            P(("seq", "dp")),
            P("dp", None, "seq"),
            P("dp", "seq", None),
        ),
        check_vma=False,
    )
```

profile of v0, /device:TPU:1, one launch (start us, length us, event | category | flops | bytes accessed | tf_op | source)
XLA Modules:
  0.0 2553.1 jit_solution(11796390207512047480)
XLA Ops:
  17.4 41.7 %all-reduce.7 = (bf16[1536]{0:T(1024)(128)(2,1)S(1)}, bf16[1536]{0:T(1024)(128)(2,1)S(1)}) all-reduce(bf16[1536]{0:T(1024)(128)(2,1)S(1)} %dynamic-update-slice, bf16[1536]{0:T(1024)(128)(2,1)S(1)} %dynamic-update-slice.1), channel_id=1, replica_groups=mesh['seq'=2,'dp'=16] {'seq','dp'}, use_global_device_ids=true, to_apply=%add.2 | all-reduce | flops 3072 | bytes 12288
  76.4 50.0 %all-gather.11.cloned.1.call-done = bf16[1536,512]{1,0:T(8,128)(2,1)} async-done(((bf16[48,512]{1,0:T(8,128)(2,1)}), bf16[1536,512]{1,0:T(8,128)(2,1)}) %all-gather.11.cloned.1.call-update) | async-done | bytes 1572880 | tf_op jit(solution)/shard_map/all_gather | solution.py:75
  129.7 62.0 %all-gather.7.cloned.1.call-done = bf16[1536,1536]{1,0:T(8,128)(2,1)} async-done(((bf16[48,1536]{1,0:T(8,128)(2,1)}), bf16[1536,1536]{1,0:T(8,128)(2,1)}) %all-gather.7.cloned.1.call-update) | async-done | bytes 4718608 | tf_op jit(solution)/shard_map/all_gather | solution.py:73
  191.7 6.7 fusion.95
  205.7 5.3 all-to-all-done.2
  211.1 4.9 all-to-all-start
  221.7 17.4 all-to-all-done
  240.3 74.2 %while.27 = (s32[]{:T(128)}, bf16[2,512,768]{1,2,0:T(8,128)(2,1)}, f32[2,4,3,512,1]{3,2,1,4,0:T(4,128)S(1)}, s32[2,512]{1,0:T(2,128)S(1)}, s32[1024]{0:T(1024)S(...) while((s32[]{:T(128)}, bf16[2,512,768]{1,2,0:T(8,128)(2,1)}, ...), condition=%wide.region_7.8_spmd, body=%wide.region_4.7_spmd.sunk | while | flops 1688070144 | bytes 83604080 | solution.py:153
  242.0 10.6 bitcast_reduce_fusion.2
  252.6 12.0 fusion.147
  264.6 12.0 fusion.148
  279.3 10.5 bitcast_reduce_fusion.2
  289.7 11.8 fusion.147
  301.5 12.0 fusion.148
  319.4 15.7 scatter_custom_fusion
  337.4 5.4 multiply_reduce_fusion.2
  344.9 23.8 gather_fusion
  368.7 7.2 all-to-all-start.4
  376.3 15.5 scatter_custom_fusion.1
  392.6 25.6 %gather_fusion.2 = f32[5120,1536]{1,0:T(8,128)} fusion(f32[513,1536]{1,0:T(8,128)S(1)} %concatenate.37, s32[5120]{0:T(1024)S(1)} %fusion.69), kind=kCustom, calls=%fused_computation.2 | custom fusion | bytes 62935040 | tf_op jit(solution)/shard_map/gather | solution.py:205
  418.2 16.7 multiply_convert_fusion.1
  434.9 220.0 %all-to-all-done.4 = bf16[16,320,1536]{2,1,0:T(8,128)(2,1)} async-done(((bf16[16,320,1536]{2,1,0:T(8,128)(2,1)}), bf16[16,320,1536]{2,1,0:T(8,128)(2,1)}, u32[]{:S(2)}, u32[]{:S(2)}) %all-to-all-start.4) | async-done | bytes 15728672 | tf_op jit(solution)/shard_map/all_to_all | solution.py:188
  654.9 65.6 %all-to-all-start.6 = ((bf16[16,320,1536]{2,1,0:T(8,128)(2,1)}), bf16[16,320,1536]{2,1,0:T(8,128)(2,1)}, u32[]{:S(2)}, u32[]{:S(2)}) async-start(bf16[16,320,1536]{2,1,0:T(8,128)(2,1)} %multiply_convert_fusion.1), calls=%async_computation.6 | async-start | bytes 31457280 | tf_op jit(solution)/shard_map/all_to_all | solution.py:207
  721.1 8.8 all-gather.17.cloned.1.call-start
  729.9 37.1 %all-gather.15.cloned.1.call-done = bf16[1,1536,1024]{2,1,0:T(8,128)(2,1)} async-done(((bf16[1,1536,512]{2,1,0:T(8,128)(2,1)}), bf16[1,1536,1024]{2,1,0:T(8,128)(2,1)}) %all-gather.15.cloned.1.call-update) | async-done | bytes 3145744 | tf_op jit(solution)/shard_map/all_gather | solution.py:81
  767.0 22.7 convolution_bitcast_fusion.1
  789.7 5.8 all-gather.17.cloned.1.call-done
  795.5 203.9 %all-to-all-done.6 = bf16[16,320,1536]{2,1,0:T(8,128)(2,1)} async-done(((bf16[16,320,1536]{2,1,0:T(8,128)(2,1)}), bf16[16,320,1536]{2,1,0:T(8,128)(2,1)}, u32[]{:S(2)}, u32[]{:S(2)}) %all-to-all-start.6) | async-done | bytes 15728672 | tf_op jit(solution)/shard_map/all_to_all | solution.py:207
  999.4 23.5 fusion.44
  1022.9 13.8 convolution_convert_fusion
  1036.6 65.9 %all-to-all-start.5 = ((bf16[16,320,1536]{2,1,0:T(8,128)(2,1)}), bf16[16,320,1536]{2,1,0:T(8,128)(2,1)}, u32[]{:S(2)}, u32[]{:S(2)}) async-start(bf16[16,320,1536]{2,1,0:T(8,128)(2,1)} %bitcast.324), calls=%async_computation.5 | async-start | bytes 31457280 | tf_op jit(solution)/shard_map/all_to_all | solution.py:194
  1102.5 23.6 convolution_convert_fusion.1
  1126.1 255.3 %all-to-all-done.5 = bf16[16,320,1536]{2,1,0:T(8,128)(2,1)} async-done(((bf16[16,320,1536]{2,1,0:T(8,128)(2,1)}), bf16[16,320,1536]{2,1,0:T(8,128)(2,1)}, u32[]{:S(2)}, u32[]{:S(2)}) %all-to-all-start.5) | async-done | bytes 15728672 | tf_op jit(solution)/shard_map/all_to_all | solution.py:194
  1381.4 65.8 %all-to-all-start.7 = ((bf16[16,320,1536]{2,1,0:T(8,128)(2,1)}), bf16[16,320,1536]{2,1,0:T(8,128)(2,1)}, u32[]{:S(2)}, u32[]{:S(2)}) async-start(bf16[16,320,1536]{2,1,0:T(8,128)(2,1)} %bitcast.323), calls=%async_computation.7 | async-start | bytes 31457280 | tf_op jit(solution)/shard_map/all_to_all | solution.py:237
  1447.3 14.1 fusion.59
  1461.5 32.8 %gather_fusion.1 = bf16[4096,1536]{1,0:T(8,128)(2,1)} fusion(bf16[5120,1536]{1,0:T(8,128)(2,1)} %bitcast.36, s32[4096]{0:T(1024)S(1)} %broadcast_clamp_fusion), kind=kCustom, calls=%fused_computation.1 | custom fusion | bytes 25182208 | tf_op jit(solution)/shard_map/gather | solution.py:197
  1494.3 29.6 %fusion.33 = f32[512,1536]{1,0:T(8,128)S(1)} fusion(bf16[4096,1536]{1,0:T(8,128)(2,1)} %gather_fusion.1, f32[512,8]{1,0:T(8,128)S(1)} %copy-done.18), kind=kLoop, calls=%fused_computation.59 | loop fusion | flops 18087936 | bytes 15745024 | tf_op jit(solution)/shard_map/reduce_sum | solution.py:198
  1523.9 202.2 %all-to-all-done.7 = bf16[16,320,1536]{2,1,0:T(8,128)(2,1)} async-done(((bf16[16,320,1536]{2,1,0:T(8,128)(2,1)}), bf16[16,320,1536]{2,1,0:T(8,128)(2,1)}, u32[]{:S(2)}, u32[]{:S(2)}) %all-to-all-start.7) | async-done | bytes 15728672 | tf_op jit(solution)/shard_map/all_to_all | solution.py:237
  1726.1 32.8 %gather_fusion.3 = bf16[4096,1536]{1,0:T(8,128)(2,1)} fusion(bf16[5120,1536]{1,0:T(8,128)(2,1)} %bitcast.44, s32[4096]{0:T(1024)S(1)} %broadcast_clamp_fusion), kind=kCustom, calls=%fused_computation.3 | custom fusion | bytes 25182208 | tf_op jit(solution)/shard_map/gather | solution.py:241
  1758.9 10.7 convert_reduce_fusion
  1783.0 22.3 fusion.48
  1806.7 173.2 %while.28 = (s32[]{:T(128)}, f32[1024,4,64]{0,2,1:T(8,128)}, f32[1024,4,64]{0,2,1:T(8,128)}, bf16[2,512,768]{1,2,0:T(8,128)(2,1)}, bf16[2,512,768]{1,2,0:T(8,128...) while((s32[]{:T(128)}, f32[1024,4,64]{0,2,1:T(8,128)}, ...), condition=%wide.region_21.22_spmd.clone, body=%wide.region_19.21_spmd.clone.sunk | while | flops 4124567552 | bytes 218034928 | solution.py:295
  1809.8 10.1 fusion.158
  1819.8 21.7 fusion.159
  1841.5 21.3 fusion.160
  1862.8 8.5 multiply_convert_fusion.8
  1872.2 8.6 fusion.161
  1880.8 12.7 fusion.162
  1896.1 10.2 fusion.158
  1906.3 21.7 fusion.159
  1928.1 21.3 fusion.160
  1949.3 8.5 multiply_convert_fusion.8
  1958.8 8.1 fusion.161
  1966.9 12.8 fusion.162
  1981.7 10.1 all_to_all.131
  1997.6 9.0 all_to_all.132
  2010.4 8.6 fusion.65
  2020.4 19.4 all_to_all.133
  2041.0 5.4 fusion.90
  2062.2 103.2 %all-reduce.6 = (f32[1536]{0:T(1024)S(1)}, f32[1536]{0:T(1024)S(1)}) all-reduce(f32[1536]{0:T(1024)S(1)} %get-tuple-element.181, f32[1536]{0:T(1024)S(1)} %copy-done.47), channel_id=6, replica_groups=mesh['seq'=2,'dp'=16] {'seq','dp'}, use_global_device_ids=true, to_apply=%region_28.29.clone | all-reduce | flops 3072 | bytes 24576
  2166.6 5.3 fusion.51
  2171.9 91.0 %reduce-scatter.11.cloned.1.call-done = f32[48,512]{1,0:T(8,128)} async-done(((f32[1536,512]{1,0:T(8,128)}), f32[48,512]{1,0:T(8,128)}) %reduce-scatter.11.cloned.1.call-update) | async-done | bytes 98320 | tf_op jit(solution)/shard_map/reduce_scatter | solution.py:338
  2262.9 141.1 %reduce-scatter.13.cloned.1.call-done = f32[48,1536]{1,0:T(8,128)} async-done(((f32[1536,1536]{1,0:T(8,128)}), f32[48,1536]{1,0:T(8,128)}) %reduce-scatter.13.cloned.1.call-update) | async-done | bytes 294928 | tf_op jit(solution)/shard_map/reduce_scatter | solution.py:339
  2403.9 141.9 %reduce-scatter.7.cloned.1.call-done = f32[48,1536]{1,0:T(8,128)} async-done(((f32[1536,1536]{1,0:T(8,128)}), f32[48,1536]{1,0:T(8,128)}) %reduce-scatter.7.cloned.1.call-update) | async-done | bytes 294928 | tf_op jit(solution)/shard_map/reduce_scatter | solution.py:336
  (264 shorter events, 112.6 us)
Async XLA Ops:
  8.0 61.3 %copy-start.2 = (bf16[512,1536]{1,0:T(8,128)(2,1)S(1)}, bf16[512,1536]{1,0:T(8,128)(2,1)}, u32[]{:S(2)}) copy-start(bf16[512,1536]{1,0:T(8,128)(2,1)} %param.18) | copy-start | bytes 4718596
  8.0 61.3 %all-gather.9.cloned.1.call-start = ((), (), s32[]{:S(2)}) async-start(), calls=%async_computation.19 | async-start | bytes 1622016 | tf_op jit(solution)/shard_map/all_gather | solution.py:74
  8.8 117.6 %all-gather.11.cloned.1.call-start = ((), (), s32[]{:S(2)}) async-start(), calls=%async_computation.20 | async-start | bytes 1622016 | tf_op jit(solution)/shard_map/all_gather | solution.py:75
  9.5 182.2 %all-gather.7.cloned.1.call-start = ((), (), s32[]{:S(2)}) async-start(), calls=%async_computation.18 | async-start | bytes 4866048 | tf_op jit(solution)/shard_map/all_gather | solution.py:73
  10.2 324.9 %all-gather.13.cloned.1.call-start = ((), (), s32[]{:S(2)}) async-start(), calls=%async_computation.21 | async-start | bytes 4866048 | tf_op jit(solution)/shard_map/all_gather | solution.py:76
  59.1 132.6 %copy-start.25 = (f32[1536]{0:T(1024)}, f32[1536]{0:T(1024)S(1)}, u32[]{:S(2)}) copy-start(f32[1536]{0:T(1024)S(1)} %convert_element_type.190) | copy-start | bytes 18436
  60.9 7.2 copy-start.48
  60.9 130.8 %copy-start.39 = (f32[512]{0:T(512)}, f32[512]{0:T(512)S(1)}, u32[]{:S(2)}) copy-start(f32[512]{0:T(512)S(1)} %fusion.79) | copy-start | bytes 6148
  69.1 132.9 %copy-start.19 = (f32[512,32]{0,1:T(8,128)}, f32[512,32]{0,1:T(8,128)S(1)}, u32[]{:S(2)}) copy-start(f32[512,32]{0,1:T(8,128)S(1)} %get-tuple-element.258) | copy-start | bytes 196612
  72.9 125.6 %all-to-all-start.1 = ((bf16[512,2,256]{0,2,1:T(8,128)(2,1)}), bf16[512,2,256]{0,2,1:T(8,128)(2,1)S(1)}, u32[]{:S(2)}, u32[]{:S(2)}) async-start(bf16[512,2,256]{0,2,1:T(8,128)(2,1)} %bitcast.20), calls=%async_computation.1 | async-start | bytes 1048576 | tf_op jit(solution)/shard_map/all_to_all | solution.py:106
  198.5 12.6 all-to-all-start.2
  211.1 28.0 %all-to-all-start = ((bf16[512,2,768]{0,2,1:T(8,128)(2,1)}), bf16[512,2,768]{0,2,1:T(8,128)(2,1)}, u32[]{:S(2)}, u32[]{:S(2)}) async-start(bf16[512,2,768]{0,2,1:T(8,128)(2,1)} %bitcast.17), calls=%async_computation | async-start | bytes 3145728 | tf_op jit(solution)/shard_map/all_to_all | solution.py:105
  314.4 28.3 %copy-start = (bf16[1024,4,64]{0,2,1:T(8,128)(2,1)}, bf16[1024,4,64]{0,2,1:T(8,128)(2,1)S(1)}, u32[]{:S(2)}) copy-start(bf16[1024,4,64]{0,2,1:T(8,128)(2,1)S(1)} %get-tuple-element.512) | copy-start | bytes 1572868
  314.5 28.3 %copy-start.23 = (s32[1024]{0:T(1024)}, s32[1024]{0:T(1024)S(1)}, u32[]{:S(2)}) copy-start(s32[1024]{0:T(1024)S(1)} %get-tuple-element.546) | copy-start | bytes 12292
  314.5 28.3 %copy-start.28 = (s32[1024]{0:T(1024)}, s32[1024]{0:T(1024)S(1)}, u32[]{:S(2)}) copy-start(s32[1024]{0:T(1024)S(1)} %get-tuple-element.547) | copy-start | bytes 12292
  314.5 28.3 %copy-start.30 = (f32[2,4,3,512,1]{3,2,1,4,0:T(4,128)}, f32[2,4,3,512,1]{3,2,1,4,0:T(4,128)S(1)}, u32[]{:S(2)}) copy-start(f32[2,4,3,512,1]{3,2,1,4,0:T(4,128)S(1)} %get-tuple-element.465) | copy-start | bytes 147460
  314.5 28.3 %copy-start.32 = (s32[2,512]{1,0:T(2,128)}, s32[2,512]{1,0:T(2,128)S(1)}, u32[]{:S(2)}) copy-start(s32[2,512]{1,0:T(2,128)S(1)} %get-tuple-element.548) | copy-start | bytes 12292
  314.5 28.3 %copy-start.34 = (s32[2,512]{1,0:T(2,128)}, s32[2,512]{1,0:T(2,128)S(1)}, u32[]{:S(2)}) copy-start(s32[2,512]{1,0:T(2,128)S(1)} %get-tuple-element.549) | copy-start | bytes 12292
  314.5 4.9 copy-start.41
  314.5 4.9 copy-start.44
  314.5 22.9 copy-start.3
  314.5 22.8 all-to-all-start.3
  319.4 56.9 %copy-start.42 = (s32[4096,1]{0,1:T(1,128)}, s32[4096,1]{0,1:T(1,128)S(1)}, u32[]{:S(2)}) copy-start(s32[4096,1]{0,1:T(1,128)S(1)} %compare_select_fusion) | copy-start | bytes 49156
  337.4 7.1 copy-start.37
  342.8 1.7 copy-start.5
  342.8 2.1 copy-start.50
  342.8 2.1 copy-start.45
  368.7 7.2 copy-start.36
  368.7 23.2 copy-start.11
  368.7 286.2 %all-to-all-start.4 = ((bf16[16,320,1536]{2,1,0:T(8,128)(2,1)}), bf16[16,320,1536]{2,1,0:T(8,128)(2,1)}, u32[]{:S(2)}, u32[]{:S(2)}) async-start(bf16[16,320,1536]{2,1,0:T(8,128)(2,1)} %bitcast.320), calls=%async_computation.4 | async-start | bytes 31457280 | tf_op jit(solution)/shard_map/all_to_all | solution.py:188
  376.1 15.8 copy-start.17
  654.9 344.5 %all-to-all-start.6 = ((bf16[16,320,1536]{2,1,0:T(8,128)(2,1)}), bf16[16,320,1536]{2,1,0:T(8,128)(2,1)}, u32[]{:S(2)}, u32[]{:S(2)}) async-start(bf16[16,320,1536]{2,1,0:T(8,128)(2,1)} %multiply_convert_fusion.1), calls=%async_computation.6 | async-start | bytes 31457280 | tf_op jit(solution)/shard_map/all_to_all | solution.py:207
  720.5 46.5 %all-gather.15.cloned.1.call-start = ((), (), s32[]{:S(2)}) async-start(), calls=%async_computation.22 | async-start | bytes 4718592 | tf_op jit(solution)/shard_map/all_gather | solution.py:81
  721.1 74.4 %all-gather.17.cloned.1.call-start = ((), (), s32[]{:S(2)}) async-start(), calls=%async_computation.23 | async-start | bytes 2359296 | tf_op jit(solution)/shard_map/all_gather | solution.py:82
  999.4 23.5 copy-start.53
  1036.6 65.9 %copy-start.52 = (bf16[1,1536,1024]{2,1,0:T(8,128)(2,1)S(1)}, bf16[1,1536,1024]{2,1,0:T(8,128)(2,1)}, u32[]{:S(2)}) copy-start(bf16[1,1536,1024]{2,1,0:T(8,128)(2,1)} %all-gather.15.cloned.1.call-done) | copy-start | bytes 9437188
  1036.6 344.8 %all-to-all-start.5 = ((bf16[16,320,1536]{2,1,0:T(8,128)(2,1)}), bf16[16,320,1536]{2,1,0:T(8,128)(2,1)}, u32[]{:S(2)}, u32[]{:S(2)}) async-start(bf16[16,320,1536]{2,1,0:T(8,128)(2,1)} %bitcast.324), calls=%async_computation.5 | async-start | bytes 31457280 | tf_op jit(solution)/shard_map/all_to_all | solution.py:194
  1381.4 65.8 %copy-start.43 = (s32[4096,1]{0,1:T(1,128)S(1)}, s32[4096,1]{0,1:T(1,128)}, u32[]{:S(2)}) copy-start(s32[4096,1]{0,1:T(1,128)} %copy-done.42) | copy-start | bytes 49156
  1381.4 344.7 %all-to-all-start.7 = ((bf16[16,320,1536]{2,1,0:T(8,128)(2,1)}), bf16[16,320,1536]{2,1,0:T(8,128)(2,1)}, u32[]{:S(2)}, u32[]{:S(2)}) async-start(bf16[16,320,1536]{2,1,0:T(8,128)(2,1)} %bitcast.323), calls=%async_computation.7 | async-start | bytes 31457280 | tf_op jit(solution)/shard_map/all_to_all | solution.py:237
  1447.2 599.3 %reduce-scatter.17.cloned.1.call-start = ((), (), s32[]{:S(2)}) async-start(), calls=%async_computation.29 | async-start | bytes 2359296 | tf_op jit(solution)/shard_map/reduce_scatter | solution.py:247
  1461.5 32.8 %copy-start.18 = (f32[512,8]{1,0:T(8,128)S(1)}, f32[512,8]{1,0:T(8,128)}, u32[]{:S(2)}) copy-start(f32[512,8]{1,0:T(8,128)} %copy-done.17) | copy-start | bytes 49156
  1758.9 10.7 copy-start.6
  1758.9 10.7 copy-start.38
  1758.9 10.7 copy-start.46
  1769.6 5.4 slice-start
  1771.0 4.0 slice-start.1
  1773.3 1.7 copy-start.7
  1779.2 26.2 %all-to-all-start.8 = ((bf16[512,2,768]{0,2,1:T(8,128)(2,1)}), bf16[512,2,768]{0,2,1:T(8,128)(2,1)S(1)}, u32[]{:S(2)}, u32[]{:S(2)}) async-start(bf16[512,2,768]{0,2,1:T(8,128)(2,1)} %bitcast.326), calls=%async_computation.8 | async-start | bytes 3145728 | tf_op jit(solution)/shard_map/all_to_all | solution.py:261
  1782.9 266.0 %reduce-scatter.15.cloned.1.call-start = ((), (), s32[]{:S(2)}) async-start(), calls=%async_computation.28 | async-start | bytes 4718592 | tf_op jit(solution)/shard_map/reduce_scatter | solution.py:244
  1805.3 366.6 %reduce-scatter.9.cloned.1.call-start = ((), (), s32[]{:S(2)}) async-start(), calls=%async_computation.25 | async-start | bytes 3244032 | tf_op jit(solution)/shard_map/reduce_scatter | solution.py:337
  1880.8 12.7 copy-start.9
  1966.9 12.8 copy-start.9
  1979.9 12.1 copy-start.20
  1979.9 12.1 copy-start.27
  1981.6 11.4 copy-start.4
  1981.6 11.4 copy-start.26
  1981.6 11.3 copy-start.40
  1995.9 267.0 %reduce-scatter.11.cloned.1.call-start = ((), (), s32[]{:S(2)}) async-start(), calls=%async_computation.26 | async-start | bytes 3244032 | tf_op jit(solution)/shard_map/reduce_scatter | solution.py:338
  2010.4 393.5 %reduce-scatter.13.cloned.1.call-start = ((), (), s32[]{:S(2)}) async-start(), calls=%async_computation.27 | async-start | bytes 9732096 | tf_op jit(solution)/shard_map/reduce_scatter | solution.py:339
  2019.0 526.8 %reduce-scatter.7.cloned.1.call-start = ((), (), s32[]{:S(2)}) async-start(), calls=%async_computation.24 | async-start | bytes 9732096 | tf_op jit(solution)/shard_map/reduce_scatter | solution.py:336
  2052.5 4.7 copy-start.14
  2052.5 4.7 copy-start.21
  2058.8 3.4 copy-start.47
  2058.8 107.8 %copy-start.49 = (f32[512]{0:T(512)S(1)}, f32[512]{0:T(512)}, u32[]{:S(2)}) copy-start(f32[512]{0:T(512)} %copy-done.48) | copy-start | bytes 6148
  (15 other events, 19.0 us)
Sparse Core Ops, SparseCore 0:
  11.7 57.5 all-gather.8
  72.2 54.1 all-gather.10
  129.3 62.3 all-gather.6
  194.5 65.2 all-gather.12
Sparse Core Ops, SparseCore 1:
  722.5 44.5 all-gather.14
  768.4 27.0 all-gather.16
  1461.6 25.7 reduce-scatter.16
  1805.4 103.9 reduce-scatter.14
  1995.9 160.3 reduce-scatter.8
  2162.3 100.5 reduce-scatter.10
  2269.2 134.7 reduce-scatter.12
  2411.3 134.5 reduce-scatter.6
where the time goes:
time: 2570 us; the launch traced here: 2550 us
  waiting for transfers between devices  1440 us (56%)
  matrix products  337 us (13%)
  starting transfers between devices  234 us (9%)
  blocking collectives  183 us (7%)
  local copies, waits for them, and re-layouts  178 us (7%)
  other arithmetic  165 us (6%)
    all_to_all x1, waiting for transfers between devices, shards(): lax.all_to_all(home_layout(result), 'dp', split_axis=0, concat_axis=0, ti...  255 us
    all_to_all x1, waiting for transfers between devices, shards(): lax.all_to_all(outgoing, 'dp', split_axis=0, concat_axis=0, tiled=True)  220 us
    all_to_all x1, waiting for transfers between devices, shards(): lax.all_to_all(grad_slots.reshape(data_count, local_experts * capacity, w...  204 us
    all_to_all x1, waiting for transfers between devices, shards(): lax.all_to_all(home_layout(grad_rows), 'dp', split_axis=0, concat_axis=0,...  202 us
    unnamed x2, blocking collectives  145 us
    reduce_scatter x1, waiting for transfers between devices, shards(): lax.psum_scatter(grad_w_query, ('seq', 'dp'), scatter_dimension=0, tiled=...  142 us
    reduce_scatter x1, waiting for transfers between devices, shards(): lax.psum_scatter(grad_w_output, ('seq', 'dp'), scatter_dimension=0, tiled...  141 us
    reduce_scatter x1, waiting for transfers between devices, shards(): lax.psum_scatter(grad_w_value, ('seq', 'dp'), scatter_dimension=0, tiled=...  91 us
  transfers between devices with their start and end apart: 21, of which 15 were waited for; matrix products, arithmetic and copies ran while one was open for 24% of the time, Pallas kernels for 0%

commit v1 on v0

--- a/solution.py
+++ b/solution.py
@@ -1,6 +1,8 @@
 import jax
 import jax.numpy as jnp
 from jax import lax
+from jax.experimental import pallas as pl
+from jax.experimental.pallas import tpu as pltpu
 from jax.sharding import PartitionSpec as P
 
 QHEADS = 24
@@ -42,7 +44,7 @@
     )
 
 
-def shards(
+def shards_general(
     tokens,
     cotangent,
     positions,
@@ -354,6 +356,651 @@
     )
 
 
+BF16 = jnp.bfloat16
+F32 = jnp.float32
+LINE = 4
+VMEM_BYTES = 60 * 1024 * 1024
+
+
+def in_planes(mesh):
+    return mesh.shape["seq"] == 2 and mesh.shape["dp"] == 4 * LINE
+
+
+def swap_seq(value):
+    return lax.ppermute(value, "seq", [(0, 1), (1, 0)])
+
+
+def swap_dp(value, mask):
+    return lax.ppermute(value, "dp", [(i, i ^ mask) for i in range(4 * LINE)])
+
+
+def swap_core(value):
+    return swap_dp(value, 1)
+
+
+def swap_y(value):
+    return swap_dp(value, 2)
+
+
+def line_up(value):
+    return lax.ppermute(value, "dp", [(i, i + 4) for i in range(4 * LINE - 4)])
+
+
+def line_down(value):
+    return lax.ppermute(value, "dp", [(i, i - 4) for i in range(4, 4 * LINE)])
+
+
+def sum_everywhere(value):
+    for mask in (1, 2, 4, 8):
+        value = value + swap_dp(value, mask)
+    return value + swap_seq(value)
+
+
+def line_gather(own):
+    ups, downs = [own], [own]
+    for _ in range(LINE - 1):
+        ups.append(line_up(ups[-1]))
+        downs.append(line_down(downs[-1]))
+    return ups[:0:-1] + [own] + downs[1:]
+
+
+def line_scatter(take, place):
+    up = down = None
+    for step in range(LINE - 1):
+        far = jnp.minimum(LINE - 1 - step + place, LINE - 1)
+        near = jnp.maximum(step - LINE + 1 + place, 0)
+        right, left = take(far), take(near)
+        if up is not None:
+            right = right + up.astype(F32)
+            left = left + down.astype(F32)
+        up = line_up(right.astype(BF16))
+        down = line_down(left.astype(BF16))
+    return take(place) + up.astype(F32) + down.astype(F32)
+
+
+def plane_gather(value, axis):
+    half = value.shape[axis] // 2
+    first = lax.slice_in_dim(value, 0, half, axis=axis)
+    second = lax.slice_in_dim(value, half, 2 * half, axis=axis)
+
+    def join(*pieces):
+        return lax.concatenate(pieces, axis)
+
+    first_near = swap_seq(first)
+    second_near = swap_y(second)
+    near = join(first_near, second_near)
+    far = join(
+        swap_y(first), swap_y(first_near), swap_seq(second), swap_seq(second_near)
+    )
+    return [
+        join(value, swap_core(value)),
+        join(near, swap_core(near)),
+        join(far, swap_core(far)),
+    ]
+
+
+def plane_scatter(pieces):
+    def over_cores(piece):
+        half = piece.shape[0] // 2
+        return piece[:half].astype(F32) + swap_core(piece[half:]).astype(F32)
+
+    far = over_cores(pieces[2]).astype(BF16)
+    near = over_cores(pieces[1])
+    own = over_cores(pieces[0])
+    half = own.shape[0] // 2
+    own_first = own[:half] + swap_y(far[:half]).astype(F32)
+    near_first = near[:half] + swap_y(far[half : 2 * half]).astype(F32)
+    own_second = own[half:] + swap_seq(far[2 * half : 3 * half]).astype(F32)
+    near_second = near[half:] + swap_seq(far[3 * half :]).astype(F32)
+    own_first = own_first + swap_seq(near_first.astype(BF16)).astype(F32)
+    own_second = own_second + swap_y(near_second.astype(BF16)).astype(F32)
+    return jnp.concatenate([own_first, own_second], axis=0)
+
+
+def turned(values, cos, sin, direction):
+    lanes = values.shape[1]
+    place = lax.broadcasted_iota(jnp.int32, values.shape, 1) % HDIM
+    swapped = jnp.where(
+        place < HDIM // 2,
+        pltpu.roll(values, lanes - HDIM // 2, 1),
+        pltpu.roll(values, HDIM // 2, 1),
+    )
+    times = lanes // cos.shape[1]
+    cos = jnp.concatenate([cos] * times, axis=1)
+    sin = jnp.concatenate([sin] * times, axis=1)
+    if direction > 0:
+        return values * cos + swapped * sin
+    return values * cos - swapped * sin
+
+
+def qkv_kernel(x_ref, gain_ref, w_ref, cos_ref, sin_ref, h_ref, q_ref, k_ref, v_ref):
+    value = x_ref[...].astype(F32)
+    scale = lax.rsqrt(jnp.mean(value * value, axis=-1, keepdims=True) + EPSILON)
+    normed = (value * scale * gain_ref[...]).astype(BF16)
+    h_ref[...] = normed
+    both = jnp.dot(normed, w_ref[...], preferred_element_type=F32)
+    q_width, kv_heads = q_ref.shape[1], k_ref.shape[0]
+    kv_width = kv_heads * HDIM
+    spun = turned(both[:, : q_width + kv_width], cos_ref[...], sin_ref[...], 1)
+    q_ref[...] = (spun[:, :q_width] * SCORE_SCALE).astype(BF16)
+    for head in range(kv_heads):
+        low = q_width + head * HDIM
+        k_ref[head] = spun[:, low : low + HDIM].astype(BF16)
+        low = low + kv_width
+        v_ref[head] = both[:, low : low + HDIM].astype(BF16)
+
+
+def project(x_sorted, gain, weights, cos, sin, q_width, kv_heads):
+    rows, width = x_sorted.shape
+    tile = 256
+    columns = weights.shape[1]
+
+    def row_block(lanes):
+        return pl.BlockSpec((tile, lanes), lambda i: (i, 0))
+
+    heads = pl.BlockSpec((kv_heads, tile, HDIM), lambda i: (0, i, 0))
+    return pl.pallas_call(
+        qkv_kernel,
+        grid=(rows // tile,),
+        in_specs=[
+            row_block(width),
+            pl.BlockSpec((1, width), lambda i: (0, 0)),
+            pl.BlockSpec((width, columns), lambda i: (0, 0)),
+            row_block(cos.shape[1]),
+            row_block(cos.shape[1]),
+        ],
+        out_specs=[row_block(width), row_block(q_width), heads, heads],
+        out_shape=[
+            jax.ShapeDtypeStruct((rows, width), BF16),
+            jax.ShapeDtypeStruct((rows, q_width), BF16),
+            jax.ShapeDtypeStruct((kv_heads, rows, HDIM), BF16),
+            jax.ShapeDtypeStruct((kv_heads, rows, HDIM), BF16),
+        ],
+        compiler_params=pltpu.CompilerParams(vmem_limit_bytes=VMEM_BYTES),
+        cost_estimate=pl.CostEstimate(
+            flops=2 * rows * width * columns,
+            bytes_accessed=2 * (2 * rows * width + width * columns + rows * columns),
+            transcendentals=rows,
+        ),
+        name="project",
+    )(x_sorted, gain, weights, cos, sin)
+
+
+Q_TILE = 256
+
+
+def windows(rows):
+    longest = rows // 2
+    for start in range(0, rows, Q_TILE):
+        low = max(0, start - longest + 1) // Q_TILE * Q_TILE
+        yield start, low, start + Q_TILE
+
+
+def allowed_keys(start_ref, row, low, high):
+    shape = (Q_TILE, high - low)
+    rows = lax.broadcasted_iota(jnp.int32, shape, 0) + row
+    keys = lax.broadcasted_iota(jnp.int32, shape, 1) + low
+    return (keys <= rows) & (keys >= start_ref[row : row + Q_TILE, :])
+
+
+def contract(left, right, left_dim, right_dim):
+    return lax.dot_general(
+        left, right, (((left_dim,), (right_dim,)), ((), ())), preferred_element_type=F32
+    )
+
+
+def probabilities(query, keys, allowed):
+    scores = jnp.where(allowed, contract(query, keys, 1, 1), -1e30)
+    expon = jnp.exp(scores - jnp.max(scores, axis=-1, keepdims=True))
+    return expon * (1.0 / jnp.sum(expon, axis=-1, keepdims=True))
+
+
+def attend_kernel(q_ref, k_ref, v_ref, start_ref, o_ref):
+    pair = pl.program_id(0)
+    ratio = QHEADS // KVHEADS
+    for row, low, high in windows(q_ref.shape[0]):
+        allowed = allowed_keys(start_ref, row, low, high)
+        for side in range(2):
+            head = (2 * pair + side) // ratio
+            lanes = slice(side * HDIM, (side + 1) * HDIM)
+            probs = probabilities(
+                q_ref[row : row + Q_TILE, lanes], k_ref[head, low:high, :], allowed
+            )
+            mixed = contract(probs.astype(BF16), v_ref[head, low:high, :], 1, 0)
+            o_ref[row : row + Q_TILE, lanes] = mixed.astype(BF16)
+
+
+def attention_cost(rows, heads, products):
+    area = sum(Q_TILE * (high - low) for _, low, high in windows(rows))
+    return pl.CostEstimate(
+        flops=2 * products * heads * area * 128,
+        bytes_accessed=8 * rows * heads * HDIM,
+        transcendentals=heads * area,
+    )
+
+
+def attend(query, keys, values, starts):
+    rows, lanes = query.shape
+    pairs = lanes // (2 * HDIM)
+    pair_block = pl.BlockSpec((rows, 2 * HDIM), lambda j: (0, j))
+    whole = pl.BlockSpec(keys.shape, lambda j: (0, 0, 0))
+    return pl.pallas_call(
+        attend_kernel,
+        grid=(pairs,),
+        in_specs=[pair_block, whole, whole, pl.BlockSpec((rows, 1), lambda j: (0, 0))],
+        out_specs=pair_block,
+        out_shape=jax.ShapeDtypeStruct(query.shape, BF16),
+        compiler_params=pltpu.CompilerParams(vmem_limit_bytes=VMEM_BYTES),
+        cost_estimate=attention_cost(rows, 2 * pairs, 2),
+        name="attend",
+    )(query, keys, values, starts)
+
+
+def attend_back_kernel(
+    q_ref, k_ref, v_ref, d_ref, start_ref, cos_ref, sin_ref,
+    dq_ref, dk_ref, dv_ref, dk_sum, dv_sum,
+):
+    pair = pl.program_id(0)
+    ratio = QHEADS // KVHEADS
+
+    @pl.when(pair == 0)
+    def _():
+        dk_sum[...] = jnp.zeros_like(dk_sum)
+        dv_sum[...] = jnp.zeros_like(dv_sum)
+
+    for row, low, high in windows(q_ref.shape[0]):
+        allowed = allowed_keys(start_ref, row, low, high)
+        grads = []
+        for side in range(2):
+            head = (2 * pair + side) // ratio
+            lanes = slice(side * HDIM, (side + 1) * HDIM)
+            query = q_ref[row : row + Q_TILE, lanes]
+            keys = k_ref[head, low:high, :]
+            probs = probabilities(query, keys, allowed)
+            grad_out = d_ref[row : row + Q_TILE, lanes]
+            grad_probs = contract(grad_out, v_ref[head, low:high, :], 1, 1)
+            inner = jnp.sum(probs * grad_probs, axis=-1, keepdims=True)
+            grad_scores = (probs * (grad_probs - inner)).astype(BF16)
+            grads.append(contract(grad_scores, keys, 1, 0) * SCORE_SCALE)
+            dk_sum[head, low:high, :] += contract(grad_scores, query, 0, 0)
+            dv_sum[head, low:high, :] += contract(probs.astype(BF16), grad_out, 0, 0)
+        grad_query = jnp.concatenate(grads, axis=1).astype(BF16).astype(F32)
+        dq_ref[row : row + Q_TILE, :] = turned(
+            grad_query,
+            cos_ref[row : row + Q_TILE, :],
+            sin_ref[row : row + Q_TILE, :],
+            -1,
+        ).astype(BF16)
+
+    @pl.when(pair == pl.num_programs(0) - 1)
+    def _():
+        heads = range(dk_sum.shape[0])
+        grad_keys = jnp.concatenate([dk_sum[head] for head in heads], axis=1)
+        grad_keys = grad_keys.astype(BF16).astype(F32)
+        dk_ref[...] = turned(grad_keys, cos_ref[...], sin_ref[...], -1).astype(BF16)
+        dv_ref[...] = jnp.concatenate([dv_sum[head] for head in heads], axis=1).astype(BF16)
+
+
+def attend_back(query, keys, values, grad_out, starts, cos, sin):
+    rows, lanes = query.shape
+    pairs = lanes // (2 * HDIM)
+    kv_heads = keys.shape[0]
+    pair_block = pl.BlockSpec((rows, 2 * HDIM), lambda j: (0, j))
+    whole = pl.BlockSpec(keys.shape, lambda j: (0, 0, 0))
+
+    def fixed(lanes_of):
+        return pl.BlockSpec((rows, lanes_of), lambda j: (0, 0))
+
+    flat = kv_heads * HDIM
+    return pl.pallas_call(
+        attend_back_kernel,
+        grid=(pairs,),
+        in_specs=[
+            pair_block, whole, whole, pair_block, fixed(1), fixed(2 * HDIM), fixed(2 * HDIM),
+        ],
+        out_specs=[pair_block, fixed(flat), fixed(flat)],
+        out_shape=[
+            jax.ShapeDtypeStruct(query.shape, BF16),
+            jax.ShapeDtypeStruct((rows, flat), BF16),
+            jax.ShapeDtypeStruct((rows, flat), BF16),
+        ],
+        scratch_shapes=[pltpu.VMEM(keys.shape, F32), pltpu.VMEM(keys.shape, F32)],
+        compiler_params=pltpu.CompilerParams(vmem_limit_bytes=VMEM_BYTES),
+        cost_estimate=attention_cost(rows, 2 * pairs, 5),
+        name="attend_back",
+    )(query, keys, values, grad_out, starts, cos, sin)
+
+
+SLOTS = 2 * LINE - 1
+MOE_TILE = 512
+
+
+def experts_kernel(place_ref, *refs):
+    h_ref, g_ref, gate_ref = refs[:3]
+    in_slots, out_slots = refs[3 : 3 + SLOTS], refs[3 + SLOTS : 3 + 2 * SLOTS]
+    (
+        f_ref, dh_ref, hidden_ref, du_ref, hcopy_ref, gcopy_ref, w_in, w_out, sems,
+    ) = refs[-9:]
+    part = in_slots[0].shape[1]
+    half = part // 2
+
+    def copies(expert, slot):
+        return (
+            pltpu.make_async_copy(
+                in_slots[slot],
+                w_in.at[:, expert * part : (expert + 1) * part],
+                sems.at[0, expert],
+            ),
+            pltpu.make_async_copy(
+                out_slots[slot],
+                w_out.at[expert * half : (expert + 1) * half, :],
+                sems.at[1, expert],
+            ),
+        )
+
+    @pl.when(pl.program_id(0) == 0)
+    def _():
+        for expert in range(LINE):
+            for slot in range(expert, expert + LINE):
+
+                @pl.when(slot == LINE - 1 + expert - place_ref[0])
+                def _():
+                    for copy in copies(expert, slot):
+                        copy.start()
+
+        for expert in range(LINE):
+            for copy in copies(expert, LINE - 1):
+                copy.wait()
+
+    rows = h_ref[...]
+    grads = g_ref[...]
+    hcopy_ref[...] = rows
+    gcopy_ref[...] = grads
+    for expert in range(LINE):
+        both = jnp.dot(
+            rows, w_in[:, expert * part : (expert + 1) * part], preferred_element_type=F32
+        )
+        back = contract(grads, w_out[expert * half : (expert + 1) * half, :], 1, 1)
+        gate = gate_ref[:, expert : expert + 1]
+        first, second = both[:, :half], both[:, half:]
+        sigma = jax.nn.sigmoid(first)
+        silu = first * sigma
+        hidden_ref[:, expert * half : (expert + 1) * half] = (gate * (silu * second)).astype(BF16)
+        back = back * (BRANCH_SCALE * gate)
+        d_first = back * second * (sigma * (1.0 + first * (1.0 - sigma)))
+        d_second = back * silu
+        du_ref[:, expert * part : expert * part + half] = d_first.astype(BF16)
+        du_ref[:, expert * part + half : (expert + 1) * part] = d_second.astype(BF16)
+    f_ref[...] = jnp.dot(hidden_ref[...], w_out[...], preferred_element_type=F32).astype(BF16)
+    dh_ref[...] = contract(du_ref[...], w_in[...], 1, 1).astype(BF16)
+
+
+def run_experts(place, rows, grads, gates, in_slots, out_slots, total, offset, kept):
+    count, width = rows.shape
+    part, half = in_slots[0].shape[1], out_slots[0].shape[0]
+    tile = MOE_TILE
+    base = offset // tile
+
+    def block(lanes):
+        return pl.BlockSpec((tile, lanes), lambda i, p: (i, 0))
+
+    def late(lanes):
+        return pl.BlockSpec((tile, lanes), lambda i, p: (i + base, 0))
+
+    anywhere = pl.BlockSpec(memory_space=pl.ANY)
+    kept = list(kept)
+    lead = 4 + 2 * SLOTS
+    return pl.pallas_call(
+        experts_kernel,
+        grid_spec=pltpu.PrefetchScalarGridSpec(
+            num_scalar_prefetch=1,
+            grid=(count // tile,),
+            in_specs=[block(width), block(width), block(LINE)]
+            + [anywhere] * (2 * SLOTS + len(kept)),
+            out_specs=[
+                block(width), block(width),
+                late(LINE * half), late(LINE * part), late(width), late(width),
+            ],
+            scratch_shapes=[
+                pltpu.VMEM((width, LINE * part), BF16),
+                pltpu.VMEM((LINE * half, width), BF16),
+                pltpu.SemaphoreType.DMA((2, LINE)),
+            ],
+        ),
+        out_shape=[
+            jax.ShapeDtypeStruct((count, width), BF16),
+            jax.ShapeDtypeStruct((count, width), BF16),
+            jax.ShapeDtypeStruct((total, LINE * half), BF16),
+            jax.ShapeDtypeStruct((total, LINE * part), BF16),
+            jax.ShapeDtypeStruct((total, width), BF16),
+            jax.ShapeDtypeStruct((total, width), BF16),
+        ],
+        input_output_aliases={lead + i: 2 + i for i in range(len(kept))},
+        compiler_params=pltpu.CompilerParams(vmem_limit_bytes=VMEM_BYTES),
+        cost_estimate=pl.CostEstimate(
+            flops=2 * count * width * LINE * (2 * part + 2 * half),
+            bytes_accessed=2 * count * (6 * width + LINE * (part + half)),
+            transcendentals=count * LINE * half,
+        ),
+        name="experts",
+    )(place, rows, grads, gates, *in_slots, *out_slots, *kept)
+
+
+def norm_back(value, gain, grad):
+    scale = lax.rsqrt(jnp.mean(value * value, axis=-1, keepdims=True) + EPSILON)
+    unit = value * scale
+    grad_gain = jnp.sum(grad * unit, axis=0)
+    scaled = grad * gain
+    inner = jnp.mean(scaled * unit, axis=-1, keepdims=True)
+    return scale * (scaled - unit * inner), grad_gain
+
+
+def shards_plane(
+    tokens,
+    cotangent,
+    positions,
+    lengths,
+    routes,
+    logits,
+    w_query,
+    w_key,
+    w_value,
+    w_output,
+    gain_attn,
+    gain_ffn,
+    w_in,
+    w_out,
+):
+    seq = lax.axis_index("seq")
+    data = lax.axis_index("dp")
+    line, row_of, core = data // 4, (data // 2) % 2, data % 2
+    tok_count, width = tokens.shape
+    group_len = positions.shape[1]
+    shard = w_query.shape[0]
+    q_width = w_query.shape[1] // 2
+    kv_width = w_key.shape[1] // 2
+    kv_heads = kv_width // HDIM
+    first_seq = seq == 0
+
+    def ordered(mine, theirs, axis):
+        low = jnp.where(first_seq, mine, theirs)
+        high = jnp.where(first_seq, theirs, mine)
+        return jnp.concatenate([low, high], axis=axis)
+
+    def half_of(weights, which):
+        half = weights.shape[1] // 2
+        return lax.dynamic_slice_in_dim(weights, which * half, half, axis=1)
+
+    other_tokens = swap_seq(tokens)
+    projections = (w_query, w_key, w_value)
+    mine = jnp.concatenate([half_of(w, seq) for w in projections], axis=1)
+    theirs = jnp.concatenate([half_of(w, 1 - seq) for w in projections], axis=1)
+    theirs = swap_seq(theirs)
+    pair = jnp.stack([jnp.where(first_seq, mine, theirs), jnp.where(first_seq, theirs, mine)])
+    w_qkv = lax.all_gather(pair, "dp", axis=1, tiled=True).reshape(width, q_width + 2 * kv_width)
+    output_full = lax.all_gather(w_output, ("seq", "dp"), axis=0, tiled=True)
+
+    gains = jnp.stack([gain_attn, gain_ffn]).astype(F32)
+    index = seq * (4 * LINE) + data
+    gains = lax.dynamic_update_slice(jnp.zeros((2, width), F32), gains, (0, index * shard))
+    gains = sum_everywhere(gains)
+    gain_one, gain_two = gains[0], gains[1]
+
+    def both_axes(value, pairs):
+        return lax.ppermute(value, ("seq", "dp"), pairs)
+
+    def device(s, d):
+        return s * 4 * LINE + d
+
+    straight, crossed = [], []
+    for s in range(2):
+        for d in range(4 * LINE):
+            c = d % 2
+            straight.append((device(s, d), device(c, d - c + s)))
+            crossed.append((device(s, d), device(c, d - c + 1 - s)))
+    crossed_back = [(there, here) for here, there in crossed]
+    in_own = w_in[0]
+    half = in_own.shape[1] // 2
+    same = both_axes(lax.dynamic_slice_in_dim(in_own, seq * half, half, axis=1), straight)
+    cross = both_axes(lax.dynamic_slice_in_dim(in_own, (1 - seq) * half, half, axis=1), crossed)
+    first_core = core == 0
+    in_part = jnp.concatenate(
+        [jnp.where(first_core, same, cross), jnp.where(first_core, cross, same)], axis=1
+    )
+    out_part = both_axes(w_out[0], straight)
+    in_slots = line_gather(in_part)
+    out_slots = line_gather(out_part)
+
+    grad_pieces = plane_gather(cotangent, 0)
+    experts_all = 4 * LINE
+    gates = jax.nn.softmax(logits, axis=-1)
+    named = routes[None, :, :] == jnp.arange(experts_all, dtype=jnp.int32)[:, None, None]
+    gate_table = jnp.sum(jnp.where(named, gates[None], 0.0), axis=2)
+    gate_pieces = [
+        lax.dynamic_index_in_dim(
+            piece.reshape(LINE, 4, piece.shape[1]), 2 * row_of + seq, axis=1, keepdims=False
+        ).T
+        for piece in plane_gather(gate_table, 1)
+    ]
+
+    places = positions[0]
+    ends = jnp.cumsum(lengths[0])
+    ranks = jnp.arange(group_len, dtype=jnp.int32)
+    reached = ranks[:, None] >= ends[None, :]
+    starts = jnp.max(jnp.where(reached, ends[None, :], 0), axis=1)
+    local = (ranks - starts).astype(F32)
+    freqs = jnp.power(THETA, -jnp.arange(HDIM // 2, dtype=F32) * 2.0 / HDIM)
+    angles = local[:, None] * freqs[None, :]
+    cos, sin = jnp.cos(angles), jnp.sin(angles)
+    cos = jnp.concatenate([cos, cos, cos, cos], axis=1)
+    sin = jnp.concatenate([-sin, sin, -sin, sin], axis=1)
+    start_column = starts[:, None]
+    own_places = lax.dynamic_slice_in_dim(places, seq * tok_count, tok_count)
+    other_places = lax.dynamic_slice_in_dim(places, (1 - seq) * tok_count, tok_count)
+    sort_own = (ranks[:, None] == own_places[None, :]).astype(BF16)
+    sort_other = (ranks[:, None] == other_places[None, :]).astype(BF16)
+
+    def to_order(own, other):
+        return (
+            contract(sort_own, own, 1, 0) + contract(sort_other, other, 1, 0)
+        ).astype(BF16)
+
+    def from_order(sort, values):
+        return contract(sort, values, 0, 0).astype(BF16)
+
+    x_sorted = to_order(tokens, other_tokens)
+    normed, query, keys, values = project(
+        x_sorted, gain_one[None, :], w_qkv, cos, sin, q_width, kv_heads
+    )
+    mixed_sorted = attend(query, keys, values, start_column)
+    mixed_other = swap_seq(from_order(sort_other, mixed_sorted))
+    mixed = ordered(from_order(sort_own, mixed_sorted), mixed_other, 1)
+    inputs = tokens.astype(F32)
+    attn = jnp.dot(mixed, output_full, preferred_element_type=F32)
+    middle = inputs + BRANCH_SCALE * attn
+    normed_ffn = rms_norm(middle, gain_two).astype(BF16)
+
+    row_pieces = plane_gather(normed_ffn, 0)
+    total = 8 * tok_count
+    place = line.astype(jnp.int32)[None]
+    ffn_pieces, back_pieces, kept, offset = [], [], (), 0
+    for rows, grads, gate in zip(row_pieces, grad_pieces, gate_pieces):
+        result = run_experts(
+            place, rows, grads, gate, in_slots, out_slots, total, offset, kept
+        )
+        ffn_pieces.append(result[0])
+        back_pieces.append(result[1])
+        kept = tuple(result[2:])
+        offset = offset + rows.shape[0]
+    hidden, grad_both, all_rows, all_grads = kept
+
+    grad_normed_ffn = plane_scatter(back_pieces)
+    grad_in_all = contract(all_rows, grad_both, 0, 0)
+    grad_out_all = contract(hidden, all_grads, 0, 0) * BRANCH_SCALE
+    ffn = plane_scatter(ffn_pieces)
+    output = (middle + BRANCH_SCALE * ffn).astype(BF16)
+
+    grad_final = cotangent.astype(F32)
+    grad_norm, grad_gain_two = norm_back(middle, gain_two, grad_normed_ffn)
+    grad_middle = grad_final + grad_norm
+    grad_attn = (BRANCH_SCALE * grad_middle).astype(BF16)
+    grad_mixed = contract(grad_attn, output_full, 1, 1).astype(BF16)
+    grad_w_output = contract(mixed, grad_attn, 0, 0)
+    grad_other = swap_seq(half_of(grad_mixed, 1 - seq))
+    grad_sorted = to_order(half_of(grad_mixed, seq), grad_other)
+    grad_query, grad_keys, grad_values = attend_back(
+        query, keys, values, grad_sorted, start_column, cos, sin
+    )
+    grad_qkv = jnp.concatenate([grad_query, grad_keys, grad_values], axis=1)
+    grad_w_qkv = contract(normed, grad_qkv, 0, 0)
+    grad_normed = contract(grad_qkv, w_qkv, 1, 1).astype(BF16)
+    sent_normed = swap_seq(from_order(sort_other, grad_normed))
+    grad_normed = from_order(sort_own, grad_normed).astype(F32) + sent_normed.astype(F32)
+    grad_first, grad_gain_one = norm_back(inputs, gain_one, grad_normed)
+    grad_tokens = grad_middle + grad_first
+
+    def expert_part(grads, size, axis):
+        return lambda which: lax.dynamic_slice_in_dim(grads, which * size, size, axis=axis)
+
+    grad_in_part = line_scatter(expert_part(grad_in_all, 2 * half, 1), line).astype(BF16)
+    grad_out_part = line_scatter(expert_part(grad_out_all, half, 0), line).astype(BF16)
+    grad_w_out = both_axes(grad_out_part, straight)
+    same = jnp.where(first_core, grad_in_part[:, :half], grad_in_part[:, half:])
+    cross = jnp.where(first_core, grad_in_part[:, half:], grad_in_part[:, :half])
+    grad_w_in = ordered(both_axes(same, straight), both_axes(cross, crossed_back), 1)
+
+    summed_output = lax.psum_scatter(
+        grad_w_output.astype(BF16), ("seq", "dp"), scatter_dimension=0, tiled=True
+    )
+    summed_qkv = lax.psum_scatter(
+        grad_w_qkv.astype(BF16).reshape(2, width // 2, q_width + 2 * kv_width),
+        "dp",
+        scatter_dimension=1,
+        tiled=True,
+    )
+    kept_rows = lax.dynamic_index_in_dim(summed_qkv, seq, axis=0, keepdims=False)
+    sent_rows = swap_seq(lax.dynamic_index_in_dim(summed_qkv, 1 - seq, axis=0, keepdims=False))
+    cuts = (q_width, q_width + kv_width)
+    grad_projections = [
+        ordered(a, b, 1).astype(F32)
+        for a, b in zip(jnp.split(kept_rows, cuts, axis=1), jnp.split(sent_rows, cuts, axis=1))
+    ]
+    grad_gains = sum_everywhere(jnp.stack([grad_gain_one, grad_gain_two]))
+    grad_gains = lax.dynamic_slice_in_dim(grad_gains, index * shard, shard, axis=1)
+    return (
+        output,
+        grad_tokens,
+        grad_projections[0],
+        grad_projections[1],
+        grad_projections[2],
+        summed_output.astype(F32),
+        grad_gains[0],
+        grad_gains[1],
+        grad_w_in.astype(F32)[None],
+        grad_w_out.astype(F32)[None],
+    )
+
+
 def solution(mesh):
     placed = (
         P(("seq", "dp"), None),
@@ -372,7 +1019,7 @@
         P("dp", "seq", None),
     )
     return jax.shard_map(
-        shards,
+        shards_plane if in_planes(mesh) else shards_general,
         mesh=mesh,
         in_specs=placed,
         out_specs=(

time: 2570 us -> 1020 us (0.40)
  waiting for transfers between devices: 1440 us -> 386 us
  matrix products: 337 us -> 99.7 us
  Pallas kernels: 0 us -> 187 us
  blocking collectives: 183 us -> 0 us
  local copies, waits for them, and re-layouts: 178 us -> 53.5 us
  starting transfers between devices: 234 us -> 158 us
  other arithmetic: 165 us -> 113 us
    all_to_all x9 -> x0, waiting for transfers between devices: 906 us -> none  [the longest x1 255 us: shards(): lax.all_to_all(home_layout(result), 'dp', split_axis=0, concat_axis=0, ti...]
    ppermute x0 -> x91, waiting for transfers between devices: none -> 339 us  [the longest x12 115 us: line_down(): return lax.ppermute(value, 'dp', [(i, i - 4) for i in range(4, 4 * LINE)])]
    reduce_scatter x6 -> x2, waiting for transfers between devices: 374 us -> 45.8 us  [the longest x1 45.8 us: shards_plane(): lax.psum_scatter(grad_w_output.astype(BF16), ('seq', 'dp'), scatter_dimen...]
    dot_general x32 -> x15, matrix products: 337 us -> 99.7 us  [the longest x14 94.5 us: contract(): lax.dot_general(left, right, (((left_dim,), (right_dim,)), ((), ())), pre...]
    all_to_all x9 -> x0, starting transfers between devices: 225 us -> none  [the longest x1 65.9 us: shards(): lax.all_to_all(home_layout(result), 'dp', split_axis=0, concat_axis=0, ti...]
    pallas_call x0 -> x6, Pallas kernels: none -> 187 us  [the longest x3 104 us: run_experts(): pl.pallas_call(experts_kernel, grid_spec=pltpu.PrefetchScalarGridSpec(num...]
    ppermute x0 -> x91, starting transfers between devices: none -> 157 us  [the longest x38 49.2 us: swap_dp(): return lax.ppermute(value, 'dp', [(i, i ^ mask) for i in range(4 * LINE)])]
    all_gather x6 -> x2, waiting for transfers between devices: 155 us -> 0.01 us  [the longest x1 0.01 us: shards_plane(): lax.all_gather(pair, 'dp', axis=1, tiled=True)]
  transfers between devices with their start and end apart: 21 -> 95, of which waited for: 15 -> 39; matrix products, arithmetic and copies ran while one was open for 24% -> 23% of each run, Pallas kernels for 0% -> 14%
where the time goes in v1:
time: 1020 us; the launch traced here: 1010 us
  waiting for transfers between devices  386 us (38%)
  Pallas kernels  187 us (18%)
  starting transfers between devices  158 us (15%)
  other arithmetic  113 us (11%)
  matrix products  99.7 us (10%)
  local copies, waits for them, and re-layouts  53.5 us (5%)
  between operations  15.4 us (2%)
    ppermute x12, waiting for transfers between devices, line_down(): return lax.ppermute(value, 'dp', [(i, i - 4) for i in range(4, 4 * LINE)])  115 us
    pallas_call x3, Pallas kernels, run_experts(): pl.pallas_call(experts_kernel, grid_spec=pltpu.PrefetchScalarGridSpec(num...  104 us
    dot_general x14, matrix products, contract(): lax.dot_general(left, right, (((left_dim,), (right_dim,)), ((), ())), pre...  94.5 us
    ppermute x23, waiting for transfers between devices, swap_seq(): return lax.ppermute(value, 'seq', [(0, 1), (1, 0)])  81.6 us
    ppermute x38, waiting for transfers between devices, swap_dp(): return lax.ppermute(value, 'dp', [(i, i ^ mask) for i in range(4 * LINE)])  74.3 us
    ppermute x38, starting transfers between devices, swap_dp(): return lax.ppermute(value, 'dp', [(i, i ^ mask) for i in range(4 * LINE)])  49.2 us
    ppermute x12, starting transfers between devices, line_up(): return lax.ppermute(value, 'dp', [(i, i + 4) for i in range(4 * LINE - 4)])  47.5 us
    reduce_scatter x1, waiting for transfers between devices, shards_plane(): lax.psum_scatter(grad_w_output.astype(BF16), ('seq', 'dp'), scatter_dimen...  45.8 us
  transfers between devices with their start and end apart: 95, of which 39 were waited for; matrix products, arithmetic and copies ran while one was open for 23% of the time, Pallas kernels for 14%

profile of v1, /device:TPU:1, one launch (start us, length us, event | category | flops | bytes accessed | tf_op | source)
XLA Modules:
  0.0 1012.2 jit_solution(4793895285469116068)
XLA Ops:
  30.1 4.4 fusion.16
  41.8 4.1 collective-permute-start.11
  49.7 4.5 collective-permute-start.12
  61.3 15.4 %collective-permute-done.46 = f32[16,256]{1,0:T(8,128)S(1)} collective-permute-done((f32[16,256]{1,0:T(8,128)S(1)}, f32[16,256]{1,0:T(8,128)S(1)}, u32[]{:S(2)}, u32[]{:S(2)}) %collective-permute-start.46) | collective-permute-done | bytes 16416 | tf_op jit(solution)/shard_map/ppermute | solution.py:370
  90.2 12.9 %collective-permute-done.5 = f32[2,1536]{1,0:T(2,128)} collective-permute-done((f32[2,1536]{1,0:T(2,128)S(1)}, f32[2,1536]{1,0:T(2,128)}, u32[]{:S(2)}, u32[]{:S(2)}) %collective-permute-start.5) | collective-permute-done | bytes 12320 | tf_op jit(solution)/shard_map/ppermute | solution.py:370
  116.7 14.4 %collective-permute-done.19.refs_13_ = bf16[256,1536]{1,0:T(8,128)(2,1)} collective-permute-done((bf16[256,1536]{1,0:T(8,128)(2,1)}, bf16[256,1536]{1,0:T(8,128)(2,1)}, u32[]{:S(2)}, u32[]{:S(2)}) %collective-permute-start.19) | collective-permute-done | bytes 786464 | tf_op jit(solution)/shard_map/ppermute | solution.py:850
  131.1 4.2 collective-permute-start.20
  135.3 16.7 %collective-permute-done.38 = bf16[256,1536]{1,0:T(8,128)(2,1)} collective-permute-done((bf16[256,1536]{1,0:T(8,128)(2,1)}, bf16[256,1536]{1,0:T(8,128)(2,1)}, u32[]{:S(2)}, u32[]{:S(2)}) %collective-permute-start.38) | collective-permute-done | bytes 786464 | tf_op jit(solution)/shard_map/ppermute | solution.py:374
  153.6 4.9 add_convert_fusion.2.x_ref
  158.6 10.1 project.1
  168.7 27.6 %attend.1 = bf16[1024,768]{1,0:T(8,128)(2,1)} custom-call(bf16[1024,768]{1,0:T(8,128)(2,1)} %get-tuple-element.35.q_ref, bf16[4,1024,64]{2,1,0:T(8,128)(2,1)} %get-tuple-element.36.k_ref, bf16[4,1024,64]{2,1,0:T(8,128)(2,1)} %get-tuple-element.37.v_ref, s32[1024,1]{1,0:T(8,128)} %copy.47.start_ref), custom_call_target="tpu_custom_call" | custom-call | flops 3623878656 | bytes 6291456 | tf_op jit(solution)/shard_map/attend/pallas_call | solution.py:587
  206.5 5.4 collective-permute-start.13
  221.3 3.9 collective-permute-start.21
  225.3 5.2 multiply_reduce_fusion.2
  230.6 5.0 collective-permute-start.49
  235.5 9.2 collective-permute-done.13.refs_5_
  246.0 9.0 collective-permute-done.16.refs_7_
  264.7 7.1 collective-permute-done.24.refs_15_
  278.5 5.0 collective-permute-start.8
  284.7 9.3 collective-permute-done.14.refs_4_
  294.0 4.1 collective-permute-start.15
  298.1 7.4 collective-permute-done.17.refs_8_
  316.1 7.5 collective-permute-done.28
  335.6 10.9 %collective-permute-done.22.refs_10_ = bf16[256,1536]{1,0:T(8,128)(2,1)S(1)} collective-permute-done((bf16[256,1536]{1,0:T(8,128)(2,1)}, bf16[256,1536]{1,0:T(8,128)(2,1)S(1)}, u32[]{:S(2)}, u32[]{:S(2)}) %collective-permute-start.22) | collective-permute-done | bytes 786464 | tf_op jit(solution)/shard_map/ppermute | solution.py:386
  349.6 8.1 collective-permute-done.25.refs_16_
  361.5 27.7 %experts.3 = (bf16[1024,1536]{1,0:T(8,128)(2,1)}, bf16[1024,1536]{1,0:T(8,128)(2,1)}, bf16[4096,1024]{1,0:T(8,128)(2,1)}, bf16[4096,2048]{1,0:T(8,128)(2,1)}, bf...) custom-call(s32[1]{0:T(128)} %bitcast.10.place_ref, bf16[1024,1536]{1,0:T(8,128)(2,1)} %pad_maximum_fusion.refs_0_, ...), custom_call_target="tpu_custom_call" | custom-call | flops 19327352832 | bytes 25165824 | tf_op jit(solution)/shard_map/experts/pallas_call | solution.py:753
  392.0 4.0 collective-permute-start.26
  404.4 27.8 %experts.4 = (bf16[1024,1536]{1,0:T(8,128)(2,1)}, bf16[1024,1536]{1,0:T(8,128)(2,1)}, bf16[4096,1024]{1,0:T(8,128)(2,1)}, bf16[4096,2048]{1,0:T(8,128)(2,1)}, bf...) custom-call(s32[1]{0:T(128)} %bitcast.10.place_ref, ...), custom_call_target="tpu_custom_call", output_to_operand_aliasing={{2}: (18, {}), {3}: (19, {}), {4}: (20, {}), {5}: (21, {})} | custom-call | flops 19327352832 | bytes 25165824 | tf_op jit(solution)/shard_map/experts/pallas_call | solution.py:753
  436.5 3.8 convert_add_fusion.5
  446.6 3.8 constant_dynamic-update-slice_fusion.refs_0_
  450.4 48.1 %experts.5 = (bf16[2048,1536]{1,0:T(8,128)(2,1)}, bf16[2048,1536]{1,0:T(8,128)(2,1)}, bf16[4096,1024]{1,0:T(8,128)(2,1)}, bf16[4096,2048]{1,0:T(8,128)(2,1)}, bf...) custom-call(s32[1]{0:T(128)} %bitcast.10.place_ref, ...), custom_call_target="tpu_custom_call", output_to_operand_aliasing={{2}: (18, {}), {3}: (19, {}), {4}: (20, {}), {5}: (21, {})} | custom-call | flops 38654705664 | bytes 50331648 | tf_op jit(solution)/shard_map/experts/pallas_call | solution.py:753
  498.5 17.3 %convolution_multiply_fusion = f32[1024,1536]{1,0:T(8,128)S(1)} fusion(bf16[4096,1024]{1,0:T(8,128)(2,1)} %get-tuple-element.58, bf16[4096,1536]{1,0:T(8,128)(2,1)} %get-tuple-element.59), kind=kOutput, calls=%fused_computation.5 | convolution fusion | flops 12886474752 | bytes 27262976 | tf_op jit(solution)/shard_map/dot_general | solution.py:547
  517.4 3.8 collective-permute-start.84
  527.2 32.6 %fusion.52 = f32[1536,2048]{1,0:T(8,128)S(1)} fusion(bf16[4096,1536]{1,0:T(8,128)(2,1)} %get-tuple-element.56, bf16[4096,2048]{1,0:T(8,128)(2,1)} %get-tuple-element.57), kind=kOutput, calls=%fused_computation.200 | convolution fusion | flops 25769803776 | bytes 41943040 | tf_op jit(solution)/shard_map/dot_general | solution.py:547
  559.9 8.2 add_convert_fusion
  578.9 9.7 collective-permute-done.63
  593.9 11.6 %collective-permute-done.54 = bf16[256,1536]{1,0:T(8,128)(2,1)S(1)} collective-permute-done((bf16[256,1536]{1,0:T(8,128)(2,1)}, bf16[256,1536]{1,0:T(8,128)(2,1)S(1)}, u32[]{:S(2)}, u32[]{:S(2)}) %collective-permute-start.54) | collective-permute-done | bytes 786464 | tf_op jit(solution)/shard_map/ppermute | solution.py:374
  609.9 12.5 %collective-permute-done.61 = bf16[256,1536]{1,0:T(8,128)(2,1)S(1)} collective-permute-done((bf16[256,1536]{1,0:T(8,128)(2,1)S(1)}, bf16[256,1536]{1,0:T(8,128)(2,1)S(1)}, u32[]{:S(2)}, u32[]{:S(2)}) %collective-permute-start.61) | collective-permute-done | bytes 786464 | tf_op jit(solution)/shard_map/ppermute | solution.py:374
  623.4 15.6 %collective-permute-done.64 = bf16[256,1536]{1,0:T(8,128)(2,1)S(1)} collective-permute-done((bf16[256,1536]{1,0:T(8,128)(2,1)S(1)}, bf16[256,1536]{1,0:T(8,128)(2,1)S(1)}, u32[]{:S(2)}, u32[]{:S(2)}) %collective-permute-start.64) | collective-permute-done | bytes 786464 | tf_op jit(solution)/shard_map/ppermute | solution.py:370
  642.6 13.4 %collective-permute-done.52 = bf16[256,1536]{1,0:T(8,128)(2,1)S(1)} collective-permute-done((bf16[256,1536]{1,0:T(8,128)(2,1)S(1)}, bf16[256,1536]{1,0:T(8,128)(2,1)S(1)}, u32[]{:S(2)}, u32[]{:S(2)}) %collective-permute-start.52) | collective-permute-done | bytes 786464 | tf_op jit(solution)/shard_map/ppermute | solution.py:374
  660.0 12.8 %collective-permute-done.55 = bf16[256,1536]{1,0:T(8,128)(2,1)S(1)} collective-permute-done((bf16[256,1536]{1,0:T(8,128)(2,1)S(1)}, bf16[256,1536]{1,0:T(8,128)(2,1)S(1)}, u32[]{:S(2)}, u32[]{:S(2)}) %collective-permute-start.55) | collective-permute-done | bytes 786464 | tf_op jit(solution)/shard_map/ppermute | solution.py:370
  676.8 3.8 multiply_add_fusion
  680.6 5.0 convolution_convert_fusion.5
  691.9 5.7 collective-permute-start.77
  698.6 4.5 collective-permute-done.68
  705.4 45.3 %attend_back.1 = (bf16[1024,768]{1,0:T(8,128)(2,1)}, bf16[1024,256]{1,0:T(8,128)(2,1)}, bf16[1024,256]{1,0:T(8,128)(2,1)}) custom-call(bf16[1024,768]{1,0:T(8,128)(2,1)} %get-tuple-element.35.q_ref, bf16[4,1024,64]{2,1,0:T(8,128)(2,1)} %get-tuple-element.36.k_ref, bf16[4,1024,64]{2,1,0:T(8,128)(2,1)} %get-tuple-element.37.v_ref, ...), custom_call_target="tpu_custom_call" | custom-call | flops 9059696640 | bytes 6291456 | tf_op jit(solution)/shard_map/attend_back/pallas_call | solution.py:655
  753.4 5.9 convolution_convert_fusion
  759.6 3.9 add_convert_fusion.12
  764.8 4.9 collective-permute-start.86
  769.8 7.0 add_convert_fusion.6
  778.0 4.2 collective-permute-done.88
  786.2 70.2 %collective-permute-done.89 = bf16[256,1536]{1,0:T(8,128)(2,1)} collective-permute-done((bf16[256,1536]{1,0:T(8,128)(2,1)}, bf16[256,1536]{1,0:T(8,128)(2,1)}, u32[]{:S(2)}, u32[]{:S(2)}) %collective-permute-start.89) | collective-permute-done | bytes 786464 | tf_op jit(solution)/shard_map/ppermute | solution.py:390
  859.7 6.1 collective-permute-start.90
  868.7 4.0 add_convert_fusion.4
  874.0 4.5 convolution_convert_fusion.2
  884.1 4.4 convolution_convert_fusion.1
  892.8 3.9 collective-permute-done.78
  896.7 9.1 collective-permute-done.81
  909.4 6.4 collective-permute-done.69
  915.9 4.2 fusion.7
  920.1 3.9 collective-permute-start.71
  932.3 4.2 fusion.6
  936.6 11.3 %collective-permute-done.82 = bf16[1536,256]{1,0:T(8,128)(2,1)S(1)} collective-permute-done((bf16[1536,256]{1,0:T(8,128)(2,1)S(1)}, bf16[1536,256]{1,0:T(8,128)(2,1)S(1)}, u32[]{:S(2)}, u32[]{:S(2)}) %collective-permute-start.82) | collective-permute-done | bytes 786464 | tf_op jit(solution)/shard_map/ppermute | solution.py:850
  955.8 45.8 %reduce-scatter.5.cloned.1.call-done = bf16[48,1536]{1,0:T(8,128)(2,1)} async-done(((bf16[1536,1536]{1,0:T(8,128)(2,1)}), bf16[48,1536]{1,0:T(8,128)(2,1)}) %reduce-scatter.5.cloned.1.call-update) | async-done | bytes 147472 | tf_op jit(solution)/shard_map/reduce_scatter | solution.py:972
  (392 shorter events, 259.5 us)
Async XLA Ops:
  7.2 151.4 %all-gather.3.cloned.1.call-start = ((), (), s32[]{:S(2)}) async-start(), calls=%async_computation.2 | async-start | bytes 4177920 | tf_op jit(solution)/shard_map/all_gather | solution.py:840
  15.1 210.2 %all-gather.5.cloned.1.call-start = ((), (), s32[]{:S(2)}) async-start(), calls=%async_computation.3 | async-start | bytes 4866048 | tf_op jit(solution)/shard_map/all_gather | solution.py:841
  15.8 938.0 %reduce-scatter.3.cloned.1.call-start = ((), (), s32[]{:S(2)}) async-start(), calls=%async_computation.4 | async-start | bytes 4177920 | tf_op jit(solution)/shard_map/reduce_scatter | solution.py:975
  18.9 35.9 %collective-permute-start.10 = (f32[16,512]{1,0:T(8,128)S(1)}, f32[16,512]{1,0:T(8,128)S(1)}, u32[]{:S(2)}, u32[]{:S(2)}) collective-permute-start(f32[16,512]{1,0:T(8,128)S(1)} %select_reduce_fusion), channel_id=1, source_target_pairs={{0,1},{1,0},{2,3},{3,2},{4,5},{5,4},{6,7},{7,6},{8,9},{9,8},{10,11... | collective-permute-start | bytes 98312 | tf_op jit(solution)/shard_map/ppermute | solution.py:374
  21.6 24.8 %collective-permute-start.41 = (f32[16,256]{1,0:T(8,128)S(1)}, f32[16,256]{1,0:T(8,128)S(1)}, u32[]{:S(2)}, u32[]{:S(2)}) collective-permute-start(f32[16,256]{1,0:T(8,128)S(1)} %get-tuple-element.122), channel_id=1, source_target_pairs={{0,2},{1,3},{2,0},{3,1},{4,6},{5,7},{6,4},{7,5},{8,10},{9,11},{10,... | collective-permute-start | bytes 49160 | tf_op jit(solution)/shard_map/ppermute | solution.py:374
  24.4 127.7 %collective-permute-start = (bf16[512,1536]{1,0:T(8,128)(2,1)}, bf16[512,1536]{1,0:T(8,128)(2,1)}, u32[]{:S(2)}, u32[]{:S(2)}) collective-permute-start(bf16[512,1536]{1,0:T(8,128)(2,1)} %param.14), channel_id=1, source_target_pairs={{0,16},{16,0},{1,17},{17,1},{2,18},{18,2},{3,19},{19,3},{4,20},{20... | collective-permute-start | bytes 4718600 | tf_op jit(solution)/shard_map/ppermute | solution.py:370
  41.8 67.0 %collective-permute-start.11 = (bf16[1536,256]{1,0:T(8,128)(2,1)}, bf16[1536,256]{1,0:T(8,128)(2,1)}, u32[]{:S(2)}, u32[]{:S(2)}) collective-permute-start(bf16[1536,256]{1,0:T(8,128)(2,1)} %get-tuple-element.102), channel_id=1, source_target_pairs={{0,0},{1,16},{2,2},{3,18},{4,4},{5,20},{6,6},{7,22},{8,8},{9,24},{... | collective-permute-start | bytes 2359304 | tf_op jit(solution)/shard_map/ppermute | solution.py:850
  49.7 62.5 %collective-permute-start.12 = (bf16[1536,256]{1,0:T(8,128)(2,1)}, bf16[1536,256]{1,0:T(8,128)(2,1)}, u32[]{:S(2)}, u32[]{:S(2)}) collective-permute-start(bf16[1536,256]{1,0:T(8,128)(2,1)} %get-tuple-element.103), channel_id=1, source_target_pairs={{0,1},{1,17},{2,3},{3,19},{4,5},{5,21},{6,7},{7,23},{8,9},{9,25},{... | collective-permute-start | bytes 2359304 | tf_op jit(solution)/shard_map/ppermute | solution.py:850
  57.8 25.6 %collective-permute-start.50 = (f32[16,512]{1,0:T(8,128)}, f32[16,512]{1,0:T(8,128)}, u32[]{:S(2)}, u32[]{:S(2)}) collective-permute-start(f32[16,512]{1,0:T(8,128)} %pad_maximum_fusion.21), channel_id=1, source_target_pairs={{0,1},{1,0},{2,3},{3,2},{4,5},{5,4},{6,7},{7,6},{8,9},{9,8},{10,11... | collective-permute-start | bytes 98312 | tf_op jit(solution)/shard_map/ppermute | solution.py:374
  79.5 51.6 %collective-permute-start.35 = (bf16[256,1536]{1,0:T(8,128)(2,1)}, bf16[256,1536]{1,0:T(8,128)(2,1)}, u32[]{:S(2)}, u32[]{:S(2)}) collective-permute-start(bf16[256,1536]{1,0:T(8,128)(2,1)} %get-tuple-element.96), channel_id=1, source_target_pairs={{0,16},{16,0},{1,17},{17,1},{2,18},{18,2},{3,19},{19,3},{4,20},{20... | collective-permute-start | bytes 2359304 | tf_op jit(solution)/shard_map/ppermute | solution.py:370
  107.3 91.6 %collective-permute-start.34 = (bf16[256,1536]{1,0:T(8,128)(2,1)}, bf16[256,1536]{1,0:T(8,128)(2,1)}, u32[]{:S(2)}, u32[]{:S(2)}) collective-permute-start(bf16[256,1536]{1,0:T(8,128)(2,1)} %get-tuple-element.96), channel_id=1, source_target_pairs={{0,2},{1,3},{2,0},{3,1},{4,6},{5,7},{6,4},{7,5},{8,10},{9,11},{10,... | collective-permute-start | bytes 2359304 | tf_op jit(solution)/shard_map/ppermute | solution.py:374
  112.1 39.9 %collective-permute-start.38 = (bf16[256,1536]{1,0:T(8,128)(2,1)}, bf16[256,1536]{1,0:T(8,128)(2,1)}, u32[]{:S(2)}, u32[]{:S(2)}) collective-permute-start(bf16[256,1536]{1,0:T(8,128)(2,1)} %get-tuple-element.97), channel_id=1, source_target_pairs={{0,2},{1,3},{2,0},{3,1},{4,6},{5,7},{6,4},{7,5},{8,10},{9,11},{10,... | collective-permute-start | bytes 2359304 | tf_op jit(solution)/shard_map/ppermute | solution.py:374
  131.1 70.5 %collective-permute-start.37 = (bf16[256,1536]{1,0:T(8,128)(2,1)}, bf16[256,1536]{1,0:T(8,128)(2,1)}, u32[]{:S(2)}, u32[]{:S(2)}) collective-permute-start(bf16[256,1536]{1,0:T(8,128)(2,1)} %get-tuple-element.97), channel_id=1, source_target_pairs={{0,16},{16,0},{1,17},{17,1},{2,18},{18,2},{3,19},{19,3},{4,20},{20... | collective-permute-start | bytes 2359304 | tf_op jit(solution)/shard_map/ppermute | solution.py:370
  131.1 73.9 %collective-permute-start.20 = (bf16[256,1536]{1,0:T(8,128)(2,1)}, bf16[256,1536]{1,0:T(8,128)(2,1)}, u32[]{:S(2)}, u32[]{:S(2)}) collective-permute-start(bf16[256,1536]{1,0:T(8,128)(2,1)} %collective-permute-done.19.refs_13_), channel_id=1, source_target_pairs={{0,4},{1,5},{2,6},{3,7},{4,8},{5,9},{6,10},{7,11},{8,12},{9,13},{1... | collective-permute-start | bytes 2359304 | tf_op jit(solution)/shard_map/ppermute | solution.py:386
  152.1 54.5 %collective-permute-start.36 = (bf16[256,1536]{1,0:T(8,128)(2,1)}, bf16[256,1536]{1,0:T(8,128)(2,1)}, u32[]{:S(2)}, u32[]{:S(2)}) collective-permute-start(bf16[256,1536]{1,0:T(8,128)(2,1)} %collective-permute-done.35), channel_id=1, source_target_pairs={{0,2},{1,3},{2,0},{3,1},{4,6},{5,7},{6,4},{7,5},{8,10},{9,11},{10,... | collective-permute-start | bytes 2359304 | tf_op jit(solution)/shard_map/ppermute | solution.py:374
  152.2 59.8 %collective-permute-start.39 = (bf16[256,1536]{1,0:T(8,128)(2,1)}, bf16[256,1536]{1,0:T(8,128)(2,1)}, u32[]{:S(2)}, u32[]{:S(2)}) collective-permute-start(bf16[256,1536]{1,0:T(8,128)(2,1)} %collective-permute-done.38), channel_id=1, source_target_pairs={{0,16},{16,0},{1,17},{17,1},{2,18},{18,2},{3,19},{19,3},{4,20},{20... | collective-permute-start | bytes 2359304 | tf_op jit(solution)/shard_map/ppermute | solution.py:370
  205.0 25.6 %collective-permute-start.9 = (bf16[512,1536]{1,0:T(8,128)(2,1)S(1)}, bf16[512,1536]{1,0:T(8,128)(2,1)}, u32[]{:S(2)}, u32[]{:S(2)}) collective-permute-start(bf16[512,1536]{1,0:T(8,128)(2,1)S(1)} %copy-done.4), channel_id=1, source_target_pairs={{0,1},{1,0},{2,3},{3,2},{4,5},{5,4},{6,7},{7,6},{8,9},{9,8},{10,11... | collective-permute-start | bytes 4718600 | tf_op jit(solution)/shard_map/ppermute | solution.py:374
  206.5 38.2 %collective-permute-start.13 = (bf16[1536,512]{1,0:T(8,128)(2,1)}, bf16[1536,512]{1,0:T(8,128)(2,1)}, u32[]{:S(2)}, u32[]{:S(2)}) collective-permute-start(bf16[1536,512]{1,0:T(8,128)(2,1)} %pad_maximum_fusion.8.refs_6_), channel_id=1, source_target_pairs={{0,4},{1,5},{2,6},{3,7},{4,8},{5,9},{6,10},{7,11},{8,12},{9,13},{1... | collective-permute-start | bytes 4718600 | tf_op jit(solution)/shard_map/ppermute | solution.py:386
  211.9 43.1 %collective-permute-start.16 = (bf16[1536,512]{1,0:T(8,128)(2,1)}, bf16[1536,512]{1,0:T(8,128)(2,1)}, u32[]{:S(2)}, u32[]{:S(2)}) collective-permute-start(bf16[1536,512]{1,0:T(8,128)(2,1)} %pad_maximum_fusion.8.refs_6_), channel_id=1, source_target_pairs={{4,0},{5,1},{6,2},{7,3},{8,4},{9,5},{10,6},{11,7},{12,8},{13,9},{1... | collective-permute-start | bytes 4718600 | tf_op jit(solution)/shard_map/ppermute | solution.py:390
  216.9 89.9 %collective-permute-start.40 = (bf16[1024,1536]{1,0:T(8,128)(2,1)}, bf16[1024,1536]{1,0:T(8,128)(2,1)}, u32[]{:S(2)}, u32[]{:S(2)}) collective-permute-start(bf16[1024,1536]{1,0:T(8,128)(2,1)} %pad_maximum_fusion.3), channel_id=1, source_target_pairs={{0,1},{1,0},{2,3},{3,2},{4,5},{5,4},{6,7},{7,6},{8,9},{9,8},{10,11... | collective-permute-start | bytes 9437192 | tf_op jit(solution)/shard_map/ppermute | solution.py:374
  221.3 40.3 %collective-permute-start.21 = (bf16[256,1536]{1,0:T(8,128)(2,1)}, bf16[256,1536]{1,0:T(8,128)(2,1)}, u32[]{:S(2)}, u32[]{:S(2)}) collective-permute-start(bf16[256,1536]{1,0:T(8,128)(2,1)} %collective-permute-done.20.refs_12_), channel_id=1, source_target_pairs={{0,4},{1,5},{2,6},{3,7},{4,8},{5,9},{6,10},{7,11},{8,12},{9,13},{1... | collective-permute-start | bytes 2359304 | tf_op jit(solution)/shard_map/ppermute | solution.py:386
  230.6 47.9 %collective-permute-start.49 = (bf16[512,1536]{1,0:T(8,128)(2,1)S(1)}, bf16[512,1536]{1,0:T(8,128)(2,1)S(1)}, u32[]{:S(2)}, u32[]{:S(2)}) collective-permute-start(bf16[512,1536]{1,0:T(8,128)(2,1)S(1)} %copy-done.19), channel_id=1, source_target_pairs={{0,1},{1,0},{2,3},{3,2},{4,5},{5,4},{6,7},{7,6},{8,9},{9,8},{10,11... | collective-permute-start | bytes 4718600 | tf_op jit(solution)/shard_map/ppermute | solution.py:374
  244.8 27.0 %collective-permute-start.24 = (bf16[256,1536]{1,0:T(8,128)(2,1)}, bf16[256,1536]{1,0:T(8,128)(2,1)S(1)}, u32[]{:S(2)}, u32[]{:S(2)}) collective-permute-start(bf16[256,1536]{1,0:T(8,128)(2,1)} %collective-permute-done.23.refs_14_), channel_id=1, source_target_pairs={{4,0},{5,1},{6,2},{7,3},{8,4},{9,5},{10,6},{11,7},{12,8},{13,9},{1... | collective-permute-start | bytes 2359304 | tf_op jit(solution)/shard_map/ppermute | solution.py:390
  255.0 39.0 %collective-permute-start.14 = (bf16[1536,512]{1,0:T(8,128)(2,1)}, bf16[1536,512]{1,0:T(8,128)(2,1)S(1)}, u32[]{:S(2)}, u32[]{:S(2)}) collective-permute-start(bf16[1536,512]{1,0:T(8,128)(2,1)} %collective-permute-done.13.refs_5_), channel_id=1, source_target_pairs={{0,4},{1,5},{2,6},{3,7},{4,8},{5,9},{6,10},{7,11},{8,12},{9,13},{1... | collective-permute-start | bytes 4718600 | tf_op jit(solution)/shard_map/ppermute | solution.py:386
  261.6 43.9 %collective-permute-start.17 = (bf16[1536,512]{1,0:T(8,128)(2,1)}, bf16[1536,512]{1,0:T(8,128)(2,1)S(1)}, u32[]{:S(2)}, u32[]{:S(2)}) collective-permute-start(bf16[1536,512]{1,0:T(8,128)(2,1)} %collective-permute-done.16.refs_7_), channel_id=1, source_target_pairs={{4,0},{5,1},{6,2},{7,3},{8,4},{9,5},{10,6},{11,7},{12,8},{13,9},{1... | collective-permute-start | bytes 4718600 | tf_op jit(solution)/shard_map/ppermute | solution.py:390
  271.8 36.5 %collective-permute-start.27 = (bf16[256,1536]{1,0:T(8,128)(2,1)S(1)}, bf16[256,1536]{1,0:T(8,128)(2,1)S(1)}, u32[]{:S(2)}, u32[]{:S(2)}) collective-permute-start(bf16[256,1536]{1,0:T(8,128)(2,1)S(1)} %get-tuple-element.98), channel_id=1, source_target_pairs={{0,2},{1,3},{2,0},{3,1},{4,6},{5,7},{6,4},{7,5},{8,10},{9,11},{10,... | collective-permute-start | bytes 2359304 | tf_op jit(solution)/shard_map/ppermute | solution.py:374
  278.5 53.7 %collective-permute-start.8 = (bf16[512,1536]{1,0:T(8,128)(2,1)S(1)}, bf16[512,1536]{1,0:T(8,128)(2,1)S(1)}, u32[]{:S(2)}, u32[]{:S(2)}) collective-permute-start(bf16[512,1536]{1,0:T(8,128)(2,1)S(1)} %multiply_convert_fusion.1), channel_id=1, source_target_pairs={{0,1},{1,0},{2,3},{3,2},{4,5},{5,4},{6,7},{7,6},{8,9},{9,8},{10,11... | collective-permute-start | bytes 4718600 | tf_op jit(solution)/shard_map/ppermute | solution.py:374
  294.0 64.8 %collective-permute-start.15 = (bf16[1536,512]{1,0:T(8,128)(2,1)S(1)}, bf16[1536,512]{1,0:T(8,128)(2,1)S(1)}, u32[]{:S(2)}, u32[]{:S(2)}) collective-permute-start(bf16[1536,512]{1,0:T(8,128)(2,1)S(1)} %collective-permute-done.14.refs_4_), channel_id=1, source_target_pairs={{0,4},{1,5},{2,6},{3,7},{4,8},{5,9},{6,10},{7,11},{8,12},{9,13},{1... | collective-permute-start | bytes 4718600 | tf_op jit(solution)/shard_map/ppermute | solution.py:386
  305.5 54.9 %collective-permute-start.18 = (bf16[1536,512]{1,0:T(8,128)(2,1)S(1)}, bf16[1536,512]{1,0:T(8,128)(2,1)S(1)}, u32[]{:S(2)}, u32[]{:S(2)}) collective-permute-start(bf16[1536,512]{1,0:T(8,128)(2,1)S(1)} %collective-permute-done.17.refs_8_), channel_id=1, source_target_pairs={{4,0},{5,1},{6,2},{7,3},{8,4},{9,5},{10,6},{11,7},{12,8},{13,9},{1... | collective-permute-start | bytes 4718600 | tf_op jit(solution)/shard_map/ppermute | solution.py:390
  327.3 30.3 %collective-permute-start.25 = (bf16[256,1536]{1,0:T(8,128)(2,1)S(1)}, bf16[256,1536]{1,0:T(8,128)(2,1)S(1)}, u32[]{:S(2)}, u32[]{:S(2)}) collective-permute-start(bf16[256,1536]{1,0:T(8,128)(2,1)S(1)} %collective-permute-done.24.refs_15_), channel_id=1, source_target_pairs={{4,0},{5,1},{6,2},{7,3},{8,4},{9,5},{10,6},{11,7},{12,8},{13,9},{1... | collective-permute-start | bytes 2359304 | tf_op jit(solution)/shard_map/ppermute | solution.py:390
  332.2 65.1 %collective-permute-start.30 = (bf16[256,1536]{1,0:T(8,128)(2,1)}, bf16[256,1536]{1,0:T(8,128)(2,1)S(1)}, u32[]{:S(2)}, u32[]{:S(2)}) collective-permute-start(bf16[256,1536]{1,0:T(8,128)(2,1)} %get-tuple-element.99), channel_id=1, source_target_pairs={{0,16},{16,0},{1,17},{17,1},{2,18},{18,2},{3,19},{19,3},{4,20},{20... | collective-permute-start | bytes 2359304 | tf_op jit(solution)/shard_map/ppermute | solution.py:370
  346.4 54.2 %collective-permute-start.48 = (bf16[512,1536]{1,0:T(8,128)(2,1)}, bf16[512,1536]{1,0:T(8,128)(2,1)}, u32[]{:S(2)}, u32[]{:S(2)}) collective-permute-start(bf16[512,1536]{1,0:T(8,128)(2,1)} %pad_maximum_fusion.9), channel_id=1, source_target_pairs={{0,1},{1,0},{2,3},{3,2},{4,5},{5,4},{6,7},{7,6},{8,9},{9,8},{10,11... | collective-permute-start | bytes 4718600 | tf_op jit(solution)/shard_map/ppermute | solution.py:374
  357.7 39.6 %collective-permute-start.29 = (bf16[256,1536]{1,0:T(8,128)(2,1)}, bf16[256,1536]{1,0:T(8,128)(2,1)S(1)}, u32[]{:S(2)}, u32[]{:S(2)}) collective-permute-start(bf16[256,1536]{1,0:T(8,128)(2,1)} %collective-permute-done.28), channel_id=1, source_target_pairs={{0,2},{1,3},{2,0},{3,1},{4,6},{5,7},{6,4},{7,5},{8,10},{9,11},{10,... | collective-permute-start | bytes 2359304 | tf_op jit(solution)/shard_map/ppermute | solution.py:374
  358.8 38.5 %collective-permute-start.32 = (bf16[256,1536]{1,0:T(8,128)(2,1)}, bf16[256,1536]{1,0:T(8,128)(2,1)S(1)}, u32[]{:S(2)}, u32[]{:S(2)}) collective-permute-start(bf16[256,1536]{1,0:T(8,128)(2,1)} %collective-permute-done.31), channel_id=1, source_target_pairs={{0,16},{16,0},{1,17},{17,1},{2,18},{18,2},{3,19},{19,3},{4,20},{20... | collective-permute-start | bytes 2359304 | tf_op jit(solution)/shard_map/ppermute | solution.py:370
  392.0 44.5 %collective-permute-start.26 = (bf16[512,1536]{1,0:T(8,128)(2,1)}, bf16[512,1536]{1,0:T(8,128)(2,1)}, u32[]{:S(2)}, u32[]{:S(2)}) collective-permute-start(bf16[512,1536]{1,0:T(8,128)(2,1)} %slice.125), channel_id=1, source_target_pairs={{0,1},{1,0},{2,3},{3,2},{4,5},{5,4},{6,7},{7,6},{8,9},{9,8},{10,11... | collective-permute-start | bytes 4718600 | tf_op jit(solution)/shard_map/ppermute | solution.py:374
  397.3 43.1 %collective-permute-start.59 = (bf16[512,1536]{1,0:T(8,128)(2,1)}, bf16[512,1536]{1,0:T(8,128)(2,1)}, u32[]{:S(2)}, u32[]{:S(2)}) collective-permute-start(bf16[512,1536]{1,0:T(8,128)(2,1)} %slice.145), channel_id=1, source_target_pairs={{0,1},{1,0},{2,3},{3,2},{4,5},{5,4},{6,7},{7,6},{8,9},{9,8},{10,11... | collective-permute-start | bytes 4718600 | tf_op jit(solution)/shard_map/ppermute | solution.py:374
  399.2 47.4 %collective-permute-start.33 = (bf16[1024,1536]{1,0:T(8,128)(2,1)}, bf16[1024,1536]{1,0:T(8,128)(2,1)}, u32[]{:S(2)}, u32[]{:S(2)}) collective-permute-start(bf16[1024,1536]{1,0:T(8,128)(2,1)} %pad_maximum_fusion.2), channel_id=1, source_target_pairs={{0,1},{1,0},{2,3},{3,2},{4,5},{5,4},{6,7},{7,6},{8,9},{9,8},{10,11... | collective-permute-start | bytes 9437192 | tf_op jit(solution)/shard_map/ppermute | solution.py:374
  517.4 75.7 %collective-permute-start.84 = (bf16[256,1536]{1,0:T(8,128)(2,1)}, bf16[256,1536]{1,0:T(8,128)(2,1)}, u32[]{:S(2)}, u32[]{:S(2)}) collective-permute-start(bf16[256,1536]{1,0:T(8,128)(2,1)} %get-tuple-element.72), channel_id=1, source_target_pairs={{0,4},{1,5},{2,6},{3,7},{4,8},{5,9},{6,10},{7,11},{8,12},{9,13},{1... | collective-permute-start | bytes 2359304 | tf_op jit(solution)/shard_map/ppermute | solution.py:386
  523.1 47.4 %collective-permute-start.51 = (bf16[1024,1536]{1,0:T(8,128)(2,1)}, bf16[1024,1536]{1,0:T(8,128)(2,1)}, u32[]{:S(2)}, u32[]{:S(2)}) collective-permute-start(bf16[1024,1536]{1,0:T(8,128)(2,1)} %slice.134), channel_id=1, source_target_pairs={{0,1},{1,0},{2,3},{3,2},{4,5},{5,4},{6,7},{7,6},{8,9},{9,8},{10,11... | collective-permute-start | bytes 9437192 | tf_op jit(solution)/shard_map/ppermute | solution.py:374
  527.0 32.9 %collective-permute-start.60 = (bf16[1024,1536]{1,0:T(8,128)(2,1)}, bf16[1024,1536]{1,0:T(8,128)(2,1)}, u32[]{:S(2)}, u32[]{:S(2)}) collective-permute-start(bf16[1024,1536]{1,0:T(8,128)(2,1)} %slice.148), channel_id=1, source_target_pairs={{0,1},{1,0},{2,3},{3,2},{4,5},{5,4},{6,7},{7,6},{8,9},{9,8},{10,11... | collective-permute-start | bytes 9437192 | tf_op jit(solution)/shard_map/ppermute | solution.py:374
  575.4 30.0 %collective-permute-start.54 = (bf16[256,1536]{1,0:T(8,128)(2,1)}, bf16[256,1536]{1,0:T(8,128)(2,1)S(1)}, u32[]{:S(2)}, u32[]{:S(2)}) collective-permute-start(bf16[256,1536]{1,0:T(8,128)(2,1)} %get-tuple-element.89), channel_id=1, source_target_pairs={{0,2},{1,3},{2,0},{3,1},{4,6},{5,7},{6,4},{7,5},{8,10},{9,11},{10,... | collective-permute-start | bytes 2359304 | tf_op jit(solution)/shard_map/ppermute | solution.py:374
  578.2 29.6 %collective-permute-start.57 = (bf16[256,1536]{1,0:T(8,128)(2,1)S(1)}, bf16[256,1536]{1,0:T(8,128)(2,1)S(1)}, u32[]{:S(2)}, u32[]{:S(2)}) collective-permute-start(bf16[256,1536]{1,0:T(8,128)(2,1)S(1)} %get-tuple-element.87), channel_id=1, source_target_pairs={{0,16},{16,0},{1,17},{17,1},{2,18},{18,2},{3,19},{19,3},{4,20},{20... | collective-permute-start | bytes 2359304 | tf_op jit(solution)/shard_map/ppermute | solution.py:370
  588.6 33.8 %collective-permute-start.61 = (bf16[256,1536]{1,0:T(8,128)(2,1)S(1)}, bf16[256,1536]{1,0:T(8,128)(2,1)S(1)}, u32[]{:S(2)}, u32[]{:S(2)}) collective-permute-start(bf16[256,1536]{1,0:T(8,128)(2,1)S(1)} %get-tuple-element.78), channel_id=1, source_target_pairs={{0,2},{1,3},{2,0},{3,1},{4,6},{5,7},{6,4},{7,5},{8,10},{9,11},{10,... | collective-permute-start | bytes 2359304 | tf_op jit(solution)/shard_map/ppermute | solution.py:374
  590.4 32.2 %collective-permute-start.65 = (bf16[256,1536]{1,0:T(8,128)(2,1)S(1)}, bf16[256,1536]{1,0:T(8,128)(2,1)S(1)}, u32[]{:S(2)}, u32[]{:S(2)}) collective-permute-start(bf16[256,1536]{1,0:T(8,128)(2,1)S(1)} %get-tuple-element.80), channel_id=1, source_target_pairs={{0,16},{16,0},{1,17},{17,1},{2,18},{18,2},{3,19},{19,3},{4,20},{20... | collective-permute-start | bytes 2359304 | tf_op jit(solution)/shard_map/ppermute | solution.py:370
  593.1 45.9 %collective-permute-start.64 = (bf16[256,1536]{1,0:T(8,128)(2,1)S(1)}, bf16[256,1536]{1,0:T(8,128)(2,1)S(1)}, u32[]{:S(2)}, u32[]{:S(2)}) collective-permute-start(bf16[256,1536]{1,0:T(8,128)(2,1)S(1)} %get-tuple-element.82), channel_id=1, source_target_pairs={{0,16},{16,0},{1,17},{17,1},{2,18},{18,2},{3,19},{19,3},{4,20},{20... | collective-permute-start | bytes 2359304 | tf_op jit(solution)/shard_map/ppermute | solution.py:370
  605.5 34.4 %collective-permute-start.67 = (bf16[256,1536]{1,0:T(8,128)(2,1)S(1)}, bf16[256,1536]{1,0:T(8,128)(2,1)S(1)}, u32[]{:S(2)}, u32[]{:S(2)}) collective-permute-start(bf16[256,1536]{1,0:T(8,128)(2,1)S(1)} %get-tuple-element.83), channel_id=1, source_target_pairs={{0,2},{1,3},{2,0},{3,1},{4,6},{5,7},{6,4},{7,5},{8,10},{9,11},{10,... | collective-permute-start | bytes 2359304 | tf_op jit(solution)/shard_map/ppermute | solution.py:374
  607.9 151.7 %collective-permute-start.87 = (bf16[256,1536]{1,0:T(8,128)(2,1)}, bf16[256,1536]{1,0:T(8,128)(2,1)}, u32[]{:S(2)}, u32[]{:S(2)}) collective-permute-start(bf16[256,1536]{1,0:T(8,128)(2,1)} %get-tuple-element.73), channel_id=1, source_target_pairs={{4,0},{5,1},{6,2},{7,3},{8,4},{9,5},{10,6},{11,7},{12,8},{13,9},{1... | collective-permute-start | bytes 2359304 | tf_op jit(solution)/shard_map/ppermute | solution.py:390
  622.4 33.6 %collective-permute-start.52 = (bf16[256,1536]{1,0:T(8,128)(2,1)S(1)}, bf16[256,1536]{1,0:T(8,128)(2,1)S(1)}, u32[]{:S(2)}, u32[]{:S(2)}) collective-permute-start(bf16[256,1536]{1,0:T(8,128)(2,1)S(1)} %get-tuple-element.86), channel_id=1, source_target_pairs={{0,2},{1,3},{2,0},{3,1},{4,6},{5,7},{6,4},{7,5},{8,10},{9,11},{10,... | collective-permute-start | bytes 2359304 | tf_op jit(solution)/shard_map/ppermute | solution.py:374
  622.6 35.9 %collective-permute-start.56 = (bf16[256,1536]{1,0:T(8,128)(2,1)S(1)}, bf16[256,1536]{1,0:T(8,128)(2,1)S(1)}, u32[]{:S(2)}, u32[]{:S(2)}) collective-permute-start(bf16[256,1536]{1,0:T(8,128)(2,1)S(1)} %get-tuple-element.88), channel_id=1, source_target_pairs={{0,16},{16,0},{1,17},{17,1},{2,18},{18,2},{3,19},{19,3},{4,20},{20... | collective-permute-start | bytes 2359304 | tf_op jit(solution)/shard_map/ppermute | solution.py:370
  639.0 33.8 %collective-permute-start.55 = (bf16[256,1536]{1,0:T(8,128)(2,1)S(1)}, bf16[256,1536]{1,0:T(8,128)(2,1)S(1)}, u32[]{:S(2)}, u32[]{:S(2)}) collective-permute-start(bf16[256,1536]{1,0:T(8,128)(2,1)S(1)} %get-tuple-element.90), channel_id=1, source_target_pairs={{0,16},{16,0},{1,17},{17,1},{2,18},{18,2},{3,19},{19,3},{4,20},{20... | collective-permute-start | bytes 2359304 | tf_op jit(solution)/shard_map/ppermute | solution.py:370
  639.8 36.2 %collective-permute-start.58 = (bf16[256,1536]{1,0:T(8,128)(2,1)S(1)}, bf16[256,1536]{1,0:T(8,128)(2,1)S(1)}, u32[]{:S(2)}, u32[]{:S(2)}) collective-permute-start(bf16[256,1536]{1,0:T(8,128)(2,1)S(1)} %get-tuple-element.91), channel_id=1, source_target_pairs={{0,2},{1,3},{2,0},{3,1},{4,6},{5,7},{6,4},{7,5},{8,10},{9,11},{10,... | collective-permute-start | bytes 2359304 | tf_op jit(solution)/shard_map/ppermute | solution.py:374
  656.0 34.0 %collective-permute-start.76 = (bf16[1536,512]{1,0:T(8,128)(2,1)S(1)}, bf16[1536,512]{1,0:T(8,128)(2,1)S(1)}, u32[]{:S(2)}, u32[]{:S(2)}) collective-permute-start(bf16[1536,512]{1,0:T(8,128)(2,1)S(1)} %get-tuple-element.68), channel_id=1, source_target_pairs={{0,4},{1,5},{2,6},{3,7},{4,8},{5,9},{6,10},{7,11},{8,12},{9,13},{1... | collective-permute-start | bytes 4718600 | tf_op jit(solution)/shard_map/ppermute | solution.py:386
  658.5 111.2 %collective-permute-start.79 = (bf16[1536,512]{1,0:T(8,128)(2,1)}, bf16[1536,512]{1,0:T(8,128)(2,1)}, u32[]{:S(2)}, u32[]{:S(2)}) collective-permute-start(bf16[1536,512]{1,0:T(8,128)(2,1)} %get-tuple-element.69), channel_id=1, source_target_pairs={{4,0},{5,1},{6,2},{7,3},{8,4},{9,5},{10,6},{11,7},{12,8},{13,9},{1... | collective-permute-start | bytes 4718600 | tf_op jit(solution)/shard_map/ppermute | solution.py:390
  672.8 86.8 %collective-permute-start.85 = (bf16[256,1536]{1,0:T(8,128)(2,1)}, bf16[256,1536]{1,0:T(8,128)(2,1)}, u32[]{:S(2)}, u32[]{:S(2)}) collective-permute-start(bf16[256,1536]{1,0:T(8,128)(2,1)} %add_convert_fusion.13), channel_id=1, source_target_pairs={{0,4},{1,5},{2,6},{3,7},{4,8},{5,9},{6,10},{7,11},{8,12},{9,13},{1... | collective-permute-start | bytes 2359304 | tf_op jit(solution)/shard_map/ppermute | solution.py:386
  691.9 77.9 %collective-permute-start.77 = (bf16[1536,512]{1,0:T(8,128)(2,1)}, bf16[1536,512]{1,0:T(8,128)(2,1)}, u32[]{:S(2)}, u32[]{:S(2)}) collective-permute-start(bf16[1536,512]{1,0:T(8,128)(2,1)} %add_convert_fusion.7), channel_id=1, source_target_pairs={{0,4},{1,5},{2,6},{3,7},{4,8},{5,9},{6,10},{7,11},{8,12},{9,13},{1... | collective-permute-start | bytes 4718600 | tf_op jit(solution)/shard_map/ppermute | solution.py:386
  759.2 242.3 %reduce-scatter.5.cloned.1.call-start = ((), (), s32[]{:S(2)}) async-start(), calls=%async_computation.5 | async-start | bytes 4866048 | tf_op jit(solution)/shard_map/reduce_scatter | solution.py:972
  776.8 91.9 %collective-permute-start.80 = (bf16[1536,512]{1,0:T(8,128)(2,1)}, bf16[1536,512]{1,0:T(8,128)(2,1)}, u32[]{:S(2)}, u32[]{:S(2)}) collective-permute-start(bf16[1536,512]{1,0:T(8,128)(2,1)} %get-tuple-element.67), channel_id=1, source_target_pairs={{4,0},{5,1},{6,2},{7,3},{8,4},{9,5},{10,6},{11,7},{12,8},{13,9},{1... | collective-permute-start | bytes 4718600 | tf_op jit(solution)/shard_map/ppermute | solution.py:390
  784.9 71.5 %collective-permute-start.89 = (bf16[256,1536]{1,0:T(8,128)(2,1)}, bf16[256,1536]{1,0:T(8,128)(2,1)}, u32[]{:S(2)}, u32[]{:S(2)}) collective-permute-start(bf16[256,1536]{1,0:T(8,128)(2,1)} %add_convert_fusion.10), channel_id=1, source_target_pairs={{4,0},{5,1},{6,2},{7,3},{8,4},{9,5},{10,6},{11,7},{12,8},{13,9},{1... | collective-permute-start | bytes 2359304 | tf_op jit(solution)/shard_map/ppermute | solution.py:390
  859.7 30.6 %collective-permute-start.90 = (bf16[256,1536]{1,0:T(8,128)(2,1)}, bf16[256,1536]{1,0:T(8,128)(2,1)}, u32[]{:S(2)}, u32[]{:S(2)}) collective-permute-start(bf16[256,1536]{1,0:T(8,128)(2,1)} %add_convert_fusion.9), channel_id=1, source_target_pairs={{0,0},{1,16},{2,2},{3,18},{4,4},{5,20},{6,6},{7,22},{8,8},{9,24},{... | collective-permute-start | bytes 2359304 | tf_op jit(solution)/shard_map/ppermute | solution.py:850
  865.8 30.9 %collective-permute-start.78 = (bf16[1536,512]{1,0:T(8,128)(2,1)}, bf16[1536,512]{1,0:T(8,128)(2,1)}, u32[]{:S(2)}, u32[]{:S(2)}) collective-permute-start(bf16[1536,512]{1,0:T(8,128)(2,1)} %get-tuple-element.66), channel_id=1, source_target_pairs={{0,4},{1,5},{2,6},{3,7},{4,8},{5,9},{6,10},{7,11},{8,12},{9,13},{1... | collective-permute-start | bytes 4718600 | tf_op jit(solution)/shard_map/ppermute | solution.py:386
  872.7 33.1 %collective-permute-start.81 = (bf16[1536,512]{1,0:T(8,128)(2,1)}, bf16[1536,512]{1,0:T(8,128)(2,1)}, u32[]{:S(2)}, u32[]{:S(2)}) collective-permute-start(bf16[1536,512]{1,0:T(8,128)(2,1)} %add_convert_fusion.4), channel_id=1, source_target_pairs={{4,0},{5,1},{6,2},{7,3},{8,4},{9,5},{10,6},{11,7},{12,8},{13,9},{1... | collective-permute-start | bytes 4718600 | tf_op jit(solution)/shard_map/ppermute | solution.py:390
  881.5 34.3 %collective-permute-start.69 = (bf16[512,1536]{1,0:T(8,128)(2,1)}, bf16[512,1536]{1,0:T(8,128)(2,1)}, u32[]{:S(2)}, u32[]{:S(2)}) collective-permute-start(bf16[512,1536]{1,0:T(8,128)(2,1)} %convolution_convert_fusion.3), channel_id=1, source_target_pairs={{0,16},{16,0},{1,17},{17,1},{2,18},{18,2},{3,19},{19,3},{4,20},{20... | collective-permute-start | bytes 4718600 | tf_op jit(solution)/shard_map/ppermute | solution.py:370
  924.1 23.8 %collective-permute-start.82 = (bf16[1536,256]{1,0:T(8,128)(2,1)S(1)}, bf16[1536,256]{1,0:T(8,128)(2,1)S(1)}, u32[]{:S(2)}, u32[]{:S(2)}) collective-permute-start(bf16[1536,256]{1,0:T(8,128)(2,1)S(1)} %get-tuple-element.94), channel_id=1, source_target_pairs={{0,0},{1,16},{2,2},{3,18},{4,4},{5,20},{6,6},{7,22},{8,8},{9,24},{... | collective-permute-start | bytes 2359304 | tf_op jit(solution)/shard_map/ppermute | solution.py:850
  954.8 48.4 %collective-permute-start.70 = (bf16[48,1280]{1,0:T(8,128)(2,1)S(1)}, bf16[48,1280]{1,0:T(8,128)(2,1)S(1)}, u32[]{:S(2)}, u32[]{:S(2)}) collective-permute-start(bf16[48,1280]{1,0:T(8,128)(2,1)S(1)} %get-tuple-element.113), channel_id=1, source_target_pairs={{0,16},{16,0},{1,17},{17,1},{2,18},{18,2},{3,19},{19,3},{4,20},{20... | collective-permute-start | bytes 368648 | tf_op jit(solution)/shard_map/ppermute | solution.py:370
  (87 other events, 1488.0 us)
Sparse Core Ops, SparseCore 0:
  15.2 51.2 all-gather.2
  69.4 74.4 all-gather.4
  759.4 86.8 reduce-scatter.2
  888.6 112.8 reduce-scatter.4

commit v2 on v1

--- a/solution.py
+++ b/solution.py
@@ -1,3 +1,5 @@
+import functools
+
 import jax
 import jax.numpy as jnp
 from jax import lax
@@ -359,6 +361,7 @@
 BF16 = jnp.bfloat16
 F32 = jnp.float32
 LINE = 4
+PAD = 128
 VMEM_BYTES = 60 * 1024 * 1024
 
 
@@ -390,18 +393,8 @@
     return lax.ppermute(value, "dp", [(i, i - 4) for i in range(4, 4 * LINE)])
 
 
-def sum_everywhere(value):
-    for mask in (1, 2, 4, 8):
-        value = value + swap_dp(value, mask)
-    return value + swap_seq(value)
-
-
-def line_gather(own):
-    ups, downs = [own], [own]
-    for _ in range(LINE - 1):
-        ups.append(line_up(ups[-1]))
-        downs.append(line_down(downs[-1]))
-    return ups[:0:-1] + [own] + downs[1:]
+def after(value, *others):
+    return lax.optimization_barrier((value,) + others)[0]
 
 
 def line_scatter(take, place):
@@ -418,43 +411,40 @@
     return take(place) + up.astype(F32) + down.astype(F32)
 
 
-def plane_gather(value, axis):
-    half = value.shape[axis] // 2
-    first = lax.slice_in_dim(value, 0, half, axis=axis)
-    second = lax.slice_in_dim(value, half, 2 * half, axis=axis)
-
-    def join(*pieces):
-        return lax.concatenate(pieces, axis)
-
-    first_near = swap_seq(first)
-    second_near = swap_y(second)
-    near = join(first_near, second_near)
-    far = join(
-        swap_y(first), swap_y(first_near), swap_seq(second), swap_seq(second_near)
-    )
-    return [
-        join(value, swap_core(value)),
-        join(near, swap_core(near)),
-        join(far, swap_core(far)),
-    ]
-
-
-def plane_scatter(pieces):
-    def over_cores(piece):
-        half = piece.shape[0] // 2
-        return piece[:half].astype(F32) + swap_core(piece[half:]).astype(F32)
-
-    far = over_cores(pieces[2]).astype(BF16)
-    near = over_cores(pieces[1])
-    own = over_cores(pieces[0])
-    half = own.shape[0] // 2
-    own_first = own[:half] + swap_y(far[:half]).astype(F32)
-    near_first = near[:half] + swap_y(far[half : 2 * half]).astype(F32)
-    own_second = own[half:] + swap_seq(far[2 * half : 3 * half]).astype(F32)
-    near_second = near[half:] + swap_seq(far[3 * half :]).astype(F32)
-    own_first = own_first + swap_seq(near_first.astype(BF16)).astype(F32)
-    own_second = own_second + swap_y(near_second.astype(BF16)).astype(F32)
-    return jnp.concatenate([own_first, own_second], axis=0)
+def near_pieces(own, own_x):
+    return swap_seq(own_x), swap_y(own)
+
+
+def far_pieces(near_x, near_y):
+    half = near_x.shape[0] // 2
+    return swap_y(near_x[:half]), swap_seq(near_y[half:])
+
+
+def with_cores(*pieces):
+    return pieces + tuple(swap_core(piece) for piece in pieces)
+
+
+def over_cores(mine, others):
+    return mine.astype(F32) + swap_core(others).astype(F32)
+
+
+def far_links(far):
+    half = far.shape[0] // 2
+    return swap_y(far[:half]), swap_seq(far[half:])
+
+
+def near_links(near, from_y, from_x):
+    half = from_y.shape[0] // 2
+    first = (near[:half] + from_y[half:].astype(F32)).astype(BF16)
+    second = (near[half : 2 * half] + from_x[half:].astype(F32)).astype(BF16)
+    return first, second
+
+
+def own_sum(near, from_y, from_x, first, second):
+    half = from_y.shape[0] // 2
+    low = near[2 * half : 3 * half] + from_y[:half].astype(F32) + first.astype(F32)
+    high = near[3 * half :] + from_x[:half].astype(F32) + second.astype(F32)
+    return jnp.concatenate([low, high], axis=0)
 
 
 def turned(values, cos, sin, direction):
@@ -493,7 +483,7 @@
 def project(x_sorted, gain, weights, cos, sin, q_width, kv_heads):
     rows, width = x_sorted.shape
     tile = 256
-    columns = weights.shape[1]
+    columns = q_width + 2 * kv_heads * HDIM
 
     def row_block(lanes):
         return pl.BlockSpec((tile, lanes), lambda i: (i, 0))
@@ -555,8 +545,8 @@
     return expon * (1.0 / jnp.sum(expon, axis=-1, keepdims=True))
 
 
-def attend_kernel(q_ref, k_ref, v_ref, start_ref, o_ref):
-    pair = pl.program_id(0)
+def attend_kernel(base, q_ref, k_ref, v_ref, start_ref, o_ref):
+    pair = pl.program_id(0) + base
     ratio = QHEADS // KVHEADS
     for row, low, high in windows(q_ref.shape[0]):
         allowed = allowed_keys(start_ref, row, low, high)
@@ -573,23 +563,22 @@
 def attention_cost(rows, heads, products):
     area = sum(Q_TILE * (high - low) for _, low, high in windows(rows))
     return pl.CostEstimate(
-        flops=2 * products * heads * area * 128,
+        flops=products * heads * area * 16,
         bytes_accessed=8 * rows * heads * HDIM,
         transcendentals=heads * area,
     )
 
 
-def attend(query, keys, values, starts):
-    rows, lanes = query.shape
-    pairs = lanes // (2 * HDIM)
-    pair_block = pl.BlockSpec((rows, 2 * HDIM), lambda j: (0, j))
+def attend(query, keys, values, starts, base, pairs):
+    rows = query.shape[0]
+    pair_block = pl.BlockSpec((rows, 2 * HDIM), lambda j: (0, j + base))
     whole = pl.BlockSpec(keys.shape, lambda j: (0, 0, 0))
     return pl.pallas_call(
-        attend_kernel,
+        functools.partial(attend_kernel, base),
         grid=(pairs,),
         in_specs=[pair_block, whole, whole, pl.BlockSpec((rows, 1), lambda j: (0, 0))],
-        out_specs=pair_block,
-        out_shape=jax.ShapeDtypeStruct(query.shape, BF16),
+        out_specs=pl.BlockSpec((rows, 2 * HDIM), lambda j: (0, j)),
+        out_shape=jax.ShapeDtypeStruct((rows, pairs * 2 * HDIM), BF16),
         compiler_params=pltpu.CompilerParams(vmem_limit_bytes=VMEM_BYTES),
         cost_estimate=attention_cost(rows, 2 * pairs, 2),
         name="attend",
@@ -672,118 +661,226 @@
 
 
 SLOTS = 2 * LINE - 1
-MOE_TILE = 512
-
-
-def experts_kernel(place_ref, *refs):
-    h_ref, g_ref, gate_ref = refs[:3]
-    in_slots, out_slots = refs[3 : 3 + SLOTS], refs[3 + SLOTS : 3 + 2 * SLOTS]
+SLOT_ORDER = (0, 3, 1, 2)
+OWN, NEAR_X, NEAR_Y, FAR_Y, FAR_X = range(5)
+FAR_TILES = (((NEAR_Y, 0), (FAR_Y, 0)), ((NEAR_X, 1), (FAR_X, 0)))
+NEAR_TILES = (((NEAR_X, 0), (NEAR_Y, 1)), ((OWN, 0), (OWN, 1)))
+
+
+def used_pieces(tiles):
+    return sorted({piece for tile in tiles for piece, _ in tile})
+
+
+def experts_kernel(tiles, half_rows, place_ref, *refs):
+    used = used_pieces(tiles)
+    sides = 2 * len(used)
+    h_pieces, g_pieces, slots = refs[:sides], refs[sides : 2 * sides], refs[2 * sides : 2 * sides + SLOTS]
+    select_ref = refs[2 * sides + SLOTS]
     (
-        f_ref, dh_ref, hidden_ref, du_ref, hcopy_ref, gcopy_ref, w_in, w_out, sems,
-    ) = refs[-9:]
-    part = in_slots[0].shape[1]
-    half = part // 2
-
-    def copies(expert, slot):
+        f_mine, f_other, d_mine, d_other, hid_a, hid_b, du_a, du_b, hcopy_ref, gcopy_ref,
+        w_in, w_out, h_buf, g_buf, hidden, du_all, weight_sems, row_sems,
+    ) = refs[-18:]
+    width = h_buf.shape[2]
+    half = slots[0].shape[1] // 3
+    part = 2 * half
+    step = pl.program_id(0)
+    steps = 2 * len(tiles)
+
+    def weight_copies(spot, slot):
         return (
             pltpu.make_async_copy(
-                in_slots[slot],
-                w_in.at[:, expert * part : (expert + 1) * part],
-                sems.at[0, expert],
+                slots[slot].at[:, :part],
+                w_in.at[:, spot * part : (spot + 1) * part],
+                weight_sems.at[0, spot],
             ),
             pltpu.make_async_copy(
-                out_slots[slot],
-                w_out.at[expert * half : (expert + 1) * half, :],
-                sems.at[1, expert],
+                slots[slot].at[:, part:],
+                w_out.at[:, spot * half : (spot + 1) * half],
+                weight_sems.at[1, spot],
             ),
         )
 
-    @pl.when(pl.program_id(0) == 0)
+    def row_copies(number, buffer):
+        side, tile = divmod(number, len(tiles))
+        copies = []
+        for spot, (piece, part_of) in enumerate(tiles[tile]):
+            index = side * len(used) + used.index(piece)
+            for kind, (pieces, held) in enumerate(((h_pieces, h_buf), (g_pieces, g_buf))):
+                copies.append(
+                    pltpu.make_async_copy(
+                        pieces[index].at[pl.ds(part_of * half_rows, half_rows), :],
+                        held.at[buffer, pl.ds(spot * half_rows, half_rows), :],
+                        row_sems.at[buffer, 2 * kind + spot],
+                    )
+                )
+        return copies
+
+    def fetch(wanted, buffer):
+        for number in range(steps):
+
+            @pl.when(wanted == number)
+            def _():
+                for copy in row_copies(number, buffer):
+                    copy.start()
+
+    buffer = step % 2
+
+    @pl.when(step == 0)
     def _():
-        for expert in range(LINE):
+        fetch(step, 0)
+        for spot, expert in enumerate(SLOT_ORDER):
             for slot in range(expert, expert + LINE):
 
                 @pl.when(slot == LINE - 1 + expert - place_ref[0])
                 def _():
-                    for copy in copies(expert, slot):
+                    for copy in weight_copies(spot, slot):
                         copy.start()
 
-        for expert in range(LINE):
-            for copy in copies(expert, LINE - 1):
-                copy.wait()
-
-    rows = h_ref[...]
-    grads = g_ref[...]
+    @pl.when(step + 1 < steps)
+    def _():
+        fetch(step + 1, 1 - buffer)
+
+    for copy in row_copies(0, buffer):
+        copy.wait()
+
+    rows = h_buf[buffer]
+    grads = g_buf[buffer, :, :width]
     hcopy_ref[...] = rows
     gcopy_ref[...] = grads
-    for expert in range(LINE):
+    gates = jnp.dot(g_buf[buffer, :, width:], select_ref[...], preferred_element_type=F32)
+    for spot in range(LINE):
+        units = slice(spot * half, (spot + 1) * half)
+
+        @pl.when(step == 0)
+        def _():
+            for copy in weight_copies(spot, LINE - 1):
+                copy.wait()
+
         both = jnp.dot(
-            rows, w_in[:, expert * part : (expert + 1) * part], preferred_element_type=F32
+            rows, w_in[:, spot * part : (spot + 1) * part], preferred_element_type=F32
         )
-        back = contract(grads, w_out[expert * half : (expert + 1) * half, :], 1, 1)
-        gate = gate_ref[:, expert : expert + 1]
+        back = jnp.dot(grads, w_out[:, units], preferred_element_type=F32)
+        gate = gates[:, units]
         first, second = both[:, :half], both[:, half:]
         sigma = jax.nn.sigmoid(first)
         silu = first * sigma
-        hidden_ref[:, expert * half : (expert + 1) * half] = (gate * (silu * second)).astype(BF16)
+        hidden[:, units] = (gate * (silu * second)).astype(BF16)
         back = back * (BRANCH_SCALE * gate)
         d_first = back * second * (sigma * (1.0 + first * (1.0 - sigma)))
         d_second = back * silu
-        du_ref[:, expert * part : expert * part + half] = d_first.astype(BF16)
-        du_ref[:, expert * part + half : (expert + 1) * part] = d_second.astype(BF16)
-    f_ref[...] = jnp.dot(hidden_ref[...], w_out[...], preferred_element_type=F32).astype(BF16)
-    dh_ref[...] = contract(du_ref[...], w_in[...], 1, 1).astype(BF16)
-
-
-def run_experts(place, rows, grads, gates, in_slots, out_slots, total, offset, kept):
-    count, width = rows.shape
-    part, half = in_slots[0].shape[1], out_slots[0].shape[0]
-    tile = MOE_TILE
-    base = offset // tile
-
-    def block(lanes):
-        return pl.BlockSpec((tile, lanes), lambda i, p: (i, 0))
+        du_all[:, spot * part : spot * part + half] = d_first.astype(BF16)
+        du_all[:, spot * part + half : (spot + 1) * part] = d_second.astype(BF16)
+    hid_a[...] = hidden[:, : 2 * half]
+    hid_b[...] = hidden[:, 2 * half :]
+    du_a[...] = du_all[:, : 2 * part]
+    du_b[...] = du_all[:, 2 * part :]
+    ffn = contract(hidden[...], w_out[...], 1, 1).astype(BF16)
+    back_rows = contract(du_all[...], w_in[...], 1, 1).astype(BF16)
+
+    @pl.when(step < len(tiles))
+    def _():
+        f_mine[...] = ffn
+        d_mine[...] = back_rows
+
+    @pl.when(step >= len(tiles))
+    def _():
+        f_other[...] = ffn
+        d_other[...] = back_rows
+
+
+def run_experts(tiles, place, row_pieces, grad_pieces, slots, select, base, kept):
+    used = used_pieces(tiles)
+    sides = len(row_pieces) // 2
+    wanted = used + [sides + piece for piece in used]
+    rows = [row_pieces[piece] for piece in wanted]
+    grads = [grad_pieces[piece] for piece in wanted]
+    tile, width = row_pieces[OWN].shape
+    wide = grad_pieces[OWN].shape[1]
+    half = slots[0].shape[1] // 3
+    part = 2 * half
+    count = len(tiles)
+    steps = 2 * count
+    total = 8 * tile
 
     def late(lanes):
         return pl.BlockSpec((tile, lanes), lambda i, p: (i + base, 0))
 
+    mine = pl.BlockSpec((tile, width), lambda i, p: (jnp.minimum(i, count - 1), 0))
+    others = pl.BlockSpec((tile, width), lambda i, p: (jnp.maximum(i - count, 0), 0))
     anywhere = pl.BlockSpec(memory_space=pl.ANY)
     kept = list(kept)
-    lead = 4 + 2 * SLOTS
+    lead = 1 + 2 * len(wanted) + SLOTS + 1
+    partial = jax.ShapeDtypeStruct((count * tile, width), BF16)
+    lanes = [2 * half, 2 * half, 2 * part, 2 * part, width, width]
     return pl.pallas_call(
-        experts_kernel,
+        functools.partial(experts_kernel, tiles, tile // 2),
         grid_spec=pltpu.PrefetchScalarGridSpec(
             num_scalar_prefetch=1,
-            grid=(count // tile,),
-            in_specs=[block(width), block(width), block(LINE)]
-            + [anywhere] * (2 * SLOTS + len(kept)),
-            out_specs=[
-                block(width), block(width),
-                late(LINE * half), late(LINE * part), late(width), late(width),
-            ],
+            grid=(steps,),
+            in_specs=[anywhere] * (2 * len(wanted) + SLOTS)
+            + [pl.BlockSpec(select.shape, lambda i, p: (0, 0))]
+            + [anywhere] * len(kept),
+            out_specs=[mine, others, mine, others] + [late(n) for n in lanes],
             scratch_shapes=[
                 pltpu.VMEM((width, LINE * part), BF16),
-                pltpu.VMEM((LINE * half, width), BF16),
+                pltpu.VMEM((width, LINE * half), BF16),
+                pltpu.VMEM((2, tile, width), BF16),
+                pltpu.VMEM((2, tile, wide), BF16),
+                pltpu.VMEM((tile, LINE * half), BF16),
+                pltpu.VMEM((tile, LINE * part), BF16),
                 pltpu.SemaphoreType.DMA((2, LINE)),
+                pltpu.SemaphoreType.DMA((2, 4)),
             ],
         ),
-        out_shape=[
-            jax.ShapeDtypeStruct((count, width), BF16),
-            jax.ShapeDtypeStruct((count, width), BF16),
-            jax.ShapeDtypeStruct((total, LINE * half), BF16),
-            jax.ShapeDtypeStruct((total, LINE * part), BF16),
-            jax.ShapeDtypeStruct((total, width), BF16),
-            jax.ShapeDtypeStruct((total, width), BF16),
-        ],
-        input_output_aliases={lead + i: 2 + i for i in range(len(kept))},
+        out_shape=[partial] * 4 + [jax.ShapeDtypeStruct((total, n), BF16) for n in lanes],
+        input_output_aliases={lead + i: 4 + i for i in range(len(kept))},
         compiler_params=pltpu.CompilerParams(vmem_limit_bytes=VMEM_BYTES),
         cost_estimate=pl.CostEstimate(
-            flops=2 * count * width * LINE * (2 * part + 2 * half),
-            bytes_accessed=2 * count * (6 * width + LINE * (part + half)),
-            transcendentals=count * LINE * half,
+            flops=steps * tile * width * LINE * (part + half) // 4,
+            bytes_accessed=2 * steps * tile * (6 * width + LINE * (part + half)),
+            transcendentals=steps * tile * LINE * half,
         ),
         name="experts",
-    )(place, rows, grads, gates, *in_slots, *out_slots, *kept)
+    )(place, *rows, *grads, *slots, select, *kept)
+
+
+def qkv_grad_kernel(h_ref, d_ref, gain_ref, o_ref):
+    shard = o_ref.shape[-2]
+    columns = d_ref.shape[1]
+    product = contract(h_ref[...], d_ref[...], 0, 0).astype(BF16)
+    gains = jnp.broadcast_to(gain_ref[...], (PAD, gain_ref.shape[1])).T.astype(BF16)
+    for block in range(h_ref.shape[1] // shard):
+        rows = slice(block * shard, (block + 1) * shard)
+        place = (block % 2, block // 2 % 2, 0, block // 4)
+        o_ref[place + (slice(None), slice(0, columns))] = product[rows]
+        o_ref[place + (slice(None), slice(columns, columns + PAD))] = gains[rows]
+
+
+def qkv_grad(normed, grads, gain_row, shard):
+    rows, width = normed.shape
+    columns = grads.shape[1]
+    tile = width // 4
+    planes = tile // (4 * shard)
+    return pl.pallas_call(
+        qkv_grad_kernel,
+        grid=(4,),
+        in_specs=[
+            pl.BlockSpec((rows, tile), lambda i: (0, i)),
+            pl.BlockSpec((rows, columns), lambda i: (0, 0)),
+            pl.BlockSpec((1, tile), lambda i: (0, i)),
+        ],
+        out_specs=pl.BlockSpec(
+            (2, 2, 1, planes, shard, columns + PAD), lambda i: (0, 0, i // 2, i % 2, 0, 0)
+        ),
+        out_shape=jax.ShapeDtypeStruct((2, 2, 2, LINE, shard, columns + PAD), BF16),
+        compiler_params=pltpu.CompilerParams(vmem_limit_bytes=VMEM_BYTES),
+        cost_estimate=pl.CostEstimate(
+            flops=rows * width * columns // 4,
+            bytes_accessed=2 * rows * (width + columns) + 2 * width * columns,
+            transcendentals=0,
+        ),
+        name="qkv_grad",
+    )(normed, grads, gain_row)
 
 
 def norm_back(value, gain, grad):
@@ -831,21 +928,6 @@
         half = weights.shape[1] // 2
         return lax.dynamic_slice_in_dim(weights, which * half, half, axis=1)
 
-    other_tokens = swap_seq(tokens)
-    projections = (w_query, w_key, w_value)
-    mine = jnp.concatenate([half_of(w, seq) for w in projections], axis=1)
-    theirs = jnp.concatenate([half_of(w, 1 - seq) for w in projections], axis=1)
-    theirs = swap_seq(theirs)
-    pair = jnp.stack([jnp.where(first_seq, mine, theirs), jnp.where(first_seq, theirs, mine)])
-    w_qkv = lax.all_gather(pair, "dp", axis=1, tiled=True).reshape(width, q_width + 2 * kv_width)
-    output_full = lax.all_gather(w_output, ("seq", "dp"), axis=0, tiled=True)
-
-    gains = jnp.stack([gain_attn, gain_ffn]).astype(F32)
-    index = seq * (4 * LINE) + data
-    gains = lax.dynamic_update_slice(jnp.zeros((2, width), F32), gains, (0, index * shard))
-    gains = sum_everywhere(gains)
-    gain_one, gain_two = gains[0], gains[1]
-
     def both_axes(value, pairs):
         return lax.ppermute(value, ("seq", "dp"), pairs)
 
@@ -859,29 +941,56 @@
             straight.append((device(s, d), device(c, d - c + s)))
             crossed.append((device(s, d), device(c, d - c + 1 - s)))
     crossed_back = [(there, here) for here, there in crossed]
+    first_core = core == 0
+
+    projections = (w_query, w_key, w_value)
+    gain_columns = jnp.pad(jnp.stack([gain_attn, gain_ffn], axis=1), ((0, 0), (0, PAD - 2)))
+    mine = jnp.concatenate([half_of(w, seq) for w in projections] + [gain_columns], axis=1)
+    theirs = jnp.concatenate([half_of(w, 1 - seq) for w in projections] + [gain_columns], axis=1)
+    theirs = swap_seq(theirs)
+    pair = jnp.stack([jnp.where(first_seq, mine, theirs), jnp.where(first_seq, theirs, mine)])
+    qkv_width = q_width + 2 * kv_width
+    w_qkv = lax.all_gather(pair, "dp", axis=1, tiled=True).reshape(width, qkv_width + PAD)
+    output_full = lax.all_gather(w_output, ("seq", "dp"), axis=0, tiled=True)
+
     in_own = w_in[0]
     half = in_own.shape[1] // 2
-    same = both_axes(lax.dynamic_slice_in_dim(in_own, seq * half, half, axis=1), straight)
+    sent = jnp.concatenate(
+        [lax.dynamic_slice_in_dim(in_own, seq * half, half, axis=1), w_out[0].T], axis=1
+    )
+    same = both_axes(sent, straight)
     cross = both_axes(lax.dynamic_slice_in_dim(in_own, (1 - seq) * half, half, axis=1), crossed)
-    first_core = core == 0
-    in_part = jnp.concatenate(
-        [jnp.where(first_core, same, cross), jnp.where(first_core, cross, same)], axis=1
-    )
-    out_part = both_axes(w_out[0], straight)
-    in_slots = line_gather(in_part)
-    out_slots = line_gather(out_part)
-
-    grad_pieces = plane_gather(cotangent, 0)
+    own_part = jnp.concatenate(
+        [
+            jnp.where(first_core, same[:, :half], cross),
+            jnp.where(first_core, cross, same[:, :half]),
+            same[:, half:],
+        ],
+        axis=1,
+    )
+    other_tokens = swap_seq(after(tokens, own_part))
+    up_one, down_one = line_up(own_part), line_down(own_part)
+
     experts_all = 4 * LINE
     gates = jax.nn.softmax(logits, axis=-1)
-    named = routes[None, :, :] == jnp.arange(experts_all, dtype=jnp.int32)[:, None, None]
-    gate_table = jnp.sum(jnp.where(named, gates[None], 0.0), axis=2)
-    gate_pieces = [
-        lax.dynamic_index_in_dim(
-            piece.reshape(LINE, 4, piece.shape[1]), 2 * row_of + seq, axis=1, keepdims=False
-        ).T
-        for piece in plane_gather(gate_table, 1)
-    ]
+    named = routes[:, :, None] == jnp.arange(experts_all, dtype=jnp.int32)[None, None, :]
+    gate_table = jnp.sum(jnp.where(named, gates[:, :, None], 0.0), axis=1)
+    gate_high = lax.reduce_precision(gate_table, 8, 7)
+    grad_rows = jnp.concatenate(
+        [
+            cotangent,
+            gate_high.astype(BF16),
+            (gate_table - gate_high).astype(BF16),
+            jnp.zeros((tok_count, PAD - 2 * experts_all), BF16),
+        ],
+        axis=1,
+    )
+    grad_near = near_pieces(grad_rows, after(grad_rows, other_tokens))
+    lane = jnp.arange(PAD, dtype=jnp.int32)[:, None]
+    hosted = jnp.repeat(
+        jnp.array(SLOT_ORDER, jnp.int32) * 4 + 2 * row_of + seq, half, total_repeat_length=LINE * half
+    )
+    select = ((lane % experts_all == hosted[None, :]) & (lane < 2 * experts_all)).astype(BF16)
 
     places = positions[0]
     ends = jnp.cumsum(lengths[0])
@@ -909,36 +1018,91 @@
         return contract(sort, values, 0, 0).astype(BF16)
 
     x_sorted = to_order(tokens, other_tokens)
+    gains = w_qkv[:, qkv_width : qkv_width + 2].astype(F32).T
+    gain_one, gain_two = gains[0], gains[1]
+    x_sorted, up_one, down_one = lax.optimization_barrier((x_sorted, up_one, down_one))
+    up_two, down_two = line_up(up_one), line_down(down_one)
     normed, query, keys, values = project(
         x_sorted, gain_one[None, :], w_qkv, cos, sin, q_width, kv_heads
     )
-    mixed_sorted = attend(query, keys, values, start_column)
-    mixed_other = swap_seq(from_order(sort_other, mixed_sorted))
-    mixed = ordered(from_order(sort_own, mixed_sorted), mixed_other, 1)
+    pairs = q_width // (2 * HDIM)
+    first_pairs = (pairs + 1) // 2
+    mixed_one = attend(query, keys, values, start_column, 0, first_pairs)
+    sent_one = swap_seq(from_order(sort_other, mixed_one))
+    query_two, grad_near_x, grad_near_y = after((query, *grad_near), mixed_one)
+    grad_near = (grad_near_x, grad_near_y)
+    grad_far = far_pieces(*grad_near)
+    mixed_two = attend(
+        query_two, keys, values, start_column, first_pairs, pairs - first_pairs
+    )
+    sent_two = swap_seq(from_order(sort_other, mixed_two))
+    mixed_mine = [from_order(sort_own, mixed_one), from_order(sort_own, mixed_two)]
+    mixed = ordered(
+        jnp.concatenate(mixed_mine, axis=1), jnp.concatenate([sent_one, sent_two], axis=1), 1
+    )
+    mixed, up_two, down_two = lax.optimization_barrier((mixed, up_two, down_two))
+    up_three, down_three = line_up(up_two), line_down(down_two)
     inputs = tokens.astype(F32)
     attn = jnp.dot(mixed, output_full, preferred_element_type=F32)
     middle = inputs + BRANCH_SCALE * attn
     normed_ffn = rms_norm(middle, gain_two).astype(BF16)
 
-    row_pieces = plane_gather(normed_ffn, 0)
-    total = 8 * tok_count
+    normed_ffn = after(normed_ffn, *grad_far)
+    row_near = near_pieces(normed_ffn, normed_ffn)
+    row_far = far_pieces(*row_near)
+    slots = [up_three, up_two, up_one, own_part, down_one, down_two, down_three]
+    row_pieces = with_cores(normed_ffn, *row_near, *row_far)
+    grad_pieces = with_cores(*after((grad_rows, *grad_near, *grad_far), row_near[0]))
     place = line.astype(jnp.int32)[None]
-    ffn_pieces, back_pieces, kept, offset = [], [], (), 0
-    for rows, grads, gate in zip(row_pieces, grad_pieces, gate_pieces):
-        result = run_experts(
-            place, rows, grads, gate, in_slots, out_slots, total, offset, kept
-        )
-        ffn_pieces.append(result[0])
-        back_pieces.append(result[1])
-        kept = tuple(result[2:])
-        offset = offset + rows.shape[0]
-    hidden, grad_both, all_rows, all_grads = kept
-
-    grad_normed_ffn = plane_scatter(back_pieces)
-    grad_in_all = contract(all_rows, grad_both, 0, 0)
-    grad_out_all = contract(hidden, all_grads, 0, 0) * BRANCH_SCALE
-    ffn = plane_scatter(ffn_pieces)
-    output = (middle + BRANCH_SCALE * ffn).astype(BF16)
+    far = run_experts(FAR_TILES, place, row_pieces, grad_pieces, slots, select, 0, ())
+    far_back = over_cores(far[2], far[3]).astype(BF16)
+    back_y, back_x = far_links(far_back)
+    near = run_experts(
+        NEAR_TILES, after(place, far_back), row_pieces, grad_pieces, slots, select, 4, far[4:]
+    )
+    hid_a, hid_b, du_a, du_b, all_rows, all_grads = near[4:]
+
+    def weight_grads(rows, grads, grad_both, hidden):
+        inner = contract(rows, grad_both, 0, 0)
+        outer = contract(grads, hidden, 0, 0) * BRANCH_SCALE
+        return [
+            jnp.concatenate(
+                [inner[:, 2 * half * i : 2 * half * (i + 1)], outer[:, half * i : half * (i + 1)]],
+                axis=1,
+            ).astype(BF16)
+            for i in range(2)
+        ]
+
+    rows_early, grads_early, back_y, back_x = lax.optimization_barrier(
+        (all_rows, all_grads, back_y, back_x)
+    )
+    outer_grads = weight_grads(rows_early, grads_early, du_a, hid_a)
+    grads_of = dict(zip(SLOT_ORDER[:2], outer_grads))
+    far_line = (line_up(outer_grads[1]), line_down(outer_grads[0]))
+    near_back = over_cores(after(near[2], *outer_grads), near[3])
+    first, second = near_links(near_back, back_y, back_x)
+    rows_late, grads_late = after((all_rows, all_grads), first, second)
+    inner_grads = weight_grads(rows_late, grads_late, du_b, hid_b)
+    grads_of.update(zip(SLOT_ORDER[2:], inner_grads))
+    first, second = swap_seq(first), swap_y(second)
+    near_back = after(near_back, *inner_grads)
+    grad_normed_ffn = own_sum(near_back, back_y, back_x, first, second)
+
+    def line_partial(first, *rest):
+        value = grads_of[first]
+        for where, expert in enumerate(rest):
+            value = jnp.where(line > where, grads_of[expert], value)
+        return value.astype(F32)
+
+    def line_step(step, arrived):
+        up, down = arrived
+        last = LINE - 1
+        right = line_partial(*range(last - step, LINE)) + up.astype(F32)
+        left = grads_of[step]
+        for where in range(step):
+            left = jnp.where(line < last - where, grads_of[step - 1 - where], left)
+        left = left.astype(F32) + down.astype(F32)
+        return right.astype(BF16), left.astype(BF16)
 
     grad_final = cotangent.astype(F32)
     grad_norm, grad_gain_two = norm_back(middle, gain_two, grad_normed_ffn)
@@ -947,46 +1111,75 @@
     grad_mixed = contract(grad_attn, output_full, 1, 1).astype(BF16)
     grad_w_output = contract(mixed, grad_attn, 0, 0)
     grad_other = swap_seq(half_of(grad_mixed, 1 - seq))
+    far_f, far_f_other, near_f, near_f_other = after(
+        (far[0], far[1], near[0], near[1]), grad_mixed
+    )
+    far_ffn = over_cores(far_f, far_f_other).astype(BF16)
+    ffn_y, ffn_x = far_links(far_ffn)
+    near_ffn = over_cores(near_f, near_f_other)
+    right, left = line_step(1, far_line)
+    grad_other = after(grad_other, right, left, far_ffn)
     grad_sorted = to_order(half_of(grad_mixed, seq), grad_other)
+    mid_line = (line_up(right), line_down(left))
     grad_query, grad_keys, grad_values = attend_back(
         query, keys, values, grad_sorted, start_column, cos, sin
     )
+    (grad_query, grad_keys, grad_values), mid_line, ffn_y, ffn_x = lax.optimization_barrier(
+        ((grad_query, grad_keys, grad_values), mid_line, ffn_y, ffn_x)
+    )
+    right, left = line_step(2, mid_line)
+    last_line = (line_up(right), line_down(left))
+    first_ffn, second_ffn = near_links(near_ffn, ffn_y, ffn_x)
+    first_ffn, second_ffn = swap_seq(first_ffn), swap_y(second_ffn)
+    ffn = own_sum(near_ffn, ffn_y, ffn_x, first_ffn, second_ffn)
+    output = (middle + BRANCH_SCALE * ffn).astype(BF16)
     grad_qkv = jnp.concatenate([grad_query, grad_keys, grad_values], axis=1)
-    grad_w_qkv = contract(normed, grad_qkv, 0, 0)
-    grad_normed = contract(grad_qkv, w_qkv, 1, 1).astype(BF16)
+    grad_qkv = after(grad_qkv, right, left)
+    wide = qkv_grad(normed, grad_qkv, grad_gain_two[None, :], shard)
+    grad_normed = contract(grad_qkv, w_qkv[:, :qkv_width], 1, 1).astype(BF16)
     sent_normed = swap_seq(from_order(sort_other, grad_normed))
     grad_normed = from_order(sort_own, grad_normed).astype(F32) + sent_normed.astype(F32)
-    grad_first, grad_gain_one = norm_back(inputs, gain_one, grad_normed)
-    grad_tokens = grad_middle + grad_first
-
-    def expert_part(grads, size, axis):
-        return lambda which: lax.dynamic_slice_in_dim(grads, which * size, size, axis=axis)
-
-    grad_in_part = line_scatter(expert_part(grad_in_all, 2 * half, 1), line).astype(BF16)
-    grad_out_part = line_scatter(expert_part(grad_out_all, half, 0), line).astype(BF16)
-    grad_w_out = both_axes(grad_out_part, straight)
-    same = jnp.where(first_core, grad_in_part[:, :half], grad_in_part[:, half:])
-    cross = jnp.where(first_core, grad_in_part[:, half:], grad_in_part[:, :half])
-    grad_w_in = ordered(both_axes(same, straight), both_axes(cross, crossed_back), 1)
+    scale = lax.rsqrt(jnp.mean(inputs * inputs, axis=-1, keepdims=True) + EPSILON)
+    unit = inputs * scale
+    scaled = grad_normed * gain_one
+    inner = jnp.mean(scaled * unit, axis=-1, keepdims=True)
+    grad_tokens = grad_middle + scale * (scaled - unit * inner)
 
     summed_output = lax.psum_scatter(
         grad_w_output.astype(BF16), ("seq", "dp"), scatter_dimension=0, tiled=True
     )
-    summed_qkv = lax.psum_scatter(
-        grad_w_qkv.astype(BF16).reshape(2, width // 2, q_width + 2 * kv_width),
-        "dp",
-        scatter_dimension=1,
-        tiled=True,
-    )
-    kept_rows = lax.dynamic_index_in_dim(summed_qkv, seq, axis=0, keepdims=False)
-    sent_rows = swap_seq(lax.dynamic_index_in_dim(summed_qkv, 1 - seq, axis=0, keepdims=False))
-    cuts = (q_width, q_width + kv_width)
-    grad_projections = [
-        ordered(a, b, 1).astype(F32)
-        for a, b in zip(jnp.split(kept_rows, cuts, axis=1), jnp.split(sent_rows, cuts, axis=1))
+
+    def chosen(value, which, axis):
+        return lax.dynamic_index_in_dim(value, which, axis=axis, keepdims=False)
+
+    kept = chosen(wide, core, 0).astype(F32)
+    kept = kept + swap_core(chosen(wide, 1 - core, 0)).astype(F32)
+    next_kept = chosen(kept, row_of, 0)
+    next_kept = next_kept + swap_y(chosen(kept, 1 - row_of, 0).astype(BF16)).astype(F32)
+    next_kept, last_line = lax.optimization_barrier((next_kept, last_line))
+    summed = line_scatter(lambda which: chosen(next_kept, which, 1), line)
+    part_grads = (
+        line_partial(*range(LINE)) + last_line[0].astype(F32) + last_line[1].astype(F32)
+    ).astype(BF16)
+    same_grads = jnp.where(first_core, part_grads[:, :half], part_grads[:, half : 2 * half])
+    cross_grads = jnp.where(first_core, part_grads[:, half : 2 * half], part_grads[:, :half])
+    same = both_axes(jnp.concatenate([same_grads, part_grads[:, 2 * half :]], axis=1), straight)
+    cross = both_axes(cross_grads, crossed_back)
+    grad_w_in = ordered(same[:, :half], cross, 1)
+    grad_w_out = same[:, half:].T
+
+    kept_rows = chosen(summed, seq, 0)
+    sent_rows = swap_seq(chosen(summed, 1 - seq, 0).astype(BF16)).astype(F32)
+    cuts = (q_width, q_width + kv_width, qkv_width)
+    pieces = [
+        (a, b) for a, b in zip(jnp.split(kept_rows, cuts, axis=1), jnp.split(sent_rows, cuts, axis=1))
     ]
-    grad_gains = sum_everywhere(jnp.stack([grad_gain_one, grad_gain_two]))
-    grad_gains = lax.dynamic_slice_in_dim(grad_gains, index * shard, shard, axis=1)
+    grad_projections = [ordered(a, b, 1) for a, b in pieces[:3]]
+    grad_gain_ffn = (pieces[3][0] + pieces[3][1])[:, 0]
+    grad_gain_attn = sum(
+        jnp.sum(grad * weight.astype(F32), axis=1)
+        for grad, weight in zip(grad_projections, projections)
+    ) / gain_attn.astype(F32)
     return (
         output,
         grad_tokens,
@@ -994,8 +1187,8 @@
         grad_projections[1],
         grad_projections[2],
         summed_output.astype(F32),
-        grad_gains[0],
-        grad_gains[1],
+        grad_gain_attn,
+        grad_gain_ffn,
         grad_w_in.astype(F32)[None],
         grad_w_out.astype(F32)[None],
     )

time: 1020 us -> 769 us (0.75)
  waiting for transfers between devices: 386 us -> 189 us
  starting transfers between devices: 158 us -> 110 us
  Pallas kernels: 187 us -> 231 us
  other arithmetic: 113 us -> 84.5 us
  local copies, waits for them, and re-layouts: 53.5 us -> 32.2 us
    ppermute x12 -> x9, waiting for transfers between devices: 115 us -> 5.61 us  [line_down(): return lax.ppermute(value, 'dp', [(i, i - 4) for i in range(4, 4 * LINE)])]
    ppermute x38 -> x24, waiting for transfers between devices: 74.3 us -> 21.2 us  [swap_dp(): return lax.ppermute(value, 'dp', [(i, i ^ mask) for i in range(4 * LINE)])]
    reduce_scatter x1, waiting for transfers between devices: 45.8 us -> 0.01 us  [shards_plane(): lax.psum_scatter(grad_w_output.astype(BF16), ('seq', 'dp'), scatter_dimen...]
    pallas_call x4 -> x5, Pallas kernels: 131 us -> 175 us  [the longest x2 136 us: run_experts(): pl.pallas_call(functools.partial(experts_kernel, tiles, tile // 2), grid_...]
    ppermute x38 -> x24, starting transfers between devices: 49.2 us -> 26.4 us  [swap_dp(): return lax.ppermute(value, 'dp', [(i, i ^ mask) for i in range(4 * LINE)])]
    concatenate x14 -> x7, other arithmetic: 25.3 us -> 5.48 us  [the longest x2 3.42 us: weight_grads(): jnp.concatenate([inner[:, 2 * half * i:2 * half * (i + 1)], outer[:, half...]
    ppermute x23 -> x15, waiting for transfers between devices: 81.6 us -> 100 us  [swap_seq(): return lax.ppermute(value, 'seq', [(0, 1), (1, 0)])]
    convert_element_type x4 -> x2, other arithmetic: 15 us -> 1.31 us  [line_scatter(): up = line_up(right.astype(BF16))]
  transfers between devices with their start and end apart: 95 -> 64, of which waited for: 39 -> 18; matrix products, arithmetic and copies ran while one was open for 23% -> 27% of each run, Pallas kernels for 14% -> 21%
where the time goes in v2:
time: 769 us; the launch traced here: 758 us
  Pallas kernels  231 us (30%)
  waiting for transfers between devices  189 us (25%)
  starting transfers between devices  110 us (14%)
  matrix products  95.5 us (12%)
  other arithmetic  84.5 us (11%)
  local copies, waits for them, and re-layouts  32.2 us (4%)
  between operations  15.4 us (2%)
    pallas_call x2, Pallas kernels, run_experts(): pl.pallas_call(functools.partial(experts_kernel, tiles, tile // 2), grid_...  136 us
    ppermute x15, waiting for transfers between devices, swap_seq(): return lax.ppermute(value, 'seq', [(0, 1), (1, 0)])  100 us
    dot_general x17, matrix products, contract(): lax.dot_general(left, right, (((left_dim,), (right_dim,)), ((), ())), pre...  89.2 us
    pallas_call x1, Pallas kernels, attend_back(): pl.pallas_call(attend_back_kernel, grid=(pairs,), in_specs=[pair_block, w...  45.8 us
    ppermute x9, starting transfers between devices, line_up(): return lax.ppermute(value, 'dp', [(i, i + 4) for i in range(4 * LINE - 4)])  40.9 us
    ppermute x9, waiting for transfers between devices, line_up(): return lax.ppermute(value, 'dp', [(i, i + 4) for i in range(4 * LINE - 4)])  35.9 us
    pallas_call x2, Pallas kernels, attend(): pl.pallas_call(functools.partial(attend_kernel, base), grid=(pairs,), in_...  30 us
    ppermute x24, starting transfers between devices, swap_dp(): return lax.ppermute(value, 'dp', [(i, i ^ mask) for i in range(4 * LINE)])  26.4 us
  transfers between devices with their start and end apart: 64, of which 18 were waited for; matrix products, arithmetic and copies ran while one was open for 27% of the time, Pallas kernels for 21%

profile of v2, /device:TPU:1, one launch (start us, length us, event | category | flops | bytes accessed | tf_op | source)
XLA Modules:
  0.0 758.0 jit_solution(17885212496209162831)
XLA Ops:
  12.1 3.3 collective-permute-done.5
  18.4 4.5 collective-permute-start
  23.2 25.6 %collective-permute-done.1 = bf16[1536,256]{1,0:T(8,128)(2,1)} collective-permute-done((bf16[1536,256]{1,0:T(8,128)(2,1)}, bf16[1536,256]{1,0:T(8,128)(2,1)}, u32[]{:S(2)}, u32[]{:S(2)}) %collective-permute-start.1) | collective-permute-done | bytes 786464 | tf_op jit(solution)/shard_map/ppermute | solution.py:932
  50.3 4.7 collective-permute-start.3
  58.9 3.8 concatenate.91.refs_6_
  70.8 23.3 %collective-permute-done.2 = bf16[512,1536]{1,0:T(8,128)(2,1)} collective-permute-done((bf16[512,1536]{1,0:T(8,128)(2,1)}, bf16[512,1536]{1,0:T(8,128)(2,1)}, u32[]{:S(2)}, u32[]{:S(2)}) %collective-permute-start.2) | collective-permute-done | bytes 1572896 | tf_op jit(solution)/shard_map/ppermute | solution.py:373
  96.4 4.9 add_convert_fusion.2.x_ref
  101.3 21.1 %collective-permute-done.3.refs_18_.refs_14_ = bf16[1536,768]{1,0:T(8,128)(2,1)} collective-permute-done((bf16[1536,768]{1,0:T(8,128)(2,1)S(1)}, bf16[1536,768]{1,0:T(8,128)(2,1)}, u32[]{:S(2)}, u32[]{:S(2)}) %collective-permute-start.3) | collective-permute-done | bytes 2359328 | tf_op jit(solution)/shard_map/ppermute | solution.py:389
  122.4 2.7 collective-permute-done.4.refs_20_.refs_16_
  125.1 4.1 collective-permute-start.10
  133.6 10.4 %project.1 = (bf16[1024,1536]{1,0:T(8,128)(2,1)}, bf16[1024,768]{1,0:T(8,128)(2,1)}, bf16[4,1024,64]{2,1,0:T(8,128)(2,1)}, bf16[4,1024,64]{2,1,0:T(8,128)(2,1)}) custom-call(bf16[1024,1536]{1,0:T(8,128)(2,1)} %add_convert_fusion.2.x_ref, f32[1,1536]{1,0:T(1,128)} %copy.83.gain_ref, bf16[1536,1408]{1,0:T(8,128)(2,1)} %bitcast.96, ...), custom_call_target="tpu_custom_call" | custom-call | flops 4026531840 | bytes 12845056 | tf_op jit(solution)/shard_map/project/pallas_call | solution.py:492
  144.0 15.0 %attend.2 = bf16[1024,384]{1,0:T(8,128)(2,1)} custom-call(bf16[1024,768]{1,0:T(8,128)(2,1)} %get-tuple-element.97.q_ref, bf16[4,1024,64]{2,1,0:T(8,128)(2,1)} %get-tuple-element.94.k_ref, bf16[4,1024,64]{2,1,0:T(8,128)(2,1)} %get-tuple-element.95.v_ref, s32[1024,1]{1,0:T(8,128)} %copy.84.start_ref), custom_call_target="tpu_custom_call" | custom-call | flops 113246208 | bytes 3145728 | tf_op jit(solution)/shard_map/attend/pallas_call | solution.py:576
  160.8 2.6 collective-permute-start.8
  163.4 15.0 %attend.3 = bf16[1024,384]{1,0:T(8,128)(2,1)} custom-call(bf16[1024,768]{1,0:T(8,128)(2,1)} %get-tuple-element.97.q_ref, bf16[4,1024,64]{2,1,0:T(8,128)(2,1)} %get-tuple-element.94.k_ref, bf16[4,1024,64]{2,1,0:T(8,128)(2,1)} %get-tuple-element.95.v_ref, s32[1024,1]{1,0:T(8,128)} %copy.84.start_ref), custom_call_target="tpu_custom_call" | custom-call | flops 113246208 | bytes 3145728 | tf_op jit(solution)/shard_map/attend/pallas_call | solution.py:576
  192.4 5.0 collective-permute-start.26
  198.7 6.3 multiply_reduce_fusion.2
  205.4 2.7 collective-permute-done.13.refs_11_
  209.9 32.2 %collective-permute-done.14.refs_0_.refs_1_ = bf16[512,1536]{1,0:T(8,128)(2,1)} collective-permute-done((bf16[512,1536]{1,0:T(8,128)(2,1)S(1)}, bf16[512,1536]{1,0:T(8,128)(2,1)}, u32[]{:S(2)}, u32[]{:S(2)}) %collective-permute-start.14) | collective-permute-done | bytes 1572896 | tf_op jit(solution)/shard_map/ppermute | solution.py:373
  246.6 3.3 collective-permute-start.24
  250.2 3.0 collective-permute-start.22
  253.2 6.2 collective-permute-done.16.refs_2_
  259.4 3.9 collective-permute-start.23
  269.3 2.6 select_select_fusion
  272.7 72.5 %experts.2 = (bf16[1024,1536]{1,0:T(8,128)(2,1)}, bf16[1024,1536]{1,0:T(8,128)(2,1)}, bf16[1024,1536]{1,0:T(8,128)(2,1)}, bf16[1024,1536]{1,0:T(8,128)(2,1)}, bf...) custom-call(s32[1]{0:T(128)} %bitcast.15.place_ref, ...), custom_call_target="tpu_custom_call" | custom-call | flops 2415919104 | bytes 50331648 | tf_op jit(solution)/shard_map/experts/pallas_call | solution.py:815
  346.2 8.1 %collective-permute-done.28 = bf16[1024,1536]{1,0:T(8,128)(2,1)S(1)} collective-permute-done((bf16[1024,1536]{1,0:T(8,128)(2,1)}, bf16[1024,1536]{1,0:T(8,128)(2,1)S(1)}, u32[]{:S(2)}, u32[]{:S(2)}) %collective-permute-start.28) | collective-permute-done | bytes 3145760 | tf_op jit(solution)/shard_map/ppermute | solution.py:377
  354.3 2.7 add_convert_fusion.1
  362.7 63.7 %experts.3 = (bf16[1024,1536]{1,0:T(8,128)(2,1)}, bf16[1024,1536]{1,0:T(8,128)(2,1)}, bf16[1024,1536]{1,0:T(8,128)(2,1)}, bf16[1024,1536]{1,0:T(8,128)(2,1)}, bf...) custom-call(s32[1]{0:T(128)} %bitcast.15.place_ref, ...), custom_call_target="tpu_custom_call", output_to_operand_aliasing={{4}: (21, {}), {5}: (22, {}), {6}: (23, {}), {7}: (24, {}),... | custom-call | flops 2415919104 | bytes 50331648 | tf_op jit(solution)/shard_map/experts/pallas_call | solution.py:815
  427.4 11.7 %fusion.14 = bf16[1536,512]{1,0:T(8,128)(2,1)S(1)} fusion(bf16[4096,1536]{1,0:T(8,128)(2,1)} %get-tuple-element.137, bf16[4096,512]{1,0:T(8,128)(2,1)} %get-tuple-element.130), kind=kOutput, calls=%fused_computation.42 | convolution fusion | flops 6444023808 | bytes 18350080 | tf_op jit(solution)/shard_map/dot_general | solution.py:537
  439.3 14.0 %convolution_convert_fusion.2 = bf16[1536,1024]{1,0:T(8,128)(2,1)S(1)} fusion(bf16[4096,1536]{1,0:T(8,128)(2,1)S(1)} %copy-done.21, bf16[4096,1024]{1,0:T(8,128)(2,1)S(1)} %copy-done.25), kind=kOutput, calls=%fused_computation.18 | convolution fusion | flops 12886474752 | bytes 24117248 | tf_op jit(solution)/shard_map/dot_general | solution.py:537
  455.3 4.8 collective-permute-start.38
  463.0 2.9 convert_add_fusion.1
  465.9 3.1 fusion.28
  470.4 16.4 %convolution_convert_fusion.1 = bf16[1536,1024]{1,0:T(8,128)(2,1)S(1)} fusion(bf16[4096,1536]{1,0:T(8,128)(2,1)S(1)} %copy-done.21, bf16[4096,1024]{1,0:T(8,128)(2,1)} %get-tuple-element.136), kind=kOutput, calls=%fused_computation.17 | convolution fusion | flops 12886474752 | bytes 24117248 | tf_op jit(solution)/shard_map/dot_general | solution.py:537
  486.8 11.2 %fusion.15 = bf16[1536,512]{1,0:T(8,128)(2,1)S(1)} fusion(bf16[4096,1536]{1,0:T(8,128)(2,1)} %get-tuple-element.137, bf16[4096,512]{1,0:T(8,128)(2,1)} %get-tuple-element.138), kind=kOutput, calls=%fused_computation.43 | convolution fusion | flops 6444023808 | bytes 18350080 | tf_op jit(solution)/shard_map/dot_general | solution.py:537
  503.1 2.6 convolution_convert_fusion.5
  509.6 3.2 add_convert_fusion.7
  512.8 5.6 collective-permute-start.41
  518.4 3.4 add_convert_fusion.6
  523.7 4.4 convolution_convert_fusion
  528.1 3.7 add_convert_fusion
  536.2 3.4 add_convert_fusion.8.d_ref
  539.5 45.8 %attend_back.1 = (bf16[1024,768]{1,0:T(8,128)(2,1)}, bf16[1024,256]{1,0:T(8,128)(2,1)}, bf16[1024,256]{1,0:T(8,128)(2,1)}) custom-call(bf16[1024,768]{1,0:T(8,128)(2,1)} %get-tuple-element.97.q_ref, bf16[4,1024,64]{2,1,0:T(8,128)(2,1)} %get-tuple-element.94.k_ref, bf16[4,1024,64]{2,1,0:T(8,128)(2,1)} %get-tuple-element.95.v_ref, ...), custom_call_target="tpu_custom_call" | custom-call | flops 566231040 | bytes 6291456 | tf_op jit(solution)/shard_map/attend_back/pallas_call | solution.py:644
  585.4 3.9 convert_add_fusion
  589.4 3.1 fusion.25
  594.2 5.2 add_convert_fusion.4
  601.1 8.4 %qkv_grad.1 = bf16[2,2,2,4,48,1408]{5,4,3,2,1,0:T(8,128)(2,1)} custom-call(bf16[1024,1536]{1,0:T(8,128)(2,1)} %get-tuple-element.156.h_ref, bf16[1024,1280]{1,0:T(8,128)(2,1)} %pad_maximum_fusion.1.d_ref, f32[1,1536]{1,0:T(1,128)} %broadcast_in_dim.42.gain_ref), custom_call_target="tpu_custom_call" | custom-call | flops 503316480 | bytes 9699328 | tf_op jit(solution)/shard_map/qkv_grad/pallas_call | solution.py:864
  609.5 3.3 dynamic-slice_bitcast_fusion
  614.9 4.5 fusion.26
  619.8 4.7 fusion.2
  624.6 3.0 convolution_convert_fusion.3
  628.6 4.4 collective-permute-start.50
  634.2 5.5 collective-permute-done.46
  641.9 2.8 convert_add_fusion.3
  644.9 17.9 %collective-permute-done.47 = bf16[512,1536]{1,0:T(8,128)(2,1)} collective-permute-done((bf16[512,1536]{1,0:T(8,128)(2,1)}, bf16[512,1536]{1,0:T(8,128)(2,1)}, u32[]{:S(2)}, u32[]{:S(2)}) %collective-permute-start.47) | collective-permute-done | bytes 1572896 | tf_op jit(solution)/shard_map/ppermute | solution.py:373
  662.9 4.0 fusion.7
  669.5 14.7 %collective-permute-done.50 = bf16[1536,768]{1,0:T(8,128)(2,1)S(1)} collective-permute-done((bf16[1536,768]{1,0:T(8,128)(2,1)}, bf16[1536,768]{1,0:T(8,128)(2,1)S(1)}, u32[]{:S(2)}, u32[]{:S(2)}) %collective-permute-start.50) | collective-permute-done | bytes 2359328 | tf_op jit(solution)/shard_map/ppermute | solution.py:389
  684.2 2.5 collective-permute-done.51
  686.8 3.9 collective-permute-start.52
  698.0 4.1 collective-permute-start.53
  702.1 5.5 add_convert_fusion.3
  709.3 2.5 collective-permute-start.60
  711.8 4.3 collective-permute-start.54
  717.6 5.9 collective-permute-start.59
  724.5 19.2 %collective-permute-done.58 = bf16[48,1408]{1,0:T(8,128)(2,1)S(1)} collective-permute-done((bf16[48,1408]{1,0:T(8,128)(2,1)S(1)}, bf16[48,1408]{1,0:T(8,128)(2,1)S(1)}, u32[]{:S(2)}, u32[]{:S(2)}) %collective-permute-start.58) | collective-permute-done | bytes 135200 | tf_op jit(solution)/shard_map/ppermute | solution.py:373
  (332 shorter events, 119.9 us)
Async XLA Ops:
  7.2 123.4 %all-gather.3.cloned.1.call-start = ((), (), s32[]{:S(2)}) async-start(), calls=%async_computation.1 | async-start | bytes 4595712 | tf_op jit(solution)/shard_map/all_gather | solution.py:953
  10.0 5.4 collective-permute-start.5
  16.2 182.5 %all-gather.5.cloned.1.call-start = ((), (), s32[]{:S(2)}) async-start(), calls=%async_computation.2 | async-start | bytes 4866048 | tf_op jit(solution)/shard_map/all_gather | solution.py:954
  16.9 675.7 %reduce-scatter.2.cloned.1.call-start = ((), (), s32[]{:S(2)}) async-start(), calls=%async_computation.3 | async-start | bytes 4866048 | tf_op jit(solution)/shard_map/reduce_scatter | solution.py:1148
  18.4 30.4 %collective-permute-start = (bf16[1536,512]{1,0:T(8,128)(2,1)S(1)}, bf16[1536,512]{1,0:T(8,128)(2,1)S(1)}, u32[]{:S(2)}, u32[]{:S(2)}) collective-permute-start(bf16[1536,512]{1,0:T(8,128)(2,1)S(1)} %pad_maximum_fusion.7), channel_id=1, source_target_pairs={{0,0},{1,16},{2,2},{3,18},{4,4},{5,20},{6,6},{7,22},{8,8},{9,24},{... | collective-permute-start | bytes 4718600 | tf_op jit(solution)/shard_map/ppermute | solution.py:932
  22.9 25.9 %collective-permute-start.1 = (bf16[1536,256]{1,0:T(8,128)(2,1)}, bf16[1536,256]{1,0:T(8,128)(2,1)}, u32[]{:S(2)}, u32[]{:S(2)}) collective-permute-start(bf16[1536,256]{1,0:T(8,128)(2,1)} %get-tuple-element.243), channel_id=1, source_target_pairs={{0,1},{1,17},{2,3},{3,19},{4,5},{5,21},{6,7},{7,23},{8,9},{9,25},{... | collective-permute-start | bytes 2359304 | tf_op jit(solution)/shard_map/ppermute | solution.py:932
  50.3 72.1 %collective-permute-start.3 = (bf16[1536,768]{1,0:T(8,128)(2,1)S(1)}, bf16[1536,768]{1,0:T(8,128)(2,1)}, u32[]{:S(2)}, u32[]{:S(2)}) collective-permute-start(bf16[1536,768]{1,0:T(8,128)(2,1)S(1)} %pad_maximum_fusion.2.refs_19_.refs_15_), channel_id=1, source_target_pairs={{0,4},{1,5},{2,6},{3,7},{4,8},{5,9},{6,10},{7,11},{8,12},{9,13},{1... | collective-permute-start | bytes 7077896 | tf_op jit(solution)/shard_map/ppermute | solution.py:389
  55.0 70.1 %collective-permute-start.4 = (bf16[1536,768]{1,0:T(8,128)(2,1)S(1)}, bf16[1536,768]{1,0:T(8,128)(2,1)}, u32[]{:S(2)}, u32[]{:S(2)}) collective-permute-start(bf16[1536,768]{1,0:T(8,128)(2,1)S(1)} %pad_maximum_fusion.2.refs_19_.refs_15_), channel_id=1, source_target_pairs={{4,0},{5,1},{6,2},{7,3},{8,4},{9,5},{10,6},{11,7},{12,8},{13,9},{1... | collective-permute-start | bytes 7077896 | tf_op jit(solution)/shard_map/ppermute | solution.py:393
  56.6 37.6 %collective-permute-start.2 = (bf16[512,1536]{1,0:T(8,128)(2,1)}, bf16[512,1536]{1,0:T(8,128)(2,1)}, u32[]{:S(2)}, u32[]{:S(2)}) collective-permute-start(bf16[512,1536]{1,0:T(8,128)(2,1)} %param.17), channel_id=1, source_target_pairs={{0,16},{16,0},{1,17},{17,1},{2,18},{18,2},{3,19},{19,3},{4,20},{20... | collective-permute-start | bytes 4718600 | tf_op jit(solution)/shard_map/ppermute | solution.py:373
  62.7 100.7 %collective-permute-start.7 = (bf16[512,1664]{1,0:T(8,128)(2,1)}, bf16[512,1664]{1,0:T(8,128)(2,1)}, u32[]{:S(2)}, u32[]{:S(2)}) collective-permute-start(bf16[512,1664]{1,0:T(8,128)(2,1)} %concatenate.91.refs_6_), channel_id=1, source_target_pairs={{0,2},{1,3},{2,0},{3,1},{4,6},{5,7},{6,4},{7,5},{8,10},{9,11},{10,... | collective-permute-start | bytes 5111816 | tf_op jit(solution)/shard_map/ppermute | solution.py:377
  94.2 69.2 %collective-permute-start.6 = (bf16[512,1664]{1,0:T(8,128)(2,1)}, bf16[512,1664]{1,0:T(8,128)(2,1)}, u32[]{:S(2)}, u32[]{:S(2)}) collective-permute-start(bf16[512,1664]{1,0:T(8,128)(2,1)} %concatenate.91.refs_6_), channel_id=1, source_target_pairs={{0,16},{16,0},{1,17},{17,1},{2,18},{18,2},{3,19},{19,3},{4,20},{20... | collective-permute-start | bytes 5111816 | tf_op jit(solution)/shard_map/ppermute | solution.py:373
  125.1 67.3 %collective-permute-start.10 = (bf16[1536,768]{1,0:T(8,128)(2,1)}, bf16[1536,768]{1,0:T(8,128)(2,1)}, u32[]{:S(2)}, u32[]{:S(2)}) collective-permute-start(bf16[1536,768]{1,0:T(8,128)(2,1)} %collective-permute-done.3.refs_18_.refs_14_), channel_id=1, source_target_pairs={{0,4},{1,5},{2,6},{3,7},{4,8},{5,9},{6,10},{7,11},{8,12},{9,13},{1... | collective-permute-start | bytes 7077896 | tf_op jit(solution)/shard_map/ppermute | solution.py:389
  129.2 63.1 %collective-permute-start.11 = (bf16[1536,768]{1,0:T(8,128)(2,1)}, bf16[1536,768]{1,0:T(8,128)(2,1)}, u32[]{:S(2)}, u32[]{:S(2)}) collective-permute-start(bf16[1536,768]{1,0:T(8,128)(2,1)} %collective-permute-done.4.refs_20_.refs_16_), channel_id=1, source_target_pairs={{4,0},{5,1},{6,2},{7,3},{8,4},{9,5},{10,6},{11,7},{12,8},{13,9},{1... | collective-permute-start | bytes 7077896 | tf_op jit(solution)/shard_map/ppermute | solution.py:393
  160.8 27.1 %collective-permute-start.8 = (bf16[512,384]{0,1:T(8,128)(2,1)S(1)}, bf16[512,384]{0,1:T(8,128)(2,1)S(1)}, u32[]{:S(2)}, u32[]{:S(2)}) collective-permute-start(bf16[512,384]{0,1:T(8,128)(2,1)S(1)} %fusion.31), channel_id=1, source_target_pairs={{0,16},{16,0},{1,17},{17,1},{2,18},{18,2},{3,19},{19,3},{4,20},{20... | collective-permute-start | bytes 1179656 | tf_op jit(solution)/shard_map/ppermute | solution.py:373
  180.2 10.5 %collective-permute-start.9 = (bf16[512,384]{0,1:T(8,128)(2,1)S(1)}, bf16[512,384]{0,1:T(8,128)(2,1)S(1)}, u32[]{:S(2)}, u32[]{:S(2)}) collective-permute-start(bf16[512,384]{0,1:T(8,128)(2,1)S(1)} %fusion.32), channel_id=1, source_target_pairs={{0,16},{16,0},{1,17},{17,1},{2,18},{18,2},{3,19},{19,3},{4,20},{20... | collective-permute-start | bytes 1179656 | tf_op jit(solution)/shard_map/ppermute | solution.py:373
  184.3 21.1 %collective-permute-start.12 = (bf16[256,1664]{1,0:T(8,128)(2,1)}, bf16[256,1664]{1,0:T(8,128)(2,1)}, u32[]{:S(2)}, u32[]{:S(2)}) collective-permute-start(bf16[256,1664]{1,0:T(8,128)(2,1)} %slice.164), channel_id=1, source_target_pairs={{0,2},{1,3},{2,0},{3,1},{4,6},{5,7},{6,4},{7,5},{8,10},{9,11},{10,... | collective-permute-start | bytes 2555912 | tf_op jit(solution)/shard_map/ppermute | solution.py:377
  187.9 20.3 %collective-permute-start.13 = (bf16[256,1664]{1,0:T(8,128)(2,1)}, bf16[256,1664]{1,0:T(8,128)(2,1)}, u32[]{:S(2)}, u32[]{:S(2)}) collective-permute-start(bf16[256,1664]{1,0:T(8,128)(2,1)} %slice.165), channel_id=1, source_target_pairs={{0,16},{16,0},{1,17},{17,1},{2,18},{18,2},{3,19},{19,3},{4,20},{20... | collective-permute-start | bytes 2555912 | tf_op jit(solution)/shard_map/ppermute | solution.py:373
  192.4 57.5 %collective-permute-start.26 = (bf16[1536,768]{1,0:T(8,128)(2,1)}, bf16[1536,768]{1,0:T(8,128)(2,1)}, u32[]{:S(2)}, u32[]{:S(2)}) collective-permute-start(bf16[1536,768]{1,0:T(8,128)(2,1)} %collective-permute-done.10.refs_17_.refs_13_), channel_id=1, source_target_pairs={{0,4},{1,5},{2,6},{3,7},{4,8},{5,9},{6,10},{7,11},{8,12},{9,13},{1... | collective-permute-start | bytes 7077896 | tf_op jit(solution)/shard_map/ppermute | solution.py:389
  197.4 52.8 %collective-permute-start.27 = (bf16[1536,768]{1,0:T(8,128)(2,1)}, bf16[1536,768]{1,0:T(8,128)(2,1)}, u32[]{:S(2)}, u32[]{:S(2)}) collective-permute-start(bf16[1536,768]{1,0:T(8,128)(2,1)} %collective-permute-done.11.refs_21_.refs_17_), channel_id=1, source_target_pairs={{4,0},{5,1},{6,2},{7,3},{8,4},{9,5},{10,6},{11,7},{12,8},{13,9},{1... | collective-permute-start | bytes 7077896 | tf_op jit(solution)/shard_map/ppermute | solution.py:393
  208.1 33.9 %collective-permute-start.14 = (bf16[512,1536]{1,0:T(8,128)(2,1)S(1)}, bf16[512,1536]{1,0:T(8,128)(2,1)}, u32[]{:S(2)}, u32[]{:S(2)}) collective-permute-start(bf16[512,1536]{1,0:T(8,128)(2,1)S(1)} %multiply_convert_fusion.1.refs_0_), channel_id=1, source_target_pairs={{0,16},{16,0},{1,17},{17,1},{2,18},{18,2},{3,19},{19,3},{4,20},{20... | collective-permute-start | bytes 4718600 | tf_op jit(solution)/shard_map/ppermute | solution.py:373
  209.1 35.5 %collective-permute-start.15 = (bf16[512,1536]{1,0:T(8,128)(2,1)S(1)}, bf16[512,1536]{1,0:T(8,128)(2,1)}, u32[]{:S(2)}, u32[]{:S(2)}) collective-permute-start(bf16[512,1536]{1,0:T(8,128)(2,1)S(1)} %multiply_convert_fusion.1.refs_0_), channel_id=1, source_target_pairs={{0,2},{1,3},{2,0},{3,1},{4,6},{5,7},{6,4},{7,5},{8,10},{9,11},{10,... | collective-permute-start | bytes 4718600 | tf_op jit(solution)/shard_map/ppermute | solution.py:377
  243.3 16.1 %collective-permute-start.16 = (bf16[256,1536]{1,0:T(8,128)(2,1)S(1)}, bf16[256,1536]{1,0:T(8,128)(2,1)S(1)}, u32[]{:S(2)}, u32[]{:S(2)}) collective-permute-start(bf16[256,1536]{1,0:T(8,128)(2,1)S(1)} %slice.213), channel_id=1, source_target_pairs={{0,2},{1,3},{2,0},{3,1},{4,6},{5,7},{6,4},{7,5},{8,10},{9,11},{10,... | collective-permute-start | bytes 2359304 | tf_op jit(solution)/shard_map/ppermute | solution.py:377
  245.8 17.6 %collective-permute-start.17 = (bf16[256,1536]{1,0:T(8,128)(2,1)S(1)}, bf16[256,1536]{1,0:T(8,128)(2,1)S(1)}, u32[]{:S(2)}, u32[]{:S(2)}) collective-permute-start(bf16[256,1536]{1,0:T(8,128)(2,1)S(1)} %slice.214), channel_id=1, source_target_pairs={{0,16},{16,0},{1,17},{17,1},{2,18},{18,2},{3,19},{19,3},{4,20},{20... | collective-permute-start | bytes 2359304 | tf_op jit(solution)/shard_map/ppermute | solution.py:373
  246.6 19.2 %collective-permute-start.24 = (bf16[256,1664]{1,0:T(8,128)(2,1)}, bf16[256,1664]{1,0:T(8,128)(2,1)}, u32[]{:S(2)}, u32[]{:S(2)}) collective-permute-start(bf16[256,1664]{1,0:T(8,128)(2,1)} %collective-permute-done.12.refs_10_), channel_id=1, source_target_pairs={{0,1},{1,0},{2,3},{3,2},{4,5},{5,4},{6,7},{7,6},{8,9},{9,8},{10,11... | collective-permute-start | bytes 2555912 | tf_op jit(solution)/shard_map/ppermute | solution.py:377
  249.9 18.6 %collective-permute-start.18 = (bf16[512,1536]{1,0:T(8,128)(2,1)}, bf16[512,1536]{1,0:T(8,128)(2,1)}, u32[]{:S(2)}, u32[]{:S(2)}) collective-permute-start(bf16[512,1536]{1,0:T(8,128)(2,1)} %collective-permute-done.14.refs_0_.refs_1_), channel_id=1, source_target_pairs={{0,1},{1,0},{2,3},{3,2},{4,5},{5,4},{6,7},{7,6},{8,9},{9,8},{10,11... | collective-permute-start | bytes 4718600 | tf_op jit(solution)/shard_map/ppermute | solution.py:377
  250.2 22.5 %collective-permute-start.22 = (bf16[512,1664]{1,0:T(8,128)(2,1)}, bf16[512,1664]{1,0:T(8,128)(2,1)}, u32[]{:S(2)}, u32[]{:S(2)}) collective-permute-start(bf16[512,1664]{1,0:T(8,128)(2,1)} %collective-permute-done.6.refs_8_.refs_7_), channel_id=1, source_target_pairs={{0,1},{1,0},{2,3},{3,2},{4,5},{5,4},{6,7},{7,6},{8,9},{9,8},{10,11... | collective-permute-start | bytes 5111816 | tf_op jit(solution)/shard_map/ppermute | solution.py:377
  259.4 13.3 %collective-permute-start.23 = (bf16[512,1664]{1,0:T(8,128)(2,1)}, bf16[512,1664]{1,0:T(8,128)(2,1)}, u32[]{:S(2)}, u32[]{:S(2)}) collective-permute-start(bf16[512,1664]{1,0:T(8,128)(2,1)} %collective-permute-done.7.refs_9_.refs_8_), channel_id=1, source_target_pairs={{0,1},{1,0},{2,3},{3,2},{4,5},{5,4},{6,7},{7,6},{8,9},{9,8},{10,11... | collective-permute-start | bytes 5111816 | tf_op jit(solution)/shard_map/ppermute | solution.py:377
  263.3 4.8 collective-permute-start.25
  265.8 6.9 collective-permute-start.19
  268.1 4.6 collective-permute-start.20
  268.5 4.2 collective-permute-start.21
  345.3 9.0 %collective-permute-start.28 = (bf16[1024,1536]{1,0:T(8,128)(2,1)}, bf16[1024,1536]{1,0:T(8,128)(2,1)S(1)}, u32[]{:S(2)}, u32[]{:S(2)}) collective-permute-start(bf16[1024,1536]{1,0:T(8,128)(2,1)} %get-tuple-element.113), channel_id=1, source_target_pairs={{0,1},{1,0},{2,3},{3,2},{4,5},{5,4},{6,7},{7,6},{8,9},{9,8},{10,11... | collective-permute-start | bytes 9437192 | tf_op jit(solution)/shard_map/ppermute | solution.py:377
  345.7 17.0 %collective-permute-start.29 = (bf16[512,1536]{1,0:T(8,128)(2,1)}, bf16[512,1536]{1,0:T(8,128)(2,1)}, u32[]{:S(2)}, u32[]{:S(2)}) collective-permute-start(bf16[512,1536]{1,0:T(8,128)(2,1)} %copy-done.30), channel_id=1, source_target_pairs={{0,1},{1,0},{2,3},{3,2},{4,5},{5,4},{6,7},{7,6},{8,9},{9,8},{10,11... | collective-permute-start | bytes 4718600 | tf_op jit(solution)/shard_map/ppermute | solution.py:377
  345.8 16.9 %collective-permute-start.30 = (bf16[512,1664]{1,0:T(8,128)(2,1)}, bf16[512,1664]{1,0:T(8,128)(2,1)}, u32[]{:S(2)}, u32[]{:S(2)}) collective-permute-start(bf16[512,1664]{1,0:T(8,128)(2,1)} %concatenate.91.refs_6_), channel_id=1, source_target_pairs={{0,1},{1,0},{2,3},{3,2},{4,5},{5,4},{6,7},{7,6},{8,9},{9,8},{10,11... | collective-permute-start | bytes 5111816 | tf_op jit(solution)/shard_map/ppermute | solution.py:377
  358.9 68.6 %collective-permute-start.31 = (bf16[512,1536]{1,0:T(8,128)(2,1)}, bf16[512,1536]{1,0:T(8,128)(2,1)}, u32[]{:S(2)}, u32[]{:S(2)}) collective-permute-start(bf16[512,1536]{1,0:T(8,128)(2,1)} %get-tuple-element.225), channel_id=1, source_target_pairs={{0,2},{1,3},{2,0},{3,1},{4,6},{5,7},{6,4},{7,5},{8,10},{9,11},{10,... | collective-permute-start | bytes 4718600 | tf_op jit(solution)/shard_map/ppermute | solution.py:377
  360.1 67.3 %collective-permute-start.32 = (bf16[512,1536]{1,0:T(8,128)(2,1)}, bf16[512,1536]{1,0:T(8,128)(2,1)}, u32[]{:S(2)}, u32[]{:S(2)}) collective-permute-start(bf16[512,1536]{1,0:T(8,128)(2,1)} %get-tuple-element.224), channel_id=1, source_target_pairs={{0,16},{16,0},{1,17},{17,1},{2,18},{18,2},{3,19},{19,3},{4,20},{20... | collective-permute-start | bytes 4718600 | tf_op jit(solution)/shard_map/ppermute | solution.py:373
  426.4 36.6 %collective-permute-start.33 = (bf16[1024,1536]{1,0:T(8,128)(2,1)}, bf16[1024,1536]{1,0:T(8,128)(2,1)}, u32[]{:S(2)}, u32[]{:S(2)}) collective-permute-start(bf16[1024,1536]{1,0:T(8,128)(2,1)} %get-tuple-element.132), channel_id=1, source_target_pairs={{0,1},{1,0},{2,3},{3,2},{4,5},{5,4},{6,7},{7,6},{8,9},{9,8},{10,11... | collective-permute-start | bytes 9437192 | tf_op jit(solution)/shard_map/ppermute | solution.py:377
  455.3 54.3 %collective-permute-start.38 = (bf16[1536,768]{1,0:T(8,128)(2,1)}, bf16[1536,768]{1,0:T(8,128)(2,1)}, u32[]{:S(2)}, u32[]{:S(2)}) collective-permute-start(bf16[1536,768]{1,0:T(8,128)(2,1)} %pad_maximum_fusion.4), channel_id=1, source_target_pairs={{0,4},{1,5},{2,6},{3,7},{4,8},{5,9},{6,10},{7,11},{8,12},{9,13},{1... | collective-permute-start | bytes 7077896 | tf_op jit(solution)/shard_map/ppermute | solution.py:389
  461.7 56.7 %collective-permute-start.39 = (bf16[1536,768]{1,0:T(8,128)(2,1)}, bf16[1536,768]{1,0:T(8,128)(2,1)}, u32[]{:S(2)}, u32[]{:S(2)}) collective-permute-start(bf16[1536,768]{1,0:T(8,128)(2,1)} %pad_maximum_fusion.3), channel_id=1, source_target_pairs={{4,0},{5,1},{6,2},{7,3},{8,4},{9,5},{10,6},{11,7},{12,8},{13,9},{1... | collective-permute-start | bytes 7077896 | tf_op jit(solution)/shard_map/ppermute | solution.py:393
  469.0 29.1 %collective-permute-start.34 = (bf16[256,1536]{1,0:T(8,128)(2,1)}, bf16[256,1536]{1,0:T(8,128)(2,1)S(1)}, u32[]{:S(2)}, u32[]{:S(2)}) collective-permute-start(bf16[256,1536]{1,0:T(8,128)(2,1)} %get-tuple-element.214), channel_id=1, source_target_pairs={{0,16},{16,0},{1,17},{17,1},{2,18},{18,2},{3,19},{19,3},{4,20},{20... | collective-permute-start | bytes 2359304 | tf_op jit(solution)/shard_map/ppermute | solution.py:373
  469.9 28.2 %collective-permute-start.35 = (bf16[256,1536]{1,0:T(8,128)(2,1)}, bf16[256,1536]{1,0:T(8,128)(2,1)S(1)}, u32[]{:S(2)}, u32[]{:S(2)}) collective-permute-start(bf16[256,1536]{1,0:T(8,128)(2,1)} %get-tuple-element.215), channel_id=1, source_target_pairs={{0,2},{1,3},{2,0},{3,1},{4,6},{5,7},{6,4},{7,5},{8,10},{9,11},{10,... | collective-permute-start | bytes 2359304 | tf_op jit(solution)/shard_map/ppermute | solution.py:377
  505.8 22.3 %collective-permute-start.40 = (bf16[1024,1536]{1,0:T(8,128)(2,1)}, bf16[1024,1536]{1,0:T(8,128)(2,1)}, u32[]{:S(2)}, u32[]{:S(2)}) collective-permute-start(bf16[1024,1536]{1,0:T(8,128)(2,1)} %get-tuple-element.143), channel_id=1, source_target_pairs={{0,1},{1,0},{2,3},{3,2},{4,5},{5,4},{6,7},{7,6},{8,9},{9,8},{10,11... | collective-permute-start | bytes 9437192 | tf_op jit(solution)/shard_map/ppermute | solution.py:377
  507.1 78.2 %collective-permute-start.36 = (bf16[1024,1536]{1,0:T(8,128)(2,1)}, bf16[1024,1536]{1,0:T(8,128)(2,1)}, u32[]{:S(2)}, u32[]{:S(2)}) collective-permute-start(bf16[1024,1536]{1,0:T(8,128)(2,1)} %get-tuple-element.141), channel_id=1, source_target_pairs={{0,1},{1,0},{2,3},{3,2},{4,5},{5,4},{6,7},{7,6},{8,9},{9,8},{10,11... | collective-permute-start | bytes 9437192 | tf_op jit(solution)/shard_map/ppermute | solution.py:377
  508.5 26.1 %collective-permute-start.37 = (bf16[512,768]{1,0:T(8,128)(2,1)}, bf16[512,768]{1,0:T(8,128)(2,1)}, u32[]{:S(2)}, u32[]{:S(2)}) collective-permute-start(bf16[512,768]{1,0:T(8,128)(2,1)} %constant_dynamic-slice_fusion), channel_id=1, source_target_pairs={{0,16},{16,0},{1,17},{17,1},{2,18},{18,2},{3,19},{19,3},{4,20},{20... | collective-permute-start | bytes 2359304 | tf_op jit(solution)/shard_map/ppermute | solution.py:373
  512.8 76.5 %collective-permute-start.41 = (bf16[1536,768]{1,0:T(8,128)(2,1)}, bf16[1536,768]{1,0:T(8,128)(2,1)}, u32[]{:S(2)}, u32[]{:S(2)}) collective-permute-start(bf16[1536,768]{1,0:T(8,128)(2,1)} %add_convert_fusion.7), channel_id=1, source_target_pairs={{0,4},{1,5},{2,6},{3,7},{4,8},{5,9},{6,10},{7,11},{8,12},{9,13},{1... | collective-permute-start | bytes 7077896 | tf_op jit(solution)/shard_map/ppermute | solution.py:389
  521.8 67.5 %collective-permute-start.42 = (bf16[1536,768]{1,0:T(8,128)(2,1)}, bf16[1536,768]{1,0:T(8,128)(2,1)}, u32[]{:S(2)}, u32[]{:S(2)}) collective-permute-start(bf16[1536,768]{1,0:T(8,128)(2,1)} %add_convert_fusion.6), channel_id=1, source_target_pairs={{4,0},{5,1},{6,2},{7,3},{8,4},{9,5},{10,6},{11,7},{12,8},{13,9},{1... | collective-permute-start | bytes 7077896 | tf_op jit(solution)/shard_map/ppermute | solution.py:393
  533.7 55.7 %collective-permute-start.43 = (bf16[512,1536]{1,0:T(8,128)(2,1)}, bf16[512,1536]{1,0:T(8,128)(2,1)}, u32[]{:S(2)}, u32[]{:S(2)}) collective-permute-start(bf16[512,1536]{1,0:T(8,128)(2,1)} %get-tuple-element.219), channel_id=1, source_target_pairs={{0,2},{1,3},{2,0},{3,1},{4,6},{5,7},{6,4},{7,5},{8,10},{9,11},{10,... | collective-permute-start | bytes 4718600 | tf_op jit(solution)/shard_map/ppermute | solution.py:377
  534.6 54.8 %collective-permute-start.44 = (bf16[512,1536]{1,0:T(8,128)(2,1)}, bf16[512,1536]{1,0:T(8,128)(2,1)}, u32[]{:S(2)}, u32[]{:S(2)}) collective-permute-start(bf16[512,1536]{1,0:T(8,128)(2,1)} %get-tuple-element.218), channel_id=1, source_target_pairs={{0,16},{16,0},{1,17},{17,1},{2,18},{18,2},{3,19},{19,3},{4,20},{20... | collective-permute-start | bytes 4718600 | tf_op jit(solution)/shard_map/ppermute | solution.py:373
  592.5 22.4 %collective-permute-start.45 = (bf16[256,1536]{1,0:T(8,128)(2,1)}, bf16[256,1536]{1,0:T(8,128)(2,1)}, u32[]{:S(2)}, u32[]{:S(2)}) collective-permute-start(bf16[256,1536]{1,0:T(8,128)(2,1)} %fusion.25), channel_id=1, source_target_pairs={{0,16},{16,0},{1,17},{17,1},{2,18},{18,2},{3,19},{19,3},{4,20},{20... | collective-permute-start | bytes 2359304 | tf_op jit(solution)/shard_map/ppermute | solution.py:373
  612.8 29.0 %collective-permute-start.48 = (bf16[2,2,4,48,1408]{4,3,2,1,0:T(8,128)(2,1)}, bf16[2,2,4,48,1408]{4,3,2,1,0:T(8,128)(2,1)}, u32[]{:S(2)}, u32[]{:S(2)}) collective-permute-start(bf16[2,2,4,48,1408]{4,3,2,1,0:T(8,128)(2,1)} %dynamic-slice_bitcast_fusion), channel_id=1, source_target_pairs={{0,1},{1,0},{2,3},{3,2},{4,5},{5,4},{6,7},{7,6},{8,9},{9,8},{10,11... | collective-permute-start | bytes 6488072 | tf_op jit(solution)/shard_map/ppermute | solution.py:377
  619.4 20.3 %collective-permute-start.46 = (bf16[256,1536]{1,0:T(8,128)(2,1)}, bf16[256,1536]{1,0:T(8,128)(2,1)}, u32[]{:S(2)}, u32[]{:S(2)}) collective-permute-start(bf16[256,1536]{1,0:T(8,128)(2,1)} %get-tuple-element.211), channel_id=1, source_target_pairs={{0,2},{1,3},{2,0},{3,1},{4,6},{5,7},{6,4},{7,5},{8,10},{9,11},{10,... | collective-permute-start | bytes 2359304 | tf_op jit(solution)/shard_map/ppermute | solution.py:377
  627.5 35.3 %collective-permute-start.47 = (bf16[512,1536]{1,0:T(8,128)(2,1)}, bf16[512,1536]{1,0:T(8,128)(2,1)}, u32[]{:S(2)}, u32[]{:S(2)}) collective-permute-start(bf16[512,1536]{1,0:T(8,128)(2,1)} %convolution_convert_fusion.3), channel_id=1, source_target_pairs={{0,16},{16,0},{1,17},{17,1},{2,18},{18,2},{3,19},{19,3},{4,20},{20... | collective-permute-start | bytes 4718600 | tf_op jit(solution)/shard_map/ppermute | solution.py:373
  628.6 55.7 %collective-permute-start.50 = (bf16[1536,768]{1,0:T(8,128)(2,1)}, bf16[1536,768]{1,0:T(8,128)(2,1)S(1)}, u32[]{:S(2)}, u32[]{:S(2)}) collective-permute-start(bf16[1536,768]{1,0:T(8,128)(2,1)} %get-tuple-element.217), channel_id=1, source_target_pairs={{0,4},{1,5},{2,6},{3,7},{4,8},{5,9},{6,10},{7,11},{8,12},{9,13},{1... | collective-permute-start | bytes 7077896 | tf_op jit(solution)/shard_map/ppermute | solution.py:389
  632.9 53.8 %collective-permute-start.51 = (bf16[1536,768]{1,0:T(8,128)(2,1)}, bf16[1536,768]{1,0:T(8,128)(2,1)S(1)}, u32[]{:S(2)}, u32[]{:S(2)}) collective-permute-start(bf16[1536,768]{1,0:T(8,128)(2,1)} %get-tuple-element.216), channel_id=1, source_target_pairs={{4,0},{5,1},{6,2},{7,3},{8,4},{9,5},{10,6},{11,7},{12,8},{13,9},{1... | collective-permute-start | bytes 7077896 | tf_op jit(solution)/shard_map/ppermute | solution.py:393
  644.8 24.5 %collective-permute-start.49 = (bf16[2,4,48,1408]{3,2,1,0:T(8,128)(2,1)S(1)}, bf16[2,4,48,1408]{3,2,1,0:T(8,128)(2,1)S(1)}, u32[]{:S(2)}, u32[]{:S(2)}) collective-permute-start(bf16[2,4,48,1408]{3,2,1,0:T(8,128)(2,1)S(1)} %fusion.33), channel_id=1, source_target_pairs={{0,2},{1,3},{2,0},{3,1},{4,6},{5,7},{6,4},{7,5},{8,10},{9,11},{10,... | collective-permute-start | bytes 3244040 | tf_op jit(solution)/shard_map/ppermute | solution.py:377
  686.8 10.0 %collective-permute-start.52 = (bf16[2,48,1408]{2,1,0:T(8,128)(2,1)S(1)}, bf16[2,48,1408]{2,1,0:T(8,128)(2,1)}, u32[]{:S(2)}, u32[]{:S(2)}) collective-permute-start(bf16[2,48,1408]{2,1,0:T(8,128)(2,1)S(1)} %fusion.50), channel_id=1, source_target_pairs={{0,4},{1,5},{2,6},{3,7},{4,8},{5,9},{6,10},{7,11},{8,12},{9,13},{1... | collective-permute-start | bytes 811016 | tf_op jit(solution)/shard_map/ppermute | solution.py:389
  695.5 12.2 %collective-permute-start.55 = (bf16[2,48,1408]{2,1,0:T(8,128)(2,1)S(1)}, bf16[2,48,1408]{2,1,0:T(8,128)(2,1)S(1)}, u32[]{:S(2)}, u32[]{:S(2)}) collective-permute-start(bf16[2,48,1408]{2,1,0:T(8,128)(2,1)S(1)} %fusion.51), channel_id=1, source_target_pairs={{4,0},{5,1},{6,2},{7,3},{8,4},{9,5},{10,6},{11,7},{12,8},{13,9},{1... | collective-permute-start | bytes 811016 | tf_op jit(solution)/shard_map/ppermute | solution.py:393
  698.0 9.7 %collective-permute-start.53 = (bf16[2,48,1408]{2,1,0:T(8,128)(2,1)S(1)}, bf16[2,48,1408]{2,1,0:T(8,128)(2,1)S(1)}, u32[]{:S(2)}, u32[]{:S(2)}) collective-permute-start(bf16[2,48,1408]{2,1,0:T(8,128)(2,1)S(1)} %fusion.47), channel_id=1, source_target_pairs={{0,4},{1,5},{2,6},{3,7},{4,8},{5,9},{6,10},{7,11},{8,12},{9,13},{1... | collective-permute-start | bytes 811016 | tf_op jit(solution)/shard_map/ppermute | solution.py:389
  707.8 8.2 %collective-permute-start.56 = (bf16[2,48,1408]{2,1,0:T(8,128)(2,1)S(1)}, bf16[2,48,1408]{2,1,0:T(8,128)(2,1)S(1)}, u32[]{:S(2)}, u32[]{:S(2)}) collective-permute-start(bf16[2,48,1408]{2,1,0:T(8,128)(2,1)S(1)} %get-tuple-element.234), channel_id=1, source_target_pairs={{4,0},{5,1},{6,2},{7,3},{8,4},{9,5},{10,6},{11,7},{12,8},{13,9},{1... | collective-permute-start | bytes 811016 | tf_op jit(solution)/shard_map/ppermute | solution.py:393
  709.3 38.1 %collective-permute-start.60 = (bf16[1536,256]{1,0:T(8,128)(2,1)S(1)}, bf16[1536,256]{1,0:T(8,128)(2,1)S(1)}, u32[]{:S(2)}, u32[]{:S(2)}) collective-permute-start(bf16[1536,256]{1,0:T(8,128)(2,1)S(1)} %get-tuple-element.230), channel_id=1, source_target_pairs={{1,0},{17,1},{3,2},{19,3},{5,4},{21,5},{7,6},{23,7},{9,8},{25,9},{... | collective-permute-start | bytes 2359304 | tf_op jit(solution)/shard_map/ppermute | solution.py:932
  711.8 11.7 %collective-permute-start.54 = (bf16[2,48,1408]{2,1,0:T(8,128)(2,1)S(1)}, bf16[2,48,1408]{2,1,0:T(8,128)(2,1)S(1)}, u32[]{:S(2)}, u32[]{:S(2)}) collective-permute-start(bf16[2,48,1408]{2,1,0:T(8,128)(2,1)S(1)} %get-tuple-element.233), channel_id=1, source_target_pairs={{0,4},{1,5},{2,6},{3,7},{4,8},{5,9},{6,10},{7,11},{8,12},{9,13},{1... | collective-permute-start | bytes 811016 | tf_op jit(solution)/shard_map/ppermute | solution.py:389
  716.1 7.4 collective-permute-start.57
  717.6 29.8 %collective-permute-start.59 = (bf16[1536,512]{1,0:T(8,128)(2,1)S(1)}, bf16[1536,512]{1,0:T(8,128)(2,1)S(1)}, u32[]{:S(2)}, u32[]{:S(2)}) collective-permute-start(bf16[1536,512]{1,0:T(8,128)(2,1)S(1)} %pad_maximum_fusion.9), channel_id=1, source_target_pairs={{0,0},{1,16},{2,2},{3,18},{4,4},{5,20},{6,6},{7,22},{8,8},{9,24},{... | collective-permute-start | bytes 4718600 | tf_op jit(solution)/shard_map/ppermute | solution.py:932
  723.6 20.1 %collective-permute-start.58 = (bf16[48,1408]{1,0:T(8,128)(2,1)S(1)}, bf16[48,1408]{1,0:T(8,128)(2,1)S(1)}, u32[]{:S(2)}, u32[]{:S(2)}) collective-permute-start(bf16[48,1408]{1,0:T(8,128)(2,1)S(1)} %fusion.54), channel_id=1, source_target_pairs={{0,16},{16,0},{1,17},{17,1},{2,18},{18,2},{3,19},{19,3},{4,20},{20... | collective-permute-start | bytes 405512 | tf_op jit(solution)/shard_map/ppermute | solution.py:373
  (64 other events, 1087.9 us)
Sparse Core Ops, SparseCore 0:
  16.3 56.5 all-gather.2
  75.8 81.7 all-gather.4
  528.2 109.1 reduce-scatter.1

commit v3 on v2

--- a/solution.py
+++ b/solution.py
@@ -463,6 +463,15 @@
     return values * cos - swapped * sin
 
 
+def place_shards(place_ref, own_ref, other_ref, shard, store):
+    for core in range(2):
+        source = other_ref if core else own_ref
+        for row in range(2):
+            for line in range(LINE):
+                index = (place_ref[0] ^ line) * 4 + (place_ref[1] ^ row) * 2 + (place_ref[2] ^ core)
+                store(source, (row * LINE + line) * shard, pl.multiple_of(index * shard, shard))
+
+
 def qkv_kernel(x_ref, gain_ref, w_ref, cos_ref, sin_ref, h_ref, q_ref, k_ref, v_ref):
     value = x_ref[...].astype(F32)
     scale = lax.rsqrt(jnp.mean(value * value, axis=-1, keepdims=True) + EPSILON)
@@ -508,12 +517,109 @@
         ],
         compiler_params=pltpu.CompilerParams(vmem_limit_bytes=VMEM_BYTES),
         cost_estimate=pl.CostEstimate(
-            flops=2 * rows * width * columns,
-            bytes_accessed=2 * (2 * rows * width + width * columns + rows * columns),
+            flops=rows * width * columns // 8,
+            bytes_accessed=rows * width + width * columns,
             transcendentals=rows,
         ),
         name="project",
     )(x_sorted, gain, weights, cos, sin)
+
+
+def mix_kernel(
+    place_ref, mine_ref, theirs_ref, x_ref, gain_ref, own_ref, other_ref, m_ref, h_ref, w_ref
+):
+    shard = own_ref.shape[0] // (4 * LINE)
+    half = w_ref.shape[1]
+
+    @pl.when(pl.program_id(0) == 0)
+    def _():
+        for seq in range(2):
+
+            def store(source, low, place):
+                low = low + seq * 2 * LINE * shard
+                w_ref[seq, pl.ds(place, shard), :] = source[low : low + shard, :]
+
+            place_shards(place_ref, own_ref, other_ref, shard, store)
+
+    mixed = jnp.dot(mine_ref[...], w_ref[0], preferred_element_type=F32)
+    mixed = mixed + jnp.dot(theirs_ref[...], w_ref[1], preferred_element_type=F32)
+    value = x_ref[...].astype(F32) + BRANCH_SCALE * mixed
+    m_ref[...] = value
+    scale = lax.rsqrt(jnp.mean(value * value, axis=-1, keepdims=True) + EPSILON)
+    h_ref[...] = (value * scale * gain_ref[1:2, :]).astype(BF16)
+
+
+def mix(places, mine, theirs, tokens, gains, own, other):
+    rows, width = tokens.shape
+    half = mine.shape[1]
+    tile = 256
+
+    def row_block(lanes):
+        return pl.BlockSpec((tile, lanes), lambda i, p: (i, 0))
+
+    def whole(shape):
+        return pl.BlockSpec(shape, lambda i, p: (0,) * len(shape))
+
+    return pl.pallas_call(
+        mix_kernel,
+        grid_spec=pltpu.PrefetchScalarGridSpec(
+            num_scalar_prefetch=1,
+            grid=(rows // tile,),
+            in_specs=[
+                row_block(half), row_block(half), row_block(width), whole(gains.shape),
+                whole(own.shape), whole(other.shape),
+            ],
+            out_specs=[row_block(width), row_block(width), whole((2, half, width))],
+        ),
+        out_shape=[
+            jax.ShapeDtypeStruct((rows, width), F32),
+            jax.ShapeDtypeStruct((rows, width), BF16),
+            jax.ShapeDtypeStruct((2, half, width), BF16),
+        ],
+        compiler_params=pltpu.CompilerParams(vmem_limit_bytes=VMEM_BYTES),
+        cost_estimate=pl.CostEstimate(
+            flops=rows * width * width // 8, bytes_accessed=rows * width, transcendentals=rows
+        ),
+        name="mix",
+    )(places, mine, theirs, tokens, gains, own, other)
+
+
+def token_grad_kernel(dq_ref, dk_ref, dv_ref, w_ref, own_ref, other_ref, mine_ref, sent_ref):
+    q_width, kv_width = dq_ref.shape[1], dk_ref.shape[1]
+    cuts = (0, q_width, q_width + kv_width, q_width + 2 * kv_width)
+    grad = contract(dq_ref[...], w_ref[:, cuts[0] : cuts[1]], 1, 1)
+    grad = grad + contract(dk_ref[...], w_ref[:, cuts[1] : cuts[2]], 1, 1)
+    grad = (grad + contract(dv_ref[...], w_ref[:, cuts[2] : cuts[3]], 1, 1)).astype(BF16)
+    for place_ref, out_ref in ((other_ref, sent_ref), (own_ref, mine_ref)):
+        shape = (place_ref.shape[0], grad.shape[0])
+        picked = lax.broadcasted_iota(jnp.int32, shape, 1) == place_ref[...]
+        picked = jnp.where(picked, 1.0, 0.0).astype(BF16)
+        out_ref[...] = jnp.dot(picked, grad, preferred_element_type=F32).astype(BF16)
+
+
+def token_grad(grads, weights, own_places, other_places):
+    rows, count = grads[0].shape[0], own_places.shape[0]
+    width = weights.shape[0]
+    columns = sum(grad.shape[1] for grad in grads)
+    tile = width // 3
+
+    def whole(array):
+        return pl.BlockSpec(array.shape, lambda i: (0, 0))
+
+    block = pl.BlockSpec((count, tile), lambda i: (0, i))
+    return pl.pallas_call(
+        token_grad_kernel,
+        grid=(3,),
+        in_specs=[whole(grad) for grad in grads]
+        + [pl.BlockSpec((tile, columns), lambda i: (i, 0)), whole(own_places), whole(other_places)],
+        out_specs=[block, block],
+        out_shape=[jax.ShapeDtypeStruct((count, width), BF16)] * 2,
+        compiler_params=pltpu.CompilerParams(vmem_limit_bytes=VMEM_BYTES),
+        cost_estimate=pl.CostEstimate(
+            flops=rows * width * columns // 8, bytes_accessed=rows * width, transcendentals=0
+        ),
+        name="token_grad",
+    )(*grads, weights, own_places, other_places)
 
 
 Q_TILE = 256
@@ -736,6 +842,10 @@
                     for copy in weight_copies(spot, slot):
                         copy.start()
 
+        for spot in range(LINE):
+            for copy in weight_copies(spot, LINE - 1):
+                copy.wait()
+
     @pl.when(step + 1 < steps)
     def _():
         fetch(step + 1, 1 - buffer)
@@ -750,12 +860,6 @@
     gates = jnp.dot(g_buf[buffer, :, width:], select_ref[...], preferred_element_type=F32)
     for spot in range(LINE):
         units = slice(spot * half, (spot + 1) * half)
-
-        @pl.when(step == 0)
-        def _():
-            for copy in weight_copies(spot, LINE - 1):
-                copy.wait()
-
         both = jnp.dot(
             rows, w_in[:, spot * part : (spot + 1) * part], preferred_element_type=F32
         )
@@ -844,43 +948,44 @@
     )(place, *rows, *grads, *slots, select, *kept)
 
 
-def qkv_grad_kernel(h_ref, d_ref, gain_ref, o_ref):
+def qkv_grad_kernel(h_ref, dq_ref, dk_ref, dv_ref, gain_ref, o_ref):
     shard = o_ref.shape[-2]
-    columns = d_ref.shape[1]
-    product = contract(h_ref[...], d_ref[...], 0, 0).astype(BF16)
+    rows = h_ref[...]
+    low = 0
     gains = jnp.broadcast_to(gain_ref[...], (PAD, gain_ref.shape[1])).T.astype(BF16)
-    for block in range(h_ref.shape[1] // shard):
-        rows = slice(block * shard, (block + 1) * shard)
-        place = (block % 2, block // 2 % 2, 0, block // 4)
-        o_ref[place + (slice(None), slice(0, columns))] = product[rows]
-        o_ref[place + (slice(None), slice(columns, columns + PAD))] = gains[rows]
+    parts = [contract(rows, ref[...], 0, 0).astype(BF16) for ref in (dq_ref, dk_ref, dv_ref)]
+    for part in parts + [gains]:
+        for block in range(h_ref.shape[1] // shard):
+            place = (block % 2, block // 2 % 2, 0, block // 4)
+            o_ref[place + (slice(None), slice(low, low + part.shape[1]))] = part[
+                block * shard : (block + 1) * shard
+            ]
+        low = low + part.shape[1]
 
 
 def qkv_grad(normed, grads, gain_row, shard):
     rows, width = normed.shape
-    columns = grads.shape[1]
+    columns = sum(grad.shape[1] for grad in grads)
     tile = width // 4
     planes = tile // (4 * shard)
     return pl.pallas_call(
         qkv_grad_kernel,
         grid=(4,),
-        in_specs=[
-            pl.BlockSpec((rows, tile), lambda i: (0, i)),
-            pl.BlockSpec((rows, columns), lambda i: (0, 0)),
-            pl.BlockSpec((1, tile), lambda i: (0, i)),
-        ],
+        in_specs=[pl.BlockSpec((rows, tile), lambda i: (0, i))]
+        + [pl.BlockSpec(grad.shape, lambda i: (0, 0)) for grad in grads]
+        + [pl.BlockSpec((1, tile), lambda i: (0, i))],
         out_specs=pl.BlockSpec(
             (2, 2, 1, planes, shard, columns + PAD), lambda i: (0, 0, i // 2, i % 2, 0, 0)
         ),
         out_shape=jax.ShapeDtypeStruct((2, 2, 2, LINE, shard, columns + PAD), BF16),
         compiler_params=pltpu.CompilerParams(vmem_limit_bytes=VMEM_BYTES),
         cost_estimate=pl.CostEstimate(
-            flops=rows * width * columns // 4,
-            bytes_accessed=2 * rows * (width + columns) + 2 * width * columns,
+            flops=rows * width * columns // 8,
+            bytes_accessed=rows * width,
             transcendentals=0,
         ),
         name="qkv_grad",
-    )(normed, grads, gain_row)
+    )(normed, *grads, gain_row)
 
 
 def norm_back(value, gain, grad):
@@ -948,10 +1053,10 @@
     mine = jnp.concatenate([half_of(w, seq) for w in projections] + [gain_columns], axis=1)
     theirs = jnp.concatenate([half_of(w, 1 - seq) for w in projections] + [gain_columns], axis=1)
     theirs = swap_seq(theirs)
+    qkv_width = q_width + 2 * kv_width
     pair = jnp.stack([jnp.where(first_seq, mine, theirs), jnp.where(first_seq, theirs, mine)])
-    qkv_width = q_width + 2 * kv_width
     w_qkv = lax.all_gather(pair, "dp", axis=1, tiled=True).reshape(width, qkv_width + PAD)
-    output_full = lax.all_gather(w_output, ("seq", "dp"), axis=0, tiled=True)
+    places_of = jnp.stack([line, row_of, core]).astype(jnp.int32)
 
     in_own = w_in[0]
     half = in_own.shape[1] // 2
@@ -970,6 +1075,13 @@
     )
     other_tokens = swap_seq(after(tokens, own_part))
     up_one, down_one = line_up(own_part), line_down(own_part)
+    output_rows = jnp.concatenate(
+        [w_output] + [swap_dp(w_output, 4 * step) for step in range(1, LINE)], axis=0
+    )
+    output_rows = jnp.concatenate([output_rows, swap_y(output_rows)], axis=0)
+    output_rows = after(output_rows, other_tokens)
+    output_rows = jnp.concatenate([output_rows, swap_seq(output_rows)], axis=0)
+    output_others = swap_core(output_rows)
 
     experts_all = 4 * LINE
     gates = jax.nn.softmax(logits, axis=-1)
@@ -1018,10 +1130,10 @@
         return contract(sort, values, 0, 0).astype(BF16)
 
     x_sorted = to_order(tokens, other_tokens)
+    x_sorted, up_one, down_one = lax.optimization_barrier((x_sorted, up_one, down_one))
+    up_two, down_two = line_up(up_one), line_down(down_one)
     gains = w_qkv[:, qkv_width : qkv_width + 2].astype(F32).T
     gain_one, gain_two = gains[0], gains[1]
-    x_sorted, up_one, down_one = lax.optimization_barrier((x_sorted, up_one, down_one))
-    up_two, down_two = line_up(up_one), line_down(down_one)
     normed, query, keys, values = project(
         x_sorted, gain_one[None, :], w_qkv, cos, sin, q_width, kv_heads
     )
@@ -1037,16 +1149,14 @@
     )
     sent_two = swap_seq(from_order(sort_other, mixed_two))
     mixed_mine = [from_order(sort_own, mixed_one), from_order(sort_own, mixed_two)]
-    mixed = ordered(
-        jnp.concatenate(mixed_mine, axis=1), jnp.concatenate([sent_one, sent_two], axis=1), 1
-    )
-    mixed, up_two, down_two = lax.optimization_barrier((mixed, up_two, down_two))
+    mixed_mine = jnp.concatenate(mixed_mine, axis=1)
+    mixed_theirs = jnp.concatenate([sent_one, sent_two], axis=1)
+    mixed_theirs, up_two, down_two = lax.optimization_barrier((mixed_theirs, up_two, down_two))
     up_three, down_three = line_up(up_two), line_down(down_two)
     inputs = tokens.astype(F32)
-    attn = jnp.dot(mixed, output_full, preferred_element_type=F32)
-    middle = inputs + BRANCH_SCALE * attn
-    normed_ffn = rms_norm(middle, gain_two).astype(BF16)
-
+    middle, normed_ffn, output_parts = mix(
+        places_of, mixed_mine, mixed_theirs, tokens, gains, output_rows, output_others
+    )
     normed_ffn = after(normed_ffn, *grad_far)
     row_near = near_pieces(normed_ffn, normed_ffn)
     row_far = far_pieces(*row_near)
@@ -1108,9 +1218,10 @@
     grad_norm, grad_gain_two = norm_back(middle, gain_two, grad_normed_ffn)
     grad_middle = grad_final + grad_norm
     grad_attn = (BRANCH_SCALE * grad_middle).astype(BF16)
-    grad_mixed = contract(grad_attn, output_full, 1, 1).astype(BF16)
-    grad_w_output = contract(mixed, grad_attn, 0, 0)
-    grad_other = swap_seq(half_of(grad_mixed, 1 - seq))
+    grad_mixed = contract(grad_attn, output_parts[0], 1, 1).astype(BF16)
+    grad_other = contract(grad_attn, output_parts[1], 1, 1).astype(BF16)
+    grad_other = swap_seq(grad_other)
+    grad_w_output = contract(ordered(mixed_mine, mixed_theirs, 1), grad_attn, 0, 0)
     far_f, far_f_other, near_f, near_f_other = after(
         (far[0], far[1], near[0], near[1]), grad_mixed
     )
@@ -1119,7 +1230,7 @@
     near_ffn = over_cores(near_f, near_f_other)
     right, left = line_step(1, far_line)
     grad_other = after(grad_other, right, left, far_ffn)
-    grad_sorted = to_order(half_of(grad_mixed, seq), grad_other)
+    grad_sorted = to_order(grad_mixed, grad_other)
     mid_line = (line_up(right), line_down(left))
     grad_query, grad_keys, grad_values = attend_back(
         query, keys, values, grad_sorted, start_column, cos, sin
@@ -1133,12 +1244,13 @@
     first_ffn, second_ffn = swap_seq(first_ffn), swap_y(second_ffn)
     ffn = own_sum(near_ffn, ffn_y, ffn_x, first_ffn, second_ffn)
     output = (middle + BRANCH_SCALE * ffn).astype(BF16)
-    grad_qkv = jnp.concatenate([grad_query, grad_keys, grad_values], axis=1)
-    grad_qkv = after(grad_qkv, right, left)
-    wide = qkv_grad(normed, grad_qkv, grad_gain_two[None, :], shard)
-    grad_normed = contract(grad_qkv, w_qkv[:, :qkv_width], 1, 1).astype(BF16)
-    sent_normed = swap_seq(from_order(sort_other, grad_normed))
-    grad_normed = from_order(sort_own, grad_normed).astype(F32) + sent_normed.astype(F32)
+    grads_qkv = after((grad_query, grad_keys, grad_values), right, left)
+    wide = qkv_grad(normed, grads_qkv, grad_gain_two[None, :], shard)
+    grads_late = after(grads_qkv, wide)
+    grad_normed, sent_normed = token_grad(
+        grads_late, w_qkv, own_places[:, None], other_places[:, None]
+    )
+    grad_normed = grad_normed.astype(F32) + swap_seq(sent_normed).astype(F32)
     scale = lax.rsqrt(jnp.mean(inputs * inputs, axis=-1, keepdims=True) + EPSILON)
     unit = inputs * scale
     scaled = grad_normed * gain_one
@@ -1156,18 +1268,23 @@
     kept = kept + swap_core(chosen(wide, 1 - core, 0)).astype(F32)
     next_kept = chosen(kept, row_of, 0)
     next_kept = next_kept + swap_y(chosen(kept, 1 - row_of, 0).astype(BF16)).astype(F32)
-    next_kept, last_line = lax.optimization_barrier((next_kept, last_line))
-    summed = line_scatter(lambda which: chosen(next_kept, which, 1), line)
+    summed = chosen(next_kept, line, 1)
+    sent_lines = [
+        swap_dp(chosen(next_kept, line ^ step, 1).astype(BF16), 4 * step) for step in range(1, LINE)
+    ]
+    summed = summed + sum(value.astype(F32) for value in sent_lines)
+    summed, last_line = lax.optimization_barrier((summed, last_line))
     part_grads = (
         line_partial(*range(LINE)) + last_line[0].astype(F32) + last_line[1].astype(F32)
     ).astype(BF16)
     same_grads = jnp.where(first_core, part_grads[:, :half], part_grads[:, half : 2 * half])
     cross_grads = jnp.where(first_core, part_grads[:, half : 2 * half], part_grads[:, :half])
-    same = both_axes(jnp.concatenate([same_grads, part_grads[:, 2 * half :]], axis=1), straight)
+    same_grads = jnp.concatenate([same_grads, part_grads[:, 2 * half :]], axis=1)
+    same = both_axes(same_grads, straight)
     cross = both_axes(cross_grads, crossed_back)
+
     grad_w_in = ordered(same[:, :half], cross, 1)
     grad_w_out = same[:, half:].T
-
     kept_rows = chosen(summed, seq, 0)
     sent_rows = swap_seq(chosen(summed, 1 - seq, 0).astype(BF16)).astype(F32)
     cuts = (q_width, q_width + kv_width, qkv_width)

time: 769 us -> 811 us (1.055)
  waiting for transfers between devices: 189 us -> 229 us
  local copies, waits for them, and re-layouts: 32.2 us -> 46 us
  other arithmetic: 84.5 us -> 96.7 us
  starting transfers between devices: 110 us -> 101 us
    ppermute x24 -> x32, waiting for transfers between devices: 21.2 us -> 107 us  [swap_dp(): return lax.ppermute(value, 'dp', [(i, i ^ mask) for i in range(4 * LINE)])]
    ppermute x9 -> x6, waiting for transfers between devices: 35.9 us -> 0.07 us  [line_up(): return lax.ppermute(value, 'dp', [(i, i + 4) for i in range(4 * LINE - 4)])]
    pallas_call x2, Pallas kernels: 136 us -> 109 us  [run_experts(): pl.pallas_call(functools.partial(experts_kernel, tiles, tile // 2), grid_...]
    pallas_call x0 -> x2, Pallas kernels: none -> 21.2 us  [the longest x1 11.2 us: token_grad(): pl.pallas_call(token_grad_kernel, grid=(3,), in_specs=[whole(grad) for gr...]
    ppermute x24 -> x32, starting transfers between devices: 26.4 us -> 38.5 us  [swap_dp(): return lax.ppermute(value, 'dp', [(i, i ^ mask) for i in range(4 * LINE)])]
    ppermute x15 -> x16, waiting for transfers between devices: 100 us -> 89.6 us  [swap_seq(): return lax.ppermute(value, 'seq', [(0, 1), (1, 0)])]
    ppermute x9 -> x6, starting transfers between devices: 40.9 us -> 32.1 us  [line_up(): return lax.ppermute(value, 'dp', [(i, i + 4) for i in range(4 * LINE - 4)])]
    ppermute x15 -> x16, starting transfers between devices: 18.5 us -> 11.9 us  [swap_seq(): return lax.ppermute(value, 'seq', [(0, 1), (1, 0)])]
  transfers between devices with their start and end apart: 64 -> 66, of which waited for: 18 -> 19; matrix products, arithmetic and copies ran while one was open for 27% -> 28% of each run, Pallas kernels for 21% -> 21%
where the time goes in v3:
time: 811 us; the launch traced here: 801 us
  waiting for transfers between devices  229 us (28%)
  Pallas kernels  224 us (28%)
  starting transfers between devices  101 us (12%)
  other arithmetic  96.7 us (12%)
  matrix products  88.1 us (11%)
  local copies, waits for them, and re-layouts  46 us (6%)
  between operations  15.8 us (2%)
    pallas_call x2, Pallas kernels, run_experts(): pl.pallas_call(functools.partial(experts_kernel, tiles, tile // 2), grid_...  109 us
    ppermute x32, waiting for transfers between devices, swap_dp(): return lax.ppermute(value, 'dp', [(i, i ^ mask) for i in range(4 * LINE)])  107 us
    ppermute x16, waiting for transfers between devices, swap_seq(): return lax.ppermute(value, 'seq', [(0, 1), (1, 0)])  89.6 us
    dot_general x15, matrix products, contract(): lax.dot_general(left, right, (((left_dim,), (right_dim,)), ((), ())), pre...  88.1 us
    pallas_call x1, Pallas kernels, attend_back(): pl.pallas_call(attend_back_kernel, grid=(pairs,), in_specs=[pair_block, w...  45.5 us
    ppermute x32, starting transfers between devices, swap_dp(): return lax.ppermute(value, 'dp', [(i, i ^ mask) for i in range(4 * LINE)])  38.5 us
    ppermute x4, waiting for transfers between devices, both_axes(): return lax.ppermute(value, ('seq', 'dp'), pairs)  32.7 us
    ppermute x6, starting transfers between devices, line_up(): return lax.ppermute(value, 'dp', [(i, i + 4) for i in range(4 * LINE - 4)])  32.1 us
  transfers between devices with their start and end apart: 66, of which 19 were waited for; matrix products, arithmetic and copies ran while one was open for 28% of the time, Pallas kernels for 21%

profile of v3, /device:TPU:1, one launch (start us, length us, event | category | flops | bytes accessed | tf_op | source)
XLA Modules:
  0.0 801.3 jit_solution(17361830006711424268)
XLA Ops:
  12.0 3.3 collective-permute-done.5
  24.7 4.4 collective-permute-start
  37.3 4.4 fusion.23
  41.7 10.0 %collective-permute-done = bf16[1536,512]{1,0:T(8,128)(2,1)S(1)} collective-permute-done((bf16[1536,512]{1,0:T(8,128)(2,1)}, bf16[1536,512]{1,0:T(8,128)(2,1)S(1)}, u32[]{:S(2)}, u32[]{:S(2)}) %collective-permute-start) | collective-permute-done | bytes 1572896 | tf_op jit(solution)/shard_map/ppermute | solution.py:1037
  54.7 4.0 collective-permute-start.3
  62.1 3.3 concatenate.98.refs_6_
  72.8 44.2 %collective-permute-done.15 = bf16[192,1536]{1,0:T(8,128)(2,1)S(1)} collective-permute-done((bf16[192,1536]{1,0:T(8,128)(2,1)S(1)}, bf16[192,1536]{1,0:T(8,128)(2,1)S(1)}, u32[]{:S(2)}, u32[]{:S(2)}) %collective-permute-start.15) | collective-permute-done | bytes 589856 | tf_op jit(solution)/shard_map/ppermute | solution.py:377
  121.3 6.7 add_convert_fusion.2.x_ref
  128.1 5.4 collective-permute-start.10
  138.8 6.1 collective-permute-done.16
  147.3 3.1 collective-permute-start.17
  153.4 10.3 %project.1 = (bf16[1024,1536]{1,0:T(8,128)(2,1)}, bf16[1024,768]{1,0:T(8,128)(2,1)}, bf16[4,1024,64]{2,1,0:T(8,128)(2,1)}, bf16[4,1024,64]{2,1,0:T(8,128)(2,1)}) custom-call(bf16[1024,1536]{1,0:T(8,128)(2,1)} %add_convert_fusion.2.x_ref, f32[1,1536]{1,0:T(1,128)} %copy.93.gain_ref, bf16[1536,1408]{1,0:T(8,128)(2,1)} %bitcast.94, ...), custom_call_target="tpu_custom_call" | custom-call | flops 251658240 | bytes 3538944 | tf_op jit(solution)/shard_map/project/pallas_call | solution.py:501
  163.7 15.0 %attend.2 = bf16[1024,384]{1,0:T(8,128)(2,1)} custom-call(bf16[1024,768]{1,0:T(8,128)(2,1)} %get-tuple-element.108.q_ref, bf16[4,1024,64]{2,1,0:T(8,128)(2,1)} %get-tuple-element.105.k_ref, bf16[4,1024,64]{2,1,0:T(8,128)(2,1)} %get-tuple-element.106.v_ref, s32[1024,1]{1,0:T(8,128)} %copy.94.start_ref), custom_call_target="tpu_custom_call" | custom-call | flops 113246208 | bytes 3145728 | tf_op jit(solution)/shard_map/attend/pallas_call | solution.py:682
  178.7 2.7 collective-permute-done.6.refs_8_.refs_7_
  181.4 15.0 %attend.3 = bf16[1024,384]{1,0:T(8,128)(2,1)} custom-call(bf16[1024,768]{1,0:T(8,128)(2,1)} %get-tuple-element.108.q_ref, bf16[4,1024,64]{2,1,0:T(8,128)(2,1)} %get-tuple-element.105.k_ref, bf16[4,1024,64]{2,1,0:T(8,128)(2,1)} %get-tuple-element.106.v_ref, s32[1024,1]{1,0:T(8,128)} %copy.94.start_ref), custom_call_target="tpu_custom_call" | custom-call | flops 113246208 | bytes 3145728 | tf_op jit(solution)/shard_map/attend/pallas_call | solution.py:682
  196.4 2.7 fusion.42
  206.6 3.1 collective-permute-done.9
  211.1 7.2 collective-permute-done.8
  222.3 5.7 collective-permute-start.32
  235.9 10.0 %mix.1 = (f32[512,1536]{1,0:T(8,128)}, bf16[512,1536]{1,0:T(8,128)(2,1)}, bf16[2,768,1536]{2,1,0:T(8,128)(2,1)}) custom-call(s32[3]{0:T(128)} %pad_add_fusion.place_ref, bf16[512,768]{1,0:T(8,128)(2,1)} %get-tuple-element.268.mine_ref, bf16[512,768]{1,0:T(8,128)(2,1)} %copy-done.32, bf16[512,1536]{1,0:T(8,128)(2,1)} %x_ref.1, f32[2,1536]{1,0:T(2,128)} %copy.101.gain_ref, ...), custom_call_target="tpu_custom_call" | custom-call | flops 150994944 | bytes 786432 | tf_op jit(solution)/shard_map/mix/pallas_call | solution.py:563
  247.5 33.0 %collective-permute-done.20.refs_0_.refs_1_ = bf16[512,1536]{1,0:T(8,128)(2,1)S(1)} collective-permute-done((bf16[512,1536]{1,0:T(8,128)(2,1)}, bf16[512,1536]{1,0:T(8,128)(2,1)S(1)}, u32[]{:S(2)}, u32[]{:S(2)}) %collective-permute-start.20) | collective-permute-done | bytes 1572896 | tf_op jit(solution)/shard_map/ppermute | solution.py:373
  283.3 3.5 collective-permute-start.30
  288.6 8.5 %collective-permute-done.22.refs_2_ = bf16[256,1536]{1,0:T(8,128)(2,1)S(1)} collective-permute-done((bf16[256,1536]{1,0:T(8,128)(2,1)S(1)}, bf16[256,1536]{1,0:T(8,128)(2,1)S(1)}, u32[]{:S(2)}, u32[]{:S(2)}) %collective-permute-start.22) | collective-permute-done | bytes 786464 | tf_op jit(solution)/shard_map/ppermute | solution.py:377
  297.1 3.5 collective-permute-start.29
  300.6 2.7 collective-permute-start.31
  306.8 2.6 select_select_fusion
  310.3 54.5 %experts.2 = (bf16[1024,1536]{1,0:T(8,128)(2,1)}, bf16[1024,1536]{1,0:T(8,128)(2,1)}, bf16[1024,1536]{1,0:T(8,128)(2,1)}, bf16[1024,1536]{1,0:T(8,128)(2,1)}, bf...) custom-call(s32[1]{0:T(128)} %bitcast.place_ref, ...), custom_call_target="tpu_custom_call" | custom-call | flops 2415919104 | bytes 50331648 | tf_op jit(solution)/shard_map/experts/pallas_call | solution.py:919
  365.8 8.1 %collective-permute-done.34 = bf16[1024,1536]{1,0:T(8,128)(2,1)S(1)} collective-permute-done((bf16[1024,1536]{1,0:T(8,128)(2,1)}, bf16[1024,1536]{1,0:T(8,128)(2,1)S(1)}, u32[]{:S(2)}, u32[]{:S(2)}) %collective-permute-start.34) | collective-permute-done | bytes 3145760 | tf_op jit(solution)/shard_map/ppermute | solution.py:377
  373.9 2.7 add_convert_fusion.1
  382.4 54.5 %experts.3 = (bf16[1024,1536]{1,0:T(8,128)(2,1)}, bf16[1024,1536]{1,0:T(8,128)(2,1)}, bf16[1024,1536]{1,0:T(8,128)(2,1)}, bf16[1024,1536]{1,0:T(8,128)(2,1)}, bf...) custom-call(s32[1]{0:T(128)} %bitcast.place_ref, ...), custom_call_target="tpu_custom_call", output_to_operand_aliasing={{4}: (21, {}), {5}: (22, {}), {6}: (23, {}), {7}: (24, {}),... | custom-call | flops 2415919104 | bytes 50331648 | tf_op jit(solution)/shard_map/experts/pallas_call | solution.py:919
  437.9 11.3 %fusion.9 = bf16[1536,512]{1,0:T(8,128)(2,1)S(1)} fusion(bf16[4096,1536]{1,0:T(8,128)(2,1)} %get-tuple-element.151, bf16[4096,512]{1,0:T(8,128)(2,1)} %get-tuple-element.144), kind=kOutput, calls=%fused_computation.36 | convolution fusion | flops 6444023808 | bytes 18350080 | tf_op jit(solution)/shard_map/dot_general | solution.py:643
  449.3 16.8 %convolution_convert_fusion.2 = bf16[1536,1024]{1,0:T(8,128)(2,1)S(1)} fusion(bf16[4096,1536]{1,0:T(8,128)(2,1)S(1)} %copy-done.27, bf16[4096,1024]{1,0:T(8,128)(2,1)} %get-tuple-element.142), kind=kOutput, calls=%fused_computation.15 | convolution fusion | flops 12886474752 | bytes 24117248 | tf_op jit(solution)/shard_map/dot_general | solution.py:643
  468.1 5.4 collective-permute-start.44
  476.6 2.9 convert_add_fusion.1
  479.4 3.1 fusion.29
  483.6 16.6 %convolution_convert_fusion.1 = bf16[1536,1024]{1,0:T(8,128)(2,1)S(1)} fusion(bf16[4096,1536]{1,0:T(8,128)(2,1)S(1)} %copy-done.27, bf16[4096,1024]{1,0:T(8,128)(2,1)} %get-tuple-element.150), kind=kOutput, calls=%fused_computation.14 | convolution fusion | flops 12886474752 | bytes 24117248 | tf_op jit(solution)/shard_map/dot_general | solution.py:643
  500.2 11.1 %fusion.10 = bf16[1536,512]{1,0:T(8,128)(2,1)S(1)} fusion(bf16[4096,1536]{1,0:T(8,128)(2,1)} %get-tuple-element.151, bf16[4096,512]{1,0:T(8,128)(2,1)} %get-tuple-element.152), kind=kOutput, calls=%fused_computation.37 | convolution fusion | flops 6444023808 | bytes 18350080 | tf_op jit(solution)/shard_map/dot_general | solution.py:643
  523.1 3.2 add_convert_fusion.7
  526.3 5.6 collective-permute-start.47
  531.9 3.4 add_convert_fusion.6
  537.2 4.4 convolution_convert_fusion
  541.6 3.7 add_convert_fusion
  550.4 3.4 add_convert_fusion.8.d_ref
  553.8 45.5 %attend_back.1 = (bf16[1024,768]{1,0:T(8,128)(2,1)}, bf16[1024,256]{1,0:T(8,128)(2,1)}, bf16[1024,256]{1,0:T(8,128)(2,1)}) custom-call(bf16[1024,768]{1,0:T(8,128)(2,1)} %get-tuple-element.108.q_ref, bf16[4,1024,64]{2,1,0:T(8,128)(2,1)} %get-tuple-element.105.k_ref, bf16[4,1024,64]{2,1,0:T(8,128)(2,1)} %get-tuple-element.106.v_ref, ...), custom_call_target="tpu_custom_call" | custom-call | flops 566231040 | bytes 6291456 | tf_op jit(solution)/shard_map/attend_back/pallas_call | solution.py:750
  599.4 6.9 convert_add_fusion
  606.6 5.3 add_convert_fusion.4
  611.9 8.3 %qkv_grad.1 = bf16[2,2,2,4,48,1408]{5,4,3,2,1,0:T(8,128)(2,1)} custom-call(bf16[1024,1536]{1,0:T(8,128)(2,1)} %get-tuple-element.173.h_ref, bf16[1024,768]{1,0:T(8,128)(2,1)} %get-tuple-element.174.dq_ref, bf16[1024,256]{1,0:T(8,128)(2,1)} %get-tuple-element.175.dk_ref, bf16[1024,256]{1,0:T(8,128)(2,1)} %get-tuple-element.176.dv_ref, ...), custom_call_target="tpu_custom_call" | custom-call | flops 251658240 | bytes 1572864 | tf_op jit(solution)/shard_map/qkv_grad/pallas_call | solution.py:971
  620.2 11.2 %token_grad.1 = (bf16[512,1536]{1,0:T(8,128)(2,1)}, bf16[512,1536]{1,0:T(8,128)(2,1)}) custom-call(bf16[1024,768]{1,0:T(8,128)(2,1)} %get-tuple-element.174.dq_ref, bf16[1024,256]{1,0:T(8,128)(2,1)} %get-tuple-element.175.dk_ref, bf16[1024,256]{1,0:T(8,128)(2,1)} %get-tuple-element.176.dv_ref, bf16[1536,1408]{1,0:T(8,128)(2,1)} %bitcast.95, ...), custom_call_target="tpu_custom_call" | custom-call | flops 251658240 | bytes 1572864 | tf_op jit(solution)/shard_map/token_grad/pallas_call | solution.py:610
  632.1 3.1 dynamic-slice_bitcast_fusion
  637.3 2.7 fusion.26
  642.5 5.9 collective-permute-start.59
  649.7 34.1 %collective-permute-done.51 = bf16[256,1536]{1,0:T(8,128)(2,1)} collective-permute-done((bf16[256,1536]{1,0:T(8,128)(2,1)}, bf16[256,1536]{1,0:T(8,128)(2,1)}, u32[]{:S(2)}, u32[]{:S(2)}) %collective-permute-start.51) | collective-permute-done | bytes 786464 | tf_op jit(solution)/shard_map/ppermute | solution.py:373
  683.8 4.5 fusion.27
  690.3 3.3 fusion.2
  693.6 2.8 convert_add_fusion.2
  698.1 4.2 fusion.5
  702.3 2.7 collective-permute-done.52
  707.2 20.9 %collective-permute-done.55 = bf16[2,4,48,1408]{3,2,1,0:T(8,128)(2,1)S(1)} collective-permute-done((bf16[2,4,48,1408]{3,2,1,0:T(8,128)(2,1)S(1)}, bf16[2,4,48,1408]{3,2,1,0:T(8,128)(2,1)S(1)}, u32[]{:S(2)}, u32[]{:S(2)}) %collective-permute-start.55) | collective-permute-done | bytes 1081376 | tf_op jit(solution)/shard_map/ppermute | solution.py:377
  728.4 3.1 collective-permute-start.58
  735.8 19.0 %collective-permute-done.57 = bf16[2,48,1408]{2,1,0:T(8,128)(2,1)S(1)} collective-permute-done((bf16[2,48,1408]{2,1,0:T(8,128)(2,1)S(1)}, bf16[2,48,1408]{2,1,0:T(8,128)(2,1)S(1)}, u32[]{:S(2)}, u32[]{:S(2)}) %collective-permute-start.57) | collective-permute-done | bytes 270368 | tf_op jit(solution)/shard_map/ppermute | solution.py:377
  755.1 3.5 add_convert_fusion.3
  758.9 4.7 collective-permute-start.62
  767.3 15.6 %collective-permute-done.63 = bf16[1536,256]{1,0:T(8,128)(2,1)S(1)} collective-permute-done((bf16[1536,256]{1,0:T(8,128)(2,1)S(1)}, bf16[1536,256]{1,0:T(8,128)(2,1)S(1)}, u32[]{:S(2)}, u32[]{:S(2)}) %collective-permute-start.63) | collective-permute-done | bytes 786464 | tf_op jit(solution)/shard_map/ppermute | solution.py:1037
  783.0 7.2 collective-permute-done.62
  (356 shorter events, 139.9 us)
Async XLA Ops:
  7.2 143.2 %all-gather.2.cloned.1.call-start = ((), (), s32[]{:S(2)}) async-start(), calls=%async_computation.1 | async-start | bytes 4595712 | tf_op jit(solution)/shard_map/all_gather | solution.py:1058
  9.9 5.4 collective-permute-start.5
  16.1 672.5 %reduce-scatter.2.cloned.1.call-start = ((), (), s32[]{:S(2)}) async-start(), calls=%async_computation.2 | async-start | bytes 4866048 | tf_op jit(solution)/shard_map/reduce_scatter | solution.py:1260
  16.2 42.5 %collective-permute-start.12 = (bf16[48,1536]{1,0:T(8,128)(2,1)}, bf16[48,1536]{1,0:T(8,128)(2,1)}, u32[]{:S(2)}, u32[]{:S(2)}) collective-permute-start(bf16[48,1536]{1,0:T(8,128)(2,1)} %param.26), channel_id=1, source_target_pairs={{0,4},{1,5},{2,6},{3,7},{4,0},{5,1},{6,2},{7,3},{8,12},{9,13},{10,... | collective-permute-start | bytes 442376 | tf_op jit(solution)/shard_map/ppermute | solution.py:377
  17.5 47.9 %collective-permute-start.13 = (bf16[48,1536]{1,0:T(8,128)(2,1)}, bf16[48,1536]{1,0:T(8,128)(2,1)}, u32[]{:S(2)}, u32[]{:S(2)}) collective-permute-start(bf16[48,1536]{1,0:T(8,128)(2,1)} %param.26), channel_id=1, source_target_pairs={{0,8},{1,9},{2,10},{3,11},{4,12},{5,13},{6,14},{7,15},{8,0},{9,1},... | collective-permute-start | bytes 442376 | tf_op jit(solution)/shard_map/ppermute | solution.py:377
  19.8 46.9 %collective-permute-start.14 = (bf16[48,1536]{1,0:T(8,128)(2,1)}, bf16[48,1536]{1,0:T(8,128)(2,1)}, u32[]{:S(2)}, u32[]{:S(2)}) collective-permute-start(bf16[48,1536]{1,0:T(8,128)(2,1)} %param.26), channel_id=1, source_target_pairs={{0,12},{1,13},{2,14},{3,15},{4,8},{5,9},{6,10},{7,11},{8,4},{9,5},... | collective-permute-start | bytes 442376 | tf_op jit(solution)/shard_map/ppermute | solution.py:377
  20.8 20.9 %collective-permute-start.1 = (bf16[1536,256]{1,0:T(8,128)(2,1)}, bf16[1536,256]{1,0:T(8,128)(2,1)}, u32[]{:S(2)}, u32[]{:S(2)}) collective-permute-start(bf16[1536,256]{1,0:T(8,128)(2,1)} %get-tuple-element.266), channel_id=1, source_target_pairs={{0,1},{1,17},{2,3},{3,19},{4,5},{5,21},{6,7},{7,23},{8,9},{9,25},{... | collective-permute-start | bytes 2359304 | tf_op jit(solution)/shard_map/ppermute | solution.py:1037
  24.7 27.0 %collective-permute-start = (bf16[1536,512]{1,0:T(8,128)(2,1)}, bf16[1536,512]{1,0:T(8,128)(2,1)S(1)}, u32[]{:S(2)}, u32[]{:S(2)}) collective-permute-start(bf16[1536,512]{1,0:T(8,128)(2,1)} %pad_maximum_fusion.6), channel_id=1, source_target_pairs={{0,0},{1,16},{2,2},{3,18},{4,4},{5,20},{6,6},{7,22},{8,8},{9,24},{... | collective-permute-start | bytes 4718600 | tf_op jit(solution)/shard_map/ppermute | solution.py:1037
  54.6 63.3 %collective-permute-start.2 = (bf16[512,1536]{1,0:T(8,128)(2,1)S(1)}, bf16[512,1536]{1,0:T(8,128)(2,1)}, u32[]{:S(2)}, u32[]{:S(2)}) collective-permute-start(bf16[512,1536]{1,0:T(8,128)(2,1)S(1)} %copy-done.13), channel_id=1, source_target_pairs={{0,16},{16,0},{1,17},{17,1},{2,18},{18,2},{3,19},{19,3},{4,20},{20... | collective-permute-start | bytes 4718600 | tf_op jit(solution)/shard_map/ppermute | solution.py:373
  54.7 73.4 %collective-permute-start.3 = (bf16[1536,768]{1,0:T(8,128)(2,1)}, bf16[1536,768]{1,0:T(8,128)(2,1)}, u32[]{:S(2)}, u32[]{:S(2)}) collective-permute-start(bf16[1536,768]{1,0:T(8,128)(2,1)} %pad_maximum_fusion.1.refs_19_.refs_15_), channel_id=1, source_target_pairs={{0,4},{1,5},{2,6},{3,7},{4,8},{5,9},{6,10},{7,11},{8,12},{9,13},{1... | collective-permute-start | bytes 7077896 | tf_op jit(solution)/shard_map/ppermute | solution.py:389
  58.7 69.4 %collective-permute-start.4 = (bf16[1536,768]{1,0:T(8,128)(2,1)}, bf16[1536,768]{1,0:T(8,128)(2,1)}, u32[]{:S(2)}, u32[]{:S(2)}) collective-permute-start(bf16[1536,768]{1,0:T(8,128)(2,1)} %pad_maximum_fusion.1.refs_19_.refs_15_), channel_id=1, source_target_pairs={{4,0},{5,1},{6,2},{7,3},{8,4},{9,5},{10,6},{11,7},{12,8},{13,9},{1... | collective-permute-start | bytes 7077896 | tf_op jit(solution)/shard_map/ppermute | solution.py:393
  65.4 113.3 %collective-permute-start.7 = (bf16[512,1664]{1,0:T(8,128)(2,1)}, bf16[512,1664]{1,0:T(8,128)(2,1)S(1)}, u32[]{:S(2)}, u32[]{:S(2)}) collective-permute-start(bf16[512,1664]{1,0:T(8,128)(2,1)} %concatenate.98.refs_6_), channel_id=1, source_target_pairs={{0,2},{1,3},{2,0},{3,1},{4,6},{5,7},{6,4},{7,5},{8,10},{9,11},{10,... | collective-permute-start | bytes 5111816 | tf_op jit(solution)/shard_map/ppermute | solution.py:377
  67.8 49.2 %collective-permute-start.15 = (bf16[192,1536]{1,0:T(8,128)(2,1)S(1)}, bf16[192,1536]{1,0:T(8,128)(2,1)S(1)}, u32[]{:S(2)}, u32[]{:S(2)}) collective-permute-start(bf16[192,1536]{1,0:T(8,128)(2,1)S(1)} %pad_maximum_fusion.10), channel_id=1, source_target_pairs={{0,2},{1,3},{2,0},{3,1},{4,6},{5,7},{6,4},{7,5},{8,10},{9,11},{10,... | collective-permute-start | bytes 1769480 | tf_op jit(solution)/shard_map/ppermute | solution.py:377
  117.9 27.0 %collective-permute-start.16 = (bf16[384,1536]{1,0:T(8,128)(2,1)}, bf16[384,1536]{1,0:T(8,128)(2,1)}, u32[]{:S(2)}, u32[]{:S(2)}) collective-permute-start(bf16[384,1536]{1,0:T(8,128)(2,1)} %constant_dynamic-update-slice_fusion), channel_id=1, source_target_pairs={{0,16},{16,0},{1,17},{17,1},{2,18},{18,2},{3,19},{19,3},{4,20},{20... | collective-permute-start | bytes 3538952 | tf_op jit(solution)/shard_map/ppermute | solution.py:373
  120.8 60.6 %collective-permute-start.6 = (bf16[512,1664]{1,0:T(8,128)(2,1)}, bf16[512,1664]{1,0:T(8,128)(2,1)}, u32[]{:S(2)}, u32[]{:S(2)}) collective-permute-start(bf16[512,1664]{1,0:T(8,128)(2,1)} %concatenate.98.refs_6_), channel_id=1, source_target_pairs={{0,16},{16,0},{1,17},{17,1},{2,18},{18,2},{3,19},{19,3},{4,20},{20... | collective-permute-start | bytes 5111816 | tf_op jit(solution)/shard_map/ppermute | solution.py:373
  128.1 94.2 %collective-permute-start.10 = (bf16[1536,768]{1,0:T(8,128)(2,1)}, bf16[1536,768]{1,0:T(8,128)(2,1)}, u32[]{:S(2)}, u32[]{:S(2)}) collective-permute-start(bf16[1536,768]{1,0:T(8,128)(2,1)} %collective-permute-done.3.refs_18_.refs_14_), channel_id=1, source_target_pairs={{0,4},{1,5},{2,6},{3,7},{4,8},{5,9},{6,10},{7,11},{8,12},{9,13},{1... | collective-permute-start | bytes 7077896 | tf_op jit(solution)/shard_map/ppermute | solution.py:389
  133.5 88.7 %collective-permute-start.11 = (bf16[1536,768]{1,0:T(8,128)(2,1)}, bf16[1536,768]{1,0:T(8,128)(2,1)}, u32[]{:S(2)}, u32[]{:S(2)}) collective-permute-start(bf16[1536,768]{1,0:T(8,128)(2,1)} %collective-permute-done.4.refs_20_.refs_16_), channel_id=1, source_target_pairs={{4,0},{5,1},{6,2},{7,3},{8,4},{9,5},{10,6},{11,7},{12,8},{13,9},{1... | collective-permute-start | bytes 7077896 | tf_op jit(solution)/shard_map/ppermute | solution.py:393
  147.3 88.6 %collective-permute-start.17 = (bf16[768,1536]{1,0:T(8,128)(2,1)}, bf16[768,1536]{1,0:T(8,128)(2,1)}, u32[]{:S(2)}, u32[]{:S(2)}) collective-permute-start(bf16[768,1536]{1,0:T(8,128)(2,1)} %constant_dynamic-update-slice_fusion.5.own_ref), channel_id=1, source_target_pairs={{0,1},{1,0},{2,3},{3,2},{4,5},{5,4},{6,7},{7,6},{8,9},{9,8},{10,11... | collective-permute-start | bytes 7077896 | tf_op jit(solution)/shard_map/ppermute | solution.py:377
  199.1 10.6 %collective-permute-start.9 = (bf16[512,384]{1,0:T(8,128)(2,1)}, bf16[512,384]{1,0:T(8,128)(2,1)S(1)}, u32[]{:S(2)}, u32[]{:S(2)}) collective-permute-start(bf16[512,384]{1,0:T(8,128)(2,1)} %fusion.42), channel_id=1, source_target_pairs={{0,16},{16,0},{1,17},{17,1},{2,18},{18,2},{3,19},{19,3},{4,20},{20... | collective-permute-start | bytes 1179656 | tf_op jit(solution)/shard_map/ppermute | solution.py:373
  202.9 15.4 %collective-permute-start.8 = (bf16[512,384]{1,0:T(8,128)(2,1)}, bf16[512,384]{1,0:T(8,128)(2,1)S(1)}, u32[]{:S(2)}, u32[]{:S(2)}) collective-permute-start(bf16[512,384]{1,0:T(8,128)(2,1)} %fusion.41), channel_id=1, source_target_pairs={{0,16},{16,0},{1,17},{17,1},{2,18},{18,2},{3,19},{19,3},{4,20},{20... | collective-permute-start | bytes 1179656 | tf_op jit(solution)/shard_map/ppermute | solution.py:373
  209.8 36.2 %collective-permute-start.18 = (bf16[256,1664]{1,0:T(8,128)(2,1)}, bf16[256,1664]{1,0:T(8,128)(2,1)}, u32[]{:S(2)}, u32[]{:S(2)}) collective-permute-start(bf16[256,1664]{1,0:T(8,128)(2,1)} %slice.166), channel_id=1, source_target_pairs={{0,2},{1,3},{2,0},{3,1},{4,6},{5,7},{6,4},{7,5},{8,10},{9,11},{10,... | collective-permute-start | bytes 2555912 | tf_op jit(solution)/shard_map/ppermute | solution.py:377
  219.1 26.9 %collective-permute-start.19 = (bf16[256,1664]{1,0:T(8,128)(2,1)}, bf16[256,1664]{1,0:T(8,128)(2,1)}, u32[]{:S(2)}, u32[]{:S(2)}) collective-permute-start(bf16[256,1664]{1,0:T(8,128)(2,1)} %slice.167), channel_id=1, source_target_pairs={{0,16},{16,0},{1,17},{17,1},{2,18},{18,2},{3,19},{19,3},{4,20},{20... | collective-permute-start | bytes 2555912 | tf_op jit(solution)/shard_map/ppermute | solution.py:373
  222.3 64.5 %collective-permute-start.32 = (bf16[1536,768]{1,0:T(8,128)(2,1)}, bf16[1536,768]{1,0:T(8,128)(2,1)}, u32[]{:S(2)}, u32[]{:S(2)}) collective-permute-start(bf16[1536,768]{1,0:T(8,128)(2,1)} %collective-permute-done.10.refs_17_.refs_13_), channel_id=1, source_target_pairs={{0,4},{1,5},{2,6},{3,7},{4,8},{5,9},{6,10},{7,11},{8,12},{9,13},{1... | collective-permute-start | bytes 7077896 | tf_op jit(solution)/shard_map/ppermute | solution.py:389
  232.3 54.5 %collective-permute-start.33 = (bf16[1536,768]{1,0:T(8,128)(2,1)}, bf16[1536,768]{1,0:T(8,128)(2,1)}, u32[]{:S(2)}, u32[]{:S(2)}) collective-permute-start(bf16[1536,768]{1,0:T(8,128)(2,1)} %collective-permute-done.11.refs_21_.refs_17_), channel_id=1, source_target_pairs={{4,0},{5,1},{6,2},{7,3},{8,4},{9,5},{10,6},{11,7},{12,8},{13,9},{1... | collective-permute-start | bytes 7077896 | tf_op jit(solution)/shard_map/ppermute | solution.py:393
  246.0 34.5 %collective-permute-start.20 = (bf16[512,1536]{1,0:T(8,128)(2,1)}, bf16[512,1536]{1,0:T(8,128)(2,1)S(1)}, u32[]{:S(2)}, u32[]{:S(2)}) collective-permute-start(bf16[512,1536]{1,0:T(8,128)(2,1)} %get-tuple-element.117.refs_0_), channel_id=1, source_target_pairs={{0,16},{16,0},{1,17},{17,1},{2,18},{18,2},{3,19},{19,3},{4,20},{20... | collective-permute-start | bytes 4718600 | tf_op jit(solution)/shard_map/ppermute | solution.py:373
  246.1 35.9 %collective-permute-start.21 = (bf16[512,1536]{1,0:T(8,128)(2,1)}, bf16[512,1536]{1,0:T(8,128)(2,1)}, u32[]{:S(2)}, u32[]{:S(2)}) collective-permute-start(bf16[512,1536]{1,0:T(8,128)(2,1)} %get-tuple-element.117.refs_0_), channel_id=1, source_target_pairs={{0,2},{1,3},{2,0},{3,1},{4,6},{5,7},{6,4},{7,5},{8,10},{9,11},{10,... | collective-permute-start | bytes 4718600 | tf_op jit(solution)/shard_map/ppermute | solution.py:377
  280.6 16.5 %collective-permute-start.22 = (bf16[256,1536]{1,0:T(8,128)(2,1)S(1)}, bf16[256,1536]{1,0:T(8,128)(2,1)S(1)}, u32[]{:S(2)}, u32[]{:S(2)}) collective-permute-start(bf16[256,1536]{1,0:T(8,128)(2,1)S(1)} %slice.216), channel_id=1, source_target_pairs={{0,2},{1,3},{2,0},{3,1},{4,6},{5,7},{6,4},{7,5},{8,10},{9,11},{10,... | collective-permute-start | bytes 2359304 | tf_op jit(solution)/shard_map/ppermute | solution.py:377
  283.2 17.4 %collective-permute-start.23 = (bf16[256,1536]{1,0:T(8,128)(2,1)S(1)}, bf16[256,1536]{1,0:T(8,128)(2,1)S(1)}, u32[]{:S(2)}, u32[]{:S(2)}) collective-permute-start(bf16[256,1536]{1,0:T(8,128)(2,1)S(1)} %slice.217), channel_id=1, source_target_pairs={{0,16},{16,0},{1,17},{17,1},{2,18},{18,2},{3,19},{19,3},{4,20},{20... | collective-permute-start | bytes 2359304 | tf_op jit(solution)/shard_map/ppermute | solution.py:373
  283.3 20.0 %collective-permute-start.30 = (bf16[256,1664]{1,0:T(8,128)(2,1)}, bf16[256,1664]{1,0:T(8,128)(2,1)}, u32[]{:S(2)}, u32[]{:S(2)}) collective-permute-start(bf16[256,1664]{1,0:T(8,128)(2,1)} %collective-permute-done.18.refs_10_), channel_id=1, source_target_pairs={{0,1},{1,0},{2,3},{3,2},{4,5},{5,4},{6,7},{7,6},{8,9},{9,8},{10,11... | collective-permute-start | bytes 2555912 | tf_op jit(solution)/shard_map/ppermute | solution.py:377
  286.8 19.2 %collective-permute-start.24 = (bf16[512,1536]{1,0:T(8,128)(2,1)S(1)}, bf16[512,1536]{1,0:T(8,128)(2,1)}, u32[]{:S(2)}, u32[]{:S(2)}) collective-permute-start(bf16[512,1536]{1,0:T(8,128)(2,1)S(1)} %collective-permute-done.20.refs_0_.refs_1_), channel_id=1, source_target_pairs={{0,1},{1,0},{2,3},{3,2},{4,5},{5,4},{6,7},{7,6},{8,9},{9,8},{10,11... | collective-permute-start | bytes 4718600 | tf_op jit(solution)/shard_map/ppermute | solution.py:377
  286.8 23.5 %collective-permute-start.28 = (bf16[512,1664]{1,0:T(8,128)(2,1)}, bf16[512,1664]{1,0:T(8,128)(2,1)}, u32[]{:S(2)}, u32[]{:S(2)}) collective-permute-start(bf16[512,1664]{1,0:T(8,128)(2,1)} %collective-permute-done.6.refs_8_.refs_7_), channel_id=1, source_target_pairs={{0,1},{1,0},{2,3},{3,2},{4,5},{5,4},{6,7},{7,6},{8,9},{9,8},{10,11... | collective-permute-start | bytes 5111816 | tf_op jit(solution)/shard_map/ppermute | solution.py:377
  297.1 13.2 %collective-permute-start.29 = (bf16[512,1664]{1,0:T(8,128)(2,1)S(1)}, bf16[512,1664]{1,0:T(8,128)(2,1)}, u32[]{:S(2)}, u32[]{:S(2)}) collective-permute-start(bf16[512,1664]{1,0:T(8,128)(2,1)S(1)} %collective-permute-done.7.refs_9_.refs_8_), channel_id=1, source_target_pairs={{0,1},{1,0},{2,3},{3,2},{4,5},{5,4},{6,7},{7,6},{8,9},{9,8},{10,11... | collective-permute-start | bytes 5111816 | tf_op jit(solution)/shard_map/ppermute | solution.py:377
  300.6 5.0 collective-permute-start.31
  303.3 7.0 collective-permute-start.25
  364.8 9.0 %collective-permute-start.34 = (bf16[1024,1536]{1,0:T(8,128)(2,1)}, bf16[1024,1536]{1,0:T(8,128)(2,1)S(1)}, u32[]{:S(2)}, u32[]{:S(2)}) collective-permute-start(bf16[1024,1536]{1,0:T(8,128)(2,1)} %get-tuple-element.127), channel_id=1, source_target_pairs={{0,1},{1,0},{2,3},{3,2},{4,5},{5,4},{6,7},{7,6},{8,9},{9,8},{10,11... | collective-permute-start | bytes 9437192 | tf_op jit(solution)/shard_map/ppermute | solution.py:377
  365.3 17.1 %collective-permute-start.35 = (bf16[512,1536]{1,0:T(8,128)(2,1)}, bf16[512,1536]{1,0:T(8,128)(2,1)}, u32[]{:S(2)}, u32[]{:S(2)}) collective-permute-start(bf16[512,1536]{1,0:T(8,128)(2,1)} %get-tuple-element.117.refs_0_), channel_id=1, source_target_pairs={{0,1},{1,0},{2,3},{3,2},{4,5},{5,4},{6,7},{7,6},{8,9},{9,8},{10,11... | collective-permute-start | bytes 4718600 | tf_op jit(solution)/shard_map/ppermute | solution.py:377
  365.4 17.0 %collective-permute-start.36 = (bf16[512,1664]{1,0:T(8,128)(2,1)}, bf16[512,1664]{1,0:T(8,128)(2,1)}, u32[]{:S(2)}, u32[]{:S(2)}) collective-permute-start(bf16[512,1664]{1,0:T(8,128)(2,1)} %concatenate.98.refs_6_), channel_id=1, source_target_pairs={{0,1},{1,0},{2,3},{3,2},{4,5},{5,4},{6,7},{7,6},{8,9},{9,8},{10,11... | collective-permute-start | bytes 5111816 | tf_op jit(solution)/shard_map/ppermute | solution.py:377
  378.5 59.4 %collective-permute-start.37 = (bf16[512,1536]{1,0:T(8,128)(2,1)}, bf16[512,1536]{1,0:T(8,128)(2,1)}, u32[]{:S(2)}, u32[]{:S(2)}) collective-permute-start(bf16[512,1536]{1,0:T(8,128)(2,1)} %get-tuple-element.247), channel_id=1, source_target_pairs={{0,2},{1,3},{2,0},{3,1},{4,6},{5,7},{6,4},{7,5},{8,10},{9,11},{10,... | collective-permute-start | bytes 4718600 | tf_op jit(solution)/shard_map/ppermute | solution.py:377
  380.0 57.9 %collective-permute-start.38 = (bf16[512,1536]{1,0:T(8,128)(2,1)}, bf16[512,1536]{1,0:T(8,128)(2,1)}, u32[]{:S(2)}, u32[]{:S(2)}) collective-permute-start(bf16[512,1536]{1,0:T(8,128)(2,1)} %get-tuple-element.246), channel_id=1, source_target_pairs={{0,16},{16,0},{1,17},{17,1},{2,18},{18,2},{3,19},{19,3},{4,20},{20... | collective-permute-start | bytes 4718600 | tf_op jit(solution)/shard_map/ppermute | solution.py:373
  436.9 39.6 %collective-permute-start.39 = (bf16[1024,1536]{1,0:T(8,128)(2,1)}, bf16[1024,1536]{1,0:T(8,128)(2,1)}, u32[]{:S(2)}, u32[]{:S(2)}) collective-permute-start(bf16[1024,1536]{1,0:T(8,128)(2,1)} %get-tuple-element.146), channel_id=1, source_target_pairs={{0,1},{1,0},{2,3},{3,2},{4,5},{5,4},{6,7},{7,6},{8,9},{9,8},{10,11... | collective-permute-start | bytes 9437192 | tf_op jit(solution)/shard_map/ppermute | solution.py:377
  468.1 54.9 %collective-permute-start.44 = (bf16[1536,768]{1,0:T(8,128)(2,1)}, bf16[1536,768]{1,0:T(8,128)(2,1)}, u32[]{:S(2)}, u32[]{:S(2)}) collective-permute-start(bf16[1536,768]{1,0:T(8,128)(2,1)} %pad_maximum_fusion.3), channel_id=1, source_target_pairs={{0,4},{1,5},{2,6},{3,7},{4,8},{5,9},{6,10},{7,11},{8,12},{9,13},{1... | collective-permute-start | bytes 7077896 | tf_op jit(solution)/shard_map/ppermute | solution.py:389
  475.1 56.7 %collective-permute-start.45 = (bf16[1536,768]{1,0:T(8,128)(2,1)}, bf16[1536,768]{1,0:T(8,128)(2,1)}, u32[]{:S(2)}, u32[]{:S(2)}) collective-permute-start(bf16[1536,768]{1,0:T(8,128)(2,1)} %pad_maximum_fusion.2), channel_id=1, source_target_pairs={{4,0},{5,1},{6,2},{7,3},{8,4},{9,5},{10,6},{11,7},{12,8},{13,9},{1... | collective-permute-start | bytes 7077896 | tf_op jit(solution)/shard_map/ppermute | solution.py:393
  482.5 28.8 %collective-permute-start.40 = (bf16[256,1536]{1,0:T(8,128)(2,1)}, bf16[256,1536]{1,0:T(8,128)(2,1)S(1)}, u32[]{:S(2)}, u32[]{:S(2)}) collective-permute-start(bf16[256,1536]{1,0:T(8,128)(2,1)} %get-tuple-element.236), channel_id=1, source_target_pairs={{0,16},{16,0},{1,17},{17,1},{2,18},{18,2},{3,19},{19,3},{4,20},{20... | collective-permute-start | bytes 2359304 | tf_op jit(solution)/shard_map/ppermute | solution.py:373
  483.3 28.0 %collective-permute-start.41 = (bf16[256,1536]{1,0:T(8,128)(2,1)}, bf16[256,1536]{1,0:T(8,128)(2,1)S(1)}, u32[]{:S(2)}, u32[]{:S(2)}) collective-permute-start(bf16[256,1536]{1,0:T(8,128)(2,1)} %get-tuple-element.237), channel_id=1, source_target_pairs={{0,2},{1,3},{2,0},{3,1},{4,6},{5,7},{6,4},{7,5},{8,10},{9,11},{10,... | collective-permute-start | bytes 2359304 | tf_op jit(solution)/shard_map/ppermute | solution.py:377
  518.8 22.8 %collective-permute-start.46 = (bf16[1024,1536]{1,0:T(8,128)(2,1)}, bf16[1024,1536]{1,0:T(8,128)(2,1)}, u32[]{:S(2)}, u32[]{:S(2)}) collective-permute-start(bf16[1024,1536]{1,0:T(8,128)(2,1)} %get-tuple-element.158), channel_id=1, source_target_pairs={{0,1},{1,0},{2,3},{3,2},{4,5},{5,4},{6,7},{7,6},{8,9},{9,8},{10,11... | collective-permute-start | bytes 9437192 | tf_op jit(solution)/shard_map/ppermute | solution.py:377
  520.1 79.3 %collective-permute-start.42 = (bf16[1024,1536]{1,0:T(8,128)(2,1)}, bf16[1024,1536]{1,0:T(8,128)(2,1)}, u32[]{:S(2)}, u32[]{:S(2)}) collective-permute-start(bf16[1024,1536]{1,0:T(8,128)(2,1)} %get-tuple-element.156), channel_id=1, source_target_pairs={{0,1},{1,0},{2,3},{3,2},{4,5},{5,4},{6,7},{7,6},{8,9},{9,8},{10,11... | collective-permute-start | bytes 9437192 | tf_op jit(solution)/shard_map/ppermute | solution.py:377
  522.5 26.1 %collective-permute-start.43 = (bf16[512,768]{1,0:T(8,128)(2,1)}, bf16[512,768]{1,0:T(8,128)(2,1)}, u32[]{:S(2)}, u32[]{:S(2)}) collective-permute-start(bf16[512,768]{1,0:T(8,128)(2,1)} %fusion.36), channel_id=1, source_target_pairs={{0,16},{16,0},{1,17},{17,1},{2,18},{18,2},{3,19},{19,3},{4,20},{20... | collective-permute-start | bytes 2359304 | tf_op jit(solution)/shard_map/ppermute | solution.py:373
  526.3 80.0 %collective-permute-start.47 = (bf16[1536,768]{1,0:T(8,128)(2,1)}, bf16[1536,768]{1,0:T(8,128)(2,1)}, u32[]{:S(2)}, u32[]{:S(2)}) collective-permute-start(bf16[1536,768]{1,0:T(8,128)(2,1)} %add_convert_fusion.7), channel_id=1, source_target_pairs={{0,4},{1,5},{2,6},{3,7},{4,8},{5,9},{6,10},{7,11},{8,12},{9,13},{1... | collective-permute-start | bytes 7077896 | tf_op jit(solution)/shard_map/ppermute | solution.py:389
  535.3 71.0 %collective-permute-start.48 = (bf16[1536,768]{1,0:T(8,128)(2,1)}, bf16[1536,768]{1,0:T(8,128)(2,1)}, u32[]{:S(2)}, u32[]{:S(2)}) collective-permute-start(bf16[1536,768]{1,0:T(8,128)(2,1)} %add_convert_fusion.6), channel_id=1, source_target_pairs={{4,0},{5,1},{6,2},{7,3},{8,4},{9,5},{10,6},{11,7},{12,8},{13,9},{1... | collective-permute-start | bytes 7077896 | tf_op jit(solution)/shard_map/ppermute | solution.py:393
  547.2 59.1 %collective-permute-start.49 = (bf16[512,1536]{1,0:T(8,128)(2,1)}, bf16[512,1536]{1,0:T(8,128)(2,1)}, u32[]{:S(2)}, u32[]{:S(2)}) collective-permute-start(bf16[512,1536]{1,0:T(8,128)(2,1)} %get-tuple-element.241), channel_id=1, source_target_pairs={{0,2},{1,3},{2,0},{3,1},{4,6},{5,7},{6,4},{7,5},{8,10},{9,11},{10,... | collective-permute-start | bytes 4718600 | tf_op jit(solution)/shard_map/ppermute | solution.py:377
  548.6 57.8 %collective-permute-start.50 = (bf16[512,1536]{1,0:T(8,128)(2,1)}, bf16[512,1536]{1,0:T(8,128)(2,1)}, u32[]{:S(2)}, u32[]{:S(2)}) collective-permute-start(bf16[512,1536]{1,0:T(8,128)(2,1)} %get-tuple-element.240), channel_id=1, source_target_pairs={{0,16},{16,0},{1,17},{17,1},{2,18},{18,2},{3,19},{19,3},{4,20},{20... | collective-permute-start | bytes 4718600 | tf_op jit(solution)/shard_map/ppermute | solution.py:373
  631.4 58.9 %collective-permute-start.53 = (bf16[512,1536]{1,0:T(8,128)(2,1)}, bf16[512,1536]{1,0:T(8,128)(2,1)}, u32[]{:S(2)}, u32[]{:S(2)}) collective-permute-start(bf16[512,1536]{1,0:T(8,128)(2,1)} %get-tuple-element.178), channel_id=1, source_target_pairs={{0,16},{16,0},{1,17},{17,1},{2,18},{18,2},{3,19},{19,3},{4,20},{20... | collective-permute-start | bytes 4718600 | tf_op jit(solution)/shard_map/ppermute | solution.py:373
  635.2 58.4 %collective-permute-start.54 = (bf16[2,2,4,48,1408]{4,3,2,1,0:T(8,128)(2,1)}, bf16[2,2,4,48,1408]{4,3,2,1,0:T(8,128)(2,1)}, u32[]{:S(2)}, u32[]{:S(2)}) collective-permute-start(bf16[2,2,4,48,1408]{4,3,2,1,0:T(8,128)(2,1)} %dynamic-slice_bitcast_fusion), channel_id=1, source_target_pairs={{0,1},{1,0},{2,3},{3,2},{4,5},{5,4},{6,7},{7,6},{8,9},{9,8},{10,11... | collective-permute-start | bytes 6488072 | tf_op jit(solution)/shard_map/ppermute | solution.py:377
  640.0 43.8 %collective-permute-start.51 = (bf16[256,1536]{1,0:T(8,128)(2,1)}, bf16[256,1536]{1,0:T(8,128)(2,1)}, u32[]{:S(2)}, u32[]{:S(2)}) collective-permute-start(bf16[256,1536]{1,0:T(8,128)(2,1)} %fusion.26), channel_id=1, source_target_pairs={{0,16},{16,0},{1,17},{17,1},{2,18},{18,2},{3,19},{19,3},{4,20},{20... | collective-permute-start | bytes 2359304 | tf_op jit(solution)/shard_map/ppermute | solution.py:373
  642.5 112.4 %collective-permute-start.59 = (bf16[1536,768]{1,0:T(8,128)(2,1)}, bf16[1536,768]{1,0:T(8,128)(2,1)}, u32[]{:S(2)}, u32[]{:S(2)}) collective-permute-start(bf16[1536,768]{1,0:T(8,128)(2,1)} %get-tuple-element.239), channel_id=1, source_target_pairs={{0,4},{1,5},{2,6},{3,7},{4,8},{5,9},{6,10},{7,11},{8,12},{9,13},{1... | collective-permute-start | bytes 7077896 | tf_op jit(solution)/shard_map/ppermute | solution.py:389
  648.4 106.5 %collective-permute-start.60 = (bf16[1536,768]{1,0:T(8,128)(2,1)}, bf16[1536,768]{1,0:T(8,128)(2,1)}, u32[]{:S(2)}, u32[]{:S(2)}) collective-permute-start(bf16[1536,768]{1,0:T(8,128)(2,1)} %get-tuple-element.238), channel_id=1, source_target_pairs={{4,0},{5,1},{6,2},{7,3},{8,4},{9,5},{10,6},{11,7},{12,8},{13,9},{1... | collective-permute-start | bytes 7077896 | tf_op jit(solution)/shard_map/ppermute | solution.py:393
  688.3 16.7 %collective-permute-start.52 = (bf16[256,1536]{1,0:T(8,128)(2,1)}, bf16[256,1536]{1,0:T(8,128)(2,1)}, u32[]{:S(2)}, u32[]{:S(2)}) collective-permute-start(bf16[256,1536]{1,0:T(8,128)(2,1)} %get-tuple-element.233), channel_id=1, source_target_pairs={{0,2},{1,3},{2,0},{3,1},{4,6},{5,7},{6,4},{7,5},{8,10},{9,11},{10,... | collective-permute-start | bytes 2359304 | tf_op jit(solution)/shard_map/ppermute | solution.py:377
  696.6 31.5 %collective-permute-start.55 = (bf16[2,4,48,1408]{3,2,1,0:T(8,128)(2,1)S(1)}, bf16[2,4,48,1408]{3,2,1,0:T(8,128)(2,1)S(1)}, u32[]{:S(2)}, u32[]{:S(2)}) collective-permute-start(bf16[2,4,48,1408]{3,2,1,0:T(8,128)(2,1)S(1)} %fusion.43), channel_id=1, source_target_pairs={{0,2},{1,3},{2,0},{3,1},{4,6},{5,7},{6,4},{7,5},{8,10},{9,11},{10,... | collective-permute-start | bytes 3244040 | tf_op jit(solution)/shard_map/ppermute | solution.py:377
  728.4 7.4 collective-permute-start.58
  731.5 23.3 %collective-permute-start.57 = (bf16[2,48,1408]{2,1,0:T(8,128)(2,1)S(1)}, bf16[2,48,1408]{2,1,0:T(8,128)(2,1)S(1)}, u32[]{:S(2)}, u32[]{:S(2)}) collective-permute-start(bf16[2,48,1408]{2,1,0:T(8,128)(2,1)S(1)} %get-tuple-element.257), channel_id=1, source_target_pairs={{0,8},{1,9},{2,10},{3,11},{4,12},{5,13},{6,14},{7,15},{8,0},{9,1},... | collective-permute-start | bytes 811016 | tf_op jit(solution)/shard_map/ppermute | solution.py:377
  731.5 23.3 %collective-permute-start.56 = (bf16[2,48,1408]{2,1,0:T(8,128)(2,1)S(1)}, bf16[2,48,1408]{2,1,0:T(8,128)(2,1)S(1)}, u32[]{:S(2)}, u32[]{:S(2)}) collective-permute-start(bf16[2,48,1408]{2,1,0:T(8,128)(2,1)S(1)} %get-tuple-element.255), channel_id=1, source_target_pairs={{0,4},{1,5},{2,6},{3,7},{4,0},{5,1},{6,2},{7,3},{8,12},{9,13},{10,... | collective-permute-start | bytes 811016 | tf_op jit(solution)/shard_map/ppermute | solution.py:377
  754.9 8.7 %collective-permute-start.61 = (bf16[48,1408]{1,0:T(8,128)(2,1)S(1)}, bf16[48,1408]{1,0:T(8,128)(2,1)S(1)}, u32[]{:S(2)}, u32[]{:S(2)}) collective-permute-start(bf16[48,1408]{1,0:T(8,128)(2,1)S(1)} %fusion.57), channel_id=1, source_target_pairs={{0,16},{16,0},{1,17},{17,1},{2,18},{18,2},{3,19},{19,3},{4,20},{20... | collective-permute-start | bytes 405512 | tf_op jit(solution)/shard_map/ppermute | solution.py:373
  758.9 31.2 %collective-permute-start.62 = (bf16[1536,512]{1,0:T(8,128)(2,1)S(1)}, bf16[1536,512]{1,0:T(8,128)(2,1)S(1)}, u32[]{:S(2)}, u32[]{:S(2)}) collective-permute-start(bf16[1536,512]{1,0:T(8,128)(2,1)S(1)} %pad_maximum_fusion.7), channel_id=1, source_target_pairs={{0,0},{1,16},{2,2},{3,18},{4,4},{5,20},{6,6},{7,22},{8,8},{9,24},{... | collective-permute-start | bytes 4718600 | tf_op jit(solution)/shard_map/ppermute | solution.py:1037
  763.6 19.3 %collective-permute-start.63 = (bf16[1536,256]{1,0:T(8,128)(2,1)S(1)}, bf16[1536,256]{1,0:T(8,128)(2,1)S(1)}, u32[]{:S(2)}, u32[]{:S(2)}) collective-permute-start(bf16[1536,256]{1,0:T(8,128)(2,1)S(1)} %get-tuple-element.252), channel_id=1, source_target_pairs={{1,0},{17,1},{3,2},{19,3},{5,4},{21,5},{7,6},{23,7},{9,8},{25,9},{... | collective-permute-start | bytes 2359304 | tf_op jit(solution)/shard_map/ppermute | solution.py:1037
  (75 other events, 1415.3 us)
Sparse Core Ops, SparseCore 0:
  16.3 58.9 all-gather.1
  541.7 108.2 reduce-scatter.1

commit v4 on v3

--- a/solution.py
+++ b/solution.py
@@ -463,23 +463,15 @@
     return values * cos - swapped * sin
 
 
-def place_shards(place_ref, own_ref, other_ref, shard, store):
-    for core in range(2):
-        source = other_ref if core else own_ref
-        for row in range(2):
-            for line in range(LINE):
-                index = (place_ref[0] ^ line) * 4 + (place_ref[1] ^ row) * 2 + (place_ref[2] ^ core)
-                store(source, (row * LINE + line) * shard, pl.multiple_of(index * shard, shard))
-
-
 def qkv_kernel(x_ref, gain_ref, w_ref, cos_ref, sin_ref, h_ref, q_ref, k_ref, v_ref):
     value = x_ref[...].astype(F32)
     scale = lax.rsqrt(jnp.mean(value * value, axis=-1, keepdims=True) + EPSILON)
     normed = (value * scale * gain_ref[...]).astype(BF16)
     h_ref[...] = normed
-    both = jnp.dot(normed, w_ref[...], preferred_element_type=F32)
     q_width, kv_heads = q_ref.shape[1], k_ref.shape[0]
     kv_width = kv_heads * HDIM
+    weights = w_ref[:, : q_width + 2 * kv_width]
+    both = jnp.dot(normed, weights, preferred_element_type=F32)
     spun = turned(both[:, : q_width + kv_width], cos_ref[...], sin_ref[...], 1)
     q_ref[...] = (spun[:, :q_width] * SCORE_SCALE).astype(BF16)
     for head in range(kv_heads):
@@ -504,7 +496,7 @@
         in_specs=[
             row_block(width),
             pl.BlockSpec((1, width), lambda i: (0, 0)),
-            pl.BlockSpec((width, columns), lambda i: (0, 0)),
+            pl.BlockSpec((width, width), lambda i: (0, 1)),
             row_block(cos.shape[1]),
             row_block(cos.shape[1]),
         ],
@@ -525,31 +517,24 @@
     )(x_sorted, gain, weights, cos, sin)
 
 
-def mix_kernel(
-    place_ref, mine_ref, theirs_ref, x_ref, gain_ref, own_ref, other_ref, m_ref, h_ref, w_ref
-):
-    shard = own_ref.shape[0] // (4 * LINE)
-    half = w_ref.shape[1]
+def mix_kernel(place_ref, mine_ref, theirs_ref, x_ref, gain_ref, w_ref, m_ref, h_ref, parts_ref):
+    half = parts_ref.shape[1]
 
     @pl.when(pl.program_id(0) == 0)
     def _():
-        for seq in range(2):
-
-            def store(source, low, place):
-                low = low + seq * 2 * LINE * shard
-                w_ref[seq, pl.ds(place, shard), :] = source[low : low + shard, :]
-
-            place_shards(place_ref, own_ref, other_ref, shard, store)
-
-    mixed = jnp.dot(mine_ref[...], w_ref[0], preferred_element_type=F32)
-    mixed = mixed + jnp.dot(theirs_ref[...], w_ref[1], preferred_element_type=F32)
+        for part in range(2):
+            low = pl.multiple_of((place_ref[0] ^ part) * half, half)
+            parts_ref[part] = w_ref[pl.ds(low, half), :]
+
+    mixed = jnp.dot(mine_ref[...], parts_ref[0], preferred_element_type=F32)
+    mixed = mixed + jnp.dot(theirs_ref[...], parts_ref[1], preferred_element_type=F32)
     value = x_ref[...].astype(F32) + BRANCH_SCALE * mixed
     m_ref[...] = value
     scale = lax.rsqrt(jnp.mean(value * value, axis=-1, keepdims=True) + EPSILON)
-    h_ref[...] = (value * scale * gain_ref[1:2, :]).astype(BF16)
-
-
-def mix(places, mine, theirs, tokens, gains, own, other):
+    h_ref[...] = (value * scale * gain_ref[...]).astype(BF16)
+
+
+def mix(place, mine, theirs, tokens, gain, weights):
     rows, width = tokens.shape
     half = mine.shape[1]
     tile = 256
@@ -566,8 +551,8 @@
             num_scalar_prefetch=1,
             grid=(rows // tile,),
             in_specs=[
-                row_block(half), row_block(half), row_block(width), whole(gains.shape),
-                whole(own.shape), whole(other.shape),
+                row_block(half), row_block(half), row_block(width), whole(gain.shape),
+                whole((width, width)),
             ],
             out_specs=[row_block(width), row_block(width), whole((2, half, width))],
         ),
@@ -581,7 +566,7 @@
             flops=rows * width * width // 8, bytes_accessed=rows * width, transcendentals=rows
         ),
         name="mix",
-    )(places, mine, theirs, tokens, gains, own, other)
+    )(place, mine, theirs, tokens, gain, weights)
 
 
 def token_grad_kernel(dq_ref, dk_ref, dv_ref, w_ref, own_ref, other_ref, mine_ref, sent_ref):
@@ -611,7 +596,7 @@
         token_grad_kernel,
         grid=(3,),
         in_specs=[whole(grad) for grad in grads]
-        + [pl.BlockSpec((tile, columns), lambda i: (i, 0)), whole(own_places), whole(other_places)],
+        + [pl.BlockSpec((tile, width), lambda i: (i, 1)), whole(own_places), whole(other_places)],
         out_specs=[block, block],
         out_shape=[jax.ShapeDtypeStruct((count, width), BF16)] * 2,
         compiler_params=pltpu.CompilerParams(vmem_limit_bytes=VMEM_BYTES),
@@ -1049,14 +1034,17 @@
     first_core = core == 0
 
     projections = (w_query, w_key, w_value)
-    gain_columns = jnp.pad(jnp.stack([gain_attn, gain_ffn], axis=1), ((0, 0), (0, PAD - 2)))
-    mine = jnp.concatenate([half_of(w, seq) for w in projections] + [gain_columns], axis=1)
-    theirs = jnp.concatenate([half_of(w, 1 - seq) for w in projections] + [gain_columns], axis=1)
+    qkv_width = q_width + 2 * kv_width
+    gain_columns = jnp.pad(
+        jnp.stack([gain_attn, gain_ffn], axis=1), ((0, 0), (0, width - qkv_width - 2))
+    )
+    mine, theirs = [
+        jnp.concatenate([w_output] + [half_of(w, which) for w in projections] + [gain_columns], axis=1)
+        for which in (seq, 1 - seq)
+    ]
     theirs = swap_seq(theirs)
-    qkv_width = q_width + 2 * kv_width
     pair = jnp.stack([jnp.where(first_seq, mine, theirs), jnp.where(first_seq, theirs, mine)])
-    w_qkv = lax.all_gather(pair, "dp", axis=1, tiled=True).reshape(width, qkv_width + PAD)
-    places_of = jnp.stack([line, row_of, core]).astype(jnp.int32)
+    gathered = lax.all_gather(pair, "dp", axis=1, tiled=True).reshape(width, 2 * width)
 
     in_own = w_in[0]
     half = in_own.shape[1] // 2
@@ -1075,14 +1063,6 @@
     )
     other_tokens = swap_seq(after(tokens, own_part))
     up_one, down_one = line_up(own_part), line_down(own_part)
-    output_rows = jnp.concatenate(
-        [w_output] + [swap_dp(w_output, 4 * step) for step in range(1, LINE)], axis=0
-    )
-    output_rows = jnp.concatenate([output_rows, swap_y(output_rows)], axis=0)
-    output_rows = after(output_rows, other_tokens)
-    output_rows = jnp.concatenate([output_rows, swap_seq(output_rows)], axis=0)
-    output_others = swap_core(output_rows)
-
     experts_all = 4 * LINE
     gates = jax.nn.softmax(logits, axis=-1)
     named = routes[:, :, None] == jnp.arange(experts_all, dtype=jnp.int32)[None, None, :]
@@ -1132,10 +1112,10 @@
     x_sorted = to_order(tokens, other_tokens)
     x_sorted, up_one, down_one = lax.optimization_barrier((x_sorted, up_one, down_one))
     up_two, down_two = line_up(up_one), line_down(down_one)
-    gains = w_qkv[:, qkv_width : qkv_width + 2].astype(F32).T
+    gains = gathered[:, width + qkv_width : width + qkv_width + 2].astype(F32).T
     gain_one, gain_two = gains[0], gains[1]
     normed, query, keys, values = project(
-        x_sorted, gain_one[None, :], w_qkv, cos, sin, q_width, kv_heads
+        x_sorted, gain_one[None, :], gathered, cos, sin, q_width, kv_heads
     )
     pairs = q_width // (2 * HDIM)
     first_pairs = (pairs + 1) // 2
@@ -1155,7 +1135,7 @@
     up_three, down_three = line_up(up_two), line_down(down_two)
     inputs = tokens.astype(F32)
     middle, normed_ffn, output_parts = mix(
-        places_of, mixed_mine, mixed_theirs, tokens, gains, output_rows, output_others
+        seq.astype(jnp.int32)[None], mixed_mine, mixed_theirs, tokens, gain_two[None, :], gathered
     )
     normed_ffn = after(normed_ffn, *grad_far)
     row_near = near_pieces(normed_ffn, normed_ffn)
@@ -1248,7 +1228,7 @@
     wide = qkv_grad(normed, grads_qkv, grad_gain_two[None, :], shard)
     grads_late = after(grads_qkv, wide)
     grad_normed, sent_normed = token_grad(
-        grads_late, w_qkv, own_places[:, None], other_places[:, None]
+        grads_late, gathered, own_places[:, None], other_places[:, None]
     )
     grad_normed = grad_normed.astype(F32) + swap_seq(sent_normed).astype(F32)
     scale = lax.rsqrt(jnp.mean(inputs * inputs, axis=-1, keepdims=True) + EPSILON)
@@ -1268,21 +1248,23 @@
     kept = kept + swap_core(chosen(wide, 1 - core, 0)).astype(F32)
     next_kept = chosen(kept, row_of, 0)
     next_kept = next_kept + swap_y(chosen(kept, 1 - row_of, 0).astype(BF16)).astype(F32)
-    summed = chosen(next_kept, line, 1)
-    sent_lines = [
-        swap_dp(chosen(next_kept, line ^ step, 1).astype(BF16), 4 * step) for step in range(1, LINE)
-    ]
-    summed = summed + sum(value.astype(F32) for value in sent_lines)
-    summed, last_line = lax.optimization_barrier((summed, last_line))
+    next_kept, last_line = lax.optimization_barrier((next_kept, last_line))
     part_grads = (
         line_partial(*range(LINE)) + last_line[0].astype(F32) + last_line[1].astype(F32)
     ).astype(BF16)
     same_grads = jnp.where(first_core, part_grads[:, :half], part_grads[:, half : 2 * half])
     cross_grads = jnp.where(first_core, part_grads[:, half : 2 * half], part_grads[:, :half])
     same_grads = jnp.concatenate([same_grads, part_grads[:, 2 * half :]], axis=1)
+    next_kept, same_grads, cross_grads = lax.optimization_barrier(
+        (next_kept, same_grads, cross_grads)
+    )
     same = both_axes(same_grads, straight)
     cross = both_axes(cross_grads, crossed_back)
-
+    sent_lines = [
+        swap_dp(chosen(next_kept, line ^ step, 1).astype(BF16), 4 * step) for step in range(1, LINE)
+    ]
+    summed = chosen(next_kept, line, 1) + sum(value.astype(F32) for value in sent_lines)
+    summed, same, cross = lax.optimization_barrier((summed, same, cross))
     grad_w_in = ordered(same[:, :half], cross, 1)
     grad_w_out = same[:, half:].T
     kept_rows = chosen(summed, seq, 0)

time: 811 us -> 769 us (0.948)
  waiting for transfers between devices: 229 us -> 217 us
  other arithmetic: 96.7 us -> 86.2 us
  local copies, waits for them, and re-layouts: 46 us -> 35.9 us
    ppermute x32 -> x27, waiting for transfers between devices: 107 us -> 31.2 us  [swap_dp(): return lax.ppermute(value, 'dp', [(i, i ^ mask) for i in range(4 * LINE)])]
    ppermute x6, waiting for transfers between devices: 0.07 us -> 53.9 us  [line_up(): return lax.ppermute(value, 'dp', [(i, i + 4) for i in range(4 * LINE - 4)])]
    ppermute x32 -> x27, starting transfers between devices: 38.5 us -> 28.2 us  [swap_dp(): return lax.ppermute(value, 'dp', [(i, i ^ mask) for i in range(4 * LINE)])]
    ppermute x16 -> x15, starting transfers between devices: 11.9 us -> 18.8 us  [swap_seq(): return lax.ppermute(value, 'seq', [(0, 1), (1, 0)])]
    ppermute x16 -> x15, waiting for transfers between devices: 89.6 us -> 88.5 us  [swap_seq(): return lax.ppermute(value, 'seq', [(0, 1), (1, 0)])]
  transfers between devices with their start and end apart: 66 -> 60, of which waited for: 19 -> 19; matrix products, arithmetic and copies ran while one was open for 28% -> 25% of each run, Pallas kernels for 21% -> 22%
where the time goes in v4:
time: 769 us; the launch traced here: 759 us
  Pallas kernels  225 us (29%)
  waiting for transfers between devices  217 us (28%)
  starting transfers between devices  97.1 us (13%)
  other arithmetic  86.2 us (11%)
  matrix products  82.5 us (11%)
  local copies, waits for them, and re-layouts  35.9 us (5%)
  between operations  15.9 us (2%)
    pallas_call x2, Pallas kernels, run_experts(): pl.pallas_call(functools.partial(experts_kernel, tiles, tile // 2), grid_...  109 us
    ppermute x15, waiting for transfers between devices, swap_seq(): return lax.ppermute(value, 'seq', [(0, 1), (1, 0)])  88.5 us
    dot_general x15, matrix products, contract(): lax.dot_general(left, right, (((left_dim,), (right_dim,)), ((), ())), pre...  82.5 us
    ppermute x6, waiting for transfers between devices, line_up(): return lax.ppermute(value, 'dp', [(i, i + 4) for i in range(4 * LINE - 4)])  53.9 us
    pallas_call x1, Pallas kernels, attend_back(): pl.pallas_call(attend_back_kernel, grid=(pairs,), in_specs=[pair_block, w...  45.6 us
    ppermute x4, waiting for transfers between devices, both_axes(): return lax.ppermute(value, ('seq', 'dp'), pairs)  35.4 us
    ppermute x27, waiting for transfers between devices, swap_dp(): return lax.ppermute(value, 'dp', [(i, i ^ mask) for i in range(4 * LINE)])  31.2 us
    ppermute x6, starting transfers between devices, line_up(): return lax.ppermute(value, 'dp', [(i, i + 4) for i in range(4 * LINE - 4)])  30.8 us
  transfers between devices with their start and end apart: 60, of which 19 were waited for; matrix products, arithmetic and copies ran while one was open for 25% of the time, Pallas kernels for 22%

profile of v4, /device:TPU:1, one launch (start us, length us, event | category | flops | bytes accessed | tf_op | source)
XLA Modules:
  0.0 759.0 jit_solution(12823313779977328534)
XLA Ops:
  14.6 6.7 collective-permute-done.5
  23.7 4.5 collective-permute-start
  28.3 25.8 %collective-permute-done.1 = bf16[1536,256]{1,0:T(8,128)(2,1)} collective-permute-done((bf16[1536,256]{1,0:T(8,128)(2,1)}, bf16[1536,256]{1,0:T(8,128)(2,1)}, u32[]{:S(2)}, u32[]{:S(2)}) %collective-permute-start.1) | collective-permute-done | bytes 786464 | tf_op jit(solution)/shard_map/ppermute | solution.py:1022
  57.0 4.9 collective-permute-start.3
  68.2 3.3 concatenate.88.refs_6_
  75.9 23.4 %collective-permute-done.2 = bf16[512,1536]{1,0:T(8,128)(2,1)} collective-permute-done((bf16[512,1536]{1,0:T(8,128)(2,1)S(1)}, bf16[512,1536]{1,0:T(8,128)(2,1)}, u32[]{:S(2)}, u32[]{:S(2)}) %collective-permute-start.2) | collective-permute-done | bytes 1572896 | tf_op jit(solution)/shard_map/ppermute | solution.py:373
  99.3 2.3 collective-permute-start.6
  101.6 5.2 add_convert_fusion.2.x_ref
  106.8 41.5 %collective-permute-done.3.refs_18_.refs_14_ = bf16[1536,768]{1,0:T(8,128)(2,1)} collective-permute-done((bf16[1536,768]{1,0:T(8,128)(2,1)}, bf16[1536,768]{1,0:T(8,128)(2,1)}, u32[]{:S(2)}, u32[]{:S(2)}) %collective-permute-start.3) | collective-permute-done | bytes 2359328 | tf_op jit(solution)/shard_map/ppermute | solution.py:389
  148.3 2.6 collective-permute-done.4.refs_20_.refs_16_
  150.9 4.2 collective-permute-start.10
  163.2 10.5 %project.1 = (bf16[1024,1536]{1,0:T(8,128)(2,1)}, bf16[1024,768]{1,0:T(8,128)(2,1)}, bf16[4,1024,64]{2,1,0:T(8,128)(2,1)}, bf16[4,1024,64]{2,1,0:T(8,128)(2,1)}) custom-call(bf16[1024,1536]{1,0:T(8,128)(2,1)} %add_convert_fusion.2.x_ref, f32[1,1536]{1,0:T(1,128)} %copy.93.gain_ref, bf16[1536,3072]{1,0:T(8,128)(2,1)} %bitcast.85, ...), custom_call_target="tpu_custom_call" | custom-call | flops 251658240 | bytes 3538944 | tf_op jit(solution)/shard_map/project/pallas_call | solution.py:493
  173.8 15.0 %attend.2 = bf16[1024,384]{1,0:T(8,128)(2,1)} custom-call(bf16[1024,768]{1,0:T(8,128)(2,1)} %get-tuple-element.113.q_ref, bf16[4,1024,64]{2,1,0:T(8,128)(2,1)} %get-tuple-element.110.k_ref, bf16[4,1024,64]{2,1,0:T(8,128)(2,1)} %get-tuple-element.111.v_ref, s32[1024,1]{1,0:T(8,128)} %copy.94.start_ref), custom_call_target="tpu_custom_call" | custom-call | flops 113246208 | bytes 3145728 | tf_op jit(solution)/shard_map/attend/pallas_call | solution.py:667
  188.8 15.6 %attend.3 = bf16[1024,384]{1,0:T(8,128)(2,1)} custom-call(bf16[1024,768]{1,0:T(8,128)(2,1)} %get-tuple-element.113.q_ref, bf16[4,1024,64]{2,1,0:T(8,128)(2,1)} %get-tuple-element.110.k_ref, bf16[4,1024,64]{2,1,0:T(8,128)(2,1)} %get-tuple-element.111.v_ref, s32[1024,1]{1,0:T(8,128)} %copy.94.start_ref), custom_call_target="tpu_custom_call" | custom-call | flops 113246208 | bytes 3145728 | tf_op jit(solution)/shard_map/attend/pallas_call | solution.py:667
  213.3 2.8 collective-permute-done.9
  218.2 6.5 collective-permute-done.8
  224.8 5.1 collective-permute-start.26
  237.7 9.2 %mix.1 = (f32[512,1536]{1,0:T(8,128)}, bf16[512,1536]{1,0:T(8,128)(2,1)}, bf16[2,768,1536]{2,1,0:T(8,128)(2,1)}) custom-call(s32[1]{0:T(128)} %bitcast.place_ref, bf16[512,768]{1,0:T(8,128)(2,1)} %get-tuple-element.277.mine_ref, bf16[512,768]{1,0:T(8,128)(2,1)} %copy-done.33, bf16[512,1536]{1,0:T(8,128)(2,1)} %x_ref.1, f32[1,1536]{1,0:T(1,128)} %copy.101.gain_ref, ...), custom_call_target="tpu_custom_call" | custom-call | flops 150994944 | bytes 786432 | tf_op jit(solution)/shard_map/mix/pallas_call | solution.py:548
  250.2 29.6 %collective-permute-done.14.refs_0_.refs_1_ = bf16[512,1536]{1,0:T(8,128)(2,1)S(1)} collective-permute-done((bf16[512,1536]{1,0:T(8,128)(2,1)}, bf16[512,1536]{1,0:T(8,128)(2,1)S(1)}, u32[]{:S(2)}, u32[]{:S(2)}) %collective-permute-start.14) | collective-permute-done | bytes 1572896 | tf_op jit(solution)/shard_map/ppermute | solution.py:373
  284.3 6.0 collective-permute-start.24
  290.9 8.6 %collective-permute-done.16.refs_2_ = bf16[256,1536]{1,0:T(8,128)(2,1)S(1)} collective-permute-done((bf16[256,1536]{1,0:T(8,128)(2,1)S(1)}, bf16[256,1536]{1,0:T(8,128)(2,1)S(1)}, u32[]{:S(2)}, u32[]{:S(2)}) %collective-permute-start.16) | collective-permute-done | bytes 786464 | tf_op jit(solution)/shard_map/ppermute | solution.py:377
  299.5 3.3 collective-permute-start.23
  304.6 3.0 collective-permute-done.25.refs_15_
  308.8 2.6 select_select_fusion
  313.5 54.5 %experts.2 = (bf16[1024,1536]{1,0:T(8,128)(2,1)}, bf16[1024,1536]{1,0:T(8,128)(2,1)}, bf16[1024,1536]{1,0:T(8,128)(2,1)}, bf16[1024,1536]{1,0:T(8,128)(2,1)}, bf...) custom-call(s32[1]{0:T(128)} %bitcast.16.place_ref, ...), custom_call_target="tpu_custom_call" | custom-call | flops 2415919104 | bytes 50331648 | tf_op jit(solution)/shard_map/experts/pallas_call | solution.py:904
  368.9 8.2 %collective-permute-done.28 = bf16[1024,1536]{1,0:T(8,128)(2,1)S(1)} collective-permute-done((bf16[1024,1536]{1,0:T(8,128)(2,1)}, bf16[1024,1536]{1,0:T(8,128)(2,1)S(1)}, u32[]{:S(2)}, u32[]{:S(2)}) %collective-permute-start.28) | collective-permute-done | bytes 3145760 | tf_op jit(solution)/shard_map/ppermute | solution.py:377
  377.1 2.7 add_convert_fusion.1
  383.2 54.5 %experts.3 = (bf16[1024,1536]{1,0:T(8,128)(2,1)}, bf16[1024,1536]{1,0:T(8,128)(2,1)}, bf16[1024,1536]{1,0:T(8,128)(2,1)}, bf16[1024,1536]{1,0:T(8,128)(2,1)}, bf...) custom-call(s32[1]{0:T(128)} %bitcast.16.place_ref, ...), custom_call_target="tpu_custom_call", output_to_operand_aliasing={{4}: (21, {}), {5}: (22, {}), {6}: (23, {}), {7}: (24, {}),... | custom-call | flops 2415919104 | bytes 50331648 | tf_op jit(solution)/shard_map/experts/pallas_call | solution.py:904
  438.7 11.3 %fusion.9 = bf16[1536,512]{1,0:T(8,128)(2,1)S(1)} fusion(bf16[4096,1536]{1,0:T(8,128)(2,1)} %get-tuple-element.155, bf16[4096,512]{1,0:T(8,128)(2,1)} %get-tuple-element.148), kind=kOutput, calls=%fused_computation.36 | convolution fusion | flops 6444023808 | bytes 18350080 | tf_op jit(solution)/shard_map/dot_general | solution.py:628
  450.1 16.8 %convolution_convert_fusion.2 = bf16[1536,1024]{1,0:T(8,128)(2,1)S(1)} fusion(bf16[4096,1536]{1,0:T(8,128)(2,1)S(1)} %copy-done.28, bf16[4096,1024]{1,0:T(8,128)(2,1)} %get-tuple-element.146), kind=kOutput, calls=%fused_computation.15 | convolution fusion | flops 12886474752 | bytes 24117248 | tf_op jit(solution)/shard_map/dot_general | solution.py:628
  468.9 5.4 collective-permute-start.38
  477.4 2.9 convert_add_fusion.1
  480.2 3.1 fusion.29
  484.7 16.6 %convolution_convert_fusion.1 = bf16[1536,1024]{1,0:T(8,128)(2,1)S(1)} fusion(bf16[4096,1536]{1,0:T(8,128)(2,1)S(1)} %copy-done.28, bf16[4096,1024]{1,0:T(8,128)(2,1)} %get-tuple-element.154), kind=kOutput, calls=%fused_computation.14 | convolution fusion | flops 12886474752 | bytes 24117248 | tf_op jit(solution)/shard_map/dot_general | solution.py:628
  501.3 11.1 %fusion.10 = bf16[1536,512]{1,0:T(8,128)(2,1)S(1)} fusion(bf16[4096,1536]{1,0:T(8,128)(2,1)} %get-tuple-element.155, bf16[4096,512]{1,0:T(8,128)(2,1)} %get-tuple-element.156), kind=kOutput, calls=%fused_computation.37 | convolution fusion | flops 6444023808 | bytes 18350080 | tf_op jit(solution)/shard_map/dot_general | solution.py:628
  517.5 2.4 fusion.33
  521.3 2.3 fusion.36
  524.4 3.2 add_convert_fusion.7
  527.6 5.6 collective-permute-start.41
  533.3 3.3 add_convert_fusion.6
  538.5 4.4 convolution_convert_fusion
  542.9 3.7 add_convert_fusion
  551.8 3.4 add_convert_fusion.8.d_ref
  555.3 45.6 %attend_back.1 = (bf16[1024,768]{1,0:T(8,128)(2,1)}, bf16[1024,256]{1,0:T(8,128)(2,1)}, bf16[1024,256]{1,0:T(8,128)(2,1)}) custom-call(bf16[1024,768]{1,0:T(8,128)(2,1)} %get-tuple-element.113.q_ref, bf16[4,1024,64]{2,1,0:T(8,128)(2,1)} %get-tuple-element.110.k_ref, bf16[4,1024,64]{2,1,0:T(8,128)(2,1)} %get-tuple-element.111.v_ref, ...), custom_call_target="tpu_custom_call" | custom-call | flops 566231040 | bytes 6291456 | tf_op jit(solution)/shard_map/attend_back/pallas_call | solution.py:735
  601.0 3.9 convert_add_fusion
  605.0 3.1 fusion.26
  609.8 5.2 add_convert_fusion.4
  615.0 8.5 %qkv_grad.1 = bf16[2,2,2,4,48,1408]{5,4,3,2,1,0:T(8,128)(2,1)} custom-call(bf16[1024,1536]{1,0:T(8,128)(2,1)} %get-tuple-element.177.h_ref, bf16[1024,768]{1,0:T(8,128)(2,1)} %get-tuple-element.178.dq_ref, bf16[1024,256]{1,0:T(8,128)(2,1)} %get-tuple-element.179.dk_ref, bf16[1024,256]{1,0:T(8,128)(2,1)} %get-tuple-element.180.dv_ref, ...), custom_call_target="tpu_custom_call" | custom-call | flops 251658240 | bytes 1572864 | tf_op jit(solution)/shard_map/qkv_grad/pallas_call | solution.py:956
  623.6 3.1 dynamic-slice_bitcast_fusion
  628.3 4.5 fusion.27
  636.4 11.1 %token_grad.1 = (bf16[512,1536]{1,0:T(8,128)(2,1)}, bf16[512,1536]{1,0:T(8,128)(2,1)}) custom-call(bf16[1024,768]{1,0:T(8,128)(2,1)} %get-tuple-element.178.dq_ref, bf16[1024,256]{1,0:T(8,128)(2,1)} %get-tuple-element.179.dk_ref, bf16[1024,256]{1,0:T(8,128)(2,1)} %get-tuple-element.180.dv_ref, bf16[1536,3072]{1,0:T(8,128)(2,1)} %bitcast.87, ...), custom_call_target="tpu_custom_call" | custom-call | flops 251658240 | bytes 1572864 | tf_op jit(solution)/shard_map/token_grad/pallas_call | solution.py:595
  648.2 5.6 collective-permute-start.50
  658.9 2.8 convert_add_fusion.2
  662.9 18.5 %collective-permute-done.47 = bf16[512,1536]{1,0:T(8,128)(2,1)} collective-permute-done((bf16[512,1536]{1,0:T(8,128)(2,1)}, bf16[512,1536]{1,0:T(8,128)(2,1)}, u32[]{:S(2)}, u32[]{:S(2)}) %collective-permute-start.47) | collective-permute-done | bytes 1572896 | tf_op jit(solution)/shard_map/ppermute | solution.py:373
  681.3 2.5 fusion.2
  683.9 4.3 fusion.5
  688.5 12.4 %collective-permute-done.50 = bf16[1536,768]{1,0:T(8,128)(2,1)} collective-permute-done((bf16[1536,768]{1,0:T(8,128)(2,1)}, bf16[1536,768]{1,0:T(8,128)(2,1)}, u32[]{:S(2)}, u32[]{:S(2)}) %collective-permute-start.50) | collective-permute-done | bytes 2359328 | tf_op jit(solution)/shard_map/ppermute | solution.py:389
  700.8 5.2 collective-permute-done.51
  706.1 3.5 add_convert_fusion.3
  710.0 6.4 collective-permute-start.55
  717.1 3.1 collective-permute-start.52
  722.1 11.1 %collective-permute-done.53 = bf16[2,48,1408]{2,1,0:T(8,128)(2,1)S(1)} collective-permute-done((bf16[2,48,1408]{2,1,0:T(8,128)(2,1)S(1)}, bf16[2,48,1408]{2,1,0:T(8,128)(2,1)S(1)}, u32[]{:S(2)}, u32[]{:S(2)}) %collective-permute-start.53) | collective-permute-done | bytes 270368 | tf_op jit(solution)/shard_map/ppermute | solution.py:377
  733.3 6.3 collective-permute-done.56
  739.6 3.4 collective-permute-done.55
  (326 shorter events, 115.3 us)
Async XLA Ops:
  7.2 153.0 %all-gather.2.cloned.1.call-start = ((), (), s32[]{:S(2)}) async-start(), calls=%async_computation.1 | async-start | bytes 10027008 | tf_op jit(solution)/shard_map/all_gather | solution.py:1047
  12.5 8.8 %collective-permute-start.5 = (bf16[48,3072]{1,0:T(8,128)(2,1)S(1)}, bf16[48,3072]{1,0:T(8,128)(2,1)S(1)}, u32[]{:S(2)}, u32[]{:S(2)}) collective-permute-start(bf16[48,3072]{1,0:T(8,128)(2,1)S(1)} %get-tuple-element.295), channel_id=1, source_target_pairs={{0,16},{16,0},{1,17},{17,1},{2,18},{18,2},{3,19},{19,3},{4,20},{20... | collective-permute-start | bytes 884744 | tf_op jit(solution)/shard_map/ppermute | solution.py:373
  22.3 632.8 %reduce-scatter.2.cloned.1.call-start = ((), (), s32[]{:S(2)}) async-start(), calls=%async_computation.2 | async-start | bytes 4866048 | tf_op jit(solution)/shard_map/reduce_scatter | solution.py:1240
  23.7 30.4 %collective-permute-start = (bf16[1536,512]{1,0:T(8,128)(2,1)S(1)}, bf16[1536,512]{1,0:T(8,128)(2,1)S(1)}, u32[]{:S(2)}, u32[]{:S(2)}) collective-permute-start(bf16[1536,512]{1,0:T(8,128)(2,1)S(1)} %pad_maximum_fusion.6), channel_id=1, source_target_pairs={{0,0},{1,16},{2,2},{3,18},{4,4},{5,20},{6,6},{7,22},{8,8},{9,24},{... | collective-permute-start | bytes 4718600 | tf_op jit(solution)/shard_map/ppermute | solution.py:1022
  28.2 25.9 %collective-permute-start.1 = (bf16[1536,256]{1,0:T(8,128)(2,1)}, bf16[1536,256]{1,0:T(8,128)(2,1)}, u32[]{:S(2)}, u32[]{:S(2)}) collective-permute-start(bf16[1536,256]{1,0:T(8,128)(2,1)} %get-tuple-element.273), channel_id=1, source_target_pairs={{0,1},{1,17},{2,3},{3,19},{4,5},{5,21},{6,7},{7,23},{8,9},{9,25},{... | collective-permute-start | bytes 2359304 | tf_op jit(solution)/shard_map/ppermute | solution.py:1022
  57.0 91.3 %collective-permute-start.3 = (bf16[1536,768]{1,0:T(8,128)(2,1)}, bf16[1536,768]{1,0:T(8,128)(2,1)}, u32[]{:S(2)}, u32[]{:S(2)}) collective-permute-start(bf16[1536,768]{1,0:T(8,128)(2,1)} %pad_maximum_fusion.1.refs_19_.refs_15_), channel_id=1, source_target_pairs={{0,4},{1,5},{2,6},{3,7},{4,8},{5,9},{6,10},{7,11},{8,12},{9,13},{1... | collective-permute-start | bytes 7077896 | tf_op jit(solution)/shard_map/ppermute | solution.py:389
  61.9 89.0 %collective-permute-start.4 = (bf16[1536,768]{1,0:T(8,128)(2,1)}, bf16[1536,768]{1,0:T(8,128)(2,1)}, u32[]{:S(2)}, u32[]{:S(2)}) collective-permute-start(bf16[1536,768]{1,0:T(8,128)(2,1)} %pad_maximum_fusion.1.refs_19_.refs_15_), channel_id=1, source_target_pairs={{4,0},{5,1},{6,2},{7,3},{8,4},{9,5},{10,6},{11,7},{12,8},{13,9},{1... | collective-permute-start | bytes 7077896 | tf_op jit(solution)/shard_map/ppermute | solution.py:393
  63.2 36.1 %collective-permute-start.2 = (bf16[512,1536]{1,0:T(8,128)(2,1)S(1)}, bf16[512,1536]{1,0:T(8,128)(2,1)}, u32[]{:S(2)}, u32[]{:S(2)}) collective-permute-start(bf16[512,1536]{1,0:T(8,128)(2,1)S(1)} %copy-done.14), channel_id=1, source_target_pairs={{0,16},{16,0},{1,17},{17,1},{2,18},{18,2},{3,19},{19,3},{4,20},{20... | collective-permute-start | bytes 4718600 | tf_op jit(solution)/shard_map/ppermute | solution.py:373
  71.5 117.3 %collective-permute-start.7 = (bf16[512,1664]{1,0:T(8,128)(2,1)}, bf16[512,1664]{1,0:T(8,128)(2,1)S(1)}, u32[]{:S(2)}, u32[]{:S(2)}) collective-permute-start(bf16[512,1664]{1,0:T(8,128)(2,1)} %concatenate.88.refs_6_), channel_id=1, source_target_pairs={{0,2},{1,3},{2,0},{3,1},{4,6},{5,7},{6,4},{7,5},{8,10},{9,11},{10,... | collective-permute-start | bytes 5111816 | tf_op jit(solution)/shard_map/ppermute | solution.py:377
  99.3 89.5 %collective-permute-start.6 = (bf16[512,1664]{1,0:T(8,128)(2,1)}, bf16[512,1664]{1,0:T(8,128)(2,1)}, u32[]{:S(2)}, u32[]{:S(2)}) collective-permute-start(bf16[512,1664]{1,0:T(8,128)(2,1)} %concatenate.88.refs_6_), channel_id=1, source_target_pairs={{0,16},{16,0},{1,17},{17,1},{2,18},{18,2},{3,19},{19,3},{4,20},{20... | collective-permute-start | bytes 5111816 | tf_op jit(solution)/shard_map/ppermute | solution.py:373
  150.9 73.8 %collective-permute-start.10 = (bf16[1536,768]{1,0:T(8,128)(2,1)}, bf16[1536,768]{1,0:T(8,128)(2,1)}, u32[]{:S(2)}, u32[]{:S(2)}) collective-permute-start(bf16[1536,768]{1,0:T(8,128)(2,1)} %collective-permute-done.3.refs_18_.refs_14_), channel_id=1, source_target_pairs={{0,4},{1,5},{2,6},{3,7},{4,8},{5,9},{6,10},{7,11},{8,12},{9,13},{1... | collective-permute-start | bytes 7077896 | tf_op jit(solution)/shard_map/ppermute | solution.py:389
  155.2 69.6 %collective-permute-start.11 = (bf16[1536,768]{1,0:T(8,128)(2,1)}, bf16[1536,768]{1,0:T(8,128)(2,1)}, u32[]{:S(2)}, u32[]{:S(2)}) collective-permute-start(bf16[1536,768]{1,0:T(8,128)(2,1)} %collective-permute-done.4.refs_20_.refs_16_), channel_id=1, source_target_pairs={{4,0},{5,1},{6,2},{7,3},{8,4},{9,5},{10,6},{11,7},{12,8},{13,9},{1... | collective-permute-start | bytes 7077896 | tf_op jit(solution)/shard_map/ppermute | solution.py:393
  188.8 110.7 %copy-start.31 = (bf16[512,1664]{1,0:T(8,128)(2,1)}, bf16[512,1664]{1,0:T(8,128)(2,1)S(1)}, u32[]{:S(2)}) copy-start(bf16[512,1664]{1,0:T(8,128)(2,1)S(1)} %collective-permute-done.7.refs_9_.refs_8_) | copy-start | bytes 5111812
  206.4 9.7 %collective-permute-start.9 = (bf16[512,384]{1,0:T(8,128)(2,1)S(1)}, bf16[512,384]{1,0:T(8,128)(2,1)S(1)}, u32[]{:S(2)}, u32[]{:S(2)}) collective-permute-start(bf16[512,384]{1,0:T(8,128)(2,1)S(1)} %fusion.42), channel_id=1, source_target_pairs={{0,16},{16,0},{1,17},{17,1},{2,18},{18,2},{3,19},{19,3},{4,20},{20... | collective-permute-start | bytes 1179656 | tf_op jit(solution)/shard_map/ppermute | solution.py:373
  208.9 15.8 %collective-permute-start.8 = (bf16[512,384]{1,0:T(8,128)(2,1)S(1)}, bf16[512,384]{1,0:T(8,128)(2,1)S(1)}, u32[]{:S(2)}, u32[]{:S(2)}) collective-permute-start(bf16[512,384]{1,0:T(8,128)(2,1)S(1)} %fusion.41), channel_id=1, source_target_pairs={{0,16},{16,0},{1,17},{17,1},{2,18},{18,2},{3,19},{19,3},{4,20},{20... | collective-permute-start | bytes 1179656 | tf_op jit(solution)/shard_map/ppermute | solution.py:373
  211.2 35.8 %collective-permute-start.12 = (bf16[256,1664]{1,0:T(8,128)(2,1)}, bf16[256,1664]{1,0:T(8,128)(2,1)}, u32[]{:S(2)}, u32[]{:S(2)}) collective-permute-start(bf16[256,1664]{1,0:T(8,128)(2,1)} %slice.167), channel_id=1, source_target_pairs={{0,2},{1,3},{2,0},{3,1},{4,6},{5,7},{6,4},{7,5},{8,10},{9,11},{10,... | collective-permute-start | bytes 2555912 | tf_op jit(solution)/shard_map/ppermute | solution.py:377
  216.1 30.9 %collective-permute-start.13 = (bf16[256,1664]{1,0:T(8,128)(2,1)}, bf16[256,1664]{1,0:T(8,128)(2,1)}, u32[]{:S(2)}, u32[]{:S(2)}) collective-permute-start(bf16[256,1664]{1,0:T(8,128)(2,1)} %slice.168), channel_id=1, source_target_pairs={{0,16},{16,0},{1,17},{17,1},{2,18},{18,2},{3,19},{19,3},{4,20},{20... | collective-permute-start | bytes 2555912 | tf_op jit(solution)/shard_map/ppermute | solution.py:373
  224.8 65.6 %collective-permute-start.26 = (bf16[1536,768]{1,0:T(8,128)(2,1)}, bf16[1536,768]{1,0:T(8,128)(2,1)}, u32[]{:S(2)}, u32[]{:S(2)}) collective-permute-start(bf16[1536,768]{1,0:T(8,128)(2,1)} %collective-permute-done.10.refs_17_.refs_13_), channel_id=1, source_target_pairs={{0,4},{1,5},{2,6},{3,7},{4,8},{5,9},{6,10},{7,11},{8,12},{9,13},{1... | collective-permute-start | bytes 7077896 | tf_op jit(solution)/shard_map/ppermute | solution.py:389
  234.2 56.3 %collective-permute-start.27 = (bf16[1536,768]{1,0:T(8,128)(2,1)}, bf16[1536,768]{1,0:T(8,128)(2,1)}, u32[]{:S(2)}, u32[]{:S(2)}) collective-permute-start(bf16[1536,768]{1,0:T(8,128)(2,1)} %collective-permute-done.11.refs_21_.refs_17_), channel_id=1, source_target_pairs={{4,0},{5,1},{6,2},{7,3},{8,4},{9,5},{10,6},{11,7},{12,8},{13,9},{1... | collective-permute-start | bytes 7077896 | tf_op jit(solution)/shard_map/ppermute | solution.py:393
  247.0 32.8 %collective-permute-start.14 = (bf16[512,1536]{1,0:T(8,128)(2,1)}, bf16[512,1536]{1,0:T(8,128)(2,1)S(1)}, u32[]{:S(2)}, u32[]{:S(2)}) collective-permute-start(bf16[512,1536]{1,0:T(8,128)(2,1)} %get-tuple-element.121.refs_0_), channel_id=1, source_target_pairs={{0,16},{16,0},{1,17},{17,1},{2,18},{18,2},{3,19},{19,3},{4,20},{20... | collective-permute-start | bytes 4718600 | tf_op jit(solution)/shard_map/ppermute | solution.py:373
  249.0 32.4 %collective-permute-start.15 = (bf16[512,1536]{1,0:T(8,128)(2,1)}, bf16[512,1536]{1,0:T(8,128)(2,1)}, u32[]{:S(2)}, u32[]{:S(2)}) collective-permute-start(bf16[512,1536]{1,0:T(8,128)(2,1)} %get-tuple-element.121.refs_0_), channel_id=1, source_target_pairs={{0,2},{1,3},{2,0},{3,1},{4,6},{5,7},{6,4},{7,5},{8,10},{9,11},{10,... | collective-permute-start | bytes 4718600 | tf_op jit(solution)/shard_map/ppermute | solution.py:377
  279.8 19.7 %collective-permute-start.16 = (bf16[256,1536]{1,0:T(8,128)(2,1)S(1)}, bf16[256,1536]{1,0:T(8,128)(2,1)S(1)}, u32[]{:S(2)}, u32[]{:S(2)}) collective-permute-start(bf16[256,1536]{1,0:T(8,128)(2,1)S(1)} %slice.217), channel_id=1, source_target_pairs={{0,2},{1,3},{2,0},{3,1},{4,6},{5,7},{6,4},{7,5},{8,10},{9,11},{10,... | collective-permute-start | bytes 2359304 | tf_op jit(solution)/shard_map/ppermute | solution.py:377
  282.6 20.3 %collective-permute-start.17 = (bf16[256,1536]{1,0:T(8,128)(2,1)S(1)}, bf16[256,1536]{1,0:T(8,128)(2,1)S(1)}, u32[]{:S(2)}, u32[]{:S(2)}) collective-permute-start(bf16[256,1536]{1,0:T(8,128)(2,1)S(1)} %slice.218), channel_id=1, source_target_pairs={{0,16},{16,0},{1,17},{17,1},{2,18},{18,2},{3,19},{19,3},{4,20},{20... | collective-permute-start | bytes 2359304 | tf_op jit(solution)/shard_map/ppermute | solution.py:373
  284.3 19.4 %collective-permute-start.24 = (bf16[256,1664]{1,0:T(8,128)(2,1)}, bf16[256,1664]{1,0:T(8,128)(2,1)}, u32[]{:S(2)}, u32[]{:S(2)}) collective-permute-start(bf16[256,1664]{1,0:T(8,128)(2,1)} %collective-permute-done.12.refs_10_), channel_id=1, source_target_pairs={{0,1},{1,0},{2,3},{3,2},{4,5},{5,4},{6,7},{7,6},{8,9},{9,8},{10,11... | collective-permute-start | bytes 2555912 | tf_op jit(solution)/shard_map/ppermute | solution.py:377
  290.4 17.6 %collective-permute-start.18 = (bf16[512,1536]{1,0:T(8,128)(2,1)S(1)}, bf16[512,1536]{1,0:T(8,128)(2,1)}, u32[]{:S(2)}, u32[]{:S(2)}) collective-permute-start(bf16[512,1536]{1,0:T(8,128)(2,1)S(1)} %collective-permute-done.14.refs_0_.refs_1_), channel_id=1, source_target_pairs={{0,1},{1,0},{2,3},{3,2},{4,5},{5,4},{6,7},{7,6},{8,9},{9,8},{10,11... | collective-permute-start | bytes 4718600 | tf_op jit(solution)/shard_map/ppermute | solution.py:377
  290.5 21.8 %collective-permute-start.22 = (bf16[512,1664]{1,0:T(8,128)(2,1)}, bf16[512,1664]{1,0:T(8,128)(2,1)}, u32[]{:S(2)}, u32[]{:S(2)}) collective-permute-start(bf16[512,1664]{1,0:T(8,128)(2,1)} %collective-permute-done.6.refs_8_.refs_7_), channel_id=1, source_target_pairs={{0,1},{1,0},{2,3},{3,2},{4,5},{5,4},{6,7},{7,6},{8,9},{9,8},{10,11... | collective-permute-start | bytes 5111816 | tf_op jit(solution)/shard_map/ppermute | solution.py:377
  299.5 12.8 %collective-permute-start.23 = (bf16[512,1664]{1,0:T(8,128)(2,1)S(1)}, bf16[512,1664]{1,0:T(8,128)(2,1)}, u32[]{:S(2)}, u32[]{:S(2)}) collective-permute-start(bf16[512,1664]{1,0:T(8,128)(2,1)S(1)} %collective-permute-done.7.refs_9_.refs_8_), channel_id=1, source_target_pairs={{0,1},{1,0},{2,3},{3,2},{4,5},{5,4},{6,7},{7,6},{8,9},{9,8},{10,11... | collective-permute-start | bytes 5111816 | tf_op jit(solution)/shard_map/ppermute | solution.py:377
  302.9 4.8 collective-permute-start.25
  303.8 8.5 %collective-permute-start.19 = (bf16[512,1536]{1,0:T(8,128)(2,1)}, bf16[512,1536]{1,0:T(8,128)(2,1)}, u32[]{:S(2)}, u32[]{:S(2)}) collective-permute-start(bf16[512,1536]{1,0:T(8,128)(2,1)} %collective-permute-done.15.refs_1_.refs_2_), channel_id=1, source_target_pairs={{0,1},{1,0},{2,3},{3,2},{4,5},{5,4},{6,7},{7,6},{8,9},{9,8},{10,11... | collective-permute-start | bytes 4718600 | tf_op jit(solution)/shard_map/ppermute | solution.py:377
  307.6 4.6 collective-permute-start.20
  308.0 4.2 collective-permute-start.21
  367.9 9.1 %collective-permute-start.28 = (bf16[1024,1536]{1,0:T(8,128)(2,1)}, bf16[1024,1536]{1,0:T(8,128)(2,1)S(1)}, u32[]{:S(2)}, u32[]{:S(2)}) collective-permute-start(bf16[1024,1536]{1,0:T(8,128)(2,1)} %get-tuple-element.131), channel_id=1, source_target_pairs={{0,1},{1,0},{2,3},{3,2},{4,5},{5,4},{6,7},{7,6},{8,9},{9,8},{10,11... | collective-permute-start | bytes 9437192 | tf_op jit(solution)/shard_map/ppermute | solution.py:377
  368.4 14.8 %collective-permute-start.29 = (bf16[512,1536]{1,0:T(8,128)(2,1)}, bf16[512,1536]{1,0:T(8,128)(2,1)}, u32[]{:S(2)}, u32[]{:S(2)}) collective-permute-start(bf16[512,1536]{1,0:T(8,128)(2,1)} %get-tuple-element.121.refs_0_), channel_id=1, source_target_pairs={{0,1},{1,0},{2,3},{3,2},{4,5},{5,4},{6,7},{7,6},{8,9},{9,8},{10,11... | collective-permute-start | bytes 4718600 | tf_op jit(solution)/shard_map/ppermute | solution.py:377
  368.5 14.7 %collective-permute-start.30 = (bf16[512,1664]{1,0:T(8,128)(2,1)}, bf16[512,1664]{1,0:T(8,128)(2,1)}, u32[]{:S(2)}, u32[]{:S(2)}) collective-permute-start(bf16[512,1664]{1,0:T(8,128)(2,1)} %concatenate.88.refs_6_), channel_id=1, source_target_pairs={{0,1},{1,0},{2,3},{3,2},{4,5},{5,4},{6,7},{7,6},{8,9},{9,8},{10,11... | collective-permute-start | bytes 5111816 | tf_op jit(solution)/shard_map/ppermute | solution.py:377
  381.7 57.1 %collective-permute-start.31 = (bf16[512,1536]{1,0:T(8,128)(2,1)}, bf16[512,1536]{1,0:T(8,128)(2,1)}, u32[]{:S(2)}, u32[]{:S(2)}) collective-permute-start(bf16[512,1536]{1,0:T(8,128)(2,1)} %get-tuple-element.257), channel_id=1, source_target_pairs={{0,2},{1,3},{2,0},{3,1},{4,6},{5,7},{6,4},{7,5},{8,10},{9,11},{10,... | collective-permute-start | bytes 4718600 | tf_op jit(solution)/shard_map/ppermute | solution.py:377
  382.5 56.2 %collective-permute-start.32 = (bf16[512,1536]{1,0:T(8,128)(2,1)}, bf16[512,1536]{1,0:T(8,128)(2,1)}, u32[]{:S(2)}, u32[]{:S(2)}) collective-permute-start(bf16[512,1536]{1,0:T(8,128)(2,1)} %get-tuple-element.256), channel_id=1, source_target_pairs={{0,16},{16,0},{1,17},{17,1},{2,18},{18,2},{3,19},{19,3},{4,20},{20... | collective-permute-start | bytes 4718600 | tf_op jit(solution)/shard_map/ppermute | solution.py:373
  437.7 39.6 %collective-permute-start.33 = (bf16[1024,1536]{1,0:T(8,128)(2,1)}, bf16[1024,1536]{1,0:T(8,128)(2,1)}, u32[]{:S(2)}, u32[]{:S(2)}) collective-permute-start(bf16[1024,1536]{1,0:T(8,128)(2,1)} %get-tuple-element.150), channel_id=1, source_target_pairs={{0,1},{1,0},{2,3},{3,2},{4,5},{5,4},{6,7},{7,6},{8,9},{9,8},{10,11... | collective-permute-start | bytes 9437192 | tf_op jit(solution)/shard_map/ppermute | solution.py:377
  450.1 74.3 %copy-start.16 = (bf16[1536,256]{1,0:T(8,128)(2,1)}, bf16[1536,256]{1,0:T(8,128)(2,1)S(1)}, u32[]{:S(2)}) copy-start(bf16[1536,256]{1,0:T(8,128)(2,1)S(1)} %get-tuple-element.270) | copy-start | bytes 2359300
  450.1 83.1 %copy-start.19 = (bf16[1536,256]{1,0:T(8,128)(2,1)}, bf16[1536,256]{1,0:T(8,128)(2,1)S(1)}, u32[]{:S(2)}) copy-start(bf16[1536,256]{1,0:T(8,128)(2,1)S(1)} %get-tuple-element.271) | copy-start | bytes 2359300
  467.2 66.1 %copy-start.4 = (bf16[1536,512]{1,0:T(8,128)(2,1)}, bf16[1536,512]{1,0:T(8,128)(2,1)S(1)}, u32[]{:S(2)}) copy-start(bf16[1536,512]{1,0:T(8,128)(2,1)S(1)} %get-tuple-element.255) | copy-start | bytes 4718596
  468.9 55.4 %collective-permute-start.38 = (bf16[1536,768]{1,0:T(8,128)(2,1)}, bf16[1536,768]{1,0:T(8,128)(2,1)}, u32[]{:S(2)}, u32[]{:S(2)}) collective-permute-start(bf16[1536,768]{1,0:T(8,128)(2,1)} %pad_maximum_fusion.3), channel_id=1, source_target_pairs={{0,4},{1,5},{2,6},{3,7},{4,8},{5,9},{6,10},{7,11},{8,12},{9,13},{1... | collective-permute-start | bytes 7077896 | tf_op jit(solution)/shard_map/ppermute | solution.py:389
  475.9 57.3 %collective-permute-start.39 = (bf16[1536,768]{1,0:T(8,128)(2,1)}, bf16[1536,768]{1,0:T(8,128)(2,1)}, u32[]{:S(2)}, u32[]{:S(2)}) collective-permute-start(bf16[1536,768]{1,0:T(8,128)(2,1)} %pad_maximum_fusion.2), channel_id=1, source_target_pairs={{4,0},{5,1},{6,2},{7,3},{8,4},{9,5},{10,6},{11,7},{12,8},{13,9},{1... | collective-permute-start | bytes 7077896 | tf_op jit(solution)/shard_map/ppermute | solution.py:393
  483.3 29.1 %collective-permute-start.34 = (bf16[256,1536]{1,0:T(8,128)(2,1)}, bf16[256,1536]{1,0:T(8,128)(2,1)S(1)}, u32[]{:S(2)}, u32[]{:S(2)}) collective-permute-start(bf16[256,1536]{1,0:T(8,128)(2,1)} %get-tuple-element.246), channel_id=1, source_target_pairs={{0,16},{16,0},{1,17},{17,1},{2,18},{18,2},{3,19},{19,3},{4,20},{20... | collective-permute-start | bytes 2359304 | tf_op jit(solution)/shard_map/ppermute | solution.py:373
  484.7 27.7 %collective-permute-start.35 = (bf16[256,1536]{1,0:T(8,128)(2,1)}, bf16[256,1536]{1,0:T(8,128)(2,1)S(1)}, u32[]{:S(2)}, u32[]{:S(2)}) collective-permute-start(bf16[256,1536]{1,0:T(8,128)(2,1)} %get-tuple-element.247), channel_id=1, source_target_pairs={{0,2},{1,3},{2,0},{3,1},{4,6},{5,7},{6,4},{7,5},{8,10},{9,11},{10,... | collective-permute-start | bytes 2359304 | tf_op jit(solution)/shard_map/ppermute | solution.py:377
  520.0 23.0 %collective-permute-start.40 = (bf16[1024,1536]{1,0:T(8,128)(2,1)}, bf16[1024,1536]{1,0:T(8,128)(2,1)}, u32[]{:S(2)}, u32[]{:S(2)}) collective-permute-start(bf16[1024,1536]{1,0:T(8,128)(2,1)} %get-tuple-element.162), channel_id=1, source_target_pairs={{0,1},{1,0},{2,3},{3,2},{4,5},{5,4},{6,7},{7,6},{8,9},{9,8},{10,11... | collective-permute-start | bytes 9437192 | tf_op jit(solution)/shard_map/ppermute | solution.py:377
  521.2 79.7 %collective-permute-start.36 = (bf16[1024,1536]{1,0:T(8,128)(2,1)}, bf16[1024,1536]{1,0:T(8,128)(2,1)}, u32[]{:S(2)}, u32[]{:S(2)}) collective-permute-start(bf16[1024,1536]{1,0:T(8,128)(2,1)} %get-tuple-element.160), channel_id=1, source_target_pairs={{0,1},{1,0},{2,3},{3,2},{4,5},{5,4},{6,7},{7,6},{8,9},{9,8},{10,11... | collective-permute-start | bytes 9437192 | tf_op jit(solution)/shard_map/ppermute | solution.py:377
  523.6 25.8 %collective-permute-start.37 = (bf16[512,768]{1,0:T(8,128)(2,1)}, bf16[512,768]{1,0:T(8,128)(2,1)}, u32[]{:S(2)}, u32[]{:S(2)}) collective-permute-start(bf16[512,768]{1,0:T(8,128)(2,1)} %fusion.36), channel_id=1, source_target_pairs={{0,16},{16,0},{1,17},{17,1},{2,18},{18,2},{3,19},{19,3},{4,20},{20... | collective-permute-start | bytes 2359304 | tf_op jit(solution)/shard_map/ppermute | solution.py:373
  527.6 77.3 %collective-permute-start.41 = (bf16[1536,768]{1,0:T(8,128)(2,1)}, bf16[1536,768]{1,0:T(8,128)(2,1)}, u32[]{:S(2)}, u32[]{:S(2)}) collective-permute-start(bf16[1536,768]{1,0:T(8,128)(2,1)} %add_convert_fusion.7), channel_id=1, source_target_pairs={{0,4},{1,5},{2,6},{3,7},{4,8},{5,9},{6,10},{7,11},{8,12},{9,13},{1... | collective-permute-start | bytes 7077896 | tf_op jit(solution)/shard_map/ppermute | solution.py:389
  536.6 68.3 %collective-permute-start.42 = (bf16[1536,768]{1,0:T(8,128)(2,1)}, bf16[1536,768]{1,0:T(8,128)(2,1)}, u32[]{:S(2)}, u32[]{:S(2)}) collective-permute-start(bf16[1536,768]{1,0:T(8,128)(2,1)} %add_convert_fusion.6), channel_id=1, source_target_pairs={{4,0},{5,1},{6,2},{7,3},{8,4},{9,5},{10,6},{11,7},{12,8},{13,9},{1... | collective-permute-start | bytes 7077896 | tf_op jit(solution)/shard_map/ppermute | solution.py:393
  548.6 56.4 %collective-permute-start.43 = (bf16[512,1536]{1,0:T(8,128)(2,1)}, bf16[512,1536]{1,0:T(8,128)(2,1)}, u32[]{:S(2)}, u32[]{:S(2)}) collective-permute-start(bf16[512,1536]{1,0:T(8,128)(2,1)} %get-tuple-element.251), channel_id=1, source_target_pairs={{0,2},{1,3},{2,0},{3,1},{4,6},{5,7},{6,4},{7,5},{8,10},{9,11},{10,... | collective-permute-start | bytes 4718600 | tf_op jit(solution)/shard_map/ppermute | solution.py:377
  549.4 55.5 %collective-permute-start.44 = (bf16[512,1536]{1,0:T(8,128)(2,1)}, bf16[512,1536]{1,0:T(8,128)(2,1)}, u32[]{:S(2)}, u32[]{:S(2)}) collective-permute-start(bf16[512,1536]{1,0:T(8,128)(2,1)} %get-tuple-element.250), channel_id=1, source_target_pairs={{0,16},{16,0},{1,17},{17,1},{2,18},{18,2},{3,19},{19,3},{4,20},{20... | collective-permute-start | bytes 4718600 | tf_op jit(solution)/shard_map/ppermute | solution.py:373
  608.1 20.2 %collective-permute-start.45 = (bf16[256,1536]{1,0:T(8,128)(2,1)}, bf16[256,1536]{1,0:T(8,128)(2,1)}, u32[]{:S(2)}, u32[]{:S(2)}) collective-permute-start(bf16[256,1536]{1,0:T(8,128)(2,1)} %fusion.26), channel_id=1, source_target_pairs={{0,16},{16,0},{1,17},{17,1},{2,18},{18,2},{3,19},{19,3},{4,20},{20... | collective-permute-start | bytes 2359304 | tf_op jit(solution)/shard_map/ppermute | solution.py:373
  626.7 32.2 %collective-permute-start.48 = (bf16[2,2,4,48,1408]{4,3,2,1,0:T(8,128)(2,1)}, bf16[2,2,4,48,1408]{4,3,2,1,0:T(8,128)(2,1)}, u32[]{:S(2)}, u32[]{:S(2)}) collective-permute-start(bf16[2,2,4,48,1408]{4,3,2,1,0:T(8,128)(2,1)} %dynamic-slice_bitcast_fusion), channel_id=1, source_target_pairs={{0,1},{1,0},{2,3},{3,2},{4,5},{5,4},{6,7},{7,6},{8,9},{9,8},{10,11... | collective-permute-start | bytes 6488072 | tf_op jit(solution)/shard_map/ppermute | solution.py:377
  632.8 23.9 %collective-permute-start.46 = (bf16[256,1536]{1,0:T(8,128)(2,1)}, bf16[256,1536]{1,0:T(8,128)(2,1)}, u32[]{:S(2)}, u32[]{:S(2)}) collective-permute-start(bf16[256,1536]{1,0:T(8,128)(2,1)} %get-tuple-element.243), channel_id=1, source_target_pairs={{0,2},{1,3},{2,0},{3,1},{4,6},{5,7},{6,4},{7,5},{8,10},{9,11},{10,... | collective-permute-start | bytes 2359304 | tf_op jit(solution)/shard_map/ppermute | solution.py:377
  647.5 33.9 %collective-permute-start.47 = (bf16[512,1536]{1,0:T(8,128)(2,1)}, bf16[512,1536]{1,0:T(8,128)(2,1)}, u32[]{:S(2)}, u32[]{:S(2)}) collective-permute-start(bf16[512,1536]{1,0:T(8,128)(2,1)} %get-tuple-element.182), channel_id=1, source_target_pairs={{0,16},{16,0},{1,17},{17,1},{2,18},{18,2},{3,19},{19,3},{4,20},{20... | collective-permute-start | bytes 4718600 | tf_op jit(solution)/shard_map/ppermute | solution.py:373
  648.2 52.7 %collective-permute-start.50 = (bf16[1536,768]{1,0:T(8,128)(2,1)}, bf16[1536,768]{1,0:T(8,128)(2,1)}, u32[]{:S(2)}, u32[]{:S(2)}) collective-permute-start(bf16[1536,768]{1,0:T(8,128)(2,1)} %get-tuple-element.249), channel_id=1, source_target_pairs={{0,4},{1,5},{2,6},{3,7},{4,8},{5,9},{6,10},{7,11},{8,12},{9,13},{1... | collective-permute-start | bytes 7077896 | tf_op jit(solution)/shard_map/ppermute | solution.py:389
  653.8 52.3 %collective-permute-start.51 = (bf16[1536,768]{1,0:T(8,128)(2,1)}, bf16[1536,768]{1,0:T(8,128)(2,1)}, u32[]{:S(2)}, u32[]{:S(2)}) collective-permute-start(bf16[1536,768]{1,0:T(8,128)(2,1)} %get-tuple-element.248), channel_id=1, source_target_pairs={{4,0},{5,1},{6,2},{7,3},{8,4},{9,5},{10,6},{11,7},{12,8},{13,9},{1... | collective-permute-start | bytes 7077896 | tf_op jit(solution)/shard_map/ppermute | solution.py:393
  661.8 26.4 %collective-permute-start.49 = (bf16[2,4,48,1408]{3,2,1,0:T(8,128)(2,1)S(1)}, bf16[2,4,48,1408]{3,2,1,0:T(8,128)(2,1)S(1)}, u32[]{:S(2)}, u32[]{:S(2)}) collective-permute-start(bf16[2,4,48,1408]{3,2,1,0:T(8,128)(2,1)S(1)} %fusion.43), channel_id=1, source_target_pairs={{0,2},{1,3},{2,0},{3,1},{4,6},{5,7},{6,4},{7,5},{8,10},{9,11},{10,... | collective-permute-start | bytes 3244040 | tf_op jit(solution)/shard_map/ppermute | solution.py:377
  709.9 12.2 %collective-permute-start.54 = (bf16[2,48,1408]{2,1,0:T(8,128)(2,1)S(1)}, bf16[2,48,1408]{2,1,0:T(8,128)(2,1)S(1)}, u32[]{:S(2)}, u32[]{:S(2)}) collective-permute-start(bf16[2,48,1408]{2,1,0:T(8,128)(2,1)S(1)} %fusion.54), channel_id=1, source_target_pairs={{0,12},{1,13},{2,14},{3,15},{4,8},{5,9},{6,10},{7,11},{8,4},{9,5},... | collective-permute-start | bytes 811016 | tf_op jit(solution)/shard_map/ppermute | solution.py:377
  710.0 32.9 %collective-permute-start.55 = (bf16[1536,512]{1,0:T(8,128)(2,1)S(1)}, bf16[1536,512]{1,0:T(8,128)(2,1)S(1)}, u32[]{:S(2)}, u32[]{:S(2)}) collective-permute-start(bf16[1536,512]{1,0:T(8,128)(2,1)S(1)} %pad_maximum_fusion.7), channel_id=1, source_target_pairs={{0,0},{1,16},{2,2},{3,18},{4,4},{5,20},{6,6},{7,22},{8,8},{9,24},{... | collective-permute-start | bytes 4718600 | tf_op jit(solution)/shard_map/ppermute | solution.py:1022
  716.5 16.7 %collective-permute-start.53 = (bf16[2,48,1408]{2,1,0:T(8,128)(2,1)S(1)}, bf16[2,48,1408]{2,1,0:T(8,128)(2,1)S(1)}, u32[]{:S(2)}, u32[]{:S(2)}) collective-permute-start(bf16[2,48,1408]{2,1,0:T(8,128)(2,1)S(1)} %get-tuple-element.276), channel_id=1, source_target_pairs={{0,8},{1,9},{2,10},{3,11},{4,12},{5,13},{6,14},{7,15},{8,0},{9,1},... | collective-permute-start | bytes 811016 | tf_op jit(solution)/shard_map/ppermute | solution.py:377
  717.1 16.1 %collective-permute-start.52 = (bf16[2,48,1408]{2,1,0:T(8,128)(2,1)S(1)}, bf16[2,48,1408]{2,1,0:T(8,128)(2,1)S(1)}, u32[]{:S(2)}, u32[]{:S(2)}) collective-permute-start(bf16[2,48,1408]{2,1,0:T(8,128)(2,1)S(1)} %get-tuple-element.275), channel_id=1, source_target_pairs={{0,4},{1,5},{2,6},{3,7},{4,0},{5,1},{6,2},{7,3},{8,12},{9,13},{10,... | collective-permute-start | bytes 811016 | tf_op jit(solution)/shard_map/ppermute | solution.py:377
  720.2 19.3 %collective-permute-start.56 = (bf16[1536,256]{1,0:T(8,128)(2,1)S(1)}, bf16[1536,256]{1,0:T(8,128)(2,1)S(1)}, u32[]{:S(2)}, u32[]{:S(2)}) collective-permute-start(bf16[1536,256]{1,0:T(8,128)(2,1)S(1)} %get-tuple-element.188), channel_id=1, source_target_pairs={{1,0},{17,1},{3,2},{19,3},{5,4},{21,5},{7,6},{23,7},{9,8},{25,9},{... | collective-permute-start | bytes 2359304 | tf_op jit(solution)/shard_map/ppermute | solution.py:1022
  743.0 5.2 collective-permute-start.57
  (62 other events, 869.2 us)
Sparse Core Ops, SparseCore 0:
  22.4 112.9 all-gather.1
  543.1 107.8 reduce-scatter.1

commit v5 on v4

--- a/solution.py
+++ b/solution.py
@@ -463,15 +463,43 @@
     return values * cos - swapped * sin
 
 
-def qkv_kernel(x_ref, gain_ref, w_ref, cos_ref, sin_ref, h_ref, q_ref, k_ref, v_ref):
+def place_shards(place_ref, own_ref, other_ref, shard, store):
+    for core in range(2):
+        source = other_ref if core else own_ref
+        for row in range(2):
+            for line in range(LINE):
+                index = (place_ref[0] ^ line) * 4 + (place_ref[1] ^ row) * 2 + (place_ref[2] ^ core)
+                store(source, (row * LINE + line) * shard, pl.multiple_of(index * shard, shard))
+
+
+def qkv_kernel(
+    place_ref, x_ref, own_ref, other_ref, cos_ref, sin_ref,
+    h_ref, q_ref, k_ref, v_ref, w_ref, gain_ref, columns_buf,
+):
+    q_width, kv_heads = q_ref.shape[1], k_ref.shape[0]
+    kv_width = kv_heads * HDIM
+    width, columns = w_ref.shape
+    shard = own_ref.shape[0] // (2 * LINE)
+
+    @pl.when(pl.program_id(0) == 0)
+    def _():
+        def store(source, low, place):
+            for seq in range(2):
+                first = seq * (columns + PAD)
+                rows = pl.ds(pl.multiple_of(place + seq * (width // 2), shard), shard)
+                w_ref[rows, :] = source[low : low + shard, first : first + columns]
+                columns_buf[rows, :] = source[
+                    low : low + shard, first + columns : first + columns + PAD
+                ].astype(F32)
+
+        place_shards(place_ref, own_ref, other_ref, shard, store)
+        gain_ref[...] = columns_buf[...].T[: gain_ref.shape[0]]
+
     value = x_ref[...].astype(F32)
     scale = lax.rsqrt(jnp.mean(value * value, axis=-1, keepdims=True) + EPSILON)
-    normed = (value * scale * gain_ref[...]).astype(BF16)
+    normed = (value * scale * gain_ref[0:1, :]).astype(BF16)
     h_ref[...] = normed
-    q_width, kv_heads = q_ref.shape[1], k_ref.shape[0]
-    kv_width = kv_heads * HDIM
-    weights = w_ref[:, : q_width + 2 * kv_width]
-    both = jnp.dot(normed, weights, preferred_element_type=F32)
+    both = jnp.dot(normed, w_ref[...], preferred_element_type=F32)
     spun = turned(both[:, : q_width + kv_width], cos_ref[...], sin_ref[...], 1)
     q_ref[...] = (spun[:, :q_width] * SCORE_SCALE).astype(BF16)
     for head in range(kv_heads):
@@ -481,31 +509,43 @@
         v_ref[head] = both[:, low : low + HDIM].astype(BF16)
 
 
-def project(x_sorted, gain, weights, cos, sin, q_width, kv_heads):
+def project(places, x_sorted, own, other, cos, sin, q_width, kv_heads):
     rows, width = x_sorted.shape
     tile = 256
     columns = q_width + 2 * kv_heads * HDIM
 
     def row_block(lanes):
-        return pl.BlockSpec((tile, lanes), lambda i: (i, 0))
-
-    heads = pl.BlockSpec((kv_heads, tile, HDIM), lambda i: (0, i, 0))
+        return pl.BlockSpec((tile, lanes), lambda i, p: (i, 0))
+
+    def whole(shape):
+        return pl.BlockSpec(shape, lambda i, p: (0, 0))
+
+    heads = pl.BlockSpec((kv_heads, tile, HDIM), lambda i, p: (0, i, 0))
     return pl.pallas_call(
         qkv_kernel,
-        grid=(rows // tile,),
-        in_specs=[
-            row_block(width),
-            pl.BlockSpec((1, width), lambda i: (0, 0)),
-            pl.BlockSpec((width, width), lambda i: (0, 1)),
-            row_block(cos.shape[1]),
-            row_block(cos.shape[1]),
-        ],
-        out_specs=[row_block(width), row_block(q_width), heads, heads],
+        grid_spec=pltpu.PrefetchScalarGridSpec(
+            num_scalar_prefetch=1,
+            grid=(rows // tile,),
+            in_specs=[
+                row_block(width),
+                whole(own.shape),
+                whole(other.shape),
+                row_block(cos.shape[1]),
+                row_block(cos.shape[1]),
+            ],
+            out_specs=[
+                row_block(width), row_block(q_width), heads, heads,
+                whole((width, columns)), whole((8, width)),
+            ],
+            scratch_shapes=[pltpu.VMEM((width, PAD), F32)],
+        ),
         out_shape=[
             jax.ShapeDtypeStruct((rows, width), BF16),
             jax.ShapeDtypeStruct((rows, q_width), BF16),
             jax.ShapeDtypeStruct((kv_heads, rows, HDIM), BF16),
             jax.ShapeDtypeStruct((kv_heads, rows, HDIM), BF16),
+            jax.ShapeDtypeStruct((width, columns), BF16),
+            jax.ShapeDtypeStruct((8, width), F32),
         ],
         compiler_params=pltpu.CompilerParams(vmem_limit_bytes=VMEM_BYTES),
         cost_estimate=pl.CostEstimate(
@@ -514,7 +554,7 @@
             transcendentals=rows,
         ),
         name="project",
-    )(x_sorted, gain, weights, cos, sin)
+    )(places, x_sorted, own, other, cos, sin)
 
 
 def mix_kernel(place_ref, mine_ref, theirs_ref, x_ref, gain_ref, w_ref, m_ref, h_ref, parts_ref):
@@ -596,7 +636,7 @@
         token_grad_kernel,
         grid=(3,),
         in_specs=[whole(grad) for grad in grads]
-        + [pl.BlockSpec((tile, width), lambda i: (i, 1)), whole(own_places), whole(other_places)],
+        + [pl.BlockSpec((tile, columns), lambda i: (i, 0)), whole(own_places), whole(other_places)],
         out_specs=[block, block],
         out_shape=[jax.ShapeDtypeStruct((count, width), BF16)] * 2,
         compiler_params=pltpu.CompilerParams(vmem_limit_bytes=VMEM_BYTES),
@@ -1035,16 +1075,17 @@
 
     projections = (w_query, w_key, w_value)
     qkv_width = q_width + 2 * kv_width
-    gain_columns = jnp.pad(
-        jnp.stack([gain_attn, gain_ffn], axis=1), ((0, 0), (0, width - qkv_width - 2))
-    )
+    qkv_width = q_width + 2 * kv_width
+    gain_columns = jnp.pad(jnp.stack([gain_attn, gain_ffn], axis=1), ((0, 0), (0, PAD - 2)))
     mine, theirs = [
-        jnp.concatenate([w_output] + [half_of(w, which) for w in projections] + [gain_columns], axis=1)
+        jnp.concatenate([half_of(w, which) for w in projections] + [gain_columns], axis=1)
         for which in (seq, 1 - seq)
     ]
-    theirs = swap_seq(theirs)
-    pair = jnp.stack([jnp.where(first_seq, mine, theirs), jnp.where(first_seq, theirs, mine)])
-    gathered = lax.all_gather(pair, "dp", axis=1, tiled=True).reshape(width, 2 * width)
+    theirs = swap_seq(jnp.concatenate([theirs, w_output], axis=1))
+    output_pair = ordered(w_output[None], theirs[None, :, qkv_width + PAD :], 0)
+    block = ordered(mine, theirs[:, : qkv_width + PAD], 1)
+    along = [block] + [swap_dp(block, 4 * step) for step in range(1, LINE)]
+    places_of = jnp.stack([line, row_of, core]).astype(jnp.int32)
 
     in_own = w_in[0]
     half = in_own.shape[1] // 2
@@ -1053,6 +1094,7 @@
     )
     same = both_axes(sent, straight)
     cross = both_axes(lax.dynamic_slice_in_dim(in_own, (1 - seq) * half, half, axis=1), crossed)
+    same, cross, along = lax.optimization_barrier((same, cross, along))
     own_part = jnp.concatenate(
         [
             jnp.where(first_core, same[:, :half], cross),
@@ -1062,7 +1104,17 @@
         axis=1,
     )
     other_tokens = swap_seq(after(tokens, own_part))
-    up_one, down_one = line_up(own_part), line_down(own_part)
+    output_full = lax.all_gather(after(output_pair, own_part), "dp", axis=1, tiled=True)
+    output_full = output_full.reshape(width, width)
+    cut = width // 2
+    lines = (line_up(own_part[:cut]), line_down(own_part[:cut]))
+    qkv_rows = after(jnp.concatenate(along, axis=0), own_part)
+    qkv_near, lines = lax.optimization_barrier((swap_y(qkv_rows), lines))
+    late_part = after(own_part[cut:], lines)
+    late_lines = (line_up(late_part), line_down(late_part))
+    qkv_rows = jnp.concatenate([qkv_rows, qkv_near], axis=0)
+    qkv_others = swap_core(qkv_rows)
+
     experts_all = 4 * LINE
     gates = jax.nn.softmax(logits, axis=-1)
     named = routes[:, :, None] == jnp.arange(experts_all, dtype=jnp.int32)[None, None, :]
@@ -1110,13 +1162,15 @@
         return contract(sort, values, 0, 0).astype(BF16)
 
     x_sorted = to_order(tokens, other_tokens)
-    x_sorted, up_one, down_one = lax.optimization_barrier((x_sorted, up_one, down_one))
+    normed, query, keys, values, w_qkv, gains = project(
+        places_of, x_sorted, qkv_rows, qkv_others, cos, sin, q_width, kv_heads
+    )
+    gain_one, gain_two = gains[0], gains[1]
+    query, late_lines = lax.optimization_barrier((query, late_lines))
+    up_one = jnp.concatenate([lines[0], late_lines[0]], axis=0)
+    down_one = jnp.concatenate([lines[1], late_lines[1]], axis=0)
+    query, up_one, down_one = lax.optimization_barrier((query, up_one, down_one))
     up_two, down_two = line_up(up_one), line_down(down_one)
-    gains = gathered[:, width + qkv_width : width + qkv_width + 2].astype(F32).T
-    gain_one, gain_two = gains[0], gains[1]
-    normed, query, keys, values = project(
-        x_sorted, gain_one[None, :], gathered, cos, sin, q_width, kv_heads
-    )
     pairs = q_width // (2 * HDIM)
     first_pairs = (pairs + 1) // 2
     mixed_one = attend(query, keys, values, start_column, 0, first_pairs)
@@ -1135,7 +1189,7 @@
     up_three, down_three = line_up(up_two), line_down(down_two)
     inputs = tokens.astype(F32)
     middle, normed_ffn, output_parts = mix(
-        seq.astype(jnp.int32)[None], mixed_mine, mixed_theirs, tokens, gain_two[None, :], gathered
+        seq.astype(jnp.int32)[None], mixed_mine, mixed_theirs, tokens, gain_two[None, :], output_full
     )
     normed_ffn = after(normed_ffn, *grad_far)
     row_near = near_pieces(normed_ffn, normed_ffn)
@@ -1209,7 +1263,7 @@
     ffn_y, ffn_x = far_links(far_ffn)
     near_ffn = over_cores(near_f, near_f_other)
     right, left = line_step(1, far_line)
-    grad_other = after(grad_other, right, left, far_ffn)
+    grad_other = after(grad_other, right, left, far_ffn, grad_w_output)
     grad_sorted = to_order(grad_mixed, grad_other)
     mid_line = (line_up(right), line_down(left))
     grad_query, grad_keys, grad_values = attend_back(
@@ -1219,38 +1273,48 @@
         ((grad_query, grad_keys, grad_values), mid_line, ffn_y, ffn_x)
     )
     right, left = line_step(2, mid_line)
-    last_line = (line_up(right), line_down(left))
+    last_first = (line_up(right[:cut]), line_down(left[:cut]))
     first_ffn, second_ffn = near_links(near_ffn, ffn_y, ffn_x)
     first_ffn, second_ffn = swap_seq(first_ffn), swap_y(second_ffn)
     ffn = own_sum(near_ffn, ffn_y, ffn_x, first_ffn, second_ffn)
     output = (middle + BRANCH_SCALE * ffn).astype(BF16)
     grads_qkv = after((grad_query, grad_keys, grad_values), right, left)
     wide = qkv_grad(normed, grads_qkv, grad_gain_two[None, :], shard)
-    grads_late = after(grads_qkv, wide)
+
+
+    def chosen(value, which, axis):
+        return lax.dynamic_index_in_dim(value, which, axis=axis, keepdims=False)
+
+    summed_output = lax.psum_scatter(
+        grad_w_output.astype(BF16), ("seq", "dp"), scatter_dimension=0, tiled=True
+    )
+    kept = chosen(wide, core, 0).astype(F32)
+    kept = kept + swap_core(chosen(wide, 1 - core, 0)).astype(F32)
+    grads_late = after(grads_qkv, kept)
     grad_normed, sent_normed = token_grad(
-        grads_late, gathered, own_places[:, None], other_places[:, None]
-    )
+        grads_late, w_qkv, own_places[:, None], other_places[:, None]
+    )
+    kept, sent_normed = lax.optimization_barrier((kept, sent_normed))
+    right_late, left_late = after((right[cut:], left[cut:]), last_first, sent_normed)
+    last_late = (line_up(right_late), line_down(left_late))
     grad_normed = grad_normed.astype(F32) + swap_seq(sent_normed).astype(F32)
     scale = lax.rsqrt(jnp.mean(inputs * inputs, axis=-1, keepdims=True) + EPSILON)
     unit = inputs * scale
     scaled = grad_normed * gain_one
     inner = jnp.mean(scaled * unit, axis=-1, keepdims=True)
     grad_tokens = grad_middle + scale * (scaled - unit * inner)
-
-    summed_output = lax.psum_scatter(
-        grad_w_output.astype(BF16), ("seq", "dp"), scatter_dimension=0, tiled=True
-    )
-
-    def chosen(value, which, axis):
-        return lax.dynamic_index_in_dim(value, which, axis=axis, keepdims=False)
-
-    kept = chosen(wide, core, 0).astype(F32)
-    kept = kept + swap_core(chosen(wide, 1 - core, 0)).astype(F32)
     next_kept = chosen(kept, row_of, 0)
     next_kept = next_kept + swap_y(chosen(kept, 1 - row_of, 0).astype(BF16)).astype(F32)
-    next_kept, last_line = lax.optimization_barrier((next_kept, last_line))
-    part_grads = (
-        line_partial(*range(LINE)) + last_line[0].astype(F32) + last_line[1].astype(F32)
+    next_kept, last_first, last_late, summed_output = lax.optimization_barrier(
+        (next_kept, last_first, last_late, summed_output)
+    )
+    own_grads = line_partial(*range(LINE))
+    part_grads = jnp.concatenate(
+        [
+            own + up.astype(F32) + down.astype(F32)
+            for own, (up, down) in ((own_grads[:cut], last_first), (own_grads[cut:], last_late))
+        ],
+        axis=0,
     ).astype(BF16)
     same_grads = jnp.where(first_core, part_grads[:, :half], part_grads[:, half : 2 * half])
     cross_grads = jnp.where(first_core, part_grads[:, half : 2 * half], part_grads[:, :half])

time: 769 us -> 760 us (0.988)
  waiting for transfers between devices: 217 us -> 167 us
  local copies, waits for them, and re-layouts: 35.9 us -> 51.9 us
  starting transfers between devices: 97.1 us -> 111 us
  other arithmetic: 86.2 us -> 96.8 us
    ppermute x6 -> x8, waiting for transfers between devices: 53.9 us -> 10.4 us  [line_up(): return lax.ppermute(value, 'dp', [(i, i + 4) for i in range(4 * LINE - 4)])]
    ppermute x15, waiting for transfers between devices: 88.5 us -> 47.9 us  [swap_seq(): return lax.ppermute(value, 'seq', [(0, 1), (1, 0)])]
    ppermute x27 -> x32, waiting for transfers between devices: 31.2 us -> 68.9 us  [swap_dp(): return lax.ppermute(value, 'dp', [(i, i ^ mask) for i in range(4 * LINE)])]
    ppermute x4, waiting for transfers between devices: 35.4 us -> 13.9 us  [both_axes(): return lax.ppermute(value, ('seq', 'dp'), pairs)]
    ppermute x6 -> x8, waiting for transfers between devices: 7.81 us -> 25.9 us  [line_down(): return lax.ppermute(value, 'dp', [(i, i - 4) for i in range(4, 4 * LINE)])]
    ppermute x27 -> x32, starting transfers between devices: 28.2 us -> 41 us  [swap_dp(): return lax.ppermute(value, 'dp', [(i, i ^ mask) for i in range(4 * LINE)])]
    ppermute x6 -> x8, starting transfers between devices: 30.8 us -> 33.1 us  [line_up(): return lax.ppermute(value, 'dp', [(i, i + 4) for i in range(4 * LINE - 4)])]
  transfers between devices with their start and end apart: 60 -> 69, of which waited for: 19 -> 26; matrix products, arithmetic and copies ran while one was open for 25% -> 28% of each run, Pallas kernels for 22% -> 23%
where the time goes in v5:
time: 760 us; the launch traced here: 751 us
  Pallas kernels  226 us (30%)
  waiting for transfers between devices  167 us (22%)
  starting transfers between devices  111 us (15%)
  other arithmetic  96.8 us (13%)
  matrix products  82.5 us (11%)
  local copies, waits for them, and re-layouts  51.9 us (7%)
  between operations  15.5 us (2%)
    pallas_call x2, Pallas kernels, run_experts(): pl.pallas_call(functools.partial(experts_kernel, tiles, tile // 2), grid_...  109 us
    dot_general x15, matrix products, contract(): lax.dot_general(left, right, (((left_dim,), (right_dim,)), ((), ())), pre...  82.5 us
    ppermute x32, waiting for transfers between devices, swap_dp(): return lax.ppermute(value, 'dp', [(i, i ^ mask) for i in range(4 * LINE)])  68.9 us
    ppermute x15, waiting for transfers between devices, swap_seq(): return lax.ppermute(value, 'seq', [(0, 1), (1, 0)])  47.9 us
    pallas_call x1, Pallas kernels, attend_back(): pl.pallas_call(attend_back_kernel, grid=(pairs,), in_specs=[pair_block, w...  45.3 us
    ppermute x32, starting transfers between devices, swap_dp(): return lax.ppermute(value, 'dp', [(i, i ^ mask) for i in range(4 * LINE)])  41 us
    ppermute x8, starting transfers between devices, line_up(): return lax.ppermute(value, 'dp', [(i, i + 4) for i in range(4 * LINE - 4)])  33.1 us
    pallas_call x2, Pallas kernels, attend(): pl.pallas_call(functools.partial(attend_kernel, base), grid=(pairs,), in_...  30 us
  transfers between devices with their start and end apart: 69, of which 26 were waited for; matrix products, arithmetic and copies ran while one was open for 28% of the time, Pallas kernels for 23%

profile of v5, /device:TPU:1, one launch (start us, length us, event | category | flops | bytes accessed | tf_op | source)
XLA Modules:
  0.0 751.4 jit_solution(10385033258810659500)
XLA Ops:
  29.5 5.0 collective-permute-done.3
  35.5 8.8 %collective-permute-done.5 = bf16[48,2816]{1,0:T(8,128)(2,1)} collective-permute-done((bf16[48,2816]{1,0:T(8,128)(2,1)S(1)}, bf16[48,2816]{1,0:T(8,128)(2,1)}, u32[]{:S(2)}, u32[]{:S(2)}) %collective-permute-start.5) | collective-permute-done | bytes 270368 | tf_op jit(solution)/shard_map/ppermute | solution.py:377
  44.3 4.5 collective-permute-done.1
  52.5 4.6 collective-permute-start.8
  64.6 3.3 concatenate.115.refs_6_
  72.4 16.0 %collective-permute-done.7 = bf16[192,2816]{1,0:T(8,128)(2,1)} collective-permute-done((bf16[192,2816]{1,0:T(8,128)(2,1)}, bf16[192,2816]{1,0:T(8,128)(2,1)}, u32[]{:S(2)}, u32[]{:S(2)}) %collective-permute-start.7) | collective-permute-done | bytes 1081376 | tf_op jit(solution)/shard_map/ppermute | solution.py:377
  88.4 12.7 %collective-permute-done.9 = bf16[768,768]{1,0:T(8,128)(2,1)} collective-permute-done((bf16[768,768]{1,0:T(8,128)(2,1)}, bf16[768,768]{1,0:T(8,128)(2,1)}, u32[]{:S(2)}, u32[]{:S(2)}) %collective-permute-start.9) | collective-permute-done | bytes 1179680 | tf_op jit(solution)/shard_map/ppermute | solution.py:393
  103.4 5.5 collective-permute-start.10
  121.1 4.9 add_convert_fusion.2.x_ref
  126.1 13.0 %project.1 = (bf16[1024,1536]{1,0:T(8,128)(2,1)}, bf16[1024,768]{1,0:T(8,128)(2,1)}, bf16[4,1024,64]{2,1,0:T(8,128)(2,1)}, bf16[4,1024,64]{2,1,0:T(8,128)(2,1)},...) custom-call(s32[3]{0:T(128)} %pad_add_fusion.place_ref, bf16[1024,1536]{1,0:T(8,128)(2,1)} %add_convert_fusion.2.x_ref, ...), custom_call_target="tpu_custom_call" | custom-call | flops 251658240 | bytes 3538944 | tf_op jit(solution)/shard_map/project/pallas_call | solution.py:524
  139.1 7.3 collective-permute-done.11
  146.4 4.4 collective-permute-done.12
  150.8 3.3 pad_maximum_fusion.2
  154.1 3.0 collective-permute-start.17
  159.6 15.0 %attend.2 = bf16[1024,384]{1,0:T(8,128)(2,1)} custom-call(bf16[1024,768]{1,0:T(8,128)(2,1)} %get-tuple-element.151.q_ref, bf16[4,1024,64]{2,1,0:T(8,128)(2,1)} %get-tuple-element.148.k_ref, bf16[4,1024,64]{2,1,0:T(8,128)(2,1)} %get-tuple-element.149.v_ref, s32[1024,1]{1,0:T(8,128)} %copy.103.start_ref), custom_call_target="tpu_custom_call" | custom-call | flops 113246208 | bytes 3145728 | tf_op jit(solution)/shard_map/attend/pallas_call | solution.py:707
  174.7 15.0 %attend.3 = bf16[1024,384]{1,0:T(8,128)(2,1)} custom-call(bf16[1024,768]{1,0:T(8,128)(2,1)} %get-tuple-element.151.q_ref, bf16[4,1024,64]{2,1,0:T(8,128)(2,1)} %get-tuple-element.148.k_ref, bf16[4,1024,64]{2,1,0:T(8,128)(2,1)} %get-tuple-element.149.v_ref, s32[1024,1]{1,0:T(8,128)} %copy.103.start_ref), custom_call_target="tpu_custom_call" | custom-call | flops 113246208 | bytes 3145728 | tf_op jit(solution)/shard_map/attend/pallas_call | solution.py:707
  203.4 7.3 collective-permute-done.15
  210.9 5.0 collective-permute-start.33
  221.9 9.7 %mix.1 = (f32[512,1536]{1,0:T(8,128)}, bf16[512,1536]{1,0:T(8,128)(2,1)}, bf16[2,768,1536]{2,1,0:T(8,128)(2,1)}) custom-call(s32[1]{0:T(128)} %bitcast.place_ref, bf16[512,768]{1,0:T(8,128)(2,1)} %get-tuple-element.342.mine_ref, bf16[512,768]{1,0:T(8,128)(2,1)} %copy-done.23, bf16[512,1536]{1,0:T(8,128)(2,1)} %x_ref.1, ...), custom_call_target="tpu_custom_call" | custom-call | flops 150994944 | bytes 786432 | tf_op jit(solution)/shard_map/mix/pallas_call | solution.py:588
  234.2 30.0 %collective-permute-done.21.refs_0_.refs_1_ = bf16[512,1536]{1,0:T(8,128)(2,1)S(1)} collective-permute-done((bf16[512,1536]{1,0:T(8,128)(2,1)}, bf16[512,1536]{1,0:T(8,128)(2,1)S(1)}, u32[]{:S(2)}, u32[]{:S(2)}) %collective-permute-start.21) | collective-permute-done | bytes 1572896 | tf_op jit(solution)/shard_map/ppermute | solution.py:373
  266.9 6.2 collective-permute-start.31
  274.6 9.2 %collective-permute-done.23.refs_2_ = bf16[256,1536]{1,0:T(8,128)(2,1)S(1)} collective-permute-done((bf16[256,1536]{1,0:T(8,128)(2,1)S(1)}, bf16[256,1536]{1,0:T(8,128)(2,1)S(1)}, u32[]{:S(2)}, u32[]{:S(2)}) %collective-permute-start.23) | collective-permute-done | bytes 786464 | tf_op jit(solution)/shard_map/ppermute | solution.py:377
  283.8 3.0 collective-permute-start.30
  288.0 4.8 collective-permute-done.32.refs_15_
  297.3 54.5 %experts.2 = (bf16[1024,1536]{1,0:T(8,128)(2,1)}, bf16[1024,1536]{1,0:T(8,128)(2,1)}, bf16[1024,1536]{1,0:T(8,128)(2,1)}, bf16[1024,1536]{1,0:T(8,128)(2,1)}, bf...) custom-call(s32[1]{0:T(128)} %bitcast.2.place_ref, ...), custom_call_target="tpu_custom_call" | custom-call | flops 2415919104 | bytes 50331648 | tf_op jit(solution)/shard_map/experts/pallas_call | solution.py:944
  352.8 7.8 %collective-permute-done.35 = bf16[1024,1536]{1,0:T(8,128)(2,1)S(1)} collective-permute-done((bf16[1024,1536]{1,0:T(8,128)(2,1)}, bf16[1024,1536]{1,0:T(8,128)(2,1)S(1)}, u32[]{:S(2)}, u32[]{:S(2)}) %collective-permute-start.35) | collective-permute-done | bytes 3145760 | tf_op jit(solution)/shard_map/ppermute | solution.py:377
  360.6 2.7 add_convert_fusion.1
  367.3 54.5 %experts.3 = (bf16[1024,1536]{1,0:T(8,128)(2,1)}, bf16[1024,1536]{1,0:T(8,128)(2,1)}, bf16[1024,1536]{1,0:T(8,128)(2,1)}, bf16[1024,1536]{1,0:T(8,128)(2,1)}, bf...) custom-call(s32[1]{0:T(128)} %bitcast.2.place_ref, ...), custom_call_target="tpu_custom_call", output_to_operand_aliasing={{4}: (21, {}), {5}: (22, {}), {6}: (23, {}), {7}: (24, {}),... | custom-call | flops 2415919104 | bytes 50331648 | tf_op jit(solution)/shard_map/experts/pallas_call | solution.py:944
  422.9 11.4 %fusion.11 = bf16[1536,512]{1,0:T(8,128)(2,1)S(1)} fusion(bf16[4096,1536]{1,0:T(8,128)(2,1)} %get-tuple-element.195, bf16[4096,512]{1,0:T(8,128)(2,1)} %get-tuple-element.188), kind=kOutput, calls=%fused_computation.37 | convolution fusion | flops 6444023808 | bytes 18350080 | tf_op jit(solution)/shard_map/dot_general | solution.py:668
  434.6 13.9 %convolution_convert_fusion.1 = bf16[1536,1024]{1,0:T(8,128)(2,1)S(1)} fusion(bf16[4096,1536]{1,0:T(8,128)(2,1)S(1)} %copy-done.15, bf16[4096,1024]{1,0:T(8,128)(2,1)S(1)} %copy-done.22), kind=kOutput, calls=%fused_computation.13 | convolution fusion | flops 12886474752 | bytes 24117248 | tf_op jit(solution)/shard_map/dot_general | solution.py:668
  450.6 5.6 collective-permute-start.45
  459.1 2.9 convert_add_fusion.1
  465.8 17.8 %convolution_convert_fusion = bf16[1536,1024]{1,0:T(8,128)(2,1)} fusion(bf16[4096,1536]{1,0:T(8,128)(2,1)S(1)} %copy-done.15, bf16[4096,1024]{1,0:T(8,128)(2,1)} %get-tuple-element.194), kind=kOutput, calls=%fused_computation.12 | convolution fusion | flops 12886474752 | bytes 24117248 | tf_op jit(solution)/shard_map/dot_general | solution.py:668
  488.3 5.5 fusion.42
  496.3 7.0 fusion.12
  506.9 3.1 fusion.45
  510.4 3.2 add_convert_fusion.6
  513.7 5.4 collective-permute-start.48
  519.1 3.4 add_convert_fusion.5
  524.0 2.8 add_convert_fusion
  534.5 7.2 fusion.38
  543.9 3.4 add_convert_fusion.7.d_ref
  547.3 45.3 %attend_back.1 = (bf16[1024,768]{1,0:T(8,128)(2,1)}, bf16[1024,256]{1,0:T(8,128)(2,1)}, bf16[1024,256]{1,0:T(8,128)(2,1)}) custom-call(bf16[1024,768]{1,0:T(8,128)(2,1)} %get-tuple-element.151.q_ref, bf16[4,1024,64]{2,1,0:T(8,128)(2,1)} %get-tuple-element.148.k_ref, bf16[4,1024,64]{2,1,0:T(8,128)(2,1)} %get-tuple-element.149.v_ref, ...), custom_call_target="tpu_custom_call" | custom-call | flops 566231040 | bytes 6291456 | tf_op jit(solution)/shard_map/attend_back/pallas_call | solution.py:775
  592.6 7.7 %add_convert_fusion.3 = (bf16[1536,768]{1,0:T(8,128)(2,1)}, bf16[1536,768]{1,0:T(8,128)(2,1)}) fusion(bf16[1536,768]{1,0:T(8,128)(2,1)} %collective-permute-done.49, pred[]{:T(512)S(6)} %lt.121, pred[]{:T(512)S(6)} %lt.120, bf16[1536,256]{1,0:T(8,128)(2,1)} %copy-done.12, bf16[1536,512]{1,0:T(8,128)(2,1)} %copy-done.3, bf16[1536,256]{1,0:T(8,128)(2,1)} %copy-done.14, ...), kind=kLoop, calls=%fused_computation.5 | loop fusion | flops 33030144 | bytes 18874372 | tf_op jit(solution)/shard_map/convert_element_type | solution.py:1249
  600.4 8.4 %qkv_grad.1 = bf16[2,2,2,4,48,1408]{5,4,3,2,1,0:T(8,128)(2,1)} custom-call(bf16[1024,1536]{1,0:T(8,128)(2,1)} %get-tuple-element.217.h_ref, bf16[1024,768]{1,0:T(8,128)(2,1)} %get-tuple-element.218.dq_ref, bf16[1024,256]{1,0:T(8,128)(2,1)} %get-tuple-element.219.dk_ref, bf16[1024,256]{1,0:T(8,128)(2,1)} %get-tuple-element.220.dv_ref, ...), custom_call_target="tpu_custom_call" | custom-call | flops 251658240 | bytes 1572864 | tf_op jit(solution)/shard_map/qkv_grad/pallas_call | solution.py:996
  610.7 2.6 collective-permute-start.54
  613.3 2.8 convert_add_fusion
  621.8 5.5 collective-permute-start.57
  630.7 6.5 collective-permute-done.52
  637.2 3.3 fusion.35
  644.5 11.0 %token_grad.1 = (bf16[512,1536]{1,0:T(8,128)(2,1)}, bf16[512,1536]{1,0:T(8,128)(2,1)}) custom-call(bf16[1024,768]{1,0:T(8,128)(2,1)} %get-tuple-element.218.dq_ref, bf16[1024,256]{1,0:T(8,128)(2,1)} %get-tuple-element.219.dk_ref, bf16[1024,256]{1,0:T(8,128)(2,1)} %get-tuple-element.220.dv_ref, bf16[1536,1280]{1,0:T(8,128)(2,1)} %get-tuple-element.221.w_ref, ...), custom_call_target="tpu_custom_call" | custom-call | flops 251658240 | bytes 1572864 | tf_op jit(solution)/shard_map/token_grad/pallas_call | solution.py:635
  657.4 3.7 collective-permute-done.58
  665.0 5.2 select_convert_fusion
  670.2 3.2 fusion.33
  673.7 8.3 %collective-permute-done.56 = bf16[2,4,48,1408]{3,2,1,0:T(8,128)(2,1)S(1)} collective-permute-done((bf16[2,4,48,1408]{3,2,1,0:T(8,128)(2,1)S(1)}, bf16[2,4,48,1408]{3,2,1,0:T(8,128)(2,1)S(1)}, u32[]{:S(2)}, u32[]{:S(2)}) %collective-permute-start.56) | collective-permute-done | bytes 1081376 | tf_op jit(solution)/shard_map/ppermute | solution.py:377
  683.5 3.1 collective-permute-done.59
  686.6 4.9 collective-permute-done.60
  691.5 4.4 fusion.16
  698.2 3.1 collective-permute-start.61
  703.2 5.8 collective-permute-start.64
  711.6 7.6 %collective-permute-done.62 = bf16[2,48,1408]{2,1,0:T(8,128)(2,1)S(1)} collective-permute-done((bf16[2,48,1408]{2,1,0:T(8,128)(2,1)S(1)}, bf16[2,48,1408]{2,1,0:T(8,128)(2,1)S(1)}, u32[]{:S(2)}, u32[]{:S(2)}) %collective-permute-start.62) | collective-permute-done | bytes 270368 | tf_op jit(solution)/shard_map/ppermute | solution.py:377
  721.9 4.2 fusion.5
  726.1 3.0 collective-permute-done.65
  729.1 6.4 collective-permute-done.64
  (347 shorter events, 166.0 us)
Async XLA Ops:
  7.2 214.8 %all-gather.2.cloned.1.call-start = ((), (), s32[]{:S(2)}) async-start(), calls=%async_computation.1 | async-start | bytes 5013504 | tf_op jit(solution)/shard_map/all_gather | solution.py:1107
  19.2 29.6 %collective-permute-start = (bf16[1536,512]{1,0:T(8,128)(2,1)S(1)}, bf16[1536,512]{1,0:T(8,128)(2,1)S(1)}, u32[]{:S(2)}, u32[]{:S(2)}) collective-permute-start(bf16[1536,512]{1,0:T(8,128)(2,1)S(1)} %pad_maximum_fusion.8), channel_id=1, source_target_pairs={{0,0},{1,16},{2,2},{3,18},{4,4},{5,20},{6,6},{7,22},{8,8},{9,24},{... | collective-permute-start | bytes 4718600 | tf_op jit(solution)/shard_map/ppermute | solution.py:1062
  21.7 27.1 %collective-permute-start.1 = (bf16[1536,256]{1,0:T(8,128)(2,1)}, bf16[1536,256]{1,0:T(8,128)(2,1)}, u32[]{:S(2)}, u32[]{:S(2)}) collective-permute-start(bf16[1536,256]{1,0:T(8,128)(2,1)} %get-tuple-element.338), channel_id=1, source_target_pairs={{0,1},{1,17},{2,3},{3,19},{4,5},{5,21},{6,7},{7,23},{8,9},{9,25},{... | collective-permute-start | bytes 2359304 | tf_op jit(solution)/shard_map/ppermute | solution.py:1062
  24.1 10.4 %collective-permute-start.3 = (bf16[48,2816]{1,0:T(8,128)(2,1)S(1)}, bf16[48,2816]{1,0:T(8,128)(2,1)}, u32[]{:S(2)}, u32[]{:S(2)}) collective-permute-start(bf16[48,2816]{1,0:T(8,128)(2,1)S(1)} %pad_maximum_fusion.16), channel_id=1, source_target_pairs={{0,4},{1,5},{2,6},{3,7},{4,0},{5,1},{6,2},{7,3},{8,12},{9,13},{10,... | collective-permute-start | bytes 811016 | tf_op jit(solution)/shard_map/ppermute | solution.py:377
  25.4 10.1 %collective-permute-start.4 = (bf16[48,2816]{1,0:T(8,128)(2,1)S(1)}, bf16[48,2816]{1,0:T(8,128)(2,1)}, u32[]{:S(2)}, u32[]{:S(2)}) collective-permute-start(bf16[48,2816]{1,0:T(8,128)(2,1)S(1)} %pad_maximum_fusion.16), channel_id=1, source_target_pairs={{0,8},{1,9},{2,10},{3,11},{4,12},{5,13},{6,14},{7,15},{8,0},{9,1},... | collective-permute-start | bytes 811016 | tf_op jit(solution)/shard_map/ppermute | solution.py:377
  27.8 16.6 %collective-permute-start.5 = (bf16[48,2816]{1,0:T(8,128)(2,1)S(1)}, bf16[48,2816]{1,0:T(8,128)(2,1)}, u32[]{:S(2)}, u32[]{:S(2)}) collective-permute-start(bf16[48,2816]{1,0:T(8,128)(2,1)S(1)} %pad_maximum_fusion.16), channel_id=1, source_target_pairs={{0,12},{1,13},{2,14},{3,15},{4,8},{5,9},{6,10},{7,11},{8,4},{9,5},... | collective-permute-start | bytes 811016 | tf_op jit(solution)/shard_map/ppermute | solution.py:377
  50.3 633.2 %reduce-scatter.2.cloned.1.call-start = ((), (), s32[]{:S(2)}) async-start(), calls=%async_computation.2 | async-start | bytes 4866048 | tf_op jit(solution)/shard_map/reduce_scatter | solution.py:1288
  52.5 35.9 %collective-permute-start.8 = (bf16[768,768]{1,0:T(8,128)(2,1)}, bf16[768,768]{1,0:T(8,128)(2,1)}, u32[]{:S(2)}, u32[]{:S(2)}) collective-permute-start(bf16[768,768]{1,0:T(8,128)(2,1)} %get-tuple-element.327), channel_id=1, source_target_pairs={{0,4},{1,5},{2,6},{3,7},{4,8},{5,9},{6,10},{7,11},{8,12},{9,13},{1... | collective-permute-start | bytes 3538952 | tf_op jit(solution)/shard_map/ppermute | solution.py:389
  57.0 44.1 %collective-permute-start.9 = (bf16[768,768]{1,0:T(8,128)(2,1)}, bf16[768,768]{1,0:T(8,128)(2,1)}, u32[]{:S(2)}, u32[]{:S(2)}) collective-permute-start(bf16[768,768]{1,0:T(8,128)(2,1)} %get-tuple-element.327), channel_id=1, source_target_pairs={{4,0},{5,1},{6,2},{7,3},{8,4},{9,5},{10,6},{11,7},{12,8},{13,9},{1... | collective-permute-start | bytes 3538952 | tf_op jit(solution)/shard_map/ppermute | solution.py:393
  60.5 27.9 %collective-permute-start.7 = (bf16[192,2816]{1,0:T(8,128)(2,1)}, bf16[192,2816]{1,0:T(8,128)(2,1)}, u32[]{:S(2)}, u32[]{:S(2)}) collective-permute-start(bf16[192,2816]{1,0:T(8,128)(2,1)} %pad_maximum_fusion.9), channel_id=1, source_target_pairs={{0,2},{1,3},{2,0},{3,1},{4,6},{5,7},{6,4},{7,5},{8,10},{9,11},{10,... | collective-permute-start | bytes 3244040 | tf_op jit(solution)/shard_map/ppermute | solution.py:377
  67.9 106.8 %collective-permute-start.14 = (bf16[512,1664]{1,0:T(8,128)(2,1)}, bf16[512,1664]{1,0:T(8,128)(2,1)}, u32[]{:S(2)}, u32[]{:S(2)}) collective-permute-start(bf16[512,1664]{1,0:T(8,128)(2,1)} %concatenate.115.refs_6_), channel_id=1, source_target_pairs={{0,2},{1,3},{2,0},{3,1},{4,6},{5,7},{6,4},{7,5},{8,10},{9,11},{10,... | collective-permute-start | bytes 5111816 | tf_op jit(solution)/shard_map/ppermute | solution.py:377
  68.1 50.9 %collective-permute-start.6 = (bf16[512,1536]{1,0:T(8,128)(2,1)S(1)}, bf16[512,1536]{1,0:T(8,128)(2,1)}, u32[]{:S(2)}, u32[]{:S(2)}) collective-permute-start(bf16[512,1536]{1,0:T(8,128)(2,1)S(1)} %copy-done.8), channel_id=1, source_target_pairs={{0,16},{16,0},{1,17},{17,1},{2,18},{18,2},{3,19},{19,3},{4,20},{20... | collective-permute-start | bytes 4718600 | tf_op jit(solution)/shard_map/ppermute | solution.py:373
  103.4 22.7 %collective-permute-start.10 = (bf16[384,2816]{1,0:T(8,128)(2,1)}, bf16[384,2816]{1,0:T(8,128)(2,1)}, u32[]{:S(2)}, u32[]{:S(2)}) collective-permute-start(bf16[384,2816]{1,0:T(8,128)(2,1)} %constant_dynamic-update-slice_fusion.2.own_ref), channel_id=1, source_target_pairs={{0,1},{1,0},{2,3},{3,2},{4,5},{5,4},{6,7},{7,6},{8,9},{9,8},{10,11... | collective-permute-start | bytes 6488072 | tf_op jit(solution)/shard_map/ppermute | solution.py:377
  113.0 33.4 %collective-permute-start.11 = (bf16[768,768]{1,0:T(8,128)(2,1)}, bf16[768,768]{1,0:T(8,128)(2,1)S(1)}, u32[]{:S(2)}, u32[]{:S(2)}) collective-permute-start(bf16[768,768]{1,0:T(8,128)(2,1)} %get-tuple-element.143), channel_id=1, source_target_pairs={{0,4},{1,5},{2,6},{3,7},{4,8},{5,9},{6,10},{7,11},{8,12},{9,13},{1... | collective-permute-start | bytes 3538952 | tf_op jit(solution)/shard_map/ppermute | solution.py:389
  114.5 36.3 %collective-permute-start.12 = (bf16[768,768]{1,0:T(8,128)(2,1)}, bf16[768,768]{1,0:T(8,128)(2,1)}, u32[]{:S(2)}, u32[]{:S(2)}) collective-permute-start(bf16[768,768]{1,0:T(8,128)(2,1)} %get-tuple-element.143), channel_id=1, source_target_pairs={{4,0},{5,1},{6,2},{7,3},{8,4},{9,5},{10,6},{11,7},{12,8},{13,9},{1... | collective-permute-start | bytes 3538952 | tf_op jit(solution)/shard_map/ppermute | solution.py:393
  119.0 55.6 %collective-permute-start.13 = (bf16[512,1664]{1,0:T(8,128)(2,1)}, bf16[512,1664]{1,0:T(8,128)(2,1)}, u32[]{:S(2)}, u32[]{:S(2)}) collective-permute-start(bf16[512,1664]{1,0:T(8,128)(2,1)} %concatenate.115.refs_6_), channel_id=1, source_target_pairs={{0,16},{16,0},{1,17},{17,1},{2,18},{18,2},{3,19},{19,3},{4,20},{20... | collective-permute-start | bytes 5111816 | tf_op jit(solution)/shard_map/ppermute | solution.py:373
  154.1 56.7 %collective-permute-start.17 = (bf16[1536,768]{1,0:T(8,128)(2,1)S(1)}, bf16[1536,768]{1,0:T(8,128)(2,1)}, u32[]{:S(2)}, u32[]{:S(2)}) collective-permute-start(bf16[1536,768]{1,0:T(8,128)(2,1)S(1)} %get-tuple-element.152.refs_18_.refs_14_), channel_id=1, source_target_pairs={{0,4},{1,5},{2,6},{3,7},{4,8},{5,9},{6,10},{7,11},{8,12},{9,13},{1... | collective-permute-start | bytes 7077896 | tf_op jit(solution)/shard_map/ppermute | solution.py:389
  157.1 53.8 %collective-permute-start.18 = (bf16[1536,768]{1,0:T(8,128)(2,1)}, bf16[1536,768]{1,0:T(8,128)(2,1)}, u32[]{:S(2)}, u32[]{:S(2)}) collective-permute-start(bf16[1536,768]{1,0:T(8,128)(2,1)} %get-tuple-element.153.refs_20_.refs_16_), channel_id=1, source_target_pairs={{4,0},{5,1},{6,2},{7,3},{8,4},{9,5},{10,6},{11,7},{12,8},{13,9},{1... | collective-permute-start | bytes 7077896 | tf_op jit(solution)/shard_map/ppermute | solution.py:393
  191.7 10.6 %collective-permute-start.16 = (bf16[512,384]{1,0:T(8,128)(2,1)S(1)}, bf16[512,384]{1,0:T(8,128)(2,1)S(1)}, u32[]{:S(2)}, u32[]{:S(2)}) collective-permute-start(bf16[512,384]{1,0:T(8,128)(2,1)S(1)} %fusion.51), channel_id=1, source_target_pairs={{0,16},{16,0},{1,17},{17,1},{2,18},{18,2},{3,19},{19,3},{4,20},{20... | collective-permute-start | bytes 1179656 | tf_op jit(solution)/shard_map/ppermute | solution.py:373
  194.5 16.2 %collective-permute-start.15 = (bf16[512,384]{1,0:T(8,128)(2,1)S(1)}, bf16[512,384]{1,0:T(8,128)(2,1)S(1)}, u32[]{:S(2)}, u32[]{:S(2)}) collective-permute-start(bf16[512,384]{1,0:T(8,128)(2,1)S(1)} %fusion.50), channel_id=1, source_target_pairs={{0,16},{16,0},{1,17},{17,1},{2,18},{18,2},{3,19},{19,3},{4,20},{20... | collective-permute-start | bytes 1179656 | tf_op jit(solution)/shard_map/ppermute | solution.py:373
  196.7 34.9 %collective-permute-start.19 = (bf16[256,1664]{1,0:T(8,128)(2,1)}, bf16[256,1664]{1,0:T(8,128)(2,1)}, u32[]{:S(2)}, u32[]{:S(2)}) collective-permute-start(bf16[256,1664]{1,0:T(8,128)(2,1)} %slice.197), channel_id=1, source_target_pairs={{0,2},{1,3},{2,0},{3,1},{4,6},{5,7},{6,4},{7,5},{8,10},{9,11},{10,... | collective-permute-start | bytes 2555912 | tf_op jit(solution)/shard_map/ppermute | solution.py:377
  202.3 29.4 %collective-permute-start.20 = (bf16[256,1664]{1,0:T(8,128)(2,1)}, bf16[256,1664]{1,0:T(8,128)(2,1)}, u32[]{:S(2)}, u32[]{:S(2)}) collective-permute-start(bf16[256,1664]{1,0:T(8,128)(2,1)} %slice.198), channel_id=1, source_target_pairs={{0,16},{16,0},{1,17},{17,1},{2,18},{18,2},{3,19},{19,3},{4,20},{20... | collective-permute-start | bytes 2555912 | tf_op jit(solution)/shard_map/ppermute | solution.py:373
  210.9 62.2 %collective-permute-start.33 = (bf16[1536,768]{1,0:T(8,128)(2,1)}, bf16[1536,768]{1,0:T(8,128)(2,1)}, u32[]{:S(2)}, u32[]{:S(2)}) collective-permute-start(bf16[1536,768]{1,0:T(8,128)(2,1)} %collective-permute-done.17.refs_17_.refs_13_), channel_id=1, source_target_pairs={{0,4},{1,5},{2,6},{3,7},{4,8},{5,9},{6,10},{7,11},{8,12},{9,13},{1... | collective-permute-start | bytes 7077896 | tf_op jit(solution)/shard_map/ppermute | solution.py:389
  218.7 54.4 %collective-permute-start.34 = (bf16[1536,768]{1,0:T(8,128)(2,1)}, bf16[1536,768]{1,0:T(8,128)(2,1)}, u32[]{:S(2)}, u32[]{:S(2)}) collective-permute-start(bf16[1536,768]{1,0:T(8,128)(2,1)} %collective-permute-done.18.refs_21_.refs_17_), channel_id=1, source_target_pairs={{4,0},{5,1},{6,2},{7,3},{8,4},{9,5},{10,6},{11,7},{12,8},{13,9},{1... | collective-permute-start | bytes 7077896 | tf_op jit(solution)/shard_map/ppermute | solution.py:393
  231.7 32.5 %collective-permute-start.21 = (bf16[512,1536]{1,0:T(8,128)(2,1)}, bf16[512,1536]{1,0:T(8,128)(2,1)S(1)}, u32[]{:S(2)}, u32[]{:S(2)}) collective-permute-start(bf16[512,1536]{1,0:T(8,128)(2,1)} %get-tuple-element.161.refs_0_), channel_id=1, source_target_pairs={{0,16},{16,0},{1,17},{17,1},{2,18},{18,2},{3,19},{19,3},{4,20},{20... | collective-permute-start | bytes 4718600 | tf_op jit(solution)/shard_map/ppermute | solution.py:373
  232.9 32.6 %collective-permute-start.22 = (bf16[512,1536]{1,0:T(8,128)(2,1)}, bf16[512,1536]{1,0:T(8,128)(2,1)S(1)}, u32[]{:S(2)}, u32[]{:S(2)}) collective-permute-start(bf16[512,1536]{1,0:T(8,128)(2,1)} %get-tuple-element.161.refs_0_), channel_id=1, source_target_pairs={{0,2},{1,3},{2,0},{3,1},{4,6},{5,7},{6,4},{7,5},{8,10},{9,11},{10,... | collective-permute-start | bytes 4718600 | tf_op jit(solution)/shard_map/ppermute | solution.py:377
  264.3 19.6 %collective-permute-start.23 = (bf16[256,1536]{1,0:T(8,128)(2,1)S(1)}, bf16[256,1536]{1,0:T(8,128)(2,1)S(1)}, u32[]{:S(2)}, u32[]{:S(2)}) collective-permute-start(bf16[256,1536]{1,0:T(8,128)(2,1)S(1)} %slice.253), channel_id=1, source_target_pairs={{0,2},{1,3},{2,0},{3,1},{4,6},{5,7},{6,4},{7,5},{8,10},{9,11},{10,... | collective-permute-start | bytes 2359304 | tf_op jit(solution)/shard_map/ppermute | solution.py:377
  265.6 21.2 %collective-permute-start.24 = (bf16[256,1536]{1,0:T(8,128)(2,1)S(1)}, bf16[256,1536]{1,0:T(8,128)(2,1)S(1)}, u32[]{:S(2)}, u32[]{:S(2)}) collective-permute-start(bf16[256,1536]{1,0:T(8,128)(2,1)S(1)} %slice.254), channel_id=1, source_target_pairs={{0,16},{16,0},{1,17},{17,1},{2,18},{18,2},{3,19},{19,3},{4,20},{20... | collective-permute-start | bytes 2359304 | tf_op jit(solution)/shard_map/ppermute | solution.py:373
  266.9 20.0 %collective-permute-start.31 = (bf16[256,1664]{1,0:T(8,128)(2,1)}, bf16[256,1664]{1,0:T(8,128)(2,1)}, u32[]{:S(2)}, u32[]{:S(2)}) collective-permute-start(bf16[256,1664]{1,0:T(8,128)(2,1)} %collective-permute-done.19.refs_10_), channel_id=1, source_target_pairs={{0,1},{1,0},{2,3},{3,2},{4,5},{5,4},{6,7},{7,6},{8,9},{9,8},{10,11... | collective-permute-start | bytes 2555912 | tf_op jit(solution)/shard_map/ppermute | solution.py:377
  273.1 20.1 %collective-permute-start.25 = (bf16[512,1536]{1,0:T(8,128)(2,1)S(1)}, bf16[512,1536]{1,0:T(8,128)(2,1)}, u32[]{:S(2)}, u32[]{:S(2)}) collective-permute-start(bf16[512,1536]{1,0:T(8,128)(2,1)S(1)} %collective-permute-done.21.refs_0_.refs_1_), channel_id=1, source_target_pairs={{0,1},{1,0},{2,3},{3,2},{4,5},{5,4},{6,7},{7,6},{8,9},{9,8},{10,11... | collective-permute-start | bytes 4718600 | tf_op jit(solution)/shard_map/ppermute | solution.py:377
  273.1 24.2 %collective-permute-start.29 = (bf16[512,1664]{1,0:T(8,128)(2,1)}, bf16[512,1664]{1,0:T(8,128)(2,1)}, u32[]{:S(2)}, u32[]{:S(2)}) collective-permute-start(bf16[512,1664]{1,0:T(8,128)(2,1)} %collective-permute-done.13.refs_8_.refs_7_), channel_id=1, source_target_pairs={{0,1},{1,0},{2,3},{3,2},{4,5},{5,4},{6,7},{7,6},{8,9},{9,8},{10,11... | collective-permute-start | bytes 5111816 | tf_op jit(solution)/shard_map/ppermute | solution.py:377
  283.8 13.5 %collective-permute-start.30 = (bf16[512,1664]{1,0:T(8,128)(2,1)}, bf16[512,1664]{1,0:T(8,128)(2,1)}, u32[]{:S(2)}, u32[]{:S(2)}) collective-permute-start(bf16[512,1664]{1,0:T(8,128)(2,1)} %collective-permute-done.14.refs_9_.refs_8_), channel_id=1, source_target_pairs={{0,1},{1,0},{2,3},{3,2},{4,5},{5,4},{6,7},{7,6},{8,9},{9,8},{10,11... | collective-permute-start | bytes 5111816 | tf_op jit(solution)/shard_map/ppermute | solution.py:377
  287.7 9.6 %collective-permute-start.26 = (bf16[512,1536]{1,0:T(8,128)(2,1)S(1)}, bf16[512,1536]{1,0:T(8,128)(2,1)}, u32[]{:S(2)}, u32[]{:S(2)}) collective-permute-start(bf16[512,1536]{1,0:T(8,128)(2,1)S(1)} %collective-permute-done.22.refs_1_.refs_2_), channel_id=1, source_target_pairs={{0,1},{1,0},{2,3},{3,2},{4,5},{5,4},{6,7},{7,6},{8,9},{9,8},{10,11... | collective-permute-start | bytes 4718600 | tf_op jit(solution)/shard_map/ppermute | solution.py:377
  351.9 8.8 %collective-permute-start.35 = (bf16[1024,1536]{1,0:T(8,128)(2,1)}, bf16[1024,1536]{1,0:T(8,128)(2,1)S(1)}, u32[]{:S(2)}, u32[]{:S(2)}) collective-permute-start(bf16[1024,1536]{1,0:T(8,128)(2,1)} %get-tuple-element.171), channel_id=1, source_target_pairs={{0,1},{1,0},{2,3},{3,2},{4,5},{5,4},{6,7},{7,6},{8,9},{9,8},{10,11... | collective-permute-start | bytes 9437192 | tf_op jit(solution)/shard_map/ppermute | solution.py:377
  352.3 15.0 %collective-permute-start.36 = (bf16[512,1536]{1,0:T(8,128)(2,1)}, bf16[512,1536]{1,0:T(8,128)(2,1)}, u32[]{:S(2)}, u32[]{:S(2)}) collective-permute-start(bf16[512,1536]{1,0:T(8,128)(2,1)} %get-tuple-element.161.refs_0_), channel_id=1, source_target_pairs={{0,1},{1,0},{2,3},{3,2},{4,5},{5,4},{6,7},{7,6},{8,9},{9,8},{10,11... | collective-permute-start | bytes 4718600 | tf_op jit(solution)/shard_map/ppermute | solution.py:377
  352.5 14.9 %collective-permute-start.37 = (bf16[512,1664]{1,0:T(8,128)(2,1)}, bf16[512,1664]{1,0:T(8,128)(2,1)}, u32[]{:S(2)}, u32[]{:S(2)}) collective-permute-start(bf16[512,1664]{1,0:T(8,128)(2,1)} %concatenate.115.refs_6_), channel_id=1, source_target_pairs={{0,1},{1,0},{2,3},{3,2},{4,5},{5,4},{6,7},{7,6},{8,9},{9,8},{10,11... | collective-permute-start | bytes 5111816 | tf_op jit(solution)/shard_map/ppermute | solution.py:377
  365.2 57.6 %collective-permute-start.38 = (bf16[512,1536]{1,0:T(8,128)(2,1)}, bf16[512,1536]{1,0:T(8,128)(2,1)}, u32[]{:S(2)}, u32[]{:S(2)}) collective-permute-start(bf16[512,1536]{1,0:T(8,128)(2,1)} %get-tuple-element.317), channel_id=1, source_target_pairs={{0,2},{1,3},{2,0},{3,1},{4,6},{5,7},{6,4},{7,5},{8,10},{9,11},{10,... | collective-permute-start | bytes 4718600 | tf_op jit(solution)/shard_map/ppermute | solution.py:377
  366.8 56.1 %collective-permute-start.39 = (bf16[512,1536]{1,0:T(8,128)(2,1)}, bf16[512,1536]{1,0:T(8,128)(2,1)}, u32[]{:S(2)}, u32[]{:S(2)}) collective-permute-start(bf16[512,1536]{1,0:T(8,128)(2,1)} %get-tuple-element.316), channel_id=1, source_target_pairs={{0,16},{16,0},{1,17},{17,1},{2,18},{18,2},{3,19},{19,3},{4,20},{20... | collective-permute-start | bytes 4718600 | tf_op jit(solution)/shard_map/ppermute | solution.py:373
  421.8 37.3 %collective-permute-start.40 = (bf16[1024,1536]{1,0:T(8,128)(2,1)}, bf16[1024,1536]{1,0:T(8,128)(2,1)}, u32[]{:S(2)}, u32[]{:S(2)}) collective-permute-start(bf16[1024,1536]{1,0:T(8,128)(2,1)} %get-tuple-element.190), channel_id=1, source_target_pairs={{0,1},{1,0},{2,3},{3,2},{4,5},{5,4},{6,7},{7,6},{8,9},{9,8},{10,11... | collective-permute-start | bytes 9437192 | tf_op jit(solution)/shard_map/ppermute | solution.py:377
  450.6 59.9 %collective-permute-start.45 = (bf16[1536,768]{1,0:T(8,128)(2,1)}, bf16[1536,768]{1,0:T(8,128)(2,1)}, u32[]{:S(2)}, u32[]{:S(2)}) collective-permute-start(bf16[1536,768]{1,0:T(8,128)(2,1)} %pad_maximum_fusion.5), channel_id=1, source_target_pairs={{0,4},{1,5},{2,6},{3,7},{4,8},{5,9},{6,10},{7,11},{8,12},{9,13},{1... | collective-permute-start | bytes 7077896 | tf_op jit(solution)/shard_map/ppermute | solution.py:389
  457.7 61.4 %collective-permute-start.46 = (bf16[1536,768]{1,0:T(8,128)(2,1)}, bf16[1536,768]{1,0:T(8,128)(2,1)}, u32[]{:S(2)}, u32[]{:S(2)}) collective-permute-start(bf16[1536,768]{1,0:T(8,128)(2,1)} %pad_maximum_fusion.4), channel_id=1, source_target_pairs={{4,0},{5,1},{6,2},{7,3},{8,4},{9,5},{10,6},{11,7},{12,8},{13,9},{1... | collective-permute-start | bytes 7077896 | tf_op jit(solution)/shard_map/ppermute | solution.py:393
  464.0 19.6 %collective-permute-start.41 = (bf16[256,1536]{1,0:T(8,128)(2,1)S(1)}, bf16[256,1536]{1,0:T(8,128)(2,1)S(1)}, u32[]{:S(2)}, u32[]{:S(2)}) collective-permute-start(bf16[256,1536]{1,0:T(8,128)(2,1)S(1)} %get-tuple-element.304), channel_id=1, source_target_pairs={{0,16},{16,0},{1,17},{17,1},{2,18},{18,2},{3,19},{19,3},{4,20},{20... | collective-permute-start | bytes 2359304 | tf_op jit(solution)/shard_map/ppermute | solution.py:373
  465.2 18.6 %collective-permute-start.42 = (bf16[256,1536]{1,0:T(8,128)(2,1)S(1)}, bf16[256,1536]{1,0:T(8,128)(2,1)S(1)}, u32[]{:S(2)}, u32[]{:S(2)}) collective-permute-start(bf16[256,1536]{1,0:T(8,128)(2,1)S(1)} %get-tuple-element.305), channel_id=1, source_target_pairs={{0,2},{1,3},{2,0},{3,1},{4,6},{5,7},{6,4},{7,5},{8,10},{9,11},{10,... | collective-permute-start | bytes 2359304 | tf_op jit(solution)/shard_map/ppermute | solution.py:377
  493.8 30.1 %collective-permute-start.47 = (bf16[1024,1536]{1,0:T(8,128)(2,1)S(1)}, bf16[1024,1536]{1,0:T(8,128)(2,1)}, u32[]{:S(2)}, u32[]{:S(2)}) collective-permute-start(bf16[1024,1536]{1,0:T(8,128)(2,1)S(1)} %copy-done.52), channel_id=1, source_target_pairs={{0,1},{1,0},{2,3},{3,2},{4,5},{5,4},{6,7},{7,6},{8,9},{9,8},{10,11... | collective-permute-start | bytes 9437192 | tf_op jit(solution)/shard_map/ppermute | solution.py:377
  505.5 107.7 %collective-permute-start.43 = (bf16[1024,1536]{1,0:T(8,128)(2,1)}, bf16[1024,1536]{1,0:T(8,128)(2,1)}, u32[]{:S(2)}, u32[]{:S(2)}) collective-permute-start(bf16[1024,1536]{1,0:T(8,128)(2,1)} %get-tuple-element.200), channel_id=1, source_target_pairs={{0,1},{1,0},{2,3},{3,2},{4,5},{5,4},{6,7},{7,6},{8,9},{9,8},{10,11... | collective-permute-start | bytes 9437192 | tf_op jit(solution)/shard_map/ppermute | solution.py:377
  510.1 19.1 %collective-permute-start.44 = (bf16[512,768]{1,0:T(8,128)(2,1)S(1)}, bf16[512,768]{1,0:T(8,128)(2,1)}, u32[]{:S(2)}, u32[]{:S(2)}) collective-permute-start(bf16[512,768]{1,0:T(8,128)(2,1)S(1)} %fusion.45), channel_id=1, source_target_pairs={{0,16},{16,0},{1,17},{17,1},{2,18},{18,2},{3,19},{19,3},{4,20},{20... | collective-permute-start | bytes 2359304 | tf_op jit(solution)/shard_map/ppermute | solution.py:373
  513.7 78.9 %collective-permute-start.48 = (bf16[1536,768]{1,0:T(8,128)(2,1)}, bf16[1536,768]{1,0:T(8,128)(2,1)}, u32[]{:S(2)}, u32[]{:S(2)}) collective-permute-start(bf16[1536,768]{1,0:T(8,128)(2,1)} %add_convert_fusion.6), channel_id=1, source_target_pairs={{0,4},{1,5},{2,6},{3,7},{4,8},{5,9},{6,10},{7,11},{8,12},{9,13},{1... | collective-permute-start | bytes 7077896 | tf_op jit(solution)/shard_map/ppermute | solution.py:389
  522.5 70.1 %collective-permute-start.49 = (bf16[1536,768]{1,0:T(8,128)(2,1)}, bf16[1536,768]{1,0:T(8,128)(2,1)}, u32[]{:S(2)}, u32[]{:S(2)}) collective-permute-start(bf16[1536,768]{1,0:T(8,128)(2,1)} %add_convert_fusion.5), channel_id=1, source_target_pairs={{4,0},{5,1},{6,2},{7,3},{8,4},{9,5},{10,6},{11,7},{12,8},{13,9},{1... | collective-permute-start | bytes 7077896 | tf_op jit(solution)/shard_map/ppermute | solution.py:393
  528.7 64.0 %collective-permute-start.50 = (bf16[512,1536]{1,0:T(8,128)(2,1)}, bf16[512,1536]{1,0:T(8,128)(2,1)}, u32[]{:S(2)}, u32[]{:S(2)}) collective-permute-start(bf16[512,1536]{1,0:T(8,128)(2,1)} %get-tuple-element.311), channel_id=1, source_target_pairs={{0,2},{1,3},{2,0},{3,1},{4,6},{5,7},{6,4},{7,5},{8,10},{9,11},{10,... | collective-permute-start | bytes 4718600 | tf_op jit(solution)/shard_map/ppermute | solution.py:377
  529.2 63.4 %collective-permute-start.51 = (bf16[512,1536]{1,0:T(8,128)(2,1)}, bf16[512,1536]{1,0:T(8,128)(2,1)}, u32[]{:S(2)}, u32[]{:S(2)}) collective-permute-start(bf16[512,1536]{1,0:T(8,128)(2,1)} %get-tuple-element.310), channel_id=1, source_target_pairs={{0,16},{16,0},{1,17},{17,1},{2,18},{18,2},{3,19},{19,3},{4,20},{20... | collective-permute-start | bytes 4718600 | tf_op jit(solution)/shard_map/ppermute | solution.py:373
  610.7 31.3 %collective-permute-start.54 = (bf16[2,2,4,48,1408]{4,3,2,1,0:T(8,128)(2,1)S(1)}, bf16[2,2,4,48,1408]{4,3,2,1,0:T(8,128)(2,1)S(1)}, u32[]{:S(2)}, u32[]{:S(2)}) collective-permute-start(bf16[2,2,4,48,1408]{4,3,2,1,0:T(8,128)(2,1)S(1)} %dynamic-slice_bitcast_fusion), channel_id=1, source_target_pairs={{0,1},{1,0},{2,3},{3,2},{4,5},{5,4},{6,7},{7,6},{8,9},{9,8},{10,11... | collective-permute-start | bytes 6488072 | tf_op jit(solution)/shard_map/ppermute | solution.py:377
  618.2 19.0 %collective-permute-start.52 = (bf16[256,1536]{1,0:T(8,128)(2,1)S(1)}, bf16[256,1536]{1,0:T(8,128)(2,1)S(1)}, u32[]{:S(2)}, u32[]{:S(2)}) collective-permute-start(bf16[256,1536]{1,0:T(8,128)(2,1)S(1)} %fusion.34), channel_id=1, source_target_pairs={{0,16},{16,0},{1,17},{17,1},{2,18},{18,2},{3,19},{19,3},{4,20},{20... | collective-permute-start | bytes 2359304 | tf_op jit(solution)/shard_map/ppermute | solution.py:373
  621.8 35.6 %collective-permute-start.57 = (bf16[768,768]{1,0:T(8,128)(2,1)}, bf16[768,768]{1,0:T(8,128)(2,1)}, u32[]{:S(2)}, u32[]{:S(2)}) collective-permute-start(bf16[768,768]{1,0:T(8,128)(2,1)} %get-tuple-element.325), channel_id=1, source_target_pairs={{0,4},{1,5},{2,6},{3,7},{4,8},{5,9},{6,10},{7,11},{8,12},{9,13},{1... | collective-permute-start | bytes 3538952 | tf_op jit(solution)/shard_map/ppermute | solution.py:389
  628.9 32.3 %collective-permute-start.58 = (bf16[768,768]{1,0:T(8,128)(2,1)}, bf16[768,768]{1,0:T(8,128)(2,1)}, u32[]{:S(2)}, u32[]{:S(2)}) collective-permute-start(bf16[768,768]{1,0:T(8,128)(2,1)} %get-tuple-element.323), channel_id=1, source_target_pairs={{4,0},{5,1},{6,2},{7,3},{8,4},{9,5},{10,6},{11,7},{12,8},{13,9},{1... | collective-permute-start | bytes 3538952 | tf_op jit(solution)/shard_map/ppermute | solution.py:393
  640.5 29.7 %collective-permute-start.53 = (bf16[256,1536]{1,0:T(8,128)(2,1)}, bf16[256,1536]{1,0:T(8,128)(2,1)}, u32[]{:S(2)}, u32[]{:S(2)}) collective-permute-start(bf16[256,1536]{1,0:T(8,128)(2,1)} %get-tuple-element.301), channel_id=1, source_target_pairs={{0,2},{1,3},{2,0},{3,1},{4,6},{5,7},{6,4},{7,5},{8,10},{9,11},{10,... | collective-permute-start | bytes 2359304 | tf_op jit(solution)/shard_map/ppermute | solution.py:377
  657.3 24.6 %collective-permute-start.56 = (bf16[2,4,48,1408]{3,2,1,0:T(8,128)(2,1)S(1)}, bf16[2,4,48,1408]{3,2,1,0:T(8,128)(2,1)S(1)}, u32[]{:S(2)}, u32[]{:S(2)}) collective-permute-start(bf16[2,4,48,1408]{3,2,1,0:T(8,128)(2,1)S(1)} %fusion.52), channel_id=1, source_target_pairs={{0,2},{1,3},{2,0},{3,1},{4,6},{5,7},{6,4},{7,5},{8,10},{9,11},{10,... | collective-permute-start | bytes 3244040 | tf_op jit(solution)/shard_map/ppermute | solution.py:377
  661.2 25.4 %collective-permute-start.59 = (bf16[768,768]{1,0:T(8,128)(2,1)}, bf16[768,768]{1,0:T(8,128)(2,1)}, u32[]{:S(2)}, u32[]{:S(2)}) collective-permute-start(bf16[768,768]{1,0:T(8,128)(2,1)} %get-tuple-element.226), channel_id=1, source_target_pairs={{0,4},{1,5},{2,6},{3,7},{4,8},{5,9},{6,10},{7,11},{8,12},{9,13},{1... | collective-permute-start | bytes 3538952 | tf_op jit(solution)/shard_map/ppermute | solution.py:389
  663.7 27.8 %collective-permute-start.60 = (bf16[768,768]{1,0:T(8,128)(2,1)}, bf16[768,768]{1,0:T(8,128)(2,1)}, u32[]{:S(2)}, u32[]{:S(2)}) collective-permute-start(bf16[768,768]{1,0:T(8,128)(2,1)} %get-tuple-element.227), channel_id=1, source_target_pairs={{4,0},{5,1},{6,2},{7,3},{8,4},{9,5},{10,6},{11,7},{12,8},{13,9},{1... | collective-permute-start | bytes 3538952 | tf_op jit(solution)/shard_map/ppermute | solution.py:393
  673.5 45.9 %collective-permute-start.55 = (bf16[512,1536]{1,0:T(8,128)(2,1)}, bf16[512,1536]{1,0:T(8,128)(2,1)}, u32[]{:S(2)}, u32[]{:S(2)}) collective-permute-start(bf16[512,1536]{1,0:T(8,128)(2,1)} %get-tuple-element.224), channel_id=1, source_target_pairs={{0,16},{16,0},{1,17},{17,1},{2,18},{18,2},{3,19},{19,3},{4,20},{20... | collective-permute-start | bytes 4718600 | tf_op jit(solution)/shard_map/ppermute | solution.py:373
  697.5 12.2 %collective-permute-start.63 = (bf16[2,48,1408]{2,1,0:T(8,128)(2,1)S(1)}, bf16[2,48,1408]{2,1,0:T(8,128)(2,1)S(1)}, u32[]{:S(2)}, u32[]{:S(2)}) collective-permute-start(bf16[2,48,1408]{2,1,0:T(8,128)(2,1)S(1)} %fusion.65), channel_id=1, source_target_pairs={{0,12},{1,13},{2,14},{3,15},{4,8},{5,9},{6,10},{7,11},{8,4},{9,5},... | collective-permute-start | bytes 811016 | tf_op jit(solution)/shard_map/ppermute | solution.py:377
  697.7 21.5 %collective-permute-start.62 = (bf16[2,48,1408]{2,1,0:T(8,128)(2,1)S(1)}, bf16[2,48,1408]{2,1,0:T(8,128)(2,1)S(1)}, u32[]{:S(2)}, u32[]{:S(2)}) collective-permute-start(bf16[2,48,1408]{2,1,0:T(8,128)(2,1)S(1)} %get-tuple-element.341), channel_id=1, source_target_pairs={{0,8},{1,9},{2,10},{3,11},{4,12},{5,13},{6,14},{7,15},{8,0},{9,1},... | collective-permute-start | bytes 811016 | tf_op jit(solution)/shard_map/ppermute | solution.py:377
  698.2 21.0 %collective-permute-start.61 = (bf16[2,48,1408]{2,1,0:T(8,128)(2,1)S(1)}, bf16[2,48,1408]{2,1,0:T(8,128)(2,1)S(1)}, u32[]{:S(2)}, u32[]{:S(2)}) collective-permute-start(bf16[2,48,1408]{2,1,0:T(8,128)(2,1)S(1)} %get-tuple-element.340), channel_id=1, source_target_pairs={{0,4},{1,5},{2,6},{3,7},{4,0},{5,1},{6,2},{7,3},{8,12},{9,13},{10,... | collective-permute-start | bytes 811016 | tf_op jit(solution)/shard_map/ppermute | solution.py:377
  703.2 32.3 %collective-permute-start.64 = (bf16[1536,512]{1,0:T(8,128)(2,1)S(1)}, bf16[1536,512]{1,0:T(8,128)(2,1)S(1)}, u32[]{:S(2)}, u32[]{:S(2)}) collective-permute-start(bf16[1536,512]{1,0:T(8,128)(2,1)S(1)} %fusion.31), channel_id=1, source_target_pairs={{0,0},{1,16},{2,2},{3,18},{4,4},{5,20},{6,6},{7,22},{8,8},{9,24},{... | collective-permute-start | bytes 4718600 | tf_op jit(solution)/shard_map/ppermute | solution.py:1062
  709.7 19.3 %collective-permute-start.65 = (bf16[1536,256]{1,0:T(8,128)(2,1)S(1)}, bf16[1536,256]{1,0:T(8,128)(2,1)S(1)}, u32[]{:S(2)}, u32[]{:S(2)}) collective-permute-start(bf16[1536,256]{1,0:T(8,128)(2,1)S(1)} %get-tuple-element.235), channel_id=1, source_target_pairs={{1,0},{17,1},{3,2},{19,3},{5,4},{21,5},{7,6},{23,7},{9,8},{25,9},{... | collective-permute-start | bytes 2359304 | tf_op jit(solution)/shard_map/ppermute | solution.py:1062
  (68 other events, 1150.1 us)
Sparse Core Ops, SparseCore 0:
  50.5 80.2 all-gather.1
  541.9 107.6 reduce-scatter.1

commit v6 on v5

--- a/solution.py
+++ b/solution.py
@@ -670,13 +670,11 @@
     )
 
 
-def probabilities(query, keys, allowed):
-    scores = jnp.where(allowed, contract(query, keys, 1, 1), -1e30)
-    expon = jnp.exp(scores - jnp.max(scores, axis=-1, keepdims=True))
-    return expon * (1.0 / jnp.sum(expon, axis=-1, keepdims=True))
-
-
-def attend_kernel(base, q_ref, k_ref, v_ref, start_ref, o_ref):
+def masked_scores(query, keys, allowed):
+    return jnp.where(allowed, contract(query, keys, 1, 1), -1e30)
+
+
+def attend_kernel(base, q_ref, k_ref, v_ref, start_ref, o_ref, level_ref):
     pair = pl.program_id(0) + base
     ratio = QHEADS // KVHEADS
     for row, low, high in windows(q_ref.shape[0]):
@@ -684,9 +682,14 @@
         for side in range(2):
             head = (2 * pair + side) // ratio
             lanes = slice(side * HDIM, (side + 1) * HDIM)
-            probs = probabilities(
+            scores = masked_scores(
                 q_ref[row : row + Q_TILE, lanes], k_ref[head, low:high, :], allowed
             )
+            highest = jnp.max(scores, axis=-1, keepdims=True)
+            expon = jnp.exp(scores - highest)
+            total = jnp.sum(expon, axis=-1, keepdims=True)
+            level_ref[0, row : row + Q_TILE, side : side + 1] = highest + jnp.log(total)
+            probs = expon * (1.0 / total)
             mixed = contract(probs.astype(BF16), v_ref[head, low:high, :], 1, 0)
             o_ref[row : row + Q_TILE, lanes] = mixed.astype(BF16)
 
@@ -708,8 +711,14 @@
         functools.partial(attend_kernel, base),
         grid=(pairs,),
         in_specs=[pair_block, whole, whole, pl.BlockSpec((rows, 1), lambda j: (0, 0))],
-        out_specs=pl.BlockSpec((rows, 2 * HDIM), lambda j: (0, j)),
-        out_shape=jax.ShapeDtypeStruct((rows, pairs * 2 * HDIM), BF16),
+        out_specs=[
+            pl.BlockSpec((rows, 2 * HDIM), lambda j: (0, j)),
+            pl.BlockSpec((1, rows, 2), lambda j: (j, 0, 0)),
+        ],
+        out_shape=[
+            jax.ShapeDtypeStruct((rows, pairs * 2 * HDIM), BF16),
+            jax.ShapeDtypeStruct((pairs, rows, 2), F32),
+        ],
         compiler_params=pltpu.CompilerParams(vmem_limit_bytes=VMEM_BYTES),
         cost_estimate=attention_cost(rows, 2 * pairs, 2),
         name="attend",
@@ -717,7 +726,7 @@
 
 
 def attend_back_kernel(
-    q_ref, k_ref, v_ref, d_ref, start_ref, cos_ref, sin_ref,
+    q_ref, k_ref, v_ref, d_ref, level_ref, start_ref, cos_ref, sin_ref,
     dq_ref, dk_ref, dv_ref, dk_sum, dv_sum,
 ):
     pair = pl.program_id(0)
@@ -736,7 +745,10 @@
             lanes = slice(side * HDIM, (side + 1) * HDIM)
             query = q_ref[row : row + Q_TILE, lanes]
             keys = k_ref[head, low:high, :]
-            probs = probabilities(query, keys, allowed)
+            probs = jnp.exp(
+                masked_scores(query, keys, allowed)
+                - level_ref[0, row : row + Q_TILE, side : side + 1]
+            )
             grad_out = d_ref[row : row + Q_TILE, lanes]
             grad_probs = contract(grad_out, v_ref[head, low:high, :], 1, 1)
             inner = jnp.sum(probs * grad_probs, axis=-1, keepdims=True)
@@ -761,7 +773,7 @@
         dv_ref[...] = jnp.concatenate([dv_sum[head] for head in heads], axis=1).astype(BF16)
 
 
-def attend_back(query, keys, values, grad_out, starts, cos, sin):
+def attend_back(query, keys, values, grad_out, levels, starts, cos, sin):
     rows, lanes = query.shape
     pairs = lanes // (2 * HDIM)
     kv_heads = keys.shape[0]
@@ -776,7 +788,8 @@
         attend_back_kernel,
         grid=(pairs,),
         in_specs=[
-            pair_block, whole, whole, pair_block, fixed(1), fixed(2 * HDIM), fixed(2 * HDIM),
+            pair_block, whole, whole, pair_block,
+            pl.BlockSpec((1, rows, 2), lambda j: (j, 0, 0)), fixed(1), fixed(2 * HDIM), fixed(2 * HDIM),
         ],
         out_specs=[pair_block, fixed(flat), fixed(flat)],
         out_shape=[
@@ -788,7 +801,7 @@
         compiler_params=pltpu.CompilerParams(vmem_limit_bytes=VMEM_BYTES),
         cost_estimate=attention_cost(rows, 2 * pairs, 5),
         name="attend_back",
-    )(query, keys, values, grad_out, starts, cos, sin)
+    )(query, keys, values, grad_out, levels, starts, cos, sin)
 
 
 SLOTS = 2 * LINE - 1
@@ -1166,32 +1179,33 @@
         places_of, x_sorted, qkv_rows, qkv_others, cos, sin, q_width, kv_heads
     )
     gain_one, gain_two = gains[0], gains[1]
-    query, late_lines = lax.optimization_barrier((query, late_lines))
+    pairs = q_width // (2 * HDIM)
+    first_pairs = 2 * pairs // 3
+    mixed_one, levels_one = attend(query, keys, values, start_column, 0, first_pairs)
+    sent_one = swap_seq(from_order(sort_other, mixed_one))
+    lines, late_lines = after((lines, late_lines), mixed_one)
     up_one = jnp.concatenate([lines[0], late_lines[0]], axis=0)
     down_one = jnp.concatenate([lines[1], late_lines[1]], axis=0)
-    query, up_one, down_one = lax.optimization_barrier((query, up_one, down_one))
+    query_two, grad_near_x, grad_near_y, up_one, down_one = after(
+        (query, *grad_near, up_one, down_one), mixed_one
+    )
     up_two, down_two = line_up(up_one), line_down(down_one)
-    pairs = q_width // (2 * HDIM)
-    first_pairs = (pairs + 1) // 2
-    mixed_one = attend(query, keys, values, start_column, 0, first_pairs)
-    sent_one = swap_seq(from_order(sort_other, mixed_one))
-    query_two, grad_near_x, grad_near_y = after((query, *grad_near), mixed_one)
     grad_near = (grad_near_x, grad_near_y)
     grad_far = far_pieces(*grad_near)
-    mixed_two = attend(
+    mixed_two, levels_two = attend(
         query_two, keys, values, start_column, first_pairs, pairs - first_pairs
     )
     sent_two = swap_seq(from_order(sort_other, mixed_two))
     mixed_mine = [from_order(sort_own, mixed_one), from_order(sort_own, mixed_two)]
     mixed_mine = jnp.concatenate(mixed_mine, axis=1)
     mixed_theirs = jnp.concatenate([sent_one, sent_two], axis=1)
-    mixed_theirs, up_two, down_two = lax.optimization_barrier((mixed_theirs, up_two, down_two))
-    up_three, down_three = line_up(up_two), line_down(down_two)
     inputs = tokens.astype(F32)
     middle, normed_ffn, output_parts = mix(
         seq.astype(jnp.int32)[None], mixed_mine, mixed_theirs, tokens, gain_two[None, :], output_full
     )
     normed_ffn = after(normed_ffn, *grad_far)
+    up_two, down_two = after((up_two, down_two), normed_ffn)
+    up_three, down_three = line_up(up_two), line_down(down_two)
     row_near = near_pieces(normed_ffn, normed_ffn)
     row_far = far_pieces(*row_near)
     slots = [up_three, up_two, up_one, own_part, down_one, down_two, down_three]
@@ -1267,13 +1281,21 @@
     grad_sorted = to_order(grad_mixed, grad_other)
     mid_line = (line_up(right), line_down(left))
     grad_query, grad_keys, grad_values = attend_back(
-        query, keys, values, grad_sorted, start_column, cos, sin
+        query,
+        keys,
+        values,
+        grad_sorted,
+        jnp.concatenate([levels_one, levels_two], axis=0),
+        start_column,
+        cos,
+        sin,
     )
     (grad_query, grad_keys, grad_values), mid_line, ffn_y, ffn_x = lax.optimization_barrier(
         ((grad_query, grad_keys, grad_values), mid_line, ffn_y, ffn_x)
     )
     right, left = line_step(2, mid_line)
-    last_first = (line_up(right[:cut]), line_down(left[:cut]))
+    third = width // 3
+    last_first = (line_up(right[:third]), line_down(left[:third]))
     first_ffn, second_ffn = near_links(near_ffn, ffn_y, ffn_x)
     first_ffn, second_ffn = swap_seq(first_ffn), swap_y(second_ffn)
     ffn = own_sum(near_ffn, ffn_y, ffn_x, first_ffn, second_ffn)
@@ -1295,7 +1317,11 @@
         grads_late, w_qkv, own_places[:, None], other_places[:, None]
     )
     kept, sent_normed = lax.optimization_barrier((kept, sent_normed))
-    right_late, left_late = after((right[cut:], left[cut:]), last_first, sent_normed)
+    right_mid, left_mid = after((right[third : 2 * third], left[third : 2 * third]), last_first)
+    last_mid = (line_up(right_mid), line_down(left_mid))
+    right_late, left_late = after(
+        (right[2 * third :], left[2 * third :]), last_mid, sent_normed
+    )
     last_late = (line_up(right_late), line_down(left_late))
     grad_normed = grad_normed.astype(F32) + swap_seq(sent_normed).astype(F32)
     scale = lax.rsqrt(jnp.mean(inputs * inputs, axis=-1, keepdims=True) + EPSILON)
@@ -1305,14 +1331,16 @@
     grad_tokens = grad_middle + scale * (scaled - unit * inner)
     next_kept = chosen(kept, row_of, 0)
     next_kept = next_kept + swap_y(chosen(kept, 1 - row_of, 0).astype(BF16)).astype(F32)
-    next_kept, last_first, last_late, summed_output = lax.optimization_barrier(
-        (next_kept, last_first, last_late, summed_output)
+    next_kept, last_first, last_mid, last_late, summed_output = lax.optimization_barrier(
+        (next_kept, last_first, last_mid, last_late, summed_output)
     )
     own_grads = line_partial(*range(LINE))
     part_grads = jnp.concatenate(
         [
             own + up.astype(F32) + down.astype(F32)
-            for own, (up, down) in ((own_grads[:cut], last_first), (own_grads[cut:], last_late))
+            for own, (up, down) in zip(
+                jnp.split(own_grads, 3, axis=0), (last_first, last_mid, last_late)
+            )
         ],
         axis=0,
     ).astype(BF16)

time: 760 us -> 786 us (1.034)
  starting transfers between devices: 111 us -> 128 us
  waiting for transfers between devices: 167 us -> 176 us
    ppermute x15, waiting for transfers between devices: 47.9 us -> 60.3 us  [swap_seq(): return lax.ppermute(value, 'seq', [(0, 1), (1, 0)])]
    ppermute x32, starting transfers between devices: 41 us -> 51.8 us  [swap_dp(): return lax.ppermute(value, 'dp', [(i, i ^ mask) for i in range(4 * LINE)])]
    ppermute x8 -> x9, starting transfers between devices: 33.1 us -> 39.3 us  [line_up(): return lax.ppermute(value, 'dp', [(i, i + 4) for i in range(4 * LINE - 4)])]
    ppermute x8 -> x9, waiting for transfers between devices: 25.9 us -> 22.8 us  [line_down(): return lax.ppermute(value, 'dp', [(i, i - 4) for i in range(4, 4 * LINE)])]
  transfers between devices with their start and end apart: 69 -> 71, of which waited for: 26 -> 22; matrix products, arithmetic and copies ran while one was open for 28% -> 28% of each run, Pallas kernels for 23% -> 21%
where the time goes in v6:
time: 786 us; the launch traced here: 778 us
  Pallas kernels  222 us (28%)
  waiting for transfers between devices  176 us (22%)
  starting transfers between devices  128 us (16%)
  other arithmetic  97.1 us (12%)
  matrix products  81.4 us (10%)
  local copies, waits for them, and re-layouts  57.5 us (7%)
  between operations  15.8 us (2%)
    pallas_call x2, Pallas kernels, run_experts(): pl.pallas_call(functools.partial(experts_kernel, tiles, tile // 2), grid_...  109 us
    dot_general x15, matrix products, contract(): lax.dot_general(left, right, (((left_dim,), (right_dim,)), ((), ())), pre...  81.4 us
    ppermute x32, waiting for transfers between devices, swap_dp(): return lax.ppermute(value, 'dp', [(i, i ^ mask) for i in range(4 * LINE)])  71.3 us
    ppermute x15, waiting for transfers between devices, swap_seq(): return lax.ppermute(value, 'seq', [(0, 1), (1, 0)])  60.3 us
    ppermute x32, starting transfers between devices, swap_dp(): return lax.ppermute(value, 'dp', [(i, i ^ mask) for i in range(4 * LINE)])  51.8 us
    pallas_call x1, Pallas kernels, attend_back(): pl.pallas_call(attend_back_kernel, grid=(pairs,), in_specs=[pair_block, w...  40.5 us
    ppermute x9, starting transfers between devices, line_up(): return lax.ppermute(value, 'dp', [(i, i + 4) for i in range(4 * LINE - 4)])  39.3 us
    pallas_call x2, Pallas kernels, attend(): pl.pallas_call(functools.partial(attend_kernel, base), grid=(pairs,), in_...  30.2 us
  transfers between devices with their start and end apart: 71, of which 22 were waited for; matrix products, arithmetic and copies ran while one was open for 28% of the time, Pallas kernels for 21%

profile of v6, /device:TPU:1, one launch (start us, length us, event | category | flops | bytes accessed | tf_op | source)
XLA Modules:
  0.0 777.9 jit_solution(6989404425306101798)
XLA Ops:
  29.5 5.0 collective-permute-done.3
  35.5 8.8 %collective-permute-done.5 = bf16[48,2816]{1,0:T(8,128)(2,1)} collective-permute-done((bf16[48,2816]{1,0:T(8,128)(2,1)S(1)}, bf16[48,2816]{1,0:T(8,128)(2,1)}, u32[]{:S(2)}, u32[]{:S(2)}) %collective-permute-start.5) | collective-permute-done | bytes 270368 | tf_op jit(solution)/shard_map/ppermute | solution.py:377
  44.3 4.5 collective-permute-done.1
  52.4 4.7 collective-permute-start.8
  67.2 21.3 %collective-permute-done.7 = bf16[192,2816]{1,0:T(8,128)(2,1)} collective-permute-done((bf16[192,2816]{1,0:T(8,128)(2,1)}, bf16[192,2816]{1,0:T(8,128)(2,1)}, u32[]{:S(2)}, u32[]{:S(2)}) %collective-permute-start.7) | collective-permute-done | bytes 1081376 | tf_op jit(solution)/shard_map/ppermute | solution.py:377
  88.5 13.0 %collective-permute-done.9 = bf16[768,768]{1,0:T(8,128)(2,1)} collective-permute-done((bf16[768,768]{1,0:T(8,128)(2,1)}, bf16[768,768]{1,0:T(8,128)(2,1)}, u32[]{:S(2)}, u32[]{:S(2)}) %collective-permute-start.9) | collective-permute-done | bytes 1179680 | tf_op jit(solution)/shard_map/ppermute | solution.py:393
  103.8 12.6 %collective-permute-start.10 = (bf16[384,2816]{1,0:T(8,128)(2,1)}, bf16[384,2816]{1,0:T(8,128)(2,1)}, u32[]{:S(2)}, u32[]{:S(2)}) collective-permute-start(bf16[384,2816]{1,0:T(8,128)(2,1)} %constant_dynamic-update-slice_fusion.2.own_ref), channel_id=1, source_target_pairs={{0,1},{1,0},{2,3},{3,2},{4,5},{5,4},{6,7},{7,6},{8,9},{9,8},{10,11... | collective-permute-start | bytes 6488072 | tf_op jit(solution)/shard_map/ppermute | solution.py:377
  134.5 4.9 add_convert_fusion.2.x_ref
  139.5 12.9 %project.1 = (bf16[1024,1536]{1,0:T(8,128)(2,1)}, bf16[1024,768]{1,0:T(8,128)(2,1)}, bf16[4,1024,64]{2,1,0:T(8,128)(2,1)}, bf16[4,1024,64]{2,1,0:T(8,128)(2,1)},...) custom-call(s32[3]{0:T(128)} %pad_add_fusion.place_ref, bf16[1024,1536]{1,0:T(8,128)(2,1)} %add_convert_fusion.2.x_ref, ...), custom_call_target="tpu_custom_call" | custom-call | flops 251658240 | bytes 3538944 | tf_op jit(solution)/shard_map/project/pallas_call | solution.py:524
  152.4 19.3 %attend.2 = (bf16[1024,512]{1,0:T(8,128)(2,1)}, f32[4,1024,2]{2,1,0:T(8,128)}) custom-call(bf16[1024,768]{1,0:T(8,128)(2,1)} %get-tuple-element.159.q_ref, bf16[4,1024,64]{2,1,0:T(8,128)(2,1)} %get-tuple-element.148.k_ref, bf16[4,1024,64]{2,1,0:T(8,128)(2,1)} %get-tuple-element.149.v_ref, s32[1024,1]{1,0:T(8,128)} %copy.109.start_ref), custom_call_target="tpu_custom_call" | custom-call | flops 150994944 | bytes 4194304 | tf_op jit(solution)/shard_map/attend/pallas_call | solution.py:710
  173.5 4.0 pad_maximum_fusion.3.refs_20_.refs_16_
  177.6 5.3 collective-permute-start.31
  185.4 10.9 %attend.3 = (bf16[1024,256]{1,0:T(8,128)(2,1)}, f32[2,1024,2]{2,1,0:T(8,128)}) custom-call(bf16[1024,768]{1,0:T(8,128)(2,1)} %get-tuple-element.159.q_ref, bf16[4,1024,64]{2,1,0:T(8,128)(2,1)} %get-tuple-element.148.k_ref, bf16[4,1024,64]{2,1,0:T(8,128)(2,1)} %get-tuple-element.149.v_ref, s32[1024,1]{1,0:T(8,128)} %copy.109.start_ref), custom_call_target="tpu_custom_call" | custom-call | flops 75497472 | bytes 2097152 | tf_op jit(solution)/shard_map/attend/pallas_call | solution.py:710
  207.9 19.9 %collective-permute-done.16 = bf16[512,256]{1,0:T(8,128)(2,1)S(1)} collective-permute-done((bf16[512,256]{1,0:T(8,128)(2,1)S(1)}, bf16[512,256]{1,0:T(8,128)(2,1)S(1)}, u32[]{:S(2)}, u32[]{:S(2)}) %collective-permute-start.16) | collective-permute-done | bytes 262176 | tf_op jit(solution)/shard_map/ppermute | solution.py:373
  229.7 9.3 %mix.1 = (f32[512,1536]{1,0:T(8,128)}, bf16[512,1536]{1,0:T(8,128)(2,1)}, bf16[2,768,1536]{2,1,0:T(8,128)(2,1)}) custom-call(s32[1]{0:T(128)} %bitcast.place_ref, bf16[512,768]{1,0:T(8,128)(2,1)} %get-tuple-element.360.mine_ref, bf16[512,768]{1,0:T(8,128)(2,1)} %copy-done.29, bf16[512,1536]{1,0:T(8,128)(2,1)} %x_ref.1, ...), custom_call_target="tpu_custom_call" | custom-call | flops 150994944 | bytes 786432 | tf_op jit(solution)/shard_map/mix/pallas_call | solution.py:588
  241.0 3.8 collective-permute-start.33
  246.2 27.0 %collective-permute-done.19.refs_0_.refs_1_ = bf16[512,1536]{1,0:T(8,128)(2,1)} collective-permute-done((bf16[512,1536]{1,0:T(8,128)(2,1)}, bf16[512,1536]{1,0:T(8,128)(2,1)}, u32[]{:S(2)}, u32[]{:S(2)}) %collective-permute-start.19) | collective-permute-done | bytes 1572896 | tf_op jit(solution)/shard_map/ppermute | solution.py:373
  277.1 4.1 collective-permute-start.29
  281.2 9.3 %collective-permute-done.21.refs_2_ = bf16[256,1536]{1,0:T(8,128)(2,1)S(1)} collective-permute-done((bf16[256,1536]{1,0:T(8,128)(2,1)S(1)}, bf16[256,1536]{1,0:T(8,128)(2,1)S(1)}, u32[]{:S(2)}, u32[]{:S(2)}) %collective-permute-start.21) | collective-permute-done | bytes 786464 | tf_op jit(solution)/shard_map/ppermute | solution.py:377
  290.5 3.8 collective-permute-start.23
  296.6 4.1 collective-permute-start.30
  300.9 3.0 collective-permute-done.30.refs_15_
  305.0 2.6 select_select_fusion
  308.5 54.9 %experts.2 = (bf16[1024,1536]{1,0:T(8,128)(2,1)}, bf16[1024,1536]{1,0:T(8,128)(2,1)}, bf16[1024,1536]{1,0:T(8,128)(2,1)}, bf16[1024,1536]{1,0:T(8,128)(2,1)}, bf...) custom-call(s32[1]{0:T(128)} %bitcast.2.place_ref, ...), custom_call_target="tpu_custom_call" | custom-call | flops 2415919104 | bytes 50331648 | tf_op jit(solution)/shard_map/experts/pallas_call | solution.py:957
  364.3 7.8 %collective-permute-done.35 = bf16[1024,1536]{1,0:T(8,128)(2,1)S(1)} collective-permute-done((bf16[1024,1536]{1,0:T(8,128)(2,1)}, bf16[1024,1536]{1,0:T(8,128)(2,1)S(1)}, u32[]{:S(2)}, u32[]{:S(2)}) %collective-permute-start.35) | collective-permute-done | bytes 3145760 | tf_op jit(solution)/shard_map/ppermute | solution.py:377
  372.1 2.7 add_convert_fusion.1
  380.5 54.6 %experts.3 = (bf16[1024,1536]{1,0:T(8,128)(2,1)}, bf16[1024,1536]{1,0:T(8,128)(2,1)}, bf16[1024,1536]{1,0:T(8,128)(2,1)}, bf16[1024,1536]{1,0:T(8,128)(2,1)}, bf...) custom-call(s32[1]{0:T(128)} %bitcast.2.place_ref, ...), custom_call_target="tpu_custom_call", output_to_operand_aliasing={{4}: (21, {}), {5}: (22, {}), {6}: (23, {}), {7}: (24, {}),... | custom-call | flops 2415919104 | bytes 50331648 | tf_op jit(solution)/shard_map/experts/pallas_call | solution.py:957
  436.2 11.1 %fusion.9 = bf16[1536,512]{1,0:T(8,128)(2,1)S(1)} fusion(bf16[4096,1536]{1,0:T(8,128)(2,1)} %get-tuple-element.203, bf16[4096,512]{1,0:T(8,128)(2,1)} %get-tuple-element.196), kind=kOutput, calls=%fused_computation.34 | convolution fusion | flops 6444023808 | bytes 18350080 | tf_op jit(solution)/shard_map/dot_general | solution.py:668
  447.9 14.2 %convolution_convert_fusion.1 = bf16[1536,1024]{1,0:T(8,128)(2,1)S(1)} fusion(bf16[4096,1536]{1,0:T(8,128)(2,1)S(1)} %copy-done.16, bf16[4096,1024]{1,0:T(8,128)(2,1)S(1)} %copy-done.22), kind=kOutput, calls=%fused_computation.13 | convolution fusion | flops 12886474752 | bytes 24117248 | tf_op jit(solution)/shard_map/dot_general | solution.py:668
  464.1 5.0 collective-permute-start.45
  472.1 2.9 convert_add_fusion.1
  478.5 17.8 %convolution_convert_fusion = bf16[1536,1024]{1,0:T(8,128)(2,1)} fusion(bf16[4096,1536]{1,0:T(8,128)(2,1)S(1)} %copy-done.16, bf16[4096,1024]{1,0:T(8,128)(2,1)} %get-tuple-element.202), kind=kOutput, calls=%fused_computation.12 | convolution fusion | flops 12886474752 | bytes 24117248 | tf_op jit(solution)/shard_map/dot_general | solution.py:668
  500.8 5.6 fusion.40
  508.8 7.0 fusion.10
  519.4 3.1 fusion.43
  523.8 3.2 add_convert_fusion.6
  527.0 5.4 collective-permute-start.48
  532.4 3.4 add_convert_fusion.5
  537.3 2.8 add_convert_fusion
  550.4 7.2 fusion.36
  562.2 40.5 %attend_back.1 = (bf16[1024,768]{1,0:T(8,128)(2,1)}, bf16[1024,256]{1,0:T(8,128)(2,1)}, bf16[1024,256]{1,0:T(8,128)(2,1)}) custom-call(bf16[1024,768]{1,0:T(8,128)(2,1)} %get-tuple-element.159.q_ref, bf16[4,1024,64]{2,1,0:T(8,128)(2,1)} %get-tuple-element.148.k_ref, bf16[4,1024,64]{2,1,0:T(8,128)(2,1)} %get-tuple-element.149.v_ref, ...), custom_call_target="tpu_custom_call" | custom-call | flops 566231040 | bytes 6291456 | tf_op jit(solution)/shard_map/attend_back/pallas_call | solution.py:787
  602.7 7.9 %add_convert_fusion.3 = (bf16[1536,768]{1,0:T(8,128)(2,1)}, bf16[1536,768]{1,0:T(8,128)(2,1)}) fusion(bf16[1536,768]{1,0:T(8,128)(2,1)} %collective-permute-done.49, pred[]{:T(512)S(6)} %lt.121, pred[]{:T(512)S(6)} %lt.120, bf16[1536,256]{1,0:T(8,128)(2,1)} %copy-done.13, bf16[1536,512]{1,0:T(8,128)(2,1)} %copy-done.3, bf16[1536,256]{1,0:T(8,128)(2,1)} %copy-done.15, ...), kind=kLoop, calls=%fused_computation.5 | loop fusion | flops 33030144 | bytes 18874372 | tf_op jit(solution)/shard_map/convert_element_type | solution.py:1263
  610.6 8.3 %qkv_grad.1 = bf16[2,2,2,4,48,1408]{5,4,3,2,1,0:T(8,128)(2,1)} custom-call(bf16[1024,1536]{1,0:T(8,128)(2,1)} %get-tuple-element.227.h_ref, bf16[1024,768]{1,0:T(8,128)(2,1)} %get-tuple-element.228.dq_ref, bf16[1024,256]{1,0:T(8,128)(2,1)} %get-tuple-element.229.dk_ref, bf16[1024,256]{1,0:T(8,128)(2,1)} %get-tuple-element.230.dv_ref, ...), custom_call_target="tpu_custom_call" | custom-call | flops 251658240 | bytes 1572864 | tf_op jit(solution)/shard_map/qkv_grad/pallas_call | solution.py:1009
  620.8 3.8 collective-permute-start.54
  624.6 2.8 convert_add_fusion
  632.9 4.1 collective-permute-start.57
  639.6 10.6 %collective-permute-done.52 = bf16[256,1536]{1,0:T(8,128)(2,1)S(1)} collective-permute-done((bf16[256,1536]{1,0:T(8,128)(2,1)S(1)}, bf16[256,1536]{1,0:T(8,128)(2,1)S(1)}, u32[]{:S(2)}, u32[]{:S(2)}) %collective-permute-start.52) | collective-permute-done | bytes 786464 | tf_op jit(solution)/shard_map/ppermute | solution.py:373
  650.2 3.3 fusion.33
  653.6 5.2 collective-permute-done.57
  658.8 5.0 collective-permute-done.58
  663.8 3.8 collective-permute-start.59
  671.5 11.0 %token_grad.1 = (bf16[512,1536]{1,0:T(8,128)(2,1)}, bf16[512,1536]{1,0:T(8,128)(2,1)}) custom-call(bf16[1024,768]{1,0:T(8,128)(2,1)} %get-tuple-element.228.dq_ref, bf16[1024,256]{1,0:T(8,128)(2,1)} %get-tuple-element.229.dk_ref, bf16[1024,256]{1,0:T(8,128)(2,1)} %get-tuple-element.230.dv_ref, bf16[1536,1280]{1,0:T(8,128)(2,1)} %get-tuple-element.231.w_ref, ...), custom_call_target="tpu_custom_call" | custom-call | flops 251658240 | bytes 1572864 | tf_op jit(solution)/shard_map/token_grad/pallas_call | solution.py:635
  685.5 5.2 select_convert_fusion
  690.7 4.9 collective-permute-start.61
  697.0 3.3 fusion.31
  701.2 7.1 collective-permute-done.56
  710.1 4.7 collective-permute-done.62
  714.8 4.4 fusion.29
  721.8 3.0 collective-permute-start.63
  726.8 7.0 collective-permute-start.66
  735.3 7.9 %collective-permute-done.64 = bf16[2,48,1408]{2,1,0:T(8,128)(2,1)S(1)} collective-permute-done((bf16[2,48,1408]{2,1,0:T(8,128)(2,1)S(1)}, bf16[2,48,1408]{2,1,0:T(8,128)(2,1)S(1)}, u32[]{:S(2)}, u32[]{:S(2)}) %collective-permute-start.64) | collective-permute-done | bytes 270368 | tf_op jit(solution)/shard_map/ppermute | solution.py:377
  745.9 4.2 fusion.5
  750.1 3.7 collective-permute-done.67
  753.8 8.0 %collective-permute-done.66 = bf16[1536,512]{1,0:T(8,128)(2,1)S(1)} collective-permute-done((bf16[1536,512]{1,0:T(8,128)(2,1)S(1)}, bf16[1536,512]{1,0:T(8,128)(2,1)S(1)}, u32[]{:S(2)}, u32[]{:S(2)}) %collective-permute-start.66) | collective-permute-done | bytes 1572896 | tf_op jit(solution)/shard_map/ppermute | solution.py:1075
  (369 shorter events, 169.9 us)
Async XLA Ops:
  7.2 222.5 %all-gather.2.cloned.1.call-start = ((), (), s32[]{:S(2)}) async-start(), calls=%async_computation.1 | async-start | bytes 5013504 | tf_op jit(solution)/shard_map/all_gather | solution.py:1120
  19.2 29.6 %collective-permute-start = (bf16[1536,512]{1,0:T(8,128)(2,1)S(1)}, bf16[1536,512]{1,0:T(8,128)(2,1)S(1)}, u32[]{:S(2)}, u32[]{:S(2)}) collective-permute-start(bf16[1536,512]{1,0:T(8,128)(2,1)S(1)} %pad_maximum_fusion.9), channel_id=1, source_target_pairs={{0,0},{1,16},{2,2},{3,18},{4,4},{5,20},{6,6},{7,22},{8,8},{9,24},{... | collective-permute-start | bytes 4718600 | tf_op jit(solution)/shard_map/ppermute | solution.py:1075
  21.7 27.1 %collective-permute-start.1 = (bf16[1536,256]{1,0:T(8,128)(2,1)}, bf16[1536,256]{1,0:T(8,128)(2,1)}, u32[]{:S(2)}, u32[]{:S(2)}) collective-permute-start(bf16[1536,256]{1,0:T(8,128)(2,1)} %get-tuple-element.356), channel_id=1, source_target_pairs={{0,1},{1,17},{2,3},{3,19},{4,5},{5,21},{6,7},{7,23},{8,9},{9,25},{... | collective-permute-start | bytes 2359304 | tf_op jit(solution)/shard_map/ppermute | solution.py:1075
  24.1 10.4 %collective-permute-start.3 = (bf16[48,2816]{1,0:T(8,128)(2,1)S(1)}, bf16[48,2816]{1,0:T(8,128)(2,1)}, u32[]{:S(2)}, u32[]{:S(2)}) collective-permute-start(bf16[48,2816]{1,0:T(8,128)(2,1)S(1)} %pad_maximum_fusion.17), channel_id=1, source_target_pairs={{0,4},{1,5},{2,6},{3,7},{4,0},{5,1},{6,2},{7,3},{8,12},{9,13},{10,... | collective-permute-start | bytes 811016 | tf_op jit(solution)/shard_map/ppermute | solution.py:377
  25.4 10.1 %collective-permute-start.4 = (bf16[48,2816]{1,0:T(8,128)(2,1)S(1)}, bf16[48,2816]{1,0:T(8,128)(2,1)}, u32[]{:S(2)}, u32[]{:S(2)}) collective-permute-start(bf16[48,2816]{1,0:T(8,128)(2,1)S(1)} %pad_maximum_fusion.17), channel_id=1, source_target_pairs={{0,8},{1,9},{2,10},{3,11},{4,12},{5,13},{6,14},{7,15},{8,0},{9,1},... | collective-permute-start | bytes 811016 | tf_op jit(solution)/shard_map/ppermute | solution.py:377
  27.8 16.6 %collective-permute-start.5 = (bf16[48,2816]{1,0:T(8,128)(2,1)S(1)}, bf16[48,2816]{1,0:T(8,128)(2,1)}, u32[]{:S(2)}, u32[]{:S(2)}) collective-permute-start(bf16[48,2816]{1,0:T(8,128)(2,1)S(1)} %pad_maximum_fusion.17), channel_id=1, source_target_pairs={{0,12},{1,13},{2,14},{3,15},{4,8},{5,9},{6,10},{7,11},{8,4},{9,5},... | collective-permute-start | bytes 811016 | tf_op jit(solution)/shard_map/ppermute | solution.py:377
  50.3 659.5 %reduce-scatter.2.cloned.1.call-start = ((), (), s32[]{:S(2)}) async-start(), calls=%async_computation.2 | async-start | bytes 4866048 | tf_op jit(solution)/shard_map/reduce_scatter | solution.py:1310
  52.4 36.1 %collective-permute-start.8 = (bf16[768,768]{1,0:T(8,128)(2,1)}, bf16[768,768]{1,0:T(8,128)(2,1)}, u32[]{:S(2)}, u32[]{:S(2)}) collective-permute-start(bf16[768,768]{1,0:T(8,128)(2,1)} %get-tuple-element.345), channel_id=1, source_target_pairs={{0,4},{1,5},{2,6},{3,7},{4,8},{5,9},{6,10},{7,11},{8,12},{9,13},{1... | collective-permute-start | bytes 3538952 | tf_op jit(solution)/shard_map/ppermute | solution.py:389
  57.1 44.4 %collective-permute-start.9 = (bf16[768,768]{1,0:T(8,128)(2,1)}, bf16[768,768]{1,0:T(8,128)(2,1)}, u32[]{:S(2)}, u32[]{:S(2)}) collective-permute-start(bf16[768,768]{1,0:T(8,128)(2,1)} %get-tuple-element.345), channel_id=1, source_target_pairs={{4,0},{5,1},{6,2},{7,3},{8,4},{9,5},{10,6},{11,7},{12,8},{13,9},{1... | collective-permute-start | bytes 3538952 | tf_op jit(solution)/shard_map/ppermute | solution.py:393
  60.6 28.0 %collective-permute-start.7 = (bf16[192,2816]{1,0:T(8,128)(2,1)}, bf16[192,2816]{1,0:T(8,128)(2,1)}, u32[]{:S(2)}, u32[]{:S(2)}) collective-permute-start(bf16[192,2816]{1,0:T(8,128)(2,1)} %pad_maximum_fusion.11), channel_id=1, source_target_pairs={{0,2},{1,3},{2,0},{3,1},{4,6},{5,7},{6,4},{7,5},{8,10},{9,11},{10,... | collective-permute-start | bytes 3244040 | tf_op jit(solution)/shard_map/ppermute | solution.py:377
  62.9 66.2 %collective-permute-start.6 = (bf16[512,1536]{1,0:T(8,128)(2,1)S(1)}, bf16[512,1536]{1,0:T(8,128)(2,1)}, u32[]{:S(2)}, u32[]{:S(2)}) collective-permute-start(bf16[512,1536]{1,0:T(8,128)(2,1)S(1)} %copy-done.8), channel_id=1, source_target_pairs={{0,16},{16,0},{1,17},{17,1},{2,18},{18,2},{3,19},{19,3},{4,20},{20... | collective-permute-start | bytes 4718600 | tf_op jit(solution)/shard_map/ppermute | solution.py:373
  103.8 35.6 %collective-permute-start.10 = (bf16[384,2816]{1,0:T(8,128)(2,1)}, bf16[384,2816]{1,0:T(8,128)(2,1)}, u32[]{:S(2)}, u32[]{:S(2)}) collective-permute-start(bf16[384,2816]{1,0:T(8,128)(2,1)} %constant_dynamic-update-slice_fusion.2.own_ref), channel_id=1, source_target_pairs={{0,1},{1,0},{2,3},{3,2},{4,5},{5,4},{6,7},{7,6},{8,9},{9,8},{10,11... | collective-permute-start | bytes 6488072 | tf_op jit(solution)/shard_map/ppermute | solution.py:377
  118.7 58.9 %collective-permute-start.12 = (bf16[512,1664]{1,0:T(8,128)(2,1)}, bf16[512,1664]{1,0:T(8,128)(2,1)}, u32[]{:S(2)}, u32[]{:S(2)}) collective-permute-start(bf16[512,1664]{1,0:T(8,128)(2,1)} %concatenate.116.refs_6_), channel_id=1, source_target_pairs={{0,2},{1,3},{2,0},{3,1},{4,6},{5,7},{6,4},{7,5},{8,10},{9,11},{10,... | collective-permute-start | bytes 5111816 | tf_op jit(solution)/shard_map/ppermute | solution.py:377
  125.4 46.3 %collective-permute-start.13 = (bf16[768,768]{1,0:T(8,128)(2,1)S(1)}, bf16[768,768]{1,0:T(8,128)(2,1)}, u32[]{:S(2)}, u32[]{:S(2)}) collective-permute-start(bf16[768,768]{1,0:T(8,128)(2,1)S(1)} %copy-done.36), channel_id=1, source_target_pairs={{0,4},{1,5},{2,6},{3,7},{4,8},{5,9},{6,10},{7,11},{8,12},{9,13},{1... | collective-permute-start | bytes 3538952 | tf_op jit(solution)/shard_map/ppermute | solution.py:389
  127.7 44.0 %collective-permute-start.14 = (bf16[768,768]{1,0:T(8,128)(2,1)S(1)}, bf16[768,768]{1,0:T(8,128)(2,1)}, u32[]{:S(2)}, u32[]{:S(2)}) collective-permute-start(bf16[768,768]{1,0:T(8,128)(2,1)S(1)} %copy-done.36), channel_id=1, source_target_pairs={{4,0},{5,1},{6,2},{7,3},{8,4},{9,5},{10,6},{11,7},{12,8},{13,9},{1... | collective-permute-start | bytes 3538952 | tf_op jit(solution)/shard_map/ppermute | solution.py:393
  129.2 48.4 %collective-permute-start.11 = (bf16[512,1664]{1,0:T(8,128)(2,1)}, bf16[512,1664]{1,0:T(8,128)(2,1)}, u32[]{:S(2)}, u32[]{:S(2)}) collective-permute-start(bf16[512,1664]{1,0:T(8,128)(2,1)} %concatenate.116.refs_6_), channel_id=1, source_target_pairs={{0,16},{16,0},{1,17},{17,1},{2,18},{18,2},{3,19},{19,3},{4,20},{20... | collective-permute-start | bytes 5111816 | tf_op jit(solution)/shard_map/ppermute | solution.py:373
  177.6 63.5 %collective-permute-start.31 = (bf16[1536,768]{1,0:T(8,128)(2,1)S(1)}, bf16[1536,768]{1,0:T(8,128)(2,1)}, u32[]{:S(2)}, u32[]{:S(2)}) collective-permute-start(bf16[1536,768]{1,0:T(8,128)(2,1)S(1)} %pad_maximum_fusion.2.refs_18_.refs_14_), channel_id=1, source_target_pairs={{0,4},{1,5},{2,6},{3,7},{4,8},{5,9},{6,10},{7,11},{8,12},{9,13},{1... | collective-permute-start | bytes 7077896 | tf_op jit(solution)/shard_map/ppermute | solution.py:389
  182.9 58.1 %collective-permute-start.32 = (bf16[1536,768]{1,0:T(8,128)(2,1)}, bf16[1536,768]{1,0:T(8,128)(2,1)}, u32[]{:S(2)}, u32[]{:S(2)}) collective-permute-start(bf16[1536,768]{1,0:T(8,128)(2,1)} %pad_maximum_fusion.3.refs_20_.refs_16_), channel_id=1, source_target_pairs={{4,0},{5,1},{6,2},{7,3},{8,4},{9,5},{10,6},{11,7},{12,8},{13,9},{1... | collective-permute-start | bytes 7077896 | tf_op jit(solution)/shard_map/ppermute | solution.py:393
  185.2 20.5 %collective-permute-start.15 = (bf16[512,512]{1,0:T(8,128)(2,1)S(1)}, bf16[512,512]{1,0:T(8,128)(2,1)S(1)}, u32[]{:S(2)}, u32[]{:S(2)}) collective-permute-start(bf16[512,512]{1,0:T(8,128)(2,1)S(1)} %fusion.47), channel_id=1, source_target_pairs={{0,16},{16,0},{1,17},{17,1},{2,18},{18,2},{3,19},{19,3},{4,20},{20... | collective-permute-start | bytes 1572872 | tf_op jit(solution)/shard_map/ppermute | solution.py:373
  200.3 38.7 %collective-permute-start.17 = (bf16[256,1664]{1,0:T(8,128)(2,1)}, bf16[256,1664]{1,0:T(8,128)(2,1)}, u32[]{:S(2)}, u32[]{:S(2)}) collective-permute-start(bf16[256,1664]{1,0:T(8,128)(2,1)} %slice.197), channel_id=1, source_target_pairs={{0,2},{1,3},{2,0},{3,1},{4,6},{5,7},{6,4},{7,5},{8,10},{9,11},{10,... | collective-permute-start | bytes 2555912 | tf_op jit(solution)/shard_map/ppermute | solution.py:377
  202.7 36.3 %collective-permute-start.18 = (bf16[256,1664]{1,0:T(8,128)(2,1)}, bf16[256,1664]{1,0:T(8,128)(2,1)}, u32[]{:S(2)}, u32[]{:S(2)}) collective-permute-start(bf16[256,1664]{1,0:T(8,128)(2,1)} %slice.198), channel_id=1, source_target_pairs={{0,16},{16,0},{1,17},{17,1},{2,18},{18,2},{3,19},{19,3},{4,20},{20... | collective-permute-start | bytes 2555912 | tf_op jit(solution)/shard_map/ppermute | solution.py:373
  205.7 22.1 %collective-permute-start.16 = (bf16[512,256]{1,0:T(8,128)(2,1)S(1)}, bf16[512,256]{1,0:T(8,128)(2,1)S(1)}, u32[]{:S(2)}, u32[]{:S(2)}) collective-permute-start(bf16[512,256]{1,0:T(8,128)(2,1)S(1)} %fusion.49), channel_id=1, source_target_pairs={{0,16},{16,0},{1,17},{17,1},{2,18},{18,2},{3,19},{19,3},{4,20},{20... | collective-permute-start | bytes 786440 | tf_op jit(solution)/shard_map/ppermute | solution.py:373
  239.0 34.2 %collective-permute-start.19 = (bf16[512,1536]{1,0:T(8,128)(2,1)}, bf16[512,1536]{1,0:T(8,128)(2,1)}, u32[]{:S(2)}, u32[]{:S(2)}) collective-permute-start(bf16[512,1536]{1,0:T(8,128)(2,1)} %get-tuple-element.167.refs_0_), channel_id=1, source_target_pairs={{0,16},{16,0},{1,17},{17,1},{2,18},{18,2},{3,19},{19,3},{4,20},{20... | collective-permute-start | bytes 4718600 | tf_op jit(solution)/shard_map/ppermute | solution.py:373
  240.3 35.0 %collective-permute-start.20 = (bf16[512,1536]{1,0:T(8,128)(2,1)}, bf16[512,1536]{1,0:T(8,128)(2,1)}, u32[]{:S(2)}, u32[]{:S(2)}) collective-permute-start(bf16[512,1536]{1,0:T(8,128)(2,1)} %get-tuple-element.167.refs_0_), channel_id=1, source_target_pairs={{0,2},{1,3},{2,0},{3,1},{4,6},{5,7},{6,4},{7,5},{8,10},{9,11},{10,... | collective-permute-start | bytes 4718600 | tf_op jit(solution)/shard_map/ppermute | solution.py:377
  241.0 55.5 %collective-permute-start.33 = (bf16[1536,768]{1,0:T(8,128)(2,1)}, bf16[1536,768]{1,0:T(8,128)(2,1)S(1)}, u32[]{:S(2)}, u32[]{:S(2)}) collective-permute-start(bf16[1536,768]{1,0:T(8,128)(2,1)} %collective-permute-done.31.refs_17_.refs_13_), channel_id=1, source_target_pairs={{0,4},{1,5},{2,6},{3,7},{4,8},{5,9},{6,10},{7,11},{8,12},{9,13},{1... | collective-permute-start | bytes 7077896 | tf_op jit(solution)/shard_map/ppermute | solution.py:389
  244.9 51.7 %collective-permute-start.34 = (bf16[1536,768]{1,0:T(8,128)(2,1)}, bf16[1536,768]{1,0:T(8,128)(2,1)}, u32[]{:S(2)}, u32[]{:S(2)}) collective-permute-start(bf16[1536,768]{1,0:T(8,128)(2,1)} %collective-permute-done.32.refs_21_.refs_17_), channel_id=1, source_target_pairs={{4,0},{5,1},{6,2},{7,3},{8,4},{9,5},{10,6},{11,7},{12,8},{13,9},{1... | collective-permute-start | bytes 7077896 | tf_op jit(solution)/shard_map/ppermute | solution.py:393
  274.3 16.2 %collective-permute-start.21 = (bf16[256,1536]{1,0:T(8,128)(2,1)S(1)}, bf16[256,1536]{1,0:T(8,128)(2,1)S(1)}, u32[]{:S(2)}, u32[]{:S(2)}) collective-permute-start(bf16[256,1536]{1,0:T(8,128)(2,1)S(1)} %slice.253), channel_id=1, source_target_pairs={{0,2},{1,3},{2,0},{3,1},{4,6},{5,7},{6,4},{7,5},{8,10},{9,11},{10,... | collective-permute-start | bytes 2359304 | tf_op jit(solution)/shard_map/ppermute | solution.py:377
  276.5 17.9 %collective-permute-start.22 = (bf16[256,1536]{1,0:T(8,128)(2,1)S(1)}, bf16[256,1536]{1,0:T(8,128)(2,1)S(1)}, u32[]{:S(2)}, u32[]{:S(2)}) collective-permute-start(bf16[256,1536]{1,0:T(8,128)(2,1)S(1)} %slice.254), channel_id=1, source_target_pairs={{0,16},{16,0},{1,17},{17,1},{2,18},{18,2},{3,19},{19,3},{4,20},{20... | collective-permute-start | bytes 2359304 | tf_op jit(solution)/shard_map/ppermute | solution.py:373
  277.1 23.6 %collective-permute-start.29 = (bf16[256,1664]{1,0:T(8,128)(2,1)}, bf16[256,1664]{1,0:T(8,128)(2,1)S(1)}, u32[]{:S(2)}, u32[]{:S(2)}) collective-permute-start(bf16[256,1664]{1,0:T(8,128)(2,1)} %collective-permute-done.17.refs_10_), channel_id=1, source_target_pairs={{0,1},{1,0},{2,3},{3,2},{4,5},{5,4},{6,7},{7,6},{8,9},{9,8},{10,11... | collective-permute-start | bytes 2555912 | tf_op jit(solution)/shard_map/ppermute | solution.py:377
  290.5 13.7 %collective-permute-start.23 = (bf16[512,1536]{1,0:T(8,128)(2,1)}, bf16[512,1536]{1,0:T(8,128)(2,1)}, u32[]{:S(2)}, u32[]{:S(2)}) collective-permute-start(bf16[512,1536]{1,0:T(8,128)(2,1)} %collective-permute-done.19.refs_0_.refs_1_), channel_id=1, source_target_pairs={{0,1},{1,0},{2,3},{3,2},{4,5},{5,4},{6,7},{7,6},{8,9},{9,8},{10,11... | collective-permute-start | bytes 4718600 | tf_op jit(solution)/shard_map/ppermute | solution.py:377
  294.4 14.1 %collective-permute-start.27 = (bf16[512,1664]{1,0:T(8,128)(2,1)}, bf16[512,1664]{1,0:T(8,128)(2,1)}, u32[]{:S(2)}, u32[]{:S(2)}) collective-permute-start(bf16[512,1664]{1,0:T(8,128)(2,1)} %collective-permute-done.11.refs_8_.refs_7_), channel_id=1, source_target_pairs={{0,1},{1,0},{2,3},{3,2},{4,5},{5,4},{6,7},{7,6},{8,9},{9,8},{10,11... | collective-permute-start | bytes 5111816 | tf_op jit(solution)/shard_map/ppermute | solution.py:377
  296.5 11.9 %collective-permute-start.28 = (bf16[512,1664]{1,0:T(8,128)(2,1)}, bf16[512,1664]{1,0:T(8,128)(2,1)}, u32[]{:S(2)}, u32[]{:S(2)}) collective-permute-start(bf16[512,1664]{1,0:T(8,128)(2,1)} %collective-permute-done.12.refs_9_.refs_8_), channel_id=1, source_target_pairs={{0,1},{1,0},{2,3},{3,2},{4,5},{5,4},{6,7},{7,6},{8,9},{9,8},{10,11... | collective-permute-start | bytes 5111816 | tf_op jit(solution)/shard_map/ppermute | solution.py:377
  363.8 16.8 %collective-permute-start.36 = (bf16[512,1536]{1,0:T(8,128)(2,1)}, bf16[512,1536]{1,0:T(8,128)(2,1)}, u32[]{:S(2)}, u32[]{:S(2)}) collective-permute-start(bf16[512,1536]{1,0:T(8,128)(2,1)} %get-tuple-element.167.refs_0_), channel_id=1, source_target_pairs={{0,1},{1,0},{2,3},{3,2},{4,5},{5,4},{6,7},{7,6},{8,9},{9,8},{10,11... | collective-permute-start | bytes 4718600 | tf_op jit(solution)/shard_map/ppermute | solution.py:377
  363.9 16.6 %collective-permute-start.37 = (bf16[512,1664]{1,0:T(8,128)(2,1)}, bf16[512,1664]{1,0:T(8,128)(2,1)}, u32[]{:S(2)}, u32[]{:S(2)}) collective-permute-start(bf16[512,1664]{1,0:T(8,128)(2,1)} %concatenate.116.refs_6_), channel_id=1, source_target_pairs={{0,1},{1,0},{2,3},{3,2},{4,5},{5,4},{6,7},{7,6},{8,9},{9,8},{10,11... | collective-permute-start | bytes 5111816 | tf_op jit(solution)/shard_map/ppermute | solution.py:377
  376.7 59.5 %collective-permute-start.38 = (bf16[512,1536]{1,0:T(8,128)(2,1)}, bf16[512,1536]{1,0:T(8,128)(2,1)}, u32[]{:S(2)}, u32[]{:S(2)}) collective-permute-start(bf16[512,1536]{1,0:T(8,128)(2,1)} %get-tuple-element.332), channel_id=1, source_target_pairs={{0,2},{1,3},{2,0},{3,1},{4,6},{5,7},{6,4},{7,5},{8,10},{9,11},{10,... | collective-permute-start | bytes 4718600 | tf_op jit(solution)/shard_map/ppermute | solution.py:377
  377.9 58.3 %collective-permute-start.39 = (bf16[512,1536]{1,0:T(8,128)(2,1)}, bf16[512,1536]{1,0:T(8,128)(2,1)}, u32[]{:S(2)}, u32[]{:S(2)}) collective-permute-start(bf16[512,1536]{1,0:T(8,128)(2,1)} %get-tuple-element.331), channel_id=1, source_target_pairs={{0,16},{16,0},{1,17},{17,1},{2,18},{18,2},{3,19},{19,3},{4,20},{20... | collective-permute-start | bytes 4718600 | tf_op jit(solution)/shard_map/ppermute | solution.py:373
  435.2 36.9 %collective-permute-start.40 = (bf16[1024,1536]{1,0:T(8,128)(2,1)}, bf16[1024,1536]{1,0:T(8,128)(2,1)}, u32[]{:S(2)}, u32[]{:S(2)}) collective-permute-start(bf16[1024,1536]{1,0:T(8,128)(2,1)} %get-tuple-element.198), channel_id=1, source_target_pairs={{0,1},{1,0},{2,3},{3,2},{4,5},{5,4},{6,7},{7,6},{8,9},{9,8},{10,11... | collective-permute-start | bytes 9437192 | tf_op jit(solution)/shard_map/ppermute | solution.py:377
  464.1 59.6 %collective-permute-start.45 = (bf16[1536,768]{1,0:T(8,128)(2,1)}, bf16[1536,768]{1,0:T(8,128)(2,1)}, u32[]{:S(2)}, u32[]{:S(2)}) collective-permute-start(bf16[1536,768]{1,0:T(8,128)(2,1)} %pad_maximum_fusion.5), channel_id=1, source_target_pairs={{0,4},{1,5},{2,6},{3,7},{4,8},{5,9},{6,10},{7,11},{8,12},{9,13},{1... | collective-permute-start | bytes 7077896 | tf_op jit(solution)/shard_map/ppermute | solution.py:389
  470.7 61.7 %collective-permute-start.46 = (bf16[1536,768]{1,0:T(8,128)(2,1)}, bf16[1536,768]{1,0:T(8,128)(2,1)}, u32[]{:S(2)}, u32[]{:S(2)}) collective-permute-start(bf16[1536,768]{1,0:T(8,128)(2,1)} %pad_maximum_fusion.4), channel_id=1, source_target_pairs={{4,0},{5,1},{6,2},{7,3},{8,4},{9,5},{10,6},{11,7},{12,8},{13,9},{1... | collective-permute-start | bytes 7077896 | tf_op jit(solution)/shard_map/ppermute | solution.py:393
  476.9 19.4 %collective-permute-start.41 = (bf16[256,1536]{1,0:T(8,128)(2,1)S(1)}, bf16[256,1536]{1,0:T(8,128)(2,1)S(1)}, u32[]{:S(2)}, u32[]{:S(2)}) collective-permute-start(bf16[256,1536]{1,0:T(8,128)(2,1)S(1)} %get-tuple-element.318), channel_id=1, source_target_pairs={{0,16},{16,0},{1,17},{17,1},{2,18},{18,2},{3,19},{19,3},{4,20},{20... | collective-permute-start | bytes 2359304 | tf_op jit(solution)/shard_map/ppermute | solution.py:373
  477.7 18.7 %collective-permute-start.42 = (bf16[256,1536]{1,0:T(8,128)(2,1)S(1)}, bf16[256,1536]{1,0:T(8,128)(2,1)S(1)}, u32[]{:S(2)}, u32[]{:S(2)}) collective-permute-start(bf16[256,1536]{1,0:T(8,128)(2,1)S(1)} %get-tuple-element.319), channel_id=1, source_target_pairs={{0,2},{1,3},{2,0},{3,1},{4,6},{5,7},{6,4},{7,5},{8,10},{9,11},{10,... | collective-permute-start | bytes 2359304 | tf_op jit(solution)/shard_map/ppermute | solution.py:377
  506.4 30.9 %collective-permute-start.47 = (bf16[1024,1536]{1,0:T(8,128)(2,1)S(1)}, bf16[1024,1536]{1,0:T(8,128)(2,1)}, u32[]{:S(2)}, u32[]{:S(2)}) collective-permute-start(bf16[1024,1536]{1,0:T(8,128)(2,1)S(1)} %copy-done.56), channel_id=1, source_target_pairs={{0,1},{1,0},{2,3},{3,2},{4,5},{5,4},{6,7},{7,6},{8,9},{9,8},{10,11... | collective-permute-start | bytes 9437192 | tf_op jit(solution)/shard_map/ppermute | solution.py:377
  518.0 106.6 %collective-permute-start.43 = (bf16[1024,1536]{1,0:T(8,128)(2,1)}, bf16[1024,1536]{1,0:T(8,128)(2,1)}, u32[]{:S(2)}, u32[]{:S(2)}) collective-permute-start(bf16[1024,1536]{1,0:T(8,128)(2,1)} %get-tuple-element.208), channel_id=1, source_target_pairs={{0,1},{1,0},{2,3},{3,2},{4,5},{5,4},{6,7},{7,6},{8,9},{9,8},{10,11... | collective-permute-start | bytes 9437192 | tf_op jit(solution)/shard_map/ppermute | solution.py:377
  522.5 20.3 %collective-permute-start.44 = (bf16[512,768]{1,0:T(8,128)(2,1)S(1)}, bf16[512,768]{1,0:T(8,128)(2,1)S(1)}, u32[]{:S(2)}, u32[]{:S(2)}) collective-permute-start(bf16[512,768]{1,0:T(8,128)(2,1)S(1)} %fusion.43), channel_id=1, source_target_pairs={{0,16},{16,0},{1,17},{17,1},{2,18},{18,2},{3,19},{19,3},{4,20},{20... | collective-permute-start | bytes 2359304 | tf_op jit(solution)/shard_map/ppermute | solution.py:373
  527.0 75.7 %collective-permute-start.48 = (bf16[1536,768]{1,0:T(8,128)(2,1)}, bf16[1536,768]{1,0:T(8,128)(2,1)}, u32[]{:S(2)}, u32[]{:S(2)}) collective-permute-start(bf16[1536,768]{1,0:T(8,128)(2,1)} %add_convert_fusion.6), channel_id=1, source_target_pairs={{0,4},{1,5},{2,6},{3,7},{4,8},{5,9},{6,10},{7,11},{8,12},{9,13},{1... | collective-permute-start | bytes 7077896 | tf_op jit(solution)/shard_map/ppermute | solution.py:389
  535.8 66.9 %collective-permute-start.49 = (bf16[1536,768]{1,0:T(8,128)(2,1)}, bf16[1536,768]{1,0:T(8,128)(2,1)}, u32[]{:S(2)}, u32[]{:S(2)}) collective-permute-start(bf16[1536,768]{1,0:T(8,128)(2,1)} %add_convert_fusion.5), channel_id=1, source_target_pairs={{4,0},{5,1},{6,2},{7,3},{8,4},{9,5},{10,6},{11,7},{12,8},{13,9},{1... | collective-permute-start | bytes 7077896 | tf_op jit(solution)/shard_map/ppermute | solution.py:393
  541.9 60.8 %collective-permute-start.50 = (bf16[512,1536]{1,0:T(8,128)(2,1)}, bf16[512,1536]{1,0:T(8,128)(2,1)}, u32[]{:S(2)}, u32[]{:S(2)}) collective-permute-start(bf16[512,1536]{1,0:T(8,128)(2,1)} %get-tuple-element.326), channel_id=1, source_target_pairs={{0,2},{1,3},{2,0},{3,1},{4,6},{5,7},{6,4},{7,5},{8,10},{9,11},{10,... | collective-permute-start | bytes 4718600 | tf_op jit(solution)/shard_map/ppermute | solution.py:377
  542.9 59.9 %collective-permute-start.51 = (bf16[512,1536]{1,0:T(8,128)(2,1)}, bf16[512,1536]{1,0:T(8,128)(2,1)}, u32[]{:S(2)}, u32[]{:S(2)}) collective-permute-start(bf16[512,1536]{1,0:T(8,128)(2,1)} %get-tuple-element.325), channel_id=1, source_target_pairs={{0,16},{16,0},{1,17},{17,1},{2,18},{18,2},{3,19},{19,3},{4,20},{20... | collective-permute-start | bytes 4718600 | tf_op jit(solution)/shard_map/ppermute | solution.py:373
  620.8 48.1 %collective-permute-start.54 = (bf16[2,2,4,48,1408]{4,3,2,1,0:T(8,128)(2,1)S(1)}, bf16[2,2,4,48,1408]{4,3,2,1,0:T(8,128)(2,1)S(1)}, u32[]{:S(2)}, u32[]{:S(2)}) collective-permute-start(bf16[2,2,4,48,1408]{4,3,2,1,0:T(8,128)(2,1)S(1)} %dynamic-slice_bitcast_fusion), channel_id=1, source_target_pairs={{0,1},{1,0},{2,3},{3,2},{4,5},{5,4},{6,7},{7,6},{8,9},{9,8},{10,11... | collective-permute-start | bytes 6488072 | tf_op jit(solution)/shard_map/ppermute | solution.py:377
  629.5 20.7 %collective-permute-start.52 = (bf16[256,1536]{1,0:T(8,128)(2,1)S(1)}, bf16[256,1536]{1,0:T(8,128)(2,1)S(1)}, u32[]{:S(2)}, u32[]{:S(2)}) collective-permute-start(bf16[256,1536]{1,0:T(8,128)(2,1)S(1)} %fusion.32), channel_id=1, source_target_pairs={{0,16},{16,0},{1,17},{17,1},{2,18},{18,2},{3,19},{19,3},{4,20},{20... | collective-permute-start | bytes 2359304 | tf_op jit(solution)/shard_map/ppermute | solution.py:373
  632.9 25.9 %collective-permute-start.57 = (bf16[512,768]{1,0:T(8,128)(2,1)S(1)}, bf16[512,768]{1,0:T(8,128)(2,1)S(1)}, u32[]{:S(2)}, u32[]{:S(2)}) collective-permute-start(bf16[512,768]{1,0:T(8,128)(2,1)S(1)} %get-tuple-element.343), channel_id=1, source_target_pairs={{0,4},{1,5},{2,6},{3,7},{4,8},{5,9},{6,10},{7,11},{8,12},{9,13},{1... | collective-permute-start | bytes 2359304 | tf_op jit(solution)/shard_map/ppermute | solution.py:389
  638.3 25.5 %collective-permute-start.58 = (bf16[512,768]{1,0:T(8,128)(2,1)S(1)}, bf16[512,768]{1,0:T(8,128)(2,1)S(1)}, u32[]{:S(2)}, u32[]{:S(2)}) collective-permute-start(bf16[512,768]{1,0:T(8,128)(2,1)S(1)} %get-tuple-element.340), channel_id=1, source_target_pairs={{4,0},{5,1},{6,2},{7,3},{8,4},{9,5},{10,6},{11,7},{12,8},{13,9},{1... | collective-permute-start | bytes 2359304 | tf_op jit(solution)/shard_map/ppermute | solution.py:393
  653.5 43.5 %collective-permute-start.53 = (bf16[256,1536]{1,0:T(8,128)(2,1)}, bf16[256,1536]{1,0:T(8,128)(2,1)}, u32[]{:S(2)}, u32[]{:S(2)}) collective-permute-start(bf16[256,1536]{1,0:T(8,128)(2,1)} %get-tuple-element.315), channel_id=1, source_target_pairs={{0,2},{1,3},{2,0},{3,1},{4,6},{5,7},{6,4},{7,5},{8,10},{9,11},{10,... | collective-permute-start | bytes 2359304 | tf_op jit(solution)/shard_map/ppermute | solution.py:377
  663.8 26.9 %collective-permute-start.59 = (bf16[512,768]{1,0:T(8,128)(2,1)}, bf16[512,768]{1,0:T(8,128)(2,1)}, u32[]{:S(2)}, u32[]{:S(2)}) collective-permute-start(bf16[512,768]{1,0:T(8,128)(2,1)} %get-tuple-element.236), channel_id=1, source_target_pairs={{0,4},{1,5},{2,6},{3,7},{4,8},{5,9},{6,10},{7,11},{8,12},{9,13},{1... | collective-permute-start | bytes 2359304 | tf_op jit(solution)/shard_map/ppermute | solution.py:389
  667.6 23.1 %collective-permute-start.60 = (bf16[512,768]{1,0:T(8,128)(2,1)}, bf16[512,768]{1,0:T(8,128)(2,1)}, u32[]{:S(2)}, u32[]{:S(2)}) collective-permute-start(bf16[512,768]{1,0:T(8,128)(2,1)} %get-tuple-element.237), channel_id=1, source_target_pairs={{4,0},{5,1},{6,2},{7,3},{8,4},{9,5},{10,6},{11,7},{12,8},{13,9},{1... | collective-permute-start | bytes 2359304 | tf_op jit(solution)/shard_map/ppermute | solution.py:393
  684.3 24.0 %collective-permute-start.56 = (bf16[2,4,48,1408]{3,2,1,0:T(8,128)(2,1)S(1)}, bf16[2,4,48,1408]{3,2,1,0:T(8,128)(2,1)S(1)}, u32[]{:S(2)}, u32[]{:S(2)}) collective-permute-start(bf16[2,4,48,1408]{3,2,1,0:T(8,128)(2,1)S(1)} %fusion.50), channel_id=1, source_target_pairs={{0,2},{1,3},{2,0},{3,1},{4,6},{5,7},{6,4},{7,5},{8,10},{9,11},{10,... | collective-permute-start | bytes 3244040 | tf_op jit(solution)/shard_map/ppermute | solution.py:377
  690.7 19.4 %collective-permute-start.61 = (bf16[512,768]{1,0:T(8,128)(2,1)}, bf16[512,768]{1,0:T(8,128)(2,1)}, u32[]{:S(2)}, u32[]{:S(2)}) collective-permute-start(bf16[512,768]{1,0:T(8,128)(2,1)} %get-tuple-element.238), channel_id=1, source_target_pairs={{0,4},{1,5},{2,6},{3,7},{4,8},{5,9},{6,10},{7,11},{8,12},{9,13},{1... | collective-permute-start | bytes 2359304 | tf_op jit(solution)/shard_map/ppermute | solution.py:389
  695.7 19.2 %collective-permute-start.62 = (bf16[512,768]{1,0:T(8,128)(2,1)}, bf16[512,768]{1,0:T(8,128)(2,1)}, u32[]{:S(2)}, u32[]{:S(2)}) collective-permute-start(bf16[512,768]{1,0:T(8,128)(2,1)} %get-tuple-element.239), channel_id=1, source_target_pairs={{4,0},{5,1},{6,2},{7,3},{8,4},{9,5},{10,6},{11,7},{12,8},{13,9},{1... | collective-permute-start | bytes 2359304 | tf_op jit(solution)/shard_map/ppermute | solution.py:393
  700.2 43.2 %collective-permute-start.55 = (bf16[512,1536]{1,0:T(8,128)(2,1)}, bf16[512,1536]{1,0:T(8,128)(2,1)}, u32[]{:S(2)}, u32[]{:S(2)}) collective-permute-start(bf16[512,1536]{1,0:T(8,128)(2,1)} %get-tuple-element.234), channel_id=1, source_target_pairs={{0,16},{16,0},{1,17},{17,1},{2,18},{18,2},{3,19},{19,3},{4,20},{20... | collective-permute-start | bytes 4718600 | tf_op jit(solution)/shard_map/ppermute | solution.py:373
  721.1 13.4 %collective-permute-start.65 = (bf16[2,48,1408]{2,1,0:T(8,128)(2,1)S(1)}, bf16[2,48,1408]{2,1,0:T(8,128)(2,1)S(1)}, u32[]{:S(2)}, u32[]{:S(2)}) collective-permute-start(bf16[2,48,1408]{2,1,0:T(8,128)(2,1)S(1)} %fusion.61), channel_id=1, source_target_pairs={{0,12},{1,13},{2,14},{3,15},{4,8},{5,9},{6,10},{7,11},{8,4},{9,5},... | collective-permute-start | bytes 811016 | tf_op jit(solution)/shard_map/ppermute | solution.py:377
  721.2 22.0 %collective-permute-start.64 = (bf16[2,48,1408]{2,1,0:T(8,128)(2,1)S(1)}, bf16[2,48,1408]{2,1,0:T(8,128)(2,1)S(1)}, u32[]{:S(2)}, u32[]{:S(2)}) collective-permute-start(bf16[2,48,1408]{2,1,0:T(8,128)(2,1)S(1)} %get-tuple-element.359), channel_id=1, source_target_pairs={{0,8},{1,9},{2,10},{3,11},{4,12},{5,13},{6,14},{7,15},{8,0},{9,1},... | collective-permute-start | bytes 811016 | tf_op jit(solution)/shard_map/ppermute | solution.py:377
  721.8 21.4 %collective-permute-start.63 = (bf16[2,48,1408]{2,1,0:T(8,128)(2,1)S(1)}, bf16[2,48,1408]{2,1,0:T(8,128)(2,1)S(1)}, u32[]{:S(2)}, u32[]{:S(2)}) collective-permute-start(bf16[2,48,1408]{2,1,0:T(8,128)(2,1)S(1)} %get-tuple-element.358), channel_id=1, source_target_pairs={{0,4},{1,5},{2,6},{3,7},{4,0},{5,1},{6,2},{7,3},{8,12},{9,13},{10,... | collective-permute-start | bytes 811016 | tf_op jit(solution)/shard_map/ppermute | solution.py:377
  726.8 35.1 %collective-permute-start.66 = (bf16[1536,512]{1,0:T(8,128)(2,1)S(1)}, bf16[1536,512]{1,0:T(8,128)(2,1)S(1)}, u32[]{:S(2)}, u32[]{:S(2)}) collective-permute-start(bf16[1536,512]{1,0:T(8,128)(2,1)S(1)} %pad_maximum_fusion.10), channel_id=1, source_target_pairs={{0,0},{1,16},{2,2},{3,18},{4,4},{5,20},{6,6},{7,22},{8,8},{9,24},{... | collective-permute-start | bytes 4718600 | tf_op jit(solution)/shard_map/ppermute | solution.py:1075
  734.5 19.3 %collective-permute-start.67 = (bf16[1536,256]{1,0:T(8,128)(2,1)S(1)}, bf16[1536,256]{1,0:T(8,128)(2,1)S(1)}, u32[]{:S(2)}, u32[]{:S(2)}) collective-permute-start(bf16[1536,256]{1,0:T(8,128)(2,1)S(1)} %get-tuple-element.249), channel_id=1, source_target_pairs={{1,0},{17,1},{3,2},{19,3},{5,4},{21,5},{7,6},{23,7},{9,8},{25,9},{... | collective-permute-start | bytes 2359304 | tf_op jit(solution)/shard_map/ppermute | solution.py:1075
  (76 other events, 1230.9 us)
Sparse Core Ops, SparseCore 0:
  50.4 68.4 all-gather.1
  557.8 108.4 reduce-scatter.1

commit v7 on v6

--- a/solution.py
+++ b/solution.py
@@ -1117,8 +1117,6 @@
         axis=1,
     )
     other_tokens = swap_seq(after(tokens, own_part))
-    output_full = lax.all_gather(after(output_pair, own_part), "dp", axis=1, tiled=True)
-    output_full = output_full.reshape(width, width)
     cut = width // 2
     lines = (line_up(own_part[:cut]), line_down(own_part[:cut]))
     qkv_rows = after(jnp.concatenate(along, axis=0), own_part)
@@ -1175,35 +1173,29 @@
         return contract(sort, values, 0, 0).astype(BF16)
 
     x_sorted = to_order(tokens, other_tokens)
+    x_sorted, late_lines = lax.optimization_barrier((x_sorted, late_lines))
+    up_one = jnp.concatenate([lines[0], late_lines[0]], axis=0)
+    down_one = jnp.concatenate([lines[1], late_lines[1]], axis=0)
+    x_sorted, up_one, down_one = lax.optimization_barrier((x_sorted, up_one, down_one))
+    up_two, down_two = line_up(up_one), line_down(down_one)
     normed, query, keys, values, w_qkv, gains = project(
         places_of, x_sorted, qkv_rows, qkv_others, cos, sin, q_width, kv_heads
     )
     gain_one, gain_two = gains[0], gains[1]
-    pairs = q_width // (2 * HDIM)
-    first_pairs = 2 * pairs // 3
-    mixed_one, levels_one = attend(query, keys, values, start_column, 0, first_pairs)
-    sent_one = swap_seq(from_order(sort_other, mixed_one))
-    lines, late_lines = after((lines, late_lines), mixed_one)
-    up_one = jnp.concatenate([lines[0], late_lines[0]], axis=0)
-    down_one = jnp.concatenate([lines[1], late_lines[1]], axis=0)
-    query_two, grad_near_x, grad_near_y, up_one, down_one = after(
-        (query, *grad_near, up_one, down_one), mixed_one
-    )
-    up_two, down_two = line_up(up_one), line_down(down_one)
-    grad_near = (grad_near_x, grad_near_y)
+    output_full = lax.all_gather(after(output_pair, query), "dp", axis=1, tiled=True)
+    output_full = output_full.reshape(width, width)
+    mixed_sorted, levels = attend(
+        query, keys, values, start_column, 0, q_width // (2 * HDIM)
+    )
+    mixed_sorted, grad_near = lax.optimization_barrier((mixed_sorted, grad_near))
+    mixed_theirs = swap_seq(from_order(sort_other, mixed_sorted))
+    mixed_mine = from_order(sort_own, mixed_sorted)
+    grad_near = after(grad_near, mixed_theirs)
     grad_far = far_pieces(*grad_near)
-    mixed_two, levels_two = attend(
-        query_two, keys, values, start_column, first_pairs, pairs - first_pairs
-    )
-    sent_two = swap_seq(from_order(sort_other, mixed_two))
-    mixed_mine = [from_order(sort_own, mixed_one), from_order(sort_own, mixed_two)]
-    mixed_mine = jnp.concatenate(mixed_mine, axis=1)
-    mixed_theirs = jnp.concatenate([sent_one, sent_two], axis=1)
     inputs = tokens.astype(F32)
     middle, normed_ffn, output_parts = mix(
         seq.astype(jnp.int32)[None], mixed_mine, mixed_theirs, tokens, gain_two[None, :], output_full
     )
-    normed_ffn = after(normed_ffn, *grad_far)
     up_two, down_two = after((up_two, down_two), normed_ffn)
     up_three, down_three = line_up(up_two), line_down(down_two)
     row_near = near_pieces(normed_ffn, normed_ffn)
@@ -1285,7 +1277,7 @@
         keys,
         values,
         grad_sorted,
-        jnp.concatenate([levels_one, levels_two], axis=0),
+        levels,
         start_column,
         cos,
         sin,
@@ -1294,12 +1286,9 @@
         ((grad_query, grad_keys, grad_values), mid_line, ffn_y, ffn_x)
     )
     right, left = line_step(2, mid_line)
-    third = width // 3
-    last_first = (line_up(right[:third]), line_down(left[:third]))
+    last_first = (line_up(right[:cut]), line_down(left[:cut]))
     first_ffn, second_ffn = near_links(near_ffn, ffn_y, ffn_x)
     first_ffn, second_ffn = swap_seq(first_ffn), swap_y(second_ffn)
-    ffn = own_sum(near_ffn, ffn_y, ffn_x, first_ffn, second_ffn)
-    output = (middle + BRANCH_SCALE * ffn).astype(BF16)
     grads_qkv = after((grad_query, grad_keys, grad_values), right, left)
     wide = qkv_grad(normed, grads_qkv, grad_gain_two[None, :], shard)
 
@@ -1317,11 +1306,7 @@
         grads_late, w_qkv, own_places[:, None], other_places[:, None]
     )
     kept, sent_normed = lax.optimization_barrier((kept, sent_normed))
-    right_mid, left_mid = after((right[third : 2 * third], left[third : 2 * third]), last_first)
-    last_mid = (line_up(right_mid), line_down(left_mid))
-    right_late, left_late = after(
-        (right[2 * third :], left[2 * third :]), last_mid, sent_normed
-    )
+    right_late, left_late = after((right[cut:], left[cut:]), last_first, sent_normed)
     last_late = (line_up(right_late), line_down(left_late))
     grad_normed = grad_normed.astype(F32) + swap_seq(sent_normed).astype(F32)
     scale = lax.rsqrt(jnp.mean(inputs * inputs, axis=-1, keepdims=True) + EPSILON)
@@ -1331,16 +1316,14 @@
     grad_tokens = grad_middle + scale * (scaled - unit * inner)
     next_kept = chosen(kept, row_of, 0)
     next_kept = next_kept + swap_y(chosen(kept, 1 - row_of, 0).astype(BF16)).astype(F32)
-    next_kept, last_first, last_mid, last_late, summed_output = lax.optimization_barrier(
-        (next_kept, last_first, last_mid, last_late, summed_output)
+    next_kept, last_first, last_late, summed_output = lax.optimization_barrier(
+        (next_kept, last_first, last_late, summed_output)
     )
     own_grads = line_partial(*range(LINE))
     part_grads = jnp.concatenate(
         [
             own + up.astype(F32) + down.astype(F32)
-            for own, (up, down) in zip(
-                jnp.split(own_grads, 3, axis=0), (last_first, last_mid, last_late)
-            )
+            for own, (up, down) in ((own_grads[:cut], last_first), (own_grads[cut:], last_late))
         ],
         axis=0,
     ).astype(BF16)
@@ -1352,24 +1335,29 @@
     )
     same = both_axes(same_grads, straight)
     cross = both_axes(cross_grads, crossed_back)
+    kept_half = chosen(next_kept, seq, 0)
+    sent_half = swap_seq(chosen(next_kept, 1 - seq, 0).astype(BF16)).astype(F32)
+    cuts = (q_width, q_width + kv_width, qkv_width)
+    pieces = list(zip(jnp.split(kept_half, cuts, axis=2), jnp.split(sent_half, cuts, axis=2)))
+    full = jnp.concatenate(
+        [ordered(a, b, 2) for a, b in pieces[:3]] + [pieces[3][0] + pieces[3][1]], axis=2
+    )
+    low = full.astype(BF16)
     sent_lines = [
-        swap_dp(chosen(next_kept, line ^ step, 1).astype(BF16), 4 * step) for step in range(1, LINE)
+        swap_dp(chosen(low, line ^ step, 0), 4 * step) for step in range(1, LINE)
     ]
-    summed = chosen(next_kept, line, 1) + sum(value.astype(F32) for value in sent_lines)
-    summed, same, cross = lax.optimization_barrier((summed, same, cross))
+    first_ffn, second_ffn = after((first_ffn, second_ffn), low)
+    ffn = own_sum(near_ffn, ffn_y, ffn_x, first_ffn, second_ffn)
+    output = (middle + BRANCH_SCALE * ffn).astype(BF16)
+    summed = chosen(full, line, 0) + sum(value.astype(F32) for value in sent_lines)
     grad_w_in = ordered(same[:, :half], cross, 1)
     grad_w_out = same[:, half:].T
-    kept_rows = chosen(summed, seq, 0)
-    sent_rows = swap_seq(chosen(summed, 1 - seq, 0).astype(BF16)).astype(F32)
-    cuts = (q_width, q_width + kv_width, qkv_width)
-    pieces = [
-        (a, b) for a, b in zip(jnp.split(kept_rows, cuts, axis=1), jnp.split(sent_rows, cuts, axis=1))
-    ]
-    grad_projections = [ordered(a, b, 1) for a, b in pieces[:3]]
-    grad_gain_ffn = (pieces[3][0] + pieces[3][1])[:, 0]
+    cuts = (2 * q_width, 2 * (q_width + kv_width), 2 * qkv_width)
+    grad_projections = jnp.split(summed, cuts, axis=1)
+    grad_gain_ffn = grad_projections[3][:, 0]
     grad_gain_attn = sum(
         jnp.sum(grad * weight.astype(F32), axis=1)
-        for grad, weight in zip(grad_projections, projections)
+        for grad, weight in zip(grad_projections[:3], projections)
     ) / gain_attn.astype(F32)
     return (
         output,

time: 786 us -> 855 us (1.088)
  waiting for transfers between devices: 176 us -> 259 us
  other arithmetic: 97.1 us -> 88.5 us
    ppermute x15 -> x14, waiting for transfers between devices: 60.3 us -> 109 us  [swap_seq(): return lax.ppermute(value, 'seq', [(0, 1), (1, 0)])]
    ppermute x32, waiting for transfers between devices: 71.3 us -> 107 us  [swap_dp(): return lax.ppermute(value, 'dp', [(i, i ^ mask) for i in range(4 * LINE)])]
    ppermute x9 -> x8, waiting for transfers between devices: 5.43 us -> 22.2 us  [line_up(): return lax.ppermute(value, 'dp', [(i, i + 4) for i in range(4 * LINE - 4)])]
    ppermute x4, waiting for transfers between devices: 16.2 us -> 0.01 us  [both_axes(): return lax.ppermute(value, ('seq', 'dp'), pairs)]
    ppermute x32, starting transfers between devices: 51.8 us -> 37.3 us  [swap_dp(): return lax.ppermute(value, 'dp', [(i, i ^ mask) for i in range(4 * LINE)])]
    ppermute x15 -> x14, starting transfers between devices: 14.8 us -> 24.3 us  [swap_seq(): return lax.ppermute(value, 'seq', [(0, 1), (1, 0)])]
    dot_general x15 -> x13, matrix products: 81.4 us -> 84.7 us  [contract(): lax.dot_general(left, right, (((left_dim,), (right_dim,)), ((), ())), pre...]
    ppermute x9 -> x8, starting transfers between devices: 39.3 us -> 36.4 us  [line_up(): return lax.ppermute(value, 'dp', [(i, i + 4) for i in range(4 * LINE - 4)])]
  transfers between devices with their start and end apart: 71 -> 68, of which waited for: 22 -> 30; matrix products, arithmetic and copies ran while one was open for 28% -> 24% of each run, Pallas kernels for 21% -> 18%
where the time goes in v7:
time: 855 us; the launch traced here: 847 us
  waiting for transfers between devices  259 us (30%)
  Pallas kernels  219 us (26%)
  starting transfers between devices  127 us (15%)
  other arithmetic  88.5 us (10%)
  matrix products  84.7 us (10%)
  local copies, waits for them, and re-layouts  52.8 us (6%)
  between operations  15.7 us (2%)
    pallas_call x2, Pallas kernels, run_experts(): pl.pallas_call(functools.partial(experts_kernel, tiles, tile // 2), grid_...  110 us
    ppermute x14, waiting for transfers between devices, swap_seq(): return lax.ppermute(value, 'seq', [(0, 1), (1, 0)])  109 us
    ppermute x32, waiting for transfers between devices, swap_dp(): return lax.ppermute(value, 'dp', [(i, i ^ mask) for i in range(4 * LINE)])  107 us
    dot_general x13, matrix products, contract(): lax.dot_general(left, right, (((left_dim,), (right_dim,)), ((), ())), pre...  84.7 us
    pallas_call x1, Pallas kernels, attend_back(): pl.pallas_call(attend_back_kernel, grid=(pairs,), in_specs=[pair_block, w...  40.6 us
    ppermute x32, starting transfers between devices, swap_dp(): return lax.ppermute(value, 'dp', [(i, i ^ mask) for i in range(4 * LINE)])  37.3 us
    ppermute x8, starting transfers between devices, line_up(): return lax.ppermute(value, 'dp', [(i, i + 4) for i in range(4 * LINE - 4)])  36.4 us
    pallas_call x1, Pallas kernels, attend(): pl.pallas_call(functools.partial(attend_kernel, base), grid=(pairs,), in_...  27.5 us
  transfers between devices with their start and end apart: 68, of which 30 were waited for; matrix products, arithmetic and copies ran while one was open for 24% of the time, Pallas kernels for 18%

profile of v7, /device:TPU:1, one launch (start us, length us, event | category | flops | bytes accessed | tf_op | source)
XLA Modules:
  0.0 847.2 jit_solution(17245888679388579415)
XLA Ops:
  10.0 4.6 collective-permute-start
  20.9 17.2 %collective-permute-done.2 = bf16[48,2944]{1,0:T(8,128)(2,1)S(1)} collective-permute-done((bf16[48,2944]{1,0:T(8,128)(2,1)}, bf16[48,2944]{1,0:T(8,128)(2,1)S(1)}, u32[]{:S(2)}, u32[]{:S(2)}) %collective-permute-start.2) | collective-permute-done | bytes 282656 | tf_op jit(solution)/shard_map/ppermute | solution.py:373
  43.6 6.5 collective-permute-done.3
  50.7 8.8 %collective-permute-done.5 = bf16[48,2816]{1,0:T(8,128)(2,1)} collective-permute-done((bf16[48,2816]{1,0:T(8,128)(2,1)S(1)}, bf16[48,2816]{1,0:T(8,128)(2,1)}, u32[]{:S(2)}, u32[]{:S(2)}) %collective-permute-start.5) | collective-permute-done | bytes 270368 | tf_op jit(solution)/shard_map/ppermute | solution.py:377
  62.8 8.0 collective-permute-start.8
  78.4 3.3 collective-permute-start.6
  82.8 13.2 %collective-permute-done.7 = bf16[192,2816]{1,0:T(8,128)(2,1)S(1)} collective-permute-done((bf16[192,2816]{1,0:T(8,128)(2,1)S(1)}, bf16[192,2816]{1,0:T(8,128)(2,1)S(1)}, u32[]{:S(2)}, u32[]{:S(2)}) %collective-permute-start.7) | collective-permute-done | bytes 1081376 | tf_op jit(solution)/shard_map/ppermute | solution.py:377
  98.6 3.6 collective-permute-start.12
  102.8 4.4 fusion.27
  107.2 4.2 collective-permute-start.10
  115.0 6.8 add_convert_fusion.2.x_ref
  121.8 14.2 %collective-permute-done.10 = bf16[768,768]{1,0:T(8,128)(2,1)} collective-permute-done((bf16[768,768]{1,0:T(8,128)(2,1)}, bf16[768,768]{1,0:T(8,128)(2,1)}, u32[]{:S(2)}, u32[]{:S(2)}) %collective-permute-start.10) | collective-permute-done | bytes 1179680 | tf_op jit(solution)/shard_map/ppermute | solution.py:389
  136.0 4.8 collective-permute-done.11
  140.9 3.0 pad_maximum_fusion.2
  143.9 13.1 %project.1 = (bf16[1024,1536]{1,0:T(8,128)(2,1)}, bf16[1024,768]{1,0:T(8,128)(2,1)}, bf16[4,1024,64]{2,1,0:T(8,128)(2,1)}, bf16[4,1024,64]{2,1,0:T(8,128)(2,1)},...) custom-call(s32[3]{0:T(128)} %pad_add_fusion.place_ref, bf16[1024,1536]{1,0:T(8,128)(2,1)} %add_convert_fusion.2.x_ref, ...), custom_call_target="tpu_custom_call" | custom-call | flops 251658240 | bytes 3538944 | tf_op jit(solution)/shard_map/project/pallas_call | solution.py:524
  157.7 3.8 concatenate.103.refs_6_
  162.7 3.3 collective-permute-start.13
  171.5 27.5 %attend.1 = (bf16[1024,768]{1,0:T(8,128)(2,1)}, f32[6,1024,2]{2,1,0:T(8,128)}) custom-call(bf16[1024,768]{1,0:T(8,128)(2,1)} %get-tuple-element.148.q_ref, bf16[4,1024,64]{2,1,0:T(8,128)(2,1)} %get-tuple-element.149.k_ref, bf16[4,1024,64]{2,1,0:T(8,128)(2,1)} %get-tuple-element.150.v_ref, s32[1024,1]{1,0:T(8,128)} %copy.84.start_ref), custom_call_target="tpu_custom_call" | custom-call | flops 226492416 | bytes 6291456 | tf_op jit(solution)/shard_map/attend/pallas_call | solution.py:710
  199.0 10.3 %collective-permute-done.14.refs_9_.refs_8_ = bf16[512,1664]{1,0:T(8,128)(2,1)} collective-permute-done((bf16[512,1664]{1,0:T(8,128)(2,1)}, bf16[512,1664]{1,0:T(8,128)(2,1)}, u32[]{:S(2)}, u32[]{:S(2)}) %collective-permute-start.14) | collective-permute-done | bytes 1703968 | tf_op jit(solution)/shard_map/ppermute | solution.py:377
  212.0 5.5 collective-permute-start.15
  219.6 10.9 %collective-permute-done.15.theirs_ref = bf16[512,768]{1,0:T(8,128)(2,1)S(1)} collective-permute-done((bf16[512,768]{1,0:T(8,128)(2,1)S(1)}, bf16[512,768]{1,0:T(8,128)(2,1)S(1)}, u32[]{:S(2)}, u32[]{:S(2)}) %collective-permute-start.15) | collective-permute-done | bytes 786464 | tf_op jit(solution)/shard_map/ppermute | solution.py:373
  233.2 9.3 %mix.1 = (f32[512,1536]{1,0:T(8,128)}, bf16[512,1536]{1,0:T(8,128)(2,1)}, bf16[2,768,1536]{2,1,0:T(8,128)(2,1)}) custom-call(s32[1]{0:T(128)} %bitcast.place_ref, bf16[512,768]{1,0:T(8,128)(2,1)} %get-tuple-element.373.mine_ref, bf16[512,768]{1,0:T(8,128)(2,1)} %copy-done.44, bf16[512,1536]{1,0:T(8,128)(2,1)} %x_ref.1, ...), custom_call_target="tpu_custom_call" | custom-call | flops 150994944 | bytes 786432 | tf_op jit(solution)/shard_map/mix/pallas_call | solution.py:588
  255.4 17.7 %collective-permute-done.16.refs_0_.refs_1_ = bf16[512,1536]{1,0:T(8,128)(2,1)} collective-permute-done((bf16[512,1536]{1,0:T(8,128)(2,1)}, bf16[512,1536]{1,0:T(8,128)(2,1)}, u32[]{:S(2)}, u32[]{:S(2)}) %collective-permute-start.16) | collective-permute-done | bytes 1572896 | tf_op jit(solution)/shard_map/ppermute | solution.py:373
  275.3 10.2 %collective-permute-done.17.refs_1_.refs_2_ = bf16[512,1536]{1,0:T(8,128)(2,1)S(1)} collective-permute-done((bf16[512,1536]{1,0:T(8,128)(2,1)}, bf16[512,1536]{1,0:T(8,128)(2,1)S(1)}, u32[]{:S(2)}, u32[]{:S(2)}) %collective-permute-start.17) | collective-permute-done | bytes 1572896 | tf_op jit(solution)/shard_map/ppermute | solution.py:377
  287.2 16.5 %collective-permute-done.24.refs_10_ = bf16[256,1664]{1,0:T(8,128)(2,1)S(1)} collective-permute-done((bf16[256,1664]{1,0:T(8,128)(2,1)S(1)}, bf16[256,1664]{1,0:T(8,128)(2,1)S(1)}, u32[]{:S(2)}, u32[]{:S(2)}) %collective-permute-start.24) | collective-permute-done | bytes 852000 | tf_op jit(solution)/shard_map/ppermute | solution.py:377
  306.2 4.6 collective-permute-start.28
  311.3 9.2 %collective-permute-done.18.refs_2_ = bf16[256,1536]{1,0:T(8,128)(2,1)S(1)} collective-permute-done((bf16[256,1536]{1,0:T(8,128)(2,1)S(1)}, bf16[256,1536]{1,0:T(8,128)(2,1)S(1)}, u32[]{:S(2)}, u32[]{:S(2)}) %collective-permute-start.18) | collective-permute-done | bytes 786464 | tf_op jit(solution)/shard_map/ppermute | solution.py:377
  320.5 3.0 collective-permute-start.27
  335.2 55.0 %experts.2 = (bf16[1024,1536]{1,0:T(8,128)(2,1)}, bf16[1024,1536]{1,0:T(8,128)(2,1)}, bf16[1024,1536]{1,0:T(8,128)(2,1)}, bf16[1024,1536]{1,0:T(8,128)(2,1)}, bf...) custom-call(s32[1]{0:T(128)} %bitcast.2.place_ref, ...), custom_call_target="tpu_custom_call" | custom-call | flops 2415919104 | bytes 50331648 | tf_op jit(solution)/shard_map/experts/pallas_call | solution.py:957
  391.2 8.2 collective-permute-done.34
  407.4 54.6 %experts.3 = (bf16[1024,1536]{1,0:T(8,128)(2,1)}, bf16[1024,1536]{1,0:T(8,128)(2,1)}, bf16[1024,1536]{1,0:T(8,128)(2,1)}, bf16[1024,1536]{1,0:T(8,128)(2,1)}, bf...) custom-call(s32[1]{0:T(128)} %bitcast.2.place_ref, ...), custom_call_target="tpu_custom_call", output_to_operand_aliasing={{4}: (21, {}), {5}: (22, {}), {6}: (23, {}), {7}: (24, {}),... | custom-call | flops 2415919104 | bytes 50331648 | tf_op jit(solution)/shard_map/experts/pallas_call | solution.py:957
  463.0 11.2 %fusion.11 = bf16[1536,512]{1,0:T(8,128)(2,1)S(1)} fusion(bf16[4096,1536]{1,0:T(8,128)(2,1)} %get-tuple-element.197, bf16[4096,512]{1,0:T(8,128)(2,1)} %get-tuple-element.190), kind=kOutput, calls=%fused_computation.37 | convolution fusion | flops 6444023808 | bytes 18350080 | tf_op jit(solution)/shard_map/dot_general | solution.py:668
  474.7 14.1 %convolution_convert_fusion.1 = bf16[1536,1024]{1,0:T(8,128)(2,1)S(1)} fusion(bf16[4096,1536]{1,0:T(8,128)(2,1)S(1)} %copy-done.22, bf16[4096,1024]{1,0:T(8,128)(2,1)S(1)} %copy-done.28), kind=kOutput, calls=%fused_computation.13 | convolution fusion | flops 12886474752 | bytes 24117248 | tf_op jit(solution)/shard_map/dot_general | solution.py:668
  490.9 6.4 collective-permute-start.44
  505.9 17.7 %convolution_convert_fusion = bf16[1536,1024]{1,0:T(8,128)(2,1)} fusion(bf16[4096,1536]{1,0:T(8,128)(2,1)S(1)} %copy-done.22, bf16[4096,1024]{1,0:T(8,128)(2,1)} %get-tuple-element.196), kind=kOutput, calls=%fused_computation.12 | convolution fusion | flops 12886474752 | bytes 24117248 | tf_op jit(solution)/shard_map/dot_general | solution.py:668
  528.7 5.6 fusion.42
  536.7 7.0 fusion.12
  546.9 3.5 add_convert_fusion.6
  550.5 5.2 collective-permute-start.47
  555.7 3.4 add_convert_fusion.5
  570.2 4.6 fusion.36
  577.0 40.0 %collective-permute-done.43 = bf16[512,768]{1,0:T(8,128)(2,1)} collective-permute-done((bf16[512,768]{1,0:T(8,128)(2,1)}, bf16[512,768]{1,0:T(8,128)(2,1)}, u32[]{:S(2)}, u32[]{:S(2)}) %collective-permute-start.43) | collective-permute-done | bytes 786464 | tf_op jit(solution)/shard_map/ppermute | solution.py:373
  619.8 3.3 add_convert_fusion.7.d_ref
  623.1 40.6 %attend_back.1 = (bf16[1024,768]{1,0:T(8,128)(2,1)}, bf16[1024,256]{1,0:T(8,128)(2,1)}, bf16[1024,256]{1,0:T(8,128)(2,1)}) custom-call(bf16[1024,768]{1,0:T(8,128)(2,1)} %get-tuple-element.148.q_ref, bf16[4,1024,64]{2,1,0:T(8,128)(2,1)} %get-tuple-element.149.k_ref, bf16[4,1024,64]{2,1,0:T(8,128)(2,1)} %get-tuple-element.150.v_ref, ...), custom_call_target="tpu_custom_call" | custom-call | flops 566231040 | bytes 6291456 | tf_op jit(solution)/shard_map/attend_back/pallas_call | solution.py:787
  663.7 7.7 add_convert_fusion.3
  671.5 8.6 %qkv_grad.1 = bf16[2,2,2,4,48,1408]{5,4,3,2,1,0:T(8,128)(2,1)} custom-call(bf16[1024,1536]{1,0:T(8,128)(2,1)} %get-tuple-element.212.h_ref, bf16[1024,768]{1,0:T(8,128)(2,1)} %get-tuple-element.221.dq_ref, bf16[1024,256]{1,0:T(8,128)(2,1)} %get-tuple-element.222.dk_ref, bf16[1024,256]{1,0:T(8,128)(2,1)} %get-tuple-element.223.dv_ref, ...), custom_call_target="tpu_custom_call" | custom-call | flops 251658240 | bytes 1572864 | tf_op jit(solution)/shard_map/qkv_grad/pallas_call | solution.py:1009
  680.0 3.1 dynamic-slice_bitcast_fusion
  686.8 3.4 fusion.68
  690.1 5.2 collective-permute-start.55
  695.3 3.2 fusion.67
  702.9 4.1 convert_add_fusion.2
  707.0 11.0 %token_grad.1 = (bf16[512,1536]{1,0:T(8,128)(2,1)}, bf16[512,1536]{1,0:T(8,128)(2,1)}) custom-call(bf16[1024,768]{1,0:T(8,128)(2,1)} %get-tuple-element.221.dq_ref, bf16[1024,256]{1,0:T(8,128)(2,1)} %get-tuple-element.222.dk_ref, bf16[1024,256]{1,0:T(8,128)(2,1)} %get-tuple-element.223.dv_ref, bf16[1536,1280]{1,0:T(8,128)(2,1)} %get-tuple-element.224.w_ref, ...), custom_call_target="tpu_custom_call" | custom-call | flops 251658240 | bytes 1572864 | tf_op jit(solution)/shard_map/token_grad/pallas_call | solution.py:635
  720.8 6.9 collective-permute-done.56
  731.4 3.8 convert_add_fusion
  735.2 4.2 fusion.31
  741.3 3.2 collective-permute-done.54
  747.5 5.6 collective-permute-done.57
  753.1 4.8 collective-permute-done.58
  757.9 4.4 fusion.16
  766.5 3.0 collective-permute-start.65
  769.6 20.9 %collective-permute-done.60 = bf16[512,1536]{1,0:T(8,128)(2,1)} collective-permute-done((bf16[512,1536]{1,0:T(8,128)(2,1)}, bf16[512,1536]{1,0:T(8,128)(2,1)}, u32[]{:S(2)}, u32[]{:S(2)}) %collective-permute-start.60) | collective-permute-done | bytes 1572896 | tf_op jit(solution)/shard_map/ppermute | solution.py:373
  790.6 8.6 %collective-permute-start.64 = (bf16[1536,512]{1,0:T(8,128)(2,1)S(1)}, bf16[1536,512]{1,0:T(8,128)(2,1)S(1)}, u32[]{:S(2)}, u32[]{:S(2)}) collective-permute-start(bf16[1536,512]{1,0:T(8,128)(2,1)S(1)} %fusion.29), channel_id=1, source_target_pairs={{0,0},{1,16},{2,2},{3,18},{4,4},{5,20},{6,6},{7,22},{8,8},{9,24},{... | collective-permute-start | bytes 4718600 | tf_op jit(solution)/shard_map/ppermute | solution.py:1075
  801.7 4.3 fusion.5
  815.1 18.1 %collective-permute-done.62 = bf16[48,2688]{1,0:T(8,128)(2,1)S(1)} collective-permute-done((bf16[48,2688]{1,0:T(8,128)(2,1)S(1)}, bf16[48,2688]{1,0:T(8,128)(2,1)S(1)}, u32[]{:S(2)}, u32[]{:S(2)}) %collective-permute-start.62) | collective-permute-done | bytes 258080 | tf_op jit(solution)/shard_map/ppermute | solution.py:377
  (384 shorter events, 169.7 us)
Async XLA Ops:
  7.2 226.0 %all-gather.2.cloned.1.call-start = ((), (), s32[]{:S(2)}) async-start(), calls=%async_computation.1 | async-start | bytes 5013504 | tf_op jit(solution)/shard_map/all_gather | solution.py:1185
  10.0 49.5 %collective-permute-start = (bf16[1536,512]{1,0:T(8,128)(2,1)S(1)}, bf16[1536,512]{1,0:T(8,128)(2,1)S(1)}, u32[]{:S(2)}, u32[]{:S(2)}) collective-permute-start(bf16[1536,512]{1,0:T(8,128)(2,1)S(1)} %pad_maximum_fusion.8), channel_id=1, source_target_pairs={{0,0},{1,16},{2,2},{3,18},{4,4},{5,20},{6,6},{7,22},{8,8},{9,24},{... | collective-permute-start | bytes 4718600 | tf_op jit(solution)/shard_map/ppermute | solution.py:1075
  19.4 18.7 %collective-permute-start.2 = (bf16[48,2944]{1,0:T(8,128)(2,1)}, bf16[48,2944]{1,0:T(8,128)(2,1)S(1)}, u32[]{:S(2)}, u32[]{:S(2)}) collective-permute-start(bf16[48,2944]{1,0:T(8,128)(2,1)} %constant_dynamic-update-slice_fusion), channel_id=1, source_target_pairs={{0,16},{16,0},{1,17},{17,1},{2,18},{18,2},{3,19},{19,3},{4,20},{20... | collective-permute-start | bytes 847880 | tf_op jit(solution)/shard_map/ppermute | solution.py:373
  19.4 40.1 %collective-permute-start.1 = (bf16[1536,256]{1,0:T(8,128)(2,1)}, bf16[1536,256]{1,0:T(8,128)(2,1)}, u32[]{:S(2)}, u32[]{:S(2)}) collective-permute-start(bf16[1536,256]{1,0:T(8,128)(2,1)} %get-tuple-element.342), channel_id=1, source_target_pairs={{0,1},{1,17},{2,3},{3,19},{4,5},{5,21},{6,7},{7,23},{8,9},{9,25},{... | collective-permute-start | bytes 2359304 | tf_op jit(solution)/shard_map/ppermute | solution.py:1075
  39.0 11.1 %collective-permute-start.3 = (bf16[48,2816]{1,0:T(8,128)(2,1)S(1)}, bf16[48,2816]{1,0:T(8,128)(2,1)}, u32[]{:S(2)}, u32[]{:S(2)}) collective-permute-start(bf16[48,2816]{1,0:T(8,128)(2,1)S(1)} %pad_maximum_fusion.13), channel_id=1, source_target_pairs={{0,4},{1,5},{2,6},{3,7},{4,0},{5,1},{6,2},{7,3},{8,12},{9,13},{10,... | collective-permute-start | bytes 811016 | tf_op jit(solution)/shard_map/ppermute | solution.py:377
  40.4 10.3 %collective-permute-start.4 = (bf16[48,2816]{1,0:T(8,128)(2,1)S(1)}, bf16[48,2816]{1,0:T(8,128)(2,1)}, u32[]{:S(2)}, u32[]{:S(2)}) collective-permute-start(bf16[48,2816]{1,0:T(8,128)(2,1)S(1)} %pad_maximum_fusion.13), channel_id=1, source_target_pairs={{0,8},{1,9},{2,10},{3,11},{4,12},{5,13},{6,14},{7,15},{8,0},{9,1},... | collective-permute-start | bytes 811016 | tf_op jit(solution)/shard_map/ppermute | solution.py:377
  42.7 16.8 %collective-permute-start.5 = (bf16[48,2816]{1,0:T(8,128)(2,1)S(1)}, bf16[48,2816]{1,0:T(8,128)(2,1)}, u32[]{:S(2)}, u32[]{:S(2)}) collective-permute-start(bf16[48,2816]{1,0:T(8,128)(2,1)S(1)} %pad_maximum_fusion.13), channel_id=1, source_target_pairs={{0,12},{1,13},{2,14},{3,15},{4,8},{5,9},{6,10},{7,11},{8,4},{9,5},... | collective-permute-start | bytes 811016 | tf_op jit(solution)/shard_map/ppermute | solution.py:377
  62.8 33.3 %collective-permute-start.8 = (bf16[768,768]{1,0:T(8,128)(2,1)S(1)}, bf16[768,768]{1,0:T(8,128)(2,1)S(1)}, u32[]{:S(2)}, u32[]{:S(2)}) collective-permute-start(bf16[768,768]{1,0:T(8,128)(2,1)S(1)} %get-tuple-element.330), channel_id=1, source_target_pairs={{0,4},{1,5},{2,6},{3,7},{4,8},{5,9},{6,10},{7,11},{8,12},{9,13},{1... | collective-permute-start | bytes 3538952 | tf_op jit(solution)/shard_map/ppermute | solution.py:389
  70.8 26.7 %collective-permute-start.9 = (bf16[768,768]{1,0:T(8,128)(2,1)S(1)}, bf16[768,768]{1,0:T(8,128)(2,1)S(1)}, u32[]{:S(2)}, u32[]{:S(2)}) collective-permute-start(bf16[768,768]{1,0:T(8,128)(2,1)S(1)} %get-tuple-element.330), channel_id=1, source_target_pairs={{4,0},{5,1},{6,2},{7,3},{8,4},{9,5},{10,6},{11,7},{12,8},{13,9},{1... | collective-permute-start | bytes 3538952 | tf_op jit(solution)/shard_map/ppermute | solution.py:393
  73.3 22.8 %collective-permute-start.7 = (bf16[192,2816]{1,0:T(8,128)(2,1)S(1)}, bf16[192,2816]{1,0:T(8,128)(2,1)S(1)}, u32[]{:S(2)}, u32[]{:S(2)}) collective-permute-start(bf16[192,2816]{1,0:T(8,128)(2,1)S(1)} %pad_maximum_fusion.9), channel_id=1, source_target_pairs={{0,2},{1,3},{2,0},{3,1},{4,6},{5,7},{6,4},{7,5},{8,10},{9,11},{10,... | collective-permute-start | bytes 3244040 | tf_op jit(solution)/shard_map/ppermute | solution.py:377
  78.4 36.5 %collective-permute-start.6 = (bf16[512,1536]{1,0:T(8,128)(2,1)S(1)}, bf16[512,1536]{1,0:T(8,128)(2,1)}, u32[]{:S(2)}, u32[]{:S(2)}) collective-permute-start(bf16[512,1536]{1,0:T(8,128)(2,1)S(1)} %copy-done.11), channel_id=1, source_target_pairs={{0,16},{16,0},{1,17},{17,1},{2,18},{18,2},{3,19},{19,3},{4,20},{20... | collective-permute-start | bytes 4718600 | tf_op jit(solution)/shard_map/ppermute | solution.py:373
  98.6 45.3 %collective-permute-start.12 = (bf16[384,2816]{1,0:T(8,128)(2,1)}, bf16[384,2816]{1,0:T(8,128)(2,1)}, u32[]{:S(2)}, u32[]{:S(2)}) collective-permute-start(bf16[384,2816]{1,0:T(8,128)(2,1)} %constant_dynamic-update-slice_fusion.4.own_ref), channel_id=1, source_target_pairs={{0,1},{1,0},{2,3},{3,2},{4,5},{5,4},{6,7},{7,6},{8,9},{9,8},{10,11... | collective-permute-start | bytes 6488072 | tf_op jit(solution)/shard_map/ppermute | solution.py:377
  107.2 28.8 %collective-permute-start.10 = (bf16[768,768]{1,0:T(8,128)(2,1)}, bf16[768,768]{1,0:T(8,128)(2,1)}, u32[]{:S(2)}, u32[]{:S(2)}) collective-permute-start(bf16[768,768]{1,0:T(8,128)(2,1)} %get-tuple-element.142), channel_id=1, source_target_pairs={{0,4},{1,5},{2,6},{3,7},{4,8},{5,9},{6,10},{7,11},{8,12},{9,13},{1... | collective-permute-start | bytes 3538952 | tf_op jit(solution)/shard_map/ppermute | solution.py:389
  111.4 29.5 %collective-permute-start.11 = (bf16[768,768]{1,0:T(8,128)(2,1)}, bf16[768,768]{1,0:T(8,128)(2,1)}, u32[]{:S(2)}, u32[]{:S(2)}) collective-permute-start(bf16[768,768]{1,0:T(8,128)(2,1)} %get-tuple-element.142), channel_id=1, source_target_pairs={{4,0},{5,1},{6,2},{7,3},{8,4},{9,5},{10,6},{11,7},{12,8},{13,9},{1... | collective-permute-start | bytes 3538952 | tf_op jit(solution)/shard_map/ppermute | solution.py:393
  157.0 590.5 %reduce-scatter.2.cloned.1.call-start = ((), (), s32[]{:S(2)}) async-start(), calls=%async_computation.2 | async-start | bytes 4866048 | tf_op jit(solution)/shard_map/reduce_scatter | solution.py:1299
  161.5 47.8 %collective-permute-start.14 = (bf16[512,1664]{1,0:T(8,128)(2,1)}, bf16[512,1664]{1,0:T(8,128)(2,1)}, u32[]{:S(2)}, u32[]{:S(2)}) collective-permute-start(bf16[512,1664]{1,0:T(8,128)(2,1)} %concatenate.103.refs_6_), channel_id=1, source_target_pairs={{0,2},{1,3},{2,0},{3,1},{4,6},{5,7},{6,4},{7,5},{8,10},{9,11},{10,... | collective-permute-start | bytes 5111816 | tf_op jit(solution)/shard_map/ppermute | solution.py:377
  162.7 46.6 %collective-permute-start.13 = (bf16[512,1664]{1,0:T(8,128)(2,1)}, bf16[512,1664]{1,0:T(8,128)(2,1)}, u32[]{:S(2)}, u32[]{:S(2)}) collective-permute-start(bf16[512,1664]{1,0:T(8,128)(2,1)} %concatenate.103.refs_6_), channel_id=1, source_target_pairs={{0,16},{16,0},{1,17},{17,1},{2,18},{18,2},{3,19},{19,3},{4,20},{20... | collective-permute-start | bytes 5111816 | tf_op jit(solution)/shard_map/ppermute | solution.py:373
  166.0 79.1 %collective-permute-start.30 = (bf16[1536,768]{1,0:T(8,128)(2,1)S(1)}, bf16[1536,768]{1,0:T(8,128)(2,1)}, u32[]{:S(2)}, u32[]{:S(2)}) collective-permute-start(bf16[1536,768]{1,0:T(8,128)(2,1)S(1)} %get-tuple-element.166.refs_18_.refs_14_), channel_id=1, source_target_pairs={{0,4},{1,5},{2,6},{3,7},{4,8},{5,9},{6,10},{7,11},{8,12},{9,13},{1... | collective-permute-start | bytes 7077896 | tf_op jit(solution)/shard_map/ppermute | solution.py:389
  168.9 79.1 %collective-permute-start.31 = (bf16[1536,768]{1,0:T(8,128)(2,1)}, bf16[1536,768]{1,0:T(8,128)(2,1)}, u32[]{:S(2)}, u32[]{:S(2)}) collective-permute-start(bf16[1536,768]{1,0:T(8,128)(2,1)} %get-tuple-element.167.refs_20_.refs_16_), channel_id=1, source_target_pairs={{4,0},{5,1},{6,2},{7,3},{8,4},{9,5},{10,6},{11,7},{12,8},{13,9},{1... | collective-permute-start | bytes 7077896 | tf_op jit(solution)/shard_map/ppermute | solution.py:393
  212.0 18.5 %collective-permute-start.15 = (bf16[512,768]{1,0:T(8,128)(2,1)S(1)}, bf16[512,768]{1,0:T(8,128)(2,1)S(1)}, u32[]{:S(2)}, u32[]{:S(2)}) collective-permute-start(bf16[512,768]{1,0:T(8,128)(2,1)S(1)} %fusion.41), channel_id=1, source_target_pairs={{0,16},{16,0},{1,17},{17,1},{2,18},{18,2},{3,19},{19,3},{4,20},{20... | collective-permute-start | bytes 2359304 | tf_op jit(solution)/shard_map/ppermute | solution.py:373
  242.4 30.7 %collective-permute-start.16 = (bf16[512,1536]{1,0:T(8,128)(2,1)}, bf16[512,1536]{1,0:T(8,128)(2,1)}, u32[]{:S(2)}, u32[]{:S(2)}) collective-permute-start(bf16[512,1536]{1,0:T(8,128)(2,1)} %get-tuple-element.157.refs_0_), channel_id=1, source_target_pairs={{0,16},{16,0},{1,17},{17,1},{2,18},{18,2},{3,19},{19,3},{4,20},{20... | collective-permute-start | bytes 4718600 | tf_op jit(solution)/shard_map/ppermute | solution.py:373
  248.0 62.7 %collective-permute-start.32 = (bf16[1536,768]{1,0:T(8,128)(2,1)}, bf16[1536,768]{1,0:T(8,128)(2,1)S(1)}, u32[]{:S(2)}, u32[]{:S(2)}) collective-permute-start(bf16[1536,768]{1,0:T(8,128)(2,1)} %collective-permute-done.30.refs_17_.refs_13_), channel_id=1, source_target_pairs={{0,4},{1,5},{2,6},{3,7},{4,8},{5,9},{6,10},{7,11},{8,12},{9,13},{1... | collective-permute-start | bytes 7077896 | tf_op jit(solution)/shard_map/ppermute | solution.py:389
  250.0 60.8 %collective-permute-start.33 = (bf16[1536,768]{1,0:T(8,128)(2,1)}, bf16[1536,768]{1,0:T(8,128)(2,1)S(1)}, u32[]{:S(2)}, u32[]{:S(2)}) collective-permute-start(bf16[1536,768]{1,0:T(8,128)(2,1)} %collective-permute-done.31.refs_21_.refs_17_), channel_id=1, source_target_pairs={{4,0},{5,1},{6,2},{7,3},{8,4},{9,5},{10,6},{11,7},{12,8},{13,9},{1... | collective-permute-start | bytes 7077896 | tf_op jit(solution)/shard_map/ppermute | solution.py:393
  251.3 34.1 %collective-permute-start.17 = (bf16[512,1536]{1,0:T(8,128)(2,1)}, bf16[512,1536]{1,0:T(8,128)(2,1)S(1)}, u32[]{:S(2)}, u32[]{:S(2)}) collective-permute-start(bf16[512,1536]{1,0:T(8,128)(2,1)} %get-tuple-element.157.refs_0_), channel_id=1, source_target_pairs={{0,2},{1,3},{2,0},{3,1},{4,6},{5,7},{6,4},{7,5},{8,10},{9,11},{10,... | collective-permute-start | bytes 4718600 | tf_op jit(solution)/shard_map/ppermute | solution.py:377
  254.1 49.5 %collective-permute-start.24 = (bf16[256,1664]{1,0:T(8,128)(2,1)S(1)}, bf16[256,1664]{1,0:T(8,128)(2,1)S(1)}, u32[]{:S(2)}, u32[]{:S(2)}) collective-permute-start(bf16[256,1664]{1,0:T(8,128)(2,1)S(1)} %slice.200), channel_id=1, source_target_pairs={{0,2},{1,3},{2,0},{3,1},{4,6},{5,7},{6,4},{7,5},{8,10},{9,11},{10,... | collective-permute-start | bytes 2555912 | tf_op jit(solution)/shard_map/ppermute | solution.py:377
  273.2 33.0 %collective-permute-start.25 = (bf16[256,1664]{1,0:T(8,128)(2,1)S(1)}, bf16[256,1664]{1,0:T(8,128)(2,1)}, u32[]{:S(2)}, u32[]{:S(2)}) collective-permute-start(bf16[256,1664]{1,0:T(8,128)(2,1)S(1)} %slice.201), channel_id=1, source_target_pairs={{0,16},{16,0},{1,17},{17,1},{2,18},{18,2},{3,19},{19,3},{4,20},{20... | collective-permute-start | bytes 2555912 | tf_op jit(solution)/shard_map/ppermute | solution.py:373
  285.4 35.1 %collective-permute-start.18 = (bf16[256,1536]{1,0:T(8,128)(2,1)S(1)}, bf16[256,1536]{1,0:T(8,128)(2,1)S(1)}, u32[]{:S(2)}, u32[]{:S(2)}) collective-permute-start(bf16[256,1536]{1,0:T(8,128)(2,1)S(1)} %slice.254), channel_id=1, source_target_pairs={{0,2},{1,3},{2,0},{3,1},{4,6},{5,7},{6,4},{7,5},{8,10},{9,11},{10,... | collective-permute-start | bytes 2359304 | tf_op jit(solution)/shard_map/ppermute | solution.py:377
  303.7 19.9 %collective-permute-start.19 = (bf16[256,1536]{1,0:T(8,128)(2,1)S(1)}, bf16[256,1536]{1,0:T(8,128)(2,1)S(1)}, u32[]{:S(2)}, u32[]{:S(2)}) collective-permute-start(bf16[256,1536]{1,0:T(8,128)(2,1)S(1)} %slice.255), channel_id=1, source_target_pairs={{0,16},{16,0},{1,17},{17,1},{2,18},{18,2},{3,19},{19,3},{4,20},{20... | collective-permute-start | bytes 2359304 | tf_op jit(solution)/shard_map/ppermute | solution.py:373
  306.2 18.5 %collective-permute-start.28 = (bf16[256,1664]{1,0:T(8,128)(2,1)S(1)}, bf16[256,1664]{1,0:T(8,128)(2,1)S(1)}, u32[]{:S(2)}, u32[]{:S(2)}) collective-permute-start(bf16[256,1664]{1,0:T(8,128)(2,1)S(1)} %collective-permute-done.24.refs_10_), channel_id=1, source_target_pairs={{0,1},{1,0},{2,3},{3,2},{4,5},{5,4},{6,7},{7,6},{8,9},{9,8},{10,11... | collective-permute-start | bytes 2555912 | tf_op jit(solution)/shard_map/ppermute | solution.py:377
  310.8 17.9 %collective-permute-start.20 = (bf16[512,1536]{1,0:T(8,128)(2,1)}, bf16[512,1536]{1,0:T(8,128)(2,1)}, u32[]{:S(2)}, u32[]{:S(2)}) collective-permute-start(bf16[512,1536]{1,0:T(8,128)(2,1)} %collective-permute-done.16.refs_0_.refs_1_), channel_id=1, source_target_pairs={{0,1},{1,0},{2,3},{3,2},{4,5},{5,4},{6,7},{7,6},{8,9},{9,8},{10,11... | collective-permute-start | bytes 4718600 | tf_op jit(solution)/shard_map/ppermute | solution.py:377
  310.8 22.0 %collective-permute-start.26 = (bf16[512,1664]{1,0:T(8,128)(2,1)}, bf16[512,1664]{1,0:T(8,128)(2,1)S(1)}, u32[]{:S(2)}, u32[]{:S(2)}) collective-permute-start(bf16[512,1664]{1,0:T(8,128)(2,1)} %collective-permute-done.13.refs_8_.refs_7_), channel_id=1, source_target_pairs={{0,1},{1,0},{2,3},{3,2},{4,5},{5,4},{6,7},{7,6},{8,9},{9,8},{10,11... | collective-permute-start | bytes 5111816 | tf_op jit(solution)/shard_map/ppermute | solution.py:377
  320.5 13.5 %collective-permute-start.27 = (bf16[512,1664]{1,0:T(8,128)(2,1)}, bf16[512,1664]{1,0:T(8,128)(2,1)}, u32[]{:S(2)}, u32[]{:S(2)}) collective-permute-start(bf16[512,1664]{1,0:T(8,128)(2,1)} %collective-permute-done.14.refs_9_.refs_8_), channel_id=1, source_target_pairs={{0,1},{1,0},{2,3},{3,2},{4,5},{5,4},{6,7},{7,6},{8,9},{9,8},{10,11... | collective-permute-start | bytes 5111816 | tf_op jit(solution)/shard_map/ppermute | solution.py:377
  390.2 9.1 %collective-permute-start.34 = (bf16[1024,1536]{1,0:T(8,128)(2,1)}, bf16[1024,1536]{1,0:T(8,128)(2,1)S(1)}, u32[]{:S(2)}, u32[]{:S(2)}) collective-permute-start(bf16[1024,1536]{1,0:T(8,128)(2,1)} %get-tuple-element.173), channel_id=1, source_target_pairs={{0,1},{1,0},{2,3},{3,2},{4,5},{5,4},{6,7},{7,6},{8,9},{9,8},{10,11... | collective-permute-start | bytes 9437192 | tf_op jit(solution)/shard_map/ppermute | solution.py:377
  390.7 16.7 %collective-permute-start.35 = (bf16[512,1536]{1,0:T(8,128)(2,1)}, bf16[512,1536]{1,0:T(8,128)(2,1)}, u32[]{:S(2)}, u32[]{:S(2)}) collective-permute-start(bf16[512,1536]{1,0:T(8,128)(2,1)} %get-tuple-element.157.refs_0_), channel_id=1, source_target_pairs={{0,1},{1,0},{2,3},{3,2},{4,5},{5,4},{6,7},{7,6},{8,9},{9,8},{10,11... | collective-permute-start | bytes 4718600 | tf_op jit(solution)/shard_map/ppermute | solution.py:377
  390.8 16.6 %collective-permute-start.36 = (bf16[512,1664]{1,0:T(8,128)(2,1)}, bf16[512,1664]{1,0:T(8,128)(2,1)}, u32[]{:S(2)}, u32[]{:S(2)}) collective-permute-start(bf16[512,1664]{1,0:T(8,128)(2,1)} %concatenate.103.refs_6_), channel_id=1, source_target_pairs={{0,1},{1,0},{2,3},{3,2},{4,5},{5,4},{6,7},{7,6},{8,9},{9,8},{10,11... | collective-permute-start | bytes 5111816 | tf_op jit(solution)/shard_map/ppermute | solution.py:377
  403.9 59.1 %collective-permute-start.37 = (bf16[512,1536]{1,0:T(8,128)(2,1)}, bf16[512,1536]{1,0:T(8,128)(2,1)}, u32[]{:S(2)}, u32[]{:S(2)}) collective-permute-start(bf16[512,1536]{1,0:T(8,128)(2,1)} %get-tuple-element.321), channel_id=1, source_target_pairs={{0,2},{1,3},{2,0},{3,1},{4,6},{5,7},{6,4},{7,5},{8,10},{9,11},{10,... | collective-permute-start | bytes 4718600 | tf_op jit(solution)/shard_map/ppermute | solution.py:377
  405.3 57.7 %collective-permute-start.38 = (bf16[512,1536]{1,0:T(8,128)(2,1)}, bf16[512,1536]{1,0:T(8,128)(2,1)}, u32[]{:S(2)}, u32[]{:S(2)}) collective-permute-start(bf16[512,1536]{1,0:T(8,128)(2,1)} %get-tuple-element.320), channel_id=1, source_target_pairs={{0,16},{16,0},{1,17},{17,1},{2,18},{18,2},{3,19},{19,3},{4,20},{20... | collective-permute-start | bytes 4718600 | tf_op jit(solution)/shard_map/ppermute | solution.py:373
  461.9 38.4 %collective-permute-start.39 = (bf16[1024,1536]{1,0:T(8,128)(2,1)}, bf16[1024,1536]{1,0:T(8,128)(2,1)}, u32[]{:S(2)}, u32[]{:S(2)}) collective-permute-start(bf16[1024,1536]{1,0:T(8,128)(2,1)} %get-tuple-element.192), channel_id=1, source_target_pairs={{0,1},{1,0},{2,3},{3,2},{4,5},{5,4},{6,7},{7,6},{8,9},{9,8},{10,11... | collective-permute-start | bytes 9437192 | tf_op jit(solution)/shard_map/ppermute | solution.py:377
  490.9 56.0 %collective-permute-start.44 = (bf16[1536,768]{1,0:T(8,128)(2,1)}, bf16[1536,768]{1,0:T(8,128)(2,1)}, u32[]{:S(2)}, u32[]{:S(2)}) collective-permute-start(bf16[1536,768]{1,0:T(8,128)(2,1)} %pad_maximum_fusion.5), channel_id=1, source_target_pairs={{0,4},{1,5},{2,6},{3,7},{4,8},{5,9},{6,10},{7,11},{8,12},{9,13},{1... | collective-permute-start | bytes 7077896 | tf_op jit(solution)/shard_map/ppermute | solution.py:389
  498.9 56.7 %collective-permute-start.45 = (bf16[1536,768]{1,0:T(8,128)(2,1)}, bf16[1536,768]{1,0:T(8,128)(2,1)}, u32[]{:S(2)}, u32[]{:S(2)}) collective-permute-start(bf16[1536,768]{1,0:T(8,128)(2,1)} %pad_maximum_fusion.4), channel_id=1, source_target_pairs={{4,0},{5,1},{6,2},{7,3},{8,4},{9,5},{10,6},{11,7},{12,8},{13,9},{1... | collective-permute-start | bytes 7077896 | tf_op jit(solution)/shard_map/ppermute | solution.py:393
  505.2 19.0 %collective-permute-start.40 = (bf16[256,1536]{1,0:T(8,128)(2,1)S(1)}, bf16[256,1536]{1,0:T(8,128)(2,1)S(1)}, u32[]{:S(2)}, u32[]{:S(2)}) collective-permute-start(bf16[256,1536]{1,0:T(8,128)(2,1)S(1)} %get-tuple-element.308), channel_id=1, source_target_pairs={{0,16},{16,0},{1,17},{17,1},{2,18},{18,2},{3,19},{19,3},{4,20},{20... | collective-permute-start | bytes 2359304 | tf_op jit(solution)/shard_map/ppermute | solution.py:373
  505.2 19.0 %collective-permute-start.41 = (bf16[256,1536]{1,0:T(8,128)(2,1)S(1)}, bf16[256,1536]{1,0:T(8,128)(2,1)S(1)}, u32[]{:S(2)}, u32[]{:S(2)}) collective-permute-start(bf16[256,1536]{1,0:T(8,128)(2,1)S(1)} %get-tuple-element.309), channel_id=1, source_target_pairs={{0,2},{1,3},{2,0},{3,1},{4,6},{5,7},{6,4},{7,5},{8,10},{9,11},{10,... | collective-permute-start | bytes 2359304 | tf_op jit(solution)/shard_map/ppermute | solution.py:377
  534.3 26.3 %collective-permute-start.46 = (bf16[1024,1536]{1,0:T(8,128)(2,1)S(1)}, bf16[1024,1536]{1,0:T(8,128)(2,1)}, u32[]{:S(2)}, u32[]{:S(2)}) collective-permute-start(bf16[1024,1536]{1,0:T(8,128)(2,1)S(1)} %copy-done.68), channel_id=1, source_target_pairs={{0,1},{1,0},{2,3},{3,2},{4,5},{5,4},{6,7},{7,6},{8,9},{9,8},{10,11... | collective-permute-start | bytes 9437192 | tf_op jit(solution)/shard_map/ppermute | solution.py:377
  550.5 113.2 %collective-permute-start.47 = (bf16[1536,768]{1,0:T(8,128)(2,1)}, bf16[1536,768]{1,0:T(8,128)(2,1)}, u32[]{:S(2)}, u32[]{:S(2)}) collective-permute-start(bf16[1536,768]{1,0:T(8,128)(2,1)} %add_convert_fusion.6), channel_id=1, source_target_pairs={{0,4},{1,5},{2,6},{3,7},{4,8},{5,9},{6,10},{7,11},{8,12},{9,13},{1... | collective-permute-start | bytes 7077896 | tf_op jit(solution)/shard_map/ppermute | solution.py:389
  559.1 104.6 %collective-permute-start.48 = (bf16[1536,768]{1,0:T(8,128)(2,1)}, bf16[1536,768]{1,0:T(8,128)(2,1)}, u32[]{:S(2)}, u32[]{:S(2)}) collective-permute-start(bf16[1536,768]{1,0:T(8,128)(2,1)} %add_convert_fusion.5), channel_id=1, source_target_pairs={{4,0},{5,1},{6,2},{7,3},{8,4},{9,5},{10,6},{11,7},{12,8},{13,9},{1... | collective-permute-start | bytes 7077896 | tf_op jit(solution)/shard_map/ppermute | solution.py:393
  565.3 98.4 %collective-permute-start.49 = (bf16[512,1536]{1,0:T(8,128)(2,1)}, bf16[512,1536]{1,0:T(8,128)(2,1)}, u32[]{:S(2)}, u32[]{:S(2)}) collective-permute-start(bf16[512,1536]{1,0:T(8,128)(2,1)} %get-tuple-element.315), channel_id=1, source_target_pairs={{0,2},{1,3},{2,0},{3,1},{4,6},{5,7},{6,4},{7,5},{8,10},{9,11},{10,... | collective-permute-start | bytes 4718600 | tf_op jit(solution)/shard_map/ppermute | solution.py:377
  565.8 97.9 %collective-permute-start.50 = (bf16[512,1536]{1,0:T(8,128)(2,1)}, bf16[512,1536]{1,0:T(8,128)(2,1)}, u32[]{:S(2)}, u32[]{:S(2)}) collective-permute-start(bf16[512,1536]{1,0:T(8,128)(2,1)} %get-tuple-element.314), channel_id=1, source_target_pairs={{0,16},{16,0},{1,17},{17,1},{2,18},{18,2},{3,19},{19,3},{4,20},{20... | collective-permute-start | bytes 4718600 | tf_op jit(solution)/shard_map/ppermute | solution.py:373
  569.5 47.4 %collective-permute-start.43 = (bf16[512,768]{1,0:T(8,128)(2,1)}, bf16[512,768]{1,0:T(8,128)(2,1)}, u32[]{:S(2)}, u32[]{:S(2)}) collective-permute-start(bf16[512,768]{1,0:T(8,128)(2,1)} %fusion.45), channel_id=1, source_target_pairs={{0,16},{16,0},{1,17},{17,1},{2,18},{18,2},{3,19},{19,3},{4,20},{20... | collective-permute-start | bytes 2359304 | tf_op jit(solution)/shard_map/ppermute | solution.py:373
  617.0 114.4 %collective-permute-start.42 = (bf16[1024,1536]{1,0:T(8,128)(2,1)}, bf16[1024,1536]{1,0:T(8,128)(2,1)}, u32[]{:S(2)}, u32[]{:S(2)}) collective-permute-start(bf16[1024,1536]{1,0:T(8,128)(2,1)} %get-tuple-element.202), channel_id=1, source_target_pairs={{0,1},{1,0},{2,3},{3,2},{4,5},{5,4},{6,7},{7,6},{8,9},{9,8},{10,11... | collective-permute-start | bytes 9437192 | tf_op jit(solution)/shard_map/ppermute | solution.py:377
  683.1 19.7 %collective-permute-start.53 = (bf16[2,2,4,48,1408]{4,3,2,1,0:T(8,128)(2,1)}, bf16[2,2,4,48,1408]{4,3,2,1,0:T(8,128)(2,1)}, u32[]{:S(2)}, u32[]{:S(2)}) collective-permute-start(bf16[2,2,4,48,1408]{4,3,2,1,0:T(8,128)(2,1)} %dynamic-slice_bitcast_fusion), channel_id=1, source_target_pairs={{0,1},{1,0},{2,3},{3,2},{4,5},{5,4},{6,7},{7,6},{8,9},{9,8},{10,11... | collective-permute-start | bytes 6488072 | tf_op jit(solution)/shard_map/ppermute | solution.py:377
  690.1 30.7 %collective-permute-start.55 = (bf16[768,768]{1,0:T(8,128)(2,1)}, bf16[768,768]{1,0:T(8,128)(2,1)}, u32[]{:S(2)}, u32[]{:S(2)}) collective-permute-start(bf16[768,768]{1,0:T(8,128)(2,1)} %get-tuple-element.329), channel_id=1, source_target_pairs={{0,4},{1,5},{2,6},{3,7},{4,8},{5,9},{6,10},{7,11},{8,12},{9,13},{1... | collective-permute-start | bytes 3538952 | tf_op jit(solution)/shard_map/ppermute | solution.py:389
  698.5 29.2 %collective-permute-start.56 = (bf16[768,768]{1,0:T(8,128)(2,1)}, bf16[768,768]{1,0:T(8,128)(2,1)}, u32[]{:S(2)}, u32[]{:S(2)}) collective-permute-start(bf16[768,768]{1,0:T(8,128)(2,1)} %get-tuple-element.327), channel_id=1, source_target_pairs={{4,0},{5,1},{6,2},{7,3},{8,4},{9,5},{10,6},{11,7},{12,8},{13,9},{1... | collective-permute-start | bytes 3538952 | tf_op jit(solution)/shard_map/ppermute | solution.py:393
  719.8 24.8 %collective-permute-start.54 = (bf16[2,4,48,1408]{3,2,1,0:T(8,128)(2,1)S(1)}, bf16[2,4,48,1408]{3,2,1,0:T(8,128)(2,1)S(1)}, u32[]{:S(2)}, u32[]{:S(2)}) collective-permute-start(bf16[2,4,48,1408]{3,2,1,0:T(8,128)(2,1)S(1)} %fusion.48), channel_id=1, source_target_pairs={{0,2},{1,3},{2,0},{3,1},{4,6},{5,7},{6,4},{7,5},{8,10},{9,11},{10,... | collective-permute-start | bytes 3244040 | tf_op jit(solution)/shard_map/ppermute | solution.py:377
  727.7 25.4 %collective-permute-start.57 = (bf16[768,768]{1,0:T(8,128)(2,1)}, bf16[768,768]{1,0:T(8,128)(2,1)}, u32[]{:S(2)}, u32[]{:S(2)}) collective-permute-start(bf16[768,768]{1,0:T(8,128)(2,1)} %get-tuple-element.228), channel_id=1, source_target_pairs={{0,4},{1,5},{2,6},{3,7},{4,8},{5,9},{6,10},{7,11},{8,12},{9,13},{1... | collective-permute-start | bytes 3538952 | tf_op jit(solution)/shard_map/ppermute | solution.py:389
  730.1 27.8 %collective-permute-start.58 = (bf16[768,768]{1,0:T(8,128)(2,1)}, bf16[768,768]{1,0:T(8,128)(2,1)}, u32[]{:S(2)}, u32[]{:S(2)}) collective-permute-start(bf16[768,768]{1,0:T(8,128)(2,1)} %get-tuple-element.229), channel_id=1, source_target_pairs={{4,0},{5,1},{6,2},{7,3},{8,4},{9,5},{10,6},{11,7},{12,8},{13,9},{1... | collective-permute-start | bytes 3538952 | tf_op jit(solution)/shard_map/ppermute | solution.py:393
  739.4 67.2 %collective-permute-start.51 = (bf16[256,1536]{1,0:T(8,128)(2,1)}, bf16[256,1536]{1,0:T(8,128)(2,1)}, u32[]{:S(2)}, u32[]{:S(2)}) collective-permute-start(bf16[256,1536]{1,0:T(8,128)(2,1)} %get-tuple-element.305), channel_id=1, source_target_pairs={{0,16},{16,0},{1,17},{17,1},{2,18},{18,2},{3,19},{19,3},{4,20},{20... | collective-permute-start | bytes 2359304 | tf_op jit(solution)/shard_map/ppermute | solution.py:373
  740.8 65.8 %collective-permute-start.52 = (bf16[256,1536]{1,0:T(8,128)(2,1)}, bf16[256,1536]{1,0:T(8,128)(2,1)}, u32[]{:S(2)}, u32[]{:S(2)}) collective-permute-start(bf16[256,1536]{1,0:T(8,128)(2,1)} %get-tuple-element.304), channel_id=1, source_target_pairs={{0,2},{1,3},{2,0},{3,1},{4,6},{5,7},{6,4},{7,5},{8,10},{9,11},{10,... | collective-permute-start | bytes 2359304 | tf_op jit(solution)/shard_map/ppermute | solution.py:377
  744.6 46.0 %collective-permute-start.60 = (bf16[512,1536]{1,0:T(8,128)(2,1)}, bf16[512,1536]{1,0:T(8,128)(2,1)}, u32[]{:S(2)}, u32[]{:S(2)}) collective-permute-start(bf16[512,1536]{1,0:T(8,128)(2,1)} %get-tuple-element.227), channel_id=1, source_target_pairs={{0,16},{16,0},{1,17},{17,1},{2,18},{18,2},{3,19},{19,3},{4,20},{20... | collective-permute-start | bytes 4718600 | tf_op jit(solution)/shard_map/ppermute | solution.py:373
  764.3 41.7 %collective-permute-start.59 = (bf16[4,48,1408]{2,1,0:T(8,128)(2,1)S(1)}, bf16[4,48,1408]{2,1,0:T(8,128)(2,1)S(1)}, u32[]{:S(2)}, u32[]{:S(2)}) collective-permute-start(bf16[4,48,1408]{2,1,0:T(8,128)(2,1)S(1)} %fusion.57), channel_id=1, source_target_pairs={{0,16},{16,0},{1,17},{17,1},{2,18},{18,2},{3,19},{19,3},{4,20},{20... | collective-permute-start | bytes 1622024 | tf_op jit(solution)/shard_map/ppermute | solution.py:373
  766.5 69.7 %collective-permute-start.65 = (bf16[1536,256]{1,0:T(8,128)(2,1)S(1)}, bf16[1536,256]{1,0:T(8,128)(2,1)S(1)}, u32[]{:S(2)}, u32[]{:S(2)}) collective-permute-start(bf16[1536,256]{1,0:T(8,128)(2,1)S(1)} %get-tuple-element.241), channel_id=1, source_target_pairs={{1,0},{17,1},{3,2},{19,3},{5,4},{21,5},{7,6},{23,7},{9,8},{25,9},{... | collective-permute-start | bytes 2359304 | tf_op jit(solution)/shard_map/ppermute | solution.py:1075
  790.6 45.6 %collective-permute-start.64 = (bf16[1536,512]{1,0:T(8,128)(2,1)S(1)}, bf16[1536,512]{1,0:T(8,128)(2,1)S(1)}, u32[]{:S(2)}, u32[]{:S(2)}) collective-permute-start(bf16[1536,512]{1,0:T(8,128)(2,1)S(1)} %fusion.29), channel_id=1, source_target_pairs={{0,0},{1,16},{2,2},{3,18},{4,4},{5,20},{6,6},{7,22},{8,8},{9,24},{... | collective-permute-start | bytes 4718600 | tf_op jit(solution)/shard_map/ppermute | solution.py:1075
  806.7 8.5 %collective-permute-start.63 = (bf16[48,2688]{1,0:T(8,128)(2,1)S(1)}, bf16[48,2688]{1,0:T(8,128)(2,1)S(1)}, u32[]{:S(2)}, u32[]{:S(2)}) collective-permute-start(bf16[48,2688]{1,0:T(8,128)(2,1)S(1)} %get-tuple-element.345), channel_id=1, source_target_pairs={{0,12},{1,13},{2,14},{3,15},{4,8},{5,9},{6,10},{7,11},{8,4},{9,5},... | collective-permute-start | bytes 774152 | tf_op jit(solution)/shard_map/ppermute | solution.py:377
  808.5 24.8 %collective-permute-start.62 = (bf16[48,2688]{1,0:T(8,128)(2,1)S(1)}, bf16[48,2688]{1,0:T(8,128)(2,1)S(1)}, u32[]{:S(2)}, u32[]{:S(2)}) collective-permute-start(bf16[48,2688]{1,0:T(8,128)(2,1)S(1)} %get-tuple-element.346), channel_id=1, source_target_pairs={{0,8},{1,9},{2,10},{3,11},{4,12},{5,13},{6,14},{7,15},{8,0},{9,1},... | collective-permute-start | bytes 774152 | tf_op jit(solution)/shard_map/ppermute | solution.py:377
  810.3 23.0 %collective-permute-start.61 = (bf16[48,2688]{1,0:T(8,128)(2,1)S(1)}, bf16[48,2688]{1,0:T(8,128)(2,1)S(1)}, u32[]{:S(2)}, u32[]{:S(2)}) collective-permute-start(bf16[48,2688]{1,0:T(8,128)(2,1)S(1)} %get-tuple-element.344), channel_id=1, source_target_pairs={{0,4},{1,5},{2,6},{3,7},{4,0},{5,1},{6,2},{7,3},{8,12},{9,13},{10,... | collective-permute-start | bytes 774152 | tf_op jit(solution)/shard_map/ppermute | solution.py:377
  (88 other events, 1473.9 us)
Sparse Core Ops, SparseCore 0:
  157.1 74.5 all-gather.1
  575.0 107.3 reduce-scatter.1

commit v8 on v6

--- a/solution.py
+++ b/solution.py
@@ -557,24 +557,32 @@
     )(places, x_sorted, own, other, cos, sin)
 
 
-def mix_kernel(place_ref, mine_ref, theirs_ref, x_ref, gain_ref, w_ref, m_ref, h_ref, parts_ref):
-    half = parts_ref.shape[1]
+def mix_kernel(
+    place_ref, mine_ref, theirs_ref, x_ref, gain_ref, own_ref, other_ref, m_ref, h_ref, parts_ref
+):
+    shard = own_ref.shape[0] // (2 * LINE)
+    width = parts_ref.shape[2]
 
     @pl.when(pl.program_id(0) == 0)
     def _():
-        for part in range(2):
-            low = pl.multiple_of((place_ref[0] ^ part) * half, half)
-            parts_ref[part] = w_ref[pl.ds(low, half), :]
+        for seq in range(2):
+
+            def store(source, low, place):
+                parts_ref[place_ref[3] ^ seq, pl.ds(place, shard), :] = source[
+                    low : low + shard, seq * width : (seq + 1) * width
+                ]
+
+            place_shards(place_ref, own_ref, other_ref, shard, store)
 
     mixed = jnp.dot(mine_ref[...], parts_ref[0], preferred_element_type=F32)
     mixed = mixed + jnp.dot(theirs_ref[...], parts_ref[1], preferred_element_type=F32)
     value = x_ref[...].astype(F32) + BRANCH_SCALE * mixed
     m_ref[...] = value
     scale = lax.rsqrt(jnp.mean(value * value, axis=-1, keepdims=True) + EPSILON)
-    h_ref[...] = (value * scale * gain_ref[...]).astype(BF16)
-
-
-def mix(place, mine, theirs, tokens, gain, weights):
+    h_ref[...] = (value * scale * gain_ref[1:2, :]).astype(BF16)
+
+
+def mix(places, mine, theirs, tokens, gains, own, other):
     rows, width = tokens.shape
     half = mine.shape[1]
     tile = 256
@@ -591,8 +599,8 @@
             num_scalar_prefetch=1,
             grid=(rows // tile,),
             in_specs=[
-                row_block(half), row_block(half), row_block(width), whole(gain.shape),
-                whole((width, width)),
+                row_block(half), row_block(half), row_block(width), whole(gains.shape),
+                whole(own.shape), whole(other.shape),
             ],
             out_specs=[row_block(width), row_block(width), whole((2, half, width))],
         ),
@@ -606,7 +614,7 @@
             flops=rows * width * width // 8, bytes_accessed=rows * width, transcendentals=rows
         ),
         name="mix",
-    )(place, mine, theirs, tokens, gain, weights)
+    )(places, mine, theirs, tokens, gains, own, other)
 
 
 def token_grad_kernel(dq_ref, dk_ref, dv_ref, w_ref, own_ref, other_ref, mine_ref, sent_ref):
@@ -1095,10 +1103,15 @@
         for which in (seq, 1 - seq)
     ]
     theirs = swap_seq(jnp.concatenate([theirs, w_output], axis=1))
-    output_pair = ordered(w_output[None], theirs[None, :, qkv_width + PAD :], 0)
-    block = ordered(mine, theirs[:, : qkv_width + PAD], 1)
+    block = jnp.concatenate(
+        [
+            ordered(mine, theirs[:, : qkv_width + PAD], 1),
+            ordered(w_output, theirs[:, qkv_width + PAD :], 1),
+        ],
+        axis=1,
+    )
     along = [block] + [swap_dp(block, 4 * step) for step in range(1, LINE)]
-    places_of = jnp.stack([line, row_of, core]).astype(jnp.int32)
+    places_of = jnp.stack([line, row_of, core, seq]).astype(jnp.int32)
 
     in_own = w_in[0]
     half = in_own.shape[1] // 2
@@ -1117,11 +1130,10 @@
         axis=1,
     )
     other_tokens = swap_seq(after(tokens, own_part))
-    output_full = lax.all_gather(after(output_pair, own_part), "dp", axis=1, tiled=True)
-    output_full = output_full.reshape(width, width)
     cut = width // 2
     lines = (line_up(own_part[:cut]), line_down(own_part[:cut]))
-    qkv_rows = after(jnp.concatenate(along, axis=0), own_part)
+    split = 2 * (qkv_width + PAD)
+    qkv_rows = after(jnp.concatenate([piece[:, :split] for piece in along], axis=0), own_part)
     qkv_near, lines = lax.optimization_barrier((swap_y(qkv_rows), lines))
     late_part = after(own_part[cut:], lines)
     late_lines = (line_up(late_part), line_down(late_part))
@@ -1179,17 +1191,21 @@
         places_of, x_sorted, qkv_rows, qkv_others, cos, sin, q_width, kv_heads
     )
     gain_one, gain_two = gains[0], gains[1]
+    output_rows = after(jnp.concatenate([piece[:, split:] for piece in along], axis=0), query)
+    output_near = swap_y(output_rows)
+    query, late_lines = lax.optimization_barrier((query, late_lines))
+    up_one = jnp.concatenate([lines[0], late_lines[0]], axis=0)
+    down_one = jnp.concatenate([lines[1], late_lines[1]], axis=0)
+    query, up_one, down_one = lax.optimization_barrier((query, up_one, down_one))
+    up_two, down_two = line_up(up_one), line_down(down_one)
     pairs = q_width // (2 * HDIM)
-    first_pairs = 2 * pairs // 3
+    first_pairs = (pairs + 1) // 2
     mixed_one, levels_one = attend(query, keys, values, start_column, 0, first_pairs)
     sent_one = swap_seq(from_order(sort_other, mixed_one))
-    lines, late_lines = after((lines, late_lines), mixed_one)
-    up_one = jnp.concatenate([lines[0], late_lines[0]], axis=0)
-    down_one = jnp.concatenate([lines[1], late_lines[1]], axis=0)
-    query_two, grad_near_x, grad_near_y, up_one, down_one = after(
-        (query, *grad_near, up_one, down_one), mixed_one
-    )
-    up_two, down_two = line_up(up_one), line_down(down_one)
+    output_rows, output_near = after((output_rows, output_near), mixed_one)
+    output_rows = jnp.concatenate([output_rows, output_near], axis=0)
+    output_others = swap_core(output_rows)
+    query_two, grad_near_x, grad_near_y = after((query, *grad_near), mixed_one)
     grad_near = (grad_near_x, grad_near_y)
     grad_far = far_pieces(*grad_near)
     mixed_two, levels_two = attend(
@@ -1199,13 +1215,13 @@
     mixed_mine = [from_order(sort_own, mixed_one), from_order(sort_own, mixed_two)]
     mixed_mine = jnp.concatenate(mixed_mine, axis=1)
     mixed_theirs = jnp.concatenate([sent_one, sent_two], axis=1)
+    mixed_theirs, up_two, down_two = lax.optimization_barrier((mixed_theirs, up_two, down_two))
+    up_three, down_three = line_up(up_two), line_down(down_two)
     inputs = tokens.astype(F32)
     middle, normed_ffn, output_parts = mix(
-        seq.astype(jnp.int32)[None], mixed_mine, mixed_theirs, tokens, gain_two[None, :], output_full
+        places_of, mixed_mine, mixed_theirs, tokens, gains, output_rows, output_others
     )
     normed_ffn = after(normed_ffn, *grad_far)
-    up_two, down_two = after((up_two, down_two), normed_ffn)
-    up_three, down_three = line_up(up_two), line_down(down_two)
     row_near = near_pieces(normed_ffn, normed_ffn)
     row_far = far_pieces(*row_near)
     slots = [up_three, up_two, up_one, own_part, down_one, down_two, down_three]
@@ -1294,8 +1310,7 @@
         ((grad_query, grad_keys, grad_values), mid_line, ffn_y, ffn_x)
     )
     right, left = line_step(2, mid_line)
-    third = width // 3
-    last_first = (line_up(right[:third]), line_down(left[:third]))
+    last_first = (line_up(right[:cut]), line_down(left[:cut]))
     first_ffn, second_ffn = near_links(near_ffn, ffn_y, ffn_x)
     first_ffn, second_ffn = swap_seq(first_ffn), swap_y(second_ffn)
     ffn = own_sum(near_ffn, ffn_y, ffn_x, first_ffn, second_ffn)
@@ -1317,11 +1332,7 @@
         grads_late, w_qkv, own_places[:, None], other_places[:, None]
     )
     kept, sent_normed = lax.optimization_barrier((kept, sent_normed))
-    right_mid, left_mid = after((right[third : 2 * third], left[third : 2 * third]), last_first)
-    last_mid = (line_up(right_mid), line_down(left_mid))
-    right_late, left_late = after(
-        (right[2 * third :], left[2 * third :]), last_mid, sent_normed
-    )
+    right_late, left_late = after((right[cut:], left[cut:]), last_first, sent_normed)
     last_late = (line_up(right_late), line_down(left_late))
     grad_normed = grad_normed.astype(F32) + swap_seq(sent_normed).astype(F32)
     scale = lax.rsqrt(jnp.mean(inputs * inputs, axis=-1, keepdims=True) + EPSILON)
@@ -1331,16 +1342,14 @@
     grad_tokens = grad_middle + scale * (scaled - unit * inner)
     next_kept = chosen(kept, row_of, 0)
     next_kept = next_kept + swap_y(chosen(kept, 1 - row_of, 0).astype(BF16)).astype(F32)
-    next_kept, last_first, last_mid, last_late, summed_output = lax.optimization_barrier(
-        (next_kept, last_first, last_mid, last_late, summed_output)
+    next_kept, last_first, last_late, summed_output = lax.optimization_barrier(
+        (next_kept, last_first, last_late, summed_output)
     )
     own_grads = line_partial(*range(LINE))
     part_grads = jnp.concatenate(
         [
             own + up.astype(F32) + down.astype(F32)
-            for own, (up, down) in zip(
-                jnp.split(own_grads, 3, axis=0), (last_first, last_mid, last_late)
-            )
+            for own, (up, down) in ((own_grads[:cut], last_first), (own_grads[cut:], last_late))
         ],
         axis=0,
     ).astype(BF16)

time: 786 us -> 796 us (1.013)
  waiting for transfers between devices: 176 us -> 199 us
    ppermute x32 -> x34, waiting for transfers between devices: 71.3 us -> 99 us  [swap_dp(): return lax.ppermute(value, 'dp', [(i, i ^ mask) for i in range(4 * LINE)])]
    ppermute x4, waiting for transfers between devices: 16.2 us -> 30.2 us  [both_axes(): return lax.ppermute(value, ('seq', 'dp'), pairs)]
    ppermute x15, waiting for transfers between devices: 60.3 us -> 50.2 us  [swap_seq(): return lax.ppermute(value, 'seq', [(0, 1), (1, 0)])]
    ppermute x32 -> x34, starting transfers between devices: 51.8 us -> 42.2 us  [swap_dp(): return lax.ppermute(value, 'dp', [(i, i ^ mask) for i in range(4 * LINE)])]
    ppermute x9 -> x8, waiting for transfers between devices: 22.8 us -> 14.8 us  [line_down(): return lax.ppermute(value, 'dp', [(i, i - 4) for i in range(4, 4 * LINE)])]
    ppermute x9 -> x8, starting transfers between devices: 39.3 us -> 46.3 us  [line_up(): return lax.ppermute(value, 'dp', [(i, i + 4) for i in range(4 * LINE - 4)])]
  transfers between devices with their start and end apart: 71 -> 70, of which waited for: 22 -> 24; matrix products, arithmetic and copies ran while one was open for 28% -> 27% of each run, Pallas kernels for 21% -> 21%
where the time goes in v8:
time: 796 us; the launch traced here: 787 us
  Pallas kernels  223 us (28%)
  waiting for transfers between devices  199 us (25%)
  starting transfers between devices  121 us (15%)
  other arithmetic  92.1 us (12%)
  matrix products  79.9 us (10%)
  local copies, waits for them, and re-layouts  56.8 us (7%)
  between operations  15.9 us (2%)
    pallas_call x2, Pallas kernels, run_experts(): pl.pallas_call(functools.partial(experts_kernel, tiles, tile // 2), grid_...  109 us
    ppermute x34, waiting for transfers between devices, swap_dp(): return lax.ppermute(value, 'dp', [(i, i ^ mask) for i in range(4 * LINE)])  99 us
    dot_general x15, matrix products, contract(): lax.dot_general(left, right, (((left_dim,), (right_dim,)), ((), ())), pre...  79.9 us
    ppermute x15, waiting for transfers between devices, swap_seq(): return lax.ppermute(value, 'seq', [(0, 1), (1, 0)])  50.2 us
    ppermute x8, starting transfers between devices, line_up(): return lax.ppermute(value, 'dp', [(i, i + 4) for i in range(4 * LINE - 4)])  46.3 us
    ppermute x34, starting transfers between devices, swap_dp(): return lax.ppermute(value, 'dp', [(i, i ^ mask) for i in range(4 * LINE)])  42.2 us
    pallas_call x1, Pallas kernels, attend_back(): pl.pallas_call(attend_back_kernel, grid=(pairs,), in_specs=[pair_block, w...  40.5 us
    ppermute x4, waiting for transfers between devices, both_axes(): return lax.ppermute(value, ('seq', 'dp'), pairs)  30.2 us
  transfers between devices with their start and end apart: 70, of which 24 were waited for; matrix products, arithmetic and copies ran while one was open for 27% of the time, Pallas kernels for 21%

profile of v8, /device:TPU:1, one launch (start us, length us, event | category | flops | bytes accessed | tf_op | source)
XLA Modules:
  0.0 787.3 jit_solution(16446224858725108333)
XLA Ops:
  24.4 21.7 %collective-permute-done.1 = bf16[1536,256]{1,0:T(8,128)(2,1)} collective-permute-done((bf16[1536,256]{1,0:T(8,128)(2,1)}, bf16[1536,256]{1,0:T(8,128)(2,1)}, u32[]{:S(2)}, u32[]{:S(2)}) %collective-permute-start.1) | collective-permute-done | bytes 786464 | tf_op jit(solution)/shard_map/ppermute | solution.py:1083
  46.1 14.3 %collective-permute-done.5 = bf16[48,5888]{1,0:T(8,128)(2,1)S(1)} collective-permute-done((bf16[48,5888]{1,0:T(8,128)(2,1)S(1)}, bf16[48,5888]{1,0:T(8,128)(2,1)S(1)}, u32[]{:S(2)}, u32[]{:S(2)}) %collective-permute-start.5) | collective-permute-done | bytes 565280 | tf_op jit(solution)/shard_map/ppermute | solution.py:377
  64.2 15.4 %collective-permute-start.8 = (bf16[768,768]{1,0:T(8,128)(2,1)}, bf16[768,768]{1,0:T(8,128)(2,1)}, u32[]{:S(2)}, u32[]{:S(2)}) collective-permute-start(bf16[768,768]{1,0:T(8,128)(2,1)} %get-tuple-element.339), channel_id=1, source_target_pairs={{0,4},{1,5},{2,6},{3,7},{4,8},{5,9},{6,10},{7,11},{8,12},{9,13},{1... | collective-permute-start | bytes 3538952 | tf_op jit(solution)/shard_map/ppermute | solution.py:389
  85.5 20.5 %collective-permute-done.7 = bf16[192,2816]{1,0:T(8,128)(2,1)} collective-permute-done((bf16[192,2816]{1,0:T(8,128)(2,1)S(1)}, bf16[192,2816]{1,0:T(8,128)(2,1)}, u32[]{:S(2)}, u32[]{:S(2)}) %collective-permute-start.7) | collective-permute-done | bytes 1081376 | tf_op jit(solution)/shard_map/ppermute | solution.py:377
  108.1 3.4 collective-permute-start.10
  120.6 4.3 collective-permute-start.11
  126.4 3.5 add_convert_fusion.2.x_ref
  129.8 13.1 %project.1 = (bf16[1024,1536]{1,0:T(8,128)(2,1)}, bf16[1024,768]{1,0:T(8,128)(2,1)}, bf16[4,1024,64]{2,1,0:T(8,128)(2,1)}, bf16[4,1024,64]{2,1,0:T(8,128)(2,1)},...) custom-call(s32[4]{0:T(128)} %pad_add_fusion.place_ref, bf16[1024,1536]{1,0:T(8,128)(2,1)} %add_convert_fusion.2.x_ref, ...), custom_call_target="tpu_custom_call" | custom-call | flops 251658240 | bytes 3538944 | tf_op jit(solution)/shard_map/project/pallas_call | solution.py:524
  149.4 4.8 collective-permute-done.12
  154.2 3.7 pad_maximum_fusion.2
  157.8 2.7 collective-permute-start.17
  163.3 15.0 %attend.2 = (bf16[1024,384]{1,0:T(8,128)(2,1)}, f32[3,1024,2]{2,1,0:T(8,128)}) custom-call(bf16[1024,768]{1,0:T(8,128)(2,1)} %get-tuple-element.158.q_ref, bf16[4,1024,64]{2,1,0:T(8,128)(2,1)} %get-tuple-element.154.k_ref, bf16[4,1024,64]{2,1,0:T(8,128)(2,1)} %get-tuple-element.155.v_ref, s32[1024,1]{1,0:T(8,128)} %copy.109.start_ref), custom_call_target="tpu_custom_call" | custom-call | flops 113246208 | bytes 3145728 | tf_op jit(solution)/shard_map/attend/pallas_call | solution.py:718
  183.3 23.4 %collective-permute-done.14.refs_9_.refs_8_ = bf16[512,1664]{1,0:T(8,128)(2,1)} collective-permute-done((bf16[512,1664]{1,0:T(8,128)(2,1)}, bf16[512,1664]{1,0:T(8,128)(2,1)}, u32[]{:S(2)}, u32[]{:S(2)}) %collective-permute-start.14) | collective-permute-done | bytes 1703968 | tf_op jit(solution)/shard_map/ppermute | solution.py:377
  206.7 15.1 %attend.3 = (bf16[1024,384]{1,0:T(8,128)(2,1)}, f32[3,1024,2]{2,1,0:T(8,128)}) custom-call(bf16[1024,768]{1,0:T(8,128)(2,1)} %get-tuple-element.158.q_ref, bf16[4,1024,64]{2,1,0:T(8,128)(2,1)} %get-tuple-element.154.k_ref, bf16[4,1024,64]{2,1,0:T(8,128)(2,1)} %get-tuple-element.155.v_ref, s32[1024,1]{1,0:T(8,128)} %copy.109.start_ref), custom_call_target="tpu_custom_call" | custom-call | flops 113246208 | bytes 3145728 | tf_op jit(solution)/shard_map/attend/pallas_call | solution.py:718
  230.5 2.8 collective-permute-done.16
  234.6 7.2 collective-permute-done.15
  242.1 4.6 collective-permute-start.35
  251.5 10.2 %mix.1 = (f32[512,1536]{1,0:T(8,128)}, bf16[512,1536]{1,0:T(8,128)(2,1)}, bf16[2,768,1536]{2,1,0:T(8,128)(2,1)}) custom-call(s32[4]{0:T(128)} %pad_add_fusion.place_ref, bf16[512,768]{1,0:T(8,128)(2,1)} %get-tuple-element.354.mine_ref, bf16[512,768]{1,0:T(8,128)(2,1)} %copy-done.24, bf16[512,1536]{1,0:T(8,128)(2,1)} %x_ref.1, ...), custom_call_target="tpu_custom_call" | custom-call | flops 150994944 | bytes 786432 | tf_op jit(solution)/shard_map/mix/pallas_call | solution.py:596
  264.5 30.5 %collective-permute-done.23.refs_0_.refs_1_ = bf16[512,1536]{1,0:T(8,128)(2,1)S(1)} collective-permute-done((bf16[512,1536]{1,0:T(8,128)(2,1)}, bf16[512,1536]{1,0:T(8,128)(2,1)S(1)}, u32[]{:S(2)}, u32[]{:S(2)}) %collective-permute-start.23) | collective-permute-done | bytes 1572896 | tf_op jit(solution)/shard_map/ppermute | solution.py:373
  298.0 4.6 collective-permute-start.33
  304.2 10.0 %collective-permute-done.25.refs_2_ = bf16[256,1536]{1,0:T(8,128)(2,1)S(1)} collective-permute-done((bf16[256,1536]{1,0:T(8,128)(2,1)S(1)}, bf16[256,1536]{1,0:T(8,128)(2,1)S(1)}, u32[]{:S(2)}, u32[]{:S(2)}) %collective-permute-start.25) | collective-permute-done | bytes 786464 | tf_op jit(solution)/shard_map/ppermute | solution.py:377
  314.2 2.9 collective-permute-start.32
  318.2 4.8 collective-permute-done.34.refs_15_
  324.2 2.6 select_select_fusion
  327.7 54.9 %experts.2 = (bf16[1024,1536]{1,0:T(8,128)(2,1)}, bf16[1024,1536]{1,0:T(8,128)(2,1)}, bf16[1024,1536]{1,0:T(8,128)(2,1)}, bf16[1024,1536]{1,0:T(8,128)(2,1)}, bf...) custom-call(s32[1]{0:T(128)} %bitcast.place_ref, ...), custom_call_target="tpu_custom_call" | custom-call | flops 2415919104 | bytes 50331648 | tf_op jit(solution)/shard_map/experts/pallas_call | solution.py:965
  383.5 8.1 %collective-permute-done.37 = bf16[1024,1536]{1,0:T(8,128)(2,1)S(1)} collective-permute-done((bf16[1024,1536]{1,0:T(8,128)(2,1)}, bf16[1024,1536]{1,0:T(8,128)(2,1)S(1)}, u32[]{:S(2)}, u32[]{:S(2)}) %collective-permute-start.37) | collective-permute-done | bytes 3145760 | tf_op jit(solution)/shard_map/ppermute | solution.py:377
  391.6 2.7 add_convert_fusion.1
  401.2 54.5 %experts.3 = (bf16[1024,1536]{1,0:T(8,128)(2,1)}, bf16[1024,1536]{1,0:T(8,128)(2,1)}, bf16[1024,1536]{1,0:T(8,128)(2,1)}, bf16[1024,1536]{1,0:T(8,128)(2,1)}, bf...) custom-call(s32[1]{0:T(128)} %bitcast.place_ref, ...), custom_call_target="tpu_custom_call", output_to_operand_aliasing={{4}: (21, {}), {5}: (22, {}), {6}: (23, {}), {7}: (24, {}),... | custom-call | flops 2415919104 | bytes 50331648 | tf_op jit(solution)/shard_map/experts/pallas_call | solution.py:965
  456.7 11.2 %fusion.11 = bf16[1536,512]{1,0:T(8,128)(2,1)S(1)} fusion(bf16[4096,1536]{1,0:T(8,128)(2,1)} %get-tuple-element.205, bf16[4096,512]{1,0:T(8,128)(2,1)} %get-tuple-element.198), kind=kOutput, calls=%fused_computation.37 | convolution fusion | flops 6444023808 | bytes 18350080 | tf_op jit(solution)/shard_map/dot_general | solution.py:676
  468.5 13.9 %convolution_convert_fusion.1 = bf16[1536,1024]{1,0:T(8,128)(2,1)S(1)} fusion(bf16[4096,1536]{1,0:T(8,128)(2,1)S(1)} %copy-done.16, bf16[4096,1024]{1,0:T(8,128)(2,1)S(1)} %copy-done.23), kind=kOutput, calls=%fused_computation.13 | convolution fusion | flops 12886474752 | bytes 24117248 | tf_op jit(solution)/shard_map/dot_general | solution.py:676
  484.5 5.3 collective-permute-start.47
  492.7 2.9 convert_add_fusion.1
  499.1 17.7 %convolution_convert_fusion = bf16[1536,1024]{1,0:T(8,128)(2,1)} fusion(bf16[4096,1536]{1,0:T(8,128)(2,1)S(1)} %copy-done.16, bf16[4096,1024]{1,0:T(8,128)(2,1)} %get-tuple-element.204), kind=kOutput, calls=%fused_computation.12 | convolution fusion | flops 12886474752 | bytes 24117248 | tf_op jit(solution)/shard_map/dot_general | solution.py:676
  522.0 5.6 fusion.42
  530.0 7.0 fusion.12
  540.6 3.1 fusion.45
  544.1 3.2 add_convert_fusion.6
  547.3 5.3 collective-permute-start.50
  552.6 3.4 add_convert_fusion.5
  557.5 2.8 add_convert_fusion
  571.1 7.2 fusion.38
  582.8 40.5 %attend_back.1 = (bf16[1024,768]{1,0:T(8,128)(2,1)}, bf16[1024,256]{1,0:T(8,128)(2,1)}, bf16[1024,256]{1,0:T(8,128)(2,1)}) custom-call(bf16[1024,768]{1,0:T(8,128)(2,1)} %get-tuple-element.158.q_ref, bf16[4,1024,64]{2,1,0:T(8,128)(2,1)} %get-tuple-element.154.k_ref, bf16[4,1024,64]{2,1,0:T(8,128)(2,1)} %get-tuple-element.155.v_ref, ...), custom_call_target="tpu_custom_call" | custom-call | flops 566231040 | bytes 6291456 | tf_op jit(solution)/shard_map/attend_back/pallas_call | solution.py:795
  623.4 7.9 %add_convert_fusion.3 = (bf16[1536,768]{1,0:T(8,128)(2,1)}, bf16[1536,768]{1,0:T(8,128)(2,1)}) fusion(bf16[1536,768]{1,0:T(8,128)(2,1)} %collective-permute-done.51, pred[]{:T(512)S(6)} %lt.121, pred[]{:T(512)S(6)} %lt.120, bf16[1536,256]{1,0:T(8,128)(2,1)} %copy-done.13, bf16[1536,512]{1,0:T(8,128)(2,1)} %copy-done.3, bf16[1536,256]{1,0:T(8,128)(2,1)} %copy-done.15, ...), kind=kLoop, calls=%fused_computation.5 | loop fusion | flops 33030144 | bytes 18874372 | tf_op jit(solution)/shard_map/convert_element_type | solution.py:1279
  631.3 8.3 %qkv_grad.1 = bf16[2,2,2,4,48,1408]{5,4,3,2,1,0:T(8,128)(2,1)} custom-call(bf16[1024,1536]{1,0:T(8,128)(2,1)} %get-tuple-element.229.h_ref, bf16[1024,768]{1,0:T(8,128)(2,1)} %get-tuple-element.230.dq_ref, bf16[1024,256]{1,0:T(8,128)(2,1)} %get-tuple-element.231.dk_ref, bf16[1024,256]{1,0:T(8,128)(2,1)} %get-tuple-element.232.dv_ref, ...), custom_call_target="tpu_custom_call" | custom-call | flops 251658240 | bytes 1572864 | tf_op jit(solution)/shard_map/qkv_grad/pallas_call | solution.py:1017
  641.6 3.8 collective-permute-start.56
  645.3 2.8 convert_add_fusion
  653.9 5.5 collective-permute-start.59
  662.5 8.5 %collective-permute-done.54 = bf16[256,1536]{1,0:T(8,128)(2,1)S(1)} collective-permute-done((bf16[256,1536]{1,0:T(8,128)(2,1)S(1)}, bf16[256,1536]{1,0:T(8,128)(2,1)S(1)}, u32[]{:S(2)}, u32[]{:S(2)}) %collective-permute-start.54) | collective-permute-done | bytes 786464 | tf_op jit(solution)/shard_map/ppermute | solution.py:373
  671.0 3.3 fusion.35
  675.1 2.5 convert_add_fusion.2
  677.6 11.0 %token_grad.1 = (bf16[512,1536]{1,0:T(8,128)(2,1)}, bf16[512,1536]{1,0:T(8,128)(2,1)}) custom-call(bf16[1024,768]{1,0:T(8,128)(2,1)} %get-tuple-element.230.dq_ref, bf16[1024,256]{1,0:T(8,128)(2,1)} %get-tuple-element.231.dk_ref, bf16[1024,256]{1,0:T(8,128)(2,1)} %get-tuple-element.232.dv_ref, bf16[1536,1280]{1,0:T(8,128)(2,1)} %get-tuple-element.233.w_ref, ...), custom_call_target="tpu_custom_call" | custom-call | flops 251658240 | bytes 1572864 | tf_op jit(solution)/shard_map/token_grad/pallas_call | solution.py:643
  691.2 4.4 collective-permute-done.60
  695.6 3.3 collective-permute-start.61
  700.2 5.2 select_convert_fusion
  705.4 3.2 fusion.33
  709.4 8.1 %collective-permute-done.58 = bf16[2,4,48,1408]{3,2,1,0:T(8,128)(2,1)S(1)} collective-permute-done((bf16[2,4,48,1408]{3,2,1,0:T(8,128)(2,1)S(1)}, bf16[2,4,48,1408]{3,2,1,0:T(8,128)(2,1)S(1)}, u32[]{:S(2)}, u32[]{:S(2)}) %collective-permute-start.58) | collective-permute-done | bytes 1081376 | tf_op jit(solution)/shard_map/ppermute | solution.py:377
  719.0 3.5 collective-permute-done.61
  722.6 4.9 collective-permute-done.62
  727.4 4.4 fusion.16
  734.1 3.1 collective-permute-start.63
  739.2 5.7 collective-permute-start.66
  746.9 8.9 %collective-permute-done.64 = bf16[2,48,1408]{2,1,0:T(8,128)(2,1)S(1)} collective-permute-done((bf16[2,48,1408]{2,1,0:T(8,128)(2,1)S(1)}, bf16[2,48,1408]{2,1,0:T(8,128)(2,1)S(1)}, u32[]{:S(2)}, u32[]{:S(2)}) %collective-permute-start.64) | collective-permute-done | bytes 270368 | tf_op jit(solution)/shard_map/ppermute | solution.py:377
  758.5 4.2 fusion.5
  765.0 6.2 collective-permute-done.66
  (389 shorter events, 162.1 us)
Async XLA Ops:
  7.2 711.9 %reduce-scatter.2.cloned.1.call-start = ((), (), s32[]{:S(2)}) async-start(), calls=%async_computation.1 | async-start | bytes 4866048 | tf_op jit(solution)/shard_map/reduce_scatter | solution.py:1325
  17.5 42.9 %collective-permute-start = (bf16[1536,512]{1,0:T(8,128)(2,1)}, bf16[1536,512]{1,0:T(8,128)(2,1)S(1)}, u32[]{:S(2)}, u32[]{:S(2)}) collective-permute-start(bf16[1536,512]{1,0:T(8,128)(2,1)} %pad_maximum_fusion.8), channel_id=1, source_target_pairs={{0,0},{1,16},{2,2},{3,18},{4,4},{5,20},{6,6},{7,22},{8,8},{9,24},{... | collective-permute-start | bytes 4718600 | tf_op jit(solution)/shard_map/ppermute | solution.py:1083
  20.0 26.1 %collective-permute-start.1 = (bf16[1536,256]{1,0:T(8,128)(2,1)}, bf16[1536,256]{1,0:T(8,128)(2,1)}, u32[]{:S(2)}, u32[]{:S(2)}) collective-permute-start(bf16[1536,256]{1,0:T(8,128)(2,1)} %get-tuple-element.350), channel_id=1, source_target_pairs={{0,1},{1,17},{2,3},{3,19},{4,5},{5,21},{6,7},{7,23},{8,9},{9,25},{... | collective-permute-start | bytes 2359304 | tf_op jit(solution)/shard_map/ppermute | solution.py:1083
  20.2 25.8 %collective-permute-start.3 = (bf16[48,5888]{1,0:T(8,128)(2,1)S(1)}, bf16[48,5888]{1,0:T(8,128)(2,1)}, u32[]{:S(2)}, u32[]{:S(2)}) collective-permute-start(bf16[48,5888]{1,0:T(8,128)(2,1)S(1)} %pad_maximum_fusion.13), channel_id=1, source_target_pairs={{0,4},{1,5},{2,6},{3,7},{4,0},{5,1},{6,2},{7,3},{8,12},{9,13},{10,... | collective-permute-start | bytes 1695752 | tf_op jit(solution)/shard_map/ppermute | solution.py:377
  22.1 24.0 %collective-permute-start.4 = (bf16[48,5888]{1,0:T(8,128)(2,1)S(1)}, bf16[48,5888]{1,0:T(8,128)(2,1)}, u32[]{:S(2)}, u32[]{:S(2)}) collective-permute-start(bf16[48,5888]{1,0:T(8,128)(2,1)S(1)} %pad_maximum_fusion.13), channel_id=1, source_target_pairs={{0,8},{1,9},{2,10},{3,11},{4,12},{5,13},{6,14},{7,15},{8,0},{9,1},... | collective-permute-start | bytes 1695752 | tf_op jit(solution)/shard_map/ppermute | solution.py:377
  24.4 36.0 %collective-permute-start.5 = (bf16[48,5888]{1,0:T(8,128)(2,1)S(1)}, bf16[48,5888]{1,0:T(8,128)(2,1)S(1)}, u32[]{:S(2)}, u32[]{:S(2)}) collective-permute-start(bf16[48,5888]{1,0:T(8,128)(2,1)S(1)} %pad_maximum_fusion.13), channel_id=1, source_target_pairs={{0,12},{1,13},{2,14},{3,15},{4,8},{5,9},{6,10},{7,11},{8,4},{9,5},... | collective-permute-start | bytes 1695752 | tf_op jit(solution)/shard_map/ppermute | solution.py:377
  64.2 41.9 %collective-permute-start.8 = (bf16[768,768]{1,0:T(8,128)(2,1)}, bf16[768,768]{1,0:T(8,128)(2,1)}, u32[]{:S(2)}, u32[]{:S(2)}) collective-permute-start(bf16[768,768]{1,0:T(8,128)(2,1)} %get-tuple-element.339), channel_id=1, source_target_pairs={{0,4},{1,5},{2,6},{3,7},{4,8},{5,9},{6,10},{7,11},{8,12},{9,13},{1... | collective-permute-start | bytes 3538952 | tf_op jit(solution)/shard_map/ppermute | solution.py:389
  79.6 27.2 %collective-permute-start.9 = (bf16[768,768]{1,0:T(8,128)(2,1)}, bf16[768,768]{1,0:T(8,128)(2,1)}, u32[]{:S(2)}, u32[]{:S(2)}) collective-permute-start(bf16[768,768]{1,0:T(8,128)(2,1)} %get-tuple-element.339), channel_id=1, source_target_pairs={{4,0},{5,1},{6,2},{7,3},{8,4},{9,5},{10,6},{11,7},{12,8},{13,9},{1... | collective-permute-start | bytes 3538952 | tf_op jit(solution)/shard_map/ppermute | solution.py:393
  82.9 23.1 %collective-permute-start.7 = (bf16[192,2816]{1,0:T(8,128)(2,1)S(1)}, bf16[192,2816]{1,0:T(8,128)(2,1)}, u32[]{:S(2)}, u32[]{:S(2)}) collective-permute-start(bf16[192,2816]{1,0:T(8,128)(2,1)S(1)} %pad_maximum_fusion.10), channel_id=1, source_target_pairs={{0,2},{1,3},{2,0},{3,1},{4,6},{5,7},{6,4},{7,5},{8,10},{9,11},{10,... | collective-permute-start | bytes 3244040 | tf_op jit(solution)/shard_map/ppermute | solution.py:377
  85.1 41.2 %collective-permute-start.6 = (bf16[512,1536]{1,0:T(8,128)(2,1)S(1)}, bf16[512,1536]{1,0:T(8,128)(2,1)S(1)}, u32[]{:S(2)}, u32[]{:S(2)}) collective-permute-start(bf16[512,1536]{1,0:T(8,128)(2,1)S(1)} %copy-done.8), channel_id=1, source_target_pairs={{0,16},{16,0},{1,17},{17,1},{2,18},{18,2},{3,19},{19,3},{4,20},{20... | collective-permute-start | bytes 4718600 | tf_op jit(solution)/shard_map/ppermute | solution.py:373
  108.1 21.7 %collective-permute-start.10 = (bf16[384,2816]{1,0:T(8,128)(2,1)S(1)}, bf16[384,2816]{1,0:T(8,128)(2,1)}, u32[]{:S(2)}, u32[]{:S(2)}) collective-permute-start(bf16[384,2816]{1,0:T(8,128)(2,1)S(1)} %constant_dynamic-update-slice_fusion.2.own_ref), channel_id=1, source_target_pairs={{0,1},{1,0},{2,3},{3,2},{4,5},{5,4},{6,7},{7,6},{8,9},{9,8},{10,11... | collective-permute-start | bytes 6488072 | tf_op jit(solution)/shard_map/ppermute | solution.py:377
  120.6 28.8 %collective-permute-start.11 = (bf16[768,768]{1,0:T(8,128)(2,1)}, bf16[768,768]{1,0:T(8,128)(2,1)}, u32[]{:S(2)}, u32[]{:S(2)}) collective-permute-start(bf16[768,768]{1,0:T(8,128)(2,1)} %get-tuple-element.149), channel_id=1, source_target_pairs={{0,4},{1,5},{2,6},{3,7},{4,8},{5,9},{6,10},{7,11},{8,12},{9,13},{1... | collective-permute-start | bytes 3538952 | tf_op jit(solution)/shard_map/ppermute | solution.py:389
  124.8 29.3 %collective-permute-start.12 = (bf16[768,768]{1,0:T(8,128)(2,1)}, bf16[768,768]{1,0:T(8,128)(2,1)}, u32[]{:S(2)}, u32[]{:S(2)}) collective-permute-start(bf16[768,768]{1,0:T(8,128)(2,1)} %get-tuple-element.149), channel_id=1, source_target_pairs={{4,0},{5,1},{6,2},{7,3},{8,4},{9,5},{10,6},{11,7},{12,8},{13,9},{1... | collective-permute-start | bytes 3538952 | tf_op jit(solution)/shard_map/ppermute | solution.py:393
  142.9 35.4 %collective-permute-start.19 = (bf16[192,3072]{1,0:T(8,128)(2,1)S(1)}, bf16[192,3072]{1,0:T(8,128)(2,1)}, u32[]{:S(2)}, u32[]{:S(2)}) collective-permute-start(bf16[192,3072]{1,0:T(8,128)(2,1)S(1)} %pad_maximum_fusion.9), channel_id=1, source_target_pairs={{0,2},{1,3},{2,0},{3,1},{4,6},{5,7},{6,4},{7,5},{8,10},{9,11},{10,... | collective-permute-start | bytes 3538952 | tf_op jit(solution)/shard_map/ppermute | solution.py:377
  146.8 59.9 %collective-permute-start.14 = (bf16[512,1664]{1,0:T(8,128)(2,1)}, bf16[512,1664]{1,0:T(8,128)(2,1)}, u32[]{:S(2)}, u32[]{:S(2)}) collective-permute-start(bf16[512,1664]{1,0:T(8,128)(2,1)} %concatenate.121.refs_6_), channel_id=1, source_target_pairs={{0,2},{1,3},{2,0},{3,1},{4,6},{5,7},{6,4},{7,5},{8,10},{9,11},{10,... | collective-permute-start | bytes 5111816 | tf_op jit(solution)/shard_map/ppermute | solution.py:377
  147.6 59.1 %collective-permute-start.13 = (bf16[512,1664]{1,0:T(8,128)(2,1)}, bf16[512,1664]{1,0:T(8,128)(2,1)}, u32[]{:S(2)}, u32[]{:S(2)}) collective-permute-start(bf16[512,1664]{1,0:T(8,128)(2,1)} %concatenate.121.refs_6_), channel_id=1, source_target_pairs={{0,16},{16,0},{1,17},{17,1},{2,18},{18,2},{3,19},{19,3},{4,20},{20... | collective-permute-start | bytes 5111816 | tf_op jit(solution)/shard_map/ppermute | solution.py:373
  157.8 84.3 %collective-permute-start.17 = (bf16[1536,768]{1,0:T(8,128)(2,1)S(1)}, bf16[1536,768]{1,0:T(8,128)(2,1)}, u32[]{:S(2)}, u32[]{:S(2)}) collective-permute-start(bf16[1536,768]{1,0:T(8,128)(2,1)S(1)} %get-tuple-element.160.refs_18_.refs_14_), channel_id=1, source_target_pairs={{0,4},{1,5},{2,6},{3,7},{4,8},{5,9},{6,10},{7,11},{8,12},{9,13},{1... | collective-permute-start | bytes 7077896 | tf_op jit(solution)/shard_map/ppermute | solution.py:389
  160.5 81.6 %collective-permute-start.18 = (bf16[1536,768]{1,0:T(8,128)(2,1)}, bf16[1536,768]{1,0:T(8,128)(2,1)}, u32[]{:S(2)}, u32[]{:S(2)}) collective-permute-start(bf16[1536,768]{1,0:T(8,128)(2,1)} %get-tuple-element.161.refs_20_.refs_16_), channel_id=1, source_target_pairs={{4,0},{5,1},{6,2},{7,3},{8,4},{9,5},{10,6},{11,7},{12,8},{13,9},{1... | collective-permute-start | bytes 7077896 | tf_op jit(solution)/shard_map/ppermute | solution.py:393
  181.8 69.7 %collective-permute-start.20 = (bf16[384,3072]{1,0:T(8,128)(2,1)}, bf16[384,3072]{1,0:T(8,128)(2,1)}, u32[]{:S(2)}, u32[]{:S(2)}) collective-permute-start(bf16[384,3072]{1,0:T(8,128)(2,1)} %constant_dynamic-update-slice_fusion.4.own_ref), channel_id=1, source_target_pairs={{0,1},{1,0},{2,3},{3,2},{4,5},{5,4},{6,7},{7,6},{8,9},{9,8},{10,11... | collective-permute-start | bytes 7077896 | tf_op jit(solution)/shard_map/ppermute | solution.py:377
  223.8 9.4 %collective-permute-start.16 = (bf16[512,384]{1,0:T(8,128)(2,1)S(1)}, bf16[512,384]{1,0:T(8,128)(2,1)S(1)}, u32[]{:S(2)}, u32[]{:S(2)}) collective-permute-start(bf16[512,384]{1,0:T(8,128)(2,1)S(1)} %fusion.51), channel_id=1, source_target_pairs={{0,16},{16,0},{1,17},{17,1},{2,18},{18,2},{3,19},{19,3},{4,20},{20... | collective-permute-start | bytes 1179656 | tf_op jit(solution)/shard_map/ppermute | solution.py:373
  225.0 16.8 %collective-permute-start.15 = (bf16[512,384]{1,0:T(8,128)(2,1)S(1)}, bf16[512,384]{1,0:T(8,128)(2,1)S(1)}, u32[]{:S(2)}, u32[]{:S(2)}) collective-permute-start(bf16[512,384]{1,0:T(8,128)(2,1)S(1)} %fusion.50), channel_id=1, source_target_pairs={{0,16},{16,0},{1,17},{17,1},{2,18},{18,2},{3,19},{19,3},{4,20},{20... | collective-permute-start | bytes 1179656 | tf_op jit(solution)/shard_map/ppermute | solution.py:373
  233.3 28.5 %collective-permute-start.21 = (bf16[256,1664]{1,0:T(8,128)(2,1)}, bf16[256,1664]{1,0:T(8,128)(2,1)}, u32[]{:S(2)}, u32[]{:S(2)}) collective-permute-start(bf16[256,1664]{1,0:T(8,128)(2,1)} %slice.228), channel_id=1, source_target_pairs={{0,2},{1,3},{2,0},{3,1},{4,6},{5,7},{6,4},{7,5},{8,10},{9,11},{10,... | collective-permute-start | bytes 2555912 | tf_op jit(solution)/shard_map/ppermute | solution.py:377
  241.8 20.0 %collective-permute-start.22 = (bf16[256,1664]{1,0:T(8,128)(2,1)}, bf16[256,1664]{1,0:T(8,128)(2,1)}, u32[]{:S(2)}, u32[]{:S(2)}) collective-permute-start(bf16[256,1664]{1,0:T(8,128)(2,1)} %slice.229), channel_id=1, source_target_pairs={{0,16},{16,0},{1,17},{17,1},{2,18},{18,2},{3,19},{19,3},{4,20},{20... | collective-permute-start | bytes 2555912 | tf_op jit(solution)/shard_map/ppermute | solution.py:373
  242.1 60.4 %collective-permute-start.35 = (bf16[1536,768]{1,0:T(8,128)(2,1)}, bf16[1536,768]{1,0:T(8,128)(2,1)}, u32[]{:S(2)}, u32[]{:S(2)}) collective-permute-start(bf16[1536,768]{1,0:T(8,128)(2,1)} %collective-permute-done.17.refs_17_.refs_13_), channel_id=1, source_target_pairs={{0,4},{1,5},{2,6},{3,7},{4,8},{5,9},{6,10},{7,11},{8,12},{9,13},{1... | collective-permute-start | bytes 7077896 | tf_op jit(solution)/shard_map/ppermute | solution.py:389
  248.3 54.3 %collective-permute-start.36 = (bf16[1536,768]{1,0:T(8,128)(2,1)}, bf16[1536,768]{1,0:T(8,128)(2,1)}, u32[]{:S(2)}, u32[]{:S(2)}) collective-permute-start(bf16[1536,768]{1,0:T(8,128)(2,1)} %collective-permute-done.18.refs_21_.refs_17_), channel_id=1, source_target_pairs={{4,0},{5,1},{6,2},{7,3},{8,4},{9,5},{10,6},{11,7},{12,8},{13,9},{1... | collective-permute-start | bytes 7077896 | tf_op jit(solution)/shard_map/ppermute | solution.py:393
  261.8 33.2 %collective-permute-start.23 = (bf16[512,1536]{1,0:T(8,128)(2,1)}, bf16[512,1536]{1,0:T(8,128)(2,1)S(1)}, u32[]{:S(2)}, u32[]{:S(2)}) collective-permute-start(bf16[512,1536]{1,0:T(8,128)(2,1)} %get-tuple-element.171.refs_0_), channel_id=1, source_target_pairs={{0,16},{16,0},{1,17},{17,1},{2,18},{18,2},{3,19},{19,3},{4,20},{20... | collective-permute-start | bytes 4718600 | tf_op jit(solution)/shard_map/ppermute | solution.py:373
  263.2 33.4 %collective-permute-start.24 = (bf16[512,1536]{1,0:T(8,128)(2,1)}, bf16[512,1536]{1,0:T(8,128)(2,1)S(1)}, u32[]{:S(2)}, u32[]{:S(2)}) collective-permute-start(bf16[512,1536]{1,0:T(8,128)(2,1)} %get-tuple-element.171.refs_0_), channel_id=1, source_target_pairs={{0,2},{1,3},{2,0},{3,1},{4,6},{5,7},{6,4},{7,5},{8,10},{9,11},{10,... | collective-permute-start | bytes 4718600 | tf_op jit(solution)/shard_map/ppermute | solution.py:377
  295.1 19.1 %collective-permute-start.25 = (bf16[256,1536]{1,0:T(8,128)(2,1)S(1)}, bf16[256,1536]{1,0:T(8,128)(2,1)S(1)}, u32[]{:S(2)}, u32[]{:S(2)}) collective-permute-start(bf16[256,1536]{1,0:T(8,128)(2,1)S(1)} %slice.285), channel_id=1, source_target_pairs={{0,2},{1,3},{2,0},{3,1},{4,6},{5,7},{6,4},{7,5},{8,10},{9,11},{10,... | collective-permute-start | bytes 2359304 | tf_op jit(solution)/shard_map/ppermute | solution.py:377
  296.6 20.4 %collective-permute-start.26 = (bf16[256,1536]{1,0:T(8,128)(2,1)S(1)}, bf16[256,1536]{1,0:T(8,128)(2,1)S(1)}, u32[]{:S(2)}, u32[]{:S(2)}) collective-permute-start(bf16[256,1536]{1,0:T(8,128)(2,1)S(1)} %slice.286), channel_id=1, source_target_pairs={{0,16},{16,0},{1,17},{17,1},{2,18},{18,2},{3,19},{19,3},{4,20},{20... | collective-permute-start | bytes 2359304 | tf_op jit(solution)/shard_map/ppermute | solution.py:373
  298.0 19.1 %collective-permute-start.33 = (bf16[256,1664]{1,0:T(8,128)(2,1)}, bf16[256,1664]{1,0:T(8,128)(2,1)}, u32[]{:S(2)}, u32[]{:S(2)}) collective-permute-start(bf16[256,1664]{1,0:T(8,128)(2,1)} %collective-permute-done.21.refs_10_), channel_id=1, source_target_pairs={{0,1},{1,0},{2,3},{3,2},{4,5},{5,4},{6,7},{7,6},{8,9},{9,8},{10,11... | collective-permute-start | bytes 2555912 | tf_op jit(solution)/shard_map/ppermute | solution.py:377
  302.6 20.8 %collective-permute-start.27 = (bf16[512,1536]{1,0:T(8,128)(2,1)S(1)}, bf16[512,1536]{1,0:T(8,128)(2,1)}, u32[]{:S(2)}, u32[]{:S(2)}) collective-permute-start(bf16[512,1536]{1,0:T(8,128)(2,1)S(1)} %collective-permute-done.23.refs_0_.refs_1_), channel_id=1, source_target_pairs={{0,1},{1,0},{2,3},{3,2},{4,5},{5,4},{6,7},{7,6},{8,9},{9,8},{10,11... | collective-permute-start | bytes 4718600 | tf_op jit(solution)/shard_map/ppermute | solution.py:377
  302.6 25.1 %collective-permute-start.31 = (bf16[512,1664]{1,0:T(8,128)(2,1)}, bf16[512,1664]{1,0:T(8,128)(2,1)}, u32[]{:S(2)}, u32[]{:S(2)}) collective-permute-start(bf16[512,1664]{1,0:T(8,128)(2,1)} %collective-permute-done.13.refs_8_.refs_7_), channel_id=1, source_target_pairs={{0,1},{1,0},{2,3},{3,2},{4,5},{5,4},{6,7},{7,6},{8,9},{9,8},{10,11... | collective-permute-start | bytes 5111816 | tf_op jit(solution)/shard_map/ppermute | solution.py:377
  314.2 13.5 %collective-permute-start.32 = (bf16[512,1664]{1,0:T(8,128)(2,1)}, bf16[512,1664]{1,0:T(8,128)(2,1)}, u32[]{:S(2)}, u32[]{:S(2)}) collective-permute-start(bf16[512,1664]{1,0:T(8,128)(2,1)} %collective-permute-done.14.refs_9_.refs_8_), channel_id=1, source_target_pairs={{0,1},{1,0},{2,3},{3,2},{4,5},{5,4},{6,7},{7,6},{8,9},{9,8},{10,11... | collective-permute-start | bytes 5111816 | tf_op jit(solution)/shard_map/ppermute | solution.py:377
  317.9 9.7 %collective-permute-start.28 = (bf16[512,1536]{1,0:T(8,128)(2,1)S(1)}, bf16[512,1536]{1,0:T(8,128)(2,1)}, u32[]{:S(2)}, u32[]{:S(2)}) collective-permute-start(bf16[512,1536]{1,0:T(8,128)(2,1)S(1)} %collective-permute-done.24.refs_1_.refs_2_), channel_id=1, source_target_pairs={{0,1},{1,0},{2,3},{3,2},{4,5},{5,4},{6,7},{7,6},{8,9},{9,8},{10,11... | collective-permute-start | bytes 4718600 | tf_op jit(solution)/shard_map/ppermute | solution.py:377
  383.0 18.2 %collective-permute-start.38 = (bf16[512,1536]{1,0:T(8,128)(2,1)}, bf16[512,1536]{1,0:T(8,128)(2,1)}, u32[]{:S(2)}, u32[]{:S(2)}) collective-permute-start(bf16[512,1536]{1,0:T(8,128)(2,1)} %get-tuple-element.171.refs_0_), channel_id=1, source_target_pairs={{0,1},{1,0},{2,3},{3,2},{4,5},{5,4},{6,7},{7,6},{8,9},{9,8},{10,11... | collective-permute-start | bytes 4718600 | tf_op jit(solution)/shard_map/ppermute | solution.py:377
  383.1 18.1 %collective-permute-start.39 = (bf16[512,1664]{1,0:T(8,128)(2,1)}, bf16[512,1664]{1,0:T(8,128)(2,1)}, u32[]{:S(2)}, u32[]{:S(2)}) collective-permute-start(bf16[512,1664]{1,0:T(8,128)(2,1)} %concatenate.121.refs_6_), channel_id=1, source_target_pairs={{0,1},{1,0},{2,3},{3,2},{4,5},{5,4},{6,7},{7,6},{8,9},{9,8},{10,11... | collective-permute-start | bytes 5111816 | tf_op jit(solution)/shard_map/ppermute | solution.py:377
  396.1 60.6 %collective-permute-start.40 = (bf16[512,1536]{1,0:T(8,128)(2,1)}, bf16[512,1536]{1,0:T(8,128)(2,1)}, u32[]{:S(2)}, u32[]{:S(2)}) collective-permute-start(bf16[512,1536]{1,0:T(8,128)(2,1)} %get-tuple-element.329), channel_id=1, source_target_pairs={{0,2},{1,3},{2,0},{3,1},{4,6},{5,7},{6,4},{7,5},{8,10},{9,11},{10,... | collective-permute-start | bytes 4718600 | tf_op jit(solution)/shard_map/ppermute | solution.py:377
  397.6 59.1 %collective-permute-start.41 = (bf16[512,1536]{1,0:T(8,128)(2,1)}, bf16[512,1536]{1,0:T(8,128)(2,1)}, u32[]{:S(2)}, u32[]{:S(2)}) collective-permute-start(bf16[512,1536]{1,0:T(8,128)(2,1)} %get-tuple-element.328), channel_id=1, source_target_pairs={{0,16},{16,0},{1,17},{17,1},{2,18},{18,2},{3,19},{19,3},{4,20},{20... | collective-permute-start | bytes 4718600 | tf_op jit(solution)/shard_map/ppermute | solution.py:373
  455.7 37.0 %collective-permute-start.42 = (bf16[1024,1536]{1,0:T(8,128)(2,1)}, bf16[1024,1536]{1,0:T(8,128)(2,1)}, u32[]{:S(2)}, u32[]{:S(2)}) collective-permute-start(bf16[1024,1536]{1,0:T(8,128)(2,1)} %get-tuple-element.200), channel_id=1, source_target_pairs={{0,1},{1,0},{2,3},{3,2},{4,5},{5,4},{6,7},{7,6},{8,9},{9,8},{10,11... | collective-permute-start | bytes 9437192 | tf_op jit(solution)/shard_map/ppermute | solution.py:377
  484.5 59.6 %collective-permute-start.47 = (bf16[1536,768]{1,0:T(8,128)(2,1)}, bf16[1536,768]{1,0:T(8,128)(2,1)}, u32[]{:S(2)}, u32[]{:S(2)}) collective-permute-start(bf16[1536,768]{1,0:T(8,128)(2,1)} %pad_maximum_fusion.5), channel_id=1, source_target_pairs={{0,4},{1,5},{2,6},{3,7},{4,8},{5,9},{6,10},{7,11},{8,12},{9,13},{1... | collective-permute-start | bytes 7077896 | tf_op jit(solution)/shard_map/ppermute | solution.py:389
  491.3 61.3 %collective-permute-start.48 = (bf16[1536,768]{1,0:T(8,128)(2,1)}, bf16[1536,768]{1,0:T(8,128)(2,1)}, u32[]{:S(2)}, u32[]{:S(2)}) collective-permute-start(bf16[1536,768]{1,0:T(8,128)(2,1)} %pad_maximum_fusion.4), channel_id=1, source_target_pairs={{4,0},{5,1},{6,2},{7,3},{8,4},{9,5},{10,6},{11,7},{12,8},{13,9},{1... | collective-permute-start | bytes 7077896 | tf_op jit(solution)/shard_map/ppermute | solution.py:393
  497.5 19.3 %collective-permute-start.43 = (bf16[256,1536]{1,0:T(8,128)(2,1)S(1)}, bf16[256,1536]{1,0:T(8,128)(2,1)S(1)}, u32[]{:S(2)}, u32[]{:S(2)}) collective-permute-start(bf16[256,1536]{1,0:T(8,128)(2,1)S(1)} %get-tuple-element.316), channel_id=1, source_target_pairs={{0,16},{16,0},{1,17},{17,1},{2,18},{18,2},{3,19},{19,3},{4,20},{20... | collective-permute-start | bytes 2359304 | tf_op jit(solution)/shard_map/ppermute | solution.py:373
  498.9 18.6 %collective-permute-start.44 = (bf16[256,1536]{1,0:T(8,128)(2,1)S(1)}, bf16[256,1536]{1,0:T(8,128)(2,1)S(1)}, u32[]{:S(2)}, u32[]{:S(2)}) collective-permute-start(bf16[256,1536]{1,0:T(8,128)(2,1)S(1)} %get-tuple-element.317), channel_id=1, source_target_pairs={{0,2},{1,3},{2,0},{3,1},{4,6},{5,7},{6,4},{7,5},{8,10},{9,11},{10,... | collective-permute-start | bytes 2359304 | tf_op jit(solution)/shard_map/ppermute | solution.py:377
  527.6 29.8 %collective-permute-start.49 = (bf16[1024,1536]{1,0:T(8,128)(2,1)S(1)}, bf16[1024,1536]{1,0:T(8,128)(2,1)}, u32[]{:S(2)}, u32[]{:S(2)}) collective-permute-start(bf16[1024,1536]{1,0:T(8,128)(2,1)S(1)} %copy-done.63), channel_id=1, source_target_pairs={{0,1},{1,0},{2,3},{3,2},{4,5},{5,4},{6,7},{7,6},{8,9},{9,8},{10,11... | collective-permute-start | bytes 9437192 | tf_op jit(solution)/shard_map/ppermute | solution.py:377
  539.2 106.1 %collective-permute-start.45 = (bf16[1024,1536]{1,0:T(8,128)(2,1)}, bf16[1024,1536]{1,0:T(8,128)(2,1)}, u32[]{:S(2)}, u32[]{:S(2)}) collective-permute-start(bf16[1024,1536]{1,0:T(8,128)(2,1)} %get-tuple-element.210), channel_id=1, source_target_pairs={{0,1},{1,0},{2,3},{3,2},{4,5},{5,4},{6,7},{7,6},{8,9},{9,8},{10,11... | collective-permute-start | bytes 9437192 | tf_op jit(solution)/shard_map/ppermute | solution.py:377
  543.8 18.8 %collective-permute-start.46 = (bf16[512,768]{1,0:T(8,128)(2,1)S(1)}, bf16[512,768]{1,0:T(8,128)(2,1)S(1)}, u32[]{:S(2)}, u32[]{:S(2)}) collective-permute-start(bf16[512,768]{1,0:T(8,128)(2,1)S(1)} %fusion.45), channel_id=1, source_target_pairs={{0,16},{16,0},{1,17},{17,1},{2,18},{18,2},{3,19},{19,3},{4,20},{20... | collective-permute-start | bytes 2359304 | tf_op jit(solution)/shard_map/ppermute | solution.py:373
  547.3 76.0 %collective-permute-start.50 = (bf16[1536,768]{1,0:T(8,128)(2,1)}, bf16[1536,768]{1,0:T(8,128)(2,1)}, u32[]{:S(2)}, u32[]{:S(2)}) collective-permute-start(bf16[1536,768]{1,0:T(8,128)(2,1)} %add_convert_fusion.6), channel_id=1, source_target_pairs={{0,4},{1,5},{2,6},{3,7},{4,8},{5,9},{6,10},{7,11},{8,12},{9,13},{1... | collective-permute-start | bytes 7077896 | tf_op jit(solution)/shard_map/ppermute | solution.py:389
  556.0 67.4 %collective-permute-start.51 = (bf16[1536,768]{1,0:T(8,128)(2,1)}, bf16[1536,768]{1,0:T(8,128)(2,1)}, u32[]{:S(2)}, u32[]{:S(2)}) collective-permute-start(bf16[1536,768]{1,0:T(8,128)(2,1)} %add_convert_fusion.5), channel_id=1, source_target_pairs={{4,0},{5,1},{6,2},{7,3},{8,4},{9,5},{10,6},{11,7},{12,8},{13,9},{1... | collective-permute-start | bytes 7077896 | tf_op jit(solution)/shard_map/ppermute | solution.py:393
  562.1 61.3 %collective-permute-start.52 = (bf16[512,1536]{1,0:T(8,128)(2,1)}, bf16[512,1536]{1,0:T(8,128)(2,1)}, u32[]{:S(2)}, u32[]{:S(2)}) collective-permute-start(bf16[512,1536]{1,0:T(8,128)(2,1)} %get-tuple-element.323), channel_id=1, source_target_pairs={{0,2},{1,3},{2,0},{3,1},{4,6},{5,7},{6,4},{7,5},{8,10},{9,11},{10,... | collective-permute-start | bytes 4718600 | tf_op jit(solution)/shard_map/ppermute | solution.py:377
  562.6 60.8 %collective-permute-start.53 = (bf16[512,1536]{1,0:T(8,128)(2,1)}, bf16[512,1536]{1,0:T(8,128)(2,1)}, u32[]{:S(2)}, u32[]{:S(2)}) collective-permute-start(bf16[512,1536]{1,0:T(8,128)(2,1)} %get-tuple-element.322), channel_id=1, source_target_pairs={{0,16},{16,0},{1,17},{17,1},{2,18},{18,2},{3,19},{19,3},{4,20},{20... | collective-permute-start | bytes 4718600 | tf_op jit(solution)/shard_map/ppermute | solution.py:373
  641.6 33.5 %collective-permute-start.56 = (bf16[2,2,4,48,1408]{4,3,2,1,0:T(8,128)(2,1)S(1)}, bf16[2,2,4,48,1408]{4,3,2,1,0:T(8,128)(2,1)S(1)}, u32[]{:S(2)}, u32[]{:S(2)}) collective-permute-start(bf16[2,2,4,48,1408]{4,3,2,1,0:T(8,128)(2,1)S(1)} %dynamic-slice_bitcast_fusion), channel_id=1, source_target_pairs={{0,1},{1,0},{2,3},{3,2},{4,5},{5,4},{6,7},{7,6},{8,9},{9,8},{10,11... | collective-permute-start | bytes 6488072 | tf_op jit(solution)/shard_map/ppermute | solution.py:377
  650.3 20.7 %collective-permute-start.54 = (bf16[256,1536]{1,0:T(8,128)(2,1)S(1)}, bf16[256,1536]{1,0:T(8,128)(2,1)S(1)}, u32[]{:S(2)}, u32[]{:S(2)}) collective-permute-start(bf16[256,1536]{1,0:T(8,128)(2,1)S(1)} %fusion.34), channel_id=1, source_target_pairs={{0,16},{16,0},{1,17},{17,1},{2,18},{18,2},{3,19},{19,3},{4,20},{20... | collective-permute-start | bytes 2359304 | tf_op jit(solution)/shard_map/ppermute | solution.py:373
  653.9 37.3 %collective-permute-start.59 = (bf16[768,768]{1,0:T(8,128)(2,1)}, bf16[768,768]{1,0:T(8,128)(2,1)}, u32[]{:S(2)}, u32[]{:S(2)}) collective-permute-start(bf16[768,768]{1,0:T(8,128)(2,1)} %get-tuple-element.337), channel_id=1, source_target_pairs={{0,4},{1,5},{2,6},{3,7},{4,8},{5,9},{6,10},{7,11},{8,12},{9,13},{1... | collective-permute-start | bytes 3538952 | tf_op jit(solution)/shard_map/ppermute | solution.py:389
  661.0 34.6 %collective-permute-start.60 = (bf16[768,768]{1,0:T(8,128)(2,1)}, bf16[768,768]{1,0:T(8,128)(2,1)}, u32[]{:S(2)}, u32[]{:S(2)}) collective-permute-start(bf16[768,768]{1,0:T(8,128)(2,1)} %get-tuple-element.335), channel_id=1, source_target_pairs={{4,0},{5,1},{6,2},{7,3},{8,4},{9,5},{10,6},{11,7},{12,8},{13,9},{1... | collective-permute-start | bytes 3538952 | tf_op jit(solution)/shard_map/ppermute | solution.py:393
  674.3 31.1 %collective-permute-start.55 = (bf16[256,1536]{1,0:T(8,128)(2,1)}, bf16[256,1536]{1,0:T(8,128)(2,1)}, u32[]{:S(2)}, u32[]{:S(2)}) collective-permute-start(bf16[256,1536]{1,0:T(8,128)(2,1)} %get-tuple-element.313), channel_id=1, source_target_pairs={{0,2},{1,3},{2,0},{3,1},{4,6},{5,7},{6,4},{7,5},{8,10},{9,11},{10,... | collective-permute-start | bytes 2359304 | tf_op jit(solution)/shard_map/ppermute | solution.py:377
  690.5 27.0 %collective-permute-start.58 = (bf16[2,4,48,1408]{3,2,1,0:T(8,128)(2,1)S(1)}, bf16[2,4,48,1408]{3,2,1,0:T(8,128)(2,1)S(1)}, u32[]{:S(2)}, u32[]{:S(2)}) collective-permute-start(bf16[2,4,48,1408]{3,2,1,0:T(8,128)(2,1)S(1)} %fusion.52), channel_id=1, source_target_pairs={{0,2},{1,3},{2,0},{3,1},{4,6},{5,7},{6,4},{7,5},{8,10},{9,11},{10,... | collective-permute-start | bytes 3244040 | tf_op jit(solution)/shard_map/ppermute | solution.py:377
  695.6 26.9 %collective-permute-start.61 = (bf16[768,768]{1,0:T(8,128)(2,1)}, bf16[768,768]{1,0:T(8,128)(2,1)}, u32[]{:S(2)}, u32[]{:S(2)}) collective-permute-start(bf16[768,768]{1,0:T(8,128)(2,1)} %get-tuple-element.238), channel_id=1, source_target_pairs={{0,4},{1,5},{2,6},{3,7},{4,8},{5,9},{6,10},{7,11},{8,12},{9,13},{1... | collective-permute-start | bytes 3538952 | tf_op jit(solution)/shard_map/ppermute | solution.py:389
  698.9 28.5 %collective-permute-start.62 = (bf16[768,768]{1,0:T(8,128)(2,1)}, bf16[768,768]{1,0:T(8,128)(2,1)}, u32[]{:S(2)}, u32[]{:S(2)}) collective-permute-start(bf16[768,768]{1,0:T(8,128)(2,1)} %get-tuple-element.239), channel_id=1, source_target_pairs={{4,0},{5,1},{6,2},{7,3},{8,4},{9,5},{10,6},{11,7},{12,8},{13,9},{1... | collective-permute-start | bytes 3538952 | tf_op jit(solution)/shard_map/ppermute | solution.py:393
  708.7 47.3 %collective-permute-start.57 = (bf16[512,1536]{1,0:T(8,128)(2,1)}, bf16[512,1536]{1,0:T(8,128)(2,1)}, u32[]{:S(2)}, u32[]{:S(2)}) collective-permute-start(bf16[512,1536]{1,0:T(8,128)(2,1)} %get-tuple-element.236), channel_id=1, source_target_pairs={{0,16},{16,0},{1,17},{17,1},{2,18},{18,2},{3,19},{19,3},{4,20},{20... | collective-permute-start | bytes 4718600 | tf_op jit(solution)/shard_map/ppermute | solution.py:373
  733.5 12.2 %collective-permute-start.65 = (bf16[2,48,1408]{2,1,0:T(8,128)(2,1)S(1)}, bf16[2,48,1408]{2,1,0:T(8,128)(2,1)S(1)}, u32[]{:S(2)}, u32[]{:S(2)}) collective-permute-start(bf16[2,48,1408]{2,1,0:T(8,128)(2,1)S(1)} %fusion.65), channel_id=1, source_target_pairs={{0,12},{1,13},{2,14},{3,15},{4,8},{5,9},{6,10},{7,11},{8,4},{9,5},... | collective-permute-start | bytes 811016 | tf_op jit(solution)/shard_map/ppermute | solution.py:377
  733.6 22.2 %collective-permute-start.64 = (bf16[2,48,1408]{2,1,0:T(8,128)(2,1)S(1)}, bf16[2,48,1408]{2,1,0:T(8,128)(2,1)S(1)}, u32[]{:S(2)}, u32[]{:S(2)}) collective-permute-start(bf16[2,48,1408]{2,1,0:T(8,128)(2,1)S(1)} %get-tuple-element.353), channel_id=1, source_target_pairs={{0,8},{1,9},{2,10},{3,11},{4,12},{5,13},{6,14},{7,15},{8,0},{9,1},... | collective-permute-start | bytes 811016 | tf_op jit(solution)/shard_map/ppermute | solution.py:377
  734.1 21.7 %collective-permute-start.63 = (bf16[2,48,1408]{2,1,0:T(8,128)(2,1)S(1)}, bf16[2,48,1408]{2,1,0:T(8,128)(2,1)S(1)}, u32[]{:S(2)}, u32[]{:S(2)}) collective-permute-start(bf16[2,48,1408]{2,1,0:T(8,128)(2,1)S(1)} %get-tuple-element.352), channel_id=1, source_target_pairs={{0,4},{1,5},{2,6},{3,7},{4,0},{5,1},{6,2},{7,3},{8,12},{9,13},{10,... | collective-permute-start | bytes 811016 | tf_op jit(solution)/shard_map/ppermute | solution.py:377
  739.2 32.0 %collective-permute-start.66 = (bf16[1536,512]{1,0:T(8,128)(2,1)S(1)}, bf16[1536,512]{1,0:T(8,128)(2,1)S(1)}, u32[]{:S(2)}, u32[]{:S(2)}) collective-permute-start(bf16[1536,512]{1,0:T(8,128)(2,1)S(1)} %fusion.31), channel_id=1, source_target_pairs={{0,0},{1,16},{2,2},{3,18},{4,4},{5,20},{6,6},{7,22},{8,8},{9,24},{... | collective-permute-start | bytes 4718600 | tf_op jit(solution)/shard_map/ppermute | solution.py:1083
  745.7 19.3 %collective-permute-start.67 = (bf16[1536,256]{1,0:T(8,128)(2,1)S(1)}, bf16[1536,256]{1,0:T(8,128)(2,1)S(1)}, u32[]{:S(2)}, u32[]{:S(2)}) collective-permute-start(bf16[1536,256]{1,0:T(8,128)(2,1)S(1)} %get-tuple-element.247), channel_id=1, source_target_pairs={{1,0},{17,1},{3,2},{19,3},{5,4},{21,5},{7,6},{23,7},{9,8},{25,9},{... | collective-permute-start | bytes 2359304 | tf_op jit(solution)/shard_map/ppermute | solution.py:1083
  (83 other events, 1404.9 us)
Sparse Core Ops, SparseCore 0:
  578.4 109.2 reduce-scatter.1

commit v9 on v4

--- a/solution.py
+++ b/solution.py
@@ -468,10 +468,9 @@
     scale = lax.rsqrt(jnp.mean(value * value, axis=-1, keepdims=True) + EPSILON)
     normed = (value * scale * gain_ref[...]).astype(BF16)
     h_ref[...] = normed
+    both = jnp.dot(normed, w_ref[...], preferred_element_type=F32)
     q_width, kv_heads = q_ref.shape[1], k_ref.shape[0]
     kv_width = kv_heads * HDIM
-    weights = w_ref[:, : q_width + 2 * kv_width]
-    both = jnp.dot(normed, weights, preferred_element_type=F32)
     spun = turned(both[:, : q_width + kv_width], cos_ref[...], sin_ref[...], 1)
     q_ref[...] = (spun[:, :q_width] * SCORE_SCALE).astype(BF16)
     for head in range(kv_heads):
@@ -496,7 +495,7 @@
         in_specs=[
             row_block(width),
             pl.BlockSpec((1, width), lambda i: (0, 0)),
-            pl.BlockSpec((width, width), lambda i: (0, 1)),
+            pl.BlockSpec((width, columns), lambda i: (0, 0)),
             row_block(cos.shape[1]),
             row_block(cos.shape[1]),
         ],
@@ -517,58 +516,6 @@
     )(x_sorted, gain, weights, cos, sin)
 
 
-def mix_kernel(place_ref, mine_ref, theirs_ref, x_ref, gain_ref, w_ref, m_ref, h_ref, parts_ref):
-    half = parts_ref.shape[1]
-
-    @pl.when(pl.program_id(0) == 0)
-    def _():
-        for part in range(2):
-            low = pl.multiple_of((place_ref[0] ^ part) * half, half)
-            parts_ref[part] = w_ref[pl.ds(low, half), :]
-
-    mixed = jnp.dot(mine_ref[...], parts_ref[0], preferred_element_type=F32)
-    mixed = mixed + jnp.dot(theirs_ref[...], parts_ref[1], preferred_element_type=F32)
-    value = x_ref[...].astype(F32) + BRANCH_SCALE * mixed
-    m_ref[...] = value
-    scale = lax.rsqrt(jnp.mean(value * value, axis=-1, keepdims=True) + EPSILON)
-    h_ref[...] = (value * scale * gain_ref[...]).astype(BF16)
-
-
-def mix(place, mine, theirs, tokens, gain, weights):
-    rows, width = tokens.shape
-    half = mine.shape[1]
-    tile = 256
-
-    def row_block(lanes):
-        return pl.BlockSpec((tile, lanes), lambda i, p: (i, 0))
-
-    def whole(shape):
-        return pl.BlockSpec(shape, lambda i, p: (0,) * len(shape))
-
-    return pl.pallas_call(
-        mix_kernel,
-        grid_spec=pltpu.PrefetchScalarGridSpec(
-            num_scalar_prefetch=1,
-            grid=(rows // tile,),
-            in_specs=[
-                row_block(half), row_block(half), row_block(width), whole(gain.shape),
-                whole((width, width)),
-            ],
-            out_specs=[row_block(width), row_block(width), whole((2, half, width))],
-        ),
-        out_shape=[
-            jax.ShapeDtypeStruct((rows, width), F32),
-            jax.ShapeDtypeStruct((rows, width), BF16),
-            jax.ShapeDtypeStruct((2, half, width), BF16),
-        ],
-        compiler_params=pltpu.CompilerParams(vmem_limit_bytes=VMEM_BYTES),
-        cost_estimate=pl.CostEstimate(
-            flops=rows * width * width // 8, bytes_accessed=rows * width, transcendentals=rows
-        ),
-        name="mix",
-    )(place, mine, theirs, tokens, gain, weights)
-
-
 def token_grad_kernel(dq_ref, dk_ref, dv_ref, w_ref, own_ref, other_ref, mine_ref, sent_ref):
     q_width, kv_width = dq_ref.shape[1], dk_ref.shape[1]
     cuts = (0, q_width, q_width + kv_width, q_width + 2 * kv_width)
@@ -596,7 +543,7 @@
         token_grad_kernel,
         grid=(3,),
         in_specs=[whole(grad) for grad in grads]
-        + [pl.BlockSpec((tile, width), lambda i: (i, 1)), whole(own_places), whole(other_places)],
+        + [pl.BlockSpec((tile, columns), lambda i: (i, 0)), whole(own_places), whole(other_places)],
         out_specs=[block, block],
         out_shape=[jax.ShapeDtypeStruct((count, width), BF16)] * 2,
         compiler_params=pltpu.CompilerParams(vmem_limit_bytes=VMEM_BYTES),
@@ -630,13 +577,11 @@
     )
 
 
-def probabilities(query, keys, allowed):
-    scores = jnp.where(allowed, contract(query, keys, 1, 1), -1e30)
-    expon = jnp.exp(scores - jnp.max(scores, axis=-1, keepdims=True))
-    return expon * (1.0 / jnp.sum(expon, axis=-1, keepdims=True))
-
-
-def attend_kernel(base, q_ref, k_ref, v_ref, start_ref, o_ref):
+def masked_scores(query, keys, allowed):
+    return jnp.where(allowed, contract(query, keys, 1, 1), -1e30)
+
+
+def attend_kernel(base, q_ref, k_ref, v_ref, start_ref, o_ref, level_ref):
     pair = pl.program_id(0) + base
     ratio = QHEADS // KVHEADS
     for row, low, high in windows(q_ref.shape[0]):
@@ -644,9 +589,14 @@
         for side in range(2):
             head = (2 * pair + side) // ratio
             lanes = slice(side * HDIM, (side + 1) * HDIM)
-            probs = probabilities(
+            scores = masked_scores(
                 q_ref[row : row + Q_TILE, lanes], k_ref[head, low:high, :], allowed
             )
+            highest = jnp.max(scores, axis=-1, keepdims=True)
+            expon = jnp.exp(scores - highest)
+            total = jnp.sum(expon, axis=-1, keepdims=True)
+            level_ref[0, row : row + Q_TILE, side : side + 1] = highest + jnp.log(total)
+            probs = expon * (1.0 / total)
             mixed = contract(probs.astype(BF16), v_ref[head, low:high, :], 1, 0)
             o_ref[row : row + Q_TILE, lanes] = mixed.astype(BF16)
 
@@ -668,8 +618,14 @@
         functools.partial(attend_kernel, base),
         grid=(pairs,),
         in_specs=[pair_block, whole, whole, pl.BlockSpec((rows, 1), lambda j: (0, 0))],
-        out_specs=pl.BlockSpec((rows, 2 * HDIM), lambda j: (0, j)),
-        out_shape=jax.ShapeDtypeStruct((rows, pairs * 2 * HDIM), BF16),
+        out_specs=[
+            pl.BlockSpec((rows, 2 * HDIM), lambda j: (0, j)),
+            pl.BlockSpec((1, rows, 2), lambda j: (j, 0, 0)),
+        ],
+        out_shape=[
+            jax.ShapeDtypeStruct((rows, pairs * 2 * HDIM), BF16),
+            jax.ShapeDtypeStruct((pairs, rows, 2), F32),
+        ],
         compiler_params=pltpu.CompilerParams(vmem_limit_bytes=VMEM_BYTES),
         cost_estimate=attention_cost(rows, 2 * pairs, 2),
         name="attend",
@@ -677,7 +633,7 @@
 
 
 def attend_back_kernel(
-    q_ref, k_ref, v_ref, d_ref, start_ref, cos_ref, sin_ref,
+    q_ref, k_ref, v_ref, d_ref, level_ref, start_ref, cos_ref, sin_ref,
     dq_ref, dk_ref, dv_ref, dk_sum, dv_sum,
 ):
     pair = pl.program_id(0)
@@ -696,7 +652,10 @@
             lanes = slice(side * HDIM, (side + 1) * HDIM)
             query = q_ref[row : row + Q_TILE, lanes]
             keys = k_ref[head, low:high, :]
-            probs = probabilities(query, keys, allowed)
+            probs = jnp.exp(
+                masked_scores(query, keys, allowed)
+                - level_ref[0, row : row + Q_TILE, side : side + 1]
+            )
             grad_out = d_ref[row : row + Q_TILE, lanes]
             grad_probs = contract(grad_out, v_ref[head, low:high, :], 1, 1)
             inner = jnp.sum(probs * grad_probs, axis=-1, keepdims=True)
@@ -721,7 +680,7 @@
         dv_ref[...] = jnp.concatenate([dv_sum[head] for head in heads], axis=1).astype(BF16)
 
 
-def attend_back(query, keys, values, grad_out, starts, cos, sin):
+def attend_back(query, keys, values, grad_out, levels, starts, cos, sin):
     rows, lanes = query.shape
     pairs = lanes // (2 * HDIM)
     kv_heads = keys.shape[0]
@@ -736,7 +695,8 @@
         attend_back_kernel,
         grid=(pairs,),
         in_specs=[
-            pair_block, whole, whole, pair_block, fixed(1), fixed(2 * HDIM), fixed(2 * HDIM),
+            pair_block, whole, whole, pair_block,
+            pl.BlockSpec((1, rows, 2), lambda j: (j, 0, 0)), fixed(1), fixed(2 * HDIM), fixed(2 * HDIM),
         ],
         out_specs=[pair_block, fixed(flat), fixed(flat)],
         out_shape=[
@@ -748,7 +708,7 @@
         compiler_params=pltpu.CompilerParams(vmem_limit_bytes=VMEM_BYTES),
         cost_estimate=attention_cost(rows, 2 * pairs, 5),
         name="attend_back",
-    )(query, keys, values, grad_out, starts, cos, sin)
+    )(query, keys, values, grad_out, levels, starts, cos, sin)
 
 
 SLOTS = 2 * LINE - 1
@@ -1035,16 +995,14 @@
 
     projections = (w_query, w_key, w_value)
     qkv_width = q_width + 2 * kv_width
-    gain_columns = jnp.pad(
-        jnp.stack([gain_attn, gain_ffn], axis=1), ((0, 0), (0, width - qkv_width - 2))
-    )
-    mine, theirs = [
-        jnp.concatenate([w_output] + [half_of(w, which) for w in projections] + [gain_columns], axis=1)
-        for which in (seq, 1 - seq)
-    ]
+    gain_columns = jnp.pad(jnp.stack([gain_attn, gain_ffn], axis=1), ((0, 0), (0, PAD - 2)))
+    mine = jnp.concatenate([half_of(w, seq) for w in projections] + [gain_columns], axis=1)
+    theirs = jnp.concatenate([half_of(w, 1 - seq) for w in projections] + [gain_columns], axis=1)
     theirs = swap_seq(theirs)
     pair = jnp.stack([jnp.where(first_seq, mine, theirs), jnp.where(first_seq, theirs, mine)])
-    gathered = lax.all_gather(pair, "dp", axis=1, tiled=True).reshape(width, 2 * width)
+    qkv_width = q_width + 2 * kv_width
+    w_qkv = lax.all_gather(pair, "dp", axis=1, tiled=True).reshape(width, qkv_width + PAD)
+    output_full = lax.all_gather(w_output, ("seq", "dp"), axis=0, tiled=True)
 
     in_own = w_in[0]
     half = in_own.shape[1] // 2
@@ -1063,6 +1021,8 @@
     )
     other_tokens = swap_seq(after(tokens, own_part))
     up_one, down_one = line_up(own_part), line_down(own_part)
+    cut = width // 2
+
     experts_all = 4 * LINE
     gates = jax.nn.softmax(logits, axis=-1)
     named = routes[:, :, None] == jnp.arange(experts_all, dtype=jnp.int32)[None, None, :]
@@ -1110,33 +1070,35 @@
         return contract(sort, values, 0, 0).astype(BF16)
 
     x_sorted = to_order(tokens, other_tokens)
+    gains = w_qkv[:, qkv_width : qkv_width + 2].astype(F32).T
+    gain_one, gain_two = gains[0], gains[1]
     x_sorted, up_one, down_one = lax.optimization_barrier((x_sorted, up_one, down_one))
     up_two, down_two = line_up(up_one), line_down(down_one)
-    gains = gathered[:, width + qkv_width : width + qkv_width + 2].astype(F32).T
-    gain_one, gain_two = gains[0], gains[1]
     normed, query, keys, values = project(
-        x_sorted, gain_one[None, :], gathered, cos, sin, q_width, kv_heads
+        x_sorted, gain_one[None, :], w_qkv, cos, sin, q_width, kv_heads
     )
     pairs = q_width // (2 * HDIM)
     first_pairs = (pairs + 1) // 2
-    mixed_one = attend(query, keys, values, start_column, 0, first_pairs)
+    mixed_one, levels_one = attend(query, keys, values, start_column, 0, first_pairs)
     sent_one = swap_seq(from_order(sort_other, mixed_one))
     query_two, grad_near_x, grad_near_y = after((query, *grad_near), mixed_one)
     grad_near = (grad_near_x, grad_near_y)
     grad_far = far_pieces(*grad_near)
-    mixed_two = attend(
+    mixed_two, levels_two = attend(
         query_two, keys, values, start_column, first_pairs, pairs - first_pairs
     )
     sent_two = swap_seq(from_order(sort_other, mixed_two))
     mixed_mine = [from_order(sort_own, mixed_one), from_order(sort_own, mixed_two)]
-    mixed_mine = jnp.concatenate(mixed_mine, axis=1)
-    mixed_theirs = jnp.concatenate([sent_one, sent_two], axis=1)
-    mixed_theirs, up_two, down_two = lax.optimization_barrier((mixed_theirs, up_two, down_two))
+    mixed = ordered(
+        jnp.concatenate(mixed_mine, axis=1), jnp.concatenate([sent_one, sent_two], axis=1), 1
+    )
+    mixed, up_two, down_two = lax.optimization_barrier((mixed, up_two, down_two))
     up_three, down_three = line_up(up_two), line_down(down_two)
     inputs = tokens.astype(F32)
-    middle, normed_ffn, output_parts = mix(
-        seq.astype(jnp.int32)[None], mixed_mine, mixed_theirs, tokens, gain_two[None, :], gathered
-    )
+    attn = jnp.dot(mixed, output_full, preferred_element_type=F32)
+    middle = inputs + BRANCH_SCALE * attn
+    normed_ffn = rms_norm(middle, gain_two).astype(BF16)
+
     normed_ffn = after(normed_ffn, *grad_far)
     row_near = near_pieces(normed_ffn, normed_ffn)
     row_far = far_pieces(*row_near)
@@ -1198,10 +1160,9 @@
     grad_norm, grad_gain_two = norm_back(middle, gain_two, grad_normed_ffn)
     grad_middle = grad_final + grad_norm
     grad_attn = (BRANCH_SCALE * grad_middle).astype(BF16)
-    grad_mixed = contract(grad_attn, output_parts[0], 1, 1).astype(BF16)
-    grad_other = contract(grad_attn, output_parts[1], 1, 1).astype(BF16)
-    grad_other = swap_seq(grad_other)
-    grad_w_output = contract(ordered(mixed_mine, mixed_theirs, 1), grad_attn, 0, 0)
+    grad_mixed = contract(grad_attn, output_full, 1, 1).astype(BF16)
+    grad_w_output = contract(mixed, grad_attn, 0, 0)
+    grad_other = swap_seq(half_of(grad_mixed, 1 - seq))
     far_f, far_f_other, near_f, near_f_other = after(
         (far[0], far[1], near[0], near[1]), grad_mixed
     )
@@ -1209,48 +1170,65 @@
     ffn_y, ffn_x = far_links(far_ffn)
     near_ffn = over_cores(near_f, near_f_other)
     right, left = line_step(1, far_line)
-    grad_other = after(grad_other, right, left, far_ffn)
-    grad_sorted = to_order(grad_mixed, grad_other)
+    grad_other = after(grad_other, right, left, far_ffn, grad_w_output)
+    grad_sorted = to_order(half_of(grad_mixed, seq), grad_other)
     mid_line = (line_up(right), line_down(left))
     grad_query, grad_keys, grad_values = attend_back(
-        query, keys, values, grad_sorted, start_column, cos, sin
+        query,
+        keys,
+        values,
+        grad_sorted,
+        jnp.concatenate([levels_one, levels_two], axis=0),
+        start_column,
+        cos,
+        sin,
     )
     (grad_query, grad_keys, grad_values), mid_line, ffn_y, ffn_x = lax.optimization_barrier(
         ((grad_query, grad_keys, grad_values), mid_line, ffn_y, ffn_x)
     )
     right, left = line_step(2, mid_line)
-    last_line = (line_up(right), line_down(left))
+    last_first = (line_up(right[:cut]), line_down(left[:cut]))
     first_ffn, second_ffn = near_links(near_ffn, ffn_y, ffn_x)
     first_ffn, second_ffn = swap_seq(first_ffn), swap_y(second_ffn)
     ffn = own_sum(near_ffn, ffn_y, ffn_x, first_ffn, second_ffn)
     output = (middle + BRANCH_SCALE * ffn).astype(BF16)
     grads_qkv = after((grad_query, grad_keys, grad_values), right, left)
     wide = qkv_grad(normed, grads_qkv, grad_gain_two[None, :], shard)
-    grads_late = after(grads_qkv, wide)
+
+
+    def chosen(value, which, axis):
+        return lax.dynamic_index_in_dim(value, which, axis=axis, keepdims=False)
+
+    summed_output = lax.psum_scatter(
+        grad_w_output.astype(BF16), ("seq", "dp"), scatter_dimension=0, tiled=True
+    )
+    kept = chosen(wide, core, 0).astype(F32)
+    kept = kept + swap_core(chosen(wide, 1 - core, 0)).astype(F32)
+    grads_late = after(grads_qkv, kept)
     grad_normed, sent_normed = token_grad(
-        grads_late, gathered, own_places[:, None], other_places[:, None]
-    )
+        grads_late, w_qkv, own_places[:, None], other_places[:, None]
+    )
+    kept, sent_normed = lax.optimization_barrier((kept, sent_normed))
+    right_late, left_late = after((right[cut:], left[cut:]), last_first, sent_normed)
+    last_late = (line_up(right_late), line_down(left_late))
     grad_normed = grad_normed.astype(F32) + swap_seq(sent_normed).astype(F32)
     scale = lax.rsqrt(jnp.mean(inputs * inputs, axis=-1, keepdims=True) + EPSILON)
     unit = inputs * scale
     scaled = grad_normed * gain_one
     inner = jnp.mean(scaled * unit, axis=-1, keepdims=True)
     grad_tokens = grad_middle + scale * (scaled - unit * inner)
-
-    summed_output = lax.psum_scatter(
-        grad_w_output.astype(BF16), ("seq", "dp"), scatter_dimension=0, tiled=True
-    )
-
-    def chosen(value, which, axis):
-        return lax.dynamic_index_in_dim(value, which, axis=axis, keepdims=False)
-
-    kept = chosen(wide, core, 0).astype(F32)
-    kept = kept + swap_core(chosen(wide, 1 - core, 0)).astype(F32)
     next_kept = chosen(kept, row_of, 0)
     next_kept = next_kept + swap_y(chosen(kept, 1 - row_of, 0).astype(BF16)).astype(F32)
-    next_kept, last_line = lax.optimization_barrier((next_kept, last_line))
-    part_grads = (
-        line_partial(*range(LINE)) + last_line[0].astype(F32) + last_line[1].astype(F32)
+    next_kept, last_first, last_late, summed_output = lax.optimization_barrier(
+        (next_kept, last_first, last_late, summed_output)
+    )
+    own_grads = line_partial(*range(LINE))
+    part_grads = jnp.concatenate(
+        [
+            own + up.astype(F32) + down.astype(F32)
+            for own, (up, down) in ((own_grads[:cut], last_first), (own_grads[cut:], last_late))
+        ],
+        axis=0,
     ).astype(BF16)
     same_grads = jnp.where(first_core, part_grads[:, :half], part_grads[:, half : 2 * half])
     cross_grads = jnp.where(first_core, part_grads[:, half : 2 * half], part_grads[:, :half])

time: 769 us -> 740 us (0.962)
  waiting for transfers between devices: 217 us -> 170 us
  starting transfers between devices: 97.1 us -> 113 us
  Pallas kernels: 225 us -> 210 us
  local copies, waits for them, and re-layouts: 35.9 us -> 45.4 us
  matrix products: 82.5 us -> 91.7 us
    ppermute x6 -> x7, waiting for transfers between devices: 53.9 us -> 21.8 us  [line_up(): return lax.ppermute(value, 'dp', [(i, i + 4) for i in range(4 * LINE - 4)])]
    ppermute x15, waiting for transfers between devices: 88.5 us -> 69.9 us  [swap_seq(): return lax.ppermute(value, 'seq', [(0, 1), (1, 0)])]
    ppermute x6 -> x7, starting transfers between devices: 8.23 us -> 20.4 us  [line_down(): return lax.ppermute(value, 'dp', [(i, i - 4) for i in range(4, 4 * LINE)])]
    pallas_call x1 -> x0, Pallas kernels: 9.24 us -> none  [mix(): pl.pallas_call(mix_kernel, grid_spec=pltpu.PrefetchScalarGridSpec(num_sca...]
    dot_general x15 -> x14, matrix products: 82.5 us -> 85.4 us  [contract(): lax.dot_general(left, right, (((left_dim,), (right_dim,)), ((), ())), pre...]
    ppermute x6 -> x7, starting transfers between devices: 30.8 us -> 33.6 us  [line_up(): return lax.ppermute(value, 'dp', [(i, i + 4) for i in range(4 * LINE - 4)])]
  transfers between devices with their start and end apart: 60 -> 63, of which waited for: 19 -> 22; matrix products, arithmetic and copies ran while one was open for 25% -> 29% of each run, Pallas kernels for 22% -> 21%
where the time goes in v9:
time: 740 us; the launch traced here: 734 us
  Pallas kernels  210 us (28%)
  waiting for transfers between devices  170 us (23%)
  starting transfers between devices  113 us (15%)
  matrix products  91.7 us (12%)
  other arithmetic  88.6 us (12%)
  local copies, waits for them, and re-layouts  45.4 us (6%)
  between operations  15.2 us (2%)
    pallas_call x2, Pallas kernels, run_experts(): pl.pallas_call(functools.partial(experts_kernel, tiles, tile // 2), grid_...  109 us
    dot_general x14, matrix products, contract(): lax.dot_general(left, right, (((left_dim,), (right_dim,)), ((), ())), pre...  85.4 us
    ppermute x15, waiting for transfers between devices, swap_seq(): return lax.ppermute(value, 'seq', [(0, 1), (1, 0)])  69.9 us
    pallas_call x1, Pallas kernels, attend_back(): pl.pallas_call(attend_back_kernel, grid=(pairs,), in_specs=[pair_block, w...  40.6 us
    ppermute x27, waiting for transfers between devices, swap_dp(): return lax.ppermute(value, 'dp', [(i, i ^ mask) for i in range(4 * LINE)])  33.8 us
    ppermute x7, starting transfers between devices, line_up(): return lax.ppermute(value, 'dp', [(i, i + 4) for i in range(4 * LINE - 4)])  33.6 us
    ppermute x4, waiting for transfers between devices, both_axes(): return lax.ppermute(value, ('seq', 'dp'), pairs)  32.9 us
    pallas_call x2, Pallas kernels, attend(): pl.pallas_call(functools.partial(attend_kernel, base), grid=(pairs,), in_...  30.3 us
  transfers between devices with their start and end apart: 63, of which 22 were waited for; matrix products, arithmetic and copies ran while one was open for 29% of the time, Pallas kernels for 21%

profile of v9, /device:TPU:1, one launch (start us, length us, event | category | flops | bytes accessed | tf_op | source)
XLA Modules:
  0.0 733.9 jit_solution(12902683781826810386)
XLA Ops:
  12.1 3.3 collective-permute-done.5
  18.4 4.5 collective-permute-start
  23.1 25.7 %collective-permute-done.1 = bf16[1536,256]{1,0:T(8,128)(2,1)} collective-permute-done((bf16[1536,256]{1,0:T(8,128)(2,1)}, bf16[1536,256]{1,0:T(8,128)(2,1)}, u32[]{:S(2)}, u32[]{:S(2)}) %collective-permute-start.1) | collective-permute-done | bytes 786464 | tf_op jit(solution)/shard_map/ppermute | solution.py:982
  50.2 4.6 collective-permute-start.3
  56.1 2.3 collective-permute-start.2
  58.9 3.8 concatenate.95.refs_6_
  66.1 5.8 fusion.23
  71.9 21.8 %collective-permute-done.2 = bf16[512,1536]{1,0:T(8,128)(2,1)} collective-permute-done((bf16[512,1536]{1,0:T(8,128)(2,1)}, bf16[512,1536]{1,0:T(8,128)(2,1)}, u32[]{:S(2)}, u32[]{:S(2)}) %collective-permute-start.2) | collective-permute-done | bytes 1572896 | tf_op jit(solution)/shard_map/ppermute | solution.py:373
  98.8 6.7 add_convert_fusion.2.x_ref
  105.6 16.8 %collective-permute-done.3.refs_18_.refs_14_ = bf16[1536,768]{1,0:T(8,128)(2,1)} collective-permute-done((bf16[1536,768]{1,0:T(8,128)(2,1)S(1)}, bf16[1536,768]{1,0:T(8,128)(2,1)}, u32[]{:S(2)}, u32[]{:S(2)}) %collective-permute-start.3) | collective-permute-done | bytes 2359328 | tf_op jit(solution)/shard_map/ppermute | solution.py:389
  122.4 2.7 collective-permute-done.4.refs_20_.refs_16_
  125.1 3.9 collective-permute-start.10
  133.3 10.4 %project.1 = (bf16[1024,1536]{1,0:T(8,128)(2,1)}, bf16[1024,768]{1,0:T(8,128)(2,1)}, bf16[4,1024,64]{2,1,0:T(8,128)(2,1)}, bf16[4,1024,64]{2,1,0:T(8,128)(2,1)}) custom-call(bf16[1024,1536]{1,0:T(8,128)(2,1)} %add_convert_fusion.2.x_ref, f32[1,1536]{1,0:T(1,128)} %copy.116.gain_ref, bf16[1536,1408]{1,0:T(8,128)(2,1)} %bitcast.77, ...), custom_call_target="tpu_custom_call" | custom-call | flops 251658240 | bytes 3538944 | tf_op jit(solution)/shard_map/project/pallas_call | solution.py:492
  143.7 15.2 %attend.2 = (bf16[1024,384]{1,0:T(8,128)(2,1)}, f32[3,1024,2]{2,1,0:T(8,128)}) custom-call(bf16[1024,768]{1,0:T(8,128)(2,1)} %get-tuple-element.122.q_ref, bf16[4,1024,64]{2,1,0:T(8,128)(2,1)} %get-tuple-element.118.k_ref, bf16[4,1024,64]{2,1,0:T(8,128)(2,1)} %get-tuple-element.119.v_ref, s32[1024,1]{1,0:T(8,128)} %copy.117.start_ref), custom_call_target="tpu_custom_call" | custom-call | flops 113246208 | bytes 3145728 | tf_op jit(solution)/shard_map/attend/pallas_call | solution.py:617
  160.7 2.7 collective-permute-start.8
  163.4 15.1 %attend.3 = (bf16[1024,384]{1,0:T(8,128)(2,1)}, f32[3,1024,2]{2,1,0:T(8,128)}) custom-call(bf16[1024,768]{1,0:T(8,128)(2,1)} %get-tuple-element.122.q_ref, bf16[4,1024,64]{2,1,0:T(8,128)(2,1)} %get-tuple-element.118.k_ref, bf16[4,1024,64]{2,1,0:T(8,128)(2,1)} %get-tuple-element.119.v_ref, s32[1024,1]{1,0:T(8,128)} %copy.117.start_ref), custom_call_target="tpu_custom_call" | custom-call | flops 113246208 | bytes 3145728 | tf_op jit(solution)/shard_map/attend/pallas_call | solution.py:617
  192.4 5.2 collective-permute-start.26
  197.6 11.9 %collective-permute-start.27 = (bf16[1536,768]{1,0:T(8,128)(2,1)}, bf16[1536,768]{1,0:T(8,128)(2,1)}, u32[]{:S(2)}, u32[]{:S(2)}) collective-permute-start(bf16[1536,768]{1,0:T(8,128)(2,1)} %collective-permute-done.11.refs_21_.refs_17_), channel_id=1, source_target_pairs={{4,0},{5,1},{6,2},{7,3},{8,4},{9,5},{10,6},{11,7},{12,8},{13,9},{1... | collective-permute-start | bytes 7077896 | tf_op jit(solution)/shard_map/ppermute | solution.py:393
  209.6 6.2 multiply_reduce_fusion.2
  218.2 31.2 %collective-permute-done.14.refs_0_.refs_1_ = bf16[512,1536]{1,0:T(8,128)(2,1)} collective-permute-done((bf16[512,1536]{1,0:T(8,128)(2,1)S(1)}, bf16[512,1536]{1,0:T(8,128)(2,1)}, u32[]{:S(2)}, u32[]{:S(2)}) %collective-permute-start.14) | collective-permute-done | bytes 1572896 | tf_op jit(solution)/shard_map/ppermute | solution.py:373
  254.7 3.4 collective-permute-start.24
  258.6 8.0 %collective-permute-done.16.refs_2_ = bf16[256,1536]{1,0:T(8,128)(2,1)S(1)} collective-permute-done((bf16[256,1536]{1,0:T(8,128)(2,1)S(1)}, bf16[256,1536]{1,0:T(8,128)(2,1)S(1)}, u32[]{:S(2)}, u32[]{:S(2)}) %collective-permute-start.16) | collective-permute-done | bytes 786464 | tf_op jit(solution)/shard_map/ppermute | solution.py:377
  266.6 4.4 collective-permute-start.23
  276.9 2.6 select_select_fusion
  280.4 54.5 %experts.2 = (bf16[1024,1536]{1,0:T(8,128)(2,1)}, bf16[1024,1536]{1,0:T(8,128)(2,1)}, bf16[1024,1536]{1,0:T(8,128)(2,1)}, bf16[1024,1536]{1,0:T(8,128)(2,1)}, bf...) custom-call(s32[1]{0:T(128)} %bitcast.15.place_ref, ...), custom_call_target="tpu_custom_call" | custom-call | flops 2415919104 | bytes 50331648 | tf_op jit(solution)/shard_map/experts/pallas_call | solution.py:864
  335.8 7.8 %collective-permute-done.28 = bf16[1024,1536]{1,0:T(8,128)(2,1)S(1)} collective-permute-done((bf16[1024,1536]{1,0:T(8,128)(2,1)}, bf16[1024,1536]{1,0:T(8,128)(2,1)S(1)}, u32[]{:S(2)}, u32[]{:S(2)}) %collective-permute-start.28) | collective-permute-done | bytes 3145760 | tf_op jit(solution)/shard_map/ppermute | solution.py:377
  343.6 2.7 add_convert_fusion.1
  352.7 54.8 %experts.3 = (bf16[1024,1536]{1,0:T(8,128)(2,1)}, bf16[1024,1536]{1,0:T(8,128)(2,1)}, bf16[1024,1536]{1,0:T(8,128)(2,1)}, bf16[1024,1536]{1,0:T(8,128)(2,1)}, bf...) custom-call(s32[1]{0:T(128)} %bitcast.15.place_ref, ...), custom_call_target="tpu_custom_call", output_to_operand_aliasing={{4}: (21, {}), {5}: (22, {}), {6}: (23, {}), {7}: (24, {}),... | custom-call | flops 2415919104 | bytes 50331648 | tf_op jit(solution)/shard_map/experts/pallas_call | solution.py:864
  408.5 11.1 %fusion.11 = bf16[1536,512]{1,0:T(8,128)(2,1)S(1)} fusion(bf16[4096,1536]{1,0:T(8,128)(2,1)} %get-tuple-element.163, bf16[4096,512]{1,0:T(8,128)(2,1)} %get-tuple-element.156), kind=kOutput, calls=%fused_computation.40 | convolution fusion | flops 6444023808 | bytes 18350080 | tf_op jit(solution)/shard_map/dot_general | solution.py:575
  420.3 14.1 %convolution_convert_fusion.1 = bf16[1536,1024]{1,0:T(8,128)(2,1)S(1)} fusion(bf16[4096,1536]{1,0:T(8,128)(2,1)S(1)} %copy-done.11, bf16[4096,1024]{1,0:T(8,128)(2,1)S(1)} %copy-done.16), kind=kOutput, calls=%fused_computation.14 | convolution fusion | flops 12886474752 | bytes 24117248 | tf_op jit(solution)/shard_map/dot_general | solution.py:575
  436.4 5.3 collective-permute-start.38
  444.7 2.9 convert_add_fusion.1
  450.3 17.5 %convolution_convert_fusion = bf16[1536,1024]{1,0:T(8,128)(2,1)} fusion(bf16[4096,1536]{1,0:T(8,128)(2,1)S(1)} %copy-done.11, bf16[4096,1024]{1,0:T(8,128)(2,1)} %get-tuple-element.162), kind=kOutput, calls=%fused_computation.13 | convolution fusion | flops 12886474752 | bytes 24117248 | tf_op jit(solution)/shard_map/dot_general | solution.py:575
  473.0 6.6 convolution_convert_fusion.2
  480.8 7.0 fusion.12
  492.4 3.2 add_convert_fusion.6
  495.6 5.4 collective-permute-start.41
  501.0 3.4 add_convert_fusion.5
  520.0 7.1 fusion.48
  527.2 2.2 fusion.20
  529.4 2.3 add_convert_fusion.7.d_ref
  531.7 40.6 %attend_back.1 = (bf16[1024,768]{1,0:T(8,128)(2,1)}, bf16[1024,256]{1,0:T(8,128)(2,1)}, bf16[1024,256]{1,0:T(8,128)(2,1)}) custom-call(bf16[1024,768]{1,0:T(8,128)(2,1)} %get-tuple-element.122.q_ref, bf16[4,1024,64]{2,1,0:T(8,128)(2,1)} %get-tuple-element.118.k_ref, bf16[4,1024,64]{2,1,0:T(8,128)(2,1)} %get-tuple-element.119.v_ref, ...), custom_call_target="tpu_custom_call" | custom-call | flops 566231040 | bytes 6291456 | tf_op jit(solution)/shard_map/attend_back/pallas_call | solution.py:694
  572.3 9.0 %add_convert_fusion.3 = (bf16[1536,768]{1,0:T(8,128)(2,1)}, bf16[1536,768]{1,0:T(8,128)(2,1)}) fusion(bf16[1536,768]{1,0:T(8,128)(2,1)} %collective-permute-done.42, pred[]{:T(512)S(6)} %lt.123, pred[]{:T(512)S(6)} %lt.122, bf16[1536,256]{1,0:T(8,128)(2,1)} %copy-done.8, bf16[1536,512]{1,0:T(8,128)(2,1)} %copy-done.2, bf16[1536,256]{1,0:T(8,128)(2,1)} %copy-done.10, ...), kind=kLoop, calls=%fused_computation.8 | loop fusion | flops 33030144 | bytes 18874372 | tf_op jit(solution)/shard_map/convert_element_type | solution.py:1157
  581.3 8.4 %qkv_grad.1 = bf16[2,2,2,4,48,1408]{5,4,3,2,1,0:T(8,128)(2,1)} custom-call(bf16[1024,1536]{1,0:T(8,128)(2,1)} %get-tuple-element.186.h_ref, bf16[1024,768]{1,0:T(8,128)(2,1)} %get-tuple-element.187.dq_ref, bf16[1024,256]{1,0:T(8,128)(2,1)} %get-tuple-element.188.dk_ref, bf16[1024,256]{1,0:T(8,128)(2,1)} %get-tuple-element.189.dv_ref, ...), custom_call_target="tpu_custom_call" | custom-call | flops 251658240 | bytes 1572864 | tf_op jit(solution)/shard_map/qkv_grad/pallas_call | solution.py:916
  592.9 2.8 convert_add_fusion
  601.4 5.2 collective-permute-start.50
  609.7 8.9 %collective-permute-done.45 = bf16[256,1536]{1,0:T(8,128)(2,1)S(1)} collective-permute-done((bf16[256,1536]{1,0:T(8,128)(2,1)S(1)}, bf16[256,1536]{1,0:T(8,128)(2,1)S(1)}, u32[]{:S(2)}, u32[]{:S(2)}) %collective-permute-start.45) | collective-permute-done | bytes 786464 | tf_op jit(solution)/shard_map/ppermute | solution.py:373
  618.7 3.3 fusion.29
  622.2 2.5 convert_add_fusion.3
  624.6 11.0 %token_grad.1 = (bf16[512,1536]{1,0:T(8,128)(2,1)}, bf16[512,1536]{1,0:T(8,128)(2,1)}) custom-call(bf16[1024,768]{1,0:T(8,128)(2,1)} %get-tuple-element.187.dq_ref, bf16[1024,256]{1,0:T(8,128)(2,1)} %get-tuple-element.188.dk_ref, bf16[1024,256]{1,0:T(8,128)(2,1)} %get-tuple-element.189.dv_ref, bf16[1536,1408]{1,0:T(8,128)(2,1)} %bitcast.78, ...), custom_call_target="tpu_custom_call" | custom-call | flops 251658240 | bytes 1572864 | tf_op jit(solution)/shard_map/token_grad/pallas_call | solution.py:542
  638.8 3.5 collective-permute-done.51
  642.3 3.9 collective-permute-start.52
  647.5 5.2 select_convert_fusion
  652.7 3.2 fusion.27
  656.5 7.1 collective-permute-done.49
  665.2 5.0 collective-permute-done.52
  670.1 4.8 collective-permute-done.53
  675.0 4.4 fusion.16
  681.7 3.1 collective-permute-start.54
  686.7 5.3 collective-permute-start.57
  694.2 9.1 %collective-permute-done.55 = bf16[2,48,1408]{2,1,0:T(8,128)(2,1)S(1)} collective-permute-done((bf16[2,48,1408]{2,1,0:T(8,128)(2,1)S(1)}, bf16[2,48,1408]{2,1,0:T(8,128)(2,1)S(1)}, u32[]{:S(2)}, u32[]{:S(2)}) %collective-permute-start.55) | collective-permute-done | bytes 270368 | tf_op jit(solution)/shard_map/ppermute | solution.py:377
  703.5 3.0 fusion.2
  706.5 4.7 fusion.5
  712.1 6.2 collective-permute-done.57
  (323 shorter events, 132.5 us)
Async XLA Ops:
  7.2 123.1 %all-gather.3.cloned.1.call-start = ((), (), s32[]{:S(2)}) async-start(), calls=%async_computation.1 | async-start | bytes 4595712 | tf_op jit(solution)/shard_map/all_gather | solution.py:1004
  10.0 5.4 collective-permute-start.5
  16.2 193.4 %all-gather.5.cloned.1.call-start = ((), (), s32[]{:S(2)}) async-start(), calls=%async_computation.2 | async-start | bytes 4866048 | tf_op jit(solution)/shard_map/all_gather | solution.py:1005
  16.9 648.2 %reduce-scatter.2.cloned.1.call-start = ((), (), s32[]{:S(2)}) async-start(), calls=%async_computation.3 | async-start | bytes 4866048 | tf_op jit(solution)/shard_map/reduce_scatter | solution.py:1202
  18.4 30.4 %collective-permute-start = (bf16[1536,512]{1,0:T(8,128)(2,1)S(1)}, bf16[1536,512]{1,0:T(8,128)(2,1)S(1)}, u32[]{:S(2)}, u32[]{:S(2)}) collective-permute-start(bf16[1536,512]{1,0:T(8,128)(2,1)S(1)} %pad_maximum_fusion.6), channel_id=1, source_target_pairs={{0,0},{1,16},{2,2},{3,18},{4,4},{5,20},{6,6},{7,22},{8,8},{9,24},{... | collective-permute-start | bytes 4718600 | tf_op jit(solution)/shard_map/ppermute | solution.py:982
  22.9 25.9 %collective-permute-start.1 = (bf16[1536,256]{1,0:T(8,128)(2,1)}, bf16[1536,256]{1,0:T(8,128)(2,1)}, u32[]{:S(2)}, u32[]{:S(2)}) collective-permute-start(bf16[1536,256]{1,0:T(8,128)(2,1)} %get-tuple-element.304), channel_id=1, source_target_pairs={{0,1},{1,17},{2,3},{3,19},{4,5},{5,21},{6,7},{7,23},{8,9},{9,25},{... | collective-permute-start | bytes 2359304 | tf_op jit(solution)/shard_map/ppermute | solution.py:982
  50.2 72.1 %collective-permute-start.3 = (bf16[1536,768]{1,0:T(8,128)(2,1)S(1)}, bf16[1536,768]{1,0:T(8,128)(2,1)}, u32[]{:S(2)}, u32[]{:S(2)}) collective-permute-start(bf16[1536,768]{1,0:T(8,128)(2,1)S(1)} %pad_maximum_fusion.1.refs_19_.refs_15_), channel_id=1, source_target_pairs={{0,4},{1,5},{2,6},{3,7},{4,8},{5,9},{6,10},{7,11},{8,12},{9,13},{1... | collective-permute-start | bytes 7077896 | tf_op jit(solution)/shard_map/ppermute | solution.py:389
  54.8 70.3 %collective-permute-start.4 = (bf16[1536,768]{1,0:T(8,128)(2,1)S(1)}, bf16[1536,768]{1,0:T(8,128)(2,1)}, u32[]{:S(2)}, u32[]{:S(2)}) collective-permute-start(bf16[1536,768]{1,0:T(8,128)(2,1)S(1)} %pad_maximum_fusion.1.refs_19_.refs_15_), channel_id=1, source_target_pairs={{4,0},{5,1},{6,2},{7,3},{8,4},{9,5},{10,6},{11,7},{12,8},{13,9},{1... | collective-permute-start | bytes 7077896 | tf_op jit(solution)/shard_map/ppermute | solution.py:393
  56.1 37.6 %collective-permute-start.2 = (bf16[512,1536]{1,0:T(8,128)(2,1)}, bf16[512,1536]{1,0:T(8,128)(2,1)}, u32[]{:S(2)}, u32[]{:S(2)}) collective-permute-start(bf16[512,1536]{1,0:T(8,128)(2,1)} %param.17), channel_id=1, source_target_pairs={{0,16},{16,0},{1,17},{17,1},{2,18},{18,2},{3,19},{19,3},{4,20},{20... | collective-permute-start | bytes 4718600 | tf_op jit(solution)/shard_map/ppermute | solution.py:373
  62.6 100.8 %collective-permute-start.7 = (bf16[512,1664]{1,0:T(8,128)(2,1)}, bf16[512,1664]{1,0:T(8,128)(2,1)}, u32[]{:S(2)}, u32[]{:S(2)}) collective-permute-start(bf16[512,1664]{1,0:T(8,128)(2,1)} %concatenate.95.refs_6_), channel_id=1, source_target_pairs={{0,2},{1,3},{2,0},{3,1},{4,6},{5,7},{6,4},{7,5},{8,10},{9,11},{10,... | collective-permute-start | bytes 5111816 | tf_op jit(solution)/shard_map/ppermute | solution.py:377
  93.7 69.7 %collective-permute-start.6 = (bf16[512,1664]{1,0:T(8,128)(2,1)}, bf16[512,1664]{1,0:T(8,128)(2,1)}, u32[]{:S(2)}, u32[]{:S(2)}) collective-permute-start(bf16[512,1664]{1,0:T(8,128)(2,1)} %concatenate.95.refs_6_), channel_id=1, source_target_pairs={{0,16},{16,0},{1,17},{17,1},{2,18},{18,2},{3,19},{19,3},{4,20},{20... | collective-permute-start | bytes 5111816 | tf_op jit(solution)/shard_map/ppermute | solution.py:373
  125.1 67.3 %collective-permute-start.10 = (bf16[1536,768]{1,0:T(8,128)(2,1)}, bf16[1536,768]{1,0:T(8,128)(2,1)}, u32[]{:S(2)}, u32[]{:S(2)}) collective-permute-start(bf16[1536,768]{1,0:T(8,128)(2,1)} %collective-permute-done.3.refs_18_.refs_14_), channel_id=1, source_target_pairs={{0,4},{1,5},{2,6},{3,7},{4,8},{5,9},{6,10},{7,11},{8,12},{9,13},{1... | collective-permute-start | bytes 7077896 | tf_op jit(solution)/shard_map/ppermute | solution.py:389
  129.0 63.4 %collective-permute-start.11 = (bf16[1536,768]{1,0:T(8,128)(2,1)}, bf16[1536,768]{1,0:T(8,128)(2,1)}, u32[]{:S(2)}, u32[]{:S(2)}) collective-permute-start(bf16[1536,768]{1,0:T(8,128)(2,1)} %collective-permute-done.4.refs_20_.refs_16_), channel_id=1, source_target_pairs={{4,0},{5,1},{6,2},{7,3},{8,4},{9,5},{10,6},{11,7},{12,8},{13,9},{1... | collective-permute-start | bytes 7077896 | tf_op jit(solution)/shard_map/ppermute | solution.py:393
  160.7 26.3 %collective-permute-start.8 = (bf16[512,384]{0,1:T(8,128)(2,1)S(1)}, bf16[512,384]{0,1:T(8,128)(2,1)S(1)}, u32[]{:S(2)}, u32[]{:S(2)}) collective-permute-start(bf16[512,384]{0,1:T(8,128)(2,1)S(1)} %fusion.34), channel_id=1, source_target_pairs={{0,16},{16,0},{1,17},{17,1},{2,18},{18,2},{3,19},{19,3},{4,20},{20... | collective-permute-start | bytes 1179656 | tf_op jit(solution)/shard_map/ppermute | solution.py:373
  180.4 10.4 %collective-permute-start.9 = (bf16[512,384]{0,1:T(8,128)(2,1)S(1)}, bf16[512,384]{0,1:T(8,128)(2,1)S(1)}, u32[]{:S(2)}, u32[]{:S(2)}) collective-permute-start(bf16[512,384]{0,1:T(8,128)(2,1)S(1)} %fusion.35), channel_id=1, source_target_pairs={{0,16},{16,0},{1,17},{17,1},{2,18},{18,2},{3,19},{19,3},{4,20},{20... | collective-permute-start | bytes 1179656 | tf_op jit(solution)/shard_map/ppermute | solution.py:373
  183.3 32.9 %collective-permute-start.12 = (bf16[256,1664]{1,0:T(8,128)(2,1)}, bf16[256,1664]{1,0:T(8,128)(2,1)}, u32[]{:S(2)}, u32[]{:S(2)}) collective-permute-start(bf16[256,1664]{1,0:T(8,128)(2,1)} %slice.179), channel_id=1, source_target_pairs={{0,2},{1,3},{2,0},{3,1},{4,6},{5,7},{6,4},{7,5},{8,10},{9,11},{10,... | collective-permute-start | bytes 2555912 | tf_op jit(solution)/shard_map/ppermute | solution.py:377
  187.0 29.2 %collective-permute-start.13 = (bf16[256,1664]{1,0:T(8,128)(2,1)}, bf16[256,1664]{1,0:T(8,128)(2,1)}, u32[]{:S(2)}, u32[]{:S(2)}) collective-permute-start(bf16[256,1664]{1,0:T(8,128)(2,1)} %slice.180), channel_id=1, source_target_pairs={{0,16},{16,0},{1,17},{17,1},{2,18},{18,2},{3,19},{19,3},{4,20},{20... | collective-permute-start | bytes 2555912 | tf_op jit(solution)/shard_map/ppermute | solution.py:373
  192.4 65.7 %collective-permute-start.26 = (bf16[1536,768]{1,0:T(8,128)(2,1)}, bf16[1536,768]{1,0:T(8,128)(2,1)}, u32[]{:S(2)}, u32[]{:S(2)}) collective-permute-start(bf16[1536,768]{1,0:T(8,128)(2,1)} %collective-permute-done.10.refs_17_.refs_13_), channel_id=1, source_target_pairs={{0,4},{1,5},{2,6},{3,7},{4,8},{5,9},{6,10},{7,11},{8,12},{9,13},{1... | collective-permute-start | bytes 7077896 | tf_op jit(solution)/shard_map/ppermute | solution.py:389
  197.6 60.4 %collective-permute-start.27 = (bf16[1536,768]{1,0:T(8,128)(2,1)}, bf16[1536,768]{1,0:T(8,128)(2,1)}, u32[]{:S(2)}, u32[]{:S(2)}) collective-permute-start(bf16[1536,768]{1,0:T(8,128)(2,1)} %collective-permute-done.11.refs_21_.refs_17_), channel_id=1, source_target_pairs={{4,0},{5,1},{6,2},{7,3},{8,4},{9,5},{10,6},{11,7},{12,8},{13,9},{1... | collective-permute-start | bytes 7077896 | tf_op jit(solution)/shard_map/ppermute | solution.py:393
  216.2 33.2 %collective-permute-start.14 = (bf16[512,1536]{1,0:T(8,128)(2,1)S(1)}, bf16[512,1536]{1,0:T(8,128)(2,1)}, u32[]{:S(2)}, u32[]{:S(2)}) collective-permute-start(bf16[512,1536]{1,0:T(8,128)(2,1)S(1)} %multiply_convert_fusion.1.refs_0_), channel_id=1, source_target_pairs={{0,16},{16,0},{1,17},{17,1},{2,18},{18,2},{3,19},{19,3},{4,20},{20... | collective-permute-start | bytes 4718600 | tf_op jit(solution)/shard_map/ppermute | solution.py:373
  217.3 34.1 %collective-permute-start.15 = (bf16[512,1536]{1,0:T(8,128)(2,1)S(1)}, bf16[512,1536]{1,0:T(8,128)(2,1)}, u32[]{:S(2)}, u32[]{:S(2)}) collective-permute-start(bf16[512,1536]{1,0:T(8,128)(2,1)S(1)} %multiply_convert_fusion.1.refs_0_), channel_id=1, source_target_pairs={{0,2},{1,3},{2,0},{3,1},{4,6},{5,7},{6,4},{7,5},{8,10},{9,11},{10,... | collective-permute-start | bytes 4718600 | tf_op jit(solution)/shard_map/ppermute | solution.py:377
  250.6 15.9 %collective-permute-start.16 = (bf16[256,1536]{1,0:T(8,128)(2,1)S(1)}, bf16[256,1536]{1,0:T(8,128)(2,1)S(1)}, u32[]{:S(2)}, u32[]{:S(2)}) collective-permute-start(bf16[256,1536]{1,0:T(8,128)(2,1)S(1)} %slice.233), channel_id=1, source_target_pairs={{0,2},{1,3},{2,0},{3,1},{4,6},{5,7},{6,4},{7,5},{8,10},{9,11},{10,... | collective-permute-start | bytes 2359304 | tf_op jit(solution)/shard_map/ppermute | solution.py:377
  252.6 18.4 %collective-permute-start.17 = (bf16[256,1536]{1,0:T(8,128)(2,1)S(1)}, bf16[256,1536]{1,0:T(8,128)(2,1)S(1)}, u32[]{:S(2)}, u32[]{:S(2)}) collective-permute-start(bf16[256,1536]{1,0:T(8,128)(2,1)S(1)} %slice.234), channel_id=1, source_target_pairs={{0,16},{16,0},{1,17},{17,1},{2,18},{18,2},{3,19},{19,3},{4,20},{20... | collective-permute-start | bytes 2359304 | tf_op jit(solution)/shard_map/ppermute | solution.py:373
  254.7 18.5 %collective-permute-start.24 = (bf16[256,1664]{1,0:T(8,128)(2,1)}, bf16[256,1664]{1,0:T(8,128)(2,1)}, u32[]{:S(2)}, u32[]{:S(2)}) collective-permute-start(bf16[256,1664]{1,0:T(8,128)(2,1)} %collective-permute-done.12.refs_10_), channel_id=1, source_target_pairs={{0,1},{1,0},{2,3},{3,2},{4,5},{5,4},{6,7},{7,6},{8,9},{9,8},{10,11... | collective-permute-start | bytes 2555912 | tf_op jit(solution)/shard_map/ppermute | solution.py:377
  258.1 18.1 %collective-permute-start.18 = (bf16[512,1536]{1,0:T(8,128)(2,1)}, bf16[512,1536]{1,0:T(8,128)(2,1)}, u32[]{:S(2)}, u32[]{:S(2)}) collective-permute-start(bf16[512,1536]{1,0:T(8,128)(2,1)} %collective-permute-done.14.refs_0_.refs_1_), channel_id=1, source_target_pairs={{0,1},{1,0},{2,3},{3,2},{4,5},{5,4},{6,7},{7,6},{8,9},{9,8},{10,11... | collective-permute-start | bytes 4718600 | tf_op jit(solution)/shard_map/ppermute | solution.py:377
  258.1 22.3 %collective-permute-start.22 = (bf16[512,1664]{1,0:T(8,128)(2,1)}, bf16[512,1664]{1,0:T(8,128)(2,1)}, u32[]{:S(2)}, u32[]{:S(2)}) collective-permute-start(bf16[512,1664]{1,0:T(8,128)(2,1)} %collective-permute-done.6.refs_8_.refs_7_), channel_id=1, source_target_pairs={{0,1},{1,0},{2,3},{3,2},{4,5},{5,4},{6,7},{7,6},{8,9},{9,8},{10,11... | collective-permute-start | bytes 5111816 | tf_op jit(solution)/shard_map/ppermute | solution.py:377
  266.6 13.8 %collective-permute-start.23 = (bf16[512,1664]{1,0:T(8,128)(2,1)}, bf16[512,1664]{1,0:T(8,128)(2,1)}, u32[]{:S(2)}, u32[]{:S(2)}) collective-permute-start(bf16[512,1664]{1,0:T(8,128)(2,1)} %collective-permute-done.7.refs_9_.refs_8_), channel_id=1, source_target_pairs={{0,1},{1,0},{2,3},{3,2},{4,5},{5,4},{6,7},{7,6},{8,9},{9,8},{10,11... | collective-permute-start | bytes 5111816 | tf_op jit(solution)/shard_map/ppermute | solution.py:377
  271.0 4.8 collective-permute-start.25
  273.2 7.2 collective-permute-start.19
  275.8 4.6 collective-permute-start.20
  276.1 4.2 collective-permute-start.21
  334.8 8.8 %collective-permute-start.28 = (bf16[1024,1536]{1,0:T(8,128)(2,1)}, bf16[1024,1536]{1,0:T(8,128)(2,1)S(1)}, u32[]{:S(2)}, u32[]{:S(2)}) collective-permute-start(bf16[1024,1536]{1,0:T(8,128)(2,1)} %get-tuple-element.139), channel_id=1, source_target_pairs={{0,1},{1,0},{2,3},{3,2},{4,5},{5,4},{6,7},{7,6},{8,9},{9,8},{10,11... | collective-permute-start | bytes 9437192 | tf_op jit(solution)/shard_map/ppermute | solution.py:377
  335.2 17.5 %collective-permute-start.29 = (bf16[512,1536]{1,0:T(8,128)(2,1)}, bf16[512,1536]{1,0:T(8,128)(2,1)}, u32[]{:S(2)}, u32[]{:S(2)}) collective-permute-start(bf16[512,1536]{1,0:T(8,128)(2,1)} %copy-done.21), channel_id=1, source_target_pairs={{0,1},{1,0},{2,3},{3,2},{4,5},{5,4},{6,7},{7,6},{8,9},{9,8},{10,11... | collective-permute-start | bytes 4718600 | tf_op jit(solution)/shard_map/ppermute | solution.py:377
  335.4 17.3 %collective-permute-start.30 = (bf16[512,1664]{1,0:T(8,128)(2,1)}, bf16[512,1664]{1,0:T(8,128)(2,1)}, u32[]{:S(2)}, u32[]{:S(2)}) collective-permute-start(bf16[512,1664]{1,0:T(8,128)(2,1)} %concatenate.95.refs_6_), channel_id=1, source_target_pairs={{0,1},{1,0},{2,3},{3,2},{4,5},{5,4},{6,7},{7,6},{8,9},{9,8},{10,11... | collective-permute-start | bytes 5111816 | tf_op jit(solution)/shard_map/ppermute | solution.py:377
  348.2 60.4 %collective-permute-start.31 = (bf16[512,1536]{1,0:T(8,128)(2,1)}, bf16[512,1536]{1,0:T(8,128)(2,1)}, u32[]{:S(2)}, u32[]{:S(2)}) collective-permute-start(bf16[512,1536]{1,0:T(8,128)(2,1)} %get-tuple-element.285), channel_id=1, source_target_pairs={{0,2},{1,3},{2,0},{3,1},{4,6},{5,7},{6,4},{7,5},{8,10},{9,11},{10,... | collective-permute-start | bytes 4718600 | tf_op jit(solution)/shard_map/ppermute | solution.py:377
  349.3 59.2 %collective-permute-start.32 = (bf16[512,1536]{1,0:T(8,128)(2,1)}, bf16[512,1536]{1,0:T(8,128)(2,1)}, u32[]{:S(2)}, u32[]{:S(2)}) collective-permute-start(bf16[512,1536]{1,0:T(8,128)(2,1)} %get-tuple-element.284), channel_id=1, source_target_pairs={{0,16},{16,0},{1,17},{17,1},{2,18},{18,2},{3,19},{19,3},{4,20},{20... | collective-permute-start | bytes 4718600 | tf_op jit(solution)/shard_map/ppermute | solution.py:373
  407.5 37.2 %collective-permute-start.33 = (bf16[1024,1536]{1,0:T(8,128)(2,1)}, bf16[1024,1536]{1,0:T(8,128)(2,1)}, u32[]{:S(2)}, u32[]{:S(2)}) collective-permute-start(bf16[1024,1536]{1,0:T(8,128)(2,1)} %get-tuple-element.158), channel_id=1, source_target_pairs={{0,1},{1,0},{2,3},{3,2},{4,5},{5,4},{6,7},{7,6},{8,9},{9,8},{10,11... | collective-permute-start | bytes 9437192 | tf_op jit(solution)/shard_map/ppermute | solution.py:377
  419.7 81.2 %copy-start.8 = (bf16[1536,256]{1,0:T(8,128)(2,1)}, bf16[1536,256]{1,0:T(8,128)(2,1)S(1)}, u32[]{:S(2)}) copy-start(bf16[1536,256]{1,0:T(8,128)(2,1)S(1)} %get-tuple-element.300) | copy-start | bytes 2359300
  436.4 56.0 %collective-permute-start.38 = (bf16[1536,768]{1,0:T(8,128)(2,1)}, bf16[1536,768]{1,0:T(8,128)(2,1)}, u32[]{:S(2)}, u32[]{:S(2)}) collective-permute-start(bf16[1536,768]{1,0:T(8,128)(2,1)} %pad_maximum_fusion.3), channel_id=1, source_target_pairs={{0,4},{1,5},{2,6},{3,7},{4,8},{5,9},{6,10},{7,11},{8,12},{9,13},{1... | collective-permute-start | bytes 7077896 | tf_op jit(solution)/shard_map/ppermute | solution.py:389
  443.3 57.7 %collective-permute-start.39 = (bf16[1536,768]{1,0:T(8,128)(2,1)}, bf16[1536,768]{1,0:T(8,128)(2,1)}, u32[]{:S(2)}, u32[]{:S(2)}) collective-permute-start(bf16[1536,768]{1,0:T(8,128)(2,1)} %pad_maximum_fusion.2), channel_id=1, source_target_pairs={{4,0},{5,1},{6,2},{7,3},{8,4},{9,5},{10,6},{11,7},{12,8},{13,9},{1... | collective-permute-start | bytes 7077896 | tf_op jit(solution)/shard_map/ppermute | solution.py:393
  449.5 19.0 %collective-permute-start.34 = (bf16[256,1536]{1,0:T(8,128)(2,1)S(1)}, bf16[256,1536]{1,0:T(8,128)(2,1)S(1)}, u32[]{:S(2)}, u32[]{:S(2)}) collective-permute-start(bf16[256,1536]{1,0:T(8,128)(2,1)S(1)} %get-tuple-element.272), channel_id=1, source_target_pairs={{0,16},{16,0},{1,17},{17,1},{2,18},{18,2},{3,19},{19,3},{4,20},{20... | collective-permute-start | bytes 2359304 | tf_op jit(solution)/shard_map/ppermute | solution.py:373
  449.6 19.0 %collective-permute-start.35 = (bf16[256,1536]{1,0:T(8,128)(2,1)S(1)}, bf16[256,1536]{1,0:T(8,128)(2,1)S(1)}, u32[]{:S(2)}, u32[]{:S(2)}) collective-permute-start(bf16[256,1536]{1,0:T(8,128)(2,1)S(1)} %get-tuple-element.273), channel_id=1, source_target_pairs={{0,2},{1,3},{2,0},{3,1},{4,6},{5,7},{6,4},{7,5},{8,10},{9,11},{10,... | collective-permute-start | bytes 2359304 | tf_op jit(solution)/shard_map/ppermute | solution.py:377
  479.7 26.4 %collective-permute-start.40 = (bf16[1024,1536]{1,0:T(8,128)(2,1)}, bf16[1024,1536]{1,0:T(8,128)(2,1)S(1)}, u32[]{:S(2)}, u32[]{:S(2)}) collective-permute-start(bf16[1024,1536]{1,0:T(8,128)(2,1)} %get-tuple-element.169), channel_id=1, source_target_pairs={{0,1},{1,0},{2,3},{3,2},{4,5},{5,4},{6,7},{7,6},{8,9},{9,8},{10,11... | collective-permute-start | bytes 9437192 | tf_op jit(solution)/shard_map/ppermute | solution.py:377
  490.0 102.9 %collective-permute-start.36 = (bf16[1024,1536]{1,0:T(8,128)(2,1)}, bf16[1024,1536]{1,0:T(8,128)(2,1)}, u32[]{:S(2)}, u32[]{:S(2)}) collective-permute-start(bf16[1024,1536]{1,0:T(8,128)(2,1)} %get-tuple-element.167), channel_id=1, source_target_pairs={{0,1},{1,0},{2,3},{3,2},{4,5},{5,4},{6,7},{7,6},{8,9},{9,8},{10,11... | collective-permute-start | bytes 9437192 | tf_op jit(solution)/shard_map/ppermute | solution.py:377
  490.9 19.2 %collective-permute-start.37 = (bf16[512,768]{1,0:T(8,128)(2,1)S(1)}, bf16[512,768]{1,0:T(8,128)(2,1)S(1)}, u32[]{:S(2)}, u32[]{:S(2)}) collective-permute-start(bf16[512,768]{1,0:T(8,128)(2,1)S(1)} %constant_dynamic-slice_fusion), channel_id=1, source_target_pairs={{0,16},{16,0},{1,17},{17,1},{2,18},{18,2},{3,19},{19,3},{4,20},{20... | collective-permute-start | bytes 2359304 | tf_op jit(solution)/shard_map/ppermute | solution.py:373
  495.6 76.7 %collective-permute-start.41 = (bf16[1536,768]{1,0:T(8,128)(2,1)}, bf16[1536,768]{1,0:T(8,128)(2,1)}, u32[]{:S(2)}, u32[]{:S(2)}) collective-permute-start(bf16[1536,768]{1,0:T(8,128)(2,1)} %add_convert_fusion.6), channel_id=1, source_target_pairs={{0,4},{1,5},{2,6},{3,7},{4,8},{5,9},{6,10},{7,11},{8,12},{9,13},{1... | collective-permute-start | bytes 7077896 | tf_op jit(solution)/shard_map/ppermute | solution.py:389
  504.4 67.9 %collective-permute-start.42 = (bf16[1536,768]{1,0:T(8,128)(2,1)}, bf16[1536,768]{1,0:T(8,128)(2,1)}, u32[]{:S(2)}, u32[]{:S(2)}) collective-permute-start(bf16[1536,768]{1,0:T(8,128)(2,1)} %add_convert_fusion.5), channel_id=1, source_target_pairs={{4,0},{5,1},{6,2},{7,3},{8,4},{9,5},{10,6},{11,7},{12,8},{13,9},{1... | collective-permute-start | bytes 7077896 | tf_op jit(solution)/shard_map/ppermute | solution.py:393
  508.9 63.4 %collective-permute-start.43 = (bf16[512,1536]{1,0:T(8,128)(2,1)}, bf16[512,1536]{1,0:T(8,128)(2,1)}, u32[]{:S(2)}, u32[]{:S(2)}) collective-permute-start(bf16[512,1536]{1,0:T(8,128)(2,1)} %get-tuple-element.279), channel_id=1, source_target_pairs={{0,2},{1,3},{2,0},{3,1},{4,6},{5,7},{6,4},{7,5},{8,10},{9,11},{10,... | collective-permute-start | bytes 4718600 | tf_op jit(solution)/shard_map/ppermute | solution.py:377
  510.1 62.2 %collective-permute-start.44 = (bf16[512,1536]{1,0:T(8,128)(2,1)}, bf16[512,1536]{1,0:T(8,128)(2,1)}, u32[]{:S(2)}, u32[]{:S(2)}) collective-permute-start(bf16[512,1536]{1,0:T(8,128)(2,1)} %get-tuple-element.278), channel_id=1, source_target_pairs={{0,16},{16,0},{1,17},{17,1},{2,18},{18,2},{3,19},{19,3},{4,20},{20... | collective-permute-start | bytes 4718600 | tf_op jit(solution)/shard_map/ppermute | solution.py:373
  591.6 30.5 %collective-permute-start.47 = (bf16[2,2,4,48,1408]{4,3,2,1,0:T(8,128)(2,1)S(1)}, bf16[2,2,4,48,1408]{4,3,2,1,0:T(8,128)(2,1)S(1)}, u32[]{:S(2)}, u32[]{:S(2)}) collective-permute-start(bf16[2,2,4,48,1408]{4,3,2,1,0:T(8,128)(2,1)S(1)} %dynamic-slice_bitcast_fusion), channel_id=1, source_target_pairs={{0,1},{1,0},{2,3},{3,2},{4,5},{5,4},{6,7},{7,6},{8,9},{9,8},{10,11... | collective-permute-start | bytes 6488072 | tf_op jit(solution)/shard_map/ppermute | solution.py:377
  597.8 20.8 %collective-permute-start.45 = (bf16[256,1536]{1,0:T(8,128)(2,1)S(1)}, bf16[256,1536]{1,0:T(8,128)(2,1)S(1)}, u32[]{:S(2)}, u32[]{:S(2)}) collective-permute-start(bf16[256,1536]{1,0:T(8,128)(2,1)S(1)} %fusion.28), channel_id=1, source_target_pairs={{0,16},{16,0},{1,17},{17,1},{2,18},{18,2},{3,19},{19,3},{4,20},{20... | collective-permute-start | bytes 2359304 | tf_op jit(solution)/shard_map/ppermute | solution.py:373
  601.4 37.4 %collective-permute-start.50 = (bf16[768,768]{1,0:T(8,128)(2,1)}, bf16[768,768]{1,0:T(8,128)(2,1)}, u32[]{:S(2)}, u32[]{:S(2)}) collective-permute-start(bf16[768,768]{1,0:T(8,128)(2,1)} %get-tuple-element.293), channel_id=1, source_target_pairs={{0,4},{1,5},{2,6},{3,7},{4,8},{5,9},{6,10},{7,11},{8,12},{9,13},{1... | collective-permute-start | bytes 3538952 | tf_op jit(solution)/shard_map/ppermute | solution.py:389
  608.2 34.1 %collective-permute-start.51 = (bf16[768,768]{1,0:T(8,128)(2,1)}, bf16[768,768]{1,0:T(8,128)(2,1)}, u32[]{:S(2)}, u32[]{:S(2)}) collective-permute-start(bf16[768,768]{1,0:T(8,128)(2,1)} %get-tuple-element.291), channel_id=1, source_target_pairs={{4,0},{5,1},{6,2},{7,3},{8,4},{9,5},{10,6},{11,7},{12,8},{13,9},{1... | collective-permute-start | bytes 3538952 | tf_op jit(solution)/shard_map/ppermute | solution.py:393
  621.9 30.8 %collective-permute-start.46 = (bf16[256,1536]{1,0:T(8,128)(2,1)}, bf16[256,1536]{1,0:T(8,128)(2,1)}, u32[]{:S(2)}, u32[]{:S(2)}) collective-permute-start(bf16[256,1536]{1,0:T(8,128)(2,1)} %get-tuple-element.269), channel_id=1, source_target_pairs={{0,2},{1,3},{2,0},{3,1},{4,6},{5,7},{6,4},{7,5},{8,10},{9,11},{10,... | collective-permute-start | bytes 2359304 | tf_op jit(solution)/shard_map/ppermute | solution.py:377
  637.5 26.1 %collective-permute-start.49 = (bf16[2,4,48,1408]{3,2,1,0:T(8,128)(2,1)S(1)}, bf16[2,4,48,1408]{3,2,1,0:T(8,128)(2,1)S(1)}, u32[]{:S(2)}, u32[]{:S(2)}) collective-permute-start(bf16[2,4,48,1408]{3,2,1,0:T(8,128)(2,1)S(1)} %fusion.36), channel_id=1, source_target_pairs={{0,2},{1,3},{2,0},{3,1},{4,6},{5,7},{6,4},{7,5},{8,10},{9,11},{10,... | collective-permute-start | bytes 3244040 | tf_op jit(solution)/shard_map/ppermute | solution.py:377
  642.3 27.8 %collective-permute-start.52 = (bf16[768,768]{1,0:T(8,128)(2,1)}, bf16[768,768]{1,0:T(8,128)(2,1)}, u32[]{:S(2)}, u32[]{:S(2)}) collective-permute-start(bf16[768,768]{1,0:T(8,128)(2,1)} %get-tuple-element.194), channel_id=1, source_target_pairs={{0,4},{1,5},{2,6},{3,7},{4,8},{5,9},{6,10},{7,11},{8,12},{9,13},{1... | collective-permute-start | bytes 3538952 | tf_op jit(solution)/shard_map/ppermute | solution.py:389
  646.2 28.8 %collective-permute-start.53 = (bf16[768,768]{1,0:T(8,128)(2,1)}, bf16[768,768]{1,0:T(8,128)(2,1)}, u32[]{:S(2)}, u32[]{:S(2)}) collective-permute-start(bf16[768,768]{1,0:T(8,128)(2,1)} %get-tuple-element.195), channel_id=1, source_target_pairs={{4,0},{5,1},{6,2},{7,3},{8,4},{9,5},{10,6},{11,7},{12,8},{13,9},{1... | collective-permute-start | bytes 3538952 | tf_op jit(solution)/shard_map/ppermute | solution.py:393
  656.0 47.5 %collective-permute-start.48 = (bf16[512,1536]{1,0:T(8,128)(2,1)}, bf16[512,1536]{1,0:T(8,128)(2,1)}, u32[]{:S(2)}, u32[]{:S(2)}) collective-permute-start(bf16[512,1536]{1,0:T(8,128)(2,1)} %get-tuple-element.192), channel_id=1, source_target_pairs={{0,16},{16,0},{1,17},{17,1},{2,18},{18,2},{3,19},{19,3},{4,20},{20... | collective-permute-start | bytes 4718600 | tf_op jit(solution)/shard_map/ppermute | solution.py:373
  681.0 11.8 %collective-permute-start.56 = (bf16[2,48,1408]{2,1,0:T(8,128)(2,1)S(1)}, bf16[2,48,1408]{2,1,0:T(8,128)(2,1)S(1)}, u32[]{:S(2)}, u32[]{:S(2)}) collective-permute-start(bf16[2,48,1408]{2,1,0:T(8,128)(2,1)S(1)} %fusion.51), channel_id=1, source_target_pairs={{0,12},{1,13},{2,14},{3,15},{4,8},{5,9},{6,10},{7,11},{8,4},{9,5},... | collective-permute-start | bytes 811016 | tf_op jit(solution)/shard_map/ppermute | solution.py:377
  681.2 22.1 %collective-permute-start.55 = (bf16[2,48,1408]{2,1,0:T(8,128)(2,1)S(1)}, bf16[2,48,1408]{2,1,0:T(8,128)(2,1)S(1)}, u32[]{:S(2)}, u32[]{:S(2)}) collective-permute-start(bf16[2,48,1408]{2,1,0:T(8,128)(2,1)S(1)} %get-tuple-element.307), channel_id=1, source_target_pairs={{0,8},{1,9},{2,10},{3,11},{4,12},{5,13},{6,14},{7,15},{8,0},{9,1},... | collective-permute-start | bytes 811016 | tf_op jit(solution)/shard_map/ppermute | solution.py:377
  681.7 21.6 %collective-permute-start.54 = (bf16[2,48,1408]{2,1,0:T(8,128)(2,1)S(1)}, bf16[2,48,1408]{2,1,0:T(8,128)(2,1)S(1)}, u32[]{:S(2)}, u32[]{:S(2)}) collective-permute-start(bf16[2,48,1408]{2,1,0:T(8,128)(2,1)S(1)} %get-tuple-element.306), channel_id=1, source_target_pairs={{0,4},{1,5},{2,6},{3,7},{4,0},{5,1},{6,2},{7,3},{8,12},{9,13},{10,... | collective-permute-start | bytes 811016 | tf_op jit(solution)/shard_map/ppermute | solution.py:377
  686.7 31.6 %collective-permute-start.57 = (bf16[1536,512]{1,0:T(8,128)(2,1)S(1)}, bf16[1536,512]{1,0:T(8,128)(2,1)S(1)}, u32[]{:S(2)}, u32[]{:S(2)}) collective-permute-start(bf16[1536,512]{1,0:T(8,128)(2,1)S(1)} %fusion.25), channel_id=1, source_target_pairs={{0,0},{1,16},{2,2},{3,18},{4,4},{5,20},{6,6},{7,22},{8,8},{9,24},{... | collective-permute-start | bytes 4718600 | tf_op jit(solution)/shard_map/ppermute | solution.py:982
  692.8 19.3 %collective-permute-start.58 = (bf16[1536,256]{1,0:T(8,128)(2,1)S(1)}, bf16[1536,256]{1,0:T(8,128)(2,1)S(1)}, u32[]{:S(2)}, u32[]{:S(2)}) collective-permute-start(bf16[1536,256]{1,0:T(8,128)(2,1)S(1)} %get-tuple-element.203), channel_id=1, source_target_pairs={{1,0},{17,1},{3,2},{19,3},{5,4},{21,5},{7,6},{23,7},{9,8},{25,9},{... | collective-permute-start | bytes 2359304 | tf_op jit(solution)/shard_map/ppermute | solution.py:982
  718.3 5.2 collective-permute-start.59
  (57 other events, 828.2 us)
Sparse Core Ops, SparseCore 0:
  16.3 56.5 all-gather.2
  75.8 81.7 all-gather.4
  527.3 106.9 reduce-scatter.1

commit v10 on v9

--- a/solution.py
+++ b/solution.py
@@ -1140,19 +1140,19 @@
     near_back = after(near_back, *inner_grads)
     grad_normed_ffn = own_sum(near_back, back_y, back_x, first, second)
 
-    def line_partial(first, *rest):
-        value = grads_of[first]
+    def line_partial(first, *rest, rows=slice(None)):
+        value = grads_of[first][rows]
         for where, expert in enumerate(rest):
-            value = jnp.where(line > where, grads_of[expert], value)
+            value = jnp.where(line > where, grads_of[expert][rows], value)
         return value.astype(F32)
 
-    def line_step(step, arrived):
-        up, down = arrived
+    def line_step(step, arrived, rows=slice(None)):
+        up, down = arrived[0][rows], arrived[1][rows]
         last = LINE - 1
-        right = line_partial(*range(last - step, LINE)) + up.astype(F32)
-        left = grads_of[step]
+        right = line_partial(*range(last - step, LINE), rows=rows) + up.astype(F32)
+        left = grads_of[step][rows]
         for where in range(step):
-            left = jnp.where(line < last - where, grads_of[step - 1 - where], left)
+            left = jnp.where(line < last - where, grads_of[step - 1 - where][rows], left)
         left = left.astype(F32) + down.astype(F32)
         return right.astype(BF16), left.astype(BF16)
 
@@ -1186,8 +1186,8 @@
     (grad_query, grad_keys, grad_values), mid_line, ffn_y, ffn_x = lax.optimization_barrier(
         ((grad_query, grad_keys, grad_values), mid_line, ffn_y, ffn_x)
     )
-    right, left = line_step(2, mid_line)
-    last_first = (line_up(right[:cut]), line_down(left[:cut]))
+    right, left = line_step(2, mid_line, slice(0, cut))
+    last_first = (line_up(right), line_down(left))
     first_ffn, second_ffn = near_links(near_ffn, ffn_y, ffn_x)
     first_ffn, second_ffn = swap_seq(first_ffn), swap_y(second_ffn)
     ffn = own_sum(near_ffn, ffn_y, ffn_x, first_ffn, second_ffn)
@@ -1209,19 +1209,22 @@
         grads_late, w_qkv, own_places[:, None], other_places[:, None]
     )
     kept, sent_normed = lax.optimization_barrier((kept, sent_normed))
-    right_late, left_late = after((right[cut:], left[cut:]), last_first, sent_normed)
+    mid_late, sent_normed = lax.optimization_barrier((mid_line, sent_normed))
+    right_late, left_late = line_step(2, mid_late, slice(cut, width))
+    right_late, left_late = after((right_late, left_late), last_first)
     last_late = (line_up(right_late), line_down(left_late))
-    grad_normed = grad_normed.astype(F32) + swap_seq(sent_normed).astype(F32)
+    came_normed = swap_seq(sent_normed)
+    next_kept = chosen(kept, row_of, 0)
+    next_kept = next_kept + swap_y(chosen(kept, 1 - row_of, 0).astype(BF16)).astype(F32)
+    next_kept, last_first, last_late, summed_output, came_normed = lax.optimization_barrier(
+        (next_kept, last_first, last_late, summed_output, came_normed)
+    )
+    grad_normed = grad_normed.astype(F32) + came_normed.astype(F32)
     scale = lax.rsqrt(jnp.mean(inputs * inputs, axis=-1, keepdims=True) + EPSILON)
     unit = inputs * scale
     scaled = grad_normed * gain_one
     inner = jnp.mean(scaled * unit, axis=-1, keepdims=True)
     grad_tokens = grad_middle + scale * (scaled - unit * inner)
-    next_kept = chosen(kept, row_of, 0)
-    next_kept = next_kept + swap_y(chosen(kept, 1 - row_of, 0).astype(BF16)).astype(F32)
-    next_kept, last_first, last_late, summed_output = lax.optimization_barrier(
-        (next_kept, last_first, last_late, summed_output)
-    )
     own_grads = line_partial(*range(LINE))
     part_grads = jnp.concatenate(
         [

time: 740 us -> 747 us (level)
  waiting for transfers between devices: 170 us -> 190 us
  starting transfers between devices: 113 us -> 97.7 us
    ppermute x15, waiting for transfers between devices: 69.9 us -> 85 us  [swap_seq(): return lax.ppermute(value, 'seq', [(0, 1), (1, 0)])]
    ppermute x7, starting transfers between devices: 20.4 us -> 9.1 us  [line_down(): return lax.ppermute(value, 'dp', [(i, i - 4) for i in range(4, 4 * LINE)])]
    convert_element_type x3 -> x4, other arithmetic: 15.6 us -> 16.1 us  [line_step(): return (right.astype(BF16), left.astype(BF16))]
  transfers between devices with their start and end apart: 63 -> 63, of which waited for: 22 -> 25; matrix products, arithmetic and copies ran while one was open for 29% -> 27% of each run, Pallas kernels for 21% -> 21%
where the time goes in v10:
time: 747 us; the launch traced here: 738 us
  Pallas kernels  210 us (28%)
  waiting for transfers between devices  190 us (25%)
  starting transfers between devices  97.7 us (13%)
  matrix products  94.4 us (13%)
  other arithmetic  86.5 us (12%)
  local copies, waits for them, and re-layouts  43.7 us (6%)
  between operations  15.3 us (2%)
    pallas_call x2, Pallas kernels, run_experts(): pl.pallas_call(functools.partial(experts_kernel, tiles, tile // 2), grid_...  109 us
    dot_general x14, matrix products, contract(): lax.dot_general(left, right, (((left_dim,), (right_dim,)), ((), ())), pre...  88.5 us
    ppermute x15, waiting for transfers between devices, swap_seq(): return lax.ppermute(value, 'seq', [(0, 1), (1, 0)])  85 us
    pallas_call x1, Pallas kernels, attend_back(): pl.pallas_call(attend_back_kernel, grid=(pairs,), in_specs=[pair_block, w...  40.6 us
    ppermute x27, waiting for transfers between devices, swap_dp(): return lax.ppermute(value, 'dp', [(i, i ^ mask) for i in range(4 * LINE)])  36 us
    ppermute x7, starting transfers between devices, line_up(): return lax.ppermute(value, 'dp', [(i, i + 4) for i in range(4 * LINE - 4)])  35 us
    ppermute x4, waiting for transfers between devices, both_axes(): return lax.ppermute(value, ('seq', 'dp'), pairs)  34.2 us
    pallas_call x2, Pallas kernels, attend(): pl.pallas_call(functools.partial(attend_kernel, base), grid=(pairs,), in_...  30.3 us
  transfers between devices with their start and end apart: 63, of which 25 were waited for; matrix products, arithmetic and copies ran while one was open for 27% of the time, Pallas kernels for 21%

profile of v10, /device:TPU:1, one launch (start us, length us, event | category | flops | bytes accessed | tf_op | source)
XLA Modules:
  0.0 737.6 jit_solution(13890350829911250849)
XLA Ops:
  12.1 3.3 collective-permute-done.5
  18.4 4.5 collective-permute-start
  23.1 25.7 %collective-permute-done.1 = bf16[1536,256]{1,0:T(8,128)(2,1)} collective-permute-done((bf16[1536,256]{1,0:T(8,128)(2,1)}, bf16[1536,256]{1,0:T(8,128)(2,1)}, u32[]{:S(2)}, u32[]{:S(2)}) %collective-permute-start.1) | collective-permute-done | bytes 786464 | tf_op jit(solution)/shard_map/ppermute | solution.py:982
  50.2 4.7 collective-permute-start.3
  58.9 3.8 concatenate.95.refs_6_
  66.2 5.8 fusion.23
  72.0 21.8 %collective-permute-done.2 = bf16[512,1536]{1,0:T(8,128)(2,1)} collective-permute-done((bf16[512,1536]{1,0:T(8,128)(2,1)}, bf16[512,1536]{1,0:T(8,128)(2,1)}, u32[]{:S(2)}, u32[]{:S(2)}) %collective-permute-start.2) | collective-permute-done | bytes 1572896 | tf_op jit(solution)/shard_map/ppermute | solution.py:373
  98.9 6.7 add_convert_fusion.2.x_ref
  105.6 16.7 %collective-permute-done.3.refs_18_.refs_14_ = bf16[1536,768]{1,0:T(8,128)(2,1)} collective-permute-done((bf16[1536,768]{1,0:T(8,128)(2,1)S(1)}, bf16[1536,768]{1,0:T(8,128)(2,1)}, u32[]{:S(2)}, u32[]{:S(2)}) %collective-permute-start.3) | collective-permute-done | bytes 2359328 | tf_op jit(solution)/shard_map/ppermute | solution.py:389
  122.4 2.7 collective-permute-done.4.refs_20_.refs_16_
  125.0 4.0 collective-permute-start.10
  133.3 10.6 %project.1 = (bf16[1024,1536]{1,0:T(8,128)(2,1)}, bf16[1024,768]{1,0:T(8,128)(2,1)}, bf16[4,1024,64]{2,1,0:T(8,128)(2,1)}, bf16[4,1024,64]{2,1,0:T(8,128)(2,1)}) custom-call(bf16[1024,1536]{1,0:T(8,128)(2,1)} %add_convert_fusion.2.x_ref, f32[1,1536]{1,0:T(1,128)} %copy.116.gain_ref, bf16[1536,1408]{1,0:T(8,128)(2,1)} %bitcast.77, ...), custom_call_target="tpu_custom_call" | custom-call | flops 251658240 | bytes 3538944 | tf_op jit(solution)/shard_map/project/pallas_call | solution.py:492
  144.0 15.1 %attend.2 = (bf16[1024,384]{1,0:T(8,128)(2,1)}, f32[3,1024,2]{2,1,0:T(8,128)}) custom-call(bf16[1024,768]{1,0:T(8,128)(2,1)} %get-tuple-element.126.q_ref, bf16[4,1024,64]{2,1,0:T(8,128)(2,1)} %get-tuple-element.122.k_ref, bf16[4,1024,64]{2,1,0:T(8,128)(2,1)} %get-tuple-element.123.v_ref, s32[1024,1]{1,0:T(8,128)} %copy.117.start_ref), custom_call_target="tpu_custom_call" | custom-call | flops 113246208 | bytes 3145728 | tf_op jit(solution)/shard_map/attend/pallas_call | solution.py:617
  160.9 2.7 collective-permute-start.8
  163.6 15.2 %attend.3 = (bf16[1024,384]{1,0:T(8,128)(2,1)}, f32[3,1024,2]{2,1,0:T(8,128)}) custom-call(bf16[1024,768]{1,0:T(8,128)(2,1)} %get-tuple-element.126.q_ref, bf16[4,1024,64]{2,1,0:T(8,128)(2,1)} %get-tuple-element.122.k_ref, bf16[4,1024,64]{2,1,0:T(8,128)(2,1)} %get-tuple-element.123.v_ref, s32[1024,1]{1,0:T(8,128)} %copy.117.start_ref), custom_call_target="tpu_custom_call" | custom-call | flops 113246208 | bytes 3145728 | tf_op jit(solution)/shard_map/attend/pallas_call | solution.py:617
  187.0 4.1 collective-permute-done.9
  191.6 5.3 collective-permute-start.26
  198.2 5.9 multiply_reduce_fusion.2
  205.9 3.5 collective-permute-done.13.refs_11_
  210.3 33.8 %collective-permute-done.14.refs_0_.refs_1_ = bf16[512,1536]{1,0:T(8,128)(2,1)S(1)} collective-permute-done((bf16[512,1536]{1,0:T(8,128)(2,1)S(1)}, bf16[512,1536]{1,0:T(8,128)(2,1)S(1)}, u32[]{:S(2)}, u32[]{:S(2)}) %collective-permute-start.14) | collective-permute-done | bytes 1572896 | tf_op jit(solution)/shard_map/ppermute | solution.py:373
  245.4 3.0 collective-permute-start.24
  249.0 3.7 collective-permute-start.22
  252.8 8.4 %collective-permute-done.16.refs_2_ = bf16[256,1536]{1,0:T(8,128)(2,1)S(1)} collective-permute-done((bf16[256,1536]{1,0:T(8,128)(2,1)S(1)}, bf16[256,1536]{1,0:T(8,128)(2,1)S(1)}, u32[]{:S(2)}, u32[]{:S(2)}) %collective-permute-start.16) | collective-permute-done | bytes 786464 | tf_op jit(solution)/shard_map/ppermute | solution.py:377
  261.1 3.0 collective-permute-start.23
  270.1 2.6 select_select_fusion
  273.6 54.6 %experts.2 = (bf16[1024,1536]{1,0:T(8,128)(2,1)}, bf16[1024,1536]{1,0:T(8,128)(2,1)}, bf16[1024,1536]{1,0:T(8,128)(2,1)}, bf16[1024,1536]{1,0:T(8,128)(2,1)}, bf...) custom-call(s32[1]{0:T(128)} %bitcast.15.place_ref, ...), custom_call_target="tpu_custom_call" | custom-call | flops 2415919104 | bytes 50331648 | tf_op jit(solution)/shard_map/experts/pallas_call | solution.py:864
  329.1 7.2 collective-permute-done.28
  336.3 2.7 add_convert_fusion.1
  344.3 54.6 %experts.3 = (bf16[1024,1536]{1,0:T(8,128)(2,1)}, bf16[1024,1536]{1,0:T(8,128)(2,1)}, bf16[1024,1536]{1,0:T(8,128)(2,1)}, bf16[1024,1536]{1,0:T(8,128)(2,1)}, bf...) custom-call(s32[1]{0:T(128)} %bitcast.15.place_ref, ...), custom_call_target="tpu_custom_call", output_to_operand_aliasing={{4}: (21, {}), {5}: (22, {}), {6}: (23, {}), {7}: (24, {}),... | custom-call | flops 2415919104 | bytes 50331648 | tf_op jit(solution)/shard_map/experts/pallas_call | solution.py:864
  399.7 11.5 %fusion.11 = bf16[1536,512]{1,0:T(8,128)(2,1)S(1)} fusion(bf16[4096,1536]{1,0:T(8,128)(2,1)} %get-tuple-element.167, bf16[4096,512]{1,0:T(8,128)(2,1)} %get-tuple-element.160), kind=kOutput, calls=%fused_computation.50 | convolution fusion | flops 6444023808 | bytes 18350080 | tf_op jit(solution)/shard_map/dot_general | solution.py:575
  411.3 16.8 %convolution_convert_fusion.1 = bf16[1536,1024]{1,0:T(8,128)(2,1)S(1)} fusion(bf16[4096,1536]{1,0:T(8,128)(2,1)S(1)} %copy-done.12, bf16[4096,1024]{1,0:T(8,128)(2,1)} %get-tuple-element.158), kind=kOutput, calls=%fused_computation.12 | convolution fusion | flops 12886474752 | bytes 24117248 | tf_op jit(solution)/shard_map/dot_general | solution.py:575
  429.9 5.7 collective-permute-start.38
  442.0 17.5 %convolution_convert_fusion = bf16[1536,1024]{1,0:T(8,128)(2,1)} fusion(bf16[4096,1536]{1,0:T(8,128)(2,1)S(1)} %copy-done.12, bf16[4096,1024]{1,0:T(8,128)(2,1)} %get-tuple-element.166), kind=kOutput, calls=%fused_computation.11 | convolution fusion | flops 12886474752 | bytes 24117248 | tf_op jit(solution)/shard_map/dot_general | solution.py:575
  464.9 6.6 convolution_convert_fusion.2
  472.6 7.0 fusion.12
  485.2 3.2 add_convert_fusion.4
  488.4 5.5 collective-permute-start.41
  493.9 3.4 add_convert_fusion.3
  512.0 7.1 fusion.60
  523.6 40.6 %attend_back.1 = (bf16[1024,768]{1,0:T(8,128)(2,1)}, bf16[1024,256]{1,0:T(8,128)(2,1)}, bf16[1024,256]{1,0:T(8,128)(2,1)}) custom-call(bf16[1024,768]{1,0:T(8,128)(2,1)} %get-tuple-element.126.q_ref, bf16[4,1024,64]{2,1,0:T(8,128)(2,1)} %get-tuple-element.122.k_ref, bf16[4,1024,64]{2,1,0:T(8,128)(2,1)} %get-tuple-element.123.v_ref, ...), custom_call_target="tpu_custom_call" | custom-call | flops 566231040 | bytes 6291456 | tf_op jit(solution)/shard_map/attend_back/pallas_call | solution.py:694
  564.3 5.0 add_convert_fusion.8
  569.4 8.7 %qkv_grad.1 = bf16[2,2,2,4,48,1408]{5,4,3,2,1,0:T(8,128)(2,1)} custom-call(bf16[1024,1536]{1,0:T(8,128)(2,1)} %get-tuple-element.190.h_ref, bf16[1024,768]{1,0:T(8,128)(2,1)} %get-tuple-element.191.dq_ref, bf16[1024,256]{1,0:T(8,128)(2,1)} %get-tuple-element.192.dk_ref, bf16[1024,256]{1,0:T(8,128)(2,1)} %get-tuple-element.193.dv_ref, ...), custom_call_target="tpu_custom_call" | custom-call | flops 251658240 | bytes 1572864 | tf_op jit(solution)/shard_map/qkv_grad/pallas_call | solution.py:916
  578.1 3.3 dynamic-slice_bitcast_fusion
  582.5 2.8 convert_add_fusion
  585.3 2.6 copy-done.8
  592.2 5.0 select_convert_fusion
  597.2 5.1 collective-permute-start.49
  603.5 8.1 %collective-permute-done.45 = bf16[256,1536]{1,0:T(8,128)(2,1)} collective-permute-done((bf16[256,1536]{1,0:T(8,128)(2,1)}, bf16[256,1536]{1,0:T(8,128)(2,1)}, u32[]{:S(2)}, u32[]{:S(2)}) %collective-permute-start.45) | collective-permute-done | bytes 786464 | tf_op jit(solution)/shard_map/ppermute | solution.py:373
  611.7 4.6 fusion.29
  616.6 4.7 convert_add_fusion.3
  621.3 11.0 %token_grad.1 = (bf16[512,1536]{1,0:T(8,128)(2,1)}, bf16[512,1536]{1,0:T(8,128)(2,1)}) custom-call(bf16[1024,768]{1,0:T(8,128)(2,1)} %get-tuple-element.191.dq_ref, bf16[1024,256]{1,0:T(8,128)(2,1)} %get-tuple-element.192.dk_ref, bf16[1024,256]{1,0:T(8,128)(2,1)} %get-tuple-element.193.dv_ref, bf16[1536,1408]{1,0:T(8,128)(2,1)} %bitcast.78, ...), custom_call_target="tpu_custom_call" | custom-call | flops 251658240 | bytes 1572864 | tf_op jit(solution)/shard_map/token_grad/pallas_call | solution.py:542
  635.3 4.5 add_convert_fusion.6
  639.9 4.8 collective-permute-start.51
  650.3 8.3 %collective-permute-done.48 = bf16[2,4,48,1408]{3,2,1,0:T(8,128)(2,1)S(1)} collective-permute-done((bf16[2,4,48,1408]{3,2,1,0:T(8,128)(2,1)S(1)}, bf16[2,4,48,1408]{3,2,1,0:T(8,128)(2,1)S(1)}, u32[]{:S(2)}, u32[]{:S(2)}) %collective-permute-start.48) | collective-permute-done | bytes 1081376 | tf_op jit(solution)/shard_map/ppermute | solution.py:377
  660.2 8.6 %collective-permute-done.51 = bf16[768,768]{1,0:T(8,128)(2,1)S(1)} collective-permute-done((bf16[768,768]{1,0:T(8,128)(2,1)}, bf16[768,768]{1,0:T(8,128)(2,1)S(1)}, u32[]{:S(2)}, u32[]{:S(2)}) %collective-permute-start.51) | collective-permute-done | bytes 1179680 | tf_op jit(solution)/shard_map/ppermute | solution.py:389
  668.8 3.9 collective-permute-done.52
  672.7 7.8 %collective-permute-done.53 = bf16[512,1536]{1,0:T(8,128)(2,1)S(1)} collective-permute-done((bf16[512,1536]{1,0:T(8,128)(2,1)}, bf16[512,1536]{1,0:T(8,128)(2,1)S(1)}, u32[]{:S(2)}, u32[]{:S(2)}) %collective-permute-start.53) | collective-permute-done | bytes 1572896 | tf_op jit(solution)/shard_map/ppermute | solution.py:373
  680.5 4.0 fusion.16
  686.5 2.9 collective-permute-start.56
  690.3 5.5 collective-permute-start.57
  695.8 2.5 fusion.2
  698.3 4.3 fusion.5
  703.3 10.2 %collective-permute-done.55 = bf16[2,48,1408]{2,1,0:T(8,128)(2,1)S(1)} collective-permute-done((bf16[2,48,1408]{2,1,0:T(8,128)(2,1)S(1)}, bf16[2,48,1408]{2,1,0:T(8,128)(2,1)S(1)}, u32[]{:S(2)}, u32[]{:S(2)}) %collective-permute-start.55) | collective-permute-done | bytes 270368 | tf_op jit(solution)/shard_map/ppermute | solution.py:377
  715.1 7.0 collective-permute-done.57
  (325 shorter events, 126.6 us)
Async XLA Ops:
  7.2 123.1 %all-gather.3.cloned.1.call-start = ((), (), s32[]{:S(2)}) async-start(), calls=%async_computation.1 | async-start | bytes 4595712 | tf_op jit(solution)/shard_map/all_gather | solution.py:1004
  10.0 5.4 collective-permute-start.5
  16.2 182.0 %all-gather.5.cloned.1.call-start = ((), (), s32[]{:S(2)}) async-start(), calls=%async_computation.2 | async-start | bytes 4866048 | tf_op jit(solution)/shard_map/all_gather | solution.py:1005
  16.9 643.2 %reduce-scatter.2.cloned.1.call-start = ((), (), s32[]{:S(2)}) async-start(), calls=%async_computation.3 | async-start | bytes 4866048 | tf_op jit(solution)/shard_map/reduce_scatter | solution.py:1202
  18.4 30.4 %collective-permute-start = (bf16[1536,512]{1,0:T(8,128)(2,1)S(1)}, bf16[1536,512]{1,0:T(8,128)(2,1)S(1)}, u32[]{:S(2)}, u32[]{:S(2)}) collective-permute-start(bf16[1536,512]{1,0:T(8,128)(2,1)S(1)} %pad_maximum_fusion.6), channel_id=1, source_target_pairs={{0,0},{1,16},{2,2},{3,18},{4,4},{5,20},{6,6},{7,22},{8,8},{9,24},{... | collective-permute-start | bytes 4718600 | tf_op jit(solution)/shard_map/ppermute | solution.py:982
  22.9 25.9 %collective-permute-start.1 = (bf16[1536,256]{1,0:T(8,128)(2,1)}, bf16[1536,256]{1,0:T(8,128)(2,1)}, u32[]{:S(2)}, u32[]{:S(2)}) collective-permute-start(bf16[1536,256]{1,0:T(8,128)(2,1)} %get-tuple-element.310), channel_id=1, source_target_pairs={{0,1},{1,17},{2,3},{3,19},{4,5},{5,21},{6,7},{7,23},{8,9},{9,25},{... | collective-permute-start | bytes 2359304 | tf_op jit(solution)/shard_map/ppermute | solution.py:982
  50.2 72.1 %collective-permute-start.3 = (bf16[1536,768]{1,0:T(8,128)(2,1)S(1)}, bf16[1536,768]{1,0:T(8,128)(2,1)}, u32[]{:S(2)}, u32[]{:S(2)}) collective-permute-start(bf16[1536,768]{1,0:T(8,128)(2,1)S(1)} %pad_maximum_fusion.5.refs_19_.refs_15_), channel_id=1, source_target_pairs={{0,4},{1,5},{2,6},{3,7},{4,8},{5,9},{6,10},{7,11},{8,12},{9,13},{1... | collective-permute-start | bytes 7077896 | tf_op jit(solution)/shard_map/ppermute | solution.py:389
  54.9 70.1 %collective-permute-start.4 = (bf16[1536,768]{1,0:T(8,128)(2,1)S(1)}, bf16[1536,768]{1,0:T(8,128)(2,1)}, u32[]{:S(2)}, u32[]{:S(2)}) collective-permute-start(bf16[1536,768]{1,0:T(8,128)(2,1)S(1)} %pad_maximum_fusion.5.refs_19_.refs_15_), channel_id=1, source_target_pairs={{4,0},{5,1},{6,2},{7,3},{8,4},{9,5},{10,6},{11,7},{12,8},{13,9},{1... | collective-permute-start | bytes 7077896 | tf_op jit(solution)/shard_map/ppermute | solution.py:393
  56.2 37.6 %collective-permute-start.2 = (bf16[512,1536]{1,0:T(8,128)(2,1)}, bf16[512,1536]{1,0:T(8,128)(2,1)}, u32[]{:S(2)}, u32[]{:S(2)}) collective-permute-start(bf16[512,1536]{1,0:T(8,128)(2,1)} %param.17), channel_id=1, source_target_pairs={{0,16},{16,0},{1,17},{17,1},{2,18},{18,2},{3,19},{19,3},{4,20},{20... | collective-permute-start | bytes 4718600 | tf_op jit(solution)/shard_map/ppermute | solution.py:373
  62.7 100.9 %collective-permute-start.7 = (bf16[512,1664]{1,0:T(8,128)(2,1)}, bf16[512,1664]{1,0:T(8,128)(2,1)}, u32[]{:S(2)}, u32[]{:S(2)}) collective-permute-start(bf16[512,1664]{1,0:T(8,128)(2,1)} %concatenate.95.refs_6_), channel_id=1, source_target_pairs={{0,2},{1,3},{2,0},{3,1},{4,6},{5,7},{6,4},{7,5},{8,10},{9,11},{10,... | collective-permute-start | bytes 5111816 | tf_op jit(solution)/shard_map/ppermute | solution.py:377
  93.8 69.8 %collective-permute-start.6 = (bf16[512,1664]{1,0:T(8,128)(2,1)}, bf16[512,1664]{1,0:T(8,128)(2,1)}, u32[]{:S(2)}, u32[]{:S(2)}) collective-permute-start(bf16[512,1664]{1,0:T(8,128)(2,1)} %concatenate.95.refs_6_), channel_id=1, source_target_pairs={{0,16},{16,0},{1,17},{17,1},{2,18},{18,2},{3,19},{19,3},{4,20},{20... | collective-permute-start | bytes 5111816 | tf_op jit(solution)/shard_map/ppermute | solution.py:373
  125.0 66.6 %collective-permute-start.10 = (bf16[1536,768]{1,0:T(8,128)(2,1)}, bf16[1536,768]{1,0:T(8,128)(2,1)}, u32[]{:S(2)}, u32[]{:S(2)}) collective-permute-start(bf16[1536,768]{1,0:T(8,128)(2,1)} %collective-permute-done.3.refs_18_.refs_14_), channel_id=1, source_target_pairs={{0,4},{1,5},{2,6},{3,7},{4,8},{5,9},{6,10},{7,11},{8,12},{9,13},{1... | collective-permute-start | bytes 7077896 | tf_op jit(solution)/shard_map/ppermute | solution.py:389
  129.0 62.6 %collective-permute-start.11 = (bf16[1536,768]{1,0:T(8,128)(2,1)}, bf16[1536,768]{1,0:T(8,128)(2,1)}, u32[]{:S(2)}, u32[]{:S(2)}) collective-permute-start(bf16[1536,768]{1,0:T(8,128)(2,1)} %collective-permute-done.4.refs_20_.refs_16_), channel_id=1, source_target_pairs={{4,0},{5,1},{6,2},{7,3},{8,4},{9,5},{10,6},{11,7},{12,8},{13,9},{1... | collective-permute-start | bytes 7077896 | tf_op jit(solution)/shard_map/ppermute | solution.py:393
  160.9 24.6 %collective-permute-start.8 = (bf16[512,384]{0,1:T(8,128)(2,1)S(1)}, bf16[512,384]{0,1:T(8,128)(2,1)S(1)}, u32[]{:S(2)}, u32[]{:S(2)}) collective-permute-start(bf16[512,384]{0,1:T(8,128)(2,1)S(1)} %fusion.34), channel_id=1, source_target_pairs={{0,16},{16,0},{1,17},{17,1},{2,18},{18,2},{3,19},{19,3},{4,20},{20... | collective-permute-start | bytes 1179656 | tf_op jit(solution)/shard_map/ppermute | solution.py:373
  180.7 10.4 %collective-permute-start.9 = (bf16[512,384]{0,1:T(8,128)(2,1)S(1)}, bf16[512,384]{0,1:T(8,128)(2,1)S(1)}, u32[]{:S(2)}, u32[]{:S(2)}) collective-permute-start(bf16[512,384]{0,1:T(8,128)(2,1)S(1)} %fusion.35), channel_id=1, source_target_pairs={{0,16},{16,0},{1,17},{17,1},{2,18},{18,2},{3,19},{19,3},{4,20},{20... | collective-permute-start | bytes 1179656 | tf_op jit(solution)/shard_map/ppermute | solution.py:373
  182.7 23.2 %collective-permute-start.12 = (bf16[256,1664]{1,0:T(8,128)(2,1)S(1)}, bf16[256,1664]{1,0:T(8,128)(2,1)}, u32[]{:S(2)}, u32[]{:S(2)}) collective-permute-start(bf16[256,1664]{1,0:T(8,128)(2,1)S(1)} %slice.207), channel_id=1, source_target_pairs={{0,2},{1,3},{2,0},{3,1},{4,6},{5,7},{6,4},{7,5},{8,10},{9,11},{10,... | collective-permute-start | bytes 2555912 | tf_op jit(solution)/shard_map/ppermute | solution.py:377
  185.5 23.9 %collective-permute-start.13 = (bf16[256,1664]{1,0:T(8,128)(2,1)S(1)}, bf16[256,1664]{1,0:T(8,128)(2,1)}, u32[]{:S(2)}, u32[]{:S(2)}) collective-permute-start(bf16[256,1664]{1,0:T(8,128)(2,1)S(1)} %slice.208), channel_id=1, source_target_pairs={{0,16},{16,0},{1,17},{17,1},{2,18},{18,2},{3,19},{19,3},{4,20},{20... | collective-permute-start | bytes 2555912 | tf_op jit(solution)/shard_map/ppermute | solution.py:373
  191.6 56.7 %collective-permute-start.26 = (bf16[1536,768]{1,0:T(8,128)(2,1)}, bf16[1536,768]{1,0:T(8,128)(2,1)}, u32[]{:S(2)}, u32[]{:S(2)}) collective-permute-start(bf16[1536,768]{1,0:T(8,128)(2,1)} %collective-permute-done.10.refs_17_.refs_13_), channel_id=1, source_target_pairs={{0,4},{1,5},{2,6},{3,7},{4,8},{5,9},{6,10},{7,11},{8,12},{9,13},{1... | collective-permute-start | bytes 7077896 | tf_op jit(solution)/shard_map/ppermute | solution.py:389
  196.9 52.1 %collective-permute-start.27 = (bf16[1536,768]{1,0:T(8,128)(2,1)}, bf16[1536,768]{1,0:T(8,128)(2,1)}, u32[]{:S(2)}, u32[]{:S(2)}) collective-permute-start(bf16[1536,768]{1,0:T(8,128)(2,1)} %collective-permute-done.11.refs_21_.refs_17_), channel_id=1, source_target_pairs={{4,0},{5,1},{6,2},{7,3},{8,4},{9,5},{10,6},{11,7},{12,8},{13,9},{1... | collective-permute-start | bytes 7077896 | tf_op jit(solution)/shard_map/ppermute | solution.py:393
  209.4 34.7 %collective-permute-start.14 = (bf16[512,1536]{1,0:T(8,128)(2,1)S(1)}, bf16[512,1536]{1,0:T(8,128)(2,1)S(1)}, u32[]{:S(2)}, u32[]{:S(2)}) collective-permute-start(bf16[512,1536]{1,0:T(8,128)(2,1)S(1)} %multiply_convert_fusion.1.refs_0_), channel_id=1, source_target_pairs={{0,16},{16,0},{1,17},{17,1},{2,18},{18,2},{3,19},{19,3},{4,20},{20... | collective-permute-start | bytes 4718600 | tf_op jit(solution)/shard_map/ppermute | solution.py:373
  209.4 35.8 %collective-permute-start.15 = (bf16[512,1536]{1,0:T(8,128)(2,1)S(1)}, bf16[512,1536]{1,0:T(8,128)(2,1)S(1)}, u32[]{:S(2)}, u32[]{:S(2)}) collective-permute-start(bf16[512,1536]{1,0:T(8,128)(2,1)S(1)} %multiply_convert_fusion.1.refs_0_), channel_id=1, source_target_pairs={{0,2},{1,3},{2,0},{3,1},{4,6},{5,7},{6,4},{7,5},{8,10},{9,11},{10,... | collective-permute-start | bytes 4718600 | tf_op jit(solution)/shard_map/ppermute | solution.py:377
  244.1 17.0 %collective-permute-start.16 = (bf16[256,1536]{1,0:T(8,128)(2,1)S(1)}, bf16[256,1536]{1,0:T(8,128)(2,1)S(1)}, u32[]{:S(2)}, u32[]{:S(2)}) collective-permute-start(bf16[256,1536]{1,0:T(8,128)(2,1)S(1)} %slice.269), channel_id=1, source_target_pairs={{0,2},{1,3},{2,0},{3,1},{4,6},{5,7},{6,4},{7,5},{8,10},{9,11},{10,... | collective-permute-start | bytes 2359304 | tf_op jit(solution)/shard_map/ppermute | solution.py:377
  245.3 18.9 %collective-permute-start.17 = (bf16[256,1536]{1,0:T(8,128)(2,1)S(1)}, bf16[256,1536]{1,0:T(8,128)(2,1)S(1)}, u32[]{:S(2)}, u32[]{:S(2)}) collective-permute-start(bf16[256,1536]{1,0:T(8,128)(2,1)S(1)} %slice.270), channel_id=1, source_target_pairs={{0,16},{16,0},{1,17},{17,1},{2,18},{18,2},{3,19},{19,3},{4,20},{20... | collective-permute-start | bytes 2359304 | tf_op jit(solution)/shard_map/ppermute | solution.py:373
  245.4 19.9 %collective-permute-start.24 = (bf16[256,1664]{1,0:T(8,128)(2,1)}, bf16[256,1664]{1,0:T(8,128)(2,1)S(1)}, u32[]{:S(2)}, u32[]{:S(2)}) collective-permute-start(bf16[256,1664]{1,0:T(8,128)(2,1)} %collective-permute-done.12.refs_10_), channel_id=1, source_target_pairs={{0,1},{1,0},{2,3},{3,2},{4,5},{5,4},{6,7},{7,6},{8,9},{9,8},{10,11... | collective-permute-start | bytes 2555912 | tf_op jit(solution)/shard_map/ppermute | solution.py:377
  248.3 21.0 %collective-permute-start.18 = (bf16[512,1536]{1,0:T(8,128)(2,1)S(1)}, bf16[512,1536]{1,0:T(8,128)(2,1)}, u32[]{:S(2)}, u32[]{:S(2)}) collective-permute-start(bf16[512,1536]{1,0:T(8,128)(2,1)S(1)} %collective-permute-done.14.refs_0_.refs_1_), channel_id=1, source_target_pairs={{0,1},{1,0},{2,3},{3,2},{4,5},{5,4},{6,7},{7,6},{8,9},{9,8},{10,11... | collective-permute-start | bytes 4718600 | tf_op jit(solution)/shard_map/ppermute | solution.py:377
  249.0 24.5 %collective-permute-start.22 = (bf16[512,1664]{1,0:T(8,128)(2,1)}, bf16[512,1664]{1,0:T(8,128)(2,1)}, u32[]{:S(2)}, u32[]{:S(2)}) collective-permute-start(bf16[512,1664]{1,0:T(8,128)(2,1)} %collective-permute-done.6.refs_8_.refs_7_), channel_id=1, source_target_pairs={{0,1},{1,0},{2,3},{3,2},{4,5},{5,4},{6,7},{7,6},{8,9},{9,8},{10,11... | collective-permute-start | bytes 5111816 | tf_op jit(solution)/shard_map/ppermute | solution.py:377
  261.1 12.4 %collective-permute-start.23 = (bf16[512,1664]{1,0:T(8,128)(2,1)}, bf16[512,1664]{1,0:T(8,128)(2,1)}, u32[]{:S(2)}, u32[]{:S(2)}) collective-permute-start(bf16[512,1664]{1,0:T(8,128)(2,1)} %collective-permute-done.7.refs_9_.refs_8_), channel_id=1, source_target_pairs={{0,1},{1,0},{2,3},{3,2},{4,5},{5,4},{6,7},{7,6},{8,9},{9,8},{10,11... | collective-permute-start | bytes 5111816 | tf_op jit(solution)/shard_map/ppermute | solution.py:377
  264.2 4.8 collective-permute-start.25
  266.2 7.3 collective-permute-start.19
  268.9 4.6 collective-permute-start.20
  269.3 4.2 collective-permute-start.21
  328.1 8.2 %collective-permute-start.28 = (bf16[1024,1536]{1,0:T(8,128)(2,1)}, bf16[1024,1536]{1,0:T(8,128)(2,1)S(1)}, u32[]{:S(2)}, u32[]{:S(2)}) collective-permute-start(bf16[1024,1536]{1,0:T(8,128)(2,1)} %get-tuple-element.143), channel_id=1, source_target_pairs={{0,1},{1,0},{2,3},{3,2},{4,5},{5,4},{6,7},{7,6},{8,9},{9,8},{10,11... | collective-permute-start | bytes 9437192 | tf_op jit(solution)/shard_map/ppermute | solution.py:377
  328.6 14.5 %collective-permute-start.29 = (bf16[512,1536]{1,0:T(8,128)(2,1)}, bf16[512,1536]{1,0:T(8,128)(2,1)}, u32[]{:S(2)}, u32[]{:S(2)}) collective-permute-start(bf16[512,1536]{1,0:T(8,128)(2,1)} %copy-done.20), channel_id=1, source_target_pairs={{0,1},{1,0},{2,3},{3,2},{4,5},{5,4},{6,7},{7,6},{8,9},{9,8},{10,11... | collective-permute-start | bytes 4718600 | tf_op jit(solution)/shard_map/ppermute | solution.py:377
  328.7 14.4 %collective-permute-start.30 = (bf16[512,1664]{1,0:T(8,128)(2,1)}, bf16[512,1664]{1,0:T(8,128)(2,1)S(1)}, u32[]{:S(2)}, u32[]{:S(2)}) collective-permute-start(bf16[512,1664]{1,0:T(8,128)(2,1)} %concatenate.95.refs_6_), channel_id=1, source_target_pairs={{0,1},{1,0},{2,3},{3,2},{4,5},{5,4},{6,7},{7,6},{8,9},{9,8},{10,11... | collective-permute-start | bytes 5111816 | tf_op jit(solution)/shard_map/ppermute | solution.py:377
  340.9 58.8 %collective-permute-start.31 = (bf16[512,1536]{1,0:T(8,128)(2,1)}, bf16[512,1536]{1,0:T(8,128)(2,1)S(1)}, u32[]{:S(2)}, u32[]{:S(2)}) collective-permute-start(bf16[512,1536]{1,0:T(8,128)(2,1)} %get-tuple-element.295), channel_id=1, source_target_pairs={{0,2},{1,3},{2,0},{3,1},{4,6},{5,7},{6,4},{7,5},{8,10},{9,11},{10,... | collective-permute-start | bytes 4718600 | tf_op jit(solution)/shard_map/ppermute | solution.py:377
  343.1 56.5 %collective-permute-start.32 = (bf16[512,1536]{1,0:T(8,128)(2,1)}, bf16[512,1536]{1,0:T(8,128)(2,1)}, u32[]{:S(2)}, u32[]{:S(2)}) collective-permute-start(bf16[512,1536]{1,0:T(8,128)(2,1)} %get-tuple-element.294), channel_id=1, source_target_pairs={{0,16},{16,0},{1,17},{17,1},{2,18},{18,2},{3,19},{19,3},{4,20},{20... | collective-permute-start | bytes 4718600 | tf_op jit(solution)/shard_map/ppermute | solution.py:373
  398.9 39.7 %collective-permute-start.33 = (bf16[1024,1536]{1,0:T(8,128)(2,1)}, bf16[1024,1536]{1,0:T(8,128)(2,1)S(1)}, u32[]{:S(2)}, u32[]{:S(2)}) collective-permute-start(bf16[1024,1536]{1,0:T(8,128)(2,1)} %get-tuple-element.162), channel_id=1, source_target_pairs={{0,1},{1,0},{2,3},{3,2},{4,5},{5,4},{6,7},{7,6},{8,9},{9,8},{10,11... | collective-permute-start | bytes 9437192 | tf_op jit(solution)/shard_map/ppermute | solution.py:377
  411.3 82.6 %copy-start.7 = (bf16[1536,256]{1,0:T(8,128)(2,1)}, bf16[1536,256]{1,0:T(8,128)(2,1)S(1)}, u32[]{:S(2)}) copy-start(bf16[1536,256]{1,0:T(8,128)(2,1)S(1)} %get-tuple-element.306) | copy-start | bytes 2359300
  429.9 55.3 %collective-permute-start.38 = (bf16[1536,768]{1,0:T(8,128)(2,1)}, bf16[1536,768]{1,0:T(8,128)(2,1)}, u32[]{:S(2)}, u32[]{:S(2)}) collective-permute-start(bf16[1536,768]{1,0:T(8,128)(2,1)} %pad_maximum_fusion.1), channel_id=1, source_target_pairs={{0,4},{1,5},{2,6},{3,7},{4,8},{5,9},{6,10},{7,11},{8,12},{9,13},{1... | collective-permute-start | bytes 7077896 | tf_op jit(solution)/shard_map/ppermute | solution.py:389
  437.1 56.7 %collective-permute-start.39 = (bf16[1536,768]{1,0:T(8,128)(2,1)}, bf16[1536,768]{1,0:T(8,128)(2,1)}, u32[]{:S(2)}, u32[]{:S(2)}) collective-permute-start(bf16[1536,768]{1,0:T(8,128)(2,1)} %pad_maximum_fusion), channel_id=1, source_target_pairs={{4,0},{5,1},{6,2},{7,3},{8,4},{9,5},{10,6},{11,7},{12,8},{13,9},{1... | collective-permute-start | bytes 7077896 | tf_op jit(solution)/shard_map/ppermute | solution.py:393
  441.7 19.0 %collective-permute-start.34 = (bf16[256,1536]{1,0:T(8,128)(2,1)S(1)}, bf16[256,1536]{1,0:T(8,128)(2,1)S(1)}, u32[]{:S(2)}, u32[]{:S(2)}) collective-permute-start(bf16[256,1536]{1,0:T(8,128)(2,1)S(1)} %get-tuple-element.280), channel_id=1, source_target_pairs={{0,16},{16,0},{1,17},{17,1},{2,18},{18,2},{3,19},{19,3},{4,20},{20... | collective-permute-start | bytes 2359304 | tf_op jit(solution)/shard_map/ppermute | solution.py:373
  441.8 19.0 %collective-permute-start.35 = (bf16[256,1536]{1,0:T(8,128)(2,1)S(1)}, bf16[256,1536]{1,0:T(8,128)(2,1)S(1)}, u32[]{:S(2)}, u32[]{:S(2)}) collective-permute-start(bf16[256,1536]{1,0:T(8,128)(2,1)S(1)} %get-tuple-element.281), channel_id=1, source_target_pairs={{0,2},{1,3},{2,0},{3,1},{4,6},{5,7},{6,4},{7,5},{8,10},{9,11},{10,... | collective-permute-start | bytes 2359304 | tf_op jit(solution)/shard_map/ppermute | solution.py:377
  471.5 27.1 %collective-permute-start.40 = (bf16[1024,1536]{1,0:T(8,128)(2,1)}, bf16[1024,1536]{1,0:T(8,128)(2,1)S(1)}, u32[]{:S(2)}, u32[]{:S(2)}) collective-permute-start(bf16[1024,1536]{1,0:T(8,128)(2,1)} %get-tuple-element.173), channel_id=1, source_target_pairs={{0,1},{1,0},{2,3},{3,2},{4,5},{5,4},{6,7},{7,6},{8,9},{9,8},{10,11... | collective-permute-start | bytes 9437192 | tf_op jit(solution)/shard_map/ppermute | solution.py:377
  481.8 100.6 %collective-permute-start.36 = (bf16[1024,1536]{1,0:T(8,128)(2,1)}, bf16[1024,1536]{1,0:T(8,128)(2,1)}, u32[]{:S(2)}, u32[]{:S(2)}) collective-permute-start(bf16[1024,1536]{1,0:T(8,128)(2,1)} %get-tuple-element.171), channel_id=1, source_target_pairs={{0,1},{1,0},{2,3},{3,2},{4,5},{5,4},{6,7},{7,6},{8,9},{9,8},{10,11... | collective-permute-start | bytes 9437192 | tf_op jit(solution)/shard_map/ppermute | solution.py:377
  482.7 19.2 %collective-permute-start.37 = (bf16[512,768]{1,0:T(8,128)(2,1)S(1)}, bf16[512,768]{1,0:T(8,128)(2,1)S(1)}, u32[]{:S(2)}, u32[]{:S(2)}) collective-permute-start(bf16[512,768]{1,0:T(8,128)(2,1)S(1)} %constant_dynamic-slice_fusion), channel_id=1, source_target_pairs={{0,16},{16,0},{1,17},{17,1},{2,18},{18,2},{3,19},{19,3},{4,20},{20... | collective-permute-start | bytes 2359304 | tf_op jit(solution)/shard_map/ppermute | solution.py:373
  488.4 75.9 %collective-permute-start.41 = (bf16[1536,768]{1,0:T(8,128)(2,1)}, bf16[1536,768]{1,0:T(8,128)(2,1)}, u32[]{:S(2)}, u32[]{:S(2)}) collective-permute-start(bf16[1536,768]{1,0:T(8,128)(2,1)} %add_convert_fusion.4), channel_id=1, source_target_pairs={{0,4},{1,5},{2,6},{3,7},{4,8},{5,9},{6,10},{7,11},{8,12},{9,13},{1... | collective-permute-start | bytes 7077896 | tf_op jit(solution)/shard_map/ppermute | solution.py:389
  497.3 67.0 %collective-permute-start.42 = (bf16[1536,768]{1,0:T(8,128)(2,1)}, bf16[1536,768]{1,0:T(8,128)(2,1)}, u32[]{:S(2)}, u32[]{:S(2)}) collective-permute-start(bf16[1536,768]{1,0:T(8,128)(2,1)} %add_convert_fusion.3), channel_id=1, source_target_pairs={{4,0},{5,1},{6,2},{7,3},{8,4},{9,5},{10,6},{11,7},{12,8},{13,9},{1... | collective-permute-start | bytes 7077896 | tf_op jit(solution)/shard_map/ppermute | solution.py:393
  501.4 62.9 %collective-permute-start.43 = (bf16[512,1536]{1,0:T(8,128)(2,1)}, bf16[512,1536]{1,0:T(8,128)(2,1)}, u32[]{:S(2)}, u32[]{:S(2)}) collective-permute-start(bf16[512,1536]{1,0:T(8,128)(2,1)} %get-tuple-element.289), channel_id=1, source_target_pairs={{0,2},{1,3},{2,0},{3,1},{4,6},{5,7},{6,4},{7,5},{8,10},{9,11},{10,... | collective-permute-start | bytes 4718600 | tf_op jit(solution)/shard_map/ppermute | solution.py:377
  501.9 62.4 %collective-permute-start.44 = (bf16[512,1536]{1,0:T(8,128)(2,1)}, bf16[512,1536]{1,0:T(8,128)(2,1)}, u32[]{:S(2)}, u32[]{:S(2)}) collective-permute-start(bf16[512,1536]{1,0:T(8,128)(2,1)} %get-tuple-element.288), channel_id=1, source_target_pairs={{0,16},{16,0},{1,17},{17,1},{2,18},{18,2},{3,19},{19,3},{4,20},{20... | collective-permute-start | bytes 4718600 | tf_op jit(solution)/shard_map/ppermute | solution.py:373
  581.4 35.3 %collective-permute-start.47 = (bf16[2,2,4,48,1408]{4,3,2,1,0:T(8,128)(2,1)}, bf16[2,2,4,48,1408]{4,3,2,1,0:T(8,128)(2,1)}, u32[]{:S(2)}, u32[]{:S(2)}) collective-permute-start(bf16[2,2,4,48,1408]{4,3,2,1,0:T(8,128)(2,1)} %dynamic-slice_bitcast_fusion), channel_id=1, source_target_pairs={{0,1},{1,0},{2,3},{3,2},{4,5},{5,4},{6,7},{7,6},{8,9},{9,8},{10,11... | collective-permute-start | bytes 6488072 | tf_op jit(solution)/shard_map/ppermute | solution.py:377
  590.1 21.5 %collective-permute-start.45 = (bf16[256,1536]{1,0:T(8,128)(2,1)}, bf16[256,1536]{1,0:T(8,128)(2,1)}, u32[]{:S(2)}, u32[]{:S(2)}) collective-permute-start(bf16[256,1536]{1,0:T(8,128)(2,1)} %fusion.28), channel_id=1, source_target_pairs={{0,16},{16,0},{1,17},{17,1},{2,18},{18,2},{3,19},{19,3},{4,20},{20... | collective-permute-start | bytes 2359304 | tf_op jit(solution)/shard_map/ppermute | solution.py:373
  597.2 42.7 %collective-permute-start.49 = (bf16[768,768]{1,0:T(8,128)(2,1)}, bf16[768,768]{1,0:T(8,128)(2,1)}, u32[]{:S(2)}, u32[]{:S(2)}) collective-permute-start(bf16[768,768]{1,0:T(8,128)(2,1)} %get-tuple-element.287), channel_id=1, source_target_pairs={{0,4},{1,5},{2,6},{3,7},{4,8},{5,9},{6,10},{7,11},{8,12},{9,13},{1... | collective-permute-start | bytes 3538952 | tf_op jit(solution)/shard_map/ppermute | solution.py:389
  602.2 37.6 %collective-permute-start.50 = (bf16[768,768]{1,0:T(8,128)(2,1)}, bf16[768,768]{1,0:T(8,128)(2,1)}, u32[]{:S(2)}, u32[]{:S(2)}) collective-permute-start(bf16[768,768]{1,0:T(8,128)(2,1)} %get-tuple-element.286), channel_id=1, source_target_pairs={{4,0},{5,1},{6,2},{7,3},{8,4},{9,5},{10,6},{11,7},{12,8},{13,9},{1... | collective-permute-start | bytes 3538952 | tf_op jit(solution)/shard_map/ppermute | solution.py:393
  616.2 29.9 %collective-permute-start.46 = (bf16[256,1536]{1,0:T(8,128)(2,1)}, bf16[256,1536]{1,0:T(8,128)(2,1)}, u32[]{:S(2)}, u32[]{:S(2)}) collective-permute-start(bf16[256,1536]{1,0:T(8,128)(2,1)} %get-tuple-element.277), channel_id=1, source_target_pairs={{0,2},{1,3},{2,0},{3,1},{4,6},{5,7},{6,4},{7,5},{8,10},{9,11},{10,... | collective-permute-start | bytes 2359304 | tf_op jit(solution)/shard_map/ppermute | solution.py:377
  634.2 24.4 %collective-permute-start.48 = (bf16[2,4,48,1408]{3,2,1,0:T(8,128)(2,1)S(1)}, bf16[2,4,48,1408]{3,2,1,0:T(8,128)(2,1)S(1)}, u32[]{:S(2)}, u32[]{:S(2)}) collective-permute-start(bf16[2,4,48,1408]{3,2,1,0:T(8,128)(2,1)S(1)} %fusion.48), channel_id=1, source_target_pairs={{0,2},{1,3},{2,0},{3,1},{4,6},{5,7},{6,4},{7,5},{8,10},{9,11},{10,... | collective-permute-start | bytes 3244040 | tf_op jit(solution)/shard_map/ppermute | solution.py:377
  639.9 28.9 %collective-permute-start.51 = (bf16[768,768]{1,0:T(8,128)(2,1)}, bf16[768,768]{1,0:T(8,128)(2,1)S(1)}, u32[]{:S(2)}, u32[]{:S(2)}) collective-permute-start(bf16[768,768]{1,0:T(8,128)(2,1)} %get-tuple-element.200), channel_id=1, source_target_pairs={{0,4},{1,5},{2,6},{3,7},{4,8},{5,9},{6,10},{7,11},{8,12},{9,13},{1... | collective-permute-start | bytes 3538952 | tf_op jit(solution)/shard_map/ppermute | solution.py:389
  644.6 28.1 %collective-permute-start.52 = (bf16[768,768]{1,0:T(8,128)(2,1)}, bf16[768,768]{1,0:T(8,128)(2,1)}, u32[]{:S(2)}, u32[]{:S(2)}) collective-permute-start(bf16[768,768]{1,0:T(8,128)(2,1)} %get-tuple-element.201), channel_id=1, source_target_pairs={{4,0},{5,1},{6,2},{7,3},{8,4},{9,5},{10,6},{11,7},{12,8},{13,9},{1... | collective-permute-start | bytes 3538952 | tf_op jit(solution)/shard_map/ppermute | solution.py:393
  645.9 34.6 %collective-permute-start.53 = (bf16[512,1536]{1,0:T(8,128)(2,1)}, bf16[512,1536]{1,0:T(8,128)(2,1)S(1)}, u32[]{:S(2)}, u32[]{:S(2)}) collective-permute-start(bf16[512,1536]{1,0:T(8,128)(2,1)} %get-tuple-element.202), channel_id=1, source_target_pairs={{0,16},{16,0},{1,17},{17,1},{2,18},{18,2},{3,19},{19,3},{4,20},{20... | collective-permute-start | bytes 4718600 | tf_op jit(solution)/shard_map/ppermute | solution.py:373
  686.5 16.8 %collective-permute-start.56 = (bf16[2,48,1408]{2,1,0:T(8,128)(2,1)S(1)}, bf16[2,48,1408]{2,1,0:T(8,128)(2,1)S(1)}, u32[]{:S(2)}, u32[]{:S(2)}) collective-permute-start(bf16[2,48,1408]{2,1,0:T(8,128)(2,1)S(1)} %fusion.63), channel_id=1, source_target_pairs={{0,12},{1,13},{2,14},{3,15},{4,8},{5,9},{6,10},{7,11},{8,4},{9,5},... | collective-permute-start | bytes 811016 | tf_op jit(solution)/shard_map/ppermute | solution.py:377
  689.5 24.0 %collective-permute-start.55 = (bf16[2,48,1408]{2,1,0:T(8,128)(2,1)S(1)}, bf16[2,48,1408]{2,1,0:T(8,128)(2,1)S(1)}, u32[]{:S(2)}, u32[]{:S(2)}) collective-permute-start(bf16[2,48,1408]{2,1,0:T(8,128)(2,1)S(1)} %get-tuple-element.313), channel_id=1, source_target_pairs={{0,8},{1,9},{2,10},{3,11},{4,12},{5,13},{6,14},{7,15},{8,0},{9,1},... | collective-permute-start | bytes 811016 | tf_op jit(solution)/shard_map/ppermute | solution.py:377
  689.7 23.8 %collective-permute-start.54 = (bf16[2,48,1408]{2,1,0:T(8,128)(2,1)S(1)}, bf16[2,48,1408]{2,1,0:T(8,128)(2,1)S(1)}, u32[]{:S(2)}, u32[]{:S(2)}) collective-permute-start(bf16[2,48,1408]{2,1,0:T(8,128)(2,1)S(1)} %get-tuple-element.312), channel_id=1, source_target_pairs={{0,4},{1,5},{2,6},{3,7},{4,0},{5,1},{6,2},{7,3},{8,12},{9,13},{10,... | collective-permute-start | bytes 811016 | tf_op jit(solution)/shard_map/ppermute | solution.py:377
  690.3 31.8 %collective-permute-start.57 = (bf16[1536,512]{1,0:T(8,128)(2,1)S(1)}, bf16[1536,512]{1,0:T(8,128)(2,1)S(1)}, u32[]{:S(2)}, u32[]{:S(2)}) collective-permute-start(bf16[1536,512]{1,0:T(8,128)(2,1)S(1)} %fusion.25), channel_id=1, source_target_pairs={{0,0},{1,16},{2,2},{3,18},{4,4},{5,20},{6,6},{7,22},{8,8},{9,24},{... | collective-permute-start | bytes 4718600 | tf_op jit(solution)/shard_map/ppermute | solution.py:982
  695.7 19.3 %collective-permute-start.58 = (bf16[1536,256]{1,0:T(8,128)(2,1)S(1)}, bf16[1536,256]{1,0:T(8,128)(2,1)S(1)}, u32[]{:S(2)}, u32[]{:S(2)}) collective-permute-start(bf16[1536,256]{1,0:T(8,128)(2,1)S(1)} %get-tuple-element.211), channel_id=1, source_target_pairs={{1,0},{17,1},{3,2},{19,3},{5,4},{21,5},{7,6},{23,7},{9,8},{25,9},{... | collective-permute-start | bytes 2359304 | tf_op jit(solution)/shard_map/ppermute | solution.py:982
  722.1 5.2 collective-permute-start.59
  (59 other events, 753.6 us)
Sparse Core Ops, SparseCore 0:
  16.3 56.5 all-gather.2
  75.8 81.8 all-gather.4
  519.3 106.7 reduce-scatter.1

commit v11 on v9

--- a/solution.py
+++ b/solution.py
@@ -1167,7 +1167,7 @@
         (far[0], far[1], near[0], near[1]), grad_mixed
     )
     far_ffn = over_cores(far_f, far_f_other).astype(BF16)
-    ffn_y, ffn_x = far_links(far_ffn)
+    ffn_y, ffn_x = far_links(after(far_ffn, grad_w_output))
     near_ffn = over_cores(near_f, near_f_other)
     right, left = line_step(1, far_line)
     grad_other = after(grad_other, right, left, far_ffn, grad_w_output)

time: 740 us -> 738 us (level)
  transfers between devices with their start and end apart: 63 -> 63, of which waited for: 22 -> 20; matrix products, arithmetic and copies ran while one was open for 29% -> 29% of each run, Pallas kernels for 21% -> 21%
where the time goes in v11:
time: 738 us; the launch traced here: 733 us
  Pallas kernels  210 us (28%)
  waiting for transfers between devices  169 us (23%)
  starting transfers between devices  114 us (15%)
  other arithmetic  91.3 us (12%)
  matrix products  88.9 us (12%)
  local copies, waits for them, and re-layouts  44.3 us (6%)
  between operations  15.2 us (2%)
    pallas_call x2, Pallas kernels, run_experts(): pl.pallas_call(functools.partial(experts_kernel, tiles, tile // 2), grid_...  109 us
    dot_general x14, matrix products, contract(): lax.dot_general(left, right, (((left_dim,), (right_dim,)), ((), ())), pre...  82.7 us
    ppermute x15, waiting for transfers between devices, swap_seq(): return lax.ppermute(value, 'seq', [(0, 1), (1, 0)])  68.9 us
    pallas_call x1, Pallas kernels, attend_back(): pl.pallas_call(attend_back_kernel, grid=(pairs,), in_specs=[pair_block, w...  40.8 us
    ppermute x27, waiting for transfers between devices, swap_dp(): return lax.ppermute(value, 'dp', [(i, i ^ mask) for i in range(4 * LINE)])  33.4 us
    ppermute x4, waiting for transfers between devices, both_axes(): return lax.ppermute(value, ('seq', 'dp'), pairs)  33.4 us
    ppermute x7, starting transfers between devices, line_up(): return lax.ppermute(value, 'dp', [(i, i + 4) for i in range(4 * LINE - 4)])  33.3 us
    pallas_call x2, Pallas kernels, attend(): pl.pallas_call(functools.partial(attend_kernel, base), grid=(pairs,), in_...  30.1 us
  transfers between devices with their start and end apart: 63, of which 20 were waited for; matrix products, arithmetic and copies ran while one was open for 29% of the time, Pallas kernels for 21%

profile of v11, /device:TPU:1, one launch (start us, length us, event | category | flops | bytes accessed | tf_op | source)
XLA Modules:
  0.0 732.8 jit_solution(1034705281403738830)
XLA Ops:
  12.1 3.3 collective-permute-done.5
  18.4 4.5 collective-permute-start
  23.1 25.7 %collective-permute-done.1 = bf16[1536,256]{1,0:T(8,128)(2,1)} collective-permute-done((bf16[1536,256]{1,0:T(8,128)(2,1)}, bf16[1536,256]{1,0:T(8,128)(2,1)}, u32[]{:S(2)}, u32[]{:S(2)}) %collective-permute-start.1) | collective-permute-done | bytes 786464 | tf_op jit(solution)/shard_map/ppermute | solution.py:982
  50.2 4.6 collective-permute-start.3
  58.9 3.8 concatenate.95.refs_6_
  66.1 5.8 fusion.23
  71.9 21.8 %collective-permute-done.2 = bf16[512,1536]{1,0:T(8,128)(2,1)} collective-permute-done((bf16[512,1536]{1,0:T(8,128)(2,1)}, bf16[512,1536]{1,0:T(8,128)(2,1)}, u32[]{:S(2)}, u32[]{:S(2)}) %collective-permute-start.2) | collective-permute-done | bytes 1572896 | tf_op jit(solution)/shard_map/ppermute | solution.py:373
  98.8 6.7 add_convert_fusion.2.x_ref
  105.6 16.8 %collective-permute-done.3.refs_18_.refs_14_ = bf16[1536,768]{1,0:T(8,128)(2,1)} collective-permute-done((bf16[1536,768]{1,0:T(8,128)(2,1)S(1)}, bf16[1536,768]{1,0:T(8,128)(2,1)}, u32[]{:S(2)}, u32[]{:S(2)}) %collective-permute-start.3) | collective-permute-done | bytes 2359328 | tf_op jit(solution)/shard_map/ppermute | solution.py:389
  122.4 2.7 collective-permute-done.4.refs_20_.refs_16_
  125.1 3.9 collective-permute-start.10
  133.3 10.4 %project.1 = (bf16[1024,1536]{1,0:T(8,128)(2,1)}, bf16[1024,768]{1,0:T(8,128)(2,1)}, bf16[4,1024,64]{2,1,0:T(8,128)(2,1)}, bf16[4,1024,64]{2,1,0:T(8,128)(2,1)}) custom-call(bf16[1024,1536]{1,0:T(8,128)(2,1)} %add_convert_fusion.2.x_ref, f32[1,1536]{1,0:T(1,128)} %copy.116.gain_ref, bf16[1536,1408]{1,0:T(8,128)(2,1)} %bitcast.77, ...), custom_call_target="tpu_custom_call" | custom-call | flops 251658240 | bytes 3538944 | tf_op jit(solution)/shard_map/project/pallas_call | solution.py:492
  143.7 15.0 %attend.2 = (bf16[1024,384]{1,0:T(8,128)(2,1)}, f32[3,1024,2]{2,1,0:T(8,128)}) custom-call(bf16[1024,768]{1,0:T(8,128)(2,1)} %get-tuple-element.123.q_ref, bf16[4,1024,64]{2,1,0:T(8,128)(2,1)} %get-tuple-element.119.k_ref, bf16[4,1024,64]{2,1,0:T(8,128)(2,1)} %get-tuple-element.120.v_ref, s32[1024,1]{1,0:T(8,128)} %copy.117.start_ref), custom_call_target="tpu_custom_call" | custom-call | flops 113246208 | bytes 3145728 | tf_op jit(solution)/shard_map/attend/pallas_call | solution.py:617
  160.5 2.8 collective-permute-start.8
  163.4 15.0 %attend.3 = (bf16[1024,384]{1,0:T(8,128)(2,1)}, f32[3,1024,2]{2,1,0:T(8,128)}) custom-call(bf16[1024,768]{1,0:T(8,128)(2,1)} %get-tuple-element.123.q_ref, bf16[4,1024,64]{2,1,0:T(8,128)(2,1)} %get-tuple-element.119.k_ref, bf16[4,1024,64]{2,1,0:T(8,128)(2,1)} %get-tuple-element.120.v_ref, s32[1024,1]{1,0:T(8,128)} %copy.117.start_ref), custom_call_target="tpu_custom_call" | custom-call | flops 113246208 | bytes 3145728 | tf_op jit(solution)/shard_map/attend/pallas_call | solution.py:617
  192.5 5.2 collective-permute-start.26
  197.6 11.8 %collective-permute-start.27 = (bf16[1536,768]{1,0:T(8,128)(2,1)}, bf16[1536,768]{1,0:T(8,128)(2,1)}, u32[]{:S(2)}, u32[]{:S(2)}) collective-permute-start(bf16[1536,768]{1,0:T(8,128)(2,1)} %collective-permute-done.11.refs_21_.refs_17_), channel_id=1, source_target_pairs={{4,0},{5,1},{6,2},{7,3},{8,4},{9,5},{10,6},{11,7},{12,8},{13,9},{1... | collective-permute-start | bytes 7077896 | tf_op jit(solution)/shard_map/ppermute | solution.py:393
  209.4 6.2 multiply_reduce_fusion.2
  218.1 31.2 %collective-permute-done.14.refs_0_.refs_1_ = bf16[512,1536]{1,0:T(8,128)(2,1)} collective-permute-done((bf16[512,1536]{1,0:T(8,128)(2,1)S(1)}, bf16[512,1536]{1,0:T(8,128)(2,1)}, u32[]{:S(2)}, u32[]{:S(2)}) %collective-permute-start.14) | collective-permute-done | bytes 1572896 | tf_op jit(solution)/shard_map/ppermute | solution.py:373
  254.6 3.3 collective-permute-start.24
  258.5 8.0 %collective-permute-done.16.refs_2_ = bf16[256,1536]{1,0:T(8,128)(2,1)S(1)} collective-permute-done((bf16[256,1536]{1,0:T(8,128)(2,1)S(1)}, bf16[256,1536]{1,0:T(8,128)(2,1)S(1)}, u32[]{:S(2)}, u32[]{:S(2)}) %collective-permute-start.16) | collective-permute-done | bytes 786464 | tf_op jit(solution)/shard_map/ppermute | solution.py:377
  266.5 4.4 collective-permute-start.23
  276.8 2.6 select_select_fusion
  280.2 54.5 %experts.2 = (bf16[1024,1536]{1,0:T(8,128)(2,1)}, bf16[1024,1536]{1,0:T(8,128)(2,1)}, bf16[1024,1536]{1,0:T(8,128)(2,1)}, bf16[1024,1536]{1,0:T(8,128)(2,1)}, bf...) custom-call(s32[1]{0:T(128)} %bitcast.15.place_ref, ...), custom_call_target="tpu_custom_call" | custom-call | flops 2415919104 | bytes 50331648 | tf_op jit(solution)/shard_map/experts/pallas_call | solution.py:864
  335.6 7.8 %collective-permute-done.28 = bf16[1024,1536]{1,0:T(8,128)(2,1)S(1)} collective-permute-done((bf16[1024,1536]{1,0:T(8,128)(2,1)}, bf16[1024,1536]{1,0:T(8,128)(2,1)S(1)}, u32[]{:S(2)}, u32[]{:S(2)}) %collective-permute-start.28) | collective-permute-done | bytes 3145760 | tf_op jit(solution)/shard_map/ppermute | solution.py:377
  343.5 2.7 add_convert_fusion.1
  350.9 54.7 %experts.3 = (bf16[1024,1536]{1,0:T(8,128)(2,1)}, bf16[1024,1536]{1,0:T(8,128)(2,1)}, bf16[1024,1536]{1,0:T(8,128)(2,1)}, bf16[1024,1536]{1,0:T(8,128)(2,1)}, bf...) custom-call(s32[1]{0:T(128)} %bitcast.15.place_ref, ...), custom_call_target="tpu_custom_call", output_to_operand_aliasing={{4}: (21, {}), {5}: (22, {}), {6}: (23, {}), {7}: (24, {}),... | custom-call | flops 2415919104 | bytes 50331648 | tf_op jit(solution)/shard_map/experts/pallas_call | solution.py:864
  406.7 11.1 %fusion.11 = bf16[1536,512]{1,0:T(8,128)(2,1)S(1)} fusion(bf16[4096,1536]{1,0:T(8,128)(2,1)} %get-tuple-element.164, bf16[4096,512]{1,0:T(8,128)(2,1)} %get-tuple-element.157), kind=kOutput, calls=%fused_computation.40 | convolution fusion | flops 6444023808 | bytes 18350080 | tf_op jit(solution)/shard_map/dot_general | solution.py:575
  418.4 14.1 %convolution_convert_fusion.1 = bf16[1536,1024]{1,0:T(8,128)(2,1)S(1)} fusion(bf16[4096,1536]{1,0:T(8,128)(2,1)S(1)} %copy-done.11, bf16[4096,1024]{1,0:T(8,128)(2,1)S(1)} %copy-done.16), kind=kOutput, calls=%fused_computation.14 | convolution fusion | flops 12886474752 | bytes 24117248 | tf_op jit(solution)/shard_map/dot_general | solution.py:575
  434.6 5.0 collective-permute-start.38
  442.6 2.9 convert_add_fusion.1
  445.5 3.1 fusion.31
  449.3 16.2 %convolution_convert_fusion = bf16[1536,1024]{1,0:T(8,128)(2,1)S(1)} fusion(bf16[4096,1536]{1,0:T(8,128)(2,1)S(1)} %copy-done.11, bf16[4096,1024]{1,0:T(8,128)(2,1)} %get-tuple-element.163), kind=kOutput, calls=%fused_computation.13 | convolution fusion | flops 12886474752 | bytes 24117248 | tf_op jit(solution)/shard_map/dot_general | solution.py:575
  465.6 11.3 %fusion.12 = bf16[1536,512]{1,0:T(8,128)(2,1)S(1)} fusion(bf16[4096,1536]{1,0:T(8,128)(2,1)} %get-tuple-element.164, bf16[4096,512]{1,0:T(8,128)(2,1)} %get-tuple-element.165), kind=kOutput, calls=%fused_computation.41 | convolution fusion | flops 6444023808 | bytes 18350080 | tf_op jit(solution)/shard_map/dot_general | solution.py:575
  482.0 2.6 convolution_convert_fusion.2
  489.2 3.2 add_convert_fusion.6
  492.4 5.5 collective-permute-start.41
  498.0 3.3 add_convert_fusion.5
  502.7 4.4 fusion.48
  507.0 3.7 add_convert_fusion
  525.6 3.3 add_convert_fusion.7.d_ref
  529.0 40.8 %attend_back.1 = (bf16[1024,768]{1,0:T(8,128)(2,1)}, bf16[1024,256]{1,0:T(8,128)(2,1)}, bf16[1024,256]{1,0:T(8,128)(2,1)}) custom-call(bf16[1024,768]{1,0:T(8,128)(2,1)} %get-tuple-element.123.q_ref, bf16[4,1024,64]{2,1,0:T(8,128)(2,1)} %get-tuple-element.119.k_ref, bf16[4,1024,64]{2,1,0:T(8,128)(2,1)} %get-tuple-element.120.v_ref, ...), custom_call_target="tpu_custom_call" | custom-call | flops 566231040 | bytes 6291456 | tf_op jit(solution)/shard_map/attend_back/pallas_call | solution.py:694
  569.8 7.8 %add_convert_fusion.3 = (bf16[1536,768]{1,0:T(8,128)(2,1)}, bf16[1536,768]{1,0:T(8,128)(2,1)}) fusion(bf16[1536,768]{1,0:T(8,128)(2,1)} %collective-permute-done.42, pred[]{:T(512)S(6)} %lt.123, pred[]{:T(512)S(6)} %lt.122, bf16[1536,256]{1,0:T(8,128)(2,1)} %copy-done.8, bf16[1536,512]{1,0:T(8,128)(2,1)} %copy-done.2, bf16[1536,256]{1,0:T(8,128)(2,1)} %copy-done.10, ...), kind=kLoop, calls=%fused_computation.8 | loop fusion | flops 33030144 | bytes 18874372 | tf_op jit(solution)/shard_map/convert_element_type | solution.py:1157
  577.5 8.3 %qkv_grad.1 = bf16[2,2,2,4,48,1408]{5,4,3,2,1,0:T(8,128)(2,1)} custom-call(bf16[1024,1536]{1,0:T(8,128)(2,1)} %get-tuple-element.188.h_ref, bf16[1024,768]{1,0:T(8,128)(2,1)} %get-tuple-element.189.dq_ref, bf16[1024,256]{1,0:T(8,128)(2,1)} %get-tuple-element.190.dk_ref, bf16[1024,256]{1,0:T(8,128)(2,1)} %get-tuple-element.191.dv_ref, ...), custom_call_target="tpu_custom_call" | custom-call | flops 251658240 | bytes 1572864 | tf_op jit(solution)/shard_map/qkv_grad/pallas_call | solution.py:916
  587.8 3.3 collective-permute-start.47
  591.1 2.8 convert_add_fusion
  599.7 4.9 collective-permute-start.50
  607.7 9.2 %collective-permute-done.45 = bf16[256,1536]{1,0:T(8,128)(2,1)S(1)} collective-permute-done((bf16[256,1536]{1,0:T(8,128)(2,1)S(1)}, bf16[256,1536]{1,0:T(8,128)(2,1)S(1)}, u32[]{:S(2)}, u32[]{:S(2)}) %collective-permute-start.45) | collective-permute-done | bytes 786464 | tf_op jit(solution)/shard_map/ppermute | solution.py:373
  616.9 3.3 fusion.29
  622.8 11.2 %token_grad.1 = (bf16[512,1536]{1,0:T(8,128)(2,1)}, bf16[512,1536]{1,0:T(8,128)(2,1)}) custom-call(bf16[1024,768]{1,0:T(8,128)(2,1)} %get-tuple-element.189.dq_ref, bf16[1024,256]{1,0:T(8,128)(2,1)} %get-tuple-element.190.dk_ref, bf16[1024,256]{1,0:T(8,128)(2,1)} %get-tuple-element.191.dv_ref, bf16[1536,1408]{1,0:T(8,128)(2,1)} %bitcast.78, ...), custom_call_target="tpu_custom_call" | custom-call | flops 251658240 | bytes 1572864 | tf_op jit(solution)/shard_map/token_grad/pallas_call | solution.py:542
  637.3 3.0 collective-permute-done.51
  640.4 4.1 collective-permute-start.52
  645.7 5.2 select_convert_fusion
  651.0 3.2 fusion.27
  655.5 6.6 collective-permute-done.49
  663.6 4.6 collective-permute-done.52
  668.3 4.8 collective-permute-done.53
  673.1 4.4 fusion.16
  680.1 2.8 collective-permute-start.54
  684.8 5.9 collective-permute-start.57
  692.4 9.3 %collective-permute-done.55 = bf16[2,48,1408]{2,1,0:T(8,128)(2,1)S(1)} collective-permute-done((bf16[2,48,1408]{2,1,0:T(8,128)(2,1)S(1)}, bf16[2,48,1408]{2,1,0:T(8,128)(2,1)S(1)}, u32[]{:S(2)}, u32[]{:S(2)}) %collective-permute-start.55) | collective-permute-done | bytes 270368 | tf_op jit(solution)/shard_map/ppermute | solution.py:377
  701.9 3.0 fusion.2
  704.9 4.7 fusion.5
  710.8 6.4 collective-permute-done.57
  (313 shorter events, 132.8 us)
Async XLA Ops:
  7.2 123.1 %all-gather.3.cloned.1.call-start = ((), (), s32[]{:S(2)}) async-start(), calls=%async_computation.1 | async-start | bytes 4595712 | tf_op jit(solution)/shard_map/all_gather | solution.py:1004
  10.0 5.4 collective-permute-start.5
  16.2 193.2 %all-gather.5.cloned.1.call-start = ((), (), s32[]{:S(2)}) async-start(), calls=%async_computation.2 | async-start | bytes 4866048 | tf_op jit(solution)/shard_map/all_gather | solution.py:1005
  16.9 646.7 %reduce-scatter.2.cloned.1.call-start = ((), (), s32[]{:S(2)}) async-start(), calls=%async_computation.3 | async-start | bytes 4866048 | tf_op jit(solution)/shard_map/reduce_scatter | solution.py:1202
  18.4 30.4 %collective-permute-start = (bf16[1536,512]{1,0:T(8,128)(2,1)S(1)}, bf16[1536,512]{1,0:T(8,128)(2,1)S(1)}, u32[]{:S(2)}, u32[]{:S(2)}) collective-permute-start(bf16[1536,512]{1,0:T(8,128)(2,1)S(1)} %pad_maximum_fusion.6), channel_id=1, source_target_pairs={{0,0},{1,16},{2,2},{3,18},{4,4},{5,20},{6,6},{7,22},{8,8},{9,24},{... | collective-permute-start | bytes 4718600 | tf_op jit(solution)/shard_map/ppermute | solution.py:982
  22.9 25.9 %collective-permute-start.1 = (bf16[1536,256]{1,0:T(8,128)(2,1)}, bf16[1536,256]{1,0:T(8,128)(2,1)}, u32[]{:S(2)}, u32[]{:S(2)}) collective-permute-start(bf16[1536,256]{1,0:T(8,128)(2,1)} %get-tuple-element.306), channel_id=1, source_target_pairs={{0,1},{1,17},{2,3},{3,19},{4,5},{5,21},{6,7},{7,23},{8,9},{9,25},{... | collective-permute-start | bytes 2359304 | tf_op jit(solution)/shard_map/ppermute | solution.py:982
  50.2 72.1 %collective-permute-start.3 = (bf16[1536,768]{1,0:T(8,128)(2,1)S(1)}, bf16[1536,768]{1,0:T(8,128)(2,1)}, u32[]{:S(2)}, u32[]{:S(2)}) collective-permute-start(bf16[1536,768]{1,0:T(8,128)(2,1)S(1)} %pad_maximum_fusion.1.refs_19_.refs_15_), channel_id=1, source_target_pairs={{0,4},{1,5},{2,6},{3,7},{4,8},{5,9},{6,10},{7,11},{8,12},{9,13},{1... | collective-permute-start | bytes 7077896 | tf_op jit(solution)/shard_map/ppermute | solution.py:389
  54.8 70.2 %collective-permute-start.4 = (bf16[1536,768]{1,0:T(8,128)(2,1)S(1)}, bf16[1536,768]{1,0:T(8,128)(2,1)}, u32[]{:S(2)}, u32[]{:S(2)}) collective-permute-start(bf16[1536,768]{1,0:T(8,128)(2,1)S(1)} %pad_maximum_fusion.1.refs_19_.refs_15_), channel_id=1, source_target_pairs={{4,0},{5,1},{6,2},{7,3},{8,4},{9,5},{10,6},{11,7},{12,8},{13,9},{1... | collective-permute-start | bytes 7077896 | tf_op jit(solution)/shard_map/ppermute | solution.py:393
  56.1 37.6 %collective-permute-start.2 = (bf16[512,1536]{1,0:T(8,128)(2,1)}, bf16[512,1536]{1,0:T(8,128)(2,1)}, u32[]{:S(2)}, u32[]{:S(2)}) collective-permute-start(bf16[512,1536]{1,0:T(8,128)(2,1)} %param.17), channel_id=1, source_target_pairs={{0,16},{16,0},{1,17},{17,1},{2,18},{18,2},{3,19},{19,3},{4,20},{20... | collective-permute-start | bytes 4718600 | tf_op jit(solution)/shard_map/ppermute | solution.py:373
  62.6 100.8 %collective-permute-start.7 = (bf16[512,1664]{1,0:T(8,128)(2,1)}, bf16[512,1664]{1,0:T(8,128)(2,1)}, u32[]{:S(2)}, u32[]{:S(2)}) collective-permute-start(bf16[512,1664]{1,0:T(8,128)(2,1)} %concatenate.95.refs_6_), channel_id=1, source_target_pairs={{0,2},{1,3},{2,0},{3,1},{4,6},{5,7},{6,4},{7,5},{8,10},{9,11},{10,... | collective-permute-start | bytes 5111816 | tf_op jit(solution)/shard_map/ppermute | solution.py:377
  93.7 69.7 %collective-permute-start.6 = (bf16[512,1664]{1,0:T(8,128)(2,1)}, bf16[512,1664]{1,0:T(8,128)(2,1)}, u32[]{:S(2)}, u32[]{:S(2)}) collective-permute-start(bf16[512,1664]{1,0:T(8,128)(2,1)} %concatenate.95.refs_6_), channel_id=1, source_target_pairs={{0,16},{16,0},{1,17},{17,1},{2,18},{18,2},{3,19},{19,3},{4,20},{20... | collective-permute-start | bytes 5111816 | tf_op jit(solution)/shard_map/ppermute | solution.py:373
  125.1 67.4 %collective-permute-start.10 = (bf16[1536,768]{1,0:T(8,128)(2,1)}, bf16[1536,768]{1,0:T(8,128)(2,1)}, u32[]{:S(2)}, u32[]{:S(2)}) collective-permute-start(bf16[1536,768]{1,0:T(8,128)(2,1)} %collective-permute-done.3.refs_18_.refs_14_), channel_id=1, source_target_pairs={{0,4},{1,5},{2,6},{3,7},{4,8},{5,9},{6,10},{7,11},{8,12},{9,13},{1... | collective-permute-start | bytes 7077896 | tf_op jit(solution)/shard_map/ppermute | solution.py:389
  129.0 63.5 %collective-permute-start.11 = (bf16[1536,768]{1,0:T(8,128)(2,1)}, bf16[1536,768]{1,0:T(8,128)(2,1)}, u32[]{:S(2)}, u32[]{:S(2)}) collective-permute-start(bf16[1536,768]{1,0:T(8,128)(2,1)} %collective-permute-done.4.refs_20_.refs_16_), channel_id=1, source_target_pairs={{4,0},{5,1},{6,2},{7,3},{8,4},{9,5},{10,6},{11,7},{12,8},{13,9},{1... | collective-permute-start | bytes 7077896 | tf_op jit(solution)/shard_map/ppermute | solution.py:393
  160.5 26.4 %collective-permute-start.8 = (bf16[512,384]{0,1:T(8,128)(2,1)S(1)}, bf16[512,384]{0,1:T(8,128)(2,1)S(1)}, u32[]{:S(2)}, u32[]{:S(2)}) collective-permute-start(bf16[512,384]{0,1:T(8,128)(2,1)S(1)} %fusion.34), channel_id=1, source_target_pairs={{0,16},{16,0},{1,17},{17,1},{2,18},{18,2},{3,19},{19,3},{4,20},{20... | collective-permute-start | bytes 1179656 | tf_op jit(solution)/shard_map/ppermute | solution.py:373
  180.3 10.5 %collective-permute-start.9 = (bf16[512,384]{0,1:T(8,128)(2,1)S(1)}, bf16[512,384]{0,1:T(8,128)(2,1)S(1)}, u32[]{:S(2)}, u32[]{:S(2)}) collective-permute-start(bf16[512,384]{0,1:T(8,128)(2,1)S(1)} %fusion.35), channel_id=1, source_target_pairs={{0,16},{16,0},{1,17},{17,1},{2,18},{18,2},{3,19},{19,3},{4,20},{20... | collective-permute-start | bytes 1179656 | tf_op jit(solution)/shard_map/ppermute | solution.py:373
  183.2 32.9 %collective-permute-start.12 = (bf16[256,1664]{1,0:T(8,128)(2,1)}, bf16[256,1664]{1,0:T(8,128)(2,1)}, u32[]{:S(2)}, u32[]{:S(2)}) collective-permute-start(bf16[256,1664]{1,0:T(8,128)(2,1)} %slice.179), channel_id=1, source_target_pairs={{0,2},{1,3},{2,0},{3,1},{4,6},{5,7},{6,4},{7,5},{8,10},{9,11},{10,... | collective-permute-start | bytes 2555912 | tf_op jit(solution)/shard_map/ppermute | solution.py:377
  187.0 29.1 %collective-permute-start.13 = (bf16[256,1664]{1,0:T(8,128)(2,1)}, bf16[256,1664]{1,0:T(8,128)(2,1)}, u32[]{:S(2)}, u32[]{:S(2)}) collective-permute-start(bf16[256,1664]{1,0:T(8,128)(2,1)} %slice.180), channel_id=1, source_target_pairs={{0,16},{16,0},{1,17},{17,1},{2,18},{18,2},{3,19},{19,3},{4,20},{20... | collective-permute-start | bytes 2555912 | tf_op jit(solution)/shard_map/ppermute | solution.py:373
  192.5 65.5 %collective-permute-start.26 = (bf16[1536,768]{1,0:T(8,128)(2,1)}, bf16[1536,768]{1,0:T(8,128)(2,1)}, u32[]{:S(2)}, u32[]{:S(2)}) collective-permute-start(bf16[1536,768]{1,0:T(8,128)(2,1)} %collective-permute-done.10.refs_17_.refs_13_), channel_id=1, source_target_pairs={{0,4},{1,5},{2,6},{3,7},{4,8},{5,9},{6,10},{7,11},{8,12},{9,13},{1... | collective-permute-start | bytes 7077896 | tf_op jit(solution)/shard_map/ppermute | solution.py:389
  197.6 60.3 %collective-permute-start.27 = (bf16[1536,768]{1,0:T(8,128)(2,1)}, bf16[1536,768]{1,0:T(8,128)(2,1)}, u32[]{:S(2)}, u32[]{:S(2)}) collective-permute-start(bf16[1536,768]{1,0:T(8,128)(2,1)} %collective-permute-done.11.refs_21_.refs_17_), channel_id=1, source_target_pairs={{4,0},{5,1},{6,2},{7,3},{8,4},{9,5},{10,6},{11,7},{12,8},{13,9},{1... | collective-permute-start | bytes 7077896 | tf_op jit(solution)/shard_map/ppermute | solution.py:393
  216.1 33.2 %collective-permute-start.14 = (bf16[512,1536]{1,0:T(8,128)(2,1)S(1)}, bf16[512,1536]{1,0:T(8,128)(2,1)}, u32[]{:S(2)}, u32[]{:S(2)}) collective-permute-start(bf16[512,1536]{1,0:T(8,128)(2,1)S(1)} %multiply_convert_fusion.1.refs_0_), channel_id=1, source_target_pairs={{0,16},{16,0},{1,17},{17,1},{2,18},{18,2},{3,19},{19,3},{4,20},{20... | collective-permute-start | bytes 4718600 | tf_op jit(solution)/shard_map/ppermute | solution.py:373
  217.2 34.2 %collective-permute-start.15 = (bf16[512,1536]{1,0:T(8,128)(2,1)S(1)}, bf16[512,1536]{1,0:T(8,128)(2,1)}, u32[]{:S(2)}, u32[]{:S(2)}) collective-permute-start(bf16[512,1536]{1,0:T(8,128)(2,1)S(1)} %multiply_convert_fusion.1.refs_0_), channel_id=1, source_target_pairs={{0,2},{1,3},{2,0},{3,1},{4,6},{5,7},{6,4},{7,5},{8,10},{9,11},{10,... | collective-permute-start | bytes 4718600 | tf_op jit(solution)/shard_map/ppermute | solution.py:377
  250.5 15.9 %collective-permute-start.16 = (bf16[256,1536]{1,0:T(8,128)(2,1)S(1)}, bf16[256,1536]{1,0:T(8,128)(2,1)S(1)}, u32[]{:S(2)}, u32[]{:S(2)}) collective-permute-start(bf16[256,1536]{1,0:T(8,128)(2,1)S(1)} %slice.233), channel_id=1, source_target_pairs={{0,2},{1,3},{2,0},{3,1},{4,6},{5,7},{6,4},{7,5},{8,10},{9,11},{10,... | collective-permute-start | bytes 2359304 | tf_op jit(solution)/shard_map/ppermute | solution.py:377
  252.6 18.3 %collective-permute-start.17 = (bf16[256,1536]{1,0:T(8,128)(2,1)S(1)}, bf16[256,1536]{1,0:T(8,128)(2,1)S(1)}, u32[]{:S(2)}, u32[]{:S(2)}) collective-permute-start(bf16[256,1536]{1,0:T(8,128)(2,1)S(1)} %slice.234), channel_id=1, source_target_pairs={{0,16},{16,0},{1,17},{17,1},{2,18},{18,2},{3,19},{19,3},{4,20},{20... | collective-permute-start | bytes 2359304 | tf_op jit(solution)/shard_map/ppermute | solution.py:373
  254.6 18.5 %collective-permute-start.24 = (bf16[256,1664]{1,0:T(8,128)(2,1)}, bf16[256,1664]{1,0:T(8,128)(2,1)}, u32[]{:S(2)}, u32[]{:S(2)}) collective-permute-start(bf16[256,1664]{1,0:T(8,128)(2,1)} %collective-permute-done.12.refs_10_), channel_id=1, source_target_pairs={{0,1},{1,0},{2,3},{3,2},{4,5},{5,4},{6,7},{7,6},{8,9},{9,8},{10,11... | collective-permute-start | bytes 2555912 | tf_op jit(solution)/shard_map/ppermute | solution.py:377
  257.9 18.1 %collective-permute-start.18 = (bf16[512,1536]{1,0:T(8,128)(2,1)}, bf16[512,1536]{1,0:T(8,128)(2,1)}, u32[]{:S(2)}, u32[]{:S(2)}) collective-permute-start(bf16[512,1536]{1,0:T(8,128)(2,1)} %collective-permute-done.14.refs_0_.refs_1_), channel_id=1, source_target_pairs={{0,1},{1,0},{2,3},{3,2},{4,5},{5,4},{6,7},{7,6},{8,9},{9,8},{10,11... | collective-permute-start | bytes 4718600 | tf_op jit(solution)/shard_map/ppermute | solution.py:377
  258.0 22.3 %collective-permute-start.22 = (bf16[512,1664]{1,0:T(8,128)(2,1)}, bf16[512,1664]{1,0:T(8,128)(2,1)}, u32[]{:S(2)}, u32[]{:S(2)}) collective-permute-start(bf16[512,1664]{1,0:T(8,128)(2,1)} %collective-permute-done.6.refs_8_.refs_7_), channel_id=1, source_target_pairs={{0,1},{1,0},{2,3},{3,2},{4,5},{5,4},{6,7},{7,6},{8,9},{9,8},{10,11... | collective-permute-start | bytes 5111816 | tf_op jit(solution)/shard_map/ppermute | solution.py:377
  266.5 13.8 %collective-permute-start.23 = (bf16[512,1664]{1,0:T(8,128)(2,1)}, bf16[512,1664]{1,0:T(8,128)(2,1)}, u32[]{:S(2)}, u32[]{:S(2)}) collective-permute-start(bf16[512,1664]{1,0:T(8,128)(2,1)} %collective-permute-done.7.refs_9_.refs_8_), channel_id=1, source_target_pairs={{0,1},{1,0},{2,3},{3,2},{4,5},{5,4},{6,7},{7,6},{8,9},{9,8},{10,11... | collective-permute-start | bytes 5111816 | tf_op jit(solution)/shard_map/ppermute | solution.py:377
  270.9 4.8 collective-permute-start.25
  273.1 7.1 collective-permute-start.19
  275.6 4.6 collective-permute-start.20
  276.0 4.2 collective-permute-start.21
  334.7 8.8 %collective-permute-start.28 = (bf16[1024,1536]{1,0:T(8,128)(2,1)}, bf16[1024,1536]{1,0:T(8,128)(2,1)S(1)}, u32[]{:S(2)}, u32[]{:S(2)}) collective-permute-start(bf16[1024,1536]{1,0:T(8,128)(2,1)} %get-tuple-element.140), channel_id=1, source_target_pairs={{0,1},{1,0},{2,3},{3,2},{4,5},{5,4},{6,7},{7,6},{8,9},{9,8},{10,11... | collective-permute-start | bytes 9437192 | tf_op jit(solution)/shard_map/ppermute | solution.py:377
  335.1 15.8 %collective-permute-start.29 = (bf16[512,1536]{1,0:T(8,128)(2,1)}, bf16[512,1536]{1,0:T(8,128)(2,1)}, u32[]{:S(2)}, u32[]{:S(2)}) collective-permute-start(bf16[512,1536]{1,0:T(8,128)(2,1)} %copy-done.21), channel_id=1, source_target_pairs={{0,1},{1,0},{2,3},{3,2},{4,5},{5,4},{6,7},{7,6},{8,9},{9,8},{10,11... | collective-permute-start | bytes 4718600 | tf_op jit(solution)/shard_map/ppermute | solution.py:377
  335.3 15.6 %collective-permute-start.30 = (bf16[512,1664]{1,0:T(8,128)(2,1)}, bf16[512,1664]{1,0:T(8,128)(2,1)}, u32[]{:S(2)}, u32[]{:S(2)}) collective-permute-start(bf16[512,1664]{1,0:T(8,128)(2,1)} %concatenate.95.refs_6_), channel_id=1, source_target_pairs={{0,1},{1,0},{2,3},{3,2},{4,5},{5,4},{6,7},{7,6},{8,9},{9,8},{10,11... | collective-permute-start | bytes 5111816 | tf_op jit(solution)/shard_map/ppermute | solution.py:377
  348.1 58.6 %collective-permute-start.31 = (bf16[512,1536]{1,0:T(8,128)(2,1)}, bf16[512,1536]{1,0:T(8,128)(2,1)}, u32[]{:S(2)}, u32[]{:S(2)}) collective-permute-start(bf16[512,1536]{1,0:T(8,128)(2,1)} %get-tuple-element.287), channel_id=1, source_target_pairs={{0,2},{1,3},{2,0},{3,1},{4,6},{5,7},{6,4},{7,5},{8,10},{9,11},{10,... | collective-permute-start | bytes 4718600 | tf_op jit(solution)/shard_map/ppermute | solution.py:377
  349.6 57.0 %collective-permute-start.32 = (bf16[512,1536]{1,0:T(8,128)(2,1)}, bf16[512,1536]{1,0:T(8,128)(2,1)}, u32[]{:S(2)}, u32[]{:S(2)}) collective-permute-start(bf16[512,1536]{1,0:T(8,128)(2,1)} %get-tuple-element.286), channel_id=1, source_target_pairs={{0,16},{16,0},{1,17},{17,1},{2,18},{18,2},{3,19},{19,3},{4,20},{20... | collective-permute-start | bytes 4718600 | tf_op jit(solution)/shard_map/ppermute | solution.py:373
  405.6 37.0 %collective-permute-start.33 = (bf16[1024,1536]{1,0:T(8,128)(2,1)}, bf16[1024,1536]{1,0:T(8,128)(2,1)}, u32[]{:S(2)}, u32[]{:S(2)}) collective-permute-start(bf16[1024,1536]{1,0:T(8,128)(2,1)} %get-tuple-element.159), channel_id=1, source_target_pairs={{0,1},{1,0},{2,3},{3,2},{4,5},{5,4},{6,7},{7,6},{8,9},{9,8},{10,11... | collective-permute-start | bytes 9437192 | tf_op jit(solution)/shard_map/ppermute | solution.py:377
  417.8 80.1 %copy-start.8 = (bf16[1536,256]{1,0:T(8,128)(2,1)}, bf16[1536,256]{1,0:T(8,128)(2,1)S(1)}, u32[]{:S(2)}) copy-start(bf16[1536,256]{1,0:T(8,128)(2,1)S(1)} %get-tuple-element.302) | copy-start | bytes 2359300
  434.6 54.6 %collective-permute-start.38 = (bf16[1536,768]{1,0:T(8,128)(2,1)}, bf16[1536,768]{1,0:T(8,128)(2,1)}, u32[]{:S(2)}, u32[]{:S(2)}) collective-permute-start(bf16[1536,768]{1,0:T(8,128)(2,1)} %pad_maximum_fusion.3), channel_id=1, source_target_pairs={{0,4},{1,5},{2,6},{3,7},{4,8},{5,9},{6,10},{7,11},{8,12},{9,13},{1... | collective-permute-start | bytes 7077896 | tf_op jit(solution)/shard_map/ppermute | solution.py:389
  441.2 56.8 %collective-permute-start.39 = (bf16[1536,768]{1,0:T(8,128)(2,1)}, bf16[1536,768]{1,0:T(8,128)(2,1)}, u32[]{:S(2)}, u32[]{:S(2)}) collective-permute-start(bf16[1536,768]{1,0:T(8,128)(2,1)} %pad_maximum_fusion.2), channel_id=1, source_target_pairs={{4,0},{5,1},{6,2},{7,3},{8,4},{9,5},{10,6},{11,7},{12,8},{13,9},{1... | collective-permute-start | bytes 7077896 | tf_op jit(solution)/shard_map/ppermute | solution.py:393
  448.6 28.3 %collective-permute-start.34 = (bf16[256,1536]{1,0:T(8,128)(2,1)}, bf16[256,1536]{1,0:T(8,128)(2,1)S(1)}, u32[]{:S(2)}, u32[]{:S(2)}) collective-permute-start(bf16[256,1536]{1,0:T(8,128)(2,1)} %get-tuple-element.274), channel_id=1, source_target_pairs={{0,16},{16,0},{1,17},{17,1},{2,18},{18,2},{3,19},{19,3},{4,20},{20... | collective-permute-start | bytes 2359304 | tf_op jit(solution)/shard_map/ppermute | solution.py:373
  448.8 28.1 %collective-permute-start.35 = (bf16[256,1536]{1,0:T(8,128)(2,1)}, bf16[256,1536]{1,0:T(8,128)(2,1)S(1)}, u32[]{:S(2)}, u32[]{:S(2)}) collective-permute-start(bf16[256,1536]{1,0:T(8,128)(2,1)} %get-tuple-element.275), channel_id=1, source_target_pairs={{0,2},{1,3},{2,0},{3,1},{4,6},{5,7},{6,4},{7,5},{8,10},{9,11},{10,... | collective-permute-start | bytes 2359304 | tf_op jit(solution)/shard_map/ppermute | solution.py:377
  484.7 22.3 %collective-permute-start.40 = (bf16[1024,1536]{1,0:T(8,128)(2,1)}, bf16[1024,1536]{1,0:T(8,128)(2,1)}, u32[]{:S(2)}, u32[]{:S(2)}) collective-permute-start(bf16[1024,1536]{1,0:T(8,128)(2,1)} %get-tuple-element.170), channel_id=1, source_target_pairs={{0,1},{1,0},{2,3},{3,2},{4,5},{5,4},{6,7},{7,6},{8,9},{9,8},{10,11... | collective-permute-start | bytes 9437192 | tf_op jit(solution)/shard_map/ppermute | solution.py:377
  486.0 105.1 %collective-permute-start.36 = (bf16[1024,1536]{1,0:T(8,128)(2,1)}, bf16[1024,1536]{1,0:T(8,128)(2,1)}, u32[]{:S(2)}, u32[]{:S(2)}) collective-permute-start(bf16[1024,1536]{1,0:T(8,128)(2,1)} %get-tuple-element.168), channel_id=1, source_target_pairs={{0,1},{1,0},{2,3},{3,2},{4,5},{5,4},{6,7},{7,6},{8,9},{9,8},{10,11... | collective-permute-start | bytes 9437192 | tf_op jit(solution)/shard_map/ppermute | solution.py:377
  487.3 26.0 %collective-permute-start.37 = (bf16[512,768]{1,0:T(8,128)(2,1)}, bf16[512,768]{1,0:T(8,128)(2,1)}, u32[]{:S(2)}, u32[]{:S(2)}) collective-permute-start(bf16[512,768]{1,0:T(8,128)(2,1)} %constant_dynamic-slice_fusion), channel_id=1, source_target_pairs={{0,16},{16,0},{1,17},{17,1},{2,18},{18,2},{3,19},{19,3},{4,20},{20... | collective-permute-start | bytes 2359304 | tf_op jit(solution)/shard_map/ppermute | solution.py:373
  492.4 77.3 %collective-permute-start.41 = (bf16[1536,768]{1,0:T(8,128)(2,1)}, bf16[1536,768]{1,0:T(8,128)(2,1)}, u32[]{:S(2)}, u32[]{:S(2)}) collective-permute-start(bf16[1536,768]{1,0:T(8,128)(2,1)} %add_convert_fusion.6), channel_id=1, source_target_pairs={{0,4},{1,5},{2,6},{3,7},{4,8},{5,9},{6,10},{7,11},{8,12},{9,13},{1... | collective-permute-start | bytes 7077896 | tf_op jit(solution)/shard_map/ppermute | solution.py:389
  501.3 68.4 %collective-permute-start.42 = (bf16[1536,768]{1,0:T(8,128)(2,1)}, bf16[1536,768]{1,0:T(8,128)(2,1)}, u32[]{:S(2)}, u32[]{:S(2)}) collective-permute-start(bf16[1536,768]{1,0:T(8,128)(2,1)} %add_convert_fusion.5), channel_id=1, source_target_pairs={{4,0},{5,1},{6,2},{7,3},{8,4},{9,5},{10,6},{11,7},{12,8},{13,9},{1... | collective-permute-start | bytes 7077896 | tf_op jit(solution)/shard_map/ppermute | solution.py:393
  512.6 57.2 %collective-permute-start.43 = (bf16[512,1536]{1,0:T(8,128)(2,1)}, bf16[512,1536]{1,0:T(8,128)(2,1)}, u32[]{:S(2)}, u32[]{:S(2)}) collective-permute-start(bf16[512,1536]{1,0:T(8,128)(2,1)} %get-tuple-element.281), channel_id=1, source_target_pairs={{0,2},{1,3},{2,0},{3,1},{4,6},{5,7},{6,4},{7,5},{8,10},{9,11},{10,... | collective-permute-start | bytes 4718600 | tf_op jit(solution)/shard_map/ppermute | solution.py:377
  513.3 56.5 %collective-permute-start.44 = (bf16[512,1536]{1,0:T(8,128)(2,1)}, bf16[512,1536]{1,0:T(8,128)(2,1)}, u32[]{:S(2)}, u32[]{:S(2)}) collective-permute-start(bf16[512,1536]{1,0:T(8,128)(2,1)} %get-tuple-element.280), channel_id=1, source_target_pairs={{0,16},{16,0},{1,17},{17,1},{2,18},{18,2},{3,19},{19,3},{4,20},{20... | collective-permute-start | bytes 4718600 | tf_op jit(solution)/shard_map/ppermute | solution.py:373
  587.8 32.5 %collective-permute-start.47 = (bf16[2,2,4,48,1408]{4,3,2,1,0:T(8,128)(2,1)S(1)}, bf16[2,2,4,48,1408]{4,3,2,1,0:T(8,128)(2,1)S(1)}, u32[]{:S(2)}, u32[]{:S(2)}) collective-permute-start(bf16[2,2,4,48,1408]{4,3,2,1,0:T(8,128)(2,1)S(1)} %dynamic-slice_bitcast_fusion), channel_id=1, source_target_pairs={{0,1},{1,0},{2,3},{3,2},{4,5},{5,4},{6,7},{7,6},{8,9},{9,8},{10,11... | collective-permute-start | bytes 6488072 | tf_op jit(solution)/shard_map/ppermute | solution.py:377
  596.0 20.8 %collective-permute-start.45 = (bf16[256,1536]{1,0:T(8,128)(2,1)S(1)}, bf16[256,1536]{1,0:T(8,128)(2,1)S(1)}, u32[]{:S(2)}, u32[]{:S(2)}) collective-permute-start(bf16[256,1536]{1,0:T(8,128)(2,1)S(1)} %fusion.28), channel_id=1, source_target_pairs={{0,16},{16,0},{1,17},{17,1},{2,18},{18,2},{3,19},{19,3},{4,20},{20... | collective-permute-start | bytes 2359304 | tf_op jit(solution)/shard_map/ppermute | solution.py:373
  599.7 37.6 %collective-permute-start.50 = (bf16[768,768]{1,0:T(8,128)(2,1)}, bf16[768,768]{1,0:T(8,128)(2,1)}, u32[]{:S(2)}, u32[]{:S(2)}) collective-permute-start(bf16[768,768]{1,0:T(8,128)(2,1)} %get-tuple-element.295), channel_id=1, source_target_pairs={{0,4},{1,5},{2,6},{3,7},{4,8},{5,9},{6,10},{7,11},{8,12},{9,13},{1... | collective-permute-start | bytes 3538952 | tf_op jit(solution)/shard_map/ppermute | solution.py:389
  606.2 34.2 %collective-permute-start.51 = (bf16[768,768]{1,0:T(8,128)(2,1)}, bf16[768,768]{1,0:T(8,128)(2,1)}, u32[]{:S(2)}, u32[]{:S(2)}) collective-permute-start(bf16[768,768]{1,0:T(8,128)(2,1)} %get-tuple-element.293), channel_id=1, source_target_pairs={{4,0},{5,1},{6,2},{7,3},{8,4},{9,5},{10,6},{11,7},{12,8},{13,9},{1... | collective-permute-start | bytes 3538952 | tf_op jit(solution)/shard_map/ppermute | solution.py:393
  620.1 30.8 %collective-permute-start.46 = (bf16[256,1536]{1,0:T(8,128)(2,1)}, bf16[256,1536]{1,0:T(8,128)(2,1)}, u32[]{:S(2)}, u32[]{:S(2)}) collective-permute-start(bf16[256,1536]{1,0:T(8,128)(2,1)} %get-tuple-element.271), channel_id=1, source_target_pairs={{0,2},{1,3},{2,0},{3,1},{4,6},{5,7},{6,4},{7,5},{8,10},{9,11},{10,... | collective-permute-start | bytes 2359304 | tf_op jit(solution)/shard_map/ppermute | solution.py:377
  636.0 26.1 %collective-permute-start.49 = (bf16[2,4,48,1408]{3,2,1,0:T(8,128)(2,1)S(1)}, bf16[2,4,48,1408]{3,2,1,0:T(8,128)(2,1)S(1)}, u32[]{:S(2)}, u32[]{:S(2)}) collective-permute-start(bf16[2,4,48,1408]{3,2,1,0:T(8,128)(2,1)S(1)} %fusion.36), channel_id=1, source_target_pairs={{0,2},{1,3},{2,0},{3,1},{4,6},{5,7},{6,4},{7,5},{8,10},{9,11},{10,... | collective-permute-start | bytes 3244040 | tf_op jit(solution)/shard_map/ppermute | solution.py:377
  640.4 27.9 %collective-permute-start.52 = (bf16[768,768]{1,0:T(8,128)(2,1)}, bf16[768,768]{1,0:T(8,128)(2,1)}, u32[]{:S(2)}, u32[]{:S(2)}) collective-permute-start(bf16[768,768]{1,0:T(8,128)(2,1)} %get-tuple-element.196), channel_id=1, source_target_pairs={{0,4},{1,5},{2,6},{3,7},{4,8},{5,9},{6,10},{7,11},{8,12},{9,13},{1... | collective-permute-start | bytes 3538952 | tf_op jit(solution)/shard_map/ppermute | solution.py:389
  644.4 28.6 %collective-permute-start.53 = (bf16[768,768]{1,0:T(8,128)(2,1)}, bf16[768,768]{1,0:T(8,128)(2,1)}, u32[]{:S(2)}, u32[]{:S(2)}) collective-permute-start(bf16[768,768]{1,0:T(8,128)(2,1)} %get-tuple-element.197), channel_id=1, source_target_pairs={{4,0},{5,1},{6,2},{7,3},{8,4},{9,5},{10,6},{11,7},{12,8},{13,9},{1... | collective-permute-start | bytes 3538952 | tf_op jit(solution)/shard_map/ppermute | solution.py:393
  654.2 47.7 %collective-permute-start.48 = (bf16[512,1536]{1,0:T(8,128)(2,1)}, bf16[512,1536]{1,0:T(8,128)(2,1)}, u32[]{:S(2)}, u32[]{:S(2)}) collective-permute-start(bf16[512,1536]{1,0:T(8,128)(2,1)} %get-tuple-element.194), channel_id=1, source_target_pairs={{0,16},{16,0},{1,17},{17,1},{2,18},{18,2},{3,19},{19,3},{4,20},{20... | collective-permute-start | bytes 4718600 | tf_op jit(solution)/shard_map/ppermute | solution.py:373
  679.1 12.4 %collective-permute-start.56 = (bf16[2,48,1408]{2,1,0:T(8,128)(2,1)S(1)}, bf16[2,48,1408]{2,1,0:T(8,128)(2,1)S(1)}, u32[]{:S(2)}, u32[]{:S(2)}) collective-permute-start(bf16[2,48,1408]{2,1,0:T(8,128)(2,1)S(1)} %fusion.51), channel_id=1, source_target_pairs={{0,12},{1,13},{2,14},{3,15},{4,8},{5,9},{6,10},{7,11},{8,4},{9,5},... | collective-permute-start | bytes 811016 | tf_op jit(solution)/shard_map/ppermute | solution.py:377
  679.3 22.5 %collective-permute-start.55 = (bf16[2,48,1408]{2,1,0:T(8,128)(2,1)S(1)}, bf16[2,48,1408]{2,1,0:T(8,128)(2,1)S(1)}, u32[]{:S(2)}, u32[]{:S(2)}) collective-permute-start(bf16[2,48,1408]{2,1,0:T(8,128)(2,1)S(1)} %get-tuple-element.309), channel_id=1, source_target_pairs={{0,8},{1,9},{2,10},{3,11},{4,12},{5,13},{6,14},{7,15},{8,0},{9,1},... | collective-permute-start | bytes 811016 | tf_op jit(solution)/shard_map/ppermute | solution.py:377
  680.1 21.6 %collective-permute-start.54 = (bf16[2,48,1408]{2,1,0:T(8,128)(2,1)S(1)}, bf16[2,48,1408]{2,1,0:T(8,128)(2,1)S(1)}, u32[]{:S(2)}, u32[]{:S(2)}) collective-permute-start(bf16[2,48,1408]{2,1,0:T(8,128)(2,1)S(1)} %get-tuple-element.308), channel_id=1, source_target_pairs={{0,4},{1,5},{2,6},{3,7},{4,0},{5,1},{6,2},{7,3},{8,12},{9,13},{10,... | collective-permute-start | bytes 811016 | tf_op jit(solution)/shard_map/ppermute | solution.py:377
  684.8 32.5 %collective-permute-start.57 = (bf16[1536,512]{1,0:T(8,128)(2,1)S(1)}, bf16[1536,512]{1,0:T(8,128)(2,1)S(1)}, u32[]{:S(2)}, u32[]{:S(2)}) collective-permute-start(bf16[1536,512]{1,0:T(8,128)(2,1)S(1)} %fusion.25), channel_id=1, source_target_pairs={{0,0},{1,16},{2,2},{3,18},{4,4},{5,20},{6,6},{7,22},{8,8},{9,24},{... | collective-permute-start | bytes 4718600 | tf_op jit(solution)/shard_map/ppermute | solution.py:982
  691.5 19.3 %collective-permute-start.58 = (bf16[1536,256]{1,0:T(8,128)(2,1)S(1)}, bf16[1536,256]{1,0:T(8,128)(2,1)S(1)}, u32[]{:S(2)}, u32[]{:S(2)}) collective-permute-start(bf16[1536,256]{1,0:T(8,128)(2,1)S(1)} %get-tuple-element.205), channel_id=1, source_target_pairs={{1,0},{17,1},{3,2},{19,3},{5,4},{21,5},{7,6},{23,7},{9,8},{25,9},{... | collective-permute-start | bytes 2359304 | tf_op jit(solution)/shard_map/ppermute | solution.py:982
  717.3 5.2 collective-permute-start.59
  (52 other events, 799.8 us)
Sparse Core Ops, SparseCore 0:
  16.3 56.5 all-gather.2
  75.8 81.8 all-gather.4
  523.0 109.2 reduce-scatter.1

commit v12 on v11

--- a/solution.py
+++ b/solution.py
@@ -1190,8 +1190,6 @@
     last_first = (line_up(right[:cut]), line_down(left[:cut]))
     first_ffn, second_ffn = near_links(near_ffn, ffn_y, ffn_x)
     first_ffn, second_ffn = swap_seq(first_ffn), swap_y(second_ffn)
-    ffn = own_sum(near_ffn, ffn_y, ffn_x, first_ffn, second_ffn)
-    output = (middle + BRANCH_SCALE * ffn).astype(BF16)
     grads_qkv = after((grad_query, grad_keys, grad_values), right, left)
     wide = qkv_grad(normed, grads_qkv, grad_gain_two[None, :], shard)
 
@@ -1209,6 +1207,9 @@
         grads_late, w_qkv, own_places[:, None], other_places[:, None]
     )
     kept, sent_normed = lax.optimization_barrier((kept, sent_normed))
+    first_ffn, second_ffn = after((first_ffn, second_ffn), sent_normed)
+    ffn = own_sum(near_ffn, ffn_y, ffn_x, first_ffn, second_ffn)
+    output = (middle + BRANCH_SCALE * ffn).astype(BF16)
     right_late, left_late = after((right[cut:], left[cut:]), last_first, sent_normed)
     last_late = (line_up(right_late), line_down(left_late))
     grad_normed = grad_normed.astype(F32) + swap_seq(sent_normed).astype(F32)

time: 738 us -> 739 us (level)
    ppermute x7, waiting for transfers between devices: 21.9 us -> 31.3 us  [line_up(): return lax.ppermute(value, 'dp', [(i, i + 4) for i in range(4 * LINE - 4)])]
    ppermute x15, waiting for transfers between devices: 68.9 us -> 59.8 us  [swap_seq(): return lax.ppermute(value, 'seq', [(0, 1), (1, 0)])]
  transfers between devices with their start and end apart: 63 -> 63, of which waited for: 20 -> 20; matrix products, arithmetic and copies ran while one was open for 29% -> 30% of each run, Pallas kernels for 21% -> 21%
where the time goes in v12:
time: 739 us; the launch traced here: 733 us
  Pallas kernels  210 us (28%)
  waiting for transfers between devices  167 us (23%)
  starting transfers between devices  111 us (15%)
  other arithmetic  95.8 us (13%)
  matrix products  88.9 us (12%)
  local copies, waits for them, and re-layouts  44.7 us (6%)
  between operations  15.2 us (2%)
    pallas_call x2, Pallas kernels, run_experts(): pl.pallas_call(functools.partial(experts_kernel, tiles, tile // 2), grid_...  109 us
    dot_general x14, matrix products, contract(): lax.dot_general(left, right, (((left_dim,), (right_dim,)), ((), ())), pre...  82.7 us
    ppermute x15, waiting for transfers between devices, swap_seq(): return lax.ppermute(value, 'seq', [(0, 1), (1, 0)])  59.8 us
    pallas_call x1, Pallas kernels, attend_back(): pl.pallas_call(attend_back_kernel, grid=(pairs,), in_specs=[pair_block, w...  40.8 us
    ppermute x4, waiting for transfers between devices, both_axes(): return lax.ppermute(value, ('seq', 'dp'), pairs)  33.6 us
    ppermute x7, starting transfers between devices, line_up(): return lax.ppermute(value, 'dp', [(i, i + 4) for i in range(4 * LINE - 4)])  32.4 us
    ppermute x7, waiting for transfers between devices, line_up(): return lax.ppermute(value, 'dp', [(i, i + 4) for i in range(4 * LINE - 4)])  31.3 us
    pallas_call x2, Pallas kernels, attend(): pl.pallas_call(functools.partial(attend_kernel, base), grid=(pairs,), in_...  30.1 us
  transfers between devices with their start and end apart: 63, of which 20 were waited for; matrix products, arithmetic and copies ran while one was open for 30% of the time, Pallas kernels for 21%

profile of v12, /device:TPU:1, one launch (start us, length us, event | category | flops | bytes accessed | tf_op | source)
XLA Modules:
  0.0 732.8 jit_solution(8049039033191308849)
XLA Ops:
  12.1 3.3 collective-permute-done.5
  18.4 4.5 collective-permute-start
  23.1 25.7 %collective-permute-done.1 = bf16[1536,256]{1,0:T(8,128)(2,1)} collective-permute-done((bf16[1536,256]{1,0:T(8,128)(2,1)}, bf16[1536,256]{1,0:T(8,128)(2,1)}, u32[]{:S(2)}, u32[]{:S(2)}) %collective-permute-start.1) | collective-permute-done | bytes 786464 | tf_op jit(solution)/shard_map/ppermute | solution.py:982
  50.2 4.6 collective-permute-start.3
  58.9 3.8 concatenate.95.refs_6_
  66.1 5.8 fusion.23
  71.9 21.8 %collective-permute-done.2 = bf16[512,1536]{1,0:T(8,128)(2,1)} collective-permute-done((bf16[512,1536]{1,0:T(8,128)(2,1)}, bf16[512,1536]{1,0:T(8,128)(2,1)}, u32[]{:S(2)}, u32[]{:S(2)}) %collective-permute-start.2) | collective-permute-done | bytes 1572896 | tf_op jit(solution)/shard_map/ppermute | solution.py:373
  98.9 6.7 add_convert_fusion.2.x_ref
  105.6 16.8 %collective-permute-done.3.refs_18_.refs_14_ = bf16[1536,768]{1,0:T(8,128)(2,1)} collective-permute-done((bf16[1536,768]{1,0:T(8,128)(2,1)S(1)}, bf16[1536,768]{1,0:T(8,128)(2,1)}, u32[]{:S(2)}, u32[]{:S(2)}) %collective-permute-start.3) | collective-permute-done | bytes 2359328 | tf_op jit(solution)/shard_map/ppermute | solution.py:389
  122.4 2.7 collective-permute-done.4.refs_20_.refs_16_
  125.1 3.9 collective-permute-start.10
  133.3 10.4 %project.1 = (bf16[1024,1536]{1,0:T(8,128)(2,1)}, bf16[1024,768]{1,0:T(8,128)(2,1)}, bf16[4,1024,64]{2,1,0:T(8,128)(2,1)}, bf16[4,1024,64]{2,1,0:T(8,128)(2,1)}) custom-call(bf16[1024,1536]{1,0:T(8,128)(2,1)} %add_convert_fusion.2.x_ref, f32[1,1536]{1,0:T(1,128)} %copy.116.gain_ref, bf16[1536,1408]{1,0:T(8,128)(2,1)} %bitcast.79, ...), custom_call_target="tpu_custom_call" | custom-call | flops 251658240 | bytes 3538944 | tf_op jit(solution)/shard_map/project/pallas_call | solution.py:492
  143.7 15.0 %attend.2 = (bf16[1024,384]{1,0:T(8,128)(2,1)}, f32[3,1024,2]{2,1,0:T(8,128)}) custom-call(bf16[1024,768]{1,0:T(8,128)(2,1)} %get-tuple-element.125.q_ref, bf16[4,1024,64]{2,1,0:T(8,128)(2,1)} %get-tuple-element.121.k_ref, bf16[4,1024,64]{2,1,0:T(8,128)(2,1)} %get-tuple-element.122.v_ref, s32[1024,1]{1,0:T(8,128)} %copy.117.start_ref), custom_call_target="tpu_custom_call" | custom-call | flops 113246208 | bytes 3145728 | tf_op jit(solution)/shard_map/attend/pallas_call | solution.py:617
  160.6 2.9 collective-permute-start.8
  163.5 15.0 %attend.3 = (bf16[1024,384]{1,0:T(8,128)(2,1)}, f32[3,1024,2]{2,1,0:T(8,128)}) custom-call(bf16[1024,768]{1,0:T(8,128)(2,1)} %get-tuple-element.125.q_ref, bf16[4,1024,64]{2,1,0:T(8,128)(2,1)} %get-tuple-element.121.k_ref, bf16[4,1024,64]{2,1,0:T(8,128)(2,1)} %get-tuple-element.122.v_ref, s32[1024,1]{1,0:T(8,128)} %copy.117.start_ref), custom_call_target="tpu_custom_call" | custom-call | flops 113246208 | bytes 3145728 | tf_op jit(solution)/shard_map/attend/pallas_call | solution.py:617
  188.4 2.5 collective-permute-done.9
  192.6 5.0 collective-permute-start.26
  197.6 11.8 %collective-permute-start.27 = (bf16[1536,768]{1,0:T(8,128)(2,1)}, bf16[1536,768]{1,0:T(8,128)(2,1)}, u32[]{:S(2)}, u32[]{:S(2)}) collective-permute-start(bf16[1536,768]{1,0:T(8,128)(2,1)} %collective-permute-done.11.refs_21_.refs_17_), channel_id=1, source_target_pairs={{4,0},{5,1},{6,2},{7,3},{8,4},{9,5},{10,6},{11,7},{12,8},{13,9},{1... | collective-permute-start | bytes 7077896 | tf_op jit(solution)/shard_map/ppermute | solution.py:393
  209.4 6.2 multiply_reduce_fusion.2
  218.3 31.0 %collective-permute-done.14.refs_0_.refs_1_ = bf16[512,1536]{1,0:T(8,128)(2,1)} collective-permute-done((bf16[512,1536]{1,0:T(8,128)(2,1)S(1)}, bf16[512,1536]{1,0:T(8,128)(2,1)}, u32[]{:S(2)}, u32[]{:S(2)}) %collective-permute-start.14) | collective-permute-done | bytes 1572896 | tf_op jit(solution)/shard_map/ppermute | solution.py:373
  254.7 3.2 collective-permute-start.24
  258.4 8.0 %collective-permute-done.16.refs_2_ = bf16[256,1536]{1,0:T(8,128)(2,1)S(1)} collective-permute-done((bf16[256,1536]{1,0:T(8,128)(2,1)S(1)}, bf16[256,1536]{1,0:T(8,128)(2,1)S(1)}, u32[]{:S(2)}, u32[]{:S(2)}) %collective-permute-start.16) | collective-permute-done | bytes 786464 | tf_op jit(solution)/shard_map/ppermute | solution.py:377
  266.5 4.4 collective-permute-start.23
  276.8 2.6 select_select_fusion
  280.2 54.5 %experts.2 = (bf16[1024,1536]{1,0:T(8,128)(2,1)}, bf16[1024,1536]{1,0:T(8,128)(2,1)}, bf16[1024,1536]{1,0:T(8,128)(2,1)}, bf16[1024,1536]{1,0:T(8,128)(2,1)}, bf...) custom-call(s32[1]{0:T(128)} %bitcast.15.place_ref, ...), custom_call_target="tpu_custom_call" | custom-call | flops 2415919104 | bytes 50331648 | tf_op jit(solution)/shard_map/experts/pallas_call | solution.py:864
  335.6 8.1 %collective-permute-done.28 = bf16[1024,1536]{1,0:T(8,128)(2,1)S(1)} collective-permute-done((bf16[1024,1536]{1,0:T(8,128)(2,1)}, bf16[1024,1536]{1,0:T(8,128)(2,1)S(1)}, u32[]{:S(2)}, u32[]{:S(2)}) %collective-permute-start.28) | collective-permute-done | bytes 3145760 | tf_op jit(solution)/shard_map/ppermute | solution.py:377
  343.7 2.7 add_convert_fusion.1
  350.9 54.7 %experts.3 = (bf16[1024,1536]{1,0:T(8,128)(2,1)}, bf16[1024,1536]{1,0:T(8,128)(2,1)}, bf16[1024,1536]{1,0:T(8,128)(2,1)}, bf16[1024,1536]{1,0:T(8,128)(2,1)}, bf...) custom-call(s32[1]{0:T(128)} %bitcast.15.place_ref, ...), custom_call_target="tpu_custom_call", output_to_operand_aliasing={{4}: (21, {}), {5}: (22, {}), {6}: (23, {}), {7}: (24, {}),... | custom-call | flops 2415919104 | bytes 50331648 | tf_op jit(solution)/shard_map/experts/pallas_call | solution.py:864
  406.7 11.1 %fusion.11 = bf16[1536,512]{1,0:T(8,128)(2,1)S(1)} fusion(bf16[4096,1536]{1,0:T(8,128)(2,1)} %get-tuple-element.166, bf16[4096,512]{1,0:T(8,128)(2,1)} %get-tuple-element.159), kind=kOutput, calls=%fused_computation.40 | convolution fusion | flops 6444023808 | bytes 18350080 | tf_op jit(solution)/shard_map/dot_general | solution.py:575
  418.4 14.1 %convolution_convert_fusion.1 = bf16[1536,1024]{1,0:T(8,128)(2,1)S(1)} fusion(bf16[4096,1536]{1,0:T(8,128)(2,1)S(1)} %copy-done.11, bf16[4096,1024]{1,0:T(8,128)(2,1)S(1)} %copy-done.16), kind=kOutput, calls=%fused_computation.14 | convolution fusion | flops 12886474752 | bytes 24117248 | tf_op jit(solution)/shard_map/dot_general | solution.py:575
  434.5 5.1 collective-permute-start.38
  442.6 2.9 convert_add_fusion.1
  445.5 3.2 fusion.31
  449.2 16.2 %convolution_convert_fusion = bf16[1536,1024]{1,0:T(8,128)(2,1)S(1)} fusion(bf16[4096,1536]{1,0:T(8,128)(2,1)S(1)} %copy-done.11, bf16[4096,1024]{1,0:T(8,128)(2,1)} %get-tuple-element.165), kind=kOutput, calls=%fused_computation.13 | convolution fusion | flops 12886474752 | bytes 24117248 | tf_op jit(solution)/shard_map/dot_general | solution.py:575
  465.5 11.3 %fusion.12 = bf16[1536,512]{1,0:T(8,128)(2,1)S(1)} fusion(bf16[4096,1536]{1,0:T(8,128)(2,1)} %get-tuple-element.166, bf16[4096,512]{1,0:T(8,128)(2,1)} %get-tuple-element.167), kind=kOutput, calls=%fused_computation.41 | convolution fusion | flops 6444023808 | bytes 18350080 | tf_op jit(solution)/shard_map/dot_general | solution.py:575
  481.9 2.6 convolution_convert_fusion.2
  489.2 3.2 add_convert_fusion.6
  492.4 5.5 collective-permute-start.41
  497.9 3.3 add_convert_fusion.5
  502.6 4.3 fusion.48
  506.9 3.7 add_convert_fusion
  525.5 3.4 add_convert_fusion.7.d_ref
  528.9 40.8 %attend_back.1 = (bf16[1024,768]{1,0:T(8,128)(2,1)}, bf16[1024,256]{1,0:T(8,128)(2,1)}, bf16[1024,256]{1,0:T(8,128)(2,1)}) custom-call(bf16[1024,768]{1,0:T(8,128)(2,1)} %get-tuple-element.125.q_ref, bf16[4,1024,64]{2,1,0:T(8,128)(2,1)} %get-tuple-element.121.k_ref, bf16[4,1024,64]{2,1,0:T(8,128)(2,1)} %get-tuple-element.122.v_ref, ...), custom_call_target="tpu_custom_call" | custom-call | flops 566231040 | bytes 6291456 | tf_op jit(solution)/shard_map/attend_back/pallas_call | solution.py:694
  569.7 9.0 %add_convert_fusion.3 = (bf16[1536,768]{1,0:T(8,128)(2,1)}, bf16[1536,768]{1,0:T(8,128)(2,1)}) fusion(bf16[1536,768]{1,0:T(8,128)(2,1)} %collective-permute-done.42, pred[]{:T(512)S(6)} %lt.123, pred[]{:T(512)S(6)} %lt.122, bf16[1536,256]{1,0:T(8,128)(2,1)} %copy-done.8, bf16[1536,512]{1,0:T(8,128)(2,1)} %copy-done.2, bf16[1536,256]{1,0:T(8,128)(2,1)} %copy-done.10, ...), kind=kLoop, calls=%fused_computation.8 | loop fusion | flops 33030144 | bytes 18874372 | tf_op jit(solution)/shard_map/convert_element_type | solution.py:1157
  578.7 8.4 %qkv_grad.1 = bf16[2,2,2,4,48,1408]{5,4,3,2,1,0:T(8,128)(2,1)} custom-call(bf16[1024,1536]{1,0:T(8,128)(2,1)} %get-tuple-element.182.h_ref, bf16[1024,768]{1,0:T(8,128)(2,1)} %get-tuple-element.191.dq_ref, bf16[1024,256]{1,0:T(8,128)(2,1)} %get-tuple-element.192.dk_ref, bf16[1024,256]{1,0:T(8,128)(2,1)} %get-tuple-element.193.dv_ref, ...), custom_call_target="tpu_custom_call" | custom-call | flops 251658240 | bytes 1572864 | tf_op jit(solution)/shard_map/qkv_grad/pallas_call | solution.py:916
  587.0 3.1 dynamic-slice_bitcast_fusion
  591.9 3.9 convert_add_fusion
  595.9 4.3 fusion.27
  603.7 5.5 collective-permute-start.50
  612.1 4.1 convert_add_fusion.3
  616.2 11.2 %token_grad.1 = (bf16[512,1536]{1,0:T(8,128)(2,1)}, bf16[512,1536]{1,0:T(8,128)(2,1)}) custom-call(bf16[1024,768]{1,0:T(8,128)(2,1)} %get-tuple-element.191.dq_ref, bf16[1024,256]{1,0:T(8,128)(2,1)} %get-tuple-element.192.dk_ref, bf16[1024,256]{1,0:T(8,128)(2,1)} %get-tuple-element.193.dv_ref, bf16[1536,1408]{1,0:T(8,128)(2,1)} %bitcast.80, ...), custom_call_target="tpu_custom_call" | custom-call | flops 251658240 | bytes 1572864 | tf_op jit(solution)/shard_map/token_grad/pallas_call | solution.py:542
  629.7 5.8 select_convert_fusion
  637.2 5.1 collective-permute-done.51
  642.3 2.7 collective-permute-start.52
  646.3 4.3 fusion.29
  650.6 2.9 collective-permute-done.49
  655.0 12.4 %collective-permute-done.52 = bf16[768,768]{1,0:T(8,128)(2,1)} collective-permute-done((bf16[768,768]{1,0:T(8,128)(2,1)}, bf16[768,768]{1,0:T(8,128)(2,1)}, u32[]{:S(2)}, u32[]{:S(2)}) %collective-permute-start.52) | collective-permute-done | bytes 1179680 | tf_op jit(solution)/shard_map/ppermute | solution.py:389
  667.4 4.8 collective-permute-done.53
  672.3 4.4 fusion.16
  684.0 6.7 collective-permute-start.57
  692.9 8.5 %collective-permute-done.55 = bf16[2,48,1408]{2,1,0:T(8,128)(2,1)S(1)} collective-permute-done((bf16[2,48,1408]{2,1,0:T(8,128)(2,1)S(1)}, bf16[2,48,1408]{2,1,0:T(8,128)(2,1)S(1)}, u32[]{:S(2)}, u32[]{:S(2)}) %collective-permute-start.55) | collective-permute-done | bytes 270368 | tf_op jit(solution)/shard_map/ppermute | solution.py:377
  701.6 3.0 fusion.2
  704.6 4.7 fusion.5
  710.8 6.4 collective-permute-done.57
  (315 shorter events, 127.9 us)
Async XLA Ops:
  7.2 123.1 %all-gather.3.cloned.1.call-start = ((), (), s32[]{:S(2)}) async-start(), calls=%async_computation.1 | async-start | bytes 4595712 | tf_op jit(solution)/shard_map/all_gather | solution.py:1004
  10.0 5.4 collective-permute-start.5
  16.2 193.2 %all-gather.5.cloned.1.call-start = ((), (), s32[]{:S(2)}) async-start(), calls=%async_computation.2 | async-start | bytes 4866048 | tf_op jit(solution)/shard_map/all_gather | solution.py:1005
  16.9 638.1 %reduce-scatter.2.cloned.1.call-start = ((), (), s32[]{:S(2)}) async-start(), calls=%async_computation.3 | async-start | bytes 4866048 | tf_op jit(solution)/shard_map/reduce_scatter | solution.py:1200
  18.4 30.4 %collective-permute-start = (bf16[1536,512]{1,0:T(8,128)(2,1)S(1)}, bf16[1536,512]{1,0:T(8,128)(2,1)S(1)}, u32[]{:S(2)}, u32[]{:S(2)}) collective-permute-start(bf16[1536,512]{1,0:T(8,128)(2,1)S(1)} %pad_maximum_fusion.6), channel_id=1, source_target_pairs={{0,0},{1,16},{2,2},{3,18},{4,4},{5,20},{6,6},{7,22},{8,8},{9,24},{... | collective-permute-start | bytes 4718600 | tf_op jit(solution)/shard_map/ppermute | solution.py:982
  22.9 25.9 %collective-permute-start.1 = (bf16[1536,256]{1,0:T(8,128)(2,1)}, bf16[1536,256]{1,0:T(8,128)(2,1)}, u32[]{:S(2)}, u32[]{:S(2)}) collective-permute-start(bf16[1536,256]{1,0:T(8,128)(2,1)} %get-tuple-element.312), channel_id=1, source_target_pairs={{0,1},{1,17},{2,3},{3,19},{4,5},{5,21},{6,7},{7,23},{8,9},{9,25},{... | collective-permute-start | bytes 2359304 | tf_op jit(solution)/shard_map/ppermute | solution.py:982
  50.2 72.1 %collective-permute-start.3 = (bf16[1536,768]{1,0:T(8,128)(2,1)S(1)}, bf16[1536,768]{1,0:T(8,128)(2,1)}, u32[]{:S(2)}, u32[]{:S(2)}) collective-permute-start(bf16[1536,768]{1,0:T(8,128)(2,1)S(1)} %pad_maximum_fusion.1.refs_19_.refs_15_), channel_id=1, source_target_pairs={{0,4},{1,5},{2,6},{3,7},{4,8},{5,9},{6,10},{7,11},{8,12},{9,13},{1... | collective-permute-start | bytes 7077896 | tf_op jit(solution)/shard_map/ppermute | solution.py:389
  54.8 70.2 %collective-permute-start.4 = (bf16[1536,768]{1,0:T(8,128)(2,1)S(1)}, bf16[1536,768]{1,0:T(8,128)(2,1)}, u32[]{:S(2)}, u32[]{:S(2)}) collective-permute-start(bf16[1536,768]{1,0:T(8,128)(2,1)S(1)} %pad_maximum_fusion.1.refs_19_.refs_15_), channel_id=1, source_target_pairs={{4,0},{5,1},{6,2},{7,3},{8,4},{9,5},{10,6},{11,7},{12,8},{13,9},{1... | collective-permute-start | bytes 7077896 | tf_op jit(solution)/shard_map/ppermute | solution.py:393
  56.1 37.6 %collective-permute-start.2 = (bf16[512,1536]{1,0:T(8,128)(2,1)}, bf16[512,1536]{1,0:T(8,128)(2,1)}, u32[]{:S(2)}, u32[]{:S(2)}) collective-permute-start(bf16[512,1536]{1,0:T(8,128)(2,1)} %param.17), channel_id=1, source_target_pairs={{0,16},{16,0},{1,17},{17,1},{2,18},{18,2},{3,19},{19,3},{4,20},{20... | collective-permute-start | bytes 4718600 | tf_op jit(solution)/shard_map/ppermute | solution.py:373
  62.6 100.9 %collective-permute-start.7 = (bf16[512,1664]{1,0:T(8,128)(2,1)}, bf16[512,1664]{1,0:T(8,128)(2,1)}, u32[]{:S(2)}, u32[]{:S(2)}) collective-permute-start(bf16[512,1664]{1,0:T(8,128)(2,1)} %concatenate.95.refs_6_), channel_id=1, source_target_pairs={{0,2},{1,3},{2,0},{3,1},{4,6},{5,7},{6,4},{7,5},{8,10},{9,11},{10,... | collective-permute-start | bytes 5111816 | tf_op jit(solution)/shard_map/ppermute | solution.py:377
  93.7 69.8 %collective-permute-start.6 = (bf16[512,1664]{1,0:T(8,128)(2,1)}, bf16[512,1664]{1,0:T(8,128)(2,1)}, u32[]{:S(2)}, u32[]{:S(2)}) collective-permute-start(bf16[512,1664]{1,0:T(8,128)(2,1)} %concatenate.95.refs_6_), channel_id=1, source_target_pairs={{0,16},{16,0},{1,17},{17,1},{2,18},{18,2},{3,19},{19,3},{4,20},{20... | collective-permute-start | bytes 5111816 | tf_op jit(solution)/shard_map/ppermute | solution.py:373
  125.1 67.5 %collective-permute-start.10 = (bf16[1536,768]{1,0:T(8,128)(2,1)}, bf16[1536,768]{1,0:T(8,128)(2,1)}, u32[]{:S(2)}, u32[]{:S(2)}) collective-permute-start(bf16[1536,768]{1,0:T(8,128)(2,1)} %collective-permute-done.3.refs_18_.refs_14_), channel_id=1, source_target_pairs={{0,4},{1,5},{2,6},{3,7},{4,8},{5,9},{6,10},{7,11},{8,12},{9,13},{1... | collective-permute-start | bytes 7077896 | tf_op jit(solution)/shard_map/ppermute | solution.py:389
  129.0 63.6 %collective-permute-start.11 = (bf16[1536,768]{1,0:T(8,128)(2,1)}, bf16[1536,768]{1,0:T(8,128)(2,1)}, u32[]{:S(2)}, u32[]{:S(2)}) collective-permute-start(bf16[1536,768]{1,0:T(8,128)(2,1)} %collective-permute-done.4.refs_20_.refs_16_), channel_id=1, source_target_pairs={{4,0},{5,1},{6,2},{7,3},{8,4},{9,5},{10,6},{11,7},{12,8},{13,9},{1... | collective-permute-start | bytes 7077896 | tf_op jit(solution)/shard_map/ppermute | solution.py:393
  160.6 26.3 %collective-permute-start.8 = (bf16[512,384]{0,1:T(8,128)(2,1)S(1)}, bf16[512,384]{0,1:T(8,128)(2,1)S(1)}, u32[]{:S(2)}, u32[]{:S(2)}) collective-permute-start(bf16[512,384]{0,1:T(8,128)(2,1)S(1)} %fusion.34), channel_id=1, source_target_pairs={{0,16},{16,0},{1,17},{17,1},{2,18},{18,2},{3,19},{19,3},{4,20},{20... | collective-permute-start | bytes 1179656 | tf_op jit(solution)/shard_map/ppermute | solution.py:373
  180.4 10.5 %collective-permute-start.9 = (bf16[512,384]{0,1:T(8,128)(2,1)S(1)}, bf16[512,384]{0,1:T(8,128)(2,1)S(1)}, u32[]{:S(2)}, u32[]{:S(2)}) collective-permute-start(bf16[512,384]{0,1:T(8,128)(2,1)S(1)} %fusion.35), channel_id=1, source_target_pairs={{0,16},{16,0},{1,17},{17,1},{2,18},{18,2},{3,19},{19,3},{4,20},{20... | collective-permute-start | bytes 1179656 | tf_op jit(solution)/shard_map/ppermute | solution.py:373
  183.3 32.8 %collective-permute-start.12 = (bf16[256,1664]{1,0:T(8,128)(2,1)}, bf16[256,1664]{1,0:T(8,128)(2,1)}, u32[]{:S(2)}, u32[]{:S(2)}) collective-permute-start(bf16[256,1664]{1,0:T(8,128)(2,1)} %slice.179), channel_id=1, source_target_pairs={{0,2},{1,3},{2,0},{3,1},{4,6},{5,7},{6,4},{7,5},{8,10},{9,11},{10,... | collective-permute-start | bytes 2555912 | tf_op jit(solution)/shard_map/ppermute | solution.py:377
  186.9 29.2 %collective-permute-start.13 = (bf16[256,1664]{1,0:T(8,128)(2,1)}, bf16[256,1664]{1,0:T(8,128)(2,1)}, u32[]{:S(2)}, u32[]{:S(2)}) collective-permute-start(bf16[256,1664]{1,0:T(8,128)(2,1)} %slice.180), channel_id=1, source_target_pairs={{0,16},{16,0},{1,17},{17,1},{2,18},{18,2},{3,19},{19,3},{4,20},{20... | collective-permute-start | bytes 2555912 | tf_op jit(solution)/shard_map/ppermute | solution.py:373
  192.6 65.3 %collective-permute-start.26 = (bf16[1536,768]{1,0:T(8,128)(2,1)}, bf16[1536,768]{1,0:T(8,128)(2,1)}, u32[]{:S(2)}, u32[]{:S(2)}) collective-permute-start(bf16[1536,768]{1,0:T(8,128)(2,1)} %collective-permute-done.10.refs_17_.refs_13_), channel_id=1, source_target_pairs={{0,4},{1,5},{2,6},{3,7},{4,8},{5,9},{6,10},{7,11},{8,12},{9,13},{1... | collective-permute-start | bytes 7077896 | tf_op jit(solution)/shard_map/ppermute | solution.py:389
  197.6 60.3 %collective-permute-start.27 = (bf16[1536,768]{1,0:T(8,128)(2,1)}, bf16[1536,768]{1,0:T(8,128)(2,1)}, u32[]{:S(2)}, u32[]{:S(2)}) collective-permute-start(bf16[1536,768]{1,0:T(8,128)(2,1)} %collective-permute-done.11.refs_21_.refs_17_), channel_id=1, source_target_pairs={{4,0},{5,1},{6,2},{7,3},{8,4},{9,5},{10,6},{11,7},{12,8},{13,9},{1... | collective-permute-start | bytes 7077896 | tf_op jit(solution)/shard_map/ppermute | solution.py:393
  216.1 33.2 %collective-permute-start.14 = (bf16[512,1536]{1,0:T(8,128)(2,1)S(1)}, bf16[512,1536]{1,0:T(8,128)(2,1)}, u32[]{:S(2)}, u32[]{:S(2)}) collective-permute-start(bf16[512,1536]{1,0:T(8,128)(2,1)S(1)} %multiply_convert_fusion.1.refs_0_), channel_id=1, source_target_pairs={{0,16},{16,0},{1,17},{17,1},{2,18},{18,2},{3,19},{19,3},{4,20},{20... | collective-permute-start | bytes 4718600 | tf_op jit(solution)/shard_map/ppermute | solution.py:373
  217.2 34.7 %collective-permute-start.15 = (bf16[512,1536]{1,0:T(8,128)(2,1)S(1)}, bf16[512,1536]{1,0:T(8,128)(2,1)}, u32[]{:S(2)}, u32[]{:S(2)}) collective-permute-start(bf16[512,1536]{1,0:T(8,128)(2,1)S(1)} %multiply_convert_fusion.1.refs_0_), channel_id=1, source_target_pairs={{0,2},{1,3},{2,0},{3,1},{4,6},{5,7},{6,4},{7,5},{8,10},{9,11},{10,... | collective-permute-start | bytes 4718600 | tf_op jit(solution)/shard_map/ppermute | solution.py:377
  250.5 15.9 %collective-permute-start.16 = (bf16[256,1536]{1,0:T(8,128)(2,1)S(1)}, bf16[256,1536]{1,0:T(8,128)(2,1)S(1)}, u32[]{:S(2)}, u32[]{:S(2)}) collective-permute-start(bf16[256,1536]{1,0:T(8,128)(2,1)S(1)} %slice.233), channel_id=1, source_target_pairs={{0,2},{1,3},{2,0},{3,1},{4,6},{5,7},{6,4},{7,5},{8,10},{9,11},{10,... | collective-permute-start | bytes 2359304 | tf_op jit(solution)/shard_map/ppermute | solution.py:377
  253.1 17.7 %collective-permute-start.17 = (bf16[256,1536]{1,0:T(8,128)(2,1)S(1)}, bf16[256,1536]{1,0:T(8,128)(2,1)S(1)}, u32[]{:S(2)}, u32[]{:S(2)}) collective-permute-start(bf16[256,1536]{1,0:T(8,128)(2,1)S(1)} %slice.234), channel_id=1, source_target_pairs={{0,16},{16,0},{1,17},{17,1},{2,18},{18,2},{3,19},{19,3},{4,20},{20... | collective-permute-start | bytes 2359304 | tf_op jit(solution)/shard_map/ppermute | solution.py:373
  254.7 18.5 %collective-permute-start.24 = (bf16[256,1664]{1,0:T(8,128)(2,1)}, bf16[256,1664]{1,0:T(8,128)(2,1)}, u32[]{:S(2)}, u32[]{:S(2)}) collective-permute-start(bf16[256,1664]{1,0:T(8,128)(2,1)} %collective-permute-done.12.refs_10_), channel_id=1, source_target_pairs={{0,1},{1,0},{2,3},{3,2},{4,5},{5,4},{6,7},{7,6},{8,9},{9,8},{10,11... | collective-permute-start | bytes 2555912 | tf_op jit(solution)/shard_map/ppermute | solution.py:377
  257.9 18.1 %collective-permute-start.18 = (bf16[512,1536]{1,0:T(8,128)(2,1)}, bf16[512,1536]{1,0:T(8,128)(2,1)}, u32[]{:S(2)}, u32[]{:S(2)}) collective-permute-start(bf16[512,1536]{1,0:T(8,128)(2,1)} %collective-permute-done.14.refs_0_.refs_1_), channel_id=1, source_target_pairs={{0,1},{1,0},{2,3},{3,2},{4,5},{5,4},{6,7},{7,6},{8,9},{9,8},{10,11... | collective-permute-start | bytes 4718600 | tf_op jit(solution)/shard_map/ppermute | solution.py:377
  257.9 22.3 %collective-permute-start.22 = (bf16[512,1664]{1,0:T(8,128)(2,1)}, bf16[512,1664]{1,0:T(8,128)(2,1)}, u32[]{:S(2)}, u32[]{:S(2)}) collective-permute-start(bf16[512,1664]{1,0:T(8,128)(2,1)} %collective-permute-done.6.refs_8_.refs_7_), channel_id=1, source_target_pairs={{0,1},{1,0},{2,3},{3,2},{4,5},{5,4},{6,7},{7,6},{8,9},{9,8},{10,11... | collective-permute-start | bytes 5111816 | tf_op jit(solution)/shard_map/ppermute | solution.py:377
  266.5 13.8 %collective-permute-start.23 = (bf16[512,1664]{1,0:T(8,128)(2,1)}, bf16[512,1664]{1,0:T(8,128)(2,1)}, u32[]{:S(2)}, u32[]{:S(2)}) collective-permute-start(bf16[512,1664]{1,0:T(8,128)(2,1)} %collective-permute-done.7.refs_9_.refs_8_), channel_id=1, source_target_pairs={{0,1},{1,0},{2,3},{3,2},{4,5},{5,4},{6,7},{7,6},{8,9},{9,8},{10,11... | collective-permute-start | bytes 5111816 | tf_op jit(solution)/shard_map/ppermute | solution.py:377
  270.9 4.8 collective-permute-start.25
  273.3 7.0 collective-permute-start.19
  275.6 4.6 collective-permute-start.20
  276.0 4.2 collective-permute-start.21
  334.7 9.0 %collective-permute-start.28 = (bf16[1024,1536]{1,0:T(8,128)(2,1)}, bf16[1024,1536]{1,0:T(8,128)(2,1)S(1)}, u32[]{:S(2)}, u32[]{:S(2)}) collective-permute-start(bf16[1024,1536]{1,0:T(8,128)(2,1)} %get-tuple-element.142), channel_id=1, source_target_pairs={{0,1},{1,0},{2,3},{3,2},{4,5},{5,4},{6,7},{7,6},{8,9},{9,8},{10,11... | collective-permute-start | bytes 9437192 | tf_op jit(solution)/shard_map/ppermute | solution.py:377
  335.1 15.8 %collective-permute-start.29 = (bf16[512,1536]{1,0:T(8,128)(2,1)}, bf16[512,1536]{1,0:T(8,128)(2,1)}, u32[]{:S(2)}, u32[]{:S(2)}) collective-permute-start(bf16[512,1536]{1,0:T(8,128)(2,1)} %copy-done.21), channel_id=1, source_target_pairs={{0,1},{1,0},{2,3},{3,2},{4,5},{5,4},{6,7},{7,6},{8,9},{9,8},{10,11... | collective-permute-start | bytes 4718600 | tf_op jit(solution)/shard_map/ppermute | solution.py:377
  335.3 15.7 %collective-permute-start.30 = (bf16[512,1664]{1,0:T(8,128)(2,1)}, bf16[512,1664]{1,0:T(8,128)(2,1)}, u32[]{:S(2)}, u32[]{:S(2)}) collective-permute-start(bf16[512,1664]{1,0:T(8,128)(2,1)} %concatenate.95.refs_6_), channel_id=1, source_target_pairs={{0,1},{1,0},{2,3},{3,2},{4,5},{5,4},{6,7},{7,6},{8,9},{9,8},{10,11... | collective-permute-start | bytes 5111816 | tf_op jit(solution)/shard_map/ppermute | solution.py:377
  348.3 58.4 %collective-permute-start.31 = (bf16[512,1536]{1,0:T(8,128)(2,1)}, bf16[512,1536]{1,0:T(8,128)(2,1)}, u32[]{:S(2)}, u32[]{:S(2)}) collective-permute-start(bf16[512,1536]{1,0:T(8,128)(2,1)} %get-tuple-element.293), channel_id=1, source_target_pairs={{0,2},{1,3},{2,0},{3,1},{4,6},{5,7},{6,4},{7,5},{8,10},{9,11},{10,... | collective-permute-start | bytes 4718600 | tf_op jit(solution)/shard_map/ppermute | solution.py:377
  349.4 57.3 %collective-permute-start.32 = (bf16[512,1536]{1,0:T(8,128)(2,1)}, bf16[512,1536]{1,0:T(8,128)(2,1)}, u32[]{:S(2)}, u32[]{:S(2)}) collective-permute-start(bf16[512,1536]{1,0:T(8,128)(2,1)} %get-tuple-element.292), channel_id=1, source_target_pairs={{0,16},{16,0},{1,17},{17,1},{2,18},{18,2},{3,19},{19,3},{4,20},{20... | collective-permute-start | bytes 4718600 | tf_op jit(solution)/shard_map/ppermute | solution.py:373
  405.7 36.9 %collective-permute-start.33 = (bf16[1024,1536]{1,0:T(8,128)(2,1)}, bf16[1024,1536]{1,0:T(8,128)(2,1)}, u32[]{:S(2)}, u32[]{:S(2)}) collective-permute-start(bf16[1024,1536]{1,0:T(8,128)(2,1)} %get-tuple-element.161), channel_id=1, source_target_pairs={{0,1},{1,0},{2,3},{3,2},{4,5},{5,4},{6,7},{7,6},{8,9},{9,8},{10,11... | collective-permute-start | bytes 9437192 | tf_op jit(solution)/shard_map/ppermute | solution.py:377
  417.9 80.0 %copy-start.8 = (bf16[1536,256]{1,0:T(8,128)(2,1)}, bf16[1536,256]{1,0:T(8,128)(2,1)S(1)}, u32[]{:S(2)}) copy-start(bf16[1536,256]{1,0:T(8,128)(2,1)S(1)} %get-tuple-element.308) | copy-start | bytes 2359300
  434.5 54.6 %collective-permute-start.38 = (bf16[1536,768]{1,0:T(8,128)(2,1)}, bf16[1536,768]{1,0:T(8,128)(2,1)}, u32[]{:S(2)}, u32[]{:S(2)}) collective-permute-start(bf16[1536,768]{1,0:T(8,128)(2,1)} %pad_maximum_fusion.3), channel_id=1, source_target_pairs={{0,4},{1,5},{2,6},{3,7},{4,8},{5,9},{6,10},{7,11},{8,12},{9,13},{1... | collective-permute-start | bytes 7077896 | tf_op jit(solution)/shard_map/ppermute | solution.py:389
  441.2 56.7 %collective-permute-start.39 = (bf16[1536,768]{1,0:T(8,128)(2,1)}, bf16[1536,768]{1,0:T(8,128)(2,1)}, u32[]{:S(2)}, u32[]{:S(2)}) collective-permute-start(bf16[1536,768]{1,0:T(8,128)(2,1)} %pad_maximum_fusion.2), channel_id=1, source_target_pairs={{4,0},{5,1},{6,2},{7,3},{8,4},{9,5},{10,6},{11,7},{12,8},{13,9},{1... | collective-permute-start | bytes 7077896 | tf_op jit(solution)/shard_map/ppermute | solution.py:393
  448.6 28.2 %collective-permute-start.34 = (bf16[256,1536]{1,0:T(8,128)(2,1)}, bf16[256,1536]{1,0:T(8,128)(2,1)S(1)}, u32[]{:S(2)}, u32[]{:S(2)}) collective-permute-start(bf16[256,1536]{1,0:T(8,128)(2,1)} %get-tuple-element.280), channel_id=1, source_target_pairs={{0,16},{16,0},{1,17},{17,1},{2,18},{18,2},{3,19},{19,3},{4,20},{20... | collective-permute-start | bytes 2359304 | tf_op jit(solution)/shard_map/ppermute | solution.py:373
  449.0 27.8 %collective-permute-start.35 = (bf16[256,1536]{1,0:T(8,128)(2,1)}, bf16[256,1536]{1,0:T(8,128)(2,1)S(1)}, u32[]{:S(2)}, u32[]{:S(2)}) collective-permute-start(bf16[256,1536]{1,0:T(8,128)(2,1)} %get-tuple-element.281), channel_id=1, source_target_pairs={{0,2},{1,3},{2,0},{3,1},{4,6},{5,7},{6,4},{7,5},{8,10},{9,11},{10,... | collective-permute-start | bytes 2359304 | tf_op jit(solution)/shard_map/ppermute | solution.py:377
  484.6 22.4 %collective-permute-start.40 = (bf16[1024,1536]{1,0:T(8,128)(2,1)}, bf16[1024,1536]{1,0:T(8,128)(2,1)}, u32[]{:S(2)}, u32[]{:S(2)}) collective-permute-start(bf16[1024,1536]{1,0:T(8,128)(2,1)} %get-tuple-element.172), channel_id=1, source_target_pairs={{0,1},{1,0},{2,3},{3,2},{4,5},{5,4},{6,7},{7,6},{8,9},{9,8},{10,11... | collective-permute-start | bytes 9437192 | tf_op jit(solution)/shard_map/ppermute | solution.py:377
  487.2 26.1 %collective-permute-start.37 = (bf16[512,768]{1,0:T(8,128)(2,1)}, bf16[512,768]{1,0:T(8,128)(2,1)}, u32[]{:S(2)}, u32[]{:S(2)}) collective-permute-start(bf16[512,768]{1,0:T(8,128)(2,1)} %constant_dynamic-slice_fusion), channel_id=1, source_target_pairs={{0,16},{16,0},{1,17},{17,1},{2,18},{18,2},{3,19},{19,3},{4,20},{20... | collective-permute-start | bytes 2359304 | tf_op jit(solution)/shard_map/ppermute | solution.py:373
  492.4 77.3 %collective-permute-start.41 = (bf16[1536,768]{1,0:T(8,128)(2,1)}, bf16[1536,768]{1,0:T(8,128)(2,1)}, u32[]{:S(2)}, u32[]{:S(2)}) collective-permute-start(bf16[1536,768]{1,0:T(8,128)(2,1)} %add_convert_fusion.6), channel_id=1, source_target_pairs={{0,4},{1,5},{2,6},{3,7},{4,8},{5,9},{6,10},{7,11},{8,12},{9,13},{1... | collective-permute-start | bytes 7077896 | tf_op jit(solution)/shard_map/ppermute | solution.py:389
  501.3 68.4 %collective-permute-start.42 = (bf16[1536,768]{1,0:T(8,128)(2,1)}, bf16[1536,768]{1,0:T(8,128)(2,1)}, u32[]{:S(2)}, u32[]{:S(2)}) collective-permute-start(bf16[1536,768]{1,0:T(8,128)(2,1)} %add_convert_fusion.5), channel_id=1, source_target_pairs={{4,0},{5,1},{6,2},{7,3},{8,4},{9,5},{10,6},{11,7},{12,8},{13,9},{1... | collective-permute-start | bytes 7077896 | tf_op jit(solution)/shard_map/ppermute | solution.py:393
  512.4 57.2 %collective-permute-start.43 = (bf16[512,1536]{1,0:T(8,128)(2,1)}, bf16[512,1536]{1,0:T(8,128)(2,1)}, u32[]{:S(2)}, u32[]{:S(2)}) collective-permute-start(bf16[512,1536]{1,0:T(8,128)(2,1)} %get-tuple-element.287), channel_id=1, source_target_pairs={{0,2},{1,3},{2,0},{3,1},{4,6},{5,7},{6,4},{7,5},{8,10},{9,11},{10,... | collective-permute-start | bytes 4718600 | tf_op jit(solution)/shard_map/ppermute | solution.py:377
  513.0 56.7 %collective-permute-start.44 = (bf16[512,1536]{1,0:T(8,128)(2,1)}, bf16[512,1536]{1,0:T(8,128)(2,1)}, u32[]{:S(2)}, u32[]{:S(2)}) collective-permute-start(bf16[512,1536]{1,0:T(8,128)(2,1)} %get-tuple-element.286), channel_id=1, source_target_pairs={{0,16},{16,0},{1,17},{17,1},{2,18},{18,2},{3,19},{19,3},{4,20},{20... | collective-permute-start | bytes 4718600 | tf_op jit(solution)/shard_map/ppermute | solution.py:373
  513.3 78.6 %collective-permute-start.36 = (bf16[1024,1536]{1,0:T(8,128)(2,1)}, bf16[1024,1536]{1,0:T(8,128)(2,1)}, u32[]{:S(2)}, u32[]{:S(2)}) collective-permute-start(bf16[1024,1536]{1,0:T(8,128)(2,1)} %get-tuple-element.170), channel_id=1, source_target_pairs={{0,1},{1,0},{2,3},{3,2},{4,5},{5,4},{6,7},{7,6},{8,9},{9,8},{10,11... | collective-permute-start | bytes 9437192 | tf_op jit(solution)/shard_map/ppermute | solution.py:377
  590.1 21.9 %collective-permute-start.47 = (bf16[2,2,4,48,1408]{4,3,2,1,0:T(8,128)(2,1)}, bf16[2,2,4,48,1408]{4,3,2,1,0:T(8,128)(2,1)}, u32[]{:S(2)}, u32[]{:S(2)}) collective-permute-start(bf16[2,2,4,48,1408]{4,3,2,1,0:T(8,128)(2,1)} %dynamic-slice_bitcast_fusion), channel_id=1, source_target_pairs={{0,1},{1,0},{2,3},{3,2},{4,5},{5,4},{6,7},{7,6},{8,9},{9,8},{10,11... | collective-permute-start | bytes 6488072 | tf_op jit(solution)/shard_map/ppermute | solution.py:377
  600.2 35.4 %collective-permute-start.45 = (bf16[256,1536]{1,0:T(8,128)(2,1)}, bf16[256,1536]{1,0:T(8,128)(2,1)}, u32[]{:S(2)}, u32[]{:S(2)}) collective-permute-start(bf16[256,1536]{1,0:T(8,128)(2,1)} %get-tuple-element.277), channel_id=1, source_target_pairs={{0,16},{16,0},{1,17},{17,1},{2,18},{18,2},{3,19},{19,3},{4,20},{20... | collective-permute-start | bytes 2359304 | tf_op jit(solution)/shard_map/ppermute | solution.py:373
  601.2 34.8 %collective-permute-start.46 = (bf16[256,1536]{1,0:T(8,128)(2,1)}, bf16[256,1536]{1,0:T(8,128)(2,1)}, u32[]{:S(2)}, u32[]{:S(2)}) collective-permute-start(bf16[256,1536]{1,0:T(8,128)(2,1)} %get-tuple-element.276), channel_id=1, source_target_pairs={{0,2},{1,3},{2,0},{3,1},{4,6},{5,7},{6,4},{7,5},{8,10},{9,11},{10,... | collective-permute-start | bytes 2359304 | tf_op jit(solution)/shard_map/ppermute | solution.py:377
  603.7 33.5 %collective-permute-start.50 = (bf16[768,768]{1,0:T(8,128)(2,1)}, bf16[768,768]{1,0:T(8,128)(2,1)}, u32[]{:S(2)}, u32[]{:S(2)}) collective-permute-start(bf16[768,768]{1,0:T(8,128)(2,1)} %get-tuple-element.301), channel_id=1, source_target_pairs={{0,4},{1,5},{2,6},{3,7},{4,8},{5,9},{6,10},{7,11},{8,12},{9,13},{1... | collective-permute-start | bytes 3538952 | tf_op jit(solution)/shard_map/ppermute | solution.py:389
  610.8 31.5 %collective-permute-start.51 = (bf16[768,768]{1,0:T(8,128)(2,1)}, bf16[768,768]{1,0:T(8,128)(2,1)}, u32[]{:S(2)}, u32[]{:S(2)}) collective-permute-start(bf16[768,768]{1,0:T(8,128)(2,1)} %get-tuple-element.299), channel_id=1, source_target_pairs={{4,0},{5,1},{6,2},{7,3},{8,4},{9,5},{10,6},{11,7},{12,8},{13,9},{1... | collective-permute-start | bytes 3538952 | tf_op jit(solution)/shard_map/ppermute | solution.py:393
  629.3 24.2 %collective-permute-start.49 = (bf16[2,4,48,1408]{3,2,1,0:T(8,128)(2,1)S(1)}, bf16[2,4,48,1408]{3,2,1,0:T(8,128)(2,1)S(1)}, u32[]{:S(2)}, u32[]{:S(2)}) collective-permute-start(bf16[2,4,48,1408]{3,2,1,0:T(8,128)(2,1)S(1)} %fusion.36), channel_id=1, source_target_pairs={{0,2},{1,3},{2,0},{3,1},{4,6},{5,7},{6,4},{7,5},{8,10},{9,11},{10,... | collective-permute-start | bytes 3244040 | tf_op jit(solution)/shard_map/ppermute | solution.py:377
  635.6 66.0 %collective-permute-start.48 = (bf16[512,1536]{1,0:T(8,128)(2,1)}, bf16[512,1536]{1,0:T(8,128)(2,1)}, u32[]{:S(2)}, u32[]{:S(2)}) collective-permute-start(bf16[512,1536]{1,0:T(8,128)(2,1)} %get-tuple-element.195), channel_id=1, source_target_pairs={{0,16},{16,0},{1,17},{17,1},{2,18},{18,2},{3,19},{19,3},{4,20},{20... | collective-permute-start | bytes 4718600 | tf_op jit(solution)/shard_map/ppermute | solution.py:373
  642.3 25.2 %collective-permute-start.52 = (bf16[768,768]{1,0:T(8,128)(2,1)}, bf16[768,768]{1,0:T(8,128)(2,1)}, u32[]{:S(2)}, u32[]{:S(2)}) collective-permute-start(bf16[768,768]{1,0:T(8,128)(2,1)} %get-tuple-element.200), channel_id=1, source_target_pairs={{0,4},{1,5},{2,6},{3,7},{4,8},{5,9},{6,10},{7,11},{8,12},{9,13},{1... | collective-permute-start | bytes 3538952 | tf_op jit(solution)/shard_map/ppermute | solution.py:389
  645.0 27.3 %collective-permute-start.53 = (bf16[768,768]{1,0:T(8,128)(2,1)}, bf16[768,768]{1,0:T(8,128)(2,1)}, u32[]{:S(2)}, u32[]{:S(2)}) collective-permute-start(bf16[768,768]{1,0:T(8,128)(2,1)} %get-tuple-element.201), channel_id=1, source_target_pairs={{4,0},{5,1},{6,2},{7,3},{8,4},{9,5},{10,6},{11,7},{12,8},{13,9},{1... | collective-permute-start | bytes 3538952 | tf_op jit(solution)/shard_map/ppermute | solution.py:393
  678.3 13.2 %collective-permute-start.56 = (bf16[2,48,1408]{2,1,0:T(8,128)(2,1)S(1)}, bf16[2,48,1408]{2,1,0:T(8,128)(2,1)S(1)}, u32[]{:S(2)}, u32[]{:S(2)}) collective-permute-start(bf16[2,48,1408]{2,1,0:T(8,128)(2,1)S(1)} %fusion.51), channel_id=1, source_target_pairs={{0,12},{1,13},{2,14},{3,15},{4,8},{5,9},{6,10},{7,11},{8,4},{9,5},... | collective-permute-start | bytes 811016 | tf_op jit(solution)/shard_map/ppermute | solution.py:377
  678.5 23.0 %collective-permute-start.55 = (bf16[2,48,1408]{2,1,0:T(8,128)(2,1)S(1)}, bf16[2,48,1408]{2,1,0:T(8,128)(2,1)S(1)}, u32[]{:S(2)}, u32[]{:S(2)}) collective-permute-start(bf16[2,48,1408]{2,1,0:T(8,128)(2,1)S(1)} %get-tuple-element.315), channel_id=1, source_target_pairs={{0,8},{1,9},{2,10},{3,11},{4,12},{5,13},{6,14},{7,15},{8,0},{9,1},... | collective-permute-start | bytes 811016 | tf_op jit(solution)/shard_map/ppermute | solution.py:377
  679.6 21.9 %collective-permute-start.54 = (bf16[2,48,1408]{2,1,0:T(8,128)(2,1)S(1)}, bf16[2,48,1408]{2,1,0:T(8,128)(2,1)S(1)}, u32[]{:S(2)}, u32[]{:S(2)}) collective-permute-start(bf16[2,48,1408]{2,1,0:T(8,128)(2,1)S(1)} %get-tuple-element.314), channel_id=1, source_target_pairs={{0,4},{1,5},{2,6},{3,7},{4,0},{5,1},{6,2},{7,3},{8,12},{9,13},{10,... | collective-permute-start | bytes 811016 | tf_op jit(solution)/shard_map/ppermute | solution.py:377
  684.0 33.2 %collective-permute-start.57 = (bf16[1536,512]{1,0:T(8,128)(2,1)S(1)}, bf16[1536,512]{1,0:T(8,128)(2,1)S(1)}, u32[]{:S(2)}, u32[]{:S(2)}) collective-permute-start(bf16[1536,512]{1,0:T(8,128)(2,1)S(1)} %fusion.25), channel_id=1, source_target_pairs={{0,0},{1,16},{2,2},{3,18},{4,4},{5,20},{6,6},{7,22},{8,8},{9,24},{... | collective-permute-start | bytes 4718600 | tf_op jit(solution)/shard_map/ppermute | solution.py:982
  691.5 19.3 %collective-permute-start.58 = (bf16[1536,256]{1,0:T(8,128)(2,1)S(1)}, bf16[1536,256]{1,0:T(8,128)(2,1)S(1)}, u32[]{:S(2)}, u32[]{:S(2)}) collective-permute-start(bf16[1536,256]{1,0:T(8,128)(2,1)S(1)} %get-tuple-element.209), channel_id=1, source_target_pairs={{1,0},{17,1},{3,2},{19,3},{5,4},{21,5},{7,6},{23,7},{9,8},{25,9},{... | collective-permute-start | bytes 2359304 | tf_op jit(solution)/shard_map/ppermute | solution.py:982
  717.3 5.2 collective-permute-start.59
  (53 other events, 783.3 us)
Sparse Core Ops, SparseCore 0:
  16.3 56.5 all-gather.2
  75.8 81.7 all-gather.4
  522.9 109.0 reduce-scatter.1
